TPU v7x, 32 devices: a whole 2x2x4 slice. The times are simulated.
32 devices in a mesh: group: 2 (over y), tm: 4 (over z), seq: 2 (over x), mp: 2 (over core).
Axes of the slice: x: 2, y: 2, z: 4, core: 2. Of those that a mesh axis runs over, the one named last changes fastest.
Arguments:
- states: bfloat16 [8, 128, 5120], P(('group', 'tm'), 'seq'), parts along dimension 0, may hold values from -6 to 6
- start_step: int32 [2], P('group'), parts along dimension 0, may hold values from 0 to 96
- w_qkv: bfloat16 [3, 5120, 3072], P(None, 'tm', ('seq', 'mp')), may hold values from -0.078125 to 0.078125
- qk_gain: float32 [2, 3072], P(None, ('seq', 'mp')), may hold values from 0.25 to 1.75
- w_out: bfloat16 [5120, 3072], P('tm', ('seq', 'mp')), may hold values from -0.109375 to 0.109375
- time_proj: bfloat16 [256, 15360], P('tm'), may hold values from -0.375 to 0.375
Outputs:
- displacement: float32 [8, 128, 5120], P(('group', 'tm'), 'seq', 'mp'), parts along dimension 0
There are 2 independent parts, one for each index of `group`. A program takes and returns all parts, laid end to end along the dimension named above; an argument that names none is the same for every part. Nothing has to cross between parts.
Inputs may be any that keep to these rules, and one draw needn't show every extreme that they name: `start_step`: the window lies inside the trajectory.
All inputs are finite; a program needn't handle non-finite values.
Results may differ from a plain program's by a relative error of at most 0.0029.
Values may be sent and summed in bfloat16 or wider, within the bound.
No kernel may reach another device: no remote copies, remote signals or barrier semaphores. Data moves between devices by JAX's collectives and lax.ppermute only.
A program may use at most 128 MiB of HBM per device.

v0:
```python
import jax
import jax.numpy as jnp
from jax import lax
from jax.sharding import PartitionSpec as P

HEAD_DIM = 128
FREQ = 256
STEPS = 100


sample_shift = 5.0
norm_eps = 1e-06


def from_behind(block, axis, distance):
    devices = range(lax.axis_size(axis))
    route = [(i - distance, i) for i in devices if i - distance in devices]
    return lax.ppermute(block, axis, route)


def sigma_of(index):
    unit = 1.0 - index.astype(jnp.float32) / jnp.float32(STEPS)
    return sample_shift * unit / (1.0 + (sample_shift - 1.0) * unit)


def embed_time(sigma_now):
    half_freq = FREQ // 2
    ranks = jnp.arange(half_freq).astype(jnp.float32)
    freqs = jnp.exp(-jnp.log(jnp.float32(10000.0)) * ranks / jnp.float32(half_freq))
    angles = (1000.0 * sigma_now)[:, None] * freqs[None, :]
    return jnp.concatenate([jnp.cos(angles), jnp.sin(angles)], axis=1).astype(jnp.bfloat16)


def head_norm(values, gain, frames, seq_len, heads_dev):
    shaped = values.reshape(frames, seq_len, heads_dev, HEAD_DIM)
    meansq = jnp.mean(shaped * shaped, axis=-1, keepdims=True)
    scaled = shaped * lax.rsqrt(meansq + norm_eps) * gain.reshape(heads_dev, HEAD_DIM)
    return scaled.astype(jnp.bfloat16)


def attend(query, keys, values):
    frames, seq_len, heads_dev, head_size = query.shape
    block = min(seq_len, 512)
    blocks = seq_len // block
    inv_root = 1.0 / jnp.sqrt(jnp.float32(head_size))
    stacked = query.reshape(frames, blocks, block, heads_dev, head_size).transpose(1, 0, 2, 3, 4)

    def one_block(q_block):
        scores = (
            jnp.einsum("wqhd,wkhd->whqk", q_block, keys, preferred_element_type=jnp.float32)
            * inv_root
        )
        expo = jnp.exp(scores)
        probs = (expo / jnp.sum(expo, axis=-1, keepdims=True)).astype(jnp.bfloat16)
        return jnp.einsum(
            "whqk,wkhd->wqhd", probs, values, preferred_element_type=jnp.float32
        ).astype(jnp.bfloat16)

    result = lax.map(one_block, stacked)
    return result.transpose(1, 0, 2, 3, 4).reshape(frames, seq_len, heads_dev * head_size)


def on_device(states, start_step, w_qkv, qk_gain, w_out, time_proj):
    frames, tok, width = states.shape
    n_tm = lax.axis_size("tm")
    n_mp = lax.axis_size("mp")
    window = frames * n_tm
    tm_pos = lax.axis_index("tm")
    steps_idx = start_step[0] + jnp.arange(window)
    sigma_now = sigma_of(steps_idx)
    step_size = sigma_of(steps_idx + 1) - sigma_now
    emb = embed_time(sigma_now)
    freq_rows = time_proj.shape[0]
    emb_cols = lax.dynamic_slice_in_dim(emb, tm_pos * freq_rows, freq_rows, 1)
    modulation = lax.psum_scatter(
        jnp.dot(emb_cols, time_proj, preferred_element_type=jnp.float32),
        "tm",
        scatter_dimension=0,
        tiled=True,
    )
    shift = modulation[:, :width]
    scale = modulation[:, width : 2 * width]
    gate = modulation[:, 2 * width :]
    field = states.astype(jnp.float32)
    mean = jnp.mean(field, axis=-1, keepdims=True)
    centred = field - mean
    var = jnp.mean(centred * centred, axis=-1, keepdims=True)
    normed = centred * lax.rsqrt(var + norm_eps)
    hidden = (normed * (1.0 + scale[:, None, :]) + shift[:, None, :]).astype(jnp.bfloat16)
    whole = lax.all_gather(hidden, "seq", axis=1, tiled=True)
    seq_len = whole.shape[1]
    flat = whole.reshape(frames * seq_len, width)
    head_cols = w_qkv.shape[2]
    heads_dev = head_cols // HEAD_DIM
    proj = jnp.einsum(
        "rd,cdh->crh",
        flat,
        lax.all_gather(w_qkv, "tm", axis=1, tiled=True),
        preferred_element_type=jnp.float32,
    )
    query = head_norm(proj[0], qk_gain[0], frames, seq_len, heads_dev)
    keys = head_norm(proj[1], qk_gain[1], frames, seq_len, heads_dev)
    values = proj[2].astype(jnp.bfloat16).reshape(frames, seq_len, heads_dev, HEAD_DIM)
    attn = attend(query, keys, values)
    out_full = lax.all_gather(w_out, "tm", axis=0, tiled=True)
    half_width = width // n_mp
    rows = frames * tok
    first = jnp.int32(0) // rows
    pieces = []
    for offset in range(rows * lax.axis_size(("seq", "mp")) // rows):
        owner = first + offset
        segment = owner // n_mp
        column = owner % n_mp
        tokens_part = lax.dynamic_slice_in_dim(attn, segment * tok, tok, 1)
        weight_part = lax.dynamic_slice_in_dim(out_full, column * half_width, half_width, 0)
        product = jnp.einsum(
            "tsh,eh->tse", tokens_part, weight_part, preferred_element_type=jnp.float32
        )
        pieces.append(product.reshape(rows, half_width))
    out_part = lax.psum_scatter(
        jnp.concatenate(pieces, axis=0), ("seq", "mp"), scatter_dimension=0, tiled=True
    ).reshape(frames, tok, half_width)
    gate_own = lax.dynamic_slice_in_dim(gate, lax.axis_index("mp") * half_width, half_width, 1)
    own_steps = lax.dynamic_slice_in_dim(step_size, tm_pos * frames, frames, 0)
    drift = gate_own[:, None, :] * out_part
    increments = own_steps[:, None, None] * drift
    local_sums = jnp.cumsum(increments, axis=0)
    block_total = local_sums[-1]
    running = block_total
    for level in range((n_tm - 1).bit_length()):
        running = running + from_behind(running, "tm", 1 << level)
    before = running - block_total
    return before[None, :, :] + local_sums


def solution(mesh):
    return jax.shard_map(
        on_device,
        mesh=mesh,
        in_specs=(
            P(("group", "tm"), "seq", None),
            P("group"),
            P(None, "tm", ("seq", "mp")),
            P(None, ("seq", "mp")),
            P("tm", ("seq", "mp")),
            P("tm", None),
        ),
        out_specs=P(("group", "tm"), "seq", "mp"),
        check_vma=False,
    )
```

profile of v0, /device:TPU:25, one launch (start us, length us, event | category | flops | bytes accessed | tf_op | source)
XLA Modules:
  0.0 721.7 jit_solution(13477119722304982495)
XLA Ops:
  7.4 0.5 divide_subtract_fusion
  7.9 0.1 fusion.24
  8.0 0.3 copy-done
  8.3 1.1 fusion.26
  9.4 0.0 all-reduce.3.cloned.1.call-update
  9.5 0.0 all-gather.4.cloned.1.call-start
  9.5 0.2 convert_reduce_fusion
  9.7 0.3 fusion.10
  10.1 0.6 dynamic-slice.1
  10.7 32.4 %all-reduce.3.cloned.1.call-done = f32[4,15360]{1,0:T(4,128)} async-done(((f32[4,15360]{1,0:T(4,128)}), f32[4,15360]{1,0:T(4,128)}) %all-reduce.3.cloned.1.call-update) | async-done | bytes 245776
  43.0 1.7 dynamic-slice_add_fusion
  44.7 1.1 fusion.13
  45.8 0.0 all-gather.4.cloned.1.call-update
  45.9 0.0 all-gather.6.cloned.1.call-start
  45.9 0.7 all-gather.6.cloned.1.call-update
  46.6 0.0 all-gather.8.cloned.1.call-start
  46.7 0.5 all-gather.8.cloned.1.call-update
  47.2 0.0 reduce-scatter.2.cloned.1.call-start
  47.3 25.9 %all-gather.4.cloned.1.call-done = bf16[1,128,5120]{2,1,0:T(8,128)(2,1)} async-done(((bf16[1,64,5120]{2,1,0:T(8,128)(2,1)}), bf16[1,128,5120]{2,1,0:T(8,128)(2,1)}) %all-gather.4.cloned.1.call-update) | async-done | bytes 1310736 | tf_op jit(solution)/shard_map/all_gather | solution.py:90
  73.2 398.3 %all-gather.6.cloned.1.call-done = bf16[3,5120,768]{2,1,0:T(8,128)(2,1)} async-done(((bf16[3,1280,768]{2,1,0:T(8,128)(2,1)}), bf16[3,5120,768]{2,1,0:T(8,128)(2,1)}) %all-gather.6.cloned.1.call-update) | async-done | bytes 23592976 | tf_op jit(solution)/shard_map/all_gather | solution.py:98
  471.4 10.0 %convolution_bitcast_fusion = f32[3,128,768]{2,1,0:T(8,128)S(1)} fusion(bf16[3,5120,768]{2,1,0:T(8,128)(2,1)} %all-gather.6.cloned.1.call-done, bf16[1,128,5120]{2,1,0:T(8,128)(2,1)} %all-gather.4.cloned.1.call-done), kind=kOutput, calls=%fused_computation.13 | convolution fusion | flops 3019898880 | bytes 26083328 | tf_op jit(solution)/shard_map/rd,cdh->crh/dot_general | solution.py:95
  481.4 0.7 slice.45
  482.1 0.1 slice_multiply_fusion.1
  482.3 0.9 copy.23
  483.2 0.2 copy.21
  483.3 1.1 reduce_sum.49
  484.5 0.2 copy.22
  484.6 0.2 copy.20
  484.8 1.1 copy.19
  485.9 0.5 fusion.15
  486.4 0.2 convolution_convert_fusion
  486.7 125.4 %all-gather.8.cloned.1.call-done = bf16[5120,768]{1,0:T(8,128)(2,1)} async-done(((bf16[1280,768]{1,0:T(8,128)(2,1)}), bf16[5120,768]{1,0:T(8,128)(2,1)}) %all-gather.8.cloned.1.call-update) | async-done | bytes 7864336 | tf_op jit(solution)/shard_map/all_gather | solution.py:105
  612.1 3.6 fusion.2
  615.7 3.6 fusion.4
  619.3 1.3 fusion.6
  620.6 1.5 fusion
  622.1 1.7 pad_maximum_fusion
  623.8 0.6 copy-done.5
  624.3 0.6 dynamic_slice.28
  624.9 1.5 dynamic-slice_reduce_fusion
  626.4 32.9 %reduce-scatter.2.cloned.1.call-done = f32[64,2560]{1,0:T(8,128)} async-done(((f32[256,2560]{1,0:T(8,128)}), f32[64,2560]{1,0:T(8,128)}) %reduce-scatter.2.cloned.1.call-update) | async-done | bytes 655376 | tf_op jit(solution)/shard_map/reduce_scatter | solution.py:120
  659.4 1.8 multiply_multiply_fusion
  661.1 1.3 collective-permute-start
  662.4 16.1 %collective-permute-done = f32[64,2560]{1,0:T(8,128)S(1)} collective-permute-done((f32[64,2560]{1,0:T(8,128)S(1)}, f32[64,2560]{1,0:T(8,128)S(1)}, u32[]{:S(2)}, u32[]{:S(2)}) %collective-permute-start) | collective-permute-done | bytes 655392 | tf_op jit(solution)/shard_map/ppermute | solution.py:18
  678.5 1.7 fusion.35
  680.2 1.3 collective-permute-start.1
  681.5 32.1 %collective-permute-done.1 = f32[64,2560]{1,0:T(8,128)S(1)} collective-permute-done((f32[64,2560]{1,0:T(8,128)S(1)}, f32[64,2560]{1,0:T(8,128)S(1)}, u32[]{:S(2)}, u32[]{:S(2)}) %collective-permute-start.1) | collective-permute-done | bytes 655392 | tf_op jit(solution)/shard_map/ppermute | solution.py:18
  713.7 1.5 fusion.16
  (21 shorter events, 0.1 us)
Async XLA Ops:
  6.5 1.8 copy-start
  6.5 3.5 copy-start.6
  6.5 3.0 copy-start.2
  6.5 36.5 %all-reduce.3.cloned.1.call-start = ((), (), s32[]{:S(2)}) async-start(), calls=%async_computation.5 | async-start | bytes 491520
  9.5 63.7 %all-gather.4.cloned.1.call-start = ((), (), s32[]{:S(2)}) async-start(), calls=%async_computation.1 | async-start | bytes 1966080 | tf_op jit(solution)/shard_map/all_gather | solution.py:90
  45.9 1.4 copy-start.4
  45.9 425.6 %all-gather.6.cloned.1.call-start = ((), (), s32[]{:S(2)}) async-start(), calls=%async_computation.2 | async-start | bytes 29491200 | tf_op jit(solution)/shard_map/all_gather | solution.py:98
  46.6 565.5 %all-gather.8.cloned.1.call-start = ((), (), s32[]{:S(2)}) async-start(), calls=%async_computation.3 | async-start | bytes 9830400 | tf_op jit(solution)/shard_map/all_gather | solution.py:105
  47.2 612.2 %reduce-scatter.2.cloned.1.call-start = ((), (), s32[]{:S(2)}) async-start(), calls=%async_computation.4 | async-start | bytes 3276800 | tf_op jit(solution)/shard_map/reduce_scatter | solution.py:120
  612.1 7.1 copy-start.1
  623.8 0.6 copy-start.5
  659.4 54.3 %copy-start.3 = (f32[64,2560]{1,0:T(8,128)S(1)}, f32[64,2560]{1,0:T(8,128)}, u32[]{:S(2)}) copy-start(f32[64,2560]{1,0:T(8,128)} %reduce-scatter.2.cloned.1.call-done) | copy-start | bytes 1966084
  661.1 17.4 %collective-permute-start = (f32[64,2560]{1,0:T(8,128)S(1)}, f32[64,2560]{1,0:T(8,128)S(1)}, u32[]{:S(2)}, u32[]{:S(2)}) collective-permute-start(f32[64,2560]{1,0:T(8,128)S(1)} %multiply_multiply_fusion), channel_id=1, source_target_pairs={{0,4},{4,8},{8,12},{1,5},{5,9},{9,13},{2,6},{6,10},{10,14},{3,7},{... | collective-permute-start | bytes 1966088 | tf_op jit(solution)/shard_map/ppermute | solution.py:18
  680.2 33.4 %collective-permute-start.1 = (f32[64,2560]{1,0:T(8,128)S(1)}, f32[64,2560]{1,0:T(8,128)S(1)}, u32[]{:S(2)}, u32[]{:S(2)}) collective-permute-start(f32[64,2560]{1,0:T(8,128)S(1)} %fusion.35), channel_id=1, source_target_pairs={{0,8},{4,12},{1,9},{5,13},{2,10},{6,14},{3,11},{7,15},{16,24},{20,... | collective-permute-start | bytes 1966088 | tf_op jit(solution)/shard_map/ppermute | solution.py:18
Sparse Core Ops, SparseCore 0:
  9.7 33.3 all-reduce.2
  46.0 27.1 all-gather.3
  74.7 396.6 all-gather.5
  472.9 139.2 all-gather.7
  623.9 35.4 reduce-scatter.1
where the time goes:
time: 722 us
  waiting for transfers between devices  664 us (92%)
  matrix products  21.8 us (3%)
  between operations  14.1 us (2%)
  other arithmetic  12 us (2%)
    all_gather x1, waiting for transfers between devices, on_device(): lax.all_gather(w_qkv, 'tm', axis=1, tiled=True)  398 us
    all_gather x1, waiting for transfers between devices, on_device(): out_full = lax.all_gather(w_out, 'tm', axis=0, tiled=True)  125 us
    ppermute x2, waiting for transfers between devices, from_behind(): return lax.ppermute(block, axis, route)  48.2 us
    unnamed x6, waiting for transfers between devices  33.6 us
    reduce_scatter x1, waiting for transfers between devices, on_device(): lax.psum_scatter(jnp.concatenate(pieces, axis=0), ('seq', 'mp'), scatter_...  32.9 us
    all_gather x1, waiting for transfers between devices, on_device(): whole = lax.all_gather(hidden, 'seq', axis=1, tiled=True)  25.9 us
  transfers between devices with their start and end apart: 7, of which 7 were waited for; matrix products, arithmetic and copies ran while one was open for 3% of the time, Pallas kernels for 0%

commit v1 on v0

v1 whole, which is shorter than its diff:
```python
import jax
import jax.numpy as jnp
from jax import lax
from jax.sharding import PartitionSpec as P

HEAD_DIM = 128
FREQ = 256
STEPS = 100


sample_shift = 5.0
norm_eps = 1e-06


def sigma_of(index):
    unit = 1.0 - index.astype(jnp.float32) / jnp.float32(STEPS)
    return sample_shift * unit / (1.0 + (sample_shift - 1.0) * unit)


def embed_time(sigma_now):
    half_freq = FREQ // 2
    ranks = jnp.arange(half_freq).astype(jnp.float32)
    freqs = jnp.exp(-jnp.log(jnp.float32(10000.0)) * ranks / jnp.float32(half_freq))
    angles = (1000.0 * sigma_now)[:, None] * freqs[None, :]
    return jnp.concatenate([jnp.cos(angles), jnp.sin(angles)], axis=1).astype(jnp.bfloat16)


def turn(block, axis, distance):
    size = lax.axis_size(axis)
    return lax.ppermute(block, axis, [(i, (i + distance) % size) for i in range(size)])


def take(array, index, dim=0):
    return lax.dynamic_index_in_dim(array, index, dim, keepdims=False)


def head_norm(values, gain):
    heads_dev = values.shape[-1] // HEAD_DIM
    shaped = values.reshape(values.shape[:-1] + (heads_dev, HEAD_DIM))
    meansq = jnp.mean(shaped * shaped, axis=-1, keepdims=True)
    scaled = shaped * lax.rsqrt(meansq + norm_eps) * gain.reshape(heads_dev, HEAD_DIM)
    return scaled.astype(jnp.bfloat16)


def attend(query, keys, values):
    inv_root = 1.0 / jnp.sqrt(jnp.float32(query.shape[-1]))
    scores = jnp.einsum("wqhd,wkhd->whqk", query, keys, preferred_element_type=jnp.float32)
    expo = jnp.exp(scores * inv_root)
    probs = (expo / jnp.sum(expo, axis=-1, keepdims=True)).astype(jnp.bfloat16)
    return jnp.einsum(
        "whqk,wkhd->wqhd", probs, values, preferred_element_type=jnp.float32
    ).astype(jnp.bfloat16)


def on_device(states, start_step, w_qkv, qk_gain, w_out, time_proj):
    frames, tok, width = states.shape
    n_tm, n_seq, n_mp = (lax.axis_size(name) for name in ("tm", "seq", "mp"))
    z, m = lax.axis_index("tm"), lax.axis_index("mp")
    part = tok // n_mp
    depth, cols = w_qkv.shape[1:]
    half = depth // n_mp
    window = frames * n_tm
    freq_rows = time_proj.shape[0]

    mine = lax.dynamic_slice_in_dim(states, m * part, part, 1).reshape(frames, part, n_tm, depth)
    raw_tm = [take(mine, z, 2)] + [turn(take(mine, (z + k) % n_tm, 2), "tm", k) for k in range(1, n_tm)]
    raw = jnp.stack(raw_tm)
    raw = jnp.stack([raw] + [turn(raw, "seq", j) for j in range(1, n_seq)], axis=1)
    raw = jnp.stack([raw] + [turn(raw, "mp", i) for i in range(1, n_mp)], axis=1)

    field = states.astype(jnp.float32)
    mean = jnp.mean(field, axis=-1)
    centred = field - mean[..., None]
    var = jnp.mean(centred * centred, axis=-1)
    stats = jnp.stack([mean, lax.rsqrt(var + norm_eps)])
    stats = jnp.stack([stats] + [turn(stats, "tm", k) for k in range(1, n_tm)])
    stats = jnp.stack([stats] + [turn(stats, "seq", j) for j in range(1, n_seq)], axis=1)
    stats = stats.reshape(n_tm, n_seq, 2, frames, n_mp, part)
    stats = jnp.stack([take(stats, (m - i) % n_mp, 4) for i in range(n_mp)], axis=1)

    steps_idx = start_step[0] + jnp.arange(window)
    sigma_now = sigma_of(steps_idx)
    step_size = sigma_of(steps_idx + 1) - sigma_now
    emb = embed_time(sigma_now)
    emb_cols = lax.dynamic_slice_in_dim(emb, z * freq_rows, freq_rows, 1)
    partial = jnp.dot(emb_cols, time_proj, preferred_element_type=jnp.float32)
    partial = partial.reshape(window, 3, n_tm, depth)
    modulation = take(partial, z, 2)
    for k in range(1, n_tm):
        modulation = modulation + turn(take(partial, (z + k) % n_tm, 2), "tm", k)
    modulation = modulation.reshape(n_tm, frames, 3, depth)
    modulation = jnp.stack([take(modulation, (z - k) % n_tm) for k in range(n_tm)])
    sizes = step_size.reshape(n_tm, frames)

    shift, scale, gate = (modulation[:, None, None, :, None, c, :] for c in range(3))
    normed = (raw.astype(jnp.float32) - stats[:, :, :, 0, :, :, None]) * stats[:, :, :, 1, :, :, None]
    hidden = (normed * (1.0 + scale) + shift).astype(jnp.bfloat16)
    rows = n_mp * n_seq * frames * part
    hidden = hidden.reshape(n_tm, rows, depth)

    proj = jnp.einsum("krd,cdh->kcrh", hidden, w_qkv, preferred_element_type=jnp.float32)
    right = left = jnp.zeros((), jnp.float16)
    for t in range(n_tm - 1):
        send_right = (right.astype(jnp.float32) + proj[(t + 1) % n_tm]).astype(jnp.float16)
        send_left = (left.astype(jnp.float32) + proj[n_tm - 1 - t]).astype(jnp.float16)
        right = lax.ppermute(send_right, "tm", [(i, i + 1) for i in range(t + 1)])
        left = lax.ppermute(send_left, "tm", [(n_tm - 1 - i, n_tm - 2 - i) for i in range(t + 1)])
    whole = proj[0] + right.astype(jnp.float32) + left.astype(jnp.float32)
    whole = whole.reshape(3, n_mp * n_seq, frames, part, cols)
    whole = whole.transpose(0, 2, 1, 3, 4).reshape(3, frames, n_mp * n_seq * part, cols)
    query = head_norm(whole[0], qk_gain[0])
    keys = head_norm(whole[1], qk_gain[1])
    values = whole[2].astype(jnp.bfloat16).reshape(query.shape)
    attn = attend(query, keys, values)
    attn = attn.reshape(frames, n_mp, n_seq, part, cols)

    attn = jnp.stack([attn[:, :, 0]] + [turn(attn[:, :, j], "seq", -j) for j in range(1, n_seq)])
    attn = jnp.stack([attn] + [turn(attn, "tm", k) for k in range(1, n_tm)])
    cores = [attn]
    for i in range(1, n_mp):
        cores.append(turn(jnp.roll(attn, i, axis=3), "mp", i))
    attn = jnp.stack(cores)

    share = w_out.reshape(n_mp, half, cols)
    share = jnp.stack([take(share, m)] + [turn(take(share, (m + i) % n_mp), "mp", i) for i in range(1, n_mp)])
    share = jnp.stack([share] + [turn(share, "seq", -j) for j in range(1, n_seq)])
    out = jnp.einsum("lkjfipc,jlec->kfipe", attn, share, preferred_element_type=jnp.float32)

    blocks = [(z - k) % n_tm for k in range(n_tm)]
    gate_own = take(gate.reshape(n_tm, frames, n_mp, half), m, 2)
    local = [
        jnp.cumsum(take(sizes, blocks[k])[:, None, None, None] * (gate_own[k][:, None, None, :] * out[k]), axis=0)
        for k in range(n_tm)
    ]
    moved = []
    for k in range(n_tm):
        total = local[k]
        for other in range(n_tm):
            if other != k:
                total = total + jnp.where(blocks[other] < blocks[k], local[other][-1], 0.0)[None]
        moved.append(total)
    moved = jnp.stack(moved)
    moved = jnp.stack([take(moved, (m - i) % n_mp, 2) for i in range(n_mp)], axis=2)
    arrived = [moved[0]] + [
        turn(moved[k].astype(jnp.bfloat16), "tm", -k).astype(jnp.float32) for k in range(1, n_tm)
    ]
    by_slice = jnp.stack(arrived)
    by_slice = jnp.stack([take(by_slice, (s - z) % n_tm) for s in range(n_tm)])
    by_slice = by_slice.reshape(n_mp, n_tm // n_mp, frames, tok, half)
    final = [take(by_slice, m)]
    for i in range(1, n_mp):
        final.append(turn(take(by_slice, (m + i) % n_mp).astype(jnp.bfloat16), "mp", i).astype(jnp.float32))
    final = jnp.stack(final)
    final = jnp.stack([take(final, (m - i) % n_mp) for i in range(n_mp)])
    return final.transpose(2, 3, 1, 0, 4).reshape(frames, tok, width // n_mp)


def solution(mesh):
    return jax.shard_map(
        on_device,
        mesh=mesh,
        in_specs=(
            P(("group", "tm"), "seq", None),
            P("group"),
            P(None, "tm", ("seq", "mp")),
            P(None, ("seq", "mp")),
            P("tm", ("seq", "mp")),
            P("tm", None),
        ),
        out_specs=P(("group", "tm"), "seq", "mp"),
        check_vma=False,
    )
```

time: 722 us -> 189 us (0.26)
  waiting for transfers between devices: 664 us -> 82.1 us
  starting transfers between devices: 2.75 us -> 56.4 us
  matrix products: 21.8 us -> 8.44 us
  between operations: 14.1 us -> 1.32 us
  other arithmetic: 12 us -> 24.1 us
    all_gather x3 -> x0, waiting for transfers between devices: 550 us -> none  [the longest x1 398 us: on_device(): lax.all_gather(w_qkv, 'tm', axis=1, tiled=True)]
    ppermute x2 -> x29, starting transfers between devices: 2.58 us -> 56.4 us  [the longest x23 29.1 us: turn(): lax.ppermute(block, axis, [(i, (i + distance) % size) for i in range(size)])]
    ppermute x2 -> x29, waiting for transfers between devices: 48.2 us -> 82.1 us  [the longest x23 59.3 us: turn(): lax.ppermute(block, axis, [(i, (i + distance) % size) for i in range(size)])]
    unnamed x6 -> x0, waiting for transfers between devices: 33.6 us -> none
    reduce_scatter x1 -> x0, waiting for transfers between devices: 32.9 us -> none  [on_device(): lax.psum_scatter(jnp.concatenate(pieces, axis=0), ('seq', 'mp'), scatter_...]
    dot_general x8 -> x5, matrix products: 21.8 us -> 8.44 us  [the longest x1 3.81 us: on_device(): jnp.einsum('lkjfipc,jlec->kfipe', attn, share, preferred_element_type=jnp...]
    another operation x1 -> x25, other arithmetic: 0.11 us -> 13.4 us  [the longest x5 10.3 us: on_device(): moved = jnp.stack(moved)]
  transfers between devices with their start and end apart: 7 -> 29, of which waited for: 7 -> 14; matrix products, arithmetic and copies ran while one was open for 3% -> 12% of each run, Pallas kernels for 0% -> 0%
where the time goes in v1:
time: 189 us; the launch traced here: 186 us
  waiting for transfers between devices  82.1 us (43%)
  starting transfers between devices  56.4 us (30%)
  other arithmetic  24.1 us (13%)
  local copies, waits for them, and re-layouts  13.7 us (7%)
  matrix products  8.44 us (4%)
    ppermute x23, waiting for transfers between devices, turn(): lax.ppermute(block, axis, [(i, (i + distance) % size) for i in range(size)])  59.3 us
    ppermute x23, starting transfers between devices, turn(): lax.ppermute(block, axis, [(i, (i + distance) % size) for i in range(size)])  29.1 us
    ppermute x3, starting transfers between devices, on_device(): lax.ppermute(send_left, 'tm', [(n_tm - 1 - i, n_tm - 2 - i) for i in rang...  24.6 us
    ppermute x3, waiting for transfers between devices, on_device(): lax.ppermute(send_left, 'tm', [(n_tm - 1 - i, n_tm - 2 - i) for i in rang...  21.7 us
    another operation x5, other arithmetic, on_device(): moved = jnp.stack(moved)  10.3 us
    dot_general x1, matrix products, on_device(): jnp.einsum('lkjfipc,jlec->kfipe', attn, share, preferred_element_type=jnp...  3.81 us
  transfers between devices with their start and end apart: 29, of which 14 were waited for; matrix products, arithmetic and copies ran while one was open for 12% of the time, Pallas kernels for 0%

profile of v1, /device:TPU:25, one launch (start us, length us, event | category | flops | bytes accessed | tf_op | source)
XLA Modules:
  0.0 186.1 jit_solution(13260965279734883995)
XLA Ops:
  0.0 1.4 convert_reduce_fusion
  1.4 1.4 fusion.11
  3.0 1.3 collective-permute-start.9
  5.8 3.1 %collective-permute-start = (f32[4,3,1280]{2,0,1:T(4,128)S(1)}, f32[4,3,1280]{2,0,1:T(4,128)S(1)}, u32[]{:S(2)}, u32[]{:S(2)}) collective-permute-start(f32[4,3,1280]{2,0,1:T(4,128)S(1)} %get-tuple-element.46), channel_id=1, source_target_pairs={{0,4},{4,8},{8,12},{12,0},{1,5},{5,9},{9,13},{13,1},{2,6},{6,10},{... | collective-permute-start | bytes 184328 | tf_op jit(solution)/shard_map/ppermute | solution.py:30
  10.4 2.0 %collective-permute-start.4 = (bf16[1,32,1280]{2,1,0:T(8,128)(2,1)S(1)}, bf16[1,32,1280]{2,1,0:T(8,128)(2,1)S(1)}, u32[]{:S(2)}, u32[]{:S(2)}) collective-permute-start(bf16[1,32,1280]{2,1,0:T(8,128)(2,1)S(1)} %bitcast.227), channel_id=1, source_target_pairs={{0,8},{4,12},{8,0},{12,4},{1,9},{5,13},{9,1},{13,5},{2,10},{6,14},... | collective-permute-start | bytes 245768 | tf_op jit(solution)/shard_map/ppermute | solution.py:30
  12.4 1.3 collective-permute-start.11
  16.7 1.4 collective-permute-start.5
  18.4 3.3 %collective-permute-done.5 = bf16[1,32,1280]{2,1,0:T(8,128)(2,1)S(1)} collective-permute-done((bf16[1,32,1280]{2,1,0:T(8,128)(2,1)S(1)}, bf16[1,32,1280]{2,1,0:T(8,128)(2,1)S(1)}, u32[]{:S(2)}, u32[]{:S(2)}) %collective-permute-start.5) | collective-permute-done | bytes 81952 | tf_op jit(solution)/shard_map/ppermute | solution.py:30
  22.2 1.1 collective-permute-done.2
  23.4 4.4 %collective-permute-done.6 = bf16[4,1,32,1280]{3,2,1,0:T(8,128)(2,1)S(1)} collective-permute-done((bf16[4,1,32,1280]{3,2,1,0:T(8,128)(2,1)S(1)}, bf16[4,1,32,1280]{3,2,1,0:T(8,128)(2,1)S(1)}, u32[]{:S(2)}, u32[]{:S(2)}) %collective-permute-start.6) | collective-permute-done | bytes 327712 | tf_op jit(solution)/shard_map/ppermute | solution.py:30
  27.9 5.0 %collective-permute-start.7 = (bf16[4,2,1,32,1280]{4,3,0,2,1:T(8,128)(2,1)S(1)}, bf16[4,2,1,32,1280]{4,3,0,2,1:T(8,128)(2,1)S(1)}, u32[]{:S(2)}, u32[]{:S(2)}) collective-permute-start(bf16[4,2,1,32,1280]{4,3,0,2,1:T(8,128)(2,1)S(1)} %get-tuple-element.36), channel_id=1, source_target_pairs={{0,1},{1,0},{2,3},{3,2},{4,5},{5,4},{6,7},{7,6},{8,9},{9,8},{10,11... | collective-permute-start | bytes 1966088 | tf_op jit(solution)/shard_map/ppermute | solution.py:30
  33.6 1.1 collective-permute-done.7
  35.1 1.0 slice-done.1
  36.1 3.4 %fusion.5 = f32[4,3,128,768]{3,2,1,0:T(8,128)S(1)} fusion(bf16[3,1280,768]{2,1,0:T(8,128)(2,1)S(1)} %bitcast.245, f32[4,128,1280]{2,1,0:T(8,128)S(1)} %bitcast.208, f32[4,1280]{1,0:T(4,128)S(1)} %get-tuple-element.54, f32[4,1280]{1,0:T(4,128)S(1)} %get-tuple-element.55, f32[4,128]{1,0:T(4,128)S(1)} %mul.284, f32[4,128]{1,0:T(4,128)S(1)} %sub.72), kind=kOutput, calls=%fused_computation.7 | convolution fusion | flops 3023175680 | bytes 13283328 | tf_op jit(solution)/shard_map/krd,cdh->kcrh/dot_general | solution.py:101
  40.4 1.8 collective-permute-start.15
  43.1 11.4 %collective-permute-done.15 = f16[3,128,768]{2,1,0:T(8,128)(2,1)S(1)} collective-permute-done((f16[3,128,768]{2,1,0:T(8,128)(2,1)S(1)}, f16[3,128,768]{2,1,0:T(8,128)(2,1)S(1)}, u32[]{:S(2)}, u32[]{:S(2)}) %collective-permute-start.15) | collective-permute-done | bytes 589856 | tf_op jit(solution)/shard_map/ppermute | solution.py:107
  54.9 18.5 %collective-permute-start.16 = (f16[3,128,768]{2,1,0:T(8,128)(2,1)S(1)}, f16[3,128,768]{2,1,0:T(8,128)(2,1)}, u32[]{:S(2)}, u32[]{:S(2)}) collective-permute-start(f16[3,128,768]{2,1,0:T(8,128)(2,1)S(1)} %get-tuple-element.12), channel_id=1, source_target_pairs={{12,8},{8,4},{13,9},{9,5},{14,10},{10,6},{15,11},{11,7},{28,24},{2... | collective-permute-start | bytes 1769480 | tf_op jit(solution)/shard_map/ppermute | solution.py:107
  73.4 1.6 constant_dynamic-slice_fusion.11
  75.1 2.1 %collective-permute-start.23 = (bf16[640,768]{1,0:T(8,128)(2,1)S(1)}, bf16[640,768]{1,0:T(8,128)(2,1)S(1)}, u32[]{:S(2)}, u32[]{:S(2)}) collective-permute-start(bf16[640,768]{1,0:T(8,128)(2,1)S(1)} %get-tuple-element.18), channel_id=1, source_target_pairs={{0,1},{1,0},{2,3},{3,2},{4,5},{5,4},{6,7},{7,6},{8,9},{9,8},{10,11... | collective-permute-start | bytes 2949128 | tf_op jit(solution)/shard_map/ppermute | solution.py:30
  77.2 1.3 collective-permute-start.14
  78.5 5.0 %collective-permute-done.16 = f16[3,128,768]{2,1,0:T(8,128)(2,1)} collective-permute-done((f16[3,128,768]{2,1,0:T(8,128)(2,1)S(1)}, f16[3,128,768]{2,1,0:T(8,128)(2,1)}, u32[]{:S(2)}, u32[]{:S(2)}) %collective-permute-start.16) | collective-permute-done | bytes 589856 | tf_op jit(solution)/shard_map/ppermute | solution.py:107
  83.5 1.6 add_convert_fusion.1
  85.1 4.2 %collective-permute-start.17 = (f16[3,128,768]{2,1,0:T(8,128)(2,1)S(1)}, f16[3,128,768]{2,1,0:T(8,128)(2,1)S(1)}, u32[]{:S(2)}, u32[]{:S(2)}) collective-permute-start(f16[3,128,768]{2,1,0:T(8,128)(2,1)S(1)} %add_convert_fusion.1), channel_id=1, source_target_pairs={{12,8},{8,4},{4,0},{13,9},{9,5},{5,1},{14,10},{10,6},{6,2},{15,11}... | collective-permute-start | bytes 1769480 | tf_op jit(solution)/shard_map/ppermute | solution.py:107
  89.4 2.2 %fusion.62 = (bf16[1,2,640,768]{3,2,1,0:T(8,128)(2,1)}, bf16[2,640,768]{2,1,0:T(8,128)(2,1)}) fusion(bf16[1,640,768]{2,1,0:T(8,128)(2,1)S(1)} %bitcast.216, bf16[1,640,768]{2,1,0:T(8,128)(2,1)S(1)} %get-tuple-element.17), kind=kLoop, calls=%fused_computation.170 | loop fusion | flops 983040 | bytes 5898240 | tf_op jit(solution)/shard_map/stack | solution.py:126
  91.6 1.2 collective-permute-start.24
  92.8 1.2 collective-permute-done.14
  94.0 5.3 %collective-permute-done.17 = f16[3,128,768]{2,1,0:T(8,128)(2,1)S(1)} collective-permute-done((f16[3,128,768]{2,1,0:T(8,128)(2,1)S(1)}, f16[3,128,768]{2,1,0:T(8,128)(2,1)S(1)}, u32[]{:S(2)}, u32[]{:S(2)}) %collective-permute-start.17) | collective-permute-done | bytes 589856 | tf_op jit(solution)/shard_map/ppermute | solution.py:107
  99.3 1.5 fusion.21
  102.5 1.0 reduce_sum.48
  104.1 1.1 copy.58
  106.4 1.3 collective-permute-start.18
  107.7 27.7 %collective-permute-done.18 = bf16[1,2,32,768]{3,2,1,0:T(8,128)(2,1)S(1)} collective-permute-done((bf16[1,2,32,768]{3,2,1,0:T(8,128)(2,1)S(1)}, bf16[1,2,32,768]{3,2,1,0:T(8,128)(2,1)S(1)}, u32[]{:S(2)}, u32[]{:S(2)}) %collective-permute-start.18) | collective-permute-done | bytes 98336 | tf_op jit(solution)/shard_map/ppermute | solution.py:30
  135.6 1.8 collective-permute-start.20
  137.6 2.5 %collective-permute-done.19 = bf16[2,1,2,32,768]{4,3,0,2,1:T(8,128)(2,1)S(1)} collective-permute-done((bf16[2,1,2,32,768]{4,3,0,2,1:T(8,128)(2,1)S(1)}, bf16[2,1,2,32,768]{4,3,0,2,1:T(8,128)(2,1)S(1)}, u32[]{:S(2)}, u32[]{:S(2)}) %collective-permute-start.19) | collective-permute-done | bytes 196640 | tf_op jit(solution)/shard_map/ppermute | solution.py:30
  140.1 12.7 %collective-permute-done.20 = bf16[2,1,2,32,768]{4,3,0,2,1:T(8,128)(2,1)S(1)} collective-permute-done((bf16[2,1,2,32,768]{4,3,0,2,1:T(8,128)(2,1)S(1)}, bf16[2,1,2,32,768]{4,3,0,2,1:T(8,128)(2,1)S(1)}, u32[]{:S(2)}, u32[]{:S(2)}) %collective-permute-start.20) | collective-permute-done | bytes 196640 | tf_op jit(solution)/shard_map/ppermute | solution.py:30
  153.1 3.1 %collective-permute-start.22 = (bf16[4,2,1,2,32,768]{5,4,1,3,0,2:T(8,128)(2,1)S(1)}, bf16[4,2,1,2,32,768]{5,4,1,3,0,2:T(8,128)(2,1)}, u32[]{:S(2)}, u32[]{:S(2)}) collective-permute-start(bf16[4,2,1,2,32,768]{5,4,1,3,0,2:T(8,128)(2,1)S(1)} %pad_maximum_fusion.2), channel_id=1, source_target_pairs={{0,1},{1,0},{2,3},{3,2},{4,5},{5,4},{6,7},{7,6},{8,9},{9,8},{10,11... | collective-permute-start | bytes 2359304 | tf_op jit(solution)/shard_map/ppermute | solution.py:30
  156.8 1.4 reshape_broadcast_in_dim_squeeze.3
  159.0 3.8 %fusion.18 = f32[4,2,32,640]{3,2,1,0:T(8,128)S(1)} fusion(bf16[1,2,640,768]{3,2,1,0:T(8,128)(2,1)} %bitcast.68, bf16[1,2,640,768]{3,2,1,0:T(8,128)(2,1)} %get-tuple-element.15, bf16[1,4,2,1,2,32,768]{6,5,0,2,4,1,3:T(8,128)(2,1)} %bitcast.62, bf16[1,4,2,1,2,32,768]{6,5,0,2,4,1,3:T(8,128)(2,1)S(1)} %get-tuple-element.23), kind=kOutput, calls=%fused_computation.22 | convolution fusion | flops 1009385472 | bytes 6160384 | tf_op jit(solution)/shard_map/lkjfipc,jlec->kfipe/dot_general | solution.py:127
  162.8 2.6 %add_bitcast_fusion.3 = f32[1,1,2,32,640]{4,3,2,1,0:T(8,128)S(1)} fusion(pred[]{:T(512)S(6)} %lt.220, pred[]{:T(512)S(6)} %lt.219, pred[]{:T(512)S(6)} %lt.218, f32[4,2,32,640]{3,2,1,0:T(8,128)S(1)} %fusion.18, f32[640]{0:T(1024)S(1)} %get-tuple-element.8, f32[]{:T(128)} %bitcast.1, f32[640]{0:T(1024)S(1)} %get-tuple-element.7, f32[]{:T(128)} %bitcast.73, ...), kind=kLoop, calls=%fused_computation.83 | loop fusion | flops 573440 | bytes 829459 | tf_op jit(solution)/shard_map/stack | solution.py:142
  165.4 2.6 %add_bitcast_fusion.2 = f32[1,1,2,32,640]{4,3,2,1,0:T(8,128)S(1)} fusion(pred[]{:T(512)S(6)} %lt.223, pred[]{:T(512)S(6)} %lt.222, pred[]{:T(512)S(6)} %lt.221, f32[4,2,32,640]{3,2,1,0:T(8,128)S(1)} %fusion.18, f32[640]{0:T(1024)S(1)} %get-tuple-element.8, f32[]{:T(128)} %bitcast.1, f32[640]{0:T(1024)S(1)} %get-tuple-element.7, f32[]{:T(128)} %bitcast.73, ...), kind=kLoop, calls=%fused_computation.82 | loop fusion | flops 573440 | bytes 829459 | tf_op jit(solution)/shard_map/stack | solution.py:142
  167.9 2.6 %add_bitcast_fusion.1 = f32[1,1,2,32,640]{4,3,2,1,0:T(8,128)S(1)} fusion(pred[]{:T(512)S(6)} %lt.226, pred[]{:T(512)S(6)} %lt.225, pred[]{:T(512)S(6)} %lt.224, f32[4,2,32,640]{3,2,1,0:T(8,128)S(1)} %fusion.18, f32[640]{0:T(1024)S(1)} %get-tuple-element.8, f32[]{:T(128)} %bitcast.1, f32[640]{0:T(1024)S(1)} %get-tuple-element.7, f32[]{:T(128)} %bitcast.73, ...), kind=kLoop, calls=%fused_computation.81 | loop fusion | flops 573440 | bytes 829459 | tf_op jit(solution)/shard_map/stack | solution.py:142
  170.5 2.6 %add_bitcast_fusion = f32[1,1,2,32,640]{4,3,2,1,0:T(8,128)S(1)} fusion(pred[]{:T(512)S(6)} %lt.229, pred[]{:T(512)S(6)} %lt.228, pred[]{:T(512)S(6)} %lt.227, f32[4,2,32,640]{3,2,1,0:T(8,128)S(1)} %fusion.18, f32[640]{0:T(1024)S(1)} %get-tuple-element.8, f32[]{:T(128)} %bitcast.1, f32[640]{0:T(1024)S(1)} %get-tuple-element.7, f32[]{:T(128)} %bitcast.73, ...), kind=kLoop, calls=%fused_computation.80 | loop fusion | flops 573440 | bytes 829459 | tf_op jit(solution)/shard_map/stack | solution.py:142
  174.0 1.4 collective-permute-start.25
  175.4 2.9 %collective-permute-done.27 = bf16[1,2,32,640]{3,2,1,0:T(8,128)(2,1)S(1)} collective-permute-done((bf16[1,2,32,640]{3,2,1,0:T(8,128)(2,1)S(1)}, bf16[1,2,32,640]{3,2,1,0:T(8,128)(2,1)S(1)}, u32[]{:S(2)}, u32[]{:S(2)}) %collective-permute-start.27) | collective-permute-done | bytes 81952 | tf_op jit(solution)/shard_map/ppermute | solution.py:30
  178.4 2.4 %collective-permute-done.25 = bf16[1,2,32,640]{3,2,1,0:T(8,128)(2,1)S(1)} collective-permute-done((bf16[1,2,32,640]{3,2,1,0:T(8,128)(2,1)S(1)}, bf16[1,2,32,640]{3,2,1,0:T(8,128)(2,1)S(1)}, u32[]{:S(2)}, u32[]{:S(2)}) %collective-permute-start.25) | collective-permute-done | bytes 81952 | tf_op jit(solution)/shard_map/ppermute | solution.py:30
  181.0 2.0 %collective-permute-start.28 = (bf16[2,1,64,640]{3,2,0,1:T(8,128)(2,1)S(1)}, bf16[2,1,64,640]{3,2,0,1:T(8,128)(2,1)S(1)}, u32[]{:S(2)}, u32[]{:S(2)}) collective-permute-start(bf16[2,1,64,640]{3,2,0,1:T(8,128)(2,1)S(1)} %fusion.34), channel_id=1, source_target_pairs={{0,1},{1,0},{2,3},{3,2},{4,5},{5,4},{6,7},{7,6},{8,9},{9,8},{10,11... | collective-permute-start | bytes 491528 | tf_op jit(solution)/shard_map/ppermute | solution.py:30
  183.0 1.0 collective-permute-done.28
  184.8 1.4 reshape.400
  (121 shorter events, 16.8 us)
Async XLA Ops:
  0.0 5.3 %copy-start = (bf16[64,15360]{1,0:T(8,128)(2,1)S(1)}, bf16[64,15360]{1,0:T(8,128)(2,1)}, u32[]{:S(2)}) copy-start(bf16[64,15360]{1,0:T(8,128)(2,1)} %param.11) | copy-start | bytes 5898244
  0.0 8.9 %copy-start.2 = (bf16[1,64,5120]{2,1,0:T(8,128)(2,1)S(1)}, bf16[1,64,5120]{2,1,0:T(8,128)(2,1)}, u32[]{:S(2)}) copy-start(bf16[1,64,5120]{2,1,0:T(8,128)(2,1)} %param.6) | copy-start | bytes 1966084
  2.9 7.0 %collective-permute-start.8 = (f32[2,1,64]{2,1,0:T(1,128)S(1)}, f32[2,1,64]{2,1,0:T(1,128)S(1)}, u32[]{:S(2)}, u32[]{:S(2)}) collective-permute-start(f32[2,1,64]{2,1,0:T(1,128)S(1)} %pad_maximum_fusion.14), channel_id=1, source_target_pairs={{0,4},{4,8},{8,12},{12,0},{1,5},{5,9},{9,13},{13,1},{2,6},{6,10},{... | collective-permute-start | bytes 1544 | tf_op jit(solution)/shard_map/ppermute | solution.py:30
  3.0 7.5 %collective-permute-start.9 = (f32[2,1,64]{2,1,0:T(1,128)S(1)}, f32[2,1,64]{2,1,0:T(1,128)S(1)}, u32[]{:S(2)}, u32[]{:S(2)}) collective-permute-start(f32[2,1,64]{2,1,0:T(1,128)S(1)} %pad_maximum_fusion.14), channel_id=1, source_target_pairs={{0,8},{4,12},{8,0},{12,4},{1,9},{5,13},{9,1},{13,5},{2,10},{6,14},... | collective-permute-start | bytes 1544 | tf_op jit(solution)/shard_map/ppermute | solution.py:30
  4.3 8.1 %collective-permute-start.10 = (f32[2,1,64]{2,1,0:T(1,128)S(1)}, f32[2,1,64]{2,1,0:T(1,128)S(1)}, u32[]{:S(2)}, u32[]{:S(2)}) collective-permute-start(f32[2,1,64]{2,1,0:T(1,128)S(1)} %pad_maximum_fusion.14), channel_id=1, source_target_pairs={{0,12},{4,0},{8,4},{12,8},{1,13},{5,1},{9,5},{13,9},{2,14},{6,2},{... | collective-permute-start | bytes 1544 | tf_op jit(solution)/shard_map/ppermute | solution.py:30
  5.8 16.4 %collective-permute-start = (f32[4,3,1280]{2,0,1:T(4,128)S(1)}, f32[4,3,1280]{2,0,1:T(4,128)S(1)}, u32[]{:S(2)}, u32[]{:S(2)}) collective-permute-start(f32[4,3,1280]{2,0,1:T(4,128)S(1)} %get-tuple-element.46), channel_id=1, source_target_pairs={{0,4},{4,8},{8,12},{12,0},{1,5},{5,9},{9,13},{13,1},{2,6},{6,10},{... | collective-permute-start | bytes 184328 | tf_op jit(solution)/shard_map/ppermute | solution.py:30
  8.9 13.3 %collective-permute-start.1 = (f32[4,3,1280]{2,0,1:T(4,128)S(1)}, f32[4,3,1280]{2,0,1:T(4,128)S(1)}, u32[]{:S(2)}, u32[]{:S(2)}) collective-permute-start(f32[4,3,1280]{2,0,1:T(4,128)S(1)} %get-tuple-element.48), channel_id=1, source_target_pairs={{0,8},{4,12},{8,0},{12,4},{1,9},{5,13},{9,1},{13,5},{2,10},{6,14},... | collective-permute-start | bytes 184328 | tf_op jit(solution)/shard_map/ppermute | solution.py:30
  9.9 8.5 %collective-permute-start.3 = (bf16[1,32,1280]{2,1,0:T(8,128)(2,1)S(1)}, bf16[1,32,1280]{2,1,0:T(8,128)(2,1)S(1)}, u32[]{:S(2)}, u32[]{:S(2)}) collective-permute-start(bf16[1,32,1280]{2,1,0:T(8,128)(2,1)S(1)} %bitcast.228), channel_id=1, source_target_pairs={{0,4},{4,8},{8,12},{12,0},{1,5},{5,9},{9,13},{13,1},{2,6},{6,10},{... | collective-permute-start | bytes 245768 | tf_op jit(solution)/shard_map/ppermute | solution.py:30
  10.4 8.0 %collective-permute-start.4 = (bf16[1,32,1280]{2,1,0:T(8,128)(2,1)S(1)}, bf16[1,32,1280]{2,1,0:T(8,128)(2,1)S(1)}, u32[]{:S(2)}, u32[]{:S(2)}) collective-permute-start(bf16[1,32,1280]{2,1,0:T(8,128)(2,1)S(1)} %bitcast.227), channel_id=1, source_target_pairs={{0,8},{4,12},{8,0},{12,4},{1,9},{5,13},{9,1},{13,5},{2,10},{6,14},... | collective-permute-start | bytes 245768 | tf_op jit(solution)/shard_map/ppermute | solution.py:30
  12.4 4.2 %collective-permute-start.11 = (f32[4,2,1,64]{3,1,2,0:T(2,128)S(1)}, f32[4,2,1,64]{3,1,2,0:T(2,128)S(1)}, u32[]{:S(2)}, u32[]{:S(2)}) collective-permute-start(f32[4,2,1,64]{3,1,2,0:T(2,128)S(1)} %pad_maximum_fusion.13), channel_id=1, source_target_pairs={{0,2},{2,0},{1,3},{3,1},{4,6},{6,4},{5,7},{7,5},{8,10},{10,8},{9,1... | collective-permute-start | bytes 6152 | tf_op jit(solution)/shard_map/ppermute | solution.py:30
  16.7 5.1 %collective-permute-start.5 = (bf16[1,32,1280]{2,1,0:T(8,128)(2,1)S(1)}, bf16[1,32,1280]{2,1,0:T(8,128)(2,1)S(1)}, u32[]{:S(2)}, u32[]{:S(2)}) collective-permute-start(bf16[1,32,1280]{2,1,0:T(8,128)(2,1)S(1)} %bitcast.229), channel_id=1, source_target_pairs={{0,12},{4,0},{8,4},{12,8},{1,13},{5,1},{9,5},{13,9},{2,14},{6,2},{... | collective-permute-start | bytes 245768 | tf_op jit(solution)/shard_map/ppermute | solution.py:30
  18.4 4.9 %collective-permute-start.2 = (f32[4,3,1280]{2,0,1:T(4,128)S(1)}, f32[4,3,1280]{2,0,1:T(4,128)S(1)}, u32[]{:S(2)}, u32[]{:S(2)}) collective-permute-start(f32[4,3,1280]{2,0,1:T(4,128)S(1)} %get-tuple-element.47), channel_id=1, source_target_pairs={{0,12},{4,0},{8,4},{12,8},{1,13},{5,1},{9,5},{13,9},{2,14},{6,2},{... | collective-permute-start | bytes 184328 | tf_op jit(solution)/shard_map/ppermute | solution.py:30
  21.8 6.0 %collective-permute-start.6 = (bf16[4,1,32,1280]{3,2,1,0:T(8,128)(2,1)S(1)}, bf16[4,1,32,1280]{3,2,1,0:T(8,128)(2,1)S(1)}, u32[]{:S(2)}, u32[]{:S(2)}) collective-permute-start(bf16[4,1,32,1280]{3,2,1,0:T(8,128)(2,1)S(1)} %get-tuple-element.41), channel_id=1, source_target_pairs={{0,2},{2,0},{1,3},{3,1},{4,6},{6,4},{5,7},{7,5},{8,10},{10,8},{9,1... | collective-permute-start | bytes 983048 | tf_op jit(solution)/shard_map/ppermute | solution.py:30
  27.8 7.2 %slice-start = ((s8[5898240]{0:T(1024)(128)(4,1)}), s8[4194304]{0:T(1024)(128)(4,1)S(1)}, s32[]{:S(2)}) async-start(s8[5898240]{0:T(1024)(128)(4,1)} %bitcast.244), calls=%async_computation | async-start | bytes 8388608
  27.9 6.7 %collective-permute-start.7 = (bf16[4,2,1,32,1280]{4,3,0,2,1:T(8,128)(2,1)S(1)}, bf16[4,2,1,32,1280]{4,3,0,2,1:T(8,128)(2,1)S(1)}, u32[]{:S(2)}, u32[]{:S(2)}) collective-permute-start(bf16[4,2,1,32,1280]{4,3,0,2,1:T(8,128)(2,1)S(1)} %get-tuple-element.36), channel_id=1, source_target_pairs={{0,1},{1,0},{2,3},{3,2},{4,5},{5,4},{6,7},{7,6},{8,9},{9,8},{10,11... | collective-permute-start | bytes 1966088 | tf_op jit(solution)/shard_map/ppermute | solution.py:30
  34.6 1.5 slice-start.1
  39.5 14.9 %copy-start.1 = (f32[4,3,128,768]{3,2,1,0:T(8,128)}, f32[4,3,128,768]{3,2,1,0:T(8,128)S(1)}, u32[]{:S(2)}) copy-start(f32[4,3,128,768]{3,2,1,0:T(8,128)S(1)} %fusion.5) | copy-start | bytes 14155780
  39.7 2.5 %collective-permute-start.12 = (f16[3,128,768]{2,1,0:T(8,128)(2,1)S(1)}, f16[3,128,768]{2,1,0:T(8,128)(2,1)S(1)}, u32[]{:S(2)}, u32[]{:S(2)}) collective-permute-start(f16[3,128,768]{2,1,0:T(8,128)(2,1)S(1)} %get-tuple-element.13), channel_id=1, source_target_pairs={{0,4},{1,5},{2,6},{3,7},{16,20},{17,21},{18,22},{19,23}} | collective-permute-start | bytes 1769480 | tf_op jit(solution)/shard_map/ppermute | solution.py:106
  40.4 14.1 %collective-permute-start.15 = (f16[3,128,768]{2,1,0:T(8,128)(2,1)S(1)}, f16[3,128,768]{2,1,0:T(8,128)(2,1)S(1)}, u32[]{:S(2)}, u32[]{:S(2)}) collective-permute-start(f16[3,128,768]{2,1,0:T(8,128)(2,1)S(1)} %get-tuple-element.14), channel_id=1, source_target_pairs={{12,8},{13,9},{14,10},{15,11},{28,24},{29,25},{30,26},{31,27}} | collective-permute-start | bytes 1769480 | tf_op jit(solution)/shard_map/ppermute | solution.py:107
  42.4 12.1 %collective-permute-start.13 = (f16[3,128,768]{2,1,0:T(8,128)(2,1)S(1)}, f16[3,128,768]{2,1,0:T(8,128)(2,1)S(1)}, u32[]{:S(2)}, u32[]{:S(2)}) collective-permute-start(f16[3,128,768]{2,1,0:T(8,128)(2,1)S(1)} %add_convert_fusion.4), channel_id=1, source_target_pairs={{0,4},{4,8},{1,5},{5,9},{2,6},{6,10},{3,7},{7,11},{16,20},{20,24},... | collective-permute-start | bytes 1769480 | tf_op jit(solution)/shard_map/ppermute | solution.py:106
  54.9 28.6 %collective-permute-start.16 = (f16[3,128,768]{2,1,0:T(8,128)(2,1)S(1)}, f16[3,128,768]{2,1,0:T(8,128)(2,1)}, u32[]{:S(2)}, u32[]{:S(2)}) collective-permute-start(f16[3,128,768]{2,1,0:T(8,128)(2,1)S(1)} %get-tuple-element.12), channel_id=1, source_target_pairs={{12,8},{8,4},{13,9},{9,5},{14,10},{10,6},{15,11},{11,7},{28,24},{2... | collective-permute-start | bytes 1769480 | tf_op jit(solution)/shard_map/ppermute | solution.py:107
  75.1 14.3 %copy-start.3 = (f32[2,768]{1,0:T(2,128)S(1)}, f32[2,768]{1,0:T(2,128)}, u32[]{:S(2)}) copy-start(f32[2,768]{1,0:T(2,128)} %param.9) | copy-start | bytes 18436
  75.1 14.3 %collective-permute-start.23 = (bf16[640,768]{1,0:T(8,128)(2,1)S(1)}, bf16[640,768]{1,0:T(8,128)(2,1)S(1)}, u32[]{:S(2)}, u32[]{:S(2)}) collective-permute-start(bf16[640,768]{1,0:T(8,128)(2,1)S(1)} %get-tuple-element.18), channel_id=1, source_target_pairs={{0,1},{1,0},{2,3},{3,2},{4,5},{5,4},{6,7},{7,6},{8,9},{9,8},{10,11... | collective-permute-start | bytes 2949128 | tf_op jit(solution)/shard_map/ppermute | solution.py:30
  77.2 16.7 %collective-permute-start.14 = (f16[3,128,768]{2,1,0:T(8,128)(2,1)S(1)}, f16[3,128,768]{2,1,0:T(8,128)(2,1)S(1)}, u32[]{:S(2)}, u32[]{:S(2)}) collective-permute-start(f16[3,128,768]{2,1,0:T(8,128)(2,1)S(1)} %get-tuple-element.11), channel_id=1, source_target_pairs={{0,4},{4,8},{8,12},{1,5},{5,9},{9,13},{2,6},{6,10},{10,14},{3,7},{... | collective-permute-start | bytes 1769480 | tf_op jit(solution)/shard_map/ppermute | solution.py:106
  85.1 14.2 %collective-permute-start.17 = (f16[3,128,768]{2,1,0:T(8,128)(2,1)S(1)}, f16[3,128,768]{2,1,0:T(8,128)(2,1)S(1)}, u32[]{:S(2)}, u32[]{:S(2)}) collective-permute-start(f16[3,128,768]{2,1,0:T(8,128)(2,1)S(1)} %add_convert_fusion.1), channel_id=1, source_target_pairs={{12,8},{8,4},{4,0},{13,9},{9,5},{5,1},{14,10},{10,6},{6,2},{15,11}... | collective-permute-start | bytes 1769480 | tf_op jit(solution)/shard_map/ppermute | solution.py:107
  91.6 67.4 %collective-permute-start.24 = (bf16[2,640,768]{2,1,0:T(8,128)(2,1)}, bf16[2,640,768]{2,1,0:T(8,128)(2,1)}, u32[]{:S(2)}, u32[]{:S(2)}) collective-permute-start(bf16[2,640,768]{2,1,0:T(8,128)(2,1)} %get-tuple-element.16), channel_id=1, source_target_pairs={{0,2},{2,0},{1,3},{3,1},{4,6},{6,4},{5,7},{7,5},{8,10},{10,8},{9,1... | collective-permute-start | bytes 5898248 | tf_op jit(solution)/shard_map/ppermute | solution.py:30
  106.4 29.0 %collective-permute-start.18 = (bf16[1,2,32,768]{3,2,1,0:T(8,128)(2,1)S(1)}, bf16[1,2,32,768]{3,2,1,0:T(8,128)(2,1)S(1)}, u32[]{:S(2)}, u32[]{:S(2)}) collective-permute-start(bf16[1,2,32,768]{3,2,1,0:T(8,128)(2,1)S(1)} %get-tuple-element.52), channel_id=1, source_target_pairs={{0,2},{2,0},{1,3},{3,1},{4,6},{6,4},{5,7},{7,5},{8,10},{10,8},{9,1... | collective-permute-start | bytes 294920 | tf_op jit(solution)/shard_map/ppermute | solution.py:30
  135.5 4.6 %collective-permute-start.19 = (bf16[2,1,2,32,768]{4,3,0,2,1:T(8,128)(2,1)S(1)}, bf16[2,1,2,32,768]{4,3,0,2,1:T(8,128)(2,1)S(1)}, u32[]{:S(2)}, u32[]{:S(2)}) collective-permute-start(bf16[2,1,2,32,768]{4,3,0,2,1:T(8,128)(2,1)S(1)} %get-tuple-element.50), channel_id=1, source_target_pairs={{0,4},{4,8},{8,12},{12,0},{1,5},{5,9},{9,13},{13,1},{2,6},{6,10},{... | collective-permute-start | bytes 589832 | tf_op jit(solution)/shard_map/ppermute | solution.py:30
  135.6 17.3 %collective-permute-start.20 = (bf16[2,1,2,32,768]{4,3,0,2,1:T(8,128)(2,1)S(1)}, bf16[2,1,2,32,768]{4,3,0,2,1:T(8,128)(2,1)S(1)}, u32[]{:S(2)}, u32[]{:S(2)}) collective-permute-start(bf16[2,1,2,32,768]{4,3,0,2,1:T(8,128)(2,1)S(1)} %get-tuple-element.50), channel_id=1, source_target_pairs={{0,8},{4,12},{8,0},{12,4},{1,9},{5,13},{9,1},{13,5},{2,10},{6,14},... | collective-permute-start | bytes 589832 | tf_op jit(solution)/shard_map/ppermute | solution.py:30
  137.3 15.5 %collective-permute-start.21 = (bf16[2,1,2,32,768]{4,3,0,2,1:T(8,128)(2,1)S(1)}, bf16[2,1,2,32,768]{4,3,0,2,1:T(8,128)(2,1)S(1)}, u32[]{:S(2)}, u32[]{:S(2)}) collective-permute-start(bf16[2,1,2,32,768]{4,3,0,2,1:T(8,128)(2,1)S(1)} %get-tuple-element.50), channel_id=1, source_target_pairs={{0,12},{4,0},{8,4},{12,8},{1,13},{5,1},{9,5},{13,9},{2,14},{6,2},{... | collective-permute-start | bytes 589832 | tf_op jit(solution)/shard_map/ppermute | solution.py:30
  153.1 5.9 %collective-permute-start.22 = (bf16[4,2,1,2,32,768]{5,4,1,3,0,2:T(8,128)(2,1)S(1)}, bf16[4,2,1,2,32,768]{5,4,1,3,0,2:T(8,128)(2,1)}, u32[]{:S(2)}, u32[]{:S(2)}) collective-permute-start(bf16[4,2,1,2,32,768]{5,4,1,3,0,2:T(8,128)(2,1)S(1)} %pad_maximum_fusion.2), channel_id=1, source_target_pairs={{0,1},{1,0},{2,3},{3,2},{4,5},{5,4},{6,7},{7,6},{8,9},{9,8},{10,11... | collective-permute-start | bytes 2359304 | tf_op jit(solution)/shard_map/ppermute | solution.py:30
  173.2 5.1 %collective-permute-start.27 = (bf16[1,2,32,640]{3,2,1,0:T(8,128)(2,1)S(1)}, bf16[1,2,32,640]{3,2,1,0:T(8,128)(2,1)S(1)}, u32[]{:S(2)}, u32[]{:S(2)}) collective-permute-start(bf16[1,2,32,640]{3,2,1,0:T(8,128)(2,1)S(1)} %get-tuple-element.38), channel_id=1, source_target_pairs={{0,4},{4,8},{8,12},{12,0},{1,5},{5,9},{9,13},{13,1},{2,6},{6,10},{... | collective-permute-start | bytes 245768 | tf_op jit(solution)/shard_map/ppermute | solution.py:30
  173.3 5.0 %collective-permute-start.26 = (bf16[1,2,32,640]{3,2,1,0:T(8,128)(2,1)S(1)}, bf16[1,2,32,640]{3,2,1,0:T(8,128)(2,1)S(1)}, u32[]{:S(2)}, u32[]{:S(2)}) collective-permute-start(bf16[1,2,32,640]{3,2,1,0:T(8,128)(2,1)S(1)} %get-tuple-element.39), channel_id=1, source_target_pairs={{0,8},{4,12},{8,0},{12,4},{1,9},{5,13},{9,1},{13,5},{2,10},{6,14},... | collective-permute-start | bytes 245768 | tf_op jit(solution)/shard_map/ppermute | solution.py:30
  174.0 6.8 %collective-permute-start.25 = (bf16[1,2,32,640]{3,2,1,0:T(8,128)(2,1)S(1)}, bf16[1,2,32,640]{3,2,1,0:T(8,128)(2,1)S(1)}, u32[]{:S(2)}, u32[]{:S(2)}) collective-permute-start(bf16[1,2,32,640]{3,2,1,0:T(8,128)(2,1)S(1)} %get-tuple-element.37), channel_id=1, source_target_pairs={{0,12},{4,0},{8,4},{12,8},{1,13},{5,1},{9,5},{13,9},{2,14},{6,2},{... | collective-permute-start | bytes 245768 | tf_op jit(solution)/shard_map/ppermute | solution.py:30
  181.0 3.0 %collective-permute-start.28 = (bf16[2,1,64,640]{3,2,0,1:T(8,128)(2,1)S(1)}, bf16[2,1,64,640]{3,2,0,1:T(8,128)(2,1)S(1)}, u32[]{:S(2)}, u32[]{:S(2)}) collective-permute-start(bf16[2,1,64,640]{3,2,0,1:T(8,128)(2,1)S(1)} %fusion.34), channel_id=1, source_target_pairs={{0,1},{1,0},{2,3},{3,2},{4,5},{5,4},{6,7},{7,6},{8,9},{9,8},{10,11... | collective-permute-start | bytes 491528 | tf_op jit(solution)/shard_map/ppermute | solution.py:30

commit v2 on v1

v2 whole, which is shorter than its diff:
```python
import functools

import jax
import jax.numpy as jnp
from jax import lax
from jax.experimental import pallas as pl
from jax.experimental.pallas import tpu as pltpu
from jax.sharding import PartitionSpec as P


HEAD_DIM = 128
FREQ = 256
STEPS = 100


sample_shift = 5.0
norm_eps = 1e-06


def sigma_of(index):
    unit = 1.0 - index.astype(jnp.float32) / jnp.float32(STEPS)
    return sample_shift * unit / (1.0 + (sample_shift - 1.0) * unit)


def embed_time(sigma_now):
    half_freq = FREQ // 2
    ranks = jnp.arange(half_freq).astype(jnp.float32)
    freqs = jnp.exp(-jnp.log(jnp.float32(10000.0)) * ranks / jnp.float32(half_freq))
    angles = (1000.0 * sigma_now)[:, None] * freqs[None, :]
    return jnp.concatenate([jnp.cos(angles), jnp.sin(angles)], axis=1).astype(jnp.bfloat16)


def turn(block, axis, distance):
    size = lax.axis_size(axis)
    return lax.ppermute(block, axis, [(i, (i + distance) % size) for i in range(size)])


def take(array, index, dim=0):
    return lax.dynamic_index_in_dim(array, index, dim, keepdims=False)


def head_norm(values, gain):
    meansq = jnp.mean(values * values, axis=-1, keepdims=True)
    return (values * lax.rsqrt(meansq + norm_eps) * gain).astype(jnp.bfloat16)


def attend_kernel(n_seq, heads, *refs):
    gain_ref, parts, outs = refs[0], refs[1 : 1 + n_seq], refs[1 + n_seq :]
    inv_root = 1.0 / jnp.sqrt(jnp.float32(HEAD_DIM))
    rows = parts[0].shape[2]
    for h in range(heads):
        lanes = pl.ds(h * HEAD_DIM, HEAD_DIM)
        q, k, v = (
            jnp.concatenate([p[c, 0, :, lanes] for p in parts], axis=0) for c in range(3)
        )
        q = head_norm(q, gain_ref[0:1, lanes])
        k = head_norm(k, gain_ref[1:2, lanes])
        scores = lax.dot_general(
            q, k, (((1,), (1,)), ((), ())), preferred_element_type=jnp.float32
        )
        expo = jnp.exp(scores * inv_root)
        probs = (expo / jnp.sum(expo, axis=-1, keepdims=True)).astype(jnp.bfloat16)
        attn = jnp.dot(
            probs, v.astype(jnp.bfloat16), preferred_element_type=jnp.float32
        ).astype(jnp.bfloat16)
        for j, out in enumerate(outs):
            out[0, :, lanes] = attn[j * rows : (j + 1) * rows]


def attend(parts, gain):
    n_seq = len(parts)
    _, frames, rows, cols = parts[0].shape
    heads = cols // HEAD_DIM
    group = 3 if heads % 3 == 0 else 1
    width = group * HEAD_DIM
    tokens = rows * n_seq
    out = jax.ShapeDtypeStruct((frames, rows, cols), jnp.bfloat16)
    return pl.pallas_call(
        functools.partial(attend_kernel, n_seq, group),
        grid=(frames, heads // group),
        in_specs=[pl.BlockSpec((2, width), lambda f, h: (0, h))]
        + [pl.BlockSpec((3, 1, rows, width), lambda f, h: (0, f, 0, h))] * n_seq,
        out_specs=[pl.BlockSpec((1, rows, width), lambda f, h: (f, 0, h))] * n_seq,
        out_shape=[out] * n_seq,
        cost_estimate=pl.CostEstimate(
            flops=4 * frames * heads * tokens * tokens * HEAD_DIM,
            bytes_accessed=14 * frames * tokens * cols,
            transcendentals=frames * heads * tokens * tokens,
        ),
        name="attend",
    )(gain, *parts)


def out_kernel(dims, place_ref, coef_ref, *refs):
    n_tm, n_seq, n_mp, frames, part, cols = dims
    attn_refs = refs[: n_tm * n_mp]
    w_refs = refs[n_tm * n_mp : n_tm * n_mp + n_seq * n_mp]
    own_ref, moved_ref, rows_scr, sum_scr = refs[n_tm * n_mp + n_seq * n_mp :]
    z, m = place_ref[0], place_ref[1]
    block = n_mp * part
    per = frames * block

    @pl.when(pl.program_id(0) == 0)
    def _():
        for k in range(n_tm):
            for l in range(n_mp):
                piece = attn_refs[k * n_mp + l]
                for j in range(n_seq):
                    for f in range(frames):
                        for i in range(n_mp):
                            source = (i - l) % n_mp * part
                            at = k * per + f * block + i * part
                            lane = (j * n_mp + l) * cols
                            rows_scr[at : at + part, lane : lane + cols] = piece[
                                j, f, source : source + part, :
                            ]

    total = None
    for j in range(n_seq):
        for l in range(n_mp):
            lane = (j * n_mp + l) * cols
            product = lax.dot_general(
                rows_scr[:, lane : lane + cols],
                w_refs[j * n_mp + l][...],
                (((1,), (1,)), ((), ())),
                preferred_element_type=jnp.float32,
            )
            total = product if total is None else total + product
    for k in range(n_tm):
        own = lax.rem(z - k + n_tm, n_tm)
        sum_scr[own] = total[k * per : (k + 1) * per]
    running = None
    for s in range(n_tm):
        k = lax.rem(z - s + n_tm, n_tm)
        for f in range(frames):
            drift = sum_scr[s, f * block : (f + 1) * block] * coef_ref[k, f : f + 1]
            running = drift if running is None else running + drift
            for i in range(n_mp):
                at = pl.multiple_of(lax.rem(m - i + n_mp, n_mp) * part, part)
                piece = running[i * part : (i + 1) * part]
                moved_ref[k, f, pl.ds(at, part), :] = piece.astype(jnp.bfloat16)

                @pl.when(k == 0)
                def _():
                    own_ref[f, pl.ds(at, part), :] = piece


def project(attn, weights, coef, place, dims):
    n_tm, n_seq, n_mp, frames, part, cols = dims
    half = weights[0][0].shape[0]
    step = 128 if half % 128 == 0 else half
    tok = n_mp * part
    rows = n_tm * frames * tok
    deep = n_seq * n_mp * cols
    return pl.pallas_call(
        functools.partial(out_kernel, dims),
        grid_spec=pltpu.PrefetchScalarGridSpec(
            num_scalar_prefetch=1,
            grid=(half // step,),
            in_specs=[pl.BlockSpec((n_tm, frames, step), lambda e, p: (0, 0, e))]
            + [pl.BlockSpec((n_seq, frames, tok, cols), lambda e, p: (0, 0, 0, 0))]
            * (n_tm * n_mp)
            + [pl.BlockSpec((step, cols), lambda e, p: (e, 0))] * (n_seq * n_mp),
            out_specs=[
                pl.BlockSpec((frames, tok, step), lambda e, p: (0, 0, e)),
                pl.BlockSpec((n_tm, frames, tok, step), lambda e, p: (0, 0, 0, e)),
            ],
            scratch_shapes=[
                pltpu.VMEM((rows, deep), jnp.bfloat16),
                pltpu.VMEM((n_tm, frames * tok, step), jnp.float32),
            ],
        ),
        out_shape=[
            jax.ShapeDtypeStruct((frames, tok, half), jnp.float32),
            jax.ShapeDtypeStruct((n_tm, frames, tok, half), jnp.bfloat16),
        ],
        cost_estimate=pl.CostEstimate(
            flops=2 * rows * deep * half, bytes_accessed=2 * (rows + half) * deep, transcendentals=0
        ),
        name="project",
    )(place, coef, *[a for k in attn for a in k], *[w for j in weights for w in j])


def sweep(states, start_step, w_qkv, qk_gain, w_out, time_proj):
    frames, tok, width = states.shape
    n_tm, n_seq, n_mp = (lax.axis_size(name) for name in ("tm", "seq", "mp"))
    z, m = lax.axis_index("tm"), lax.axis_index("mp")
    part = tok // n_mp
    depth, cols = w_qkv.shape[1:]
    half = depth // n_mp
    window = frames * n_tm
    freq_rows = time_proj.shape[0]

    mine = lax.dynamic_slice_in_dim(states, m * part, part, 1).reshape(frames, part, n_tm, depth)
    raw = [take(mine, z, 2)]
    for k in range(1, n_tm):
        raw.append(turn(take(mine, (z + k) % n_tm, 2), "tm", k))
    raw = jnp.stack(raw)
    sides = [raw]
    for j in range(1, n_seq):
        sides.append(turn(raw, "seq", j))
    rows = []
    for side in sides:
        rows.append([side] + [turn(side, "mp", i) for i in range(1, n_mp)])

    field = states.astype(jnp.float32)
    mean = jnp.mean(field, axis=-1)
    centred = field - mean[..., None]
    var = jnp.mean(centred * centred, axis=-1)
    stats = jnp.stack([mean, lax.rsqrt(var + norm_eps)])
    stats = jnp.stack([stats] + [turn(stats, "seq", j) for j in range(1, n_seq)])
    extra = stats.reshape(-1)
    extra_rows = -(-extra.shape[0] // depth)
    extra = jnp.pad(extra, (0, extra_rows * depth - extra.shape[0])).reshape(extra_rows, depth)

    steps_idx = start_step[0] + jnp.arange(window)
    sigma_now = sigma_of(steps_idx)
    step_size = sigma_of(steps_idx + 1) - sigma_now
    emb = embed_time(sigma_now)
    emb_cols = lax.dynamic_slice_in_dim(emb, z * freq_rows, freq_rows, 1)
    partial = jnp.dot(emb_cols, time_proj, preferred_element_type=jnp.float32)
    partial = partial.reshape(window * 3, n_tm, depth)
    modulation = take(partial, z, 1)
    extras = [extra]
    for k in range(1, n_tm):
        block = jnp.concatenate([take(partial, (z + k) % n_tm, 1), extra])
        block = turn(block, "tm", k)
        modulation = modulation + block[: window * 3]
        extras.append(block[window * 3 :])
    modulation = modulation.reshape(n_tm, frames, 3, depth)
    modulation = jnp.stack([take(modulation, (z - k) % n_tm) for k in range(n_tm)])
    sizes = step_size.reshape(n_tm, frames)
    stats = jnp.stack(extras).reshape(n_tm, -1)[:, : n_seq * 2 * frames * tok]
    stats = stats.reshape(n_tm, n_seq, 2, frames, n_mp, part)

    shift, scale, gate = (modulation[:, :, c] for c in range(3))

    def hidden_of(j):
        blocks = []
        for i in range(n_mp):
            stat = take(stats[:, j], (m - i) % n_mp, 3)[..., None]
            normed = (rows[j][i].astype(jnp.float32) - stat[:, 0]) * stat[:, 1]
            blocks.append(normed * (1.0 + scale[:, :, None]) + shift[:, :, None])
        return jnp.stack(blocks, axis=2).astype(jnp.bfloat16)

    proj, right, left = [], [], []
    for j in range(n_seq):
        hidden = hidden_of(j).reshape(n_tm, frames * tok, depth)
        proj.append(jnp.einsum("krd,cdh->kcrh", hidden, w_qkv, preferred_element_type=jnp.float32))
        right.append(None)
        left.append(None)
    for t in range(n_tm - 1):
        for j in range(n_seq):
            send_right, send_left = proj[j][(t + 1) % n_tm], proj[j][n_tm - 1 - t]
            if t:
                right[j], left[j] = lax.optimization_barrier((right[j], left[j]))
                send_right = send_right + right[j].astype(jnp.float32)
                send_left = send_left + left[j].astype(jnp.float32)
            send_right, send_left = send_right.astype(jnp.float16), send_left.astype(jnp.float16)
            right[j] = lax.ppermute(send_right, "tm", [(i, i + 1) for i in range(t + 1)])
            left[j] = lax.ppermute(
                send_left, "tm", [(n_tm - 1 - i, n_tm - 2 - i) for i in range(t + 1)]
            )
    parts = [
        (p[0] + r.astype(jnp.float32) + l.astype(jnp.float32)).reshape(3, frames, tok, cols)
        for p, r, l in zip(proj, right, left)
    ]
    attn = attend(parts, qk_gain)

    attn = jnp.stack([attn[0]] + [turn(attn[j], "seq", -j) for j in range(1, n_seq)])
    gathered = [attn]
    for k in range(1, n_tm):
        gathered.append(turn(attn, "tm", k))
    gathered = [[g] + [turn(g, "mp", i) for i in range(1, n_mp)] for g in gathered]

    share = w_out.reshape(n_mp, half, cols)
    shares = [take(share, m)]
    shares += [turn(take(share, (m + i) % n_mp), "mp", i) for i in range(1, n_mp)]
    weights = [shares]
    for j in range(1, n_seq):
        weights.append([turn(s, "seq", -j) for s in shares])

    gate_own = take(gate.reshape(n_tm, frames, n_mp, half), m, 2)
    coef = jnp.stack([take(sizes, (z - k) % n_tm) for k in range(n_tm)])[..., None] * gate_own
    place = jnp.stack([z, m]).astype(jnp.int32)
    own, moved = project(
        gathered, weights, coef, place, (n_tm, n_seq, n_mp, frames, part, cols)
    )
    arrived = [own]
    for k in range(1, n_tm):
        arrived.append(turn(moved[k], "tm", -k).astype(jnp.float32))
    by_slice = jnp.stack(arrived)
    by_slice = jnp.stack([take(by_slice, (s - z) % n_tm) for s in range(n_tm)])
    by_slice = by_slice.reshape(n_mp, n_tm // n_mp, frames, tok, half)
    final = [take(by_slice, m)]
    for i in range(1, n_mp):
        final.append(turn(take(by_slice, (m + i) % n_mp).astype(jnp.bfloat16), "mp", i).astype(jnp.float32))
    final = jnp.stack(final)
    final = jnp.stack([take(final, (m - i) % n_mp) for i in range(n_mp)])
    return final.transpose(2, 3, 1, 0, 4).reshape(frames, tok, width // n_mp)


def solution(mesh):
    return jax.shard_map(
        sweep,
        mesh=mesh,
        in_specs=(
            P(("group", "tm"), "seq", None),
            P("group"),
            P(None, "tm", ("seq", "mp")),
            P(None, ("seq", "mp")),
            P("tm", ("seq", "mp")),
            P("tm", None),
        ),
        out_specs=P(("group", "tm"), "seq", "mp"),
        check_vma=False,
    )
```

time: 189 us -> 169 us (0.89)
  waiting for transfers between devices: 82.1 us -> 56.8 us
  starting transfers between devices: 56.4 us -> 68.8 us
  Pallas kernels: 0 us -> 11.3 us
  other arithmetic: 24.1 us -> 14 us
  local copies, waits for them, and re-layouts: 13.7 us -> 7.97 us
    ppermute x6 -> x12, waiting for transfers between devices: 22.9 us -> 5.25 us  [the longest x6 5.12 us: sweep(): lax.ppermute(send_left, 'tm', [(n_tm - 1 - i, n_tm - 2 - i) for i in rang...]
    pallas_call x0 -> x2, Pallas kernels: none -> 11.3 us  [the longest x1 7.64 us: project(): pl.pallas_call(functools.partial(out_kernel, dims), grid_spec=pltpu.Prefe...]
    ppermute x23 -> x25, starting transfers between devices: 29.1 us -> 39.6 us  [turn(): lax.ppermute(block, axis, [(i, (i + distance) % size) for i in range(size)])]
    ppermute x23 -> x25, waiting for transfers between devices: 59.3 us -> 51.5 us  [turn(): lax.ppermute(block, axis, [(i, (i + distance) % size) for i in range(size)])]
    another operation x25 -> x18, other arithmetic: 13.4 us -> 6.38 us  [the longest x1 2.56 us: sweep(): jnp.stack([take(sizes, (z - k) % n_tm) for k in range(n_tm)])[..., None]]
    slice x9 -> x6, local copies, waits for them, and re-layouts: 2.98 us -> 0.03 us  [the longest x4 0.02 us: hidden_of(): normed = (rows[j][i].astype(jnp.float32) - stat[:, 0]) * stat[:, 1]]
    ppermute x3 -> x0, other arithmetic: 1.99 us -> none  [turn(): lax.ppermute(block, axis, [(i, (i + distance) % size) for i in range(size)])]
    ppermute x6 -> x12, starting transfers between devices: 27.2 us -> 29.2 us  [the longest x6 23.9 us: sweep(): lax.ppermute(send_left, 'tm', [(n_tm - 1 - i, n_tm - 2 - i) for i in rang...]
  transfers between devices with their start and end apart: 29 -> 37, of which waited for: 14 -> 14; matrix products, arithmetic and copies ran while one was open for 12% -> 9% of each run, Pallas kernels for 0% -> 2%
where the time goes in v2:
time: 169 us; the launch traced here: 167 us
  starting transfers between devices  68.8 us (41%)
  waiting for transfers between devices  56.8 us (34%)
  other arithmetic  14 us (8%)
  Pallas kernels  11.3 us (7%)
  local copies, waits for them, and re-layouts  7.97 us (5%)
  matrix products  6.65 us (4%)
    ppermute x25, waiting for transfers between devices, turn(): lax.ppermute(block, axis, [(i, (i + distance) % size) for i in range(size)])  51.5 us
    ppermute x25, starting transfers between devices, turn(): lax.ppermute(block, axis, [(i, (i + distance) % size) for i in range(size)])  39.6 us
    ppermute x6, starting transfers between devices, sweep(): lax.ppermute(send_left, 'tm', [(n_tm - 1 - i, n_tm - 2 - i) for i in rang...  23.9 us
    pallas_call x1, Pallas kernels, project(): pl.pallas_call(functools.partial(out_kernel, dims), grid_spec=pltpu.Prefe...  7.64 us
    dot_general x2, matrix products, sweep(): jnp.einsum('krd,cdh->kcrh', hidden, w_qkv, preferred_element_type=jnp.flo...  6.21 us
    ppermute x6, starting transfers between devices, sweep(): lax.ppermute(send_right, 'tm', [(i, i + 1) for i in range(t + 1)])  5.3 us
    ppermute x6, waiting for transfers between devices, sweep(): lax.ppermute(send_left, 'tm', [(n_tm - 1 - i, n_tm - 2 - i) for i in rang...  5.12 us
    pallas_call x1, Pallas kernels, attend(): pl.pallas_call(functools.partial(attend_kernel, n_seq, group), grid=(fram...  3.62 us
  transfers between devices with their start and end apart: 37, of which 14 were waited for; matrix products, arithmetic and copies ran while one was open for 9% of the time, Pallas kernels for 2%

profile of v2, /device:TPU:25, one launch (start us, length us, event | category | flops | bytes accessed | tf_op | source)
XLA Modules:
  0.0 167.1 jit_solution(11440394445685887609)
XLA Ops:
  0.0 1.4 convert_reduce_fusion
  1.4 1.4 fusion.11
  2.9 1.3 collective-permute-start
  4.2 1.0 constant_dynamic-slice_fusion.14
  7.5 0.7 constant_dynamic-slice_fusion.13
  8.2 3.1 %collective-permute-start.4 = (bf16[1,32,1280]{2,1,0:T(8,128)(2,1)S(1)}, bf16[1,32,1280]{2,1,0:T(8,128)(2,1)S(1)}, u32[]{:S(2)}, u32[]{:S(2)}) collective-permute-start(bf16[1,32,1280]{2,1,0:T(8,128)(2,1)S(1)} %bitcast.224), channel_id=1, source_target_pairs={{0,4},{4,8},{8,12},{12,0},{1,5},{5,9},{9,13},{13,1},{2,6},{6,10},{... | collective-permute-start | bytes 245768 | tf_op jit(solution)/shard_map/ppermute | solution.py:35
  11.9 2.3 %collective-permute-start.2 = (f32[13,1280]{1,0:T(8,128)S(1)}, f32[13,1280]{1,0:T(8,128)S(1)}, u32[]{:S(2)}, u32[]{:S(2)}) collective-permute-start(f32[13,1280]{1,0:T(8,128)S(1)} %get-tuple-element.79), channel_id=1, source_target_pairs={{0,8},{4,12},{8,0},{12,4},{1,9},{5,13},{9,1},{13,5},{2,10},{6,14},... | collective-permute-start | bytes 199688 | tf_op jit(solution)/shard_map/ppermute | solution.py:35
  14.1 2.2 %collective-permute-start.1 = (f32[13,1280]{1,0:T(8,128)S(1)}, f32[13,1280]{1,0:T(8,128)S(1)}, u32[]{:S(2)}, u32[]{:S(2)}) collective-permute-start(f32[13,1280]{1,0:T(8,128)S(1)} %get-tuple-element.78), channel_id=1, source_target_pairs={{0,4},{4,8},{8,12},{12,0},{1,5},{5,9},{9,13},{13,1},{2,6},{6,10},{... | collective-permute-start | bytes 199688 | tf_op jit(solution)/shard_map/ppermute | solution.py:35
  16.4 5.9 %collective-permute-done.2 = f32[13,1280]{1,0:T(8,128)S(1)} collective-permute-done((f32[13,1280]{1,0:T(8,128)S(1)}, f32[13,1280]{1,0:T(8,128)S(1)}, u32[]{:S(2)}, u32[]{:S(2)}) %collective-permute-start.2) | collective-permute-done | bytes 66592 | tf_op jit(solution)/shard_map/ppermute | solution.py:35
  23.8 2.5 %collective-permute-start.7 = (bf16[4,1,32,1280]{3,2,0,1:T(8,128)(2,1)S(1)}, bf16[4,1,32,1280]{3,2,0,1:T(8,128)(2,1)S(1)}, u32[]{:S(2)}, u32[]{:S(2)}) collective-permute-start(bf16[4,1,32,1280]{3,2,0,1:T(8,128)(2,1)S(1)} %pad_maximum_fusion.4), channel_id=1, source_target_pairs={{0,1},{1,0},{2,3},{3,2},{4,5},{5,4},{6,7},{7,6},{8,9},{9,8},{10,11... | collective-permute-start | bytes 983048 | tf_op jit(solution)/shard_map/ppermute | solution.py:35
  26.3 4.2 %collective-permute-done.14 = bf16[4,1,32,1280]{3,2,0,1:T(8,128)(2,1)S(1)} collective-permute-done((bf16[4,1,32,1280]{3,2,0,1:T(8,128)(2,1)S(1)}, bf16[4,1,32,1280]{3,2,0,1:T(8,128)(2,1)S(1)}, u32[]{:S(2)}, u32[]{:S(2)}) %collective-permute-start.14) | collective-permute-done | bytes 327712 | tf_op jit(solution)/shard_map/ppermute | solution.py:35
  30.5 3.1 %collective-permute-start.15 = (bf16[4,1,32,1280]{3,2,0,1:T(8,128)(2,1)S(1)}, bf16[4,1,32,1280]{3,2,0,1:T(8,128)(2,1)S(1)}, u32[]{:S(2)}, u32[]{:S(2)}) collective-permute-start(bf16[4,1,32,1280]{3,2,0,1:T(8,128)(2,1)S(1)} %collective-permute-done.14), channel_id=1, source_target_pairs={{0,1},{1,0},{2,3},{3,2},{4,5},{5,4},{6,7},{7,6},{8,9},{9,8},{10,11... | collective-permute-start | bytes 983048 | tf_op jit(solution)/shard_map/ppermute | solution.py:35
  33.9 1.0 collective-permute-done.15
  35.5 4.5 %fusion.7 = f32[4,3,64,768]{3,2,1,0:T(8,128)S(1)} fusion(bf16[4,64,1280,1]{2,1,3,0:T(8,128)(2,1)S(1)} %bitcast.207, bf16[3,1280,768]{2,1,0:T(8,128)(2,1)} %param.8), kind=kOutput, calls=%fused_computation.5 | convolution fusion | flops 1509949440 | bytes 8912896 | tf_op jit(solution)/shard_map/krd,cdh->kcrh/dot_general | solution.py:249
  40.8 3.6 %collective-permute-start.17 = (f16[3,64,768]{2,1,0:T(8,128)(2,1)S(1)}, f16[3,64,768]{2,1,0:T(8,128)(2,1)S(1)}, u32[]{:S(2)}, u32[]{:S(2)}) collective-permute-start(f16[3,64,768]{2,1,0:T(8,128)(2,1)S(1)} %get-tuple-element.33), channel_id=1, source_target_pairs={{12,8},{13,9},{14,10},{15,11},{28,24},{29,25},{30,26},{31,27}} | collective-permute-start | bytes 884744 | tf_op jit(solution)/shard_map/ppermute | solution.py:261
  44.5 1.7 %fusion.4 = f32[4,3,64,768]{3,2,1,0:T(8,128)S(1)} fusion(bf16[4,64,1280,1]{2,1,3,0:T(8,128)(2,1)S(1)} %bitcast.206, bf16[3,1280,768]{2,1,0:T(8,128)(2,1)S(1)} %bitcast.243), kind=kOutput, calls=%fused_computation.4 | convolution fusion | flops 1509949440 | bytes 8912896 | tf_op jit(solution)/shard_map/krd,cdh->kcrh/dot_general | solution.py:249
  47.0 1.3 collective-permute-start.9
  48.5 0.7 collective-permute-start.30
  49.2 1.2 collective-permute-done.17
  51.2 4.7 %collective-permute-start.19 = (f16[3,64,768]{2,1,0:T(8,128)(2,1)S(1)}, f16[3,64,768]{2,1,0:T(8,128)(2,1)S(1)}, u32[]{:S(2)}, u32[]{:S(2)}) collective-permute-start(f16[3,64,768]{2,1,0:T(8,128)(2,1)S(1)} %get-tuple-element.31), channel_id=1, source_target_pairs={{12,8},{8,4},{13,9},{9,5},{14,10},{10,6},{15,11},{11,7},{28,24},{2... | collective-permute-start | bytes 884744 | tf_op jit(solution)/shard_map/ppermute | solution.py:261
  55.9 0.7 collective-permute-done.9
  57.5 4.7 %collective-permute-start.11 = (f16[3,64,768]{2,1,0:T(8,128)(2,1)S(1)}, f16[3,64,768]{2,1,0:T(8,128)(2,1)S(1)}, u32[]{:S(2)}, u32[]{:S(2)}) collective-permute-start(f16[3,64,768]{2,1,0:T(8,128)(2,1)S(1)} %get-tuple-element.37), channel_id=1, source_target_pairs={{12,8},{8,4},{13,9},{9,5},{14,10},{10,6},{15,11},{11,7},{28,24},{2... | collective-permute-start | bytes 884744 | tf_op jit(solution)/shard_map/ppermute | solution.py:261
  62.6 1.3 collective-permute-start.20
  63.9 4.8 %collective-permute-start.21 = (f16[3,64,768]{2,1,0:T(8,128)(2,1)S(1)}, f16[3,64,768]{2,1,0:T(8,128)(2,1)S(1)}, u32[]{:S(2)}, u32[]{:S(2)}) collective-permute-start(f16[3,64,768]{2,1,0:T(8,128)(2,1)S(1)} %get-tuple-element.30), channel_id=1, source_target_pairs={{12,8},{8,4},{4,0},{13,9},{9,5},{5,1},{14,10},{10,6},{6,2},{15,11}... | collective-permute-start | bytes 884744 | tf_op jit(solution)/shard_map/ppermute | solution.py:261
  68.9 1.3 collective-permute-start.12
  70.2 4.8 %collective-permute-start.13 = (f16[3,64,768]{2,1,0:T(8,128)(2,1)S(1)}, f16[3,64,768]{2,1,0:T(8,128)(2,1)S(1)}, u32[]{:S(2)}, u32[]{:S(2)}) collective-permute-start(f16[3,64,768]{2,1,0:T(8,128)(2,1)S(1)} %get-tuple-element.36), channel_id=1, source_target_pairs={{12,8},{8,4},{4,0},{13,9},{9,5},{5,1},{14,10},{10,6},{6,2},{15,11}... | collective-permute-start | bytes 884744 | tf_op jit(solution)/shard_map/ppermute | solution.py:261
  75.4 1.1 collective-permute-start.32
  76.5 1.0 fusion.14.refs_2_
  77.6 3.0 %collective-permute-done.13 = f16[3,64,768]{2,1,0:T(8,128)(2,1)S(1)} collective-permute-done((f16[3,64,768]{2,1,0:T(8,128)(2,1)S(1)}, f16[3,64,768]{2,1,0:T(8,128)(2,1)S(1)}, u32[]{:S(2)}, u32[]{:S(2)}) %collective-permute-start.13) | collective-permute-done | bytes 294944 | tf_op jit(solution)/shard_map/ppermute | solution.py:261
  80.6 1.0 fusion.17.refs_1_
  81.5 3.6 %attend.1 = (bf16[1,64,768]{2,1,0:T(8,128)(2,1)}, bf16[1,64,768]{2,1,0:T(8,128)(2,1)}) custom-call(f32[2,768]{1,0:T(2,128)} %refs_0_.1, f32[3,1,64,768]{3,2,1,0:T(8,128)} %fusion.17.refs_1_, f32[3,1,64,768]{3,2,1,0:T(8,128)} %fusion.14.refs_2_), custom_call_target="tpu_custom_call" | custom-call | flops 50331648 | bytes 1376256 | tf_op jit(solution)/shard_map/attend/pallas_call | solution.py:78
  86.1 32.4 %collective-permute-done.22 = bf16[1,64,768]{2,1,0:T(8,128)(2,1)S(1)} collective-permute-done((bf16[1,64,768]{2,1,0:T(8,128)(2,1)}, bf16[1,64,768]{2,1,0:T(8,128)(2,1)S(1)}, u32[]{:S(2)}, u32[]{:S(2)}) %collective-permute-start.22) | collective-permute-done | bytes 98336 | tf_op jit(solution)/shard_map/ppermute | solution.py:35
  118.5 0.9 pad_maximum_fusion.5.refs_0_
  119.4 2.1 %collective-permute-start.24 = (bf16[2,1,64,768]{3,2,1,0:T(8,128)(2,1)S(1)}, bf16[2,1,64,768]{3,2,1,0:T(8,128)(2,1)S(1)}, u32[]{:S(2)}, u32[]{:S(2)}) collective-permute-start(bf16[2,1,64,768]{3,2,1,0:T(8,128)(2,1)S(1)} %pad_maximum_fusion.5.refs_0_), channel_id=1, source_target_pairs={{0,4},{4,8},{8,12},{12,0},{1,5},{5,9},{9,13},{13,1},{2,6},{6,10},{... | collective-permute-start | bytes 589832 | tf_op jit(solution)/shard_map/ppermute | solution.py:35
  121.5 0.7 collective-permute-start.26
  122.2 1.4 collective-permute-start.28
  124.2 2.6 %maximum_bitcast_fusion.2 = f32[4]{0:T(128)S(1)} fusion(f32[1,1]{0,1:T(1,128)} %bitcast.6, f32[1,1]{0,1:T(1,128)} %bitcast.5, f32[1,1]{0,1:T(1,128)} %bitcast.4, f32[1,1]{0,1:T(1,128)} %bitcast.3), kind=kLoop, calls=%fused_computation.126 | loop fusion | flops 12 | bytes 32 | tf_op jit(solution)/shard_map/stack | solution.py:284
  126.8 4.4 %collective-permute-start.23 = (bf16[2,1,64,768]{3,2,1,0:T(8,128)(2,1)S(1)}, bf16[2,1,64,768]{3,2,1,0:T(8,128)(2,1)S(1)}, u32[]{:S(2)}, u32[]{:S(2)}) collective-permute-start(bf16[2,1,64,768]{3,2,1,0:T(8,128)(2,1)S(1)} %pad_maximum_fusion.5.refs_0_), channel_id=1, source_target_pairs={{0,1},{1,0},{2,3},{3,2},{4,5},{5,4},{6,7},{7,6},{8,9},{9,8},{10,11... | collective-permute-start | bytes 589832 | tf_op jit(solution)/shard_map/ppermute | solution.py:35
  131.7 9.0 %collective-permute-start.27 = (bf16[2,1,64,768]{3,2,1,0:T(8,128)(2,1)S(1)}, bf16[2,1,64,768]{3,2,1,0:T(8,128)(2,1)S(1)}, u32[]{:S(2)}, u32[]{:S(2)}) collective-permute-start(bf16[2,1,64,768]{3,2,1,0:T(8,128)(2,1)S(1)} %collective-permute-done.26.refs_4_), channel_id=1, source_target_pairs={{0,1},{1,0},{2,3},{3,2},{4,5},{5,4},{6,7},{7,6},{8,9},{9,8},{10,11... | collective-permute-start | bytes 589832 | tf_op jit(solution)/shard_map/ppermute | solution.py:35
  140.7 1.4 bitcast_multiply_fusion.coef_ref
  143.6 7.6 %project.1 = (f32[1,64,640]{2,1,0:T(8,128)}, bf16[4,1,64,640]{3,2,1,0:T(8,128)(2,1)}) custom-call(s32[2]{0:T(128)} %pad_add_fusion.place_ref, f32[4,1,640]{2,1,0:T(1,128)} %bitcast_multiply_fusion.coef_ref, bf16[2,1,64,768]{3,2,1,0:T(8,128)(2,1)} %copy-done.3, bf16[2,1,64,768]{3,2,1,0:T(8,128)(2,1)} %copy-done.7, bf16[2,1,64,768]{3,2,1,0:T(8,128)(2,1)} %copy-done.4, ...), custom_call_target="tpu_custom_call" | custom-call | flops 1006632960 | bytes 5505024 | tf_op jit(solution)/shard_map/project/pallas_call | solution.py:155
  151.2 1.0 slice_bitcast_fusion.10
  152.4 1.8 %collective-permute-start.34 = (bf16[1,64,640]{2,1,0:T(8,128)(2,1)S(1)}, bf16[1,64,640]{2,1,0:T(8,128)(2,1)S(1)}, u32[]{:S(2)}, u32[]{:S(2)}) collective-permute-start(bf16[1,64,640]{2,1,0:T(8,128)(2,1)S(1)} %get-tuple-element.51), channel_id=1, source_target_pairs={{0,8},{4,12},{8,0},{12,4},{1,9},{5,13},{9,1},{13,5},{2,10},{6,14},... | collective-permute-start | bytes 245768 | tf_op jit(solution)/shard_map/ppermute | solution.py:35
  154.2 1.3 collective-permute-start.33
  155.6 6.5 %collective-permute-done.34 = bf16[1,64,640]{2,1,0:T(8,128)(2,1)S(1)} collective-permute-done((bf16[1,64,640]{2,1,0:T(8,128)(2,1)S(1)}, bf16[1,64,640]{2,1,0:T(8,128)(2,1)S(1)}, u32[]{:S(2)}, u32[]{:S(2)}) %collective-permute-start.34) | collective-permute-done | bytes 81952 | tf_op jit(solution)/shard_map/ppermute | solution.py:35
  162.1 1.0 pad_maximum_fusion.2
  163.9 1.0 collective-permute-done.36
  165.7 1.4 reshape.339
  (137 shorter events, 14.1 us)
Async XLA Ops:
  0.0 6.0 %copy-start = (bf16[64,15360]{1,0:T(8,128)(2,1)S(1)}, bf16[64,15360]{1,0:T(8,128)(2,1)}, u32[]{:S(2)}) copy-start(bf16[64,15360]{1,0:T(8,128)(2,1)} %param.11) | copy-start | bytes 5898244
  2.9 4.2 %collective-permute-start = (f32[2,1,64]{2,1,0:T(1,128)S(1)}, f32[2,1,64]{2,1,0:T(1,128)S(1)}, u32[]{:S(2)}, u32[]{:S(2)}) collective-permute-start(f32[2,1,64]{2,1,0:T(1,128)S(1)} %pad_maximum_fusion.14), channel_id=1, source_target_pairs={{0,2},{2,0},{1,3},{3,1},{4,6},{6,4},{5,7},{7,5},{8,10},{10,8},{9,1... | collective-permute-start | bytes 1544 | tf_op jit(solution)/shard_map/ppermute | solution.py:35
  7.3 6.9 %collective-permute-start.3 = (f32[13,1280]{1,0:T(8,128)S(1)}, f32[13,1280]{1,0:T(8,128)S(1)}, u32[]{:S(2)}, u32[]{:S(2)}) collective-permute-start(f32[13,1280]{1,0:T(8,128)S(1)} %get-tuple-element.80), channel_id=1, source_target_pairs={{0,12},{4,0},{8,4},{12,8},{1,13},{5,1},{9,5},{13,9},{2,14},{6,2},{... | collective-permute-start | bytes 199688 | tf_op jit(solution)/shard_map/ppermute | solution.py:35
  8.2 15.1 %collective-permute-start.4 = (bf16[1,32,1280]{2,1,0:T(8,128)(2,1)S(1)}, bf16[1,32,1280]{2,1,0:T(8,128)(2,1)S(1)}, u32[]{:S(2)}, u32[]{:S(2)}) collective-permute-start(bf16[1,32,1280]{2,1,0:T(8,128)(2,1)S(1)} %bitcast.224), channel_id=1, source_target_pairs={{0,4},{4,8},{8,12},{12,0},{1,5},{5,9},{9,13},{13,1},{2,6},{6,10},{... | collective-permute-start | bytes 245768 | tf_op jit(solution)/shard_map/ppermute | solution.py:35
  11.4 11.9 %collective-permute-start.5 = (bf16[1,32,1280]{2,1,0:T(8,128)(2,1)S(1)}, bf16[1,32,1280]{2,1,0:T(8,128)(2,1)S(1)}, u32[]{:S(2)}, u32[]{:S(2)}) collective-permute-start(bf16[1,32,1280]{2,1,0:T(8,128)(2,1)S(1)} %bitcast.225), channel_id=1, source_target_pairs={{0,8},{4,12},{8,0},{12,4},{1,9},{5,13},{9,1},{13,5},{2,10},{6,14},... | collective-permute-start | bytes 245768 | tf_op jit(solution)/shard_map/ppermute | solution.py:35
  11.5 11.8 %collective-permute-start.6 = (bf16[1,32,1280]{2,1,0:T(8,128)(2,1)S(1)}, bf16[1,32,1280]{2,1,0:T(8,128)(2,1)S(1)}, u32[]{:S(2)}, u32[]{:S(2)}) collective-permute-start(bf16[1,32,1280]{2,1,0:T(8,128)(2,1)S(1)} %bitcast.226), channel_id=1, source_target_pairs={{0,12},{4,0},{8,4},{12,8},{1,13},{5,1},{9,5},{13,9},{2,14},{6,2},{... | collective-permute-start | bytes 245768 | tf_op jit(solution)/shard_map/ppermute | solution.py:35
  11.9 10.4 %collective-permute-start.2 = (f32[13,1280]{1,0:T(8,128)S(1)}, f32[13,1280]{1,0:T(8,128)S(1)}, u32[]{:S(2)}, u32[]{:S(2)}) collective-permute-start(f32[13,1280]{1,0:T(8,128)S(1)} %get-tuple-element.79), channel_id=1, source_target_pairs={{0,8},{4,12},{8,0},{12,4},{1,9},{5,13},{9,1},{13,5},{2,10},{6,14},... | collective-permute-start | bytes 199688 | tf_op jit(solution)/shard_map/ppermute | solution.py:35
  14.1 8.2 %collective-permute-start.1 = (f32[13,1280]{1,0:T(8,128)S(1)}, f32[13,1280]{1,0:T(8,128)S(1)}, u32[]{:S(2)}, u32[]{:S(2)}) collective-permute-start(f32[13,1280]{1,0:T(8,128)S(1)} %get-tuple-element.78), channel_id=1, source_target_pairs={{0,4},{4,8},{8,12},{12,0},{1,5},{5,9},{9,13},{13,1},{2,6},{6,10},{... | collective-permute-start | bytes 199688 | tf_op jit(solution)/shard_map/ppermute | solution.py:35
  23.4 7.1 %collective-permute-start.14 = (bf16[4,1,32,1280]{3,2,0,1:T(8,128)(2,1)S(1)}, bf16[4,1,32,1280]{3,2,0,1:T(8,128)(2,1)S(1)}, u32[]{:S(2)}, u32[]{:S(2)}) collective-permute-start(bf16[4,1,32,1280]{3,2,0,1:T(8,128)(2,1)S(1)} %pad_maximum_fusion.4), channel_id=1, source_target_pairs={{0,2},{2,0},{1,3},{3,1},{4,6},{6,4},{5,7},{7,5},{8,10},{10,8},{9,1... | collective-permute-start | bytes 983048 | tf_op jit(solution)/shard_map/ppermute | solution.py:35
  23.8 10.1 %collective-permute-start.7 = (bf16[4,1,32,1280]{3,2,0,1:T(8,128)(2,1)S(1)}, bf16[4,1,32,1280]{3,2,0,1:T(8,128)(2,1)S(1)}, u32[]{:S(2)}, u32[]{:S(2)}) collective-permute-start(bf16[4,1,32,1280]{3,2,0,1:T(8,128)(2,1)S(1)} %pad_maximum_fusion.4), channel_id=1, source_target_pairs={{0,1},{1,0},{2,3},{3,2},{4,5},{5,4},{6,7},{7,6},{8,9},{9,8},{10,11... | collective-permute-start | bytes 983048 | tf_op jit(solution)/shard_map/ppermute | solution.py:35
  30.5 4.3 %collective-permute-start.15 = (bf16[4,1,32,1280]{3,2,0,1:T(8,128)(2,1)S(1)}, bf16[4,1,32,1280]{3,2,0,1:T(8,128)(2,1)S(1)}, u32[]{:S(2)}, u32[]{:S(2)}) collective-permute-start(bf16[4,1,32,1280]{3,2,0,1:T(8,128)(2,1)S(1)} %collective-permute-done.14), channel_id=1, source_target_pairs={{0,1},{1,0},{2,3},{3,2},{4,5},{5,4},{6,7},{7,6},{8,9},{9,8},{10,11... | collective-permute-start | bytes 983048 | tf_op jit(solution)/shard_map/ppermute | solution.py:35
  35.4 9.1 %slice-start = ((s8[5898240]{0:T(1024)(128)(4,1)}), s8[4194304]{0:T(1024)(128)(4,1)S(1)}, s32[]{:S(2)}) async-start(s8[5898240]{0:T(1024)(128)(4,1)} %bitcast.242), calls=%async_computation | async-start | bytes 8388608
  35.5 9.0 %slice-start.1 = ((s8[5898240]{0:T(1024)(128)(4,1)}), s8[1703936]{0:T(1024)(128)(4,1)S(1)}, s32[]{:S(2)}) async-start(s8[5898240]{0:T(1024)(128)(4,1)} %bitcast.242), calls=%async_computation.1 | async-start | bytes 3407872
  40.1 9.1 %collective-permute-start.16 = (f16[3,64,768]{2,1,0:T(8,128)(2,1)S(1)}, f16[3,64,768]{2,1,0:T(8,128)(2,1)S(1)}, u32[]{:S(2)}, u32[]{:S(2)}) collective-permute-start(f16[3,64,768]{2,1,0:T(8,128)(2,1)S(1)} %get-tuple-element.34), channel_id=1, source_target_pairs={{0,4},{1,5},{2,6},{3,7},{16,20},{17,21},{18,22},{19,23}} | collective-permute-start | bytes 884744 | tf_op jit(solution)/shard_map/ppermute | solution.py:260
  40.8 9.6 %collective-permute-start.17 = (f16[3,64,768]{2,1,0:T(8,128)(2,1)S(1)}, f16[3,64,768]{2,1,0:T(8,128)(2,1)S(1)}, u32[]{:S(2)}, u32[]{:S(2)}) collective-permute-start(f16[3,64,768]{2,1,0:T(8,128)(2,1)S(1)} %get-tuple-element.33), channel_id=1, source_target_pairs={{12,8},{13,9},{14,10},{15,11},{28,24},{29,25},{30,26},{31,27}} | collective-permute-start | bytes 884744 | tf_op jit(solution)/shard_map/ppermute | solution.py:261
  44.5 3.8 %copy-start.2 = (bf16[1280,768]{1,0:T(8,128)(2,1)S(1)}, bf16[1280,768]{1,0:T(8,128)(2,1)}, u32[]{:S(2)}) copy-start(bf16[1280,768]{1,0:T(8,128)(2,1)} %param.10) | copy-start | bytes 5898244
  46.3 9.6 %collective-permute-start.8 = (f16[3,64,768]{2,1,0:T(8,128)(2,1)S(1)}, f16[3,64,768]{2,1,0:T(8,128)(2,1)S(1)}, u32[]{:S(2)}, u32[]{:S(2)}) collective-permute-start(f16[3,64,768]{2,1,0:T(8,128)(2,1)S(1)} %get-tuple-element.40), channel_id=1, source_target_pairs={{0,4},{1,5},{2,6},{3,7},{16,20},{17,21},{18,22},{19,23}} | collective-permute-start | bytes 884744 | tf_op jit(solution)/shard_map/ppermute | solution.py:260
  47.0 9.7 %collective-permute-start.9 = (f16[3,64,768]{2,1,0:T(8,128)(2,1)S(1)}, f16[3,64,768]{2,1,0:T(8,128)(2,1)S(1)}, u32[]{:S(2)}, u32[]{:S(2)}) collective-permute-start(f16[3,64,768]{2,1,0:T(8,128)(2,1)S(1)} %get-tuple-element.39), channel_id=1, source_target_pairs={{12,8},{13,9},{14,10},{15,11},{28,24},{29,25},{30,26},{31,27}} | collective-permute-start | bytes 884744 | tf_op jit(solution)/shard_map/ppermute | solution.py:261
  48.4 26.5 %copy-start.1 = (bf16[640,768]{1,0:T(8,128)(2,1)}, bf16[640,768]{1,0:T(8,128)(2,1)S(1)}, u32[]{:S(2)}) copy-start(bf16[640,768]{1,0:T(8,128)(2,1)S(1)} %get-tuple-element.42.refs_8_) | copy-start | bytes 2949124
  48.5 26.5 %collective-permute-start.30 = (bf16[640,768]{1,0:T(8,128)(2,1)S(1)}, bf16[640,768]{1,0:T(8,128)(2,1)}, u32[]{:S(2)}, u32[]{:S(2)}) collective-permute-start(bf16[640,768]{1,0:T(8,128)(2,1)S(1)} %get-tuple-element.41), channel_id=1, source_target_pairs={{0,1},{1,0},{2,3},{3,2},{4,5},{5,4},{6,7},{7,6},{8,9},{9,8},{10,11... | collective-permute-start | bytes 2949128 | tf_op jit(solution)/shard_map/ppermute | solution.py:35
  50.5 11.8 %collective-permute-start.18 = (f16[3,64,768]{2,1,0:T(8,128)(2,1)S(1)}, f16[3,64,768]{2,1,0:T(8,128)(2,1)S(1)}, u32[]{:S(2)}, u32[]{:S(2)}) collective-permute-start(f16[3,64,768]{2,1,0:T(8,128)(2,1)S(1)} %get-tuple-element.32), channel_id=1, source_target_pairs={{0,4},{4,8},{1,5},{5,9},{2,6},{6,10},{3,7},{7,11},{16,20},{20,24},... | collective-permute-start | bytes 884744 | tf_op jit(solution)/shard_map/ppermute | solution.py:260
  51.2 11.2 %collective-permute-start.19 = (f16[3,64,768]{2,1,0:T(8,128)(2,1)S(1)}, f16[3,64,768]{2,1,0:T(8,128)(2,1)S(1)}, u32[]{:S(2)}, u32[]{:S(2)}) collective-permute-start(f16[3,64,768]{2,1,0:T(8,128)(2,1)S(1)} %get-tuple-element.31), channel_id=1, source_target_pairs={{12,8},{8,4},{13,9},{9,5},{14,10},{10,6},{15,11},{11,7},{28,24},{2... | collective-permute-start | bytes 884744 | tf_op jit(solution)/shard_map/ppermute | solution.py:261
  56.8 11.8 %collective-permute-start.10 = (f16[3,64,768]{2,1,0:T(8,128)(2,1)S(1)}, f16[3,64,768]{2,1,0:T(8,128)(2,1)S(1)}, u32[]{:S(2)}, u32[]{:S(2)}) collective-permute-start(f16[3,64,768]{2,1,0:T(8,128)(2,1)S(1)} %get-tuple-element.38), channel_id=1, source_target_pairs={{0,4},{4,8},{1,5},{5,9},{2,6},{6,10},{3,7},{7,11},{16,20},{20,24},... | collective-permute-start | bytes 884744 | tf_op jit(solution)/shard_map/ppermute | solution.py:260
  57.5 11.2 %collective-permute-start.11 = (f16[3,64,768]{2,1,0:T(8,128)(2,1)S(1)}, f16[3,64,768]{2,1,0:T(8,128)(2,1)S(1)}, u32[]{:S(2)}, u32[]{:S(2)}) collective-permute-start(f16[3,64,768]{2,1,0:T(8,128)(2,1)S(1)} %get-tuple-element.37), channel_id=1, source_target_pairs={{12,8},{8,4},{13,9},{9,5},{14,10},{10,6},{15,11},{11,7},{28,24},{2... | collective-permute-start | bytes 884744 | tf_op jit(solution)/shard_map/ppermute | solution.py:261
  62.6 12.8 %collective-permute-start.20 = (f16[3,64,768]{2,1,0:T(8,128)(2,1)S(1)}, f16[3,64,768]{2,1,0:T(8,128)(2,1)S(1)}, u32[]{:S(2)}, u32[]{:S(2)}) collective-permute-start(f16[3,64,768]{2,1,0:T(8,128)(2,1)S(1)} %get-tuple-element.29), channel_id=1, source_target_pairs={{0,4},{4,8},{8,12},{1,5},{5,9},{9,13},{2,6},{6,10},{10,14},{3,7},{... | collective-permute-start | bytes 884744 | tf_op jit(solution)/shard_map/ppermute | solution.py:260
  63.9 12.6 %collective-permute-start.21 = (f16[3,64,768]{2,1,0:T(8,128)(2,1)S(1)}, f16[3,64,768]{2,1,0:T(8,128)(2,1)S(1)}, u32[]{:S(2)}, u32[]{:S(2)}) collective-permute-start(f16[3,64,768]{2,1,0:T(8,128)(2,1)S(1)} %get-tuple-element.30), channel_id=1, source_target_pairs={{12,8},{8,4},{4,0},{13,9},{9,5},{5,1},{14,10},{10,6},{6,2},{15,11}... | collective-permute-start | bytes 884744 | tf_op jit(solution)/shard_map/ppermute | solution.py:261
  68.9 8.7 %collective-permute-start.12 = (f16[3,64,768]{2,1,0:T(8,128)(2,1)S(1)}, f16[3,64,768]{2,1,0:T(8,128)(2,1)S(1)}, u32[]{:S(2)}, u32[]{:S(2)}) collective-permute-start(f16[3,64,768]{2,1,0:T(8,128)(2,1)S(1)} %get-tuple-element.35), channel_id=1, source_target_pairs={{0,4},{4,8},{8,12},{1,5},{5,9},{9,13},{2,6},{6,10},{10,14},{3,7},{... | collective-permute-start | bytes 884744 | tf_op jit(solution)/shard_map/ppermute | solution.py:260
  70.2 10.4 %collective-permute-start.13 = (f16[3,64,768]{2,1,0:T(8,128)(2,1)S(1)}, f16[3,64,768]{2,1,0:T(8,128)(2,1)S(1)}, u32[]{:S(2)}, u32[]{:S(2)}) collective-permute-start(f16[3,64,768]{2,1,0:T(8,128)(2,1)S(1)} %get-tuple-element.36), channel_id=1, source_target_pairs={{12,8},{8,4},{4,0},{13,9},{9,5},{5,1},{14,10},{10,6},{6,2},{15,11}... | collective-permute-start | bytes 884744 | tf_op jit(solution)/shard_map/ppermute | solution.py:261
  75.0 51.8 %collective-permute-start.31 = (bf16[640,768]{1,0:T(8,128)(2,1)S(1)}, bf16[640,768]{1,0:T(8,128)(2,1)}, u32[]{:S(2)}, u32[]{:S(2)}) collective-permute-start(bf16[640,768]{1,0:T(8,128)(2,1)S(1)} %get-tuple-element.42.refs_8_), channel_id=1, source_target_pairs={{0,2},{2,0},{1,3},{3,1},{4,6},{6,4},{5,7},{7,5},{8,10},{10,8},{9,1... | collective-permute-start | bytes 2949128 | tf_op jit(solution)/shard_map/ppermute | solution.py:35
  75.4 66.7 %collective-permute-start.32 = (bf16[640,768]{1,0:T(8,128)(2,1)}, bf16[640,768]{1,0:T(8,128)(2,1)}, u32[]{:S(2)}, u32[]{:S(2)}) collective-permute-start(bf16[640,768]{1,0:T(8,128)(2,1)} %collective-permute-done.30.refs_9_), channel_id=1, source_target_pairs={{0,2},{2,0},{1,3},{3,1},{4,6},{6,4},{5,7},{7,5},{8,10},{10,8},{9,1... | collective-permute-start | bytes 2949128 | tf_op jit(solution)/shard_map/ppermute | solution.py:35
  85.1 33.4 %collective-permute-start.22 = (bf16[1,64,768]{2,1,0:T(8,128)(2,1)}, bf16[1,64,768]{2,1,0:T(8,128)(2,1)S(1)}, u32[]{:S(2)}, u32[]{:S(2)}) collective-permute-start(bf16[1,64,768]{2,1,0:T(8,128)(2,1)} %get-tuple-element.26), channel_id=1, source_target_pairs={{0,2},{2,0},{1,3},{3,1},{4,6},{6,4},{5,7},{7,5},{8,10},{10,8},{9,1... | collective-permute-start | bytes 294920 | tf_op jit(solution)/shard_map/ppermute | solution.py:35
  119.4 22.7 %copy-start.3 = (bf16[2,1,64,768]{3,2,1,0:T(8,128)(2,1)}, bf16[2,1,64,768]{3,2,1,0:T(8,128)(2,1)S(1)}, u32[]{:S(2)}) copy-start(bf16[2,1,64,768]{3,2,1,0:T(8,128)(2,1)S(1)} %pad_maximum_fusion.5.refs_0_) | copy-start | bytes 589828
  119.4 11.7 %collective-permute-start.24 = (bf16[2,1,64,768]{3,2,1,0:T(8,128)(2,1)S(1)}, bf16[2,1,64,768]{3,2,1,0:T(8,128)(2,1)S(1)}, u32[]{:S(2)}, u32[]{:S(2)}) collective-permute-start(bf16[2,1,64,768]{3,2,1,0:T(8,128)(2,1)S(1)} %pad_maximum_fusion.5.refs_0_), channel_id=1, source_target_pairs={{0,4},{4,8},{8,12},{12,0},{1,5},{5,9},{9,13},{13,1},{2,6},{6,10},{... | collective-permute-start | bytes 589832 | tf_op jit(solution)/shard_map/ppermute | solution.py:35
  121.5 10.1 %collective-permute-start.26 = (bf16[2,1,64,768]{3,2,1,0:T(8,128)(2,1)S(1)}, bf16[2,1,64,768]{3,2,1,0:T(8,128)(2,1)S(1)}, u32[]{:S(2)}, u32[]{:S(2)}) collective-permute-start(bf16[2,1,64,768]{3,2,1,0:T(8,128)(2,1)S(1)} %pad_maximum_fusion.5.refs_0_), channel_id=1, source_target_pairs={{0,8},{4,12},{8,0},{12,4},{1,9},{5,13},{9,1},{13,5},{2,10},{6,14},... | collective-permute-start | bytes 589832 | tf_op jit(solution)/shard_map/ppermute | solution.py:35
  122.2 18.4 %collective-permute-start.28 = (bf16[2,1,64,768]{3,2,1,0:T(8,128)(2,1)S(1)}, bf16[2,1,64,768]{3,2,1,0:T(8,128)(2,1)S(1)}, u32[]{:S(2)}, u32[]{:S(2)}) collective-permute-start(bf16[2,1,64,768]{3,2,1,0:T(8,128)(2,1)S(1)} %pad_maximum_fusion.5.refs_0_), channel_id=1, source_target_pairs={{0,12},{4,0},{8,4},{12,8},{1,13},{5,1},{9,5},{13,9},{2,14},{6,2},{... | collective-permute-start | bytes 589832 | tf_op jit(solution)/shard_map/ppermute | solution.py:35
  126.8 15.3 %collective-permute-start.23 = (bf16[2,1,64,768]{3,2,1,0:T(8,128)(2,1)S(1)}, bf16[2,1,64,768]{3,2,1,0:T(8,128)(2,1)S(1)}, u32[]{:S(2)}, u32[]{:S(2)}) collective-permute-start(bf16[2,1,64,768]{3,2,1,0:T(8,128)(2,1)S(1)} %pad_maximum_fusion.5.refs_0_), channel_id=1, source_target_pairs={{0,1},{1,0},{2,3},{3,2},{4,5},{5,4},{6,7},{7,6},{8,9},{9,8},{10,11... | collective-permute-start | bytes 589832 | tf_op jit(solution)/shard_map/ppermute | solution.py:35
  131.1 11.0 %copy-start.4 = (bf16[2,1,64,768]{3,2,1,0:T(8,128)(2,1)}, bf16[2,1,64,768]{3,2,1,0:T(8,128)(2,1)S(1)}, u32[]{:S(2)}) copy-start(bf16[2,1,64,768]{3,2,1,0:T(8,128)(2,1)S(1)} %collective-permute-done.24.refs_2_) | copy-start | bytes 589828
  131.1 11.0 %collective-permute-start.25 = (bf16[2,1,64,768]{3,2,1,0:T(8,128)(2,1)S(1)}, bf16[2,1,64,768]{3,2,1,0:T(8,128)(2,1)S(1)}, u32[]{:S(2)}, u32[]{:S(2)}) collective-permute-start(bf16[2,1,64,768]{3,2,1,0:T(8,128)(2,1)S(1)} %collective-permute-done.24.refs_2_), channel_id=1, source_target_pairs={{0,1},{1,0},{2,3},{3,2},{4,5},{5,4},{6,7},{7,6},{8,9},{9,8},{10,11... | collective-permute-start | bytes 589832 | tf_op jit(solution)/shard_map/ppermute | solution.py:35
  131.7 10.5 %copy-start.5 = (bf16[2,1,64,768]{3,2,1,0:T(8,128)(2,1)}, bf16[2,1,64,768]{3,2,1,0:T(8,128)(2,1)S(1)}, u32[]{:S(2)}) copy-start(bf16[2,1,64,768]{3,2,1,0:T(8,128)(2,1)S(1)} %collective-permute-done.26.refs_4_) | copy-start | bytes 589828
  131.7 10.5 %collective-permute-start.27 = (bf16[2,1,64,768]{3,2,1,0:T(8,128)(2,1)S(1)}, bf16[2,1,64,768]{3,2,1,0:T(8,128)(2,1)S(1)}, u32[]{:S(2)}, u32[]{:S(2)}) collective-permute-start(bf16[2,1,64,768]{3,2,1,0:T(8,128)(2,1)S(1)} %collective-permute-done.26.refs_4_), channel_id=1, source_target_pairs={{0,1},{1,0},{2,3},{3,2},{4,5},{5,4},{6,7},{7,6},{8,9},{9,8},{10,11... | collective-permute-start | bytes 589832 | tf_op jit(solution)/shard_map/ppermute | solution.py:35
  140.6 1.5 copy-start.6
  140.6 1.5 collective-permute-start.29
  142.1 0.7 copy-start.8
  142.1 0.8 copy-start.9
  152.2 3.3 %collective-permute-start.35 = (bf16[1,64,640]{2,1,0:T(8,128)(2,1)S(1)}, bf16[1,64,640]{2,1,0:T(8,128)(2,1)S(1)}, u32[]{:S(2)}, u32[]{:S(2)}) collective-permute-start(bf16[1,64,640]{2,1,0:T(8,128)(2,1)S(1)} %get-tuple-element.50), channel_id=1, source_target_pairs={{0,4},{4,8},{8,12},{12,0},{1,5},{5,9},{9,13},{13,1},{2,6},{6,10},{... | collective-permute-start | bytes 245768 | tf_op jit(solution)/shard_map/ppermute | solution.py:35
  152.4 9.7 %collective-permute-start.34 = (bf16[1,64,640]{2,1,0:T(8,128)(2,1)S(1)}, bf16[1,64,640]{2,1,0:T(8,128)(2,1)S(1)}, u32[]{:S(2)}, u32[]{:S(2)}) collective-permute-start(bf16[1,64,640]{2,1,0:T(8,128)(2,1)S(1)} %get-tuple-element.51), channel_id=1, source_target_pairs={{0,8},{4,12},{8,0},{12,4},{1,9},{5,13},{9,1},{13,5},{2,10},{6,14},... | collective-permute-start | bytes 245768 | tf_op jit(solution)/shard_map/ppermute | solution.py:35
  154.2 7.9 %collective-permute-start.33 = (bf16[1,64,640]{2,1,0:T(8,128)(2,1)S(1)}, bf16[1,64,640]{2,1,0:T(8,128)(2,1)S(1)}, u32[]{:S(2)}, u32[]{:S(2)}) collective-permute-start(bf16[1,64,640]{2,1,0:T(8,128)(2,1)S(1)} %get-tuple-element.49), channel_id=1, source_target_pairs={{0,12},{4,0},{8,4},{12,8},{1,13},{5,1},{9,5},{13,9},{2,14},{6,2},{... | collective-permute-start | bytes 245768 | tf_op jit(solution)/shard_map/ppermute | solution.py:35
  163.3 1.7 %collective-permute-start.36 = (bf16[2,1,64,640]{3,2,0,1:T(8,128)(2,1)S(1)}, bf16[2,1,64,640]{3,2,0,1:T(8,128)(2,1)S(1)}, u32[]{:S(2)}, u32[]{:S(2)}) collective-permute-start(bf16[2,1,64,640]{3,2,0,1:T(8,128)(2,1)S(1)} %fusion.27), channel_id=1, source_target_pairs={{0,1},{1,0},{2,3},{3,2},{4,5},{5,4},{6,7},{7,6},{8,9},{9,8},{10,11... | collective-permute-start | bytes 491528 | tf_op jit(solution)/shard_map/ppermute | solution.py:35
  (2 other events, 1.3 us)

commit v3 on v2

v3 whole, which is shorter than its diff:
```python
import functools

import jax
import jax.numpy as jnp
from jax import lax
from jax.experimental import pallas as pl
from jax.experimental.pallas import tpu as pltpu
from jax.sharding import PartitionSpec as P


HEAD_DIM = 128
FREQ = 256
STEPS = 100
LANES = 128


sample_shift = 5.0
norm_eps = 1e-06


def sigma_of(index):
    unit = 1.0 - index.astype(jnp.float32) / jnp.float32(STEPS)
    return sample_shift * unit / (1.0 + (sample_shift - 1.0) * unit)


def turn(block, axis, distance):
    size = lax.axis_size(axis)
    return lax.ppermute(block, axis, [(i, (i + distance) % size) for i in range(size)])


def take(array, index, dim=0):
    return lax.dynamic_index_in_dim(array, index, dim, keepdims=False)


def head_norm(values, gain):
    meansq = jnp.mean(values * values, axis=-1, keepdims=True)
    return (values * lax.rsqrt(meansq + norm_eps) * gain).astype(jnp.bfloat16)


def attend_kernel(n_seq, heads, *refs):
    gain_ref, parts, outs = refs[0], refs[1 : 1 + n_seq], refs[1 + n_seq :]
    inv_root = 1.0 / jnp.sqrt(jnp.float32(HEAD_DIM))
    rows = parts[0].shape[2]
    for h in range(heads):
        lanes = pl.ds(h * HEAD_DIM, HEAD_DIM)
        q, k, v = (
            jnp.concatenate([p[c, 0, :, lanes] for p in parts], axis=0) for c in range(3)
        )
        q = head_norm(q, gain_ref[0:1, lanes])
        k = head_norm(k, gain_ref[1:2, lanes])
        scores = lax.dot_general(
            q, k, (((1,), (1,)), ((), ())), preferred_element_type=jnp.float32
        )
        expo = jnp.exp(scores * inv_root)
        probs = (expo / jnp.sum(expo, axis=-1, keepdims=True)).astype(jnp.bfloat16)
        attn = jnp.dot(
            probs, v.astype(jnp.bfloat16), preferred_element_type=jnp.float32
        ).astype(jnp.bfloat16)
        for j, out in enumerate(outs):
            out[0, :, lanes] = attn[j * rows : (j + 1) * rows]


def attend(parts, gain):
    n_seq = len(parts)
    _, frames, rows, cols = parts[0].shape
    heads = cols // HEAD_DIM
    group = 3 if heads % 3 == 0 else 1
    width = group * HEAD_DIM
    tokens = rows * n_seq
    out = jax.ShapeDtypeStruct((frames, rows, cols), jnp.bfloat16)
    return pl.pallas_call(
        functools.partial(attend_kernel, n_seq, group),
        grid=(frames, heads // group),
        in_specs=[pl.BlockSpec((2, width), lambda f, h: (0, h))]
        + [pl.BlockSpec((3, 1, rows, width), lambda f, h: (0, f, 0, h))] * n_seq,
        out_specs=[pl.BlockSpec((1, rows, width), lambda f, h: (f, 0, h))] * n_seq,
        out_shape=[out] * n_seq,
        cost_estimate=pl.CostEstimate(
            flops=4 * frames * heads * tokens * tokens * HEAD_DIM,
            bytes_accessed=14 * frames * tokens * cols,
            transcendentals=frames * heads * tokens * tokens,
        ),
        name="attend",
    )(gain, *parts)


def spread_kernel(n_tm, place_ref, states_ref, *outs):
    z, m = place_ref[0], place_ref[1]
    frames, _, width = states_ref.shape
    part, depth = outs[0].shape[1], width // n_tm
    own = pl.ds(pl.multiple_of(m * part, part), part)
    lane = lax.broadcasted_iota(jnp.int32, (part, LANES), 1)
    for f in range(frames):
        field = states_ref[f, own, :].astype(jnp.float32)
        mean = jnp.mean(field, axis=-1, keepdims=True)
        centred = field - mean
        var = jnp.mean(centred * centred, axis=-1, keepdims=True)
        tail = jnp.zeros((part, LANES), jnp.float32)
        for place, rest in enumerate((mean, lax.rsqrt(var + norm_eps))):
            for term in range(3):
                cut = rest.astype(jnp.bfloat16).astype(jnp.float32)
                tail = jnp.where(lane == 3 * place + term, cut, tail)
                rest = rest - cut
        tail = tail.astype(jnp.bfloat16)
        for k, out in enumerate(outs):
            out[f, :, depth:] = tail
            for s in range(n_tm):

                @pl.when(lax.rem(z + k, n_tm) == s)
                def _():
                    out[f, :, :depth] = states_ref[f, own, s * depth : (s + 1) * depth]


def spread(states, place, n_tm, part):
    frames, _, width = states.shape
    out = jax.ShapeDtypeStruct((frames, part, width // n_tm + LANES), jnp.bfloat16)
    return pl.pallas_call(
        functools.partial(spread_kernel, n_tm),
        in_specs=[pl.BlockSpec(memory_space=pltpu.SMEM), pl.BlockSpec(memory_space=pltpu.VMEM)],
        out_specs=[pl.BlockSpec(memory_space=pltpu.VMEM)] * n_tm,
        out_shape=[out] * n_tm,
        cost_estimate=pl.CostEstimate(
            flops=10 * part * width, bytes_accessed=4 * part * width, transcendentals=0
        ),
        name="spread",
    )(place, states)


def time_kernel(n_tm, place_ref, step_ref, proj_ref, *outs):
    z = place_ref[0]
    freq_rows, wide = proj_ref.shape
    window, depth = outs[0].shape[1:]
    half_freq = FREQ // 2
    index = step_ref[0] + lax.broadcasted_iota(jnp.int32, (window, freq_rows), 0)
    feature = z * freq_rows + lax.broadcasted_iota(jnp.int32, (window, freq_rows), 1)
    late = feature >= half_freq
    rank = jnp.where(late, feature - half_freq, feature).astype(jnp.float32)
    freqs = jnp.exp(-jnp.log(jnp.float32(10000.0)) * rank / jnp.float32(half_freq))
    angles = (1000.0 * sigma_of(index)) * freqs
    emb = jnp.where(late, jnp.sin(angles), jnp.cos(angles)).astype(jnp.bfloat16)
    for k, out in enumerate(outs):
        for s in range(n_tm):

            @pl.when(lax.rem(z + k, n_tm) == s)
            def _():
                for c in range(3):
                    first = c * (wide // 3) + s * depth
                    out[c] = jnp.dot(
                        emb, proj_ref[:, first : first + depth], preferred_element_type=jnp.float32
                    )


def time_shares(start_step, time_proj, place, n_tm, window):
    freq_rows, wide = time_proj.shape
    out = jax.ShapeDtypeStruct((3, window, wide // (3 * n_tm)), jnp.float32)
    smem, vmem = (pl.BlockSpec(memory_space=space) for space in (pltpu.SMEM, pltpu.VMEM))
    return pl.pallas_call(
        functools.partial(time_kernel, n_tm),
        in_specs=[smem, smem, vmem],
        out_specs=[vmem] * n_tm,
        out_shape=[out] * n_tm,
        cost_estimate=pl.CostEstimate(
            flops=2 * window * freq_rows * wide, bytes_accessed=2 * freq_rows * wide, transcendentals=0
        ),
        name="time_shares",
    )(place, start_step, time_proj)


def qkv_kernel(n_tm, n_mp, place_ref, *refs):
    shares, rows, w_ref = refs[:n_tm], refs[n_tm : n_tm + n_mp], refs[n_tm + n_mp]
    proj_ref, mod_scr, hidden_scr = refs[n_tm + n_mp + 1 :]
    z = place_ref[0]
    _, frames, part, wide = rows[0].shape
    depth = wide - LANES

    @pl.when((pl.program_id(0) == 0) & (pl.program_id(1) == 0))
    def _():
        total = shares[0][...]
        for share in shares[1:]:
            total = total + share[...]
        mod_scr[...] = total
        for k in range(n_tm):
            for f in range(frames):
                step = pl.ds(lax.rem(z - k + n_tm, n_tm) * frames + f, 1)
                shift, scale = mod_scr[0, step, :], mod_scr[1, step, :]
                for i in range(n_mp):
                    tail = rows[i][k, f, :, depth:].astype(jnp.float32)
                    mean = tail[:, 0:1] + tail[:, 1:2] + tail[:, 2:3]
                    rstd = tail[:, 3:4] + tail[:, 4:5] + tail[:, 5:6]
                    normed = (rows[i][k, f, :, :depth].astype(jnp.float32) - mean) * rstd
                    at = ((k * frames + f) * n_mp + i) * part
                    hidden_scr[at : at + part, :] = (normed * (1.0 + scale) + shift).astype(
                        jnp.bfloat16
                    )

    product = jnp.dot(hidden_scr[...], w_ref[0], preferred_element_type=jnp.float32)
    proj_ref[:, 0] = product.reshape(proj_ref.shape[0], proj_ref.shape[2], proj_ref.shape[3])


def qkv(shares, rows, w_qkv, place):
    n_tm, n_mp = len(shares), len(rows)
    _, frames, part, _ = rows[0].shape
    three, depth, cols = w_qkv.shape
    window = shares[0].shape[1]
    step = 384 if cols % 384 == 0 else cols
    block = frames * n_mp * part
    return pl.pallas_call(
        functools.partial(qkv_kernel, n_tm, n_mp),
        grid_spec=pltpu.PrefetchScalarGridSpec(
            num_scalar_prefetch=1,
            grid=(three, cols // step),
            in_specs=[pl.BlockSpec(shares[0].shape, lambda c, h, p: (0, 0, 0))] * n_tm
            + [pl.BlockSpec(rows[0].shape, lambda c, h, p: (0, 0, 0, 0))] * n_mp
            + [pl.BlockSpec((1, depth, step), lambda c, h, p: (c, 0, h))],
            out_specs=pl.BlockSpec((n_tm, 1, block, step), lambda c, h, p: (0, c, 0, h)),
            scratch_shapes=[
                pltpu.VMEM((3, window, depth), jnp.float32),
                pltpu.VMEM((n_tm * block, depth), jnp.bfloat16),
            ],
        ),
        out_shape=jax.ShapeDtypeStruct((n_tm, three, block, cols), jnp.float32),
        cost_estimate=pl.CostEstimate(
            flops=2 * n_tm * block * depth * three * cols,
            bytes_accessed=2 * three * depth * cols + 4 * n_tm * block * three * cols,
            transcendentals=0,
        ),
        name="qkv",
    )(place, *shares, *rows, w_qkv)


def project_kernel(dims, place_ref, coef_ref, *refs):
    n_tm, n_seq, n_mp, frames, part, _ = dims
    attn_refs = refs[: n_tm * n_mp]
    w_refs = refs[n_tm * n_mp : n_tm * n_mp + n_seq * n_mp]
    outs = refs[n_tm * n_mp + n_seq * n_mp :]
    own_ref, moved_refs, (rows_scr, w_scr, sum_scr, sems) = outs[0], outs[1:-4], outs[-4:]
    z, m = place_ref[0], place_ref[1]
    block = n_mp * part
    per = frames * block
    copies = []
    for j in range(n_seq):
        for l in range(n_mp):
            at = j * n_mp + l
            group = [pltpu.make_async_copy(w_refs[at], w_scr.at[at], sems.at[at, 0])]
            for k in range(n_tm):
                for f in range(frames):
                    for i in range(n_mp):
                        first = k * per + f * block + i * part
                        source = (i - l) % n_mp * part
                        group.append(
                            pltpu.make_async_copy(
                                attn_refs[k * n_mp + l].at[j, f, pl.ds(source, part)],
                                rows_scr.at[at, pl.ds(first, part)],
                                sems.at[at, len(group)],
                            )
                        )
            for copy in group:
                copy.start()
            copies.append(group)
    total = None
    for at, group in enumerate(copies):
        for copy in group:
            copy.wait()
        product = lax.dot_general(
            rows_scr[at], w_scr[at], (((1,), (1,)), ((), ())), preferred_element_type=jnp.float32
        )
        total = product if total is None else total + product
    for k in range(n_tm):
        for f in range(frames):
            first = k * per + f * block
            drift = total[first : first + block] * coef_ref[k, f : f + 1]
            sum_scr[lax.rem(z - k + n_tm, n_tm), f] = drift
    for s in range(n_tm):
        for f in range(frames):
            if s or f:
                before = sum_scr[s, f - 1] if f else sum_scr[s - 1, frames - 1]
                sum_scr[s, f] = sum_scr[s, f] + before
    for k in range(n_tm):
        own = lax.rem(z - k + n_tm, n_tm)
        for f in range(frames):
            for i in range(n_mp):
                to = pl.ds(pl.multiple_of(lax.rem(m - i + n_mp, n_mp) * part, part), part)
                piece = sum_scr[own, f, i * part : (i + 1) * part, :]
                moved_refs[k][f, to, :] = piece.astype(jnp.bfloat16)
                if k == 0:
                    own_ref[f, to, :] = piece


def project(attn, weights, coef, place, dims):
    n_tm, n_seq, n_mp, frames, part, cols = dims
    half = weights[0][0].shape[0]
    tok = n_mp * part
    rows = n_tm * frames * tok
    deep = n_seq * n_mp * cols
    smem, vmem, anywhere = (
        pl.BlockSpec(memory_space=space) for space in (pltpu.SMEM, pltpu.VMEM, pl.ANY)
    )
    return pl.pallas_call(
        functools.partial(project_kernel, dims),
        in_specs=[smem, vmem] + [anywhere] * (n_tm * n_mp + n_seq * n_mp),
        out_specs=[vmem] * (1 + n_tm),
        scratch_shapes=[
            pltpu.VMEM((n_seq * n_mp, rows, cols), jnp.bfloat16),
            pltpu.VMEM((n_seq * n_mp, half, cols), jnp.bfloat16),
            pltpu.VMEM((n_tm, frames, tok, half), jnp.float32),
            pltpu.SemaphoreType.DMA((n_seq * n_mp, 1 + n_tm * frames * n_mp)),
        ],
        out_shape=[jax.ShapeDtypeStruct((frames, tok, half), jnp.float32)]
        + [jax.ShapeDtypeStruct((frames, tok, half), jnp.bfloat16)] * n_tm,
        cost_estimate=pl.CostEstimate(
            flops=2 * rows * deep * half, bytes_accessed=2 * (rows + half) * deep, transcendentals=0
        ),
        name="project",
    )(place, coef, *[a for k in attn for a in k], *[w for j in weights for w in j])


def finish_kernel(n_tm, n_mp, place_ref, *refs):
    out = refs[-1]
    z, m = place_ref[0], place_ref[1]
    half = refs[0].shape[-1]
    slices = n_tm // n_mp
    for u in range(slices):
        k_here = lax.rem(m * slices + u - z + n_tm, n_tm)
        for h in range(n_mp):
            first = (u * n_mp + h) * half
            for k in range(n_tm):
                for l in range(n_mp):

                    @pl.when((k_here == k) & (lax.rem(m - h + n_mp, n_mp) == l))
                    def _():
                        out[:, :, first : first + half] = refs[k * n_mp + l][...].astype(
                            jnp.float32
                        )


def finish(blocks, place):
    n_tm, n_mp = len(blocks), len(blocks[0])
    frames, tok, half = blocks[0][0].shape
    smem, vmem = (pl.BlockSpec(memory_space=space) for space in (pltpu.SMEM, pltpu.VMEM))
    return pl.pallas_call(
        functools.partial(finish_kernel, n_tm, n_mp),
        in_specs=[smem] + [vmem] * (n_tm * n_mp),
        out_specs=vmem,
        out_shape=jax.ShapeDtypeStruct((frames, tok, n_tm * half), jnp.float32),
        cost_estimate=pl.CostEstimate(
            flops=0, bytes_accessed=8 * frames * tok * n_tm * half, transcendentals=0
        ),
        name="finish",
    )(place, *[b for k in blocks for b in k])


def sweep(states, start_step, w_qkv, qk_gain, w_out, time_proj):
    frames, tok, _ = states.shape
    n_tm, n_seq, n_mp = (lax.axis_size(name) for name in ("tm", "seq", "mp"))
    z, m = lax.axis_index("tm"), lax.axis_index("mp")
    place = jnp.stack([z, m]).astype(jnp.int32)
    part = tok // n_mp
    depth, cols = w_qkv.shape[1:]
    half = depth // n_mp
    window = frames * n_tm

    raw = list(spread(states, place, n_tm, part))
    for k in range(1, n_tm):
        raw[k] = turn(raw[k], "tm", k)
    raw = jnp.stack(raw)
    sides = [raw]
    for j in range(1, n_seq):
        sides.append(turn(raw, "seq", j))
    rows = []
    for side in sides:
        rows.append([side] + [turn(side, "mp", i) for i in range(1, n_mp)])

    shares = list(time_shares(start_step, time_proj, place, n_tm, window))
    for k in range(1, n_tm):
        shares[k] = turn(shares[k], "tm", k)

    share = w_out.reshape(n_mp, half, cols)
    weights = [take(share, m)]
    weights += [turn(take(share, (m + i) % n_mp), "mp", i) for i in range(1, n_mp)]
    weights = [weights]
    for j in range(1, n_seq):
        weights.append([turn(s, "seq", -j) for s in weights[0]])

    steps_idx = start_step[0] + jnp.arange(window)
    step_size = sigma_of(steps_idx + 1) - sigma_of(steps_idx)
    gate = lax.dynamic_slice_in_dim(sum(s[2] for s in shares), m * half, half, 1)
    coef = (step_size[:, None] * gate).reshape(n_tm, frames, half)
    coef = jnp.stack([take(coef, (z - k) % n_tm) for k in range(n_tm)])

    proj = []
    for j in range(n_seq):
        proj.append(qkv(shares, rows[j], w_qkv, place))
    right, left = [None] * n_seq, [None] * n_seq
    for t in range(n_tm - 1):
        for j in range(n_seq):
            send_right, send_left = proj[j][(t + 1) % n_tm], proj[j][n_tm - 1 - t]
            if t:
                right[j], left[j], coef = lax.optimization_barrier((right[j], left[j], coef))
                send_right = send_right + right[j].astype(jnp.float32)
                send_left = send_left + left[j].astype(jnp.float32)
            send_right, send_left = send_right.astype(jnp.float16), send_left.astype(jnp.float16)
            right[j] = lax.ppermute(send_right, "tm", [(i, i + 1) for i in range(t + 1)])
            left[j] = lax.ppermute(
                send_left, "tm", [(n_tm - 1 - i, n_tm - 2 - i) for i in range(t + 1)]
            )
    parts = [
        (p[0] + r.astype(jnp.float32) + l.astype(jnp.float32)).reshape(3, frames, tok, cols)
        for p, r, l in zip(proj, right, left)
    ]
    attn = attend(parts, qk_gain)

    attn = jnp.stack([attn[0]] + [turn(attn[j], "seq", -j) for j in range(1, n_seq)])
    gathered = [attn]
    for k in range(1, n_tm):
        gathered.append(turn(attn, "tm", k))
    gathered = [[g] + [turn(g, "mp", i) for i in range(1, n_mp)] for g in gathered]

    own, *moved = project(
        gathered, weights, coef, place, (n_tm, n_seq, n_mp, frames, part, cols)
    )
    blocks = []
    for k in range(n_tm):
        block = moved[0]
        if k:
            block = turn(moved[k], "tm", -k)
        others = [turn(block, "mp", i) for i in range(1, n_mp)]
        blocks.append([block if k else own] + others)
    return finish(blocks, place)


def solution(mesh):
    return jax.shard_map(
        sweep,
        mesh=mesh,
        in_specs=(
            P(("group", "tm"), "seq", None),
            P("group"),
            P(None, "tm", ("seq", "mp")),
            P(None, ("seq", "mp")),
            P("tm", ("seq", "mp")),
            P("tm", None),
        ),
        out_specs=P(("group", "tm"), "seq", "mp"),
        check_vma=False,
    )
```

time: 169 us -> 165 us (0.976)
  the two profiles are of different devices: /device:TPU:25 before, /device:TPU:0 now
where the time goes in v3:
time: 165 us; the launch traced here: 164 us
  waiting for transfers between devices  60.9 us (37%)
  starting transfers between devices  55.3 us (34%)
  Pallas kernels  33.4 us (20%)
  other arithmetic  9.25 us (6%)
  local copies, waits for them, and re-layouts  4.37 us (3%)
    ppermute x27, waiting for transfers between devices, turn(): lax.ppermute(block, axis, [(i, (i + distance) % size) for i in range(size)])  49.9 us
    ppermute x27, starting transfers between devices, turn(): lax.ppermute(block, axis, [(i, (i + distance) % size) for i in range(size)])  27.9 us
    ppermute x6, starting transfers between devices, sweep(): lax.ppermute(send_right, 'tm', [(i, i + 1) for i in range(t + 1)])  21.3 us
    pallas_call x2, Pallas kernels, qkv(): pl.pallas_call(functools.partial(qkv_kernel, n_tm, n_mp), grid_spec=pltpu...  16.8 us
    ppermute x6, waiting for transfers between devices, sweep(): lax.ppermute(send_left, 'tm', [(n_tm - 1 - i, n_tm - 2 - i) for i in rang...  6.87 us
    ppermute x6, starting transfers between devices, sweep(): lax.ppermute(send_left, 'tm', [(n_tm - 1 - i, n_tm - 2 - i) for i in rang...  6.12 us
    pallas_call x1, Pallas kernels, project(): pl.pallas_call(functools.partial(project_kernel, dims), in_specs=[smem, v...  5.44 us
    convert_element_type x4, other arithmetic, sweep(): send_left.astype(jnp.float16)  4.89 us
  transfers between devices with their start and end apart: 39, of which 17 were waited for; matrix products, arithmetic and copies ran while one was open for 6% of the time, Pallas kernels for 14%

profile of v3, /device:TPU:0, one launch (start us, length us, event | category | flops | bytes accessed | tf_op | source)
XLA Modules:
  0.0 164.5 jit_solution(8442806685559899926)
XLA Ops:
  1.4 3.1 %time_shares.1 = (f32[3,4,1280]{2,1,0:T(4,128)}, f32[3,4,1280]{2,1,0:T(4,128)}, f32[3,4,1280]{2,1,0:T(4,128)}, f32[3,4,1280]{2,1,0:T(4,128)}) custom-call(s32[2]{0:T(128)} %pad_add_fusion.place_ref, s32[1]{0:T(128)} %copy.7.step_ref, bf16[64,15360]{1,0:T(8,128)(2,1)} %proj_ref.1), custom_call_target="tpu_custom_call" | custom-call | flops 7864320 | bytes 1966080 | tf_op jit(solution)/shard_map/time_shares/pallas_call | solution.py:157
  4.5 3.1 %collective-permute-start = (f32[3,4,1280]{2,1,0:T(4,128)}, f32[3,4,1280]{2,1,0:T(4,128)S(1)}, u32[]{:S(2)}, u32[]{:S(2)}) collective-permute-start(f32[3,4,1280]{2,1,0:T(4,128)} %get-tuple-element.33), channel_id=1, source_target_pairs={{0,4},{4,8},{8,12},{12,0},{1,5},{5,9},{9,13},{13,1},{2,6},{6,10},{... | collective-permute-start | bytes 184328 | tf_op jit(solution)/shard_map/ppermute | solution.py:28
  7.6 2.6 %collective-permute-start.1 = (f32[3,4,1280]{2,1,0:T(4,128)}, f32[3,4,1280]{2,1,0:T(4,128)S(1)}, u32[]{:S(2)}, u32[]{:S(2)}) collective-permute-start(f32[3,4,1280]{2,1,0:T(4,128)} %get-tuple-element.34), channel_id=1, source_target_pairs={{0,8},{4,12},{8,0},{12,4},{1,9},{5,13},{9,1},{13,5},{2,10},{6,14},... | collective-permute-start | bytes 184328 | tf_op jit(solution)/shard_map/ppermute | solution.py:28
  10.1 2.2 %spread.1 = (bf16[1,32,1408]{2,1,0:T(8,128)(2,1)}, bf16[1,32,1408]{2,1,0:T(8,128)(2,1)}, bf16[1,32,1408]{2,1,0:T(8,128)(2,1)}, bf16[1,32,1408]{2,1,0:T(8,128)(2,1)}) custom-call(s32[2]{0:T(128)} %pad_add_fusion.place_ref, bf16[1,64,5120]{2,1,0:T(8,128)(2,1)} %states_ref.1), custom_call_target="tpu_custom_call" | custom-call | flops 1638400 | bytes 655360 | tf_op jit(solution)/shard_map/spread/pallas_call | solution.py:117
  12.4 1.9 %collective-permute-start.4 = (bf16[1,32,1408]{2,1,0:T(8,128)(2,1)}, bf16[1,32,1408]{2,1,0:T(8,128)(2,1)S(1)}, u32[]{:S(2)}, u32[]{:S(2)}) collective-permute-start(bf16[1,32,1408]{2,1,0:T(8,128)(2,1)} %get-tuple-element.38), channel_id=1, source_target_pairs={{0,8},{4,12},{8,0},{12,4},{1,9},{5,13},{9,1},{13,5},{2,10},{6,14},... | collective-permute-start | bytes 270344 | tf_op jit(solution)/shard_map/ppermute | solution.py:28
  14.3 1.9 %collective-permute-start.5 = (bf16[1,32,1408]{2,1,0:T(8,128)(2,1)}, bf16[1,32,1408]{2,1,0:T(8,128)(2,1)S(1)}, u32[]{:S(2)}, u32[]{:S(2)}) collective-permute-start(bf16[1,32,1408]{2,1,0:T(8,128)(2,1)} %get-tuple-element.39), channel_id=1, source_target_pairs={{0,12},{4,0},{8,4},{12,8},{1,13},{5,1},{9,5},{13,9},{2,14},{6,2},{... | collective-permute-start | bytes 270344 | tf_op jit(solution)/shard_map/ppermute | solution.py:28
  16.2 1.2 dynamic-slice_bitcast_fusion
  17.4 2.5 %collective-permute-done.3 = bf16[1,32,1408]{2,1,0:T(8,128)(2,1)S(1)} collective-permute-done((bf16[1,32,1408]{2,1,0:T(8,128)(2,1)}, bf16[1,32,1408]{2,1,0:T(8,128)(2,1)S(1)}, u32[]{:S(2)}, u32[]{:S(2)}) %collective-permute-start.3) | collective-permute-done | bytes 90144 | tf_op jit(solution)/shard_map/ppermute | solution.py:28
  19.9 2.3 %collective-permute-done.4 = bf16[1,32,1408]{2,1,0:T(8,128)(2,1)S(1)} collective-permute-done((bf16[1,32,1408]{2,1,0:T(8,128)(2,1)}, bf16[1,32,1408]{2,1,0:T(8,128)(2,1)S(1)}, u32[]{:S(2)}, u32[]{:S(2)}) %collective-permute-start.4) | collective-permute-done | bytes 90144 | tf_op jit(solution)/shard_map/ppermute | solution.py:28
  22.3 1.6 collective-permute-start.6
  25.0 8.2 %collective-permute-done.6.refs_4_ = bf16[4,1,32,1408]{3,2,1,0:T(8,128)(2,1)} collective-permute-done((bf16[4,1,32,1408]{3,2,1,0:T(8,128)(2,1)S(1)}, bf16[4,1,32,1408]{3,2,1,0:T(8,128)(2,1)}, u32[]{:S(2)}, u32[]{:S(2)}) %collective-permute-start.6) | collective-permute-done | bytes 360480 | tf_op jit(solution)/shard_map/ppermute | solution.py:28
  34.0 8.4 %qkv.3 = f32[4,3,64,768]{3,2,1,0:T(8,128)} custom-call(s32[2]{0:T(128)} %pad_add_fusion.place_ref, f32[3,4,1280]{2,1,0:T(4,128)} %get-tuple-element.32.refs_0_, f32[3,4,1280]{2,1,0:T(4,128)} %copy-done.7, f32[3,4,1280]{2,1,0:T(4,128)} %copy-done.8, f32[3,4,1280]{2,1,0:T(4,128)} %copy-done.9, bf16[4,1,32,1408]{3,2,1,0:T(8,128)(2,1)} %copy-done.4, ...), custom_call_target="tpu_custom_call" | custom-call | flops 1509949440 | bytes 8257536 | tf_op jit(solution)/shard_map/qkv/pallas_call | solution.py:207
  42.3 2.1 %fusion.9 = (f16[3,64,768]{2,1,0:T(8,128)(2,1)}, f16[3,64,768]{2,1,0:T(8,128)(2,1)}) fusion(f32[4,3,64,768]{3,2,1,0:T(8,128)} %qkv.3), kind=kLoop, calls=%fused_computation.27 | loop fusion | flops 294912 | bytes 1769472 | tf_op jit(solution)/shard_map/convert_element_type | solution.py:401
  44.4 4.8 %collective-permute-start.11 = (f16[3,64,768]{2,1,0:T(8,128)(2,1)}, f16[3,64,768]{2,1,0:T(8,128)(2,1)}, u32[]{:S(2)}, u32[]{:S(2)}) collective-permute-start(f16[3,64,768]{2,1,0:T(8,128)(2,1)} %get-tuple-element.68), channel_id=1, source_target_pairs={{0,4},{1,5},{2,6},{3,7},{16,20},{17,21},{18,22},{19,23}} | collective-permute-start | bytes 884744 | tf_op jit(solution)/shard_map/ppermute | solution.py:402
  49.3 1.5 collective-permute-start.12
  50.8 8.4 %qkv.2 = f32[4,3,64,768]{3,2,1,0:T(8,128)} custom-call(s32[2]{0:T(128)} %pad_add_fusion.place_ref, f32[3,4,1280]{2,1,0:T(4,128)} %get-tuple-element.32.refs_0_, f32[3,4,1280]{2,1,0:T(4,128)} %copy-done.7, f32[3,4,1280]{2,1,0:T(4,128)} %copy-done.8, f32[3,4,1280]{2,1,0:T(4,128)} %copy-done.9, bf16[4,1,32,1408]{3,2,1,0:T(8,128)(2,1)} %collective-permute-done.6.refs_4_, ...), custom_call_target="tpu_custom_call" | custom-call | flops 1509949440 | bytes 8257536 | tf_op jit(solution)/shard_map/qkv/pallas_call | solution.py:207
  59.2 1.5 fusion.7
  60.7 1.3 collective-permute-start.8
  63.3 1.2 add_convert_fusion.4
  64.5 1.3 collective-permute-start.15
  66.5 2.9 %collective-permute-done.8 = f16[3,64,768]{2,1,0:T(8,128)(2,1)S(1)} collective-permute-done((f16[3,64,768]{2,1,0:T(8,128)(2,1)S(1)}, f16[3,64,768]{2,1,0:T(8,128)(2,1)S(1)}, u32[]{:S(2)}, u32[]{:S(2)}) %collective-permute-start.8) | collective-permute-done | bytes 294944 | tf_op jit(solution)/shard_map/ppermute | solution.py:402
  69.5 4.4 %collective-permute-start.13 = (f16[3,64,768]{2,1,0:T(8,128)(2,1)S(1)}, f16[3,64,768]{2,1,0:T(8,128)(2,1)S(1)}, u32[]{:S(2)}, u32[]{:S(2)}) collective-permute-start(f16[3,64,768]{2,1,0:T(8,128)(2,1)S(1)} %get-tuple-element.66), channel_id=1, source_target_pairs={{0,4},{4,8},{1,5},{5,9},{2,6},{6,10},{3,7},{7,11},{16,20},{20,24},... | collective-permute-start | bytes 884744 | tf_op jit(solution)/shard_map/ppermute | solution.py:402
  74.6 1.1 collective-permute-done.15
  75.7 1.5 collective-permute-start.30
  77.3 4.4 %collective-permute-start.17 = (f16[3,64,768]{2,1,0:T(8,128)(2,1)S(1)}, f16[3,64,768]{2,1,0:T(8,128)(2,1)S(1)}, u32[]{:S(2)}, u32[]{:S(2)}) collective-permute-start(f16[3,64,768]{2,1,0:T(8,128)(2,1)S(1)} %get-tuple-element.61), channel_id=1, source_target_pairs={{0,4},{4,8},{8,12},{1,5},{5,9},{9,13},{2,6},{6,10},{10,14},{3,7},{... | collective-permute-start | bytes 884744 | tf_op jit(solution)/shard_map/ppermute | solution.py:402
  82.0 1.3 collective-permute-start.18
  83.4 5.0 %collective-permute-start.19 = (f16[3,64,768]{2,1,0:T(8,128)(2,1)S(1)}, f16[3,64,768]{2,1,0:T(8,128)(2,1)S(1)}, u32[]{:S(2)}, u32[]{:S(2)}) collective-permute-start(f16[3,64,768]{2,1,0:T(8,128)(2,1)S(1)} %get-tuple-element.59), channel_id=1, source_target_pairs={{0,4},{4,8},{8,12},{1,5},{5,9},{9,13},{2,6},{6,10},{10,14},{3,7},{... | collective-permute-start | bytes 884744 | tf_op jit(solution)/shard_map/ppermute | solution.py:402
  88.5 1.3 collective-permute-start.20
  89.8 1.6 collective-permute-start.31
  91.4 2.3 %collective-permute-done.18 = f16[3,64,768]{2,1,0:T(8,128)(2,1)S(1)} collective-permute-done((f16[3,64,768]{2,1,0:T(8,128)(2,1)S(1)}, f16[3,64,768]{2,1,0:T(8,128)(2,1)S(1)}, u32[]{:S(2)}, u32[]{:S(2)}) %collective-permute-start.18) | collective-permute-done | bytes 294944 | tf_op jit(solution)/shard_map/ppermute | solution.py:403
  93.6 0.9 fusion.5.refs_1_
  94.5 4.6 %collective-permute-done.20 = f16[3,64,768]{2,1,0:T(8,128)(2,1)S(1)} collective-permute-done((f16[3,64,768]{2,1,0:T(8,128)(2,1)S(1)}, f16[3,64,768]{2,1,0:T(8,128)(2,1)S(1)}, u32[]{:S(2)}, u32[]{:S(2)}) %collective-permute-start.20) | collective-permute-done | bytes 294944 | tf_op jit(solution)/shard_map/ppermute | solution.py:403
  99.1 0.9 fusion.2.refs_2_
  100.0 3.6 %attend.1 = (bf16[1,64,768]{2,1,0:T(8,128)(2,1)}, bf16[1,64,768]{2,1,0:T(8,128)(2,1)}) custom-call(f32[2,768]{1,0:T(2,128)} %refs_0_.1, f32[3,1,64,768]{3,2,1,0:T(8,128)} %fusion.5.refs_1_, f32[3,1,64,768]{3,2,1,0:T(8,128)} %fusion.2.refs_2_), custom_call_target="tpu_custom_call" | custom-call | flops 50331648 | bytes 1376256 | tf_op jit(solution)/shard_map/attend/pallas_call | solution.py:71
  103.6 1.5 collective-permute-start.21
  105.1 16.5 %collective-permute-done.21 = bf16[1,64,768]{2,1,0:T(8,128)(2,1)S(1)} collective-permute-done((bf16[1,64,768]{2,1,0:T(8,128)(2,1)}, bf16[1,64,768]{2,1,0:T(8,128)(2,1)S(1)}, u32[]{:S(2)}, u32[]{:S(2)}) %collective-permute-start.21) | collective-permute-done | bytes 98336 | tf_op jit(solution)/shard_map/ppermute | solution.py:28
  121.7 0.9 pad_maximum_fusion.1.refs_0_
  122.6 2.5 %collective-permute-start.23 = (bf16[2,1,64,768]{3,2,1,0:T(8,128)(2,1)S(1)}, bf16[2,1,64,768]{3,2,1,0:T(8,128)(2,1)S(1)}, u32[]{:S(2)}, u32[]{:S(2)}) collective-permute-start(bf16[2,1,64,768]{3,2,1,0:T(8,128)(2,1)S(1)} %pad_maximum_fusion.1.refs_0_), channel_id=1, source_target_pairs={{0,4},{4,8},{8,12},{12,0},{1,5},{5,9},{9,13},{13,1},{2,6},{6,10},{... | collective-permute-start | bytes 589832 | tf_op jit(solution)/shard_map/ppermute | solution.py:28
  125.1 2.4 %collective-permute-start.27 = (bf16[2,1,64,768]{3,2,1,0:T(8,128)(2,1)S(1)}, bf16[2,1,64,768]{3,2,1,0:T(8,128)(2,1)S(1)}, u32[]{:S(2)}, u32[]{:S(2)}) collective-permute-start(bf16[2,1,64,768]{3,2,1,0:T(8,128)(2,1)S(1)} %pad_maximum_fusion.1.refs_0_), channel_id=1, source_target_pairs={{0,12},{4,0},{8,4},{12,8},{1,13},{5,1},{9,5},{13,9},{2,14},{6,2},{... | collective-permute-start | bytes 589832 | tf_op jit(solution)/shard_map/ppermute | solution.py:28
  127.6 4.7 %collective-permute-done.23.refs_2_ = bf16[2,1,64,768]{3,2,1,0:T(8,128)(2,1)S(1)} collective-permute-done((bf16[2,1,64,768]{3,2,1,0:T(8,128)(2,1)S(1)}, bf16[2,1,64,768]{3,2,1,0:T(8,128)(2,1)S(1)}, u32[]{:S(2)}, u32[]{:S(2)}) %collective-permute-start.23) | collective-permute-done | bytes 196640 | tf_op jit(solution)/shard_map/ppermute | solution.py:28
  132.3 5.9 %collective-permute-done.25.refs_4_ = bf16[2,1,64,768]{3,2,1,0:T(8,128)(2,1)S(1)} collective-permute-done((bf16[2,1,64,768]{3,2,1,0:T(8,128)(2,1)S(1)}, bf16[2,1,64,768]{3,2,1,0:T(8,128)(2,1)S(1)}, u32[]{:S(2)}, u32[]{:S(2)}) %collective-permute-start.25) | collective-permute-done | bytes 196640 | tf_op jit(solution)/shard_map/ppermute | solution.py:28
  138.8 0.9 collective-permute-done.26.refs_5_
  141.0 5.4 %project.1 = (f32[1,64,640]{2,1,0:T(8,128)}, bf16[1,64,640]{2,1,0:T(8,128)(2,1)}, bf16[1,64,640]{2,1,0:T(8,128)(2,1)}, bf16[1,64,640]{2,1,0:T(8,128)(2,1)}, bf16[1,64,640]{2,1,0:T(8,128)(2,1)}) custom-call(s32[2]{0:T(128)} %pad_add_fusion.place_ref, f32[4,1,640]{2,1,0:T(1,128)} %pad_maximum_fusion.2.coef_ref, bf16[2,1,64,768]{3,2,1,0:T(8,128)(2,1)} %copy-done.5, ...), custom_call_target="tpu_custom_call" | custom-call | flops 1006632960 | bytes 5505024 | tf_op jit(solution)/shard_map/project/pallas_call | solution.py:298
  146.5 5.4 %collective-permute-start.33 = (bf16[1,64,640]{2,1,0:T(8,128)(2,1)}, bf16[1,64,640]{2,1,0:T(8,128)(2,1)S(1)}, u32[]{:S(2)}, u32[]{:S(2)}) collective-permute-start(bf16[1,64,640]{2,1,0:T(8,128)(2,1)} %get-tuple-element.56), channel_id=1, source_target_pairs={{0,12},{4,0},{8,4},{12,8},{1,13},{5,1},{9,5},{13,9},{2,14},{6,2},{... | collective-permute-start | bytes 245768 | tf_op jit(solution)/shard_map/ppermute | solution.py:28
  152.6 2.5 %collective-permute-done.33.refs_2_ = bf16[1,64,640]{2,1,0:T(8,128)(2,1)S(1)} collective-permute-done((bf16[1,64,640]{2,1,0:T(8,128)(2,1)}, bf16[1,64,640]{2,1,0:T(8,128)(2,1)S(1)}, u32[]{:S(2)}, u32[]{:S(2)}) %collective-permute-start.33) | collective-permute-done | bytes 81952 | tf_op jit(solution)/shard_map/ppermute | solution.py:28
  155.1 5.0 %collective-permute-done.35.refs_4_ = bf16[1,64,640]{2,1,0:T(8,128)(2,1)S(1)} collective-permute-done((bf16[1,64,640]{2,1,0:T(8,128)(2,1)}, bf16[1,64,640]{2,1,0:T(8,128)(2,1)S(1)}, u32[]{:S(2)}, u32[]{:S(2)}) %collective-permute-start.35) | collective-permute-done | bytes 81952 | tf_op jit(solution)/shard_map/ppermute | solution.py:28
  160.7 0.7 collective-permute-done.36.refs_5_
  162.2 2.2 %finish.1 = f32[1,64,2560]{2,1,0:T(8,128)} custom-call(s32[2]{0:T(128)} %pad_add_fusion.place_ref, f32[1,64,640]{2,1,0:T(8,128)} %get-tuple-element.54.refs_0_, bf16[1,64,640]{2,1,0:T(8,128)(2,1)} %copy-done.21, bf16[1,64,640]{2,1,0:T(8,128)(2,1)} %copy-done.18, bf16[1,64,640]{2,1,0:T(8,128)(2,1)} %copy-done.22, bf16[1,64,640]{2,1,0:T(8,128)(2,1)} %copy-done.19, ...), custom_call_target="tpu_custom_call" | custom-call | bytes 1310720 | tf_op jit(solution)/shard_map/finish/pallas_call | solution.py:340
  (107 shorter events, 9.7 us)
Async XLA Ops:
  0.0 16.2 %copy-start.3 = (bf16[1280,768]{1,0:T(8,128)(2,1)S(1)}, bf16[1280,768]{1,0:T(8,128)(2,1)}, u32[]{:S(2)}) copy-start(bf16[1280,768]{1,0:T(8,128)(2,1)} %param.10) | copy-start | bytes 5898244
  4.5 20.2 %collective-permute-start = (f32[3,4,1280]{2,1,0:T(4,128)}, f32[3,4,1280]{2,1,0:T(4,128)S(1)}, u32[]{:S(2)}, u32[]{:S(2)}) collective-permute-start(f32[3,4,1280]{2,1,0:T(4,128)} %get-tuple-element.33), channel_id=1, source_target_pairs={{0,4},{4,8},{8,12},{12,0},{1,5},{5,9},{9,13},{13,1},{2,6},{6,10},{... | collective-permute-start | bytes 184328 | tf_op jit(solution)/shard_map/ppermute | solution.py:28
  7.6 17.3 %collective-permute-start.1 = (f32[3,4,1280]{2,1,0:T(4,128)}, f32[3,4,1280]{2,1,0:T(4,128)S(1)}, u32[]{:S(2)}, u32[]{:S(2)}) collective-permute-start(f32[3,4,1280]{2,1,0:T(4,128)} %get-tuple-element.34), channel_id=1, source_target_pairs={{0,8},{4,12},{8,0},{12,4},{1,9},{5,13},{9,1},{13,5},{2,10},{6,14},... | collective-permute-start | bytes 184328 | tf_op jit(solution)/shard_map/ppermute | solution.py:28
  12.3 9.8 %copy-start.17 = (bf16[1,32,1408]{2,1,0:T(8,128)(2,1)S(1)}, bf16[1,32,1408]{2,1,0:T(8,128)(2,1)}, u32[]{:S(2)}) copy-start(bf16[1,32,1408]{2,1,0:T(8,128)(2,1)} %get-tuple-element.36) | copy-start | bytes 270340
  12.4 7.5 %collective-permute-start.3 = (bf16[1,32,1408]{2,1,0:T(8,128)(2,1)}, bf16[1,32,1408]{2,1,0:T(8,128)(2,1)S(1)}, u32[]{:S(2)}, u32[]{:S(2)}) collective-permute-start(bf16[1,32,1408]{2,1,0:T(8,128)(2,1)} %get-tuple-element.37), channel_id=1, source_target_pairs={{0,4},{4,8},{8,12},{12,0},{1,5},{5,9},{9,13},{13,1},{2,6},{6,10},{... | collective-permute-start | bytes 270344 | tf_op jit(solution)/shard_map/ppermute | solution.py:28
  12.4 9.8 %collective-permute-start.4 = (bf16[1,32,1408]{2,1,0:T(8,128)(2,1)}, bf16[1,32,1408]{2,1,0:T(8,128)(2,1)S(1)}, u32[]{:S(2)}, u32[]{:S(2)}) collective-permute-start(bf16[1,32,1408]{2,1,0:T(8,128)(2,1)} %get-tuple-element.38), channel_id=1, source_target_pairs={{0,8},{4,12},{8,0},{12,4},{1,9},{5,13},{9,1},{13,5},{2,10},{6,14},... | collective-permute-start | bytes 270344 | tf_op jit(solution)/shard_map/ppermute | solution.py:28
  14.3 7.9 %collective-permute-start.5 = (bf16[1,32,1408]{2,1,0:T(8,128)(2,1)}, bf16[1,32,1408]{2,1,0:T(8,128)(2,1)S(1)}, u32[]{:S(2)}, u32[]{:S(2)}) collective-permute-start(bf16[1,32,1408]{2,1,0:T(8,128)(2,1)} %get-tuple-element.39), channel_id=1, source_target_pairs={{0,12},{4,0},{8,4},{12,8},{1,13},{5,1},{9,5},{13,9},{2,14},{6,2},{... | collective-permute-start | bytes 270344 | tf_op jit(solution)/shard_map/ppermute | solution.py:28
  17.4 58.3 %copy-start.2 = (bf16[640,768]{1,0:T(8,128)(2,1)}, bf16[640,768]{1,0:T(8,128)(2,1)S(1)}, u32[]{:S(2)}) copy-start(bf16[640,768]{1,0:T(8,128)(2,1)S(1)} %get-tuple-element.72.refs_8_) | copy-start | bytes 2949124
  19.9 5.0 %collective-permute-start.2 = (f32[3,4,1280]{2,1,0:T(4,128)}, f32[3,4,1280]{2,1,0:T(4,128)S(1)}, u32[]{:S(2)}, u32[]{:S(2)}) collective-permute-start(f32[3,4,1280]{2,1,0:T(4,128)} %get-tuple-element.35), channel_id=1, source_target_pairs={{0,12},{4,0},{8,4},{12,8},{1,13},{5,1},{9,5},{13,9},{2,14},{6,2},{... | collective-permute-start | bytes 184328 | tf_op jit(solution)/shard_map/ppermute | solution.py:28
  22.2 11.0 %copy-start.4 = (bf16[4,1,32,1408]{3,2,1,0:T(8,128)(2,1)}, bf16[4,1,32,1408]{3,2,1,0:T(8,128)(2,1)S(1)}, u32[]{:S(2)}) copy-start(bf16[4,1,32,1408]{3,2,1,0:T(8,128)(2,1)S(1)} %pad_maximum_fusion.refs_4_) | copy-start | bytes 1081348
  22.2 11.0 %collective-permute-start.10 = (bf16[4,1,32,1408]{3,2,1,0:T(8,128)(2,1)S(1)}, bf16[4,1,32,1408]{3,2,1,0:T(8,128)(2,1)S(1)}, u32[]{:S(2)}, u32[]{:S(2)}) collective-permute-start(bf16[4,1,32,1408]{3,2,1,0:T(8,128)(2,1)S(1)} %pad_maximum_fusion.refs_4_), channel_id=1, source_target_pairs={{0,1},{1,0},{2,3},{3,2},{4,5},{5,4},{6,7},{7,6},{8,9},{9,8},{10,11... | collective-permute-start | bytes 1081352 | tf_op jit(solution)/shard_map/ppermute | solution.py:28
  22.3 10.9 %collective-permute-start.6 = (bf16[4,1,32,1408]{3,2,1,0:T(8,128)(2,1)S(1)}, bf16[4,1,32,1408]{3,2,1,0:T(8,128)(2,1)}, u32[]{:S(2)}, u32[]{:S(2)}) collective-permute-start(bf16[4,1,32,1408]{3,2,1,0:T(8,128)(2,1)S(1)} %pad_maximum_fusion.refs_4_), channel_id=1, source_target_pairs={{0,2},{2,0},{1,3},{3,1},{4,6},{6,4},{5,7},{7,5},{8,10},{10,8},{9,1... | collective-permute-start | bytes 1081352 | tf_op jit(solution)/shard_map/ppermute | solution.py:28
  24.7 8.6 %copy-start.7 = (f32[3,4,1280]{2,1,0:T(4,128)}, f32[3,4,1280]{2,1,0:T(4,128)S(1)}, u32[]{:S(2)}) copy-start(f32[3,4,1280]{2,1,0:T(4,128)S(1)} %collective-permute-done.refs_1_) | copy-start | bytes 184324
  24.7 63.8 %collective-permute-start.29 = (bf16[640,768]{1,0:T(8,128)(2,1)}, bf16[640,768]{1,0:T(8,128)(2,1)}, u32[]{:S(2)}, u32[]{:S(2)}) collective-permute-start(bf16[640,768]{1,0:T(8,128)(2,1)} %get-tuple-element.71), channel_id=1, source_target_pairs={{0,1},{1,0},{2,3},{3,2},{4,5},{5,4},{6,7},{7,6},{8,9},{9,8},{10,11... | collective-permute-start | bytes 2949128 | tf_op jit(solution)/shard_map/ppermute | solution.py:28
  24.8 8.4 %copy-start.8 = (f32[3,4,1280]{2,1,0:T(4,128)}, f32[3,4,1280]{2,1,0:T(4,128)S(1)}, u32[]{:S(2)}) copy-start(f32[3,4,1280]{2,1,0:T(4,128)S(1)} %collective-permute-done.1.refs_2_) | copy-start | bytes 184324
  33.2 17.6 %collective-permute-start.7 = (bf16[4,1,32,1408]{3,2,1,0:T(8,128)(2,1)}, bf16[4,1,32,1408]{3,2,1,0:T(8,128)(2,1)}, u32[]{:S(2)}, u32[]{:S(2)}) collective-permute-start(bf16[4,1,32,1408]{3,2,1,0:T(8,128)(2,1)} %collective-permute-done.6.refs_4_), channel_id=1, source_target_pairs={{0,1},{1,0},{2,3},{3,2},{4,5},{5,4},{6,7},{7,6},{8,9},{9,8},{10,11... | collective-permute-start | bytes 1081352 | tf_op jit(solution)/shard_map/ppermute | solution.py:28
  44.4 18.8 %collective-permute-start.11 = (f16[3,64,768]{2,1,0:T(8,128)(2,1)}, f16[3,64,768]{2,1,0:T(8,128)(2,1)}, u32[]{:S(2)}, u32[]{:S(2)}) collective-permute-start(f16[3,64,768]{2,1,0:T(8,128)(2,1)} %get-tuple-element.68), channel_id=1, source_target_pairs={{0,4},{1,5},{2,6},{3,7},{16,20},{17,21},{18,22},{19,23}} | collective-permute-start | bytes 884744 | tf_op jit(solution)/shard_map/ppermute | solution.py:402
  49.3 14.0 %copy-start = (f32[4,3,64,768]{3,2,1,0:T(8,128)S(1)}, f32[4,3,64,768]{3,2,1,0:T(8,128)}, u32[]{:S(2)}) copy-start(f32[4,3,64,768]{3,2,1,0:T(8,128)} %qkv.3) | copy-start | bytes 7077892
  49.3 14.0 %collective-permute-start.12 = (f16[3,64,768]{2,1,0:T(8,128)(2,1)}, f16[3,64,768]{2,1,0:T(8,128)(2,1)}, u32[]{:S(2)}, u32[]{:S(2)}) collective-permute-start(f16[3,64,768]{2,1,0:T(8,128)(2,1)} %get-tuple-element.67), channel_id=1, source_target_pairs={{12,8},{13,9},{14,10},{15,11},{28,24},{29,25},{30,26},{31,27}} | collective-permute-start | bytes 884744 | tf_op jit(solution)/shard_map/ppermute | solution.py:403
  59.2 10.1 %copy-start.1 = (f32[4,3,64,768]{3,2,1,0:T(8,128)S(1)}, f32[4,3,64,768]{3,2,1,0:T(8,128)}, u32[]{:S(2)}) copy-start(f32[4,3,64,768]{3,2,1,0:T(8,128)} %qkv.2) | copy-start | bytes 7077892
  60.7 8.7 %collective-permute-start.8 = (f16[3,64,768]{2,1,0:T(8,128)(2,1)S(1)}, f16[3,64,768]{2,1,0:T(8,128)(2,1)S(1)}, u32[]{:S(2)}, u32[]{:S(2)}) collective-permute-start(f16[3,64,768]{2,1,0:T(8,128)(2,1)S(1)} %get-tuple-element.70), channel_id=1, source_target_pairs={{0,4},{1,5},{2,6},{3,7},{16,20},{17,21},{18,22},{19,23}} | collective-permute-start | bytes 884744 | tf_op jit(solution)/shard_map/ppermute | solution.py:402
  62.0 7.4 %collective-permute-start.9 = (f16[3,64,768]{2,1,0:T(8,128)(2,1)S(1)}, f16[3,64,768]{2,1,0:T(8,128)(2,1)S(1)}, u32[]{:S(2)}, u32[]{:S(2)}) collective-permute-start(f16[3,64,768]{2,1,0:T(8,128)(2,1)S(1)} %get-tuple-element.69), channel_id=1, source_target_pairs={{12,8},{13,9},{14,10},{15,11},{28,24},{29,25},{30,26},{31,27}} | collective-permute-start | bytes 884744 | tf_op jit(solution)/shard_map/ppermute | solution.py:403
  64.5 11.2 %collective-permute-start.15 = (f16[3,64,768]{2,1,0:T(8,128)(2,1)S(1)}, f16[3,64,768]{2,1,0:T(8,128)(2,1)S(1)}, u32[]{:S(2)}, u32[]{:S(2)}) collective-permute-start(f16[3,64,768]{2,1,0:T(8,128)(2,1)S(1)} %get-tuple-element.64), channel_id=1, source_target_pairs={{0,4},{4,8},{1,5},{5,9},{2,6},{6,10},{3,7},{7,11},{16,20},{20,24},... | collective-permute-start | bytes 884744 | tf_op jit(solution)/shard_map/ppermute | solution.py:402
  65.8 11.4 %collective-permute-start.16 = (f16[3,64,768]{2,1,0:T(8,128)(2,1)S(1)}, f16[3,64,768]{2,1,0:T(8,128)(2,1)S(1)}, u32[]{:S(2)}, u32[]{:S(2)}) collective-permute-start(f16[3,64,768]{2,1,0:T(8,128)(2,1)S(1)} %get-tuple-element.63), channel_id=1, source_target_pairs={{12,8},{8,4},{13,9},{9,5},{14,10},{10,6},{15,11},{11,7},{28,24},{2... | collective-permute-start | bytes 884744 | tf_op jit(solution)/shard_map/ppermute | solution.py:403
  69.5 12.5 %collective-permute-start.13 = (f16[3,64,768]{2,1,0:T(8,128)(2,1)S(1)}, f16[3,64,768]{2,1,0:T(8,128)(2,1)S(1)}, u32[]{:S(2)}, u32[]{:S(2)}) collective-permute-start(f16[3,64,768]{2,1,0:T(8,128)(2,1)S(1)} %get-tuple-element.66), channel_id=1, source_target_pairs={{0,4},{4,8},{1,5},{5,9},{2,6},{6,10},{3,7},{7,11},{16,20},{20,24},... | collective-permute-start | bytes 884744 | tf_op jit(solution)/shard_map/ppermute | solution.py:402
  73.9 9.4 %collective-permute-start.14 = (f16[3,64,768]{2,1,0:T(8,128)(2,1)S(1)}, f16[3,64,768]{2,1,0:T(8,128)(2,1)S(1)}, u32[]{:S(2)}, u32[]{:S(2)}) collective-permute-start(f16[3,64,768]{2,1,0:T(8,128)(2,1)S(1)} %get-tuple-element.65), channel_id=1, source_target_pairs={{12,8},{8,4},{13,9},{9,5},{14,10},{10,6},{15,11},{11,7},{28,24},{2... | collective-permute-start | bytes 884744 | tf_op jit(solution)/shard_map/ppermute | solution.py:403
  75.7 51.9 %collective-permute-start.30 = (bf16[640,768]{1,0:T(8,128)(2,1)S(1)}, bf16[640,768]{1,0:T(8,128)(2,1)}, u32[]{:S(2)}, u32[]{:S(2)}) collective-permute-start(bf16[640,768]{1,0:T(8,128)(2,1)S(1)} %get-tuple-element.72.refs_8_), channel_id=1, source_target_pairs={{0,2},{2,0},{1,3},{3,1},{4,6},{6,4},{5,7},{7,5},{8,10},{10,8},{9,1... | collective-permute-start | bytes 2949128 | tf_op jit(solution)/shard_map/ppermute | solution.py:28
  77.3 12.5 %collective-permute-start.17 = (f16[3,64,768]{2,1,0:T(8,128)(2,1)S(1)}, f16[3,64,768]{2,1,0:T(8,128)(2,1)S(1)}, u32[]{:S(2)}, u32[]{:S(2)}) collective-permute-start(f16[3,64,768]{2,1,0:T(8,128)(2,1)S(1)} %get-tuple-element.61), channel_id=1, source_target_pairs={{0,4},{4,8},{8,12},{1,5},{5,9},{9,13},{2,6},{6,10},{10,14},{3,7},{... | collective-permute-start | bytes 884744 | tf_op jit(solution)/shard_map/ppermute | solution.py:402
  82.0 11.6 %collective-permute-start.18 = (f16[3,64,768]{2,1,0:T(8,128)(2,1)S(1)}, f16[3,64,768]{2,1,0:T(8,128)(2,1)S(1)}, u32[]{:S(2)}, u32[]{:S(2)}) collective-permute-start(f16[3,64,768]{2,1,0:T(8,128)(2,1)S(1)} %get-tuple-element.62), channel_id=1, source_target_pairs={{12,8},{8,4},{4,0},{13,9},{9,5},{5,1},{14,10},{10,6},{6,2},{15,11}... | collective-permute-start | bytes 884744 | tf_op jit(solution)/shard_map/ppermute | solution.py:403
  83.4 11.1 %collective-permute-start.19 = (f16[3,64,768]{2,1,0:T(8,128)(2,1)S(1)}, f16[3,64,768]{2,1,0:T(8,128)(2,1)S(1)}, u32[]{:S(2)}, u32[]{:S(2)}) collective-permute-start(f16[3,64,768]{2,1,0:T(8,128)(2,1)S(1)} %get-tuple-element.59), channel_id=1, source_target_pairs={{0,4},{4,8},{8,12},{1,5},{5,9},{9,13},{2,6},{6,10},{10,14},{3,7},{... | collective-permute-start | bytes 884744 | tf_op jit(solution)/shard_map/ppermute | solution.py:402
  88.5 10.6 %collective-permute-start.20 = (f16[3,64,768]{2,1,0:T(8,128)(2,1)S(1)}, f16[3,64,768]{2,1,0:T(8,128)(2,1)S(1)}, u32[]{:S(2)}, u32[]{:S(2)}) collective-permute-start(f16[3,64,768]{2,1,0:T(8,128)(2,1)S(1)} %get-tuple-element.60), channel_id=1, source_target_pairs={{12,8},{8,4},{4,0},{13,9},{9,5},{5,1},{14,10},{10,6},{6,2},{15,11}... | collective-permute-start | bytes 884744 | tf_op jit(solution)/shard_map/ppermute | solution.py:403
  89.8 48.9 %collective-permute-start.31 = (bf16[640,768]{1,0:T(8,128)(2,1)}, bf16[640,768]{1,0:T(8,128)(2,1)}, u32[]{:S(2)}, u32[]{:S(2)}) collective-permute-start(bf16[640,768]{1,0:T(8,128)(2,1)} %collective-permute-done.29.refs_9_), channel_id=1, source_target_pairs={{0,2},{2,0},{1,3},{3,1},{4,6},{6,4},{5,7},{7,5},{8,10},{10,8},{9,1... | collective-permute-start | bytes 2949128 | tf_op jit(solution)/shard_map/ppermute | solution.py:28
  103.6 18.0 %collective-permute-start.21 = (bf16[1,64,768]{2,1,0:T(8,128)(2,1)}, bf16[1,64,768]{2,1,0:T(8,128)(2,1)S(1)}, u32[]{:S(2)}, u32[]{:S(2)}) collective-permute-start(bf16[1,64,768]{2,1,0:T(8,128)(2,1)} %get-tuple-element.53), channel_id=1, source_target_pairs={{0,2},{2,0},{1,3},{3,1},{4,6},{6,4},{5,7},{7,5},{8,10},{10,8},{9,1... | collective-permute-start | bytes 294920 | tf_op jit(solution)/shard_map/ppermute | solution.py:28
  122.6 17.4 %copy-start.5 = (bf16[2,1,64,768]{3,2,1,0:T(8,128)(2,1)}, bf16[2,1,64,768]{3,2,1,0:T(8,128)(2,1)S(1)}, u32[]{:S(2)}) copy-start(bf16[2,1,64,768]{3,2,1,0:T(8,128)(2,1)S(1)} %pad_maximum_fusion.1.refs_0_) | copy-start | bytes 589828
  122.6 9.7 %collective-permute-start.23 = (bf16[2,1,64,768]{3,2,1,0:T(8,128)(2,1)S(1)}, bf16[2,1,64,768]{3,2,1,0:T(8,128)(2,1)S(1)}, u32[]{:S(2)}, u32[]{:S(2)}) collective-permute-start(bf16[2,1,64,768]{3,2,1,0:T(8,128)(2,1)S(1)} %pad_maximum_fusion.1.refs_0_), channel_id=1, source_target_pairs={{0,4},{4,8},{8,12},{12,0},{1,5},{5,9},{9,13},{13,1},{2,6},{6,10},{... | collective-permute-start | bytes 589832 | tf_op jit(solution)/shard_map/ppermute | solution.py:28
  125.1 13.1 %collective-permute-start.25 = (bf16[2,1,64,768]{3,2,1,0:T(8,128)(2,1)S(1)}, bf16[2,1,64,768]{3,2,1,0:T(8,128)(2,1)S(1)}, u32[]{:S(2)}, u32[]{:S(2)}) collective-permute-start(bf16[2,1,64,768]{3,2,1,0:T(8,128)(2,1)S(1)} %pad_maximum_fusion.1.refs_0_), channel_id=1, source_target_pairs={{0,8},{4,12},{8,0},{12,4},{1,9},{5,13},{9,1},{13,5},{2,10},{6,14},... | collective-permute-start | bytes 589832 | tf_op jit(solution)/shard_map/ppermute | solution.py:28
  125.1 13.1 %collective-permute-start.27 = (bf16[2,1,64,768]{3,2,1,0:T(8,128)(2,1)S(1)}, bf16[2,1,64,768]{3,2,1,0:T(8,128)(2,1)S(1)}, u32[]{:S(2)}, u32[]{:S(2)}) collective-permute-start(bf16[2,1,64,768]{3,2,1,0:T(8,128)(2,1)S(1)} %pad_maximum_fusion.1.refs_0_), channel_id=1, source_target_pairs={{0,12},{4,0},{8,4},{12,8},{1,13},{5,1},{9,5},{13,9},{2,14},{6,2},{... | collective-permute-start | bytes 589832 | tf_op jit(solution)/shard_map/ppermute | solution.py:28
  127.6 11.2 %collective-permute-start.22 = (bf16[2,1,64,768]{3,2,1,0:T(8,128)(2,1)S(1)}, bf16[2,1,64,768]{3,2,1,0:T(8,128)(2,1)S(1)}, u32[]{:S(2)}, u32[]{:S(2)}) collective-permute-start(bf16[2,1,64,768]{3,2,1,0:T(8,128)(2,1)S(1)} %pad_maximum_fusion.1.refs_0_), channel_id=1, source_target_pairs={{0,1},{1,0},{2,3},{3,2},{4,5},{5,4},{6,7},{7,6},{8,9},{9,8},{10,11... | collective-permute-start | bytes 589832 | tf_op jit(solution)/shard_map/ppermute | solution.py:28
  132.3 6.5 %collective-permute-start.24 = (bf16[2,1,64,768]{3,2,1,0:T(8,128)(2,1)S(1)}, bf16[2,1,64,768]{3,2,1,0:T(8,128)(2,1)S(1)}, u32[]{:S(2)}, u32[]{:S(2)}) collective-permute-start(bf16[2,1,64,768]{3,2,1,0:T(8,128)(2,1)S(1)} %collective-permute-done.23.refs_2_), channel_id=1, source_target_pairs={{0,1},{1,0},{2,3},{3,2},{4,5},{5,4},{6,7},{7,6},{8,9},{9,8},{10,11... | collective-permute-start | bytes 589832 | tf_op jit(solution)/shard_map/ppermute | solution.py:28
  138.2 1.4 collective-permute-start.26
  138.2 1.7 %collective-permute-start.28 = (bf16[2,1,64,768]{3,2,1,0:T(8,128)(2,1)S(1)}, bf16[2,1,64,768]{3,2,1,0:T(8,128)(2,1)S(1)}, u32[]{:S(2)}, u32[]{:S(2)}) collective-permute-start(bf16[2,1,64,768]{3,2,1,0:T(8,128)(2,1)S(1)} %collective-permute-done.27.refs_6_), channel_id=1, source_target_pairs={{0,1},{1,0},{2,3},{3,2},{4,5},{5,4},{6,7},{7,6},{8,9},{9,8},{10,11... | collective-permute-start | bytes 589832 | tf_op jit(solution)/shard_map/ppermute | solution.py:28
  146.5 8.6 %collective-permute-start.33 = (bf16[1,64,640]{2,1,0:T(8,128)(2,1)}, bf16[1,64,640]{2,1,0:T(8,128)(2,1)S(1)}, u32[]{:S(2)}, u32[]{:S(2)}) collective-permute-start(bf16[1,64,640]{2,1,0:T(8,128)(2,1)} %get-tuple-element.56), channel_id=1, source_target_pairs={{0,12},{4,0},{8,4},{12,8},{1,13},{5,1},{9,5},{13,9},{2,14},{6,2},{... | collective-permute-start | bytes 245768 | tf_op jit(solution)/shard_map/ppermute | solution.py:28
  151.9 8.2 %collective-permute-start.35 = (bf16[1,64,640]{2,1,0:T(8,128)(2,1)}, bf16[1,64,640]{2,1,0:T(8,128)(2,1)S(1)}, u32[]{:S(2)}, u32[]{:S(2)}) collective-permute-start(bf16[1,64,640]{2,1,0:T(8,128)(2,1)} %get-tuple-element.57), channel_id=1, source_target_pairs={{0,8},{4,12},{8,0},{12,4},{1,9},{5,13},{9,1},{13,5},{2,10},{6,14},... | collective-permute-start | bytes 245768 | tf_op jit(solution)/shard_map/ppermute | solution.py:28
  152.0 8.1 %collective-permute-start.37 = (bf16[1,64,640]{2,1,0:T(8,128)(2,1)}, bf16[1,64,640]{2,1,0:T(8,128)(2,1)S(1)}, u32[]{:S(2)}, u32[]{:S(2)}) collective-permute-start(bf16[1,64,640]{2,1,0:T(8,128)(2,1)} %get-tuple-element.58), channel_id=1, source_target_pairs={{0,4},{4,8},{8,12},{12,0},{1,5},{5,9},{9,13},{13,1},{2,6},{6,10},{... | collective-permute-start | bytes 245768 | tf_op jit(solution)/shard_map/ppermute | solution.py:28
  152.6 8.1 %collective-permute-start.32 = (bf16[1,64,640]{2,1,0:T(8,128)(2,1)}, bf16[1,64,640]{2,1,0:T(8,128)(2,1)S(1)}, u32[]{:S(2)}, u32[]{:S(2)}) collective-permute-start(bf16[1,64,640]{2,1,0:T(8,128)(2,1)} %get-tuple-element.55), channel_id=1, source_target_pairs={{0,1},{1,0},{2,3},{3,2},{4,5},{5,4},{6,7},{7,6},{8,9},{9,8},{10,11... | collective-permute-start | bytes 245768 | tf_op jit(solution)/shard_map/ppermute | solution.py:28
  155.1 5.6 %collective-permute-start.34 = (bf16[1,64,640]{2,1,0:T(8,128)(2,1)S(1)}, bf16[1,64,640]{2,1,0:T(8,128)(2,1)S(1)}, u32[]{:S(2)}, u32[]{:S(2)}) collective-permute-start(bf16[1,64,640]{2,1,0:T(8,128)(2,1)S(1)} %collective-permute-done.33.refs_2_), channel_id=1, source_target_pairs={{0,1},{1,0},{2,3},{3,2},{4,5},{5,4},{6,7},{7,6},{8,9},{9,8},{10,11... | collective-permute-start | bytes 245768 | tf_op jit(solution)/shard_map/ppermute | solution.py:28
  160.2 1.3 collective-permute-start.36
  160.2 1.4 collective-permute-start.38
  (16 other events, 36.5 us)

commit v4 on v3

v4 whole, which is shorter than its diff:
```python
import functools

import jax
import jax.numpy as jnp
from jax import lax
from jax.experimental import pallas as pl
from jax.experimental.pallas import tpu as pltpu
from jax.sharding import PartitionSpec as P


HEAD_DIM = 128
FREQ = 256
STEPS = 100
LANES = 128


sample_shift = 5.0
norm_eps = 1e-06


def sigma_of(index):
    unit = 1.0 - index.astype(jnp.float32) / jnp.float32(STEPS)
    return sample_shift * unit / (1.0 + (sample_shift - 1.0) * unit)


def turn(block, axis, distance):
    size = lax.axis_size(axis)
    return lax.ppermute(block, axis, [(i, (i + distance) % size) for i in range(size)])


def take(array, index, dim=0):
    return lax.dynamic_index_in_dim(array, index, dim, keepdims=False)


def head_norm(values, gain):
    meansq = jnp.mean(values * values, axis=-1, keepdims=True)
    return (values * lax.rsqrt(meansq + norm_eps) * gain).astype(jnp.bfloat16)


def head_groups(cols):
    heads = cols // HEAD_DIM
    first = (heads + 1) // 2 * HEAD_DIM
    return ((0, first), (first, cols - first)) if first < cols else ((0, cols),)


def attend_kernel(n_seq, heads, gain_ref, whole_ref, *outs):
    inv_root = 1.0 / jnp.sqrt(jnp.float32(HEAD_DIM))
    rows = whole_ref.shape[3]
    for h in range(heads):
        lanes = pl.ds(h * HEAD_DIM, HEAD_DIM)
        q, k, v = (
            jnp.concatenate([whole_ref[c, j, 0, :, lanes] for j in range(n_seq)], axis=0)
            for c in range(3)
        )
        q = head_norm(q, gain_ref[0:1, lanes])
        k = head_norm(k, gain_ref[1:2, lanes])
        scores = lax.dot_general(
            q, k, (((1,), (1,)), ((), ())), preferred_element_type=jnp.float32
        )
        expo = jnp.exp(scores * inv_root)
        probs = (expo / jnp.sum(expo, axis=-1, keepdims=True)).astype(jnp.bfloat16)
        attn = jnp.dot(
            probs, v.astype(jnp.bfloat16), preferred_element_type=jnp.float32
        ).astype(jnp.bfloat16)
        for j, out in enumerate(outs):
            out[0, :, lanes] = attn[j * rows : (j + 1) * rows]


def attend(whole, gain):
    _, n_seq, frames, rows, cols = whole.shape
    heads = cols // HEAD_DIM
    tokens = rows * n_seq
    out = jax.ShapeDtypeStruct((frames, rows, cols), jnp.bfloat16)
    return pl.pallas_call(
        functools.partial(attend_kernel, n_seq, heads),
        grid=(frames,),
        in_specs=[
            pl.BlockSpec((2, cols), lambda f: (0, 0)),
            pl.BlockSpec((3, n_seq, 1, rows, cols), lambda f: (0, 0, f, 0, 0)),
        ],
        out_specs=[pl.BlockSpec((1, rows, cols), lambda f: (f, 0, 0))] * n_seq,
        out_shape=[out] * n_seq,
        cost_estimate=pl.CostEstimate(
            flops=4 * frames * heads * tokens * tokens * HEAD_DIM,
            bytes_accessed=14 * frames * tokens * cols,
            transcendentals=frames * heads * tokens * tokens,
        ),
        name="attend",
    )(gain, whole)


def spread_kernel(n_tm, states_ref, *outs):
    z, m = lax.axis_index("tm"), lax.axis_index("mp")
    frames, _, width = states_ref.shape
    part, depth = outs[0].shape[1], width // n_tm
    own = pl.ds(pl.multiple_of(m * part, part), part)
    lane = lax.broadcasted_iota(jnp.int32, (part, LANES), 1)
    for f in range(frames):
        field = states_ref[f, own, :].astype(jnp.float32)
        mean = jnp.mean(field, axis=-1, keepdims=True)
        centred = field - mean
        var = jnp.mean(centred * centred, axis=-1, keepdims=True)
        tail = jnp.zeros((part, LANES), jnp.float32)
        for place, rest in enumerate((mean, lax.rsqrt(var + norm_eps))):
            for term in range(3):
                cut = rest.astype(jnp.bfloat16).astype(jnp.float32)
                tail = jnp.where(lane == 3 * place + term, cut, tail)
                rest = rest - cut
        tail = tail.astype(jnp.bfloat16)
        for k, out in enumerate(outs):
            out[f, :, depth:] = tail
            for s in range(n_tm):

                @pl.when(lax.rem(z + k, n_tm) == s)
                def _():
                    out[f, :, :depth] = states_ref[f, own, s * depth : (s + 1) * depth]


def spread(states, n_tm, part):
    frames, _, width = states.shape
    out = jax.ShapeDtypeStruct((frames, part, width // n_tm + LANES), jnp.bfloat16)
    return pl.pallas_call(
        functools.partial(spread_kernel, n_tm),
        in_specs=[pl.BlockSpec(memory_space=pltpu.VMEM)],
        out_specs=[pl.BlockSpec(memory_space=pltpu.VMEM)] * n_tm,
        out_shape=[out] * n_tm,
        cost_estimate=pl.CostEstimate(
            flops=10 * part * width, bytes_accessed=4 * part * width, transcendentals=0
        ),
        name="spread",
    )(states)


def time_kernel(n_tm, step_ref, proj_ref, *outs):
    z = lax.axis_index("tm")
    freq_rows, wide = proj_ref.shape
    window, depth = outs[0].shape[1:]
    half_freq = FREQ // 2
    index = step_ref[0] + lax.broadcasted_iota(jnp.int32, (window, freq_rows), 0)
    feature = z * freq_rows + lax.broadcasted_iota(jnp.int32, (window, freq_rows), 1)
    late = feature >= half_freq
    rank = jnp.where(late, feature - half_freq, feature).astype(jnp.float32)
    freqs = jnp.exp(-jnp.log(jnp.float32(10000.0)) * rank / jnp.float32(half_freq))
    angles = (1000.0 * sigma_of(index)) * freqs
    emb = jnp.where(late, jnp.sin(angles), jnp.cos(angles)).astype(jnp.bfloat16)
    for k, out in enumerate(outs):
        for s in range(n_tm):

            @pl.when(lax.rem(z + k, n_tm) == s)
            def _():
                for c in range(3):
                    first = c * (wide // 3) + s * depth
                    out[c] = jnp.dot(
                        emb, proj_ref[:, first : first + depth], preferred_element_type=jnp.float32
                    )


def time_shares(start_step, time_proj, n_tm, window):
    freq_rows, wide = time_proj.shape
    out = jax.ShapeDtypeStruct((3, window, wide // (3 * n_tm)), jnp.float32)
    smem, vmem = (pl.BlockSpec(memory_space=space) for space in (pltpu.SMEM, pltpu.VMEM))
    return pl.pallas_call(
        functools.partial(time_kernel, n_tm),
        in_specs=[smem, vmem],
        out_specs=[vmem] * n_tm,
        out_shape=[out] * n_tm,
        cost_estimate=pl.CostEstimate(
            flops=2 * window * freq_rows * wide, bytes_accessed=2 * freq_rows * wide, transcendentals=0
        ),
        name="time_shares",
    )(start_step, time_proj)


def modulate_kernel(n_tm, n_seq, n_mp, step_ref, *refs):
    shares, rows, (hidden_ref, coef_ref, mod_scr) = refs[:n_tm], refs[n_tm:-3], refs[-3:]
    z = lax.axis_index("tm")
    _, frames, part, wide = rows[0].shape
    depth = wide - LANES
    total = shares[0][...]
    for share in shares[1:]:
        total = total + share[...]
    mod_scr[...] = total
    for k in range(n_tm):
        for f in range(frames):
            step = pl.ds(lax.rem(z - k + n_tm, n_tm) * frames + f, 1)
            shift, scale = mod_scr[0, step, :], mod_scr[1, step, :]
            index = jnp.full((1, depth), step_ref[0] + step.start, jnp.int32)
            size = sigma_of(index + 1) - sigma_of(index)
            coef_ref[k, f : f + 1, :] = size * mod_scr[2, step, :]
            for j in range(n_seq):
                for i in range(n_mp):
                    row = rows[j * n_mp + i]
                    tail = row[k, f, :, depth:].astype(jnp.float32)
                    mean = tail[:, 0:1] + tail[:, 1:2] + tail[:, 2:3]
                    rstd = tail[:, 3:4] + tail[:, 4:5] + tail[:, 5:6]
                    normed = (row[k, f, :, :depth].astype(jnp.float32) - mean) * rstd
                    hidden_ref[k, j, f, i * part : (i + 1) * part, :] = (
                        normed * (1.0 + scale) + shift
                    ).astype(jnp.bfloat16)


def modulate(start_step, shares, rows):
    n_tm, n_seq, n_mp = len(shares), len(rows), len(rows[0])
    _, frames, part, wide = rows[0][0].shape
    depth = wide - LANES
    window = shares[0].shape[1]
    smem, vmem = (pl.BlockSpec(memory_space=space) for space in (pltpu.SMEM, pltpu.VMEM))
    shape = (n_tm, n_seq, frames, n_mp * part, depth)
    return pl.pallas_call(
        functools.partial(modulate_kernel, n_tm, n_seq, n_mp),
        in_specs=[smem] + [vmem] * (n_tm + n_seq * n_mp),
        out_specs=[vmem] * 2,
        scratch_shapes=[pltpu.VMEM((3, window, depth), jnp.float32)],
        out_shape=[
            jax.ShapeDtypeStruct(shape, jnp.bfloat16),
            jax.ShapeDtypeStruct((n_tm, frames, depth), jnp.float32),
        ],
        cost_estimate=pl.CostEstimate(
            flops=4 * n_tm * n_seq * frames * n_mp * part * depth,
            bytes_accessed=4 * n_tm * n_seq * frames * n_mp * part * depth,
            transcendentals=0,
        ),
        name="modulate",
    )(start_step, *shares, *[r for side in rows for r in side])


def project_kernel(dims, widths, coef_ref, *refs):
    n_tm, n_seq, n_mp, frames, part, _ = dims
    n_attn = len(widths) * n_tm * n_mp
    attn_refs = refs[:n_attn]
    w_refs = refs[n_attn : n_attn + n_seq * n_mp]
    outs = refs[n_attn + n_seq * n_mp :]
    own_ref, moved_refs, (rows_scr, w_scr, sum_scr, sems) = outs[0], outs[1:-4], outs[-4:]
    z, m = lax.axis_index("tm"), lax.axis_index("mp")
    block = n_mp * part
    per = frames * block
    half = own_ref.shape[-1]
    copies = []
    for j in range(n_seq):
        for l in range(n_mp):
            at = j * n_mp + l
            group = [pltpu.make_async_copy(w_refs[at], w_scr.at[at], sems.at[at, 0])]
            for k in range(n_tm):
                for f in range(frames):
                    for i in range(n_mp):
                        first = k * per + f * block + i * part
                        source = (i - l) % n_mp * part
                        for h, (lane, width) in enumerate(widths):
                            piece = attn_refs[(h * n_tm + k) * n_mp + l]
                            group.append(
                                pltpu.make_async_copy(
                                    piece.at[j, f, pl.ds(source, part)],
                                    rows_scr.at[at, pl.ds(first, part), pl.ds(lane, width)],
                                    sems.at[at, len(group)],
                                )
                            )
            for copy in group:
                copy.start()
            copies.append(group)
    total = None
    for at, group in enumerate(copies):
        for copy in group:
            copy.wait()
        product = lax.dot_general(
            rows_scr[at], w_scr[at], (((1,), (1,)), ((), ())), preferred_element_type=jnp.float32
        )
        total = product if total is None else total + product
    for k in range(n_tm):
        for f in range(frames):
            first = k * per + f * block
            factor = coef_ref[k, f : f + 1, :half]
            for mm in range(1, n_mp):
                other = coef_ref[k, f : f + 1, mm * half : (mm + 1) * half]
                factor = jnp.where(m == mm, other, factor)
            drift = total[first : first + block] * factor
            sum_scr[lax.rem(z - k + n_tm, n_tm), f] = drift
    for s in range(n_tm):
        for f in range(frames):
            if s or f:
                before = sum_scr[s, f - 1] if f else sum_scr[s - 1, frames - 1]
                sum_scr[s, f] = sum_scr[s, f] + before
    for k in range(n_tm):
        own = lax.rem(z - k + n_tm, n_tm)
        for f in range(frames):
            for i in range(n_mp):
                to = pl.ds(pl.multiple_of(lax.rem(m - i + n_mp, n_mp) * part, part), part)
                piece = sum_scr[own, f, i * part : (i + 1) * part, :]
                moved_refs[k][f, to, :] = piece.astype(jnp.bfloat16)
                if k == 0:
                    own_ref[f, to, :] = piece


def project(attn, weights, coef, dims, widths):
    n_tm, n_seq, n_mp, frames, part, cols = dims
    half = weights[0][0].shape[0]
    tok = n_mp * part
    rows = n_tm * frames * tok
    deep = n_seq * n_mp * cols
    vmem, anywhere = (pl.BlockSpec(memory_space=space) for space in (pltpu.VMEM, pl.ANY))
    return pl.pallas_call(
        functools.partial(project_kernel, dims, widths),
        in_specs=[vmem] + [anywhere] * (len(widths) * n_tm * n_mp + n_seq * n_mp),
        out_specs=[vmem] * (1 + n_tm),
        scratch_shapes=[
            pltpu.VMEM((n_seq * n_mp, rows, cols), jnp.bfloat16),
            pltpu.VMEM((n_seq * n_mp, half, cols), jnp.bfloat16),
            pltpu.VMEM((n_tm, frames, tok, half), jnp.float32),
            pltpu.SemaphoreType.DMA((n_seq * n_mp, 1 + len(widths) * n_tm * frames * n_mp)),
        ],
        out_shape=[jax.ShapeDtypeStruct((frames, tok, half), jnp.float32)]
        + [jax.ShapeDtypeStruct((frames, tok, half), jnp.bfloat16)] * n_tm,
        cost_estimate=pl.CostEstimate(
            flops=2 * rows * deep * half, bytes_accessed=2 * (rows + half) * deep, transcendentals=0
        ),
        name="project",
    )(coef, *[a for h in attn for k in h for a in k], *[w for j in weights for w in j])


def finish_kernel(n_tm, n_mp, *refs):
    out = refs[-1]
    z, m = lax.axis_index("tm"), lax.axis_index("mp")
    half = refs[0].shape[-1]
    slices = n_tm // n_mp
    for u in range(slices):
        k_here = lax.rem(m * slices + u - z + n_tm, n_tm)
        for h in range(n_mp):
            first = (u * n_mp + h) * half
            for k in range(n_tm):
                for l in range(n_mp):

                    @pl.when((k_here == k) & (lax.rem(m - h + n_mp, n_mp) == l))
                    def _():
                        out[:, :, first : first + half] = refs[k * n_mp + l][...].astype(
                            jnp.float32
                        )


def finish(blocks):
    n_tm, n_mp = len(blocks), len(blocks[0])
    frames, tok, half = blocks[0][0].shape
    vmem = pl.BlockSpec(memory_space=pltpu.VMEM)
    return pl.pallas_call(
        functools.partial(finish_kernel, n_tm, n_mp),
        in_specs=[vmem] * (n_tm * n_mp),
        out_specs=vmem,
        out_shape=jax.ShapeDtypeStruct((frames, tok, n_tm * half), jnp.float32),
        cost_estimate=pl.CostEstimate(
            flops=0, bytes_accessed=8 * frames * tok * n_tm * half, transcendentals=0
        ),
        name="finish",
    )(*[b for k in blocks for b in k])


def sweep(states, start_step, w_qkv, qk_gain, w_out, time_proj):
    frames, tok, _ = states.shape
    n_tm, n_seq, n_mp = (lax.axis_size(name) for name in ("tm", "seq", "mp"))
    m = lax.axis_index("mp")
    part = tok // n_mp
    depth, cols = w_qkv.shape[1:]
    half = depth // n_mp
    window = frames * n_tm

    raw = list(spread(states, n_tm, part))
    for k in range(1, n_tm):
        raw[k] = turn(raw[k], "tm", k)
    raw = jnp.stack(raw)
    sides = [raw]
    for j in range(1, n_seq):
        sides.append(turn(raw, "seq", j))
    rows = []
    for side in sides:
        rows.append([side] + [turn(side, "mp", i) for i in range(1, n_mp)])

    shares = list(time_shares(start_step, time_proj, n_tm, window))
    for k in range(1, n_tm):
        shares[k] = turn(shares[k], "tm", k)

    share = w_out.reshape(n_mp, half, cols)
    weights = [take(share, m)]
    weights += [turn(take(share, (m + i) % n_mp), "mp", i) for i in range(1, n_mp)]
    weights = [weights]
    for j in range(1, n_seq):
        weights.append([turn(s, "seq", -j) for s in weights[0]])

    hidden, coef = modulate(start_step, shares, rows)
    hidden = hidden.reshape(n_tm, n_seq * frames * tok, depth)
    groups = head_groups(cols)
    proj = []
    for lane, size in groups:
        proj.append(
            jnp.einsum(
                "krd,cdh->kcrh",
                hidden,
                w_qkv[:, :, lane : lane + size],
                preferred_element_type=jnp.float32,
            )
        )
    right, left = [None] * len(groups), [None] * len(groups)
    for t in range(n_tm - 1):
        for h in range(len(groups)):
            send_right, send_left = proj[h][(t + 1) % n_tm], proj[h][n_tm - 1 - t]
            if t:
                right[h], left[h] = lax.optimization_barrier((right[h], left[h]))
                send_right = send_right + right[h].astype(jnp.float32)
                send_left = send_left + left[h].astype(jnp.float32)
            send_right, send_left = (send_right.astype(jnp.float16), send_left.astype(jnp.float16))
            right[h] = lax.ppermute(send_right, "tm", [(i, i + 1) for i in range(t + 1)])
            left[h] = lax.ppermute(
                send_left, "tm", [(n_tm - 1 - i, n_tm - 2 - i) for i in range(t + 1)]
            )
    gathered = []
    for h, (lane, size) in enumerate(groups):
        total = proj[h][0] + right[h].astype(jnp.float32) + left[h].astype(jnp.float32)
        total = total.reshape(3, n_seq, frames, tok, size)
        attn = attend(total, qk_gain[:, lane : lane + size])
        attn = jnp.stack([attn[0]] + [turn(attn[j], "seq", -j) for j in range(1, n_seq)])
        pieces = [attn]
        for k in range(1, n_tm):
            pieces.append(turn(attn, "tm", k))
        gathered.append([[g] + [turn(g, "mp", i) for i in range(1, n_mp)] for g in pieces])

    own, *moved = project(
        gathered, weights, coef, (n_tm, n_seq, n_mp, frames, part, cols), groups
    )
    blocks = []
    for k in range(n_tm):
        block = moved[0]
        if k:
            block = turn(moved[k], "tm", -k)
        others = [turn(block, "mp", i) for i in range(1, n_mp)]
        blocks.append([block if k else own] + others)
    return finish(blocks)


def solution(mesh):
    return jax.shard_map(
        sweep,
        mesh=mesh,
        in_specs=(
            P(("group", "tm"), "seq", None),
            P("group"),
            P(None, "tm", ("seq", "mp")),
            P(None, ("seq", "mp")),
            P("tm", ("seq", "mp")),
            P("tm", None),
        ),
        out_specs=P(("group", "tm"), "seq", "mp"),
        check_vma=False,
    )
```

time: 165 us -> 162 us (0.982)
  Pallas kernels: 33.4 us -> 22.4 us
  matrix products: 0 us -> 7.92 us
  starting transfers between devices: 55.3 us -> 61.4 us
  other arithmetic: 9.25 us -> 6.39 us
  waiting for transfers between devices: 60.9 us -> 59 us
    pallas_call x6, Pallas kernels: 31.2 us -> 20.2 us  [the longest x1 5.85 us: project(): pl.pallas_call(functools.partial(project_kernel, dims, widths), in_specs=...]
    dot_general x0 -> x2, matrix products: none -> 7.92 us  [sweep(): jnp.einsum('krd,cdh->kcrh', hidden, w_qkv[:, :, lane:lane + size], prefer...]
    ppermute x6, waiting for transfers between devices: 6.87 us -> 1.7 us  [sweep(): lax.ppermute(send_left, 'tm', [(n_tm - 1 - i, n_tm - 2 - i) for i in rang...]
    convert_element_type x4, other arithmetic: 4.89 us -> 0.5 us  [sweep(): send_left.astype(jnp.float16)]
    ppermute x27 -> x35, starting transfers between devices: 27.9 us -> 32 us  [turn(): lax.ppermute(block, axis, [(i, (i + distance) % size) for i in range(size)])]
    add x0 -> x2, other arithmetic: none -> 2.87 us  [sweep(): proj[h][0] + right[h].astype(jnp.float32) + left[h].astype(jnp.float32)]
    ppermute x6, starting transfers between devices: 21.3 us -> 24.1 us  [sweep(): lax.ppermute(send_right, 'tm', [(i, i + 1) for i in range(t + 1)])]
    ppermute x6, waiting for transfers between devices: 4.21 us -> 6.66 us  [sweep(): lax.ppermute(send_right, 'tm', [(i, i + 1) for i in range(t + 1)])]
  transfers between devices with their start and end apart: 39 -> 47, of which waited for: 17 -> 24; matrix products, arithmetic and copies ran while one was open for 6% -> 4% of each run, Pallas kernels for 14% -> 5%
where the time goes in v4:
time: 162 us; the launch traced here: 161 us
  starting transfers between devices  61.4 us (38%)
  waiting for transfers between devices  59 us (36%)
  Pallas kernels  22.4 us (14%)
  matrix products  7.92 us (5%)
  other arithmetic  6.39 us (4%)
  local copies, waits for them, and re-layouts  2.76 us (2%)
    ppermute x35, waiting for transfers between devices, turn(): lax.ppermute(block, axis, [(i, (i + distance) % size) for i in range(size)])  50.6 us
    ppermute x35, starting transfers between devices, turn(): lax.ppermute(block, axis, [(i, (i + distance) % size) for i in range(size)])  32 us
    ppermute x6, starting transfers between devices, sweep(): lax.ppermute(send_right, 'tm', [(i, i + 1) for i in range(t + 1)])  24.1 us
    dot_general x2, matrix products, sweep(): jnp.einsum('krd,cdh->kcrh', hidden, w_qkv[:, :, lane:lane + size], prefer...  7.92 us
    ppermute x6, waiting for transfers between devices, sweep(): lax.ppermute(send_right, 'tm', [(i, i + 1) for i in range(t + 1)])  6.66 us
    pallas_call x1, Pallas kernels, project(): pl.pallas_call(functools.partial(project_kernel, dims, widths), in_specs=...  5.85 us
    pallas_call x2, Pallas kernels, attend(): pl.pallas_call(functools.partial(attend_kernel, n_seq, heads), grid=(fram...  5.3 us
    ppermute x6, starting transfers between devices, sweep(): lax.ppermute(send_left, 'tm', [(n_tm - 1 - i, n_tm - 2 - i) for i in rang...  5.28 us
  transfers between devices with their start and end apart: 47, of which 24 were waited for; matrix products, arithmetic and copies ran while one was open for 4% of the time, Pallas kernels for 5%

profile of v4, /device:TPU:0, one launch (start us, length us, event | category | flops | bytes accessed | tf_op | source)
XLA Modules:
  0.0 161.0 jit_solution(8388700144018341994)
XLA Ops:
  0.0 2.2 %spread.1 = (bf16[1,32,1408]{2,1,0:T(8,128)(2,1)}, bf16[1,32,1408]{2,1,0:T(8,128)(2,1)}, bf16[1,32,1408]{2,1,0:T(8,128)(2,1)}, bf16[1,32,1408]{2,1,0:T(8,128)(2,1)}) custom-call(bf16[1,64,5120]{2,1,0:T(8,128)(2,1)} %states_ref.1), custom_call_target="tpu_custom_call" | custom-call | flops 1638400 | bytes 655360 | tf_op jit(solution)/shard_map/spread/pallas_call | solution.py:122
  2.2 3.1 %collective-permute-start.3 = (bf16[1,32,1408]{2,1,0:T(8,128)(2,1)}, bf16[1,32,1408]{2,1,0:T(8,128)(2,1)S(1)}, u32[]{:S(2)}, u32[]{:S(2)}) collective-permute-start(bf16[1,32,1408]{2,1,0:T(8,128)(2,1)} %get-tuple-element.37), channel_id=1, source_target_pairs={{0,4},{4,8},{8,12},{12,0},{1,5},{5,9},{9,13},{13,1},{2,6},{6,10},{... | collective-permute-start | bytes 270344 | tf_op jit(solution)/shard_map/ppermute | solution.py:28
  5.3 2.6 %collective-permute-start.4 = (bf16[1,32,1408]{2,1,0:T(8,128)(2,1)}, bf16[1,32,1408]{2,1,0:T(8,128)(2,1)S(1)}, u32[]{:S(2)}, u32[]{:S(2)}) collective-permute-start(bf16[1,32,1408]{2,1,0:T(8,128)(2,1)} %get-tuple-element.38), channel_id=1, source_target_pairs={{0,8},{4,12},{8,0},{12,4},{1,9},{5,13},{9,1},{13,5},{2,10},{6,14},... | collective-permute-start | bytes 270344 | tf_op jit(solution)/shard_map/ppermute | solution.py:28
  7.8 1.4 collective-permute-start.5
  9.2 1.6 collective-permute-done.3
  10.8 3.3 %collective-permute-done.4 = bf16[1,32,1408]{2,1,0:T(8,128)(2,1)S(1)} collective-permute-done((bf16[1,32,1408]{2,1,0:T(8,128)(2,1)}, bf16[1,32,1408]{2,1,0:T(8,128)(2,1)S(1)}, u32[]{:S(2)}, u32[]{:S(2)}) %collective-permute-start.4) | collective-permute-done | bytes 90144 | tf_op jit(solution)/shard_map/ppermute | solution.py:28
  14.3 0.9 pad_maximum_fusion.refs_4_
  15.3 1.6 collective-permute-start.7
  16.8 8.6 %collective-permute-done.7.refs_6_ = bf16[4,1,32,1408]{3,2,1,0:T(8,128)(2,1)S(1)} collective-permute-done((bf16[4,1,32,1408]{3,2,1,0:T(8,128)(2,1)S(1)}, bf16[4,1,32,1408]{3,2,1,0:T(8,128)(2,1)S(1)}, u32[]{:S(2)}, u32[]{:S(2)}) %collective-permute-start.7) | collective-permute-done | bytes 360480 | tf_op jit(solution)/shard_map/ppermute | solution.py:28
  26.0 3.1 %time_shares.1 = (f32[3,4,1280]{2,1,0:T(4,128)}, f32[3,4,1280]{2,1,0:T(4,128)}, f32[3,4,1280]{2,1,0:T(4,128)}, f32[3,4,1280]{2,1,0:T(4,128)}) custom-call(s32[1]{0:T(128)S(6)} %copy.8.step_ref, bf16[64,15360]{1,0:T(8,128)(2,1)} %proj_ref.1), custom_call_target="tpu_custom_call" | custom-call | flops 7864320 | bytes 1966080 | tf_op jit(solution)/shard_map/time_shares/pallas_call | solution.py:162
  29.1 2.5 %collective-permute-start = (f32[3,4,1280]{2,1,0:T(4,128)}, f32[3,4,1280]{2,1,0:T(4,128)S(1)}, u32[]{:S(2)}, u32[]{:S(2)}) collective-permute-start(f32[3,4,1280]{2,1,0:T(4,128)} %get-tuple-element.33), channel_id=1, source_target_pairs={{0,4},{4,8},{8,12},{12,0},{1,5},{5,9},{9,13},{13,1},{2,6},{6,10},{... | collective-permute-start | bytes 184328 | tf_op jit(solution)/shard_map/ppermute | solution.py:28
  32.0 2.0 %collective-permute-start.2 = (f32[3,4,1280]{2,1,0:T(4,128)}, f32[3,4,1280]{2,1,0:T(4,128)S(1)}, u32[]{:S(2)}, u32[]{:S(2)}) collective-permute-start(f32[3,4,1280]{2,1,0:T(4,128)} %get-tuple-element.35), channel_id=1, source_target_pairs={{0,12},{4,0},{8,4},{12,8},{1,13},{5,1},{9,5},{13,9},{2,14},{6,2},{... | collective-permute-start | bytes 184328 | tf_op jit(solution)/shard_map/ppermute | solution.py:28
  34.0 1.9 %collective-permute-done.refs_1_ = f32[3,4,1280]{2,1,0:T(4,128)S(1)} collective-permute-done((f32[3,4,1280]{2,1,0:T(4,128)}, f32[3,4,1280]{2,1,0:T(4,128)S(1)}, u32[]{:S(2)}, u32[]{:S(2)}) %collective-permute-start) | collective-permute-done | bytes 61472 | tf_op jit(solution)/shard_map/ppermute | solution.py:28
  35.9 2.4 %collective-permute-done.1.refs_2_ = f32[3,4,1280]{2,1,0:T(4,128)S(1)} collective-permute-done((f32[3,4,1280]{2,1,0:T(4,128)}, f32[3,4,1280]{2,1,0:T(4,128)S(1)}, u32[]{:S(2)}, u32[]{:S(2)}) %collective-permute-start.1) | collective-permute-done | bytes 61472 | tf_op jit(solution)/shard_map/ppermute | solution.py:28
  39.1 3.7 %modulate.1 = (bf16[4,2,1,64,1280]{4,3,2,1,0:T(8,128)(2,1)}, f32[4,1,1280]{2,1,0:T(1,128)}) custom-call(s32[1]{0:T(128)S(6)} %copy.8.step_ref, f32[3,4,1280]{2,1,0:T(4,128)} %get-tuple-element.32.refs_0_, f32[3,4,1280]{2,1,0:T(4,128)} %copy-done.29, f32[3,4,1280]{2,1,0:T(4,128)} %copy-done.30, f32[3,4,1280]{2,1,0:T(4,128)} %copy-done.31, ...), custom_call_target="tpu_custom_call" | custom-call | flops 2621440 | bytes 2621440 | tf_op jit(solution)/shard_map/modulate/pallas_call | solution.py:209
  42.8 4.2 %fusion.9 = f32[4,3,128,384]{3,2,1,0:T(8,128)S(1)} fusion(bf16[4,128,1280,1]{2,1,3,0:T(8,128)(2,1)} %bitcast.95, bf16[3,1280,768]{2,1,0:T(8,128)(2,1)} %param.8), kind=kOutput, calls=%fused_computation.7 | convolution fusion | flops 1509949440 | bytes 6619136 | tf_op jit(solution)/shard_map/krd,cdh->kcrh/dot_general | solution.py:391
  47.0 3.7 %fusion.6 = f32[4,3,128,384]{3,2,1,0:T(8,128)S(1)} fusion(bf16[4,128,1280,1]{2,1,3,0:T(8,128)(2,1)S(1)} %bitcast.96, bf16[3,1280,768]{2,1,0:T(8,128)(2,1)} %param.8), kind=kOutput, calls=%fused_computation.6 | convolution fusion | flops 1509949440 | bytes 6619136 | tf_op jit(solution)/shard_map/krd,cdh->kcrh/dot_general | solution.py:391
  50.9 3.9 %collective-permute-start.23 = (f16[3,128,384]{2,1,0:T(8,128)(2,1)S(1)}, f16[3,128,384]{2,1,0:T(8,128)(2,1)S(1)}, u32[]{:S(2)}, u32[]{:S(2)}) collective-permute-start(f16[3,128,384]{2,1,0:T(8,128)(2,1)S(1)} %get-tuple-element.64), channel_id=1, source_target_pairs={{0,4},{1,5},{2,6},{3,7},{16,20},{17,21},{18,22},{19,23}} | collective-permute-start | bytes 884744 | tf_op jit(solution)/shard_map/ppermute | solution.py:407
  56.2 1.3 collective-permute-start.9
  57.8 4.3 %collective-permute-done.23 = f16[3,128,384]{2,1,0:T(8,128)(2,1)S(1)} collective-permute-done((f16[3,128,384]{2,1,0:T(8,128)(2,1)S(1)}, f16[3,128,384]{2,1,0:T(8,128)(2,1)S(1)}, u32[]{:S(2)}, u32[]{:S(2)}) %collective-permute-start.23) | collective-permute-done | bytes 294944 | tf_op jit(solution)/shard_map/ppermute | solution.py:407
  62.3 4.4 %collective-permute-start.25 = (f16[3,128,384]{2,1,0:T(8,128)(2,1)S(1)}, f16[3,128,384]{2,1,0:T(8,128)(2,1)S(1)}, u32[]{:S(2)}, u32[]{:S(2)}) collective-permute-start(f16[3,128,384]{2,1,0:T(8,128)(2,1)S(1)} %get-tuple-element.62), channel_id=1, source_target_pairs={{0,4},{4,8},{1,5},{5,9},{2,6},{6,10},{3,7},{7,11},{16,20},{20,24},... | collective-permute-start | bytes 884744 | tf_op jit(solution)/shard_map/ppermute | solution.py:407
  67.4 1.0 collective-permute-done.9
  68.6 4.4 %collective-permute-start.11 = (f16[3,128,384]{2,1,0:T(8,128)(2,1)S(1)}, f16[3,128,384]{2,1,0:T(8,128)(2,1)S(1)}, u32[]{:S(2)}, u32[]{:S(2)}) collective-permute-start(f16[3,128,384]{2,1,0:T(8,128)(2,1)S(1)} %get-tuple-element.68), channel_id=1, source_target_pairs={{0,4},{4,8},{1,5},{5,9},{2,6},{6,10},{3,7},{7,11},{16,20},{20,24},... | collective-permute-start | bytes 884744 | tf_op jit(solution)/shard_map/ppermute | solution.py:407
  73.7 1.0 collective-permute-done.25
  74.7 1.5 collective-permute-start.38
  76.4 4.4 %collective-permute-start.27 = (f16[3,128,384]{2,1,0:T(8,128)(2,1)S(1)}, f16[3,128,384]{2,1,0:T(8,128)(2,1)S(1)}, u32[]{:S(2)}, u32[]{:S(2)}) collective-permute-start(f16[3,128,384]{2,1,0:T(8,128)(2,1)S(1)} %get-tuple-element.59), channel_id=1, source_target_pairs={{0,4},{4,8},{8,12},{1,5},{5,9},{9,13},{2,6},{6,10},{10,14},{3,7},{... | collective-permute-start | bytes 884744 | tf_op jit(solution)/shard_map/ppermute | solution.py:407
  81.1 1.3 collective-permute-start.28
  82.4 1.1 add_convert_fusion.5
  83.4 5.7 %collective-permute-start.13 = (f16[3,128,384]{2,1,0:T(8,128)(2,1)}, f16[3,128,384]{2,1,0:T(8,128)(2,1)}, u32[]{:S(2)}, u32[]{:S(2)}) collective-permute-start(f16[3,128,384]{2,1,0:T(8,128)(2,1)} %get-tuple-element.65), channel_id=1, source_target_pairs={{0,4},{4,8},{8,12},{1,5},{5,9},{9,13},{2,6},{6,10},{10,14},{3,7},{... | collective-permute-start | bytes 884744 | tf_op jit(solution)/shard_map/ppermute | solution.py:407
  89.2 1.3 collective-permute-start.14
  91.1 1.5 collective-permute-start.39
  93.4 2.6 %attend.3 = (bf16[1,64,384]{2,1,0:T(8,128)(2,1)}, bf16[1,64,384]{2,1,0:T(8,128)(2,1)}) custom-call(f32[2,384]{1,0:T(2,128)} %get-tuple-element.73.gain_ref, f32[3,2,1,64,384]{4,3,2,1,0:T(8,128)} %bitcast.85), custom_call_target="tpu_custom_call" | custom-call | flops 25165824 | bytes 688128 | tf_op jit(solution)/shard_map/attend/pallas_call | solution.py:74
  96.7 1.7 %collective-permute-done.14 = f16[3,128,384]{2,1,0:T(8,128)(2,1)} collective-permute-done((f16[3,128,384]{2,1,0:T(8,128)(2,1)}, f16[3,128,384]{2,1,0:T(8,128)(2,1)}, u32[]{:S(2)}, u32[]{:S(2)}) %collective-permute-start.14) | collective-permute-done | bytes 294944 | tf_op jit(solution)/shard_map/ppermute | solution.py:408
  98.3 1.9 %fusion.15 = f32[3,128,384]{2,1,0:T(8,128)} fusion(f32[4,3,128,384]{3,2,1,0:T(8,128)S(1)} %fusion.6, f16[3,128,384]{2,1,0:T(8,128)(2,1)} %collective-permute-done.14, f16[3,128,384]{2,1,0:T(8,128)(2,1)} %collective-permute-done.13), kind=kLoop, calls=%fused_computation.21 | loop fusion | flops 589824 | bytes 1769472 | tf_op jit(solution)/shard_map/add | solution.py:413
  100.3 2.7 %attend.2 = (bf16[1,64,384]{2,1,0:T(8,128)(2,1)}, bf16[1,64,384]{2,1,0:T(8,128)(2,1)}) custom-call(f32[2,384]{1,0:T(2,128)} %get-tuple-element.74.gain_ref, f32[3,2,1,64,384]{4,3,2,1,0:T(8,128)} %bitcast.84), custom_call_target="tpu_custom_call" | custom-call | flops 25165824 | bytes 688128 | tf_op jit(solution)/shard_map/attend/pallas_call | solution.py:74
  103.0 1.5 collective-permute-start.15
  104.4 14.9 %collective-permute-done.29 = bf16[1,64,384]{2,1,0:T(8,128)(2,1)S(1)} collective-permute-done((bf16[1,64,384]{2,1,0:T(8,128)(2,1)}, bf16[1,64,384]{2,1,0:T(8,128)(2,1)S(1)}, u32[]{:S(2)}, u32[]{:S(2)}) %collective-permute-start.29) | collective-permute-done | bytes 49184 | tf_op jit(solution)/shard_map/ppermute | solution.py:28
  119.3 2.5 %collective-permute-start.31 = (bf16[2,1,64,384]{3,2,1,0:T(8,128)(2,1)S(1)}, bf16[2,1,64,384]{3,2,1,0:T(8,128)(2,1)S(1)}, u32[]{:S(2)}, u32[]{:S(2)}) collective-permute-start(bf16[2,1,64,384]{3,2,1,0:T(8,128)(2,1)S(1)} %pad_maximum_fusion.2.refs_8_), channel_id=1, source_target_pairs={{0,4},{4,8},{8,12},{12,0},{1,5},{5,9},{9,13},{13,1},{2,6},{6,10},{... | collective-permute-start | bytes 294920 | tf_op jit(solution)/shard_map/ppermute | solution.py:28
  121.9 2.4 %collective-permute-start.35 = (bf16[2,1,64,384]{3,2,1,0:T(8,128)(2,1)S(1)}, bf16[2,1,64,384]{3,2,1,0:T(8,128)(2,1)S(1)}, u32[]{:S(2)}, u32[]{:S(2)}) collective-permute-start(bf16[2,1,64,384]{3,2,1,0:T(8,128)(2,1)S(1)} %pad_maximum_fusion.2.refs_8_), channel_id=1, source_target_pairs={{0,12},{4,0},{8,4},{12,8},{1,13},{5,1},{9,5},{13,9},{2,14},{6,2},{... | collective-permute-start | bytes 294920 | tf_op jit(solution)/shard_map/ppermute | solution.py:28
  126.5 1.7 %collective-permute-done.33.refs_12_ = bf16[2,1,64,384]{3,2,1,0:T(8,128)(2,1)S(1)} collective-permute-done((bf16[2,1,64,384]{3,2,1,0:T(8,128)(2,1)S(1)}, bf16[2,1,64,384]{3,2,1,0:T(8,128)(2,1)S(1)}, u32[]{:S(2)}, u32[]{:S(2)}) %collective-permute-start.33) | collective-permute-done | bytes 98336 | tf_op jit(solution)/shard_map/ppermute | solution.py:28
  128.6 2.5 %collective-permute-start.21 = (bf16[2,1,64,384]{3,2,1,0:T(8,128)(2,1)S(1)}, bf16[2,1,64,384]{3,2,1,0:T(8,128)(2,1)S(1)}, u32[]{:S(2)}, u32[]{:S(2)}) collective-permute-start(bf16[2,1,64,384]{3,2,1,0:T(8,128)(2,1)S(1)} %pad_maximum_fusion.1.refs_0_), channel_id=1, source_target_pairs={{0,12},{4,0},{8,4},{12,8},{1,13},{5,1},{9,5},{13,9},{2,14},{6,2},{... | collective-permute-start | bytes 294920 | tf_op jit(solution)/shard_map/ppermute | solution.py:28
  131.1 2.3 %collective-permute-done.17.refs_2_ = bf16[2,1,64,384]{3,2,1,0:T(8,128)(2,1)S(1)} collective-permute-done((bf16[2,1,64,384]{3,2,1,0:T(8,128)(2,1)S(1)}, bf16[2,1,64,384]{3,2,1,0:T(8,128)(2,1)S(1)}, u32[]{:S(2)}, u32[]{:S(2)}) %collective-permute-start.17) | collective-permute-done | bytes 98336 | tf_op jit(solution)/shard_map/ppermute | solution.py:28
  133.4 3.1 %collective-permute-done.19.refs_4_ = bf16[2,1,64,384]{3,2,1,0:T(8,128)(2,1)S(1)} collective-permute-done((bf16[2,1,64,384]{3,2,1,0:T(8,128)(2,1)S(1)}, bf16[2,1,64,384]{3,2,1,0:T(8,128)(2,1)S(1)}, u32[]{:S(2)}, u32[]{:S(2)}) %collective-permute-start.19) | collective-permute-done | bytes 98336 | tf_op jit(solution)/shard_map/ppermute | solution.py:28
  139.8 5.9 %project.1 = (f32[1,64,640]{2,1,0:T(8,128)}, bf16[1,64,640]{2,1,0:T(8,128)(2,1)}, bf16[1,64,640]{2,1,0:T(8,128)(2,1)}, bf16[1,64,640]{2,1,0:T(8,128)(2,1)}, bf16[1,64,640]{2,1,0:T(8,128)(2,1)}) custom-call(f32[4,1,1280]{2,1,0:T(1,128)} %get-tuple-element.40.coef_ref, bf16[2,1,64,384]{3,2,1,0:T(8,128)(2,1)} %copy-done.4, bf16[2,1,64,384]{3,2,1,0:T(8,128)(2,1)} %copy-done.15, ...), custom_call_target="tpu_custom_call" | custom-call | flops 1006632960 | bytes 5505024 | tf_op jit(solution)/shard_map/project/pallas_call | solution.py:300
  145.7 2.8 %collective-permute-start.41 = (bf16[1,64,640]{2,1,0:T(8,128)(2,1)}, bf16[1,64,640]{2,1,0:T(8,128)(2,1)S(1)}, u32[]{:S(2)}, u32[]{:S(2)}) collective-permute-start(bf16[1,64,640]{2,1,0:T(8,128)(2,1)} %get-tuple-element.56), channel_id=1, source_target_pairs={{0,12},{4,0},{8,4},{12,8},{1,13},{5,1},{9,5},{13,9},{2,14},{6,2},{... | collective-permute-start | bytes 245768 | tf_op jit(solution)/shard_map/ppermute | solution.py:28
  149.1 2.5 %collective-permute-done.41.refs_2_ = bf16[1,64,640]{2,1,0:T(8,128)(2,1)S(1)} collective-permute-done((bf16[1,64,640]{2,1,0:T(8,128)(2,1)}, bf16[1,64,640]{2,1,0:T(8,128)(2,1)S(1)}, u32[]{:S(2)}, u32[]{:S(2)}) %collective-permute-start.41) | collective-permute-done | bytes 81952 | tf_op jit(solution)/shard_map/ppermute | solution.py:28
  151.6 5.0 %collective-permute-done.43.refs_4_ = bf16[1,64,640]{2,1,0:T(8,128)(2,1)S(1)} collective-permute-done((bf16[1,64,640]{2,1,0:T(8,128)(2,1)}, bf16[1,64,640]{2,1,0:T(8,128)(2,1)S(1)}, u32[]{:S(2)}, u32[]{:S(2)}) %collective-permute-start.43) | collective-permute-done | bytes 81952 | tf_op jit(solution)/shard_map/ppermute | solution.py:28
  158.7 2.2 %finish.1 = f32[1,64,2560]{2,1,0:T(8,128)} custom-call(f32[1,64,640]{2,1,0:T(8,128)} %get-tuple-element.54.refs_0_, bf16[1,64,640]{2,1,0:T(8,128)(2,1)} %copy-done.25, bf16[1,64,640]{2,1,0:T(8,128)(2,1)} %copy-done.22, bf16[1,64,640]{2,1,0:T(8,128)(2,1)} %copy-done.26, bf16[1,64,640]{2,1,0:T(8,128)(2,1)} %copy-done.23, bf16[1,64,640]{2,1,0:T(8,128)(2,1)} %copy-done.27, ...), custom_call_target="tpu_custom_call" | custom-call | bytes 1310720 | tf_op jit(solution)/shard_map/finish/pallas_call | solution.py:342
  (138 shorter events, 15.7 us)
Async XLA Ops:
  2.2 8.6 %collective-permute-start.3 = (bf16[1,32,1408]{2,1,0:T(8,128)(2,1)}, bf16[1,32,1408]{2,1,0:T(8,128)(2,1)S(1)}, u32[]{:S(2)}, u32[]{:S(2)}) collective-permute-start(bf16[1,32,1408]{2,1,0:T(8,128)(2,1)} %get-tuple-element.37), channel_id=1, source_target_pairs={{0,4},{4,8},{8,12},{12,0},{1,5},{5,9},{9,13},{13,1},{2,6},{6,10},{... | collective-permute-start | bytes 270344 | tf_op jit(solution)/shard_map/ppermute | solution.py:28
  5.3 8.8 %collective-permute-start.4 = (bf16[1,32,1408]{2,1,0:T(8,128)(2,1)}, bf16[1,32,1408]{2,1,0:T(8,128)(2,1)S(1)}, u32[]{:S(2)}, u32[]{:S(2)}) collective-permute-start(bf16[1,32,1408]{2,1,0:T(8,128)(2,1)} %get-tuple-element.38), channel_id=1, source_target_pairs={{0,8},{4,12},{8,0},{12,4},{1,9},{5,13},{9,1},{13,5},{2,10},{6,14},... | collective-permute-start | bytes 270344 | tf_op jit(solution)/shard_map/ppermute | solution.py:28
  7.8 6.5 %collective-permute-start.5 = (bf16[1,32,1408]{2,1,0:T(8,128)(2,1)}, bf16[1,32,1408]{2,1,0:T(8,128)(2,1)S(1)}, u32[]{:S(2)}, u32[]{:S(2)}) collective-permute-start(bf16[1,32,1408]{2,1,0:T(8,128)(2,1)} %get-tuple-element.39), channel_id=1, source_target_pairs={{0,12},{4,0},{8,4},{12,8},{1,13},{5,1},{9,5},{13,9},{2,14},{6,2},{... | collective-permute-start | bytes 270344 | tf_op jit(solution)/shard_map/ppermute | solution.py:28
  15.3 10.1 %collective-permute-start.7 = (bf16[4,1,32,1408]{3,2,1,0:T(8,128)(2,1)S(1)}, bf16[4,1,32,1408]{3,2,1,0:T(8,128)(2,1)S(1)}, u32[]{:S(2)}, u32[]{:S(2)}) collective-permute-start(bf16[4,1,32,1408]{3,2,1,0:T(8,128)(2,1)S(1)} %pad_maximum_fusion.refs_4_), channel_id=1, source_target_pairs={{0,2},{2,0},{1,3},{3,1},{4,6},{6,4},{5,7},{7,5},{8,10},{10,8},{9,1... | collective-permute-start | bytes 1081352 | tf_op jit(solution)/shard_map/ppermute | solution.py:28
  16.8 21.4 %collective-permute-start.6 = (bf16[4,1,32,1408]{3,2,1,0:T(8,128)(2,1)S(1)}, bf16[4,1,32,1408]{3,2,1,0:T(8,128)(2,1)S(1)}, u32[]{:S(2)}, u32[]{:S(2)}) collective-permute-start(bf16[4,1,32,1408]{3,2,1,0:T(8,128)(2,1)S(1)} %pad_maximum_fusion.refs_4_), channel_id=1, source_target_pairs={{0,1},{1,0},{2,3},{3,2},{4,5},{5,4},{6,7},{7,6},{8,9},{9,8},{10,11... | collective-permute-start | bytes 1081352 | tf_op jit(solution)/shard_map/ppermute | solution.py:28
  25.4 12.9 %collective-permute-start.8 = (bf16[4,1,32,1408]{3,2,1,0:T(8,128)(2,1)S(1)}, bf16[4,1,32,1408]{3,2,1,0:T(8,128)(2,1)S(1)}, u32[]{:S(2)}, u32[]{:S(2)}) collective-permute-start(bf16[4,1,32,1408]{3,2,1,0:T(8,128)(2,1)S(1)} %collective-permute-done.7.refs_6_), channel_id=1, source_target_pairs={{0,1},{1,0},{2,3},{3,2},{4,5},{5,4},{6,7},{7,6},{8,9},{9,8},{10,11... | collective-permute-start | bytes 1081352 | tf_op jit(solution)/shard_map/ppermute | solution.py:28
  29.1 6.7 %collective-permute-start = (f32[3,4,1280]{2,1,0:T(4,128)}, f32[3,4,1280]{2,1,0:T(4,128)S(1)}, u32[]{:S(2)}, u32[]{:S(2)}) collective-permute-start(f32[3,4,1280]{2,1,0:T(4,128)} %get-tuple-element.33), channel_id=1, source_target_pairs={{0,4},{4,8},{8,12},{12,0},{1,5},{5,9},{9,13},{13,1},{2,6},{6,10},{... | collective-permute-start | bytes 184328 | tf_op jit(solution)/shard_map/ppermute | solution.py:28
  31.6 6.6 %collective-permute-start.1 = (f32[3,4,1280]{2,1,0:T(4,128)}, f32[3,4,1280]{2,1,0:T(4,128)S(1)}, u32[]{:S(2)}, u32[]{:S(2)}) collective-permute-start(f32[3,4,1280]{2,1,0:T(4,128)} %get-tuple-element.34), channel_id=1, source_target_pairs={{0,8},{4,12},{8,0},{12,4},{1,9},{5,13},{9,1},{13,5},{2,10},{6,14},... | collective-permute-start | bytes 184328 | tf_op jit(solution)/shard_map/ppermute | solution.py:28
  32.0 6.3 %collective-permute-start.2 = (f32[3,4,1280]{2,1,0:T(4,128)}, f32[3,4,1280]{2,1,0:T(4,128)S(1)}, u32[]{:S(2)}, u32[]{:S(2)}) collective-permute-start(f32[3,4,1280]{2,1,0:T(4,128)} %get-tuple-element.35), channel_id=1, source_target_pairs={{0,12},{4,0},{8,4},{12,8},{1,13},{5,1},{9,5},{13,9},{2,14},{6,2},{... | collective-permute-start | bytes 184328 | tf_op jit(solution)/shard_map/ppermute | solution.py:28
  50.9 11.2 %collective-permute-start.23 = (f16[3,128,384]{2,1,0:T(8,128)(2,1)S(1)}, f16[3,128,384]{2,1,0:T(8,128)(2,1)S(1)}, u32[]{:S(2)}, u32[]{:S(2)}) collective-permute-start(f16[3,128,384]{2,1,0:T(8,128)(2,1)S(1)} %get-tuple-element.64), channel_id=1, source_target_pairs={{0,4},{1,5},{2,6},{3,7},{16,20},{17,21},{18,22},{19,23}} | collective-permute-start | bytes 884744 | tf_op jit(solution)/shard_map/ppermute | solution.py:407
  54.7 7.4 %collective-permute-start.24 = (f16[3,128,384]{2,1,0:T(8,128)(2,1)S(1)}, f16[3,128,384]{2,1,0:T(8,128)(2,1)S(1)}, u32[]{:S(2)}, u32[]{:S(2)}) collective-permute-start(f16[3,128,384]{2,1,0:T(8,128)(2,1)S(1)} %get-tuple-element.63), channel_id=1, source_target_pairs={{12,8},{13,9},{14,10},{15,11},{28,24},{29,25},{30,26},{31,27}} | collective-permute-start | bytes 884744 | tf_op jit(solution)/shard_map/ppermute | solution.py:408
  55.5 11.9 %collective-permute-start.10 = (f16[3,128,384]{2,1,0:T(8,128)(2,1)S(1)}, f16[3,128,384]{2,1,0:T(8,128)(2,1)S(1)}, u32[]{:S(2)}, u32[]{:S(2)}) collective-permute-start(f16[3,128,384]{2,1,0:T(8,128)(2,1)S(1)} %get-tuple-element.69), channel_id=1, source_target_pairs={{12,8},{13,9},{14,10},{15,11},{28,24},{29,25},{30,26},{31,27}} | collective-permute-start | bytes 884744 | tf_op jit(solution)/shard_map/ppermute | solution.py:408
  56.2 12.2 %collective-permute-start.9 = (f16[3,128,384]{2,1,0:T(8,128)(2,1)S(1)}, f16[3,128,384]{2,1,0:T(8,128)(2,1)S(1)}, u32[]{:S(2)}, u32[]{:S(2)}) collective-permute-start(f16[3,128,384]{2,1,0:T(8,128)(2,1)S(1)} %get-tuple-element.70), channel_id=1, source_target_pairs={{0,4},{1,5},{2,6},{3,7},{16,20},{17,21},{18,22},{19,23}} | collective-permute-start | bytes 884744 | tf_op jit(solution)/shard_map/ppermute | solution.py:407
  57.7 31.5 %collective-permute-start.37 = (bf16[640,768]{1,0:T(8,128)(2,1)S(1)}, bf16[640,768]{1,0:T(8,128)(2,1)}, u32[]{:S(2)}, u32[]{:S(2)}) collective-permute-start(bf16[640,768]{1,0:T(8,128)(2,1)S(1)} %get-tuple-element.71), channel_id=1, source_target_pairs={{0,1},{1,0},{2,3},{3,2},{4,5},{5,4},{6,7},{7,6},{8,9},{9,8},{10,11... | collective-permute-start | bytes 2949128 | tf_op jit(solution)/shard_map/ppermute | solution.py:28
  62.3 12.5 %collective-permute-start.25 = (f16[3,128,384]{2,1,0:T(8,128)(2,1)S(1)}, f16[3,128,384]{2,1,0:T(8,128)(2,1)S(1)}, u32[]{:S(2)}, u32[]{:S(2)}) collective-permute-start(f16[3,128,384]{2,1,0:T(8,128)(2,1)S(1)} %get-tuple-element.62), channel_id=1, source_target_pairs={{0,4},{4,8},{1,5},{5,9},{2,6},{6,10},{3,7},{7,11},{16,20},{20,24},... | collective-permute-start | bytes 884744 | tf_op jit(solution)/shard_map/ppermute | solution.py:407
  66.7 9.5 %collective-permute-start.26 = (f16[3,128,384]{2,1,0:T(8,128)(2,1)S(1)}, f16[3,128,384]{2,1,0:T(8,128)(2,1)S(1)}, u32[]{:S(2)}, u32[]{:S(2)}) collective-permute-start(f16[3,128,384]{2,1,0:T(8,128)(2,1)S(1)} %get-tuple-element.61), channel_id=1, source_target_pairs={{12,8},{8,4},{13,9},{9,5},{14,10},{10,6},{15,11},{11,7},{28,24},{2... | collective-permute-start | bytes 884744 | tf_op jit(solution)/shard_map/ppermute | solution.py:408
  68.6 12.5 %collective-permute-start.11 = (f16[3,128,384]{2,1,0:T(8,128)(2,1)S(1)}, f16[3,128,384]{2,1,0:T(8,128)(2,1)S(1)}, u32[]{:S(2)}, u32[]{:S(2)}) collective-permute-start(f16[3,128,384]{2,1,0:T(8,128)(2,1)S(1)} %get-tuple-element.68), channel_id=1, source_target_pairs={{0,4},{4,8},{1,5},{5,9},{2,6},{6,10},{3,7},{7,11},{16,20},{20,24},... | collective-permute-start | bytes 884744 | tf_op jit(solution)/shard_map/ppermute | solution.py:407
  73.0 9.3 %collective-permute-start.12 = (f16[3,128,384]{2,1,0:T(8,128)(2,1)S(1)}, f16[3,128,384]{2,1,0:T(8,128)(2,1)S(1)}, u32[]{:S(2)}, u32[]{:S(2)}) collective-permute-start(f16[3,128,384]{2,1,0:T(8,128)(2,1)S(1)} %get-tuple-element.67), channel_id=1, source_target_pairs={{12,8},{8,4},{13,9},{9,5},{14,10},{10,6},{15,11},{11,7},{28,24},{2... | collective-permute-start | bytes 884744 | tf_op jit(solution)/shard_map/ppermute | solution.py:408
  74.7 50.4 %collective-permute-start.38 = (bf16[640,768]{1,0:T(8,128)(2,1)S(1)}, bf16[640,768]{1,0:T(8,128)(2,1)}, u32[]{:S(2)}, u32[]{:S(2)}) collective-permute-start(bf16[640,768]{1,0:T(8,128)(2,1)S(1)} %get-tuple-element.72.refs_16_), channel_id=1, source_target_pairs={{0,2},{2,0},{1,3},{3,1},{4,6},{6,4},{5,7},{7,5},{8,10},{10,8},{9,1... | collective-permute-start | bytes 2949128 | tf_op jit(solution)/shard_map/ppermute | solution.py:28
  76.4 14.6 %collective-permute-start.27 = (f16[3,128,384]{2,1,0:T(8,128)(2,1)S(1)}, f16[3,128,384]{2,1,0:T(8,128)(2,1)S(1)}, u32[]{:S(2)}, u32[]{:S(2)}) collective-permute-start(f16[3,128,384]{2,1,0:T(8,128)(2,1)S(1)} %get-tuple-element.59), channel_id=1, source_target_pairs={{0,4},{4,8},{8,12},{1,5},{5,9},{9,13},{2,6},{6,10},{10,14},{3,7},{... | collective-permute-start | bytes 884744 | tf_op jit(solution)/shard_map/ppermute | solution.py:407
  81.1 11.5 %collective-permute-start.28 = (f16[3,128,384]{2,1,0:T(8,128)(2,1)S(1)}, f16[3,128,384]{2,1,0:T(8,128)(2,1)S(1)}, u32[]{:S(2)}, u32[]{:S(2)}) collective-permute-start(f16[3,128,384]{2,1,0:T(8,128)(2,1)S(1)} %get-tuple-element.60), channel_id=1, source_target_pairs={{12,8},{8,4},{4,0},{13,9},{9,5},{5,1},{14,10},{10,6},{6,2},{15,11}... | collective-permute-start | bytes 884744 | tf_op jit(solution)/shard_map/ppermute | solution.py:408
  83.4 13.2 %collective-permute-start.13 = (f16[3,128,384]{2,1,0:T(8,128)(2,1)}, f16[3,128,384]{2,1,0:T(8,128)(2,1)}, u32[]{:S(2)}, u32[]{:S(2)}) collective-permute-start(f16[3,128,384]{2,1,0:T(8,128)(2,1)} %get-tuple-element.65), channel_id=1, source_target_pairs={{0,4},{4,8},{8,12},{1,5},{5,9},{9,13},{2,6},{6,10},{10,14},{3,7},{... | collective-permute-start | bytes 884744 | tf_op jit(solution)/shard_map/ppermute | solution.py:407
  89.2 9.2 %collective-permute-start.14 = (f16[3,128,384]{2,1,0:T(8,128)(2,1)}, f16[3,128,384]{2,1,0:T(8,128)(2,1)}, u32[]{:S(2)}, u32[]{:S(2)}) collective-permute-start(f16[3,128,384]{2,1,0:T(8,128)(2,1)} %get-tuple-element.66), channel_id=1, source_target_pairs={{12,8},{8,4},{4,0},{13,9},{9,5},{5,1},{14,10},{10,6},{6,2},{15,11}... | collective-permute-start | bytes 884744 | tf_op jit(solution)/shard_map/ppermute | solution.py:408
  91.1 48.1 %collective-permute-start.39 = (bf16[640,768]{1,0:T(8,128)(2,1)}, bf16[640,768]{1,0:T(8,128)(2,1)}, u32[]{:S(2)}, u32[]{:S(2)}) collective-permute-start(bf16[640,768]{1,0:T(8,128)(2,1)} %collective-permute-done.37.refs_17_), channel_id=1, source_target_pairs={{0,2},{2,0},{1,3},{3,1},{4,6},{6,4},{5,7},{7,5},{8,10},{10,8},{9,1... | collective-permute-start | bytes 2949128 | tf_op jit(solution)/shard_map/ppermute | solution.py:28
  96.1 23.2 %copy-start.32 = (bf16[1,64,384]{2,1,0:T(8,128)(2,1)S(1)}, bf16[1,64,384]{2,1,0:T(8,128)(2,1)}, u32[]{:S(2)}) copy-start(bf16[1,64,384]{2,1,0:T(8,128)(2,1)} %get-tuple-element.52) | copy-start | bytes 147460
  96.1 23.2 %collective-permute-start.29 = (bf16[1,64,384]{2,1,0:T(8,128)(2,1)}, bf16[1,64,384]{2,1,0:T(8,128)(2,1)S(1)}, u32[]{:S(2)}, u32[]{:S(2)}) collective-permute-start(bf16[1,64,384]{2,1,0:T(8,128)(2,1)} %get-tuple-element.53), channel_id=1, source_target_pairs={{0,2},{2,0},{1,3},{3,1},{4,6},{6,4},{5,7},{7,5},{8,10},{10,8},{9,1... | collective-permute-start | bytes 147464 | tf_op jit(solution)/shard_map/ppermute | solution.py:28
  103.0 18.9 %collective-permute-start.15 = (bf16[1,64,384]{2,1,0:T(8,128)(2,1)}, bf16[1,64,384]{2,1,0:T(8,128)(2,1)S(1)}, u32[]{:S(2)}, u32[]{:S(2)}) collective-permute-start(bf16[1,64,384]{2,1,0:T(8,128)(2,1)} %get-tuple-element.47), channel_id=1, source_target_pairs={{0,2},{2,0},{1,3},{3,1},{4,6},{6,4},{5,7},{7,5},{8,10},{10,8},{9,1... | collective-permute-start | bytes 147464 | tf_op jit(solution)/shard_map/ppermute | solution.py:28
  119.3 6.6 %collective-permute-start.31 = (bf16[2,1,64,384]{3,2,1,0:T(8,128)(2,1)S(1)}, bf16[2,1,64,384]{3,2,1,0:T(8,128)(2,1)S(1)}, u32[]{:S(2)}, u32[]{:S(2)}) collective-permute-start(bf16[2,1,64,384]{3,2,1,0:T(8,128)(2,1)S(1)} %pad_maximum_fusion.2.refs_8_), channel_id=1, source_target_pairs={{0,4},{4,8},{8,12},{12,0},{1,5},{5,9},{9,13},{13,1},{2,6},{6,10},{... | collective-permute-start | bytes 294920 | tf_op jit(solution)/shard_map/ppermute | solution.py:28
  121.9 6.3 %collective-permute-start.33 = (bf16[2,1,64,384]{3,2,1,0:T(8,128)(2,1)S(1)}, bf16[2,1,64,384]{3,2,1,0:T(8,128)(2,1)S(1)}, u32[]{:S(2)}, u32[]{:S(2)}) collective-permute-start(bf16[2,1,64,384]{3,2,1,0:T(8,128)(2,1)S(1)} %pad_maximum_fusion.2.refs_8_), channel_id=1, source_target_pairs={{0,8},{4,12},{8,0},{12,4},{1,9},{5,13},{9,1},{13,5},{2,10},{6,14},... | collective-permute-start | bytes 294920 | tf_op jit(solution)/shard_map/ppermute | solution.py:28
  121.9 6.7 %collective-permute-start.35 = (bf16[2,1,64,384]{3,2,1,0:T(8,128)(2,1)S(1)}, bf16[2,1,64,384]{3,2,1,0:T(8,128)(2,1)S(1)}, u32[]{:S(2)}, u32[]{:S(2)}) collective-permute-start(bf16[2,1,64,384]{3,2,1,0:T(8,128)(2,1)S(1)} %pad_maximum_fusion.2.refs_8_), channel_id=1, source_target_pairs={{0,12},{4,0},{8,4},{12,8},{1,13},{5,1},{9,5},{13,9},{2,14},{6,2},{... | collective-permute-start | bytes 294920 | tf_op jit(solution)/shard_map/ppermute | solution.py:28
  125.2 5.9 %collective-permute-start.30 = (bf16[2,1,64,384]{3,2,1,0:T(8,128)(2,1)S(1)}, bf16[2,1,64,384]{3,2,1,0:T(8,128)(2,1)S(1)}, u32[]{:S(2)}, u32[]{:S(2)}) collective-permute-start(bf16[2,1,64,384]{3,2,1,0:T(8,128)(2,1)S(1)} %pad_maximum_fusion.2.refs_8_), channel_id=1, source_target_pairs={{0,1},{1,0},{2,3},{3,2},{4,5},{5,4},{6,7},{7,6},{8,9},{9,8},{10,11... | collective-permute-start | bytes 294920 | tf_op jit(solution)/shard_map/ppermute | solution.py:28
  126.0 7.5 %collective-permute-start.17 = (bf16[2,1,64,384]{3,2,1,0:T(8,128)(2,1)S(1)}, bf16[2,1,64,384]{3,2,1,0:T(8,128)(2,1)S(1)}, u32[]{:S(2)}, u32[]{:S(2)}) collective-permute-start(bf16[2,1,64,384]{3,2,1,0:T(8,128)(2,1)S(1)} %pad_maximum_fusion.1.refs_0_), channel_id=1, source_target_pairs={{0,4},{4,8},{8,12},{12,0},{1,5},{5,9},{9,13},{13,1},{2,6},{6,10},{... | collective-permute-start | bytes 294920 | tf_op jit(solution)/shard_map/ppermute | solution.py:28
  128.2 8.4 %collective-permute-start.19 = (bf16[2,1,64,384]{3,2,1,0:T(8,128)(2,1)S(1)}, bf16[2,1,64,384]{3,2,1,0:T(8,128)(2,1)S(1)}, u32[]{:S(2)}, u32[]{:S(2)}) collective-permute-start(bf16[2,1,64,384]{3,2,1,0:T(8,128)(2,1)S(1)} %pad_maximum_fusion.1.refs_0_), channel_id=1, source_target_pairs={{0,8},{4,12},{8,0},{12,4},{1,9},{5,13},{9,1},{13,5},{2,10},{6,14},... | collective-permute-start | bytes 294920 | tf_op jit(solution)/shard_map/ppermute | solution.py:28
  128.6 8.0 %collective-permute-start.21 = (bf16[2,1,64,384]{3,2,1,0:T(8,128)(2,1)S(1)}, bf16[2,1,64,384]{3,2,1,0:T(8,128)(2,1)S(1)}, u32[]{:S(2)}, u32[]{:S(2)}) collective-permute-start(bf16[2,1,64,384]{3,2,1,0:T(8,128)(2,1)S(1)} %pad_maximum_fusion.1.refs_0_), channel_id=1, source_target_pairs={{0,12},{4,0},{8,4},{12,8},{1,13},{5,1},{9,5},{13,9},{2,14},{6,2},{... | collective-permute-start | bytes 294920 | tf_op jit(solution)/shard_map/ppermute | solution.py:28
  131.1 6.0 %collective-permute-start.16 = (bf16[2,1,64,384]{3,2,1,0:T(8,128)(2,1)S(1)}, bf16[2,1,64,384]{3,2,1,0:T(8,128)(2,1)S(1)}, u32[]{:S(2)}, u32[]{:S(2)}) collective-permute-start(bf16[2,1,64,384]{3,2,1,0:T(8,128)(2,1)S(1)} %pad_maximum_fusion.1.refs_0_), channel_id=1, source_target_pairs={{0,1},{1,0},{2,3},{3,2},{4,5},{5,4},{6,7},{7,6},{8,9},{9,8},{10,11... | collective-permute-start | bytes 294920 | tf_op jit(solution)/shard_map/ppermute | solution.py:28
  133.4 3.7 %collective-permute-start.32 = (bf16[2,1,64,384]{3,2,1,0:T(8,128)(2,1)S(1)}, bf16[2,1,64,384]{3,2,1,0:T(8,128)(2,1)S(1)}, u32[]{:S(2)}, u32[]{:S(2)}) collective-permute-start(bf16[2,1,64,384]{3,2,1,0:T(8,128)(2,1)S(1)} %collective-permute-done.31.refs_10_), channel_id=1, source_target_pairs={{0,1},{1,0},{2,3},{3,2},{4,5},{5,4},{6,7},{7,6},{8,9},{9,8},{10,11... | collective-permute-start | bytes 294920 | tf_op jit(solution)/shard_map/ppermute | solution.py:28
  136.5 1.3 collective-permute-start.34
  136.6 1.4 collective-permute-start.36
  137.1 1.3 collective-permute-start.18
  137.2 1.4 collective-permute-start.20
  137.9 1.3 collective-permute-start.22
  145.7 6.0 %collective-permute-start.41 = (bf16[1,64,640]{2,1,0:T(8,128)(2,1)}, bf16[1,64,640]{2,1,0:T(8,128)(2,1)S(1)}, u32[]{:S(2)}, u32[]{:S(2)}) collective-permute-start(bf16[1,64,640]{2,1,0:T(8,128)(2,1)} %get-tuple-element.56), channel_id=1, source_target_pairs={{0,12},{4,0},{8,4},{12,8},{1,13},{5,1},{9,5},{13,9},{2,14},{6,2},{... | collective-permute-start | bytes 245768 | tf_op jit(solution)/shard_map/ppermute | solution.py:28
  148.4 8.2 %collective-permute-start.43 = (bf16[1,64,640]{2,1,0:T(8,128)(2,1)}, bf16[1,64,640]{2,1,0:T(8,128)(2,1)S(1)}, u32[]{:S(2)}, u32[]{:S(2)}) collective-permute-start(bf16[1,64,640]{2,1,0:T(8,128)(2,1)} %get-tuple-element.57), channel_id=1, source_target_pairs={{0,8},{4,12},{8,0},{12,4},{1,9},{5,13},{9,1},{13,5},{2,10},{6,14},... | collective-permute-start | bytes 245768 | tf_op jit(solution)/shard_map/ppermute | solution.py:28
  148.4 8.3 %collective-permute-start.45 = (bf16[1,64,640]{2,1,0:T(8,128)(2,1)}, bf16[1,64,640]{2,1,0:T(8,128)(2,1)S(1)}, u32[]{:S(2)}, u32[]{:S(2)}) collective-permute-start(bf16[1,64,640]{2,1,0:T(8,128)(2,1)} %get-tuple-element.58), channel_id=1, source_target_pairs={{0,4},{4,8},{8,12},{12,0},{1,5},{5,9},{9,13},{13,1},{2,6},{6,10},{... | collective-permute-start | bytes 245768 | tf_op jit(solution)/shard_map/ppermute | solution.py:28
  149.1 8.1 %collective-permute-start.40 = (bf16[1,64,640]{2,1,0:T(8,128)(2,1)}, bf16[1,64,640]{2,1,0:T(8,128)(2,1)S(1)}, u32[]{:S(2)}, u32[]{:S(2)}) collective-permute-start(bf16[1,64,640]{2,1,0:T(8,128)(2,1)} %get-tuple-element.55), channel_id=1, source_target_pairs={{0,1},{1,0},{2,3},{3,2},{4,5},{5,4},{6,7},{7,6},{8,9},{9,8},{10,11... | collective-permute-start | bytes 245768 | tf_op jit(solution)/shard_map/ppermute | solution.py:28
  151.6 5.6 %collective-permute-start.42 = (bf16[1,64,640]{2,1,0:T(8,128)(2,1)S(1)}, bf16[1,64,640]{2,1,0:T(8,128)(2,1)S(1)}, u32[]{:S(2)}, u32[]{:S(2)}) collective-permute-start(bf16[1,64,640]{2,1,0:T(8,128)(2,1)S(1)} %collective-permute-done.41.refs_2_), channel_id=1, source_target_pairs={{0,1},{1,0},{2,3},{3,2},{4,5},{5,4},{6,7},{7,6},{8,9},{9,8},{10,11... | collective-permute-start | bytes 245768 | tf_op jit(solution)/shard_map/ppermute | solution.py:28
  156.7 1.3 collective-permute-start.44
  156.7 1.4 collective-permute-start.46
  (34 other events, 196.5 us)

commit v5 on v4

--- a/solution.py
+++ b/solution.py
@@ -85,6 +85,7 @@
             bytes_accessed=14 * frames * tokens * cols,
             transcendentals=frames * heads * tokens * tokens,
         ),
+        compiler_params=pltpu.CompilerParams(vmem_limit_bytes=12 << 20),
         name="attend",
     )(gain, whole)
 
@@ -127,6 +128,7 @@
         cost_estimate=pl.CostEstimate(
             flops=10 * part * width, bytes_accessed=4 * part * width, transcendentals=0
         ),
+        compiler_params=pltpu.CompilerParams(vmem_limit_bytes=8 << 20),
         name="spread",
     )(states)
 
@@ -167,36 +169,39 @@
         cost_estimate=pl.CostEstimate(
             flops=2 * window * freq_rows * wide, bytes_accessed=2 * freq_rows * wide, transcendentals=0
         ),
+        compiler_params=pltpu.CompilerParams(vmem_limit_bytes=12 << 20),
         name="time_shares",
     )(start_step, time_proj)
 
 
 def modulate_kernel(n_tm, n_seq, n_mp, step_ref, *refs):
     shares, rows, (hidden_ref, coef_ref, mod_scr) = refs[:n_tm], refs[n_tm:-3], refs[-3:]
-    z = lax.axis_index("tm")
+    z, k = lax.axis_index("tm"), pl.program_id(0)
     _, frames, part, wide = rows[0].shape
     depth = wide - LANES
-    total = shares[0][...]
-    for share in shares[1:]:
-        total = total + share[...]
-    mod_scr[...] = total
-    for k in range(n_tm):
-        for f in range(frames):
-            step = pl.ds(lax.rem(z - k + n_tm, n_tm) * frames + f, 1)
-            shift, scale = mod_scr[0, step, :], mod_scr[1, step, :]
-            index = jnp.full((1, depth), step_ref[0] + step.start, jnp.int32)
-            size = sigma_of(index + 1) - sigma_of(index)
-            coef_ref[k, f : f + 1, :] = size * mod_scr[2, step, :]
-            for j in range(n_seq):
-                for i in range(n_mp):
-                    row = rows[j * n_mp + i]
-                    tail = row[k, f, :, depth:].astype(jnp.float32)
-                    mean = tail[:, 0:1] + tail[:, 1:2] + tail[:, 2:3]
-                    rstd = tail[:, 3:4] + tail[:, 4:5] + tail[:, 5:6]
-                    normed = (row[k, f, :, :depth].astype(jnp.float32) - mean) * rstd
-                    hidden_ref[k, j, f, i * part : (i + 1) * part, :] = (
-                        normed * (1.0 + scale) + shift
-                    ).astype(jnp.bfloat16)
+
+    @pl.when(k == 0)
+    def _():
+        total = shares[0][...]
+        for share in shares[1:]:
+            total = total + share[...]
+        mod_scr[...] = total
+
+    for f in range(frames):
+        step = lax.rem(z - k + n_tm, n_tm) * frames + f
+        shift, scale, gate = (mod_scr[c, pl.ds(step, 1), :] for c in range(3))
+        index = jnp.full((1, depth), step_ref[0] + step, jnp.int32)
+        coef_ref[0, f : f + 1, :] = (sigma_of(index + 1) - sigma_of(index)) * gate
+        for j in range(n_seq):
+            for i in range(n_mp):
+                row = rows[j * n_mp + i]
+                tail = row[0, f, :, depth:].astype(jnp.float32)
+                mean = tail[:, 0:1] + tail[:, 1:2] + tail[:, 2:3]
+                rstd = tail[:, 3:4] + tail[:, 4:5] + tail[:, 5:6]
+                normed = (row[0, f, :, :depth].astype(jnp.float32) - mean) * rstd
+                hidden_ref[0, j, f, i * part : (i + 1) * part, :] = (
+                    normed * (1.0 + scale) + shift
+                ).astype(jnp.bfloat16)
 
 
 def modulate(start_step, shares, rows):
@@ -204,12 +209,17 @@
     _, frames, part, wide = rows[0][0].shape
     depth = wide - LANES
     window = shares[0].shape[1]
-    smem, vmem = (pl.BlockSpec(memory_space=space) for space in (pltpu.SMEM, pltpu.VMEM))
     shape = (n_tm, n_seq, frames, n_mp * part, depth)
     return pl.pallas_call(
         functools.partial(modulate_kernel, n_tm, n_seq, n_mp),
-        in_specs=[smem] + [vmem] * (n_tm + n_seq * n_mp),
-        out_specs=[vmem] * 2,
+        grid=(n_tm,),
+        in_specs=[pl.BlockSpec(memory_space=pltpu.SMEM)]
+        + [pl.BlockSpec((3, window, depth), lambda k: (0, 0, 0))] * n_tm
+        + [pl.BlockSpec((1, frames, part, wide), lambda k: (k, 0, 0, 0))] * (n_seq * n_mp),
+        out_specs=[
+            pl.BlockSpec((1,) + shape[1:], lambda k: (k, 0, 0, 0, 0)),
+            pl.BlockSpec((1, frames, depth), lambda k: (k, 0, 0)),
+        ],
         scratch_shapes=[pltpu.VMEM((3, window, depth), jnp.float32)],
         out_shape=[
             jax.ShapeDtypeStruct(shape, jnp.bfloat16),
@@ -220,6 +230,7 @@
             bytes_accessed=4 * n_tm * n_seq * frames * n_mp * part * depth,
             transcendentals=0,
         ),
+        compiler_params=pltpu.CompilerParams(vmem_limit_bytes=24 << 20),
         name="modulate",
     )(start_step, *shares, *[r for side in rows for r in side])
 
@@ -230,16 +241,15 @@
     attn_refs = refs[:n_attn]
     w_refs = refs[n_attn : n_attn + n_seq * n_mp]
     outs = refs[n_attn + n_seq * n_mp :]
-    own_ref, moved_refs, (rows_scr, w_scr, sum_scr, sems) = outs[0], outs[1:-4], outs[-4:]
+    own_ref, moved_refs, (rows_scr, sum_scr) = outs[0], outs[1:-2], outs[-2:]
     z, m = lax.axis_index("tm"), lax.axis_index("mp")
     block = n_mp * part
     per = frames * block
     half = own_ref.shape[-1]
-    copies = []
+    total = None
     for j in range(n_seq):
         for l in range(n_mp):
             at = j * n_mp + l
-            group = [pltpu.make_async_copy(w_refs[at], w_scr.at[at], sems.at[at, 0])]
             for k in range(n_tm):
                 for f in range(frames):
                     for i in range(n_mp):
@@ -247,24 +257,16 @@
                         source = (i - l) % n_mp * part
                         for h, (lane, width) in enumerate(widths):
                             piece = attn_refs[(h * n_tm + k) * n_mp + l]
-                            group.append(
-                                pltpu.make_async_copy(
-                                    piece.at[j, f, pl.ds(source, part)],
-                                    rows_scr.at[at, pl.ds(first, part), pl.ds(lane, width)],
-                                    sems.at[at, len(group)],
-                                )
-                            )
-            for copy in group:
-                copy.start()
-            copies.append(group)
-    total = None
-    for at, group in enumerate(copies):
-        for copy in group:
-            copy.wait()
-        product = lax.dot_general(
-            rows_scr[at], w_scr[at], (((1,), (1,)), ((), ())), preferred_element_type=jnp.float32
-        )
-        total = product if total is None else total + product
+                            rows_scr[at, first : first + part, lane : lane + width] = piece[
+                                j, f, source : source + part, :
+                            ]
+            product = lax.dot_general(
+                rows_scr[at],
+                w_refs[at][...],
+                (((1,), (1,)), ((), ())),
+                preferred_element_type=jnp.float32,
+            )
+            total = product if total is None else total + product
     for k in range(n_tm):
         for f in range(frames):
             first = k * per + f * block
@@ -296,22 +298,21 @@
     tok = n_mp * part
     rows = n_tm * frames * tok
     deep = n_seq * n_mp * cols
-    vmem, anywhere = (pl.BlockSpec(memory_space=space) for space in (pltpu.VMEM, pl.ANY))
+    vmem = pl.BlockSpec(memory_space=pltpu.VMEM)
     return pl.pallas_call(
         functools.partial(project_kernel, dims, widths),
-        in_specs=[vmem] + [anywhere] * (len(widths) * n_tm * n_mp + n_seq * n_mp),
+        in_specs=[vmem] * (1 + len(widths) * n_tm * n_mp + n_seq * n_mp),
         out_specs=[vmem] * (1 + n_tm),
         scratch_shapes=[
             pltpu.VMEM((n_seq * n_mp, rows, cols), jnp.bfloat16),
-            pltpu.VMEM((n_seq * n_mp, half, cols), jnp.bfloat16),
             pltpu.VMEM((n_tm, frames, tok, half), jnp.float32),
-            pltpu.SemaphoreType.DMA((n_seq * n_mp, 1 + len(widths) * n_tm * frames * n_mp)),
         ],
         out_shape=[jax.ShapeDtypeStruct((frames, tok, half), jnp.float32)]
         + [jax.ShapeDtypeStruct((frames, tok, half), jnp.bfloat16)] * n_tm,
         cost_estimate=pl.CostEstimate(
             flops=2 * rows * deep * half, bytes_accessed=2 * (rows + half) * deep, transcendentals=0
         ),
+        compiler_params=pltpu.CompilerParams(vmem_limit_bytes=32 << 20),
         name="project",
     )(coef, *[a for h in attn for k in h for a in k], *[w for j in weights for w in j])
 
@@ -347,6 +348,7 @@
         cost_estimate=pl.CostEstimate(
             flops=0, bytes_accessed=8 * frames * tok * n_tm * half, transcendentals=0
         ),
+        compiler_params=pltpu.CompilerParams(vmem_limit_bytes=8 << 20),
         name="finish",
     )(*[b for k in blocks for b in k])
 
@@ -354,7 +356,7 @@
 def sweep(states, start_step, w_qkv, qk_gain, w_out, time_proj):
     frames, tok, _ = states.shape
     n_tm, n_seq, n_mp = (lax.axis_size(name) for name in ("tm", "seq", "mp"))
-    m = lax.axis_index("mp")
+    z, m = lax.axis_index("tm"), lax.axis_index("mp")
     part = tok // n_mp
     depth, cols = w_qkv.shape[1:]
     half = depth // n_mp
@@ -395,22 +397,39 @@
                 preferred_element_type=jnp.float32,
             )
         )
-    right, left = [None] * len(groups), [None] * len(groups)
+    even = z % 2 == 0
+    evens = [(i, i ^ 1) for i in range(n_tm)]
+    odds = []
+    for i in range(n_tm):
+        for c in range(n_mp):
+            other = i + 1 if i % 2 else i - 1
+            inside = 0 <= other < n_tm
+            to = other * n_mp + c if inside else i * n_mp + (c + 1) % n_mp
+            odds.append((i * n_mp + c, to))
+
+    def incoming(pair):
+        first, second = (0.0 if p is None else p.astype(jnp.float32) for p in pair)
+        right = jnp.where(z > 0, jnp.where(even, second, first), 0.0)
+        return right, jnp.where(z < n_tm - 1, jnp.where(even, first, second), 0.0)
+
+    flows = [(None, None)] * len(groups)
     for t in range(n_tm - 1):
         for h in range(len(groups)):
-            send_right, send_left = proj[h][(t + 1) % n_tm], proj[h][n_tm - 1 - t]
+            right, left = proj[h][(t + 1) % n_tm], proj[h][n_tm - 1 - t]
             if t:
-                right[h], left[h] = lax.optimization_barrier((right[h], left[h]))
-                send_right = send_right + right[h].astype(jnp.float32)
-                send_left = send_left + left[h].astype(jnp.float32)
-            send_right, send_left = (send_right.astype(jnp.float16), send_left.astype(jnp.float16))
-            right[h] = lax.ppermute(send_right, "tm", [(i, i + 1) for i in range(t + 1)])
-            left[h] = lax.ppermute(
-                send_left, "tm", [(n_tm - 1 - i, n_tm - 2 - i) for i in range(t + 1)]
-            )
+                more_right, more_left = incoming(flows[h])
+                right, left = right + more_right, left + more_left
+            first = jnp.where(even, right, left).astype(jnp.float16)
+            second = jnp.where(even, left, right).astype(jnp.float16)
+            first = lax.ppermute(first, "tm", evens)
+            if t:
+                second = lax.ppermute(second, ("tm", "mp"), odds)
+                first, second = lax.optimization_barrier((first, second))
+            flows[h] = (first, second if t else None)
     gathered = []
     for h, (lane, size) in enumerate(groups):
-        total = proj[h][0] + right[h].astype(jnp.float32) + left[h].astype(jnp.float32)
+        right, left = incoming(flows[h])
+        total = proj[h][0] + right + left
         total = total.reshape(3, n_seq, frames, tok, size)
         attn = attend(total, qk_gain[:, lane : lane + size])
         attn = jnp.stack([attn[0]] + [turn(attn[j], "seq", -j) for j in range(1, n_seq)])

time: 162 us -> 146 us (0.901)
  waiting for transfers between devices: 59 us -> 81.2 us
  starting transfers between devices: 61.4 us -> 41 us
  Pallas kernels: 22.4 us -> 6.83 us
  matrix products: 7.92 us -> 5.7 us
    ppermute x12 -> x10, starting transfers between devices: 29.4 us -> 9.49 us  [the longest x6 9.48 us: sweep(): first = lax.ppermute(first, 'tm', evens)]
    ppermute x12 -> x10, waiting for transfers between devices: 8.37 us -> 20 us  [the longest x6 20 us: sweep(): first = lax.ppermute(first, 'tm', evens)]
    ppermute x35, waiting for transfers between devices: 50.6 us -> 61.1 us  [turn(): lax.ppermute(block, axis, [(i, (i + distance) % size) for i in range(size)])]
    pallas_call x1, Pallas kernels: 5.85 us -> 1.54 us  [project(): pl.pallas_call(functools.partial(project_kernel, dims, widths), in_specs=...]
    convert_element_type x6, other arithmetic: 1.76 us -> 6.04 us  [the longest x4 4.49 us: sweep(): second = jnp.where(even, left, right).astype(jnp.float16)]
    pallas_call x2, Pallas kernels: 5.3 us -> 1.9 us  [attend(): pl.pallas_call(functools.partial(attend_kernel, n_seq, heads), grid=(fram...]
    pallas_call x1, Pallas kernels: 3.7 us -> 1.16 us  [modulate(): pl.pallas_call(functools.partial(modulate_kernel, n_tm, n_seq, n_mp), gri...]
    pallas_call x1, Pallas kernels: 3.09 us -> 0.83 us  [time_shares(): pl.pallas_call(functools.partial(time_kernel, n_tm), in_specs=[smem, vmem...]
  transfers between devices with their start and end apart: 47 -> 45, of which waited for: 24 -> 26; matrix products, arithmetic and copies ran while one was open for 4% -> 5% of each run, Pallas kernels for 5% -> 2%
where the time goes in v5:
time: 146 us
  waiting for transfers between devices  81.2 us (56%)
  starting transfers between devices  41 us (28%)
  other arithmetic  7.52 us (5%)
  Pallas kernels  6.83 us (5%)
  matrix products  5.7 us (4%)
  local copies, waits for them, and re-layouts  2.8 us (2%)
    ppermute x35, waiting for transfers between devices, turn(): lax.ppermute(block, axis, [(i, (i + distance) % size) for i in range(size)])  61.1 us
    ppermute x35, starting transfers between devices, turn(): lax.ppermute(block, axis, [(i, (i + distance) % size) for i in range(size)])  31.5 us
    ppermute x6, waiting for transfers between devices, sweep(): first = lax.ppermute(first, 'tm', evens)  20 us
    ppermute x6, starting transfers between devices, sweep(): first = lax.ppermute(first, 'tm', evens)  9.48 us
    dot_general x2, matrix products, sweep(): jnp.einsum('krd,cdh->kcrh', hidden, w_qkv[:, :, lane:lane + size], prefer...  5.7 us
    convert_element_type x4, other arithmetic, sweep(): second = jnp.where(even, left, right).astype(jnp.float16)  4.49 us
  transfers between devices with their start and end apart: 45, of which 26 were waited for; matrix products, arithmetic and copies ran while one was open for 5% of the time, Pallas kernels for 2%

profile of v5, /device:TPU:0, one launch (start us, length us, event | category | flops | bytes accessed | tf_op | source)
XLA Modules:
  0.0 146.0 jit_solution(16541610346789178640)
XLA Ops:
  0.0 1.1 copy-done.1
  1.5 3.1 %collective-permute-start.3 = (bf16[1,32,1408]{2,1,0:T(8,128)(2,1)S(1)}, bf16[1,32,1408]{2,1,0:T(8,128)(2,1)S(1)}, u32[]{:S(2)}, u32[]{:S(2)}) collective-permute-start(bf16[1,32,1408]{2,1,0:T(8,128)(2,1)S(1)} %get-tuple-element.37), channel_id=1, source_target_pairs={{0,4},{4,8},{8,12},{12,0},{1,5},{5,9},{9,13},{13,1},{2,6},{6,10},{... | collective-permute-start | bytes 270344 | tf_op jit(solution)/shard_map/ppermute | solution.py:28
  4.6 2.6 %collective-permute-start.4 = (bf16[1,32,1408]{2,1,0:T(8,128)(2,1)S(1)}, bf16[1,32,1408]{2,1,0:T(8,128)(2,1)S(1)}, u32[]{:S(2)}, u32[]{:S(2)}) collective-permute-start(bf16[1,32,1408]{2,1,0:T(8,128)(2,1)S(1)} %get-tuple-element.38), channel_id=1, source_target_pairs={{0,8},{4,12},{8,0},{12,4},{1,9},{5,13},{9,1},{13,5},{2,10},{6,14},... | collective-permute-start | bytes 270344 | tf_op jit(solution)/shard_map/ppermute | solution.py:28
  7.2 1.4 collective-permute-start.5
  8.5 1.4 collective-permute-done.3
  9.9 3.3 %collective-permute-done.4 = bf16[1,32,1408]{2,1,0:T(8,128)(2,1)S(1)} collective-permute-done((bf16[1,32,1408]{2,1,0:T(8,128)(2,1)S(1)}, bf16[1,32,1408]{2,1,0:T(8,128)(2,1)S(1)}, u32[]{:S(2)}, u32[]{:S(2)}) %collective-permute-start.4) | collective-permute-done | bytes 90144 | tf_op jit(solution)/shard_map/ppermute | solution.py:28
  13.5 1.6 %collective-permute-start.7 = (bf16[4,1,32,1408]{3,2,1,0:T(8,128)(2,1)S(1)}, bf16[4,1,32,1408]{3,2,1,0:T(8,128)(2,1)S(1)}, u32[]{:S(2)}, u32[]{:S(2)}) collective-permute-start(bf16[4,1,32,1408]{3,2,1,0:T(8,128)(2,1)S(1)} %pad_maximum_fusion.refs_4_), channel_id=1, source_target_pairs={{0,2},{2,0},{1,3},{3,1},{4,6},{6,4},{5,7},{7,5},{8,10},{10,8},{9,1... | collective-permute-start | bytes 1081352 | tf_op jit(solution)/shard_map/ppermute | solution.py:28
  15.0 8.6 %collective-permute-done.7.refs_6_ = bf16[4,1,32,1408]{3,2,1,0:T(8,128)(2,1)S(1)} collective-permute-done((bf16[4,1,32,1408]{3,2,1,0:T(8,128)(2,1)S(1)}, bf16[4,1,32,1408]{3,2,1,0:T(8,128)(2,1)S(1)}, u32[]{:S(2)}, u32[]{:S(2)}) %collective-permute-start.7) | collective-permute-done | bytes 360480 | tf_op jit(solution)/shard_map/ppermute | solution.py:28
  24.3 1.5 %copy-done = bf16[64,15360]{1,0:T(8,128)(2,1)S(1)} copy-done((bf16[64,15360]{1,0:T(8,128)(2,1)S(1)}, bf16[64,15360]{1,0:T(8,128)(2,1)}, u32[]{:S(2)}) %copy-start) | copy-done | bytes 1966104
  26.6 2.6 %collective-permute-start = (f32[3,4,1280]{2,1,0:T(4,128)S(1)}, f32[3,4,1280]{2,1,0:T(4,128)S(1)}, u32[]{:S(2)}, u32[]{:S(2)}) collective-permute-start(f32[3,4,1280]{2,1,0:T(4,128)S(1)} %get-tuple-element.33), channel_id=1, source_target_pairs={{0,4},{4,8},{8,12},{12,0},{1,5},{5,9},{9,13},{13,1},{2,6},{6,10},{... | collective-permute-start | bytes 184328 | tf_op jit(solution)/shard_map/ppermute | solution.py:28
  29.7 1.9 %collective-permute-start.2 = (f32[3,4,1280]{2,1,0:T(4,128)S(1)}, f32[3,4,1280]{2,1,0:T(4,128)S(1)}, u32[]{:S(2)}, u32[]{:S(2)}) collective-permute-start(f32[3,4,1280]{2,1,0:T(4,128)S(1)} %get-tuple-element.35), channel_id=1, source_target_pairs={{0,12},{4,0},{8,4},{12,8},{1,13},{5,1},{9,5},{13,9},{2,14},{6,2},{... | collective-permute-start | bytes 184328 | tf_op jit(solution)/shard_map/ppermute | solution.py:28
  31.6 1.5 %collective-permute-done.refs_1_ = f32[3,4,1280]{2,1,0:T(4,128)S(1)} collective-permute-done((f32[3,4,1280]{2,1,0:T(4,128)S(1)}, f32[3,4,1280]{2,1,0:T(4,128)S(1)}, u32[]{:S(2)}, u32[]{:S(2)}) %collective-permute-start) | collective-permute-done | bytes 61472 | tf_op jit(solution)/shard_map/ppermute | solution.py:28
  33.1 2.5 %collective-permute-done.1.refs_2_ = f32[3,4,1280]{2,1,0:T(4,128)S(1)} collective-permute-done((f32[3,4,1280]{2,1,0:T(4,128)S(1)}, f32[3,4,1280]{2,1,0:T(4,128)S(1)}, u32[]{:S(2)}, u32[]{:S(2)}) %collective-permute-start.1) | collective-permute-done | bytes 61472 | tf_op jit(solution)/shard_map/ppermute | solution.py:28
  35.6 1.2 modulate.1
  36.8 3.8 %fusion.9 = f32[4,3,128,384]{3,2,1,0:T(8,128)S(1)} fusion(bf16[4,128,1280,1]{2,1,3,0:T(8,128)(2,1)S(1)} %bitcast.117, bf16[3,1280,768]{2,1,0:T(8,128)(2,1)} %param.8), kind=kOutput, calls=%fused_computation.7 | convolution fusion | flops 1509949440 | bytes 6619136 | tf_op jit(solution)/shard_map/krd,cdh->kcrh/dot_general | solution.py:393
  40.7 1.9 %fusion.6 = f32[4,3,128,384]{3,2,1,0:T(8,128)S(1)} fusion(bf16[4,128,1280,1]{2,1,3,0:T(8,128)(2,1)S(1)} %bitcast.118, bf16[3,1280,768]{2,1,0:T(8,128)(2,1)S(1)} %bitcast.126), kind=kOutput, calls=%fused_computation.6 | convolution fusion | flops 1509949440 | bytes 6619136 | tf_op jit(solution)/shard_map/krd,cdh->kcrh/dot_general | solution.py:393
  43.4 1.8 %collective-permute-start.22 = (f16[3,128,384]{2,1,0:T(8,128)(2,1)}, f16[3,128,384]{2,1,0:T(8,128)(2,1)}, u32[]{:S(2)}, u32[]{:S(2)}) collective-permute-start(f16[3,128,384]{2,1,0:T(8,128)(2,1)} %select_convert_fusion.4), channel_id=1, source_target_pairs={{0,4},{4,0},{8,12},{12,8},{1,5},{5,1},{9,13},{13,9},{2,6},{6,2},{1... | collective-permute-start | bytes 884744 | tf_op jit(solution)/shard_map/ppermute | solution.py:424
  46.4 7.2 %collective-permute-done.22 = f16[3,128,384]{2,1,0:T(8,128)(2,1)} collective-permute-done((f16[3,128,384]{2,1,0:T(8,128)(2,1)}, f16[3,128,384]{2,1,0:T(8,128)(2,1)}, u32[]{:S(2)}, u32[]{:S(2)}) %collective-permute-start.22) | collective-permute-done | bytes 294944 | tf_op jit(solution)/shard_map/ppermute | solution.py:424
  53.6 1.4 select_convert_fusion.2
  55.0 1.9 %collective-permute-start.23 = (f16[3,128,384]{2,1,0:T(8,128)(2,1)S(1)}, f16[3,128,384]{2,1,0:T(8,128)(2,1)S(1)}, u32[]{:S(2)}, u32[]{:S(2)}) collective-permute-start(f16[3,128,384]{2,1,0:T(8,128)(2,1)S(1)} %get-tuple-element.64), channel_id=1, source_target_pairs={{0,4},{4,0},{8,12},{12,8},{1,5},{5,1},{9,13},{13,9},{2,6},{6,2},{1... | collective-permute-start | bytes 884744 | tf_op jit(solution)/shard_map/ppermute | solution.py:424
  56.8 2.9 %collective-permute-done.9 = f16[3,128,384]{2,1,0:T(8,128)(2,1)S(1)} collective-permute-done((f16[3,128,384]{2,1,0:T(8,128)(2,1)}, f16[3,128,384]{2,1,0:T(8,128)(2,1)S(1)}, u32[]{:S(2)}, u32[]{:S(2)}) %collective-permute-start.9) | collective-permute-done | bytes 294944 | tf_op jit(solution)/shard_map/ppermute | solution.py:424
  59.8 1.3 select_convert_fusion.7
  61.1 1.9 %collective-permute-start.10 = (f16[3,128,384]{2,1,0:T(8,128)(2,1)S(1)}, f16[3,128,384]{2,1,0:T(8,128)(2,1)S(1)}, u32[]{:S(2)}, u32[]{:S(2)}) collective-permute-start(f16[3,128,384]{2,1,0:T(8,128)(2,1)S(1)} %get-tuple-element.66), channel_id=1, source_target_pairs={{0,4},{4,0},{8,12},{12,8},{1,5},{5,1},{9,13},{13,9},{2,6},{6,2},{1... | collective-permute-start | bytes 884744 | tf_op jit(solution)/shard_map/ppermute | solution.py:424
  63.0 3.1 %collective-permute-done.23 = f16[3,128,384]{2,1,0:T(8,128)(2,1)S(1)} collective-permute-done((f16[3,128,384]{2,1,0:T(8,128)(2,1)S(1)}, f16[3,128,384]{2,1,0:T(8,128)(2,1)S(1)}, u32[]{:S(2)}, u32[]{:S(2)}) %collective-permute-start.23) | collective-permute-done | bytes 294944 | tf_op jit(solution)/shard_map/ppermute | solution.py:424
  66.1 1.5 %collective-permute-start.36 = (bf16[640,768]{1,0:T(8,128)(2,1)S(1)}, bf16[640,768]{1,0:T(8,128)(2,1)S(1)}, u32[]{:S(2)}, u32[]{:S(2)}) collective-permute-start(bf16[640,768]{1,0:T(8,128)(2,1)S(1)} %get-tuple-element.68.refs_16_), channel_id=1, source_target_pairs={{0,2},{2,0},{1,3},{3,1},{4,6},{6,4},{5,7},{7,5},{8,10},{10,8},{9,1... | collective-permute-start | bytes 2949128 | tf_op jit(solution)/shard_map/ppermute | solution.py:28
  67.6 1.5 %select_convert_fusion = (f16[3,128,384]{2,1,0:T(8,128)(2,1)S(1)}, f16[3,128,384]{2,1,0:T(8,128)(2,1)S(1)}) fusion(pred[]{:T(512)S(6)} %eq.6, f16[3,128,384]{2,1,0:T(8,128)(2,1)S(1)} %collective-permute-done.24, f16[3,128,384]{2,1,0:T(8,128)(2,1)S(1)} %collective-permute-done.23, pred[]{:T(512)S(6)} %lt.26, f32[4,3,128,384]{3,2,1,0:T(8,128)} %copy-done.4, ...), kind=kLoop, calls=%fused_computation.54 | loop fusion | flops 1769472 | bytes 2359299 | tf_op jit(solution)/shard_map/convert_element_type | solution.py:423
  69.1 1.9 %collective-permute-start.25 = (f16[3,128,384]{2,1,0:T(8,128)(2,1)S(1)}, f16[3,128,384]{2,1,0:T(8,128)(2,1)S(1)}, u32[]{:S(2)}, u32[]{:S(2)}) collective-permute-start(f16[3,128,384]{2,1,0:T(8,128)(2,1)S(1)} %get-tuple-element.60), channel_id=1, source_target_pairs={{0,4},{4,0},{8,12},{12,8},{1,5},{5,1},{9,13},{13,9},{2,6},{6,2},{1... | collective-permute-start | bytes 884744 | tf_op jit(solution)/shard_map/ppermute | solution.py:424
  71.0 1.5 %collective-permute-done.10 = f16[3,128,384]{2,1,0:T(8,128)(2,1)S(1)} collective-permute-done((f16[3,128,384]{2,1,0:T(8,128)(2,1)S(1)}, f16[3,128,384]{2,1,0:T(8,128)(2,1)S(1)}, u32[]{:S(2)}, u32[]{:S(2)}) %collective-permute-start.10) | collective-permute-done | bytes 294944 | tf_op jit(solution)/shard_map/ppermute | solution.py:424
  72.7 1.9 %collective-permute-start.12 = (f16[3,128,384]{2,1,0:T(8,128)(2,1)S(1)}, f16[3,128,384]{2,1,0:T(8,128)(2,1)S(1)}, u32[]{:S(2)}, u32[]{:S(2)}) collective-permute-start(f16[3,128,384]{2,1,0:T(8,128)(2,1)S(1)} %get-tuple-element.62), channel_id=1, source_target_pairs={{0,4},{4,0},{8,12},{12,8},{1,5},{5,1},{9,13},{13,9},{2,6},{6,2},{1... | collective-permute-start | bytes 884744 | tf_op jit(solution)/shard_map/ppermute | solution.py:424
  74.6 4.4 %collective-permute-done.25 = f16[3,128,384]{2,1,0:T(8,128)(2,1)S(1)} collective-permute-done((f16[3,128,384]{2,1,0:T(8,128)(2,1)S(1)}, f16[3,128,384]{2,1,0:T(8,128)(2,1)S(1)}, u32[]{:S(2)}, u32[]{:S(2)}) %collective-permute-start.25) | collective-permute-done | bytes 294944 | tf_op jit(solution)/shard_map/ppermute | solution.py:424
  79.0 1.2 collective-permute-start.37
  80.2 1.2 fusion.34
  81.5 0.9 attend.3
  82.4 0.9 collective-permute-start.27
  84.4 0.9 attend.2
  85.3 1.5 %collective-permute-start.14 = (bf16[1,64,384]{2,1,0:T(8,128)(2,1)S(1)}, bf16[1,64,384]{2,1,0:T(8,128)(2,1)S(1)}, u32[]{:S(2)}, u32[]{:S(2)}) collective-permute-start(bf16[1,64,384]{2,1,0:T(8,128)(2,1)S(1)} %get-tuple-element.47), channel_id=1, source_target_pairs={{0,2},{2,0},{1,3},{3,1},{4,6},{6,4},{5,7},{7,5},{8,10},{10,8},{9,1... | collective-permute-start | bytes 147464 | tf_op jit(solution)/shard_map/ppermute | solution.py:28
  86.9 23.9 %collective-permute-done.27 = bf16[1,64,384]{2,1,0:T(8,128)(2,1)S(1)} collective-permute-done((bf16[1,64,384]{2,1,0:T(8,128)(2,1)S(1)}, bf16[1,64,384]{2,1,0:T(8,128)(2,1)S(1)}, u32[]{:S(2)}, u32[]{:S(2)}) %collective-permute-start.27) | collective-permute-done | bytes 49184 | tf_op jit(solution)/shard_map/ppermute | solution.py:28
  110.8 1.7 %collective-permute-start.29 = (bf16[2,1,64,384]{3,2,1,0:T(8,128)(2,1)S(1)}, bf16[2,1,64,384]{3,2,1,0:T(8,128)(2,1)S(1)}, u32[]{:S(2)}, u32[]{:S(2)}) collective-permute-start(bf16[2,1,64,384]{3,2,1,0:T(8,128)(2,1)S(1)} %pad_maximum_fusion.2.refs_8_), channel_id=1, source_target_pairs={{0,4},{4,8},{8,12},{12,0},{1,5},{5,9},{9,13},{13,1},{2,6},{6,10},{... | collective-permute-start | bytes 294920 | tf_op jit(solution)/shard_map/ppermute | solution.py:28
  112.8 2.2 %collective-permute-start.33 = (bf16[2,1,64,384]{3,2,1,0:T(8,128)(2,1)S(1)}, bf16[2,1,64,384]{3,2,1,0:T(8,128)(2,1)S(1)}, u32[]{:S(2)}, u32[]{:S(2)}) collective-permute-start(bf16[2,1,64,384]{3,2,1,0:T(8,128)(2,1)S(1)} %pad_maximum_fusion.2.refs_8_), channel_id=1, source_target_pairs={{0,12},{4,0},{8,4},{12,8},{1,13},{5,1},{9,5},{13,9},{2,14},{6,2},{... | collective-permute-start | bytes 294920 | tf_op jit(solution)/shard_map/ppermute | solution.py:28
  115.1 2.3 %collective-permute-done.29.refs_10_ = bf16[2,1,64,384]{3,2,1,0:T(8,128)(2,1)S(1)} collective-permute-done((bf16[2,1,64,384]{3,2,1,0:T(8,128)(2,1)S(1)}, bf16[2,1,64,384]{3,2,1,0:T(8,128)(2,1)S(1)}, u32[]{:S(2)}, u32[]{:S(2)}) %collective-permute-start.29) | collective-permute-done | bytes 98336 | tf_op jit(solution)/shard_map/ppermute | solution.py:28
  117.4 2.6 %collective-permute-done.31.refs_12_ = bf16[2,1,64,384]{3,2,1,0:T(8,128)(2,1)S(1)} collective-permute-done((bf16[2,1,64,384]{3,2,1,0:T(8,128)(2,1)S(1)}, bf16[2,1,64,384]{3,2,1,0:T(8,128)(2,1)S(1)}, u32[]{:S(2)}, u32[]{:S(2)}) %collective-permute-start.31) | collective-permute-done | bytes 98336 | tf_op jit(solution)/shard_map/ppermute | solution.py:28
  120.1 3.8 %collective-permute-start.20 = (bf16[2,1,64,384]{3,2,1,0:T(8,128)(2,1)S(1)}, bf16[2,1,64,384]{3,2,1,0:T(8,128)(2,1)S(1)}, u32[]{:S(2)}, u32[]{:S(2)}) collective-permute-start(bf16[2,1,64,384]{3,2,1,0:T(8,128)(2,1)S(1)} %pad_maximum_fusion.1.refs_0_), channel_id=1, source_target_pairs={{0,12},{4,0},{8,4},{12,8},{1,13},{5,1},{9,5},{13,9},{2,14},{6,2},{... | collective-permute-start | bytes 294920 | tf_op jit(solution)/shard_map/ppermute | solution.py:28
  124.4 3.7 %collective-permute-done.18.refs_4_ = bf16[2,1,64,384]{3,2,1,0:T(8,128)(2,1)S(1)} collective-permute-done((bf16[2,1,64,384]{3,2,1,0:T(8,128)(2,1)S(1)}, bf16[2,1,64,384]{3,2,1,0:T(8,128)(2,1)S(1)}, u32[]{:S(2)}, u32[]{:S(2)}) %collective-permute-start.18) | collective-permute-done | bytes 98336 | tf_op jit(solution)/shard_map/ppermute | solution.py:28
  131.0 1.5 %project.1 = (f32[1,64,640]{2,1,0:T(8,128)S(1)}, bf16[1,64,640]{2,1,0:T(8,128)(2,1)S(1)}, bf16[1,64,640]{2,1,0:T(8,128)(2,1)S(1)}, bf16[1,64,640]{2,1,0:T(8,128)(2,1)S(1)}, bf16[1,64,640]{2,1,0:T(8,128)(2,1)S(1)}) custom-call(f32[4,1,1280]{2,1,0:T(1,128)S(1)} %get-tuple-element.40.coef_ref, bf16[2,1,64,384]{3,2,1,0:T(8,128)(2,1)S(1)} %pad_maximum_fusion.1.refs_0_, ...), custom_call_target="tpu_custom_call" | custom-call | flops 1006632960 | bytes 5505024 | tf_op jit(solution)/shard_map/project/pallas_call | solution.py:302
  132.5 2.4 %collective-permute-start.39 = (bf16[1,64,640]{2,1,0:T(8,128)(2,1)S(1)}, bf16[1,64,640]{2,1,0:T(8,128)(2,1)S(1)}, u32[]{:S(2)}, u32[]{:S(2)}) collective-permute-start(bf16[1,64,640]{2,1,0:T(8,128)(2,1)S(1)} %get-tuple-element.56), channel_id=1, source_target_pairs={{0,12},{4,0},{8,4},{12,8},{1,13},{5,1},{9,5},{13,9},{2,14},{6,2},{... | collective-permute-start | bytes 245768 | tf_op jit(solution)/shard_map/ppermute | solution.py:28
  135.6 2.2 %collective-permute-done.39.refs_2_ = bf16[1,64,640]{2,1,0:T(8,128)(2,1)S(1)} collective-permute-done((bf16[1,64,640]{2,1,0:T(8,128)(2,1)S(1)}, bf16[1,64,640]{2,1,0:T(8,128)(2,1)S(1)}, u32[]{:S(2)}, u32[]{:S(2)}) %collective-permute-start.39) | collective-permute-done | bytes 81952 | tf_op jit(solution)/shard_map/ppermute | solution.py:28
  137.8 5.7 %collective-permute-done.41.refs_4_ = bf16[1,64,640]{2,1,0:T(8,128)(2,1)S(1)} collective-permute-done((bf16[1,64,640]{2,1,0:T(8,128)(2,1)S(1)}, bf16[1,64,640]{2,1,0:T(8,128)(2,1)S(1)}, u32[]{:S(2)}, u32[]{:S(2)}) %collective-permute-start.41) | collective-permute-done | bytes 81952 | tf_op jit(solution)/shard_map/ppermute | solution.py:28
  144.9 1.0 finish.1
  (83 shorter events, 11.2 us)
Async XLA Ops:
  1.5 8.4 %collective-permute-start.3 = (bf16[1,32,1408]{2,1,0:T(8,128)(2,1)S(1)}, bf16[1,32,1408]{2,1,0:T(8,128)(2,1)S(1)}, u32[]{:S(2)}, u32[]{:S(2)}) collective-permute-start(bf16[1,32,1408]{2,1,0:T(8,128)(2,1)S(1)} %get-tuple-element.37), channel_id=1, source_target_pairs={{0,4},{4,8},{8,12},{12,0},{1,5},{5,9},{9,13},{13,1},{2,6},{6,10},{... | collective-permute-start | bytes 270344 | tf_op jit(solution)/shard_map/ppermute | solution.py:28
  4.6 8.6 %collective-permute-start.4 = (bf16[1,32,1408]{2,1,0:T(8,128)(2,1)S(1)}, bf16[1,32,1408]{2,1,0:T(8,128)(2,1)S(1)}, u32[]{:S(2)}, u32[]{:S(2)}) collective-permute-start(bf16[1,32,1408]{2,1,0:T(8,128)(2,1)S(1)} %get-tuple-element.38), channel_id=1, source_target_pairs={{0,8},{4,12},{8,0},{12,4},{1,9},{5,13},{9,1},{13,5},{2,10},{6,14},... | collective-permute-start | bytes 270344 | tf_op jit(solution)/shard_map/ppermute | solution.py:28
  7.2 6.3 %collective-permute-start.5 = (bf16[1,32,1408]{2,1,0:T(8,128)(2,1)S(1)}, bf16[1,32,1408]{2,1,0:T(8,128)(2,1)S(1)}, u32[]{:S(2)}, u32[]{:S(2)}) collective-permute-start(bf16[1,32,1408]{2,1,0:T(8,128)(2,1)S(1)} %get-tuple-element.39), channel_id=1, source_target_pairs={{0,12},{4,0},{8,4},{12,8},{1,13},{5,1},{9,5},{13,9},{2,14},{6,2},{... | collective-permute-start | bytes 270344 | tf_op jit(solution)/shard_map/ppermute | solution.py:28
  13.5 10.1 %collective-permute-start.7 = (bf16[4,1,32,1408]{3,2,1,0:T(8,128)(2,1)S(1)}, bf16[4,1,32,1408]{3,2,1,0:T(8,128)(2,1)S(1)}, u32[]{:S(2)}, u32[]{:S(2)}) collective-permute-start(bf16[4,1,32,1408]{3,2,1,0:T(8,128)(2,1)S(1)} %pad_maximum_fusion.refs_4_), channel_id=1, source_target_pairs={{0,2},{2,0},{1,3},{3,1},{4,6},{6,4},{5,7},{7,5},{8,10},{10,8},{9,1... | collective-permute-start | bytes 1081352 | tf_op jit(solution)/shard_map/ppermute | solution.py:28
  15.0 20.6 %collective-permute-start.6 = (bf16[4,1,32,1408]{3,2,1,0:T(8,128)(2,1)S(1)}, bf16[4,1,32,1408]{3,2,1,0:T(8,128)(2,1)S(1)}, u32[]{:S(2)}, u32[]{:S(2)}) collective-permute-start(bf16[4,1,32,1408]{3,2,1,0:T(8,128)(2,1)S(1)} %pad_maximum_fusion.refs_4_), channel_id=1, source_target_pairs={{0,1},{1,0},{2,3},{3,2},{4,5},{5,4},{6,7},{7,6},{8,9},{9,8},{10,11... | collective-permute-start | bytes 1081352 | tf_op jit(solution)/shard_map/ppermute | solution.py:28
  23.6 12.0 %collective-permute-start.8 = (bf16[4,1,32,1408]{3,2,1,0:T(8,128)(2,1)S(1)}, bf16[4,1,32,1408]{3,2,1,0:T(8,128)(2,1)S(1)}, u32[]{:S(2)}, u32[]{:S(2)}) collective-permute-start(bf16[4,1,32,1408]{3,2,1,0:T(8,128)(2,1)S(1)} %collective-permute-done.7.refs_6_), channel_id=1, source_target_pairs={{0,1},{1,0},{2,3},{3,2},{4,5},{5,4},{6,7},{7,6},{8,9},{9,8},{10,11... | collective-permute-start | bytes 1081352 | tf_op jit(solution)/shard_map/ppermute | solution.py:28
  26.6 6.5 %collective-permute-start = (f32[3,4,1280]{2,1,0:T(4,128)S(1)}, f32[3,4,1280]{2,1,0:T(4,128)S(1)}, u32[]{:S(2)}, u32[]{:S(2)}) collective-permute-start(f32[3,4,1280]{2,1,0:T(4,128)S(1)} %get-tuple-element.33), channel_id=1, source_target_pairs={{0,4},{4,8},{8,12},{12,0},{1,5},{5,9},{9,13},{13,1},{2,6},{6,10},{... | collective-permute-start | bytes 184328 | tf_op jit(solution)/shard_map/ppermute | solution.py:28
  29.2 6.4 %collective-permute-start.1 = (f32[3,4,1280]{2,1,0:T(4,128)S(1)}, f32[3,4,1280]{2,1,0:T(4,128)S(1)}, u32[]{:S(2)}, u32[]{:S(2)}) collective-permute-start(f32[3,4,1280]{2,1,0:T(4,128)S(1)} %get-tuple-element.34), channel_id=1, source_target_pairs={{0,8},{4,12},{8,0},{12,4},{1,9},{5,13},{9,1},{13,5},{2,10},{6,14},... | collective-permute-start | bytes 184328 | tf_op jit(solution)/shard_map/ppermute | solution.py:28
  29.7 5.9 %collective-permute-start.2 = (f32[3,4,1280]{2,1,0:T(4,128)S(1)}, f32[3,4,1280]{2,1,0:T(4,128)S(1)}, u32[]{:S(2)}, u32[]{:S(2)}) collective-permute-start(f32[3,4,1280]{2,1,0:T(4,128)S(1)} %get-tuple-element.35), channel_id=1, source_target_pairs={{0,12},{4,0},{8,4},{12,8},{1,13},{5,1},{9,5},{13,9},{2,14},{6,2},{... | collective-permute-start | bytes 184328 | tf_op jit(solution)/shard_map/ppermute | solution.py:28
  35.6 5.0 %slice-start = ((s8[5898240]{0:T(1024)(128)(4,1)}), s8[4194304]{0:T(1024)(128)(4,1)S(1)}, s32[]{:S(2)}) async-start(s8[5898240]{0:T(1024)(128)(4,1)} %bitcast.125), calls=%async_computation | async-start | bytes 8388608
  43.4 10.2 %collective-permute-start.22 = (f16[3,128,384]{2,1,0:T(8,128)(2,1)}, f16[3,128,384]{2,1,0:T(8,128)(2,1)}, u32[]{:S(2)}, u32[]{:S(2)}) collective-permute-start(f16[3,128,384]{2,1,0:T(8,128)(2,1)} %select_convert_fusion.4), channel_id=1, source_target_pairs={{0,4},{4,0},{8,12},{12,8},{1,5},{5,1},{9,13},{13,9},{2,6},{6,2},{1... | collective-permute-start | bytes 884744 | tf_op jit(solution)/shard_map/ppermute | solution.py:424
  45.9 13.8 %collective-permute-start.9 = (f16[3,128,384]{2,1,0:T(8,128)(2,1)}, f16[3,128,384]{2,1,0:T(8,128)(2,1)S(1)}, u32[]{:S(2)}, u32[]{:S(2)}) collective-permute-start(f16[3,128,384]{2,1,0:T(8,128)(2,1)} %select_convert_fusion.9), channel_id=1, source_target_pairs={{0,4},{4,0},{8,12},{12,8},{1,5},{5,1},{9,13},{13,9},{2,6},{6,2},{1... | collective-permute-start | bytes 884744 | tf_op jit(solution)/shard_map/ppermute | solution.py:424
  46.3 28.3 %collective-permute-start.35 = (bf16[640,768]{1,0:T(8,128)(2,1)S(1)}, bf16[640,768]{1,0:T(8,128)(2,1)S(1)}, u32[]{:S(2)}, u32[]{:S(2)}) collective-permute-start(bf16[640,768]{1,0:T(8,128)(2,1)S(1)} %get-tuple-element.67), channel_id=1, source_target_pairs={{0,1},{1,0},{2,3},{3,2},{4,5},{5,4},{6,7},{7,6},{8,9},{9,8},{10,11... | collective-permute-start | bytes 2949128 | tf_op jit(solution)/shard_map/ppermute | solution.py:28
  46.4 26.0 %copy-start.3 = (f32[4,3,128,384]{3,2,1,0:T(8,128)S(1)}, f32[4,3,128,384]{3,2,1,0:T(8,128)}, u32[]{:S(2)}) copy-start(f32[4,3,128,384]{3,2,1,0:T(8,128)} %copy-done.2) | copy-start | bytes 7077892
  55.0 11.1 %collective-permute-start.23 = (f16[3,128,384]{2,1,0:T(8,128)(2,1)S(1)}, f16[3,128,384]{2,1,0:T(8,128)(2,1)S(1)}, u32[]{:S(2)}, u32[]{:S(2)}) collective-permute-start(f16[3,128,384]{2,1,0:T(8,128)(2,1)S(1)} %get-tuple-element.64), channel_id=1, source_target_pairs={{0,4},{4,0},{8,12},{12,8},{1,5},{5,1},{9,13},{13,9},{2,6},{6,2},{1... | collective-permute-start | bytes 884744 | tf_op jit(solution)/shard_map/ppermute | solution.py:424
  56.8 10.8 %collective-permute-start.24 = (f16[3,128,384]{2,1,0:T(8,128)(2,1)S(1)}, f16[3,128,384]{2,1,0:T(8,128)(2,1)S(1)}, u32[]{:S(2)}, u32[]{:S(2)}) collective-permute-start(f16[3,128,384]{2,1,0:T(8,128)(2,1)S(1)} %get-tuple-element.63), channel_id=1, source_target_pairs={{0,1},{1,0},{4,8},{5,9},{8,4},{9,5},{12,13},{13,12},{2,3},{3,2},{6... | collective-permute-start | bytes 884744 | tf_op jit(solution)/shard_map/ppermute | solution.py:426
  61.1 11.3 %collective-permute-start.10 = (f16[3,128,384]{2,1,0:T(8,128)(2,1)S(1)}, f16[3,128,384]{2,1,0:T(8,128)(2,1)S(1)}, u32[]{:S(2)}, u32[]{:S(2)}) collective-permute-start(f16[3,128,384]{2,1,0:T(8,128)(2,1)S(1)} %get-tuple-element.66), channel_id=1, source_target_pairs={{0,4},{4,0},{8,12},{12,8},{1,5},{5,1},{9,13},{13,9},{2,6},{6,2},{1... | collective-permute-start | bytes 884744 | tf_op jit(solution)/shard_map/ppermute | solution.py:424
  63.0 9.5 %collective-permute-start.11 = (f16[3,128,384]{2,1,0:T(8,128)(2,1)S(1)}, f16[3,128,384]{2,1,0:T(8,128)(2,1)S(1)}, u32[]{:S(2)}, u32[]{:S(2)}) collective-permute-start(f16[3,128,384]{2,1,0:T(8,128)(2,1)S(1)} %get-tuple-element.65), channel_id=1, source_target_pairs={{0,1},{1,0},{4,8},{5,9},{8,4},{9,5},{12,13},{13,12},{2,3},{3,2},{6... | collective-permute-start | bytes 884744 | tf_op jit(solution)/shard_map/ppermute | solution.py:426
  66.1 8.5 %copy-start.6 = (f32[2,768]{1,0:T(2,128)S(1)}, f32[2,768]{1,0:T(2,128)}, u32[]{:S(2)}) copy-start(f32[2,768]{1,0:T(2,128)} %param.9) | copy-start | bytes 18436
  66.1 48.9 %collective-permute-start.36 = (bf16[640,768]{1,0:T(8,128)(2,1)S(1)}, bf16[640,768]{1,0:T(8,128)(2,1)S(1)}, u32[]{:S(2)}, u32[]{:S(2)}) collective-permute-start(bf16[640,768]{1,0:T(8,128)(2,1)S(1)} %get-tuple-element.68.refs_16_), channel_id=1, source_target_pairs={{0,2},{2,0},{1,3},{3,1},{4,6},{6,4},{5,7},{7,5},{8,10},{10,8},{9,1... | collective-permute-start | bytes 2949128 | tf_op jit(solution)/shard_map/ppermute | solution.py:28
  69.1 9.9 %collective-permute-start.25 = (f16[3,128,384]{2,1,0:T(8,128)(2,1)S(1)}, f16[3,128,384]{2,1,0:T(8,128)(2,1)S(1)}, u32[]{:S(2)}, u32[]{:S(2)}) collective-permute-start(f16[3,128,384]{2,1,0:T(8,128)(2,1)S(1)} %get-tuple-element.60), channel_id=1, source_target_pairs={{0,4},{4,0},{8,12},{12,8},{1,5},{5,1},{9,13},{13,9},{2,6},{6,2},{1... | collective-permute-start | bytes 884744 | tf_op jit(solution)/shard_map/ppermute | solution.py:424
  72.4 7.8 %collective-permute-start.26 = (f16[3,128,384]{2,1,0:T(8,128)(2,1)S(1)}, f16[3,128,384]{2,1,0:T(8,128)(2,1)S(1)}, u32[]{:S(2)}, u32[]{:S(2)}) collective-permute-start(f16[3,128,384]{2,1,0:T(8,128)(2,1)S(1)} %get-tuple-element.59), channel_id=1, source_target_pairs={{0,1},{1,0},{4,8},{5,9},{8,4},{9,5},{12,13},{13,12},{2,3},{3,2},{6... | collective-permute-start | bytes 884744 | tf_op jit(solution)/shard_map/ppermute | solution.py:426
  72.7 11.5 %collective-permute-start.12 = (f16[3,128,384]{2,1,0:T(8,128)(2,1)S(1)}, f16[3,128,384]{2,1,0:T(8,128)(2,1)S(1)}, u32[]{:S(2)}, u32[]{:S(2)}) collective-permute-start(f16[3,128,384]{2,1,0:T(8,128)(2,1)S(1)} %get-tuple-element.62), channel_id=1, source_target_pairs={{0,4},{4,0},{8,12},{12,8},{1,5},{5,1},{9,13},{13,9},{2,6},{6,2},{1... | collective-permute-start | bytes 884744 | tf_op jit(solution)/shard_map/ppermute | solution.py:424
  74.6 9.6 %collective-permute-start.13 = (f16[3,128,384]{2,1,0:T(8,128)(2,1)S(1)}, f16[3,128,384]{2,1,0:T(8,128)(2,1)S(1)}, u32[]{:S(2)}, u32[]{:S(2)}) collective-permute-start(f16[3,128,384]{2,1,0:T(8,128)(2,1)S(1)} %get-tuple-element.61), channel_id=1, source_target_pairs={{0,1},{1,0},{4,8},{5,9},{8,4},{9,5},{12,13},{13,12},{2,3},{3,2},{6... | collective-permute-start | bytes 884744 | tf_op jit(solution)/shard_map/ppermute | solution.py:426
  79.0 52.0 %collective-permute-start.37 = (bf16[640,768]{1,0:T(8,128)(2,1)S(1)}, bf16[640,768]{1,0:T(8,128)(2,1)S(1)}, u32[]{:S(2)}, u32[]{:S(2)}) collective-permute-start(bf16[640,768]{1,0:T(8,128)(2,1)S(1)} %collective-permute-done.35.refs_17_), channel_id=1, source_target_pairs={{0,2},{2,0},{1,3},{3,1},{4,6},{6,4},{5,7},{7,5},{8,10},{10,8},{9,1... | collective-permute-start | bytes 2949128 | tf_op jit(solution)/shard_map/ppermute | solution.py:28
  82.4 28.4 %collective-permute-start.27 = (bf16[1,64,384]{2,1,0:T(8,128)(2,1)S(1)}, bf16[1,64,384]{2,1,0:T(8,128)(2,1)S(1)}, u32[]{:S(2)}, u32[]{:S(2)}) collective-permute-start(bf16[1,64,384]{2,1,0:T(8,128)(2,1)S(1)} %get-tuple-element.53), channel_id=1, source_target_pairs={{0,2},{2,0},{1,3},{3,1},{4,6},{6,4},{5,7},{7,5},{8,10},{10,8},{9,1... | collective-permute-start | bytes 147464 | tf_op jit(solution)/shard_map/ppermute | solution.py:28
  85.3 27.5 %collective-permute-start.14 = (bf16[1,64,384]{2,1,0:T(8,128)(2,1)S(1)}, bf16[1,64,384]{2,1,0:T(8,128)(2,1)S(1)}, u32[]{:S(2)}, u32[]{:S(2)}) collective-permute-start(bf16[1,64,384]{2,1,0:T(8,128)(2,1)S(1)} %get-tuple-element.47), channel_id=1, source_target_pairs={{0,2},{2,0},{1,3},{3,1},{4,6},{6,4},{5,7},{7,5},{8,10},{10,8},{9,1... | collective-permute-start | bytes 147464 | tf_op jit(solution)/shard_map/ppermute | solution.py:28
  110.8 6.6 %collective-permute-start.29 = (bf16[2,1,64,384]{3,2,1,0:T(8,128)(2,1)S(1)}, bf16[2,1,64,384]{3,2,1,0:T(8,128)(2,1)S(1)}, u32[]{:S(2)}, u32[]{:S(2)}) collective-permute-start(bf16[2,1,64,384]{3,2,1,0:T(8,128)(2,1)S(1)} %pad_maximum_fusion.2.refs_8_), channel_id=1, source_target_pairs={{0,4},{4,8},{8,12},{12,0},{1,5},{5,9},{9,13},{13,1},{2,6},{6,10},{... | collective-permute-start | bytes 294920 | tf_op jit(solution)/shard_map/ppermute | solution.py:28
  112.5 7.5 %collective-permute-start.31 = (bf16[2,1,64,384]{3,2,1,0:T(8,128)(2,1)S(1)}, bf16[2,1,64,384]{3,2,1,0:T(8,128)(2,1)S(1)}, u32[]{:S(2)}, u32[]{:S(2)}) collective-permute-start(bf16[2,1,64,384]{3,2,1,0:T(8,128)(2,1)S(1)} %pad_maximum_fusion.2.refs_8_), channel_id=1, source_target_pairs={{0,8},{4,12},{8,0},{12,4},{1,9},{5,13},{9,1},{13,5},{2,10},{6,14},... | collective-permute-start | bytes 294920 | tf_op jit(solution)/shard_map/ppermute | solution.py:28
  112.8 7.3 %collective-permute-start.33 = (bf16[2,1,64,384]{3,2,1,0:T(8,128)(2,1)S(1)}, bf16[2,1,64,384]{3,2,1,0:T(8,128)(2,1)S(1)}, u32[]{:S(2)}, u32[]{:S(2)}) collective-permute-start(bf16[2,1,64,384]{3,2,1,0:T(8,128)(2,1)S(1)} %pad_maximum_fusion.2.refs_8_), channel_id=1, source_target_pairs={{0,12},{4,0},{8,4},{12,8},{1,13},{5,1},{9,5},{13,9},{2,14},{6,2},{... | collective-permute-start | bytes 294920 | tf_op jit(solution)/shard_map/ppermute | solution.py:28
  115.0 8.9 %collective-permute-start.28 = (bf16[2,1,64,384]{3,2,1,0:T(8,128)(2,1)S(1)}, bf16[2,1,64,384]{3,2,1,0:T(8,128)(2,1)S(1)}, u32[]{:S(2)}, u32[]{:S(2)}) collective-permute-start(bf16[2,1,64,384]{3,2,1,0:T(8,128)(2,1)S(1)} %pad_maximum_fusion.2.refs_8_), channel_id=1, source_target_pairs={{0,1},{1,0},{2,3},{3,2},{4,5},{5,4},{6,7},{7,6},{8,9},{9,8},{10,11... | collective-permute-start | bytes 294920 | tf_op jit(solution)/shard_map/ppermute | solution.py:28
  117.4 6.9 %collective-permute-start.16 = (bf16[2,1,64,384]{3,2,1,0:T(8,128)(2,1)S(1)}, bf16[2,1,64,384]{3,2,1,0:T(8,128)(2,1)S(1)}, u32[]{:S(2)}, u32[]{:S(2)}) collective-permute-start(bf16[2,1,64,384]{3,2,1,0:T(8,128)(2,1)S(1)} %pad_maximum_fusion.1.refs_0_), channel_id=1, source_target_pairs={{0,4},{4,8},{8,12},{12,0},{1,5},{5,9},{9,13},{13,1},{2,6},{6,10},{... | collective-permute-start | bytes 294920 | tf_op jit(solution)/shard_map/ppermute | solution.py:28
  120.1 8.1 %collective-permute-start.18 = (bf16[2,1,64,384]{3,2,1,0:T(8,128)(2,1)S(1)}, bf16[2,1,64,384]{3,2,1,0:T(8,128)(2,1)S(1)}, u32[]{:S(2)}, u32[]{:S(2)}) collective-permute-start(bf16[2,1,64,384]{3,2,1,0:T(8,128)(2,1)S(1)} %pad_maximum_fusion.1.refs_0_), channel_id=1, source_target_pairs={{0,8},{4,12},{8,0},{12,4},{1,9},{5,13},{9,1},{13,5},{2,10},{6,14},... | collective-permute-start | bytes 294920 | tf_op jit(solution)/shard_map/ppermute | solution.py:28
  120.1 8.9 %collective-permute-start.20 = (bf16[2,1,64,384]{3,2,1,0:T(8,128)(2,1)S(1)}, bf16[2,1,64,384]{3,2,1,0:T(8,128)(2,1)S(1)}, u32[]{:S(2)}, u32[]{:S(2)}) collective-permute-start(bf16[2,1,64,384]{3,2,1,0:T(8,128)(2,1)S(1)} %pad_maximum_fusion.1.refs_0_), channel_id=1, source_target_pairs={{0,12},{4,0},{8,4},{12,8},{1,13},{5,1},{9,5},{13,9},{2,14},{6,2},{... | collective-permute-start | bytes 294920 | tf_op jit(solution)/shard_map/ppermute | solution.py:28
  123.9 5.1 %collective-permute-start.15 = (bf16[2,1,64,384]{3,2,1,0:T(8,128)(2,1)S(1)}, bf16[2,1,64,384]{3,2,1,0:T(8,128)(2,1)S(1)}, u32[]{:S(2)}, u32[]{:S(2)}) collective-permute-start(bf16[2,1,64,384]{3,2,1,0:T(8,128)(2,1)S(1)} %pad_maximum_fusion.1.refs_0_), channel_id=1, source_target_pairs={{0,1},{1,0},{2,3},{3,2},{4,5},{5,4},{6,7},{7,6},{8,9},{9,8},{10,11... | collective-permute-start | bytes 294920 | tf_op jit(solution)/shard_map/ppermute | solution.py:28
  124.3 5.2 %collective-permute-start.30 = (bf16[2,1,64,384]{3,2,1,0:T(8,128)(2,1)S(1)}, bf16[2,1,64,384]{3,2,1,0:T(8,128)(2,1)S(1)}, u32[]{:S(2)}, u32[]{:S(2)}) collective-permute-start(bf16[2,1,64,384]{3,2,1,0:T(8,128)(2,1)S(1)} %collective-permute-done.29.refs_10_), channel_id=1, source_target_pairs={{0,1},{1,0},{2,3},{3,2},{4,5},{5,4},{6,7},{7,6},{8,9},{9,8},{10,11... | collective-permute-start | bytes 294920 | tf_op jit(solution)/shard_map/ppermute | solution.py:28
  128.1 1.5 %collective-permute-start.32 = (bf16[2,1,64,384]{3,2,1,0:T(8,128)(2,1)S(1)}, bf16[2,1,64,384]{3,2,1,0:T(8,128)(2,1)S(1)}, u32[]{:S(2)}, u32[]{:S(2)}) collective-permute-start(bf16[2,1,64,384]{3,2,1,0:T(8,128)(2,1)S(1)} %collective-permute-done.31.refs_12_), channel_id=1, source_target_pairs={{0,1},{1,0},{2,3},{3,2},{4,5},{5,4},{6,7},{7,6},{8,9},{9,8},{10,11... | collective-permute-start | bytes 294920 | tf_op jit(solution)/shard_map/ppermute | solution.py:28
  129.0 1.3 collective-permute-start.34
  129.0 1.5 collective-permute-start.17
  129.5 1.3 collective-permute-start.19
  129.6 1.4 collective-permute-start.21
  132.5 5.3 %collective-permute-start.39 = (bf16[1,64,640]{2,1,0:T(8,128)(2,1)S(1)}, bf16[1,64,640]{2,1,0:T(8,128)(2,1)S(1)}, u32[]{:S(2)}, u32[]{:S(2)}) collective-permute-start(bf16[1,64,640]{2,1,0:T(8,128)(2,1)S(1)} %get-tuple-element.56), channel_id=1, source_target_pairs={{0,12},{4,0},{8,4},{12,8},{1,13},{5,1},{9,5},{13,9},{2,14},{6,2},{... | collective-permute-start | bytes 245768 | tf_op jit(solution)/shard_map/ppermute | solution.py:28
  134.9 8.6 %collective-permute-start.41 = (bf16[1,64,640]{2,1,0:T(8,128)(2,1)S(1)}, bf16[1,64,640]{2,1,0:T(8,128)(2,1)S(1)}, u32[]{:S(2)}, u32[]{:S(2)}) collective-permute-start(bf16[1,64,640]{2,1,0:T(8,128)(2,1)S(1)} %get-tuple-element.57), channel_id=1, source_target_pairs={{0,8},{4,12},{8,0},{12,4},{1,9},{5,13},{9,1},{13,5},{2,10},{6,14},... | collective-permute-start | bytes 245768 | tf_op jit(solution)/shard_map/ppermute | solution.py:28
  135.6 8.0 %collective-permute-start.43 = (bf16[1,64,640]{2,1,0:T(8,128)(2,1)S(1)}, bf16[1,64,640]{2,1,0:T(8,128)(2,1)S(1)}, u32[]{:S(2)}, u32[]{:S(2)}) collective-permute-start(bf16[1,64,640]{2,1,0:T(8,128)(2,1)S(1)} %get-tuple-element.58), channel_id=1, source_target_pairs={{0,4},{4,8},{8,12},{12,0},{1,5},{5,9},{9,13},{13,1},{2,6},{6,10},{... | collective-permute-start | bytes 245768 | tf_op jit(solution)/shard_map/ppermute | solution.py:28
  135.6 8.5 %collective-permute-start.38 = (bf16[1,64,640]{2,1,0:T(8,128)(2,1)S(1)}, bf16[1,64,640]{2,1,0:T(8,128)(2,1)S(1)}, u32[]{:S(2)}, u32[]{:S(2)}) collective-permute-start(bf16[1,64,640]{2,1,0:T(8,128)(2,1)S(1)} %get-tuple-element.55), channel_id=1, source_target_pairs={{0,1},{1,0},{2,3},{3,2},{4,5},{5,4},{6,7},{7,6},{8,9},{9,8},{10,11... | collective-permute-start | bytes 245768 | tf_op jit(solution)/shard_map/ppermute | solution.py:28
  137.8 6.2 %collective-permute-start.40 = (bf16[1,64,640]{2,1,0:T(8,128)(2,1)S(1)}, bf16[1,64,640]{2,1,0:T(8,128)(2,1)S(1)}, u32[]{:S(2)}, u32[]{:S(2)}) collective-permute-start(bf16[1,64,640]{2,1,0:T(8,128)(2,1)S(1)} %collective-permute-done.39.refs_2_), channel_id=1, source_target_pairs={{0,1},{1,0},{2,3},{3,2},{4,5},{5,4},{6,7},{7,6},{8,9},{9,8},{10,11... | collective-permute-start | bytes 245768 | tf_op jit(solution)/shard_map/ppermute | solution.py:28
  143.5 1.3 collective-permute-start.42
  143.5 1.4 collective-permute-start.44
  (6 other events, 15.7 us)

commit v6 on v5

--- a/solution.py
+++ b/solution.py
@@ -26,10 +26,6 @@
 def turn(block, axis, distance):
     size = lax.axis_size(axis)
     return lax.ppermute(block, axis, [(i, (i + distance) % size) for i in range(size)])
-
-
-def take(array, index, dim=0):
-    return lax.dynamic_index_in_dim(array, index, dim, keepdims=False)
 
 
 def head_norm(values, gain):
@@ -85,7 +81,7 @@
             bytes_accessed=14 * frames * tokens * cols,
             transcendentals=frames * heads * tokens * tokens,
         ),
-        compiler_params=pltpu.CompilerParams(vmem_limit_bytes=12 << 20),
+        compiler_params=pltpu.CompilerParams(vmem_limit_bytes=6 << 20),
         name="attend",
     )(gain, whole)
 
@@ -128,7 +124,7 @@
         cost_estimate=pl.CostEstimate(
             flops=10 * part * width, bytes_accessed=4 * part * width, transcendentals=0
         ),
-        compiler_params=pltpu.CompilerParams(vmem_limit_bytes=8 << 20),
+        compiler_params=pltpu.CompilerParams(vmem_limit_bytes=4 << 20),
         name="spread",
     )(states)
 
@@ -169,19 +165,54 @@
         cost_estimate=pl.CostEstimate(
             flops=2 * window * freq_rows * wide, bytes_accessed=2 * freq_rows * wide, transcendentals=0
         ),
-        compiler_params=pltpu.CompilerParams(vmem_limit_bytes=12 << 20),
+        compiler_params=pltpu.CompilerParams(vmem_limit_bytes=6 << 20),
         name="time_shares",
     )(start_step, time_proj)
 
 
-def modulate_kernel(n_tm, n_seq, n_mp, step_ref, *refs):
-    shares, rows, (hidden_ref, coef_ref, mod_scr) = refs[:n_tm], refs[n_tm:-3], refs[-3:]
+def load_kernel(n_mp, w_ref, *refs):
+    outs, sems = refs[:-1], refs[-1]
+    copies = []
+    for i, out in enumerate(outs):
+        rows = out.shape[0]
+        share = lax.rem(lax.axis_index("mp") + i, n_mp)
+        source = w_ref.at[pl.ds(pl.multiple_of(share * rows, rows), rows)]
+        copies.append(pltpu.make_async_copy(source, out, sems.at[i]))
+    for copy in copies:
+        copy.start()
+    for copy in copies:
+        copy.wait()
+
+
+def load_out(weights, n_mp):
+    share = jax.ShapeDtypeStruct((weights.shape[0] // n_mp, weights.shape[1]), weights.dtype)
+    return pl.pallas_call(
+        functools.partial(load_kernel, n_mp),
+        in_specs=[pl.BlockSpec(memory_space=pl.ANY)],
+        out_specs=[pl.BlockSpec(memory_space=pltpu.VMEM)] * n_mp,
+        out_shape=[share] * n_mp,
+        scratch_shapes=[pltpu.SemaphoreType.DMA((n_mp,))],
+        cost_estimate=pl.CostEstimate(flops=0, bytes_accessed=2 * weights.size, transcendentals=0),
+        compiler_params=pltpu.CompilerParams(vmem_limit_bytes=8 << 20),
+        name="load_out",
+    )(weights)
+
+
+def modulate_kernel(n_tm, n_seq, n_mp, cuts, step_ref, w_ref, *refs):
+    shares, rows = refs[:n_tm], refs[n_tm : n_tm + n_seq * n_mp]
+    hidden_ref, coef_ref, *w_outs, mod_scr, sems = refs[n_tm + n_seq * n_mp :]
+    copies = [
+        pltpu.make_async_copy(w_ref.at[:, :, pl.ds(lane, size)], out, sems.at[h])
+        for h, ((lane, size), out) in enumerate(zip(cuts, w_outs))
+    ]
     z, k = lax.axis_index("tm"), pl.program_id(0)
     _, frames, part, wide = rows[0].shape
     depth = wide - LANES
 
     @pl.when(k == 0)
     def _():
+        for copy in copies:
+            copy.start()
         total = shares[0][...]
         for share in shares[1:]:
             total = total + share[...]
@@ -203,36 +234,46 @@
                     normed * (1.0 + scale) + shift
                 ).astype(jnp.bfloat16)
 
-
-def modulate(start_step, shares, rows):
+    @pl.when(k == n_tm - 1)
+    def _():
+        for copy in copies:
+            copy.wait()
+
+
+def modulate(start_step, w_qkv, cuts, shares, rows):
     n_tm, n_seq, n_mp = len(shares), len(rows), len(rows[0])
     _, frames, part, wide = rows[0][0].shape
     depth = wide - LANES
     window = shares[0].shape[1]
     shape = (n_tm, n_seq, frames, n_mp * part, depth)
     return pl.pallas_call(
-        functools.partial(modulate_kernel, n_tm, n_seq, n_mp),
+        functools.partial(modulate_kernel, n_tm, n_seq, n_mp, cuts),
         grid=(n_tm,),
-        in_specs=[pl.BlockSpec(memory_space=pltpu.SMEM)]
+        in_specs=[pl.BlockSpec(memory_space=pltpu.SMEM), pl.BlockSpec(memory_space=pl.ANY)]
         + [pl.BlockSpec((3, window, depth), lambda k: (0, 0, 0))] * n_tm
         + [pl.BlockSpec((1, frames, part, wide), lambda k: (k, 0, 0, 0))] * (n_seq * n_mp),
         out_specs=[
             pl.BlockSpec((1,) + shape[1:], lambda k: (k, 0, 0, 0, 0)),
             pl.BlockSpec((1, frames, depth), lambda k: (k, 0, 0)),
+        ]
+        + [pl.BlockSpec(memory_space=pl.ANY)] * len(cuts),
+        scratch_shapes=[
+            pltpu.VMEM((3, window, depth), jnp.float32),
+            pltpu.SemaphoreType.DMA((len(cuts),)),
         ],
-        scratch_shapes=[pltpu.VMEM((3, window, depth), jnp.float32)],
         out_shape=[
             jax.ShapeDtypeStruct(shape, jnp.bfloat16),
             jax.ShapeDtypeStruct((n_tm, frames, depth), jnp.float32),
-        ],
+        ]
+        + [jax.ShapeDtypeStruct(w_qkv.shape[:2] + (size,), w_qkv.dtype) for _, size in cuts],
         cost_estimate=pl.CostEstimate(
             flops=4 * n_tm * n_seq * frames * n_mp * part * depth,
             bytes_accessed=4 * n_tm * n_seq * frames * n_mp * part * depth,
             transcendentals=0,
         ),
-        compiler_params=pltpu.CompilerParams(vmem_limit_bytes=24 << 20),
+        compiler_params=pltpu.CompilerParams(vmem_limit_bytes=8 << 20),
         name="modulate",
-    )(start_step, *shares, *[r for side in rows for r in side])
+    )(start_step, w_qkv, *shares, *[r for side in rows for r in side])
 
 
 def project_kernel(dims, widths, coef_ref, *refs):
@@ -312,7 +353,7 @@
         cost_estimate=pl.CostEstimate(
             flops=2 * rows * deep * half, bytes_accessed=2 * (rows + half) * deep, transcendentals=0
         ),
-        compiler_params=pltpu.CompilerParams(vmem_limit_bytes=32 << 20),
+        compiler_params=pltpu.CompilerParams(vmem_limit_bytes=24 << 20),
         name="project",
     )(coef, *[a for h in attn for k in h for a in k], *[w for j in weights for w in j])
 
@@ -348,7 +389,7 @@
         cost_estimate=pl.CostEstimate(
             flops=0, bytes_accessed=8 * frames * tok * n_tm * half, transcendentals=0
         ),
-        compiler_params=pltpu.CompilerParams(vmem_limit_bytes=8 << 20),
+        compiler_params=pltpu.CompilerParams(vmem_limit_bytes=6 << 20),
         name="finish",
     )(*[b for k in blocks for b in k])
 
@@ -356,10 +397,9 @@
 def sweep(states, start_step, w_qkv, qk_gain, w_out, time_proj):
     frames, tok, _ = states.shape
     n_tm, n_seq, n_mp = (lax.axis_size(name) for name in ("tm", "seq", "mp"))
-    z, m = lax.axis_index("tm"), lax.axis_index("mp")
+    z = lax.axis_index("tm")
     part = tok // n_mp
     depth, cols = w_qkv.shape[1:]
-    half = depth // n_mp
     window = frames * n_tm
 
     raw = list(spread(states, n_tm, part))
@@ -377,23 +417,22 @@
     for k in range(1, n_tm):
         shares[k] = turn(shares[k], "tm", k)
 
-    share = w_out.reshape(n_mp, half, cols)
-    weights = [take(share, m)]
-    weights += [turn(take(share, (m + i) % n_mp), "mp", i) for i in range(1, n_mp)]
+    shares_out = load_out(w_out, n_mp)
+    weights = [turn(share, "mp", i) if i else share for i, share in enumerate(shares_out)]
     weights = [weights]
     for j in range(1, n_seq):
         weights.append([turn(s, "seq", -j) for s in weights[0]])
 
-    hidden, coef = modulate(start_step, shares, rows)
+    groups = head_groups(cols)
+    hidden, coef, *parts_qkv = modulate(start_step, w_qkv, groups, shares, rows)
     hidden = hidden.reshape(n_tm, n_seq * frames * tok, depth)
-    groups = head_groups(cols)
     proj = []
-    for lane, size in groups:
+    for part_qkv in parts_qkv:
         proj.append(
             jnp.einsum(
                 "krd,cdh->kcrh",
                 hidden,
-                w_qkv[:, :, lane : lane + size],
+                part_qkv,
                 preferred_element_type=jnp.float32,
             )
         )

time: 146 us -> 146 us (level)
  local copies, waits for them, and re-layouts: 2.8 us -> 5.32 us
  starting transfers between devices: 41 us -> 39.1 us
  matrix products: 5.7 us -> 3.93 us
    ppermute x6, waiting for transfers between devices: 20 us -> 16.9 us  [sweep(): first = lax.ppermute(first, 'tm', evens)]
    unnamed x18 -> x16, local copies, waits for them, and re-layouts: 2.67 us -> 5.32 us
    ppermute x35, waiting for transfers between devices: 61.1 us -> 63.6 us  [turn(): lax.ppermute(block, axis, [(i, (i + distance) % size) for i in range(size)])]
    ppermute x35, starting transfers between devices: 31.5 us -> 29.2 us  [turn(): lax.ppermute(block, axis, [(i, (i + distance) % size) for i in range(size)])]
    dot_general x2, matrix products: 5.7 us -> 3.93 us  [sweep(): jnp.einsum('krd,cdh->kcrh', hidden, part_qkv, preferred_element_type=jnp....]
  transfers between devices with their start and end apart: 45 -> 45, of which waited for: 26 -> 26; matrix products, arithmetic and copies ran while one was open for 5% -> 6% of each run, Pallas kernels for 2% -> 2%
where the time goes in v6:
time: 146 us
  waiting for transfers between devices  80.5 us (55%)
  starting transfers between devices  39.1 us (27%)
  Pallas kernels  8.05 us (6%)
  other arithmetic  7.72 us (5%)
  local copies, waits for them, and re-layouts  5.32 us (4%)
  matrix products  3.93 us (3%)
    ppermute x35, waiting for transfers between devices, turn(): lax.ppermute(block, axis, [(i, (i + distance) % size) for i in range(size)])  63.6 us
    ppermute x35, starting transfers between devices, turn(): lax.ppermute(block, axis, [(i, (i + distance) % size) for i in range(size)])  29.2 us
    ppermute x6, waiting for transfers between devices, sweep(): first = lax.ppermute(first, 'tm', evens)  16.9 us
    ppermute x6, starting transfers between devices, sweep(): first = lax.ppermute(first, 'tm', evens)  9.96 us
    unnamed x16, local copies, waits for them, and re-layouts  5.32 us
    convert_element_type x4, other arithmetic, sweep(): second = jnp.where(even, left, right).astype(jnp.float16)  4.5 us
    dot_general x2, matrix products, sweep(): jnp.einsum('krd,cdh->kcrh', hidden, part_qkv, preferred_element_type=jnp....  3.93 us
  transfers between devices with their start and end apart: 45, of which 26 were waited for; matrix products, arithmetic and copies ran while one was open for 6% of the time, Pallas kernels for 2%

profile of v6, /device:TPU:0, one launch (start us, length us, event | category | flops | bytes accessed | tf_op | source)
XLA Modules:
  0.0 145.5 jit_solution(3894822333690792576)
XLA Ops:
  0.0 1.1 copy-done.3
  1.5 3.1 %collective-permute-start.3 = (bf16[1,32,1408]{2,1,0:T(8,128)(2,1)S(1)}, bf16[1,32,1408]{2,1,0:T(8,128)(2,1)S(1)}, u32[]{:S(2)}, u32[]{:S(2)}) collective-permute-start(bf16[1,32,1408]{2,1,0:T(8,128)(2,1)S(1)} %get-tuple-element.41), channel_id=1, source_target_pairs={{0,4},{4,8},{8,12},{12,0},{1,5},{5,9},{9,13},{13,1},{2,6},{6,10},{... | collective-permute-start | bytes 270344 | tf_op jit(solution)/shard_map/ppermute | solution.py:28
  4.6 2.6 %collective-permute-start.4 = (bf16[1,32,1408]{2,1,0:T(8,128)(2,1)S(1)}, bf16[1,32,1408]{2,1,0:T(8,128)(2,1)S(1)}, u32[]{:S(2)}, u32[]{:S(2)}) collective-permute-start(bf16[1,32,1408]{2,1,0:T(8,128)(2,1)S(1)} %get-tuple-element.42), channel_id=1, source_target_pairs={{0,8},{4,12},{8,0},{12,4},{1,9},{5,13},{9,1},{13,5},{2,10},{6,14},... | collective-permute-start | bytes 270344 | tf_op jit(solution)/shard_map/ppermute | solution.py:28
  7.2 1.4 collective-permute-start.5
  8.5 1.4 collective-permute-done.3
  9.9 3.3 %collective-permute-done.4 = bf16[1,32,1408]{2,1,0:T(8,128)(2,1)S(1)} collective-permute-done((bf16[1,32,1408]{2,1,0:T(8,128)(2,1)S(1)}, bf16[1,32,1408]{2,1,0:T(8,128)(2,1)S(1)}, u32[]{:S(2)}, u32[]{:S(2)}) %collective-permute-start.4) | collective-permute-done | bytes 90144 | tf_op jit(solution)/shard_map/ppermute | solution.py:28
  13.5 1.6 %collective-permute-start.7 = (bf16[4,1,32,1408]{3,2,1,0:T(8,128)(2,1)S(1)}, bf16[4,1,32,1408]{3,2,1,0:T(8,128)(2,1)S(1)}, u32[]{:S(2)}, u32[]{:S(2)}) collective-permute-start(bf16[4,1,32,1408]{3,2,1,0:T(8,128)(2,1)S(1)} %pad_maximum_fusion.refs_4_), channel_id=1, source_target_pairs={{0,2},{2,0},{1,3},{3,1},{4,6},{6,4},{5,7},{7,5},{8,10},{10,8},{9,1... | collective-permute-start | bytes 1081352 | tf_op jit(solution)/shard_map/ppermute | solution.py:28
  15.0 8.6 %collective-permute-done.7.refs_6_ = bf16[4,1,32,1408]{3,2,1,0:T(8,128)(2,1)S(1)} collective-permute-done((bf16[4,1,32,1408]{3,2,1,0:T(8,128)(2,1)S(1)}, bf16[4,1,32,1408]{3,2,1,0:T(8,128)(2,1)S(1)}, u32[]{:S(2)}, u32[]{:S(2)}) %collective-permute-start.7) | collective-permute-done | bytes 360480 | tf_op jit(solution)/shard_map/ppermute | solution.py:28
  24.3 1.5 %copy-done.1 = bf16[64,15360]{1,0:T(8,128)(2,1)S(1)} copy-done((bf16[64,15360]{1,0:T(8,128)(2,1)S(1)}, bf16[64,15360]{1,0:T(8,128)(2,1)}, u32[]{:S(2)}) %copy-start.1) | copy-done | bytes 1966104
  26.6 2.6 %collective-permute-start = (f32[3,4,1280]{2,1,0:T(4,128)S(1)}, f32[3,4,1280]{2,1,0:T(4,128)S(1)}, u32[]{:S(2)}, u32[]{:S(2)}) collective-permute-start(f32[3,4,1280]{2,1,0:T(4,128)S(1)} %get-tuple-element.37), channel_id=1, source_target_pairs={{0,4},{4,8},{8,12},{12,0},{1,5},{5,9},{9,13},{13,1},{2,6},{6,10},{... | collective-permute-start | bytes 184328 | tf_op jit(solution)/shard_map/ppermute | solution.py:28
  29.7 1.9 %collective-permute-start.2 = (f32[3,4,1280]{2,1,0:T(4,128)S(1)}, f32[3,4,1280]{2,1,0:T(4,128)S(1)}, u32[]{:S(2)}, u32[]{:S(2)}) collective-permute-start(f32[3,4,1280]{2,1,0:T(4,128)S(1)} %get-tuple-element.39), channel_id=1, source_target_pairs={{0,12},{4,0},{8,4},{12,8},{1,13},{5,1},{9,5},{13,9},{2,14},{6,2},{... | collective-permute-start | bytes 184328 | tf_op jit(solution)/shard_map/ppermute | solution.py:28
  31.6 1.5 %collective-permute-done.refs_1_ = f32[3,4,1280]{2,1,0:T(4,128)S(1)} collective-permute-done((f32[3,4,1280]{2,1,0:T(4,128)S(1)}, f32[3,4,1280]{2,1,0:T(4,128)S(1)}, u32[]{:S(2)}, u32[]{:S(2)}) %collective-permute-start) | collective-permute-done | bytes 61472 | tf_op jit(solution)/shard_map/ppermute | solution.py:28
  33.1 2.5 %collective-permute-done.1.refs_2_ = f32[3,4,1280]{2,1,0:T(4,128)S(1)} collective-permute-done((f32[3,4,1280]{2,1,0:T(4,128)S(1)}, f32[3,4,1280]{2,1,0:T(4,128)S(1)}, u32[]{:S(2)}, u32[]{:S(2)}) %collective-permute-start.1) | collective-permute-done | bytes 61472 | tf_op jit(solution)/shard_map/ppermute | solution.py:28
  35.6 2.7 %copy-done = bf16[3,1280,768]{2,1,0:T(8,128)(2,1)S(1)} copy-done((bf16[3,1280,768]{2,1,0:T(8,128)(2,1)S(1)}, bf16[3,1280,768]{2,1,0:T(8,128)(2,1)}, u32[]{:S(2)}) %copy-start) | copy-done | bytes 5898264
  38.3 1.7 %modulate.1 = (bf16[4,2,1,64,1280]{4,3,2,1,0:T(8,128)(2,1)S(1)}, f32[4,1,1280]{2,1,0:T(1,128)S(1)}, bf16[3,1280,384]{2,1,0:T(8,128)(2,1)S(1)}, bf16[3,1280,384]{2,1,0:T(8,128)(2,1)S(1)}) custom-call(s32[1]{0:T(128)S(6)} %copy.17.step_ref, bf16[3,1280,768]{2,1,0:T(8,128)(2,1)S(1)} %copy-done, f32[3,4,1280]{2,1,0:T(4,128)S(1)} %get-tuple-element.36.refs_0_, ...), custom_call_target="tpu_custom_call" | custom-call | flops 2621440 | bytes 2621440 | tf_op jit(solution)/shard_map/modulate/pallas_call | solution.py:249
  40.0 2.0 %fusion.4 = f32[4,3,128,384]{3,2,1,0:T(8,128)S(1)} fusion(bf16[4,128,1280,1]{2,1,3,0:T(8,128)(2,1)S(1)} %bitcast.120, bf16[3,1280,384]{2,1,0:T(8,128)(2,1)S(1)} %get-tuple-element.53), kind=kOutput, calls=%fused_computation.4 | convolution fusion | flops 1509949440 | bytes 6619136 | tf_op jit(solution)/shard_map/krd,cdh->kcrh/dot_general | solution.py:432
  42.9 1.8 %collective-permute-start.22 = (f16[3,128,384]{2,1,0:T(8,128)(2,1)}, f16[3,128,384]{2,1,0:T(8,128)(2,1)}, u32[]{:S(2)}, u32[]{:S(2)}) collective-permute-start(f16[3,128,384]{2,1,0:T(8,128)(2,1)} %select_convert_fusion.4), channel_id=1, source_target_pairs={{0,4},{4,0},{8,12},{12,8},{1,5},{5,1},{9,13},{13,9},{2,6},{6,2},{1... | collective-permute-start | bytes 884744 | tf_op jit(solution)/shard_map/ppermute | solution.py:463
  44.7 2.0 %fusion.7 = f32[4,3,128,384]{3,2,0,1:T(8,128)S(1)} fusion(bf16[4,128,1280,1]{2,1,0,3:T(8,128)(2,1)S(1)} %bitcast.121, bf16[3,1280,384]{2,1,0:T(8,128)(2,1)S(1)} %get-tuple-element.45), kind=kOutput, calls=%fused_computation.5 | convolution fusion | flops 1509949440 | bytes 6619136 | tf_op jit(solution)/shard_map/krd,cdh->kcrh/dot_general | solution.py:432
  48.9 4.1 %collective-permute-done.22 = f16[3,128,384]{2,1,0:T(8,128)(2,1)} collective-permute-done((f16[3,128,384]{2,1,0:T(8,128)(2,1)}, f16[3,128,384]{2,1,0:T(8,128)(2,1)}, u32[]{:S(2)}, u32[]{:S(2)}) %collective-permute-start.22) | collective-permute-done | bytes 294944 | tf_op jit(solution)/shard_map/ppermute | solution.py:463
  53.1 1.4 select_convert_fusion.2
  54.5 1.9 %collective-permute-start.23 = (f16[3,128,384]{2,1,0:T(8,128)(2,1)S(1)}, f16[3,128,384]{2,1,0:T(8,128)(2,1)S(1)}, u32[]{:S(2)}, u32[]{:S(2)}) collective-permute-start(f16[3,128,384]{2,1,0:T(8,128)(2,1)S(1)} %get-tuple-element.72), channel_id=1, source_target_pairs={{0,4},{4,0},{8,12},{12,8},{1,5},{5,1},{9,13},{13,9},{2,6},{6,2},{1... | collective-permute-start | bytes 884744 | tf_op jit(solution)/shard_map/ppermute | solution.py:463
  56.4 2.9 %collective-permute-done.9 = f16[3,128,384]{2,1,0:T(8,128)(2,1)S(1)} collective-permute-done((f16[3,128,384]{2,1,0:T(8,128)(2,1)}, f16[3,128,384]{2,1,0:T(8,128)(2,1)S(1)}, u32[]{:S(2)}, u32[]{:S(2)}) %collective-permute-start.9) | collective-permute-done | bytes 294944 | tf_op jit(solution)/shard_map/ppermute | solution.py:463
  59.3 1.3 select_convert_fusion.7
  60.6 1.9 %collective-permute-start.10 = (f16[3,128,384]{2,1,0:T(8,128)(2,1)S(1)}, f16[3,128,384]{2,1,0:T(8,128)(2,1)S(1)}, u32[]{:S(2)}, u32[]{:S(2)}) collective-permute-start(f16[3,128,384]{2,1,0:T(8,128)(2,1)S(1)} %get-tuple-element.74), channel_id=1, source_target_pairs={{0,4},{4,0},{8,12},{12,8},{1,5},{5,1},{9,13},{13,9},{2,6},{6,2},{1... | collective-permute-start | bytes 884744 | tf_op jit(solution)/shard_map/ppermute | solution.py:463
  62.5 3.1 %collective-permute-done.23 = f16[3,128,384]{2,1,0:T(8,128)(2,1)S(1)} collective-permute-done((f16[3,128,384]{2,1,0:T(8,128)(2,1)S(1)}, f16[3,128,384]{2,1,0:T(8,128)(2,1)S(1)}, u32[]{:S(2)}, u32[]{:S(2)}) %collective-permute-start.23) | collective-permute-done | bytes 294944 | tf_op jit(solution)/shard_map/ppermute | solution.py:463
  65.6 1.5 %collective-permute-start.36 = (bf16[640,768]{1,0:T(8,128)(2,1)S(1)}, bf16[640,768]{1,0:T(8,128)(2,1)S(1)}, u32[]{:S(2)}, u32[]{:S(2)}) collective-permute-start(bf16[640,768]{1,0:T(8,128)(2,1)S(1)} %get-tuple-element.60.refs_16_), channel_id=1, source_target_pairs={{0,2},{2,0},{1,3},{3,1},{4,6},{6,4},{5,7},{7,5},{8,10},{10,8},{9,1... | collective-permute-start | bytes 2949128 | tf_op jit(solution)/shard_map/ppermute | solution.py:28
  67.1 1.5 %select_convert_fusion = (f16[3,128,384]{2,1,0:T(8,128)(2,1)S(1)}, f16[3,128,384]{2,1,0:T(8,128)(2,1)S(1)}) fusion(pred[]{:T(512)S(6)} %eq.5, f16[3,128,384]{2,1,0:T(8,128)(2,1)S(1)} %collective-permute-done.24, f16[3,128,384]{2,1,0:T(8,128)(2,1)S(1)} %collective-permute-done.23, pred[]{:T(512)S(6)} %lt.9, f32[4,3,128,384]{3,2,1,0:T(8,128)} %copy-done.6, ...), kind=kLoop, calls=%fused_computation.50 | loop fusion | flops 1769472 | bytes 2359299 | tf_op jit(solution)/shard_map/convert_element_type | solution.py:462
  68.6 1.9 %collective-permute-start.25 = (f16[3,128,384]{2,1,0:T(8,128)(2,1)S(1)}, f16[3,128,384]{2,1,0:T(8,128)(2,1)S(1)}, u32[]{:S(2)}, u32[]{:S(2)}) collective-permute-start(f16[3,128,384]{2,1,0:T(8,128)(2,1)S(1)} %get-tuple-element.68), channel_id=1, source_target_pairs={{0,4},{4,0},{8,12},{12,8},{1,5},{5,1},{9,13},{13,9},{2,6},{6,2},{1... | collective-permute-start | bytes 884744 | tf_op jit(solution)/shard_map/ppermute | solution.py:463
  70.5 1.4 collective-permute-done.10
  72.2 1.9 %collective-permute-start.12 = (f16[3,128,384]{2,1,0:T(8,128)(2,1)S(1)}, f16[3,128,384]{2,1,0:T(8,128)(2,1)S(1)}, u32[]{:S(2)}, u32[]{:S(2)}) collective-permute-start(f16[3,128,384]{2,1,0:T(8,128)(2,1)S(1)} %get-tuple-element.70), channel_id=1, source_target_pairs={{0,4},{4,0},{8,12},{12,8},{1,5},{5,1},{9,13},{13,9},{2,6},{6,2},{1... | collective-permute-start | bytes 884744 | tf_op jit(solution)/shard_map/ppermute | solution.py:463
  74.1 4.5 %collective-permute-done.25 = f16[3,128,384]{2,1,0:T(8,128)(2,1)S(1)} collective-permute-done((f16[3,128,384]{2,1,0:T(8,128)(2,1)S(1)}, f16[3,128,384]{2,1,0:T(8,128)(2,1)S(1)}, u32[]{:S(2)}, u32[]{:S(2)}) %collective-permute-start.25) | collective-permute-done | bytes 294944 | tf_op jit(solution)/shard_map/ppermute | solution.py:463
  78.6 1.2 collective-permute-start.37
  79.7 1.2 fusion.32
  83.9 0.9 attend.2
  84.8 1.5 %collective-permute-start.14 = (bf16[1,64,384]{2,1,0:T(8,128)(2,1)S(1)}, bf16[1,64,384]{2,1,0:T(8,128)(2,1)S(1)}, u32[]{:S(2)}, u32[]{:S(2)}) collective-permute-start(bf16[1,64,384]{2,1,0:T(8,128)(2,1)S(1)} %get-tuple-element.52), channel_id=1, source_target_pairs={{0,2},{2,0},{1,3},{3,1},{4,6},{6,4},{5,7},{7,5},{8,10},{10,8},{9,1... | collective-permute-start | bytes 147464 | tf_op jit(solution)/shard_map/ppermute | solution.py:28
  86.4 23.9 %collective-permute-done.27 = bf16[1,64,384]{2,1,0:T(8,128)(2,1)S(1)} collective-permute-done((bf16[1,64,384]{2,1,0:T(8,128)(2,1)S(1)}, bf16[1,64,384]{2,1,0:T(8,128)(2,1)S(1)}, u32[]{:S(2)}, u32[]{:S(2)}) %collective-permute-start.27) | collective-permute-done | bytes 49184 | tf_op jit(solution)/shard_map/ppermute | solution.py:28
  110.3 1.7 %collective-permute-start.29 = (bf16[2,1,64,384]{3,2,1,0:T(8,128)(2,1)S(1)}, bf16[2,1,64,384]{3,2,1,0:T(8,128)(2,1)S(1)}, u32[]{:S(2)}, u32[]{:S(2)}) collective-permute-start(bf16[2,1,64,384]{3,2,1,0:T(8,128)(2,1)S(1)} %pad_maximum_fusion.2.refs_8_), channel_id=1, source_target_pairs={{0,4},{4,8},{8,12},{12,0},{1,5},{5,9},{9,13},{13,1},{2,6},{6,10},{... | collective-permute-start | bytes 294920 | tf_op jit(solution)/shard_map/ppermute | solution.py:28
  112.4 2.1 %collective-permute-start.33 = (bf16[2,1,64,384]{3,2,1,0:T(8,128)(2,1)S(1)}, bf16[2,1,64,384]{3,2,1,0:T(8,128)(2,1)S(1)}, u32[]{:S(2)}, u32[]{:S(2)}) collective-permute-start(bf16[2,1,64,384]{3,2,1,0:T(8,128)(2,1)S(1)} %pad_maximum_fusion.2.refs_8_), channel_id=1, source_target_pairs={{0,12},{4,0},{8,4},{12,8},{1,13},{5,1},{9,5},{13,9},{2,14},{6,2},{... | collective-permute-start | bytes 294920 | tf_op jit(solution)/shard_map/ppermute | solution.py:28
  114.6 2.4 %collective-permute-done.29.refs_10_ = bf16[2,1,64,384]{3,2,1,0:T(8,128)(2,1)S(1)} collective-permute-done((bf16[2,1,64,384]{3,2,1,0:T(8,128)(2,1)S(1)}, bf16[2,1,64,384]{3,2,1,0:T(8,128)(2,1)S(1)}, u32[]{:S(2)}, u32[]{:S(2)}) %collective-permute-start.29) | collective-permute-done | bytes 98336 | tf_op jit(solution)/shard_map/ppermute | solution.py:28
  117.0 4.8 %collective-permute-done.31.refs_12_ = bf16[2,1,64,384]{3,2,1,0:T(8,128)(2,1)S(1)} collective-permute-done((bf16[2,1,64,384]{3,2,1,0:T(8,128)(2,1)S(1)}, bf16[2,1,64,384]{3,2,1,0:T(8,128)(2,1)S(1)}, u32[]{:S(2)}, u32[]{:S(2)}) %collective-permute-start.31) | collective-permute-done | bytes 98336 | tf_op jit(solution)/shard_map/ppermute | solution.py:28
  121.7 1.6 %collective-permute-start.20 = (bf16[2,1,64,384]{3,2,1,0:T(8,128)(2,1)S(1)}, bf16[2,1,64,384]{3,2,1,0:T(8,128)(2,1)S(1)}, u32[]{:S(2)}, u32[]{:S(2)}) collective-permute-start(bf16[2,1,64,384]{3,2,1,0:T(8,128)(2,1)S(1)} %pad_maximum_fusion.1.refs_0_), channel_id=1, source_target_pairs={{0,12},{4,0},{8,4},{12,8},{1,13},{5,1},{9,5},{13,9},{2,14},{6,2},{... | collective-permute-start | bytes 294920 | tf_op jit(solution)/shard_map/ppermute | solution.py:28
  123.9 3.8 %collective-permute-done.18.refs_4_ = bf16[2,1,64,384]{3,2,1,0:T(8,128)(2,1)S(1)} collective-permute-done((bf16[2,1,64,384]{3,2,1,0:T(8,128)(2,1)S(1)}, bf16[2,1,64,384]{3,2,1,0:T(8,128)(2,1)S(1)}, u32[]{:S(2)}, u32[]{:S(2)}) %collective-permute-start.18) | collective-permute-done | bytes 98336 | tf_op jit(solution)/shard_map/ppermute | solution.py:28
  127.6 1.0 collective-permute-done.20.refs_6_
  130.6 1.5 %project.1 = (f32[1,64,640]{2,1,0:T(8,128)S(1)}, bf16[1,64,640]{2,1,0:T(8,128)(2,1)S(1)}, bf16[1,64,640]{2,1,0:T(8,128)(2,1)S(1)}, bf16[1,64,640]{2,1,0:T(8,128)(2,1)S(1)}, bf16[1,64,640]{2,1,0:T(8,128)(2,1)S(1)}) custom-call(f32[4,1,1280]{2,1,0:T(1,128)S(1)} %get-tuple-element.44.coef_ref, bf16[2,1,64,384]{3,2,1,0:T(8,128)(2,1)S(1)} %pad_maximum_fusion.1.refs_0_, ...), custom_call_target="tpu_custom_call" | custom-call | flops 1006632960 | bytes 5505024 | tf_op jit(solution)/shard_map/project/pallas_call | solution.py:343
  132.2 2.3 %collective-permute-start.39 = (bf16[1,64,640]{2,1,0:T(8,128)(2,1)S(1)}, bf16[1,64,640]{2,1,0:T(8,128)(2,1)S(1)}, u32[]{:S(2)}, u32[]{:S(2)}) collective-permute-start(bf16[1,64,640]{2,1,0:T(8,128)(2,1)S(1)} %get-tuple-element.64), channel_id=1, source_target_pairs={{0,12},{4,0},{8,4},{12,8},{1,13},{5,1},{9,5},{13,9},{2,14},{6,2},{... | collective-permute-start | bytes 245768 | tf_op jit(solution)/shard_map/ppermute | solution.py:28
  135.1 2.2 %collective-permute-done.39.refs_2_ = bf16[1,64,640]{2,1,0:T(8,128)(2,1)S(1)} collective-permute-done((bf16[1,64,640]{2,1,0:T(8,128)(2,1)S(1)}, bf16[1,64,640]{2,1,0:T(8,128)(2,1)S(1)}, u32[]{:S(2)}, u32[]{:S(2)}) %collective-permute-start.39) | collective-permute-done | bytes 81952 | tf_op jit(solution)/shard_map/ppermute | solution.py:28
  137.3 5.7 %collective-permute-done.41.refs_4_ = bf16[1,64,640]{2,1,0:T(8,128)(2,1)S(1)} collective-permute-done((bf16[1,64,640]{2,1,0:T(8,128)(2,1)S(1)}, bf16[1,64,640]{2,1,0:T(8,128)(2,1)S(1)}, u32[]{:S(2)}, u32[]{:S(2)}) %collective-permute-start.41) | collective-permute-done | bytes 81952 | tf_op jit(solution)/shard_map/ppermute | solution.py:28
  144.5 1.0 finish.1
  (80 shorter events, 13.3 us)
Async XLA Ops:
  1.5 8.4 %collective-permute-start.3 = (bf16[1,32,1408]{2,1,0:T(8,128)(2,1)S(1)}, bf16[1,32,1408]{2,1,0:T(8,128)(2,1)S(1)}, u32[]{:S(2)}, u32[]{:S(2)}) collective-permute-start(bf16[1,32,1408]{2,1,0:T(8,128)(2,1)S(1)} %get-tuple-element.41), channel_id=1, source_target_pairs={{0,4},{4,8},{8,12},{12,0},{1,5},{5,9},{9,13},{13,1},{2,6},{6,10},{... | collective-permute-start | bytes 270344 | tf_op jit(solution)/shard_map/ppermute | solution.py:28
  4.6 8.6 %collective-permute-start.4 = (bf16[1,32,1408]{2,1,0:T(8,128)(2,1)S(1)}, bf16[1,32,1408]{2,1,0:T(8,128)(2,1)S(1)}, u32[]{:S(2)}, u32[]{:S(2)}) collective-permute-start(bf16[1,32,1408]{2,1,0:T(8,128)(2,1)S(1)} %get-tuple-element.42), channel_id=1, source_target_pairs={{0,8},{4,12},{8,0},{12,4},{1,9},{5,13},{9,1},{13,5},{2,10},{6,14},... | collective-permute-start | bytes 270344 | tf_op jit(solution)/shard_map/ppermute | solution.py:28
  7.2 6.3 %collective-permute-start.5 = (bf16[1,32,1408]{2,1,0:T(8,128)(2,1)S(1)}, bf16[1,32,1408]{2,1,0:T(8,128)(2,1)S(1)}, u32[]{:S(2)}, u32[]{:S(2)}) collective-permute-start(bf16[1,32,1408]{2,1,0:T(8,128)(2,1)S(1)} %get-tuple-element.43), channel_id=1, source_target_pairs={{0,12},{4,0},{8,4},{12,8},{1,13},{5,1},{9,5},{13,9},{2,14},{6,2},{... | collective-permute-start | bytes 270344 | tf_op jit(solution)/shard_map/ppermute | solution.py:28
  13.5 10.1 %collective-permute-start.7 = (bf16[4,1,32,1408]{3,2,1,0:T(8,128)(2,1)S(1)}, bf16[4,1,32,1408]{3,2,1,0:T(8,128)(2,1)S(1)}, u32[]{:S(2)}, u32[]{:S(2)}) collective-permute-start(bf16[4,1,32,1408]{3,2,1,0:T(8,128)(2,1)S(1)} %pad_maximum_fusion.refs_4_), channel_id=1, source_target_pairs={{0,2},{2,0},{1,3},{3,1},{4,6},{6,4},{5,7},{7,5},{8,10},{10,8},{9,1... | collective-permute-start | bytes 1081352 | tf_op jit(solution)/shard_map/ppermute | solution.py:28
  15.0 20.6 %collective-permute-start.6 = (bf16[4,1,32,1408]{3,2,1,0:T(8,128)(2,1)S(1)}, bf16[4,1,32,1408]{3,2,1,0:T(8,128)(2,1)S(1)}, u32[]{:S(2)}, u32[]{:S(2)}) collective-permute-start(bf16[4,1,32,1408]{3,2,1,0:T(8,128)(2,1)S(1)} %pad_maximum_fusion.refs_4_), channel_id=1, source_target_pairs={{0,1},{1,0},{2,3},{3,2},{4,5},{5,4},{6,7},{7,6},{8,9},{9,8},{10,11... | collective-permute-start | bytes 1081352 | tf_op jit(solution)/shard_map/ppermute | solution.py:28
  23.6 12.0 %collective-permute-start.8 = (bf16[4,1,32,1408]{3,2,1,0:T(8,128)(2,1)S(1)}, bf16[4,1,32,1408]{3,2,1,0:T(8,128)(2,1)S(1)}, u32[]{:S(2)}, u32[]{:S(2)}) collective-permute-start(bf16[4,1,32,1408]{3,2,1,0:T(8,128)(2,1)S(1)} %collective-permute-done.7.refs_6_), channel_id=1, source_target_pairs={{0,1},{1,0},{2,3},{3,2},{4,5},{5,4},{6,7},{7,6},{8,9},{9,8},{10,11... | collective-permute-start | bytes 1081352 | tf_op jit(solution)/shard_map/ppermute | solution.py:28
  26.6 6.5 %collective-permute-start = (f32[3,4,1280]{2,1,0:T(4,128)S(1)}, f32[3,4,1280]{2,1,0:T(4,128)S(1)}, u32[]{:S(2)}, u32[]{:S(2)}) collective-permute-start(f32[3,4,1280]{2,1,0:T(4,128)S(1)} %get-tuple-element.37), channel_id=1, source_target_pairs={{0,4},{4,8},{8,12},{12,0},{1,5},{5,9},{9,13},{13,1},{2,6},{6,10},{... | collective-permute-start | bytes 184328 | tf_op jit(solution)/shard_map/ppermute | solution.py:28
  29.2 6.4 %collective-permute-start.1 = (f32[3,4,1280]{2,1,0:T(4,128)S(1)}, f32[3,4,1280]{2,1,0:T(4,128)S(1)}, u32[]{:S(2)}, u32[]{:S(2)}) collective-permute-start(f32[3,4,1280]{2,1,0:T(4,128)S(1)} %get-tuple-element.38), channel_id=1, source_target_pairs={{0,8},{4,12},{8,0},{12,4},{1,9},{5,13},{9,1},{13,5},{2,10},{6,14},... | collective-permute-start | bytes 184328 | tf_op jit(solution)/shard_map/ppermute | solution.py:28
  29.7 5.9 %collective-permute-start.2 = (f32[3,4,1280]{2,1,0:T(4,128)S(1)}, f32[3,4,1280]{2,1,0:T(4,128)S(1)}, u32[]{:S(2)}, u32[]{:S(2)}) collective-permute-start(f32[3,4,1280]{2,1,0:T(4,128)S(1)} %get-tuple-element.39), channel_id=1, source_target_pairs={{0,12},{4,0},{8,4},{12,8},{1,13},{5,1},{9,5},{13,9},{2,14},{6,2},{... | collective-permute-start | bytes 184328 | tf_op jit(solution)/shard_map/ppermute | solution.py:28
  42.9 10.2 %collective-permute-start.22 = (f16[3,128,384]{2,1,0:T(8,128)(2,1)}, f16[3,128,384]{2,1,0:T(8,128)(2,1)}, u32[]{:S(2)}, u32[]{:S(2)}) collective-permute-start(f16[3,128,384]{2,1,0:T(8,128)(2,1)} %select_convert_fusion.4), channel_id=1, source_target_pairs={{0,4},{4,0},{8,12},{12,8},{1,5},{5,1},{9,13},{13,9},{2,6},{6,2},{1... | collective-permute-start | bytes 884744 | tf_op jit(solution)/shard_map/ppermute | solution.py:463
  44.7 3.5 %copy-start.2 = (bf16[1280,768]{1,0:T(8,128)(2,1)S(1)}, bf16[1280,768]{1,0:T(8,128)(2,1)}, u32[]{:S(2)}) copy-start(bf16[1280,768]{1,0:T(8,128)(2,1)} %w_ref.3) | copy-start | bytes 5898244
  47.6 11.7 %collective-permute-start.9 = (f16[3,128,384]{2,1,0:T(8,128)(2,1)}, f16[3,128,384]{2,1,0:T(8,128)(2,1)S(1)}, u32[]{:S(2)}, u32[]{:S(2)}) collective-permute-start(f16[3,128,384]{2,1,0:T(8,128)(2,1)} %select_convert_fusion.9), channel_id=1, source_target_pairs={{0,4},{4,0},{8,12},{12,8},{1,5},{5,1},{9,13},{13,9},{2,6},{6,2},{1... | collective-permute-start | bytes 884744 | tf_op jit(solution)/shard_map/ppermute | solution.py:463
  48.8 25.2 %collective-permute-start.35 = (bf16[640,768]{1,0:T(8,128)(2,1)S(1)}, bf16[640,768]{1,0:T(8,128)(2,1)S(1)}, u32[]{:S(2)}, u32[]{:S(2)}) collective-permute-start(bf16[640,768]{1,0:T(8,128)(2,1)S(1)} %get-tuple-element.61), channel_id=1, source_target_pairs={{0,1},{1,0},{2,3},{3,2},{4,5},{5,4},{6,7},{7,6},{8,9},{9,8},{10,11... | collective-permute-start | bytes 2949128 | tf_op jit(solution)/shard_map/ppermute | solution.py:28
  48.9 23.0 %copy-start.5 = (f32[4,3,128,384]{3,2,0,1:T(8,128)S(1)}, f32[4,3,128,384]{3,2,0,1:T(8,128)}, u32[]{:S(2)}) copy-start(f32[4,3,128,384]{3,2,0,1:T(8,128)} %copy-done.4) | copy-start | bytes 7077892
  54.5 11.1 %collective-permute-start.23 = (f16[3,128,384]{2,1,0:T(8,128)(2,1)S(1)}, f16[3,128,384]{2,1,0:T(8,128)(2,1)S(1)}, u32[]{:S(2)}, u32[]{:S(2)}) collective-permute-start(f16[3,128,384]{2,1,0:T(8,128)(2,1)S(1)} %get-tuple-element.72), channel_id=1, source_target_pairs={{0,4},{4,0},{8,12},{12,8},{1,5},{5,1},{9,13},{13,9},{2,6},{6,2},{1... | collective-permute-start | bytes 884744 | tf_op jit(solution)/shard_map/ppermute | solution.py:463
  56.4 10.7 %collective-permute-start.24 = (f16[3,128,384]{2,1,0:T(8,128)(2,1)S(1)}, f16[3,128,384]{2,1,0:T(8,128)(2,1)S(1)}, u32[]{:S(2)}, u32[]{:S(2)}) collective-permute-start(f16[3,128,384]{2,1,0:T(8,128)(2,1)S(1)} %get-tuple-element.71), channel_id=1, source_target_pairs={{0,1},{1,0},{4,8},{5,9},{8,4},{9,5},{12,13},{13,12},{2,3},{3,2},{6... | collective-permute-start | bytes 884744 | tf_op jit(solution)/shard_map/ppermute | solution.py:465
  60.6 11.3 %collective-permute-start.10 = (f16[3,128,384]{2,1,0:T(8,128)(2,1)S(1)}, f16[3,128,384]{2,1,0:T(8,128)(2,1)S(1)}, u32[]{:S(2)}, u32[]{:S(2)}) collective-permute-start(f16[3,128,384]{2,1,0:T(8,128)(2,1)S(1)} %get-tuple-element.74), channel_id=1, source_target_pairs={{0,4},{4,0},{8,12},{12,8},{1,5},{5,1},{9,13},{13,9},{2,6},{6,2},{1... | collective-permute-start | bytes 884744 | tf_op jit(solution)/shard_map/ppermute | solution.py:463
  62.5 9.5 %collective-permute-start.11 = (f16[3,128,384]{2,1,0:T(8,128)(2,1)S(1)}, f16[3,128,384]{2,1,0:T(8,128)(2,1)S(1)}, u32[]{:S(2)}, u32[]{:S(2)}) collective-permute-start(f16[3,128,384]{2,1,0:T(8,128)(2,1)S(1)} %get-tuple-element.73), channel_id=1, source_target_pairs={{0,1},{1,0},{4,8},{5,9},{8,4},{9,5},{12,13},{13,12},{2,3},{3,2},{6... | collective-permute-start | bytes 884744 | tf_op jit(solution)/shard_map/ppermute | solution.py:465
  65.6 8.5 %copy-start.7 = (f32[2,768]{1,0:T(2,128)S(1)}, f32[2,768]{1,0:T(2,128)}, u32[]{:S(2)}) copy-start(f32[2,768]{1,0:T(2,128)} %param.9) | copy-start | bytes 18436
  65.6 48.9 %collective-permute-start.36 = (bf16[640,768]{1,0:T(8,128)(2,1)S(1)}, bf16[640,768]{1,0:T(8,128)(2,1)S(1)}, u32[]{:S(2)}, u32[]{:S(2)}) collective-permute-start(bf16[640,768]{1,0:T(8,128)(2,1)S(1)} %get-tuple-element.60.refs_16_), channel_id=1, source_target_pairs={{0,2},{2,0},{1,3},{3,1},{4,6},{6,4},{5,7},{7,5},{8,10},{10,8},{9,1... | collective-permute-start | bytes 2949128 | tf_op jit(solution)/shard_map/ppermute | solution.py:28
  68.6 9.9 %collective-permute-start.25 = (f16[3,128,384]{2,1,0:T(8,128)(2,1)S(1)}, f16[3,128,384]{2,1,0:T(8,128)(2,1)S(1)}, u32[]{:S(2)}, u32[]{:S(2)}) collective-permute-start(f16[3,128,384]{2,1,0:T(8,128)(2,1)S(1)} %get-tuple-element.68), channel_id=1, source_target_pairs={{0,4},{4,0},{8,12},{12,8},{1,5},{5,1},{9,13},{13,9},{2,6},{6,2},{1... | collective-permute-start | bytes 884744 | tf_op jit(solution)/shard_map/ppermute | solution.py:463
  71.9 7.8 %collective-permute-start.26 = (f16[3,128,384]{2,1,0:T(8,128)(2,1)S(1)}, f16[3,128,384]{2,1,0:T(8,128)(2,1)S(1)}, u32[]{:S(2)}, u32[]{:S(2)}) collective-permute-start(f16[3,128,384]{2,1,0:T(8,128)(2,1)S(1)} %get-tuple-element.67), channel_id=1, source_target_pairs={{0,1},{1,0},{4,8},{5,9},{8,4},{9,5},{12,13},{13,12},{2,3},{3,2},{6... | collective-permute-start | bytes 884744 | tf_op jit(solution)/shard_map/ppermute | solution.py:465
  72.2 11.5 %collective-permute-start.12 = (f16[3,128,384]{2,1,0:T(8,128)(2,1)S(1)}, f16[3,128,384]{2,1,0:T(8,128)(2,1)S(1)}, u32[]{:S(2)}, u32[]{:S(2)}) collective-permute-start(f16[3,128,384]{2,1,0:T(8,128)(2,1)S(1)} %get-tuple-element.70), channel_id=1, source_target_pairs={{0,4},{4,0},{8,12},{12,8},{1,5},{5,1},{9,13},{13,9},{2,6},{6,2},{1... | collective-permute-start | bytes 884744 | tf_op jit(solution)/shard_map/ppermute | solution.py:463
  74.1 9.6 %collective-permute-start.13 = (f16[3,128,384]{2,1,0:T(8,128)(2,1)S(1)}, f16[3,128,384]{2,1,0:T(8,128)(2,1)S(1)}, u32[]{:S(2)}, u32[]{:S(2)}) collective-permute-start(f16[3,128,384]{2,1,0:T(8,128)(2,1)S(1)} %get-tuple-element.69), channel_id=1, source_target_pairs={{0,1},{1,0},{4,8},{5,9},{8,4},{9,5},{12,13},{13,12},{2,3},{3,2},{6... | collective-permute-start | bytes 884744 | tf_op jit(solution)/shard_map/ppermute | solution.py:465
  78.6 52.0 %collective-permute-start.37 = (bf16[640,768]{1,0:T(8,128)(2,1)S(1)}, bf16[640,768]{1,0:T(8,128)(2,1)S(1)}, u32[]{:S(2)}, u32[]{:S(2)}) collective-permute-start(bf16[640,768]{1,0:T(8,128)(2,1)S(1)} %collective-permute-done.35.refs_17_), channel_id=1, source_target_pairs={{0,2},{2,0},{1,3},{3,1},{4,6},{6,4},{5,7},{7,5},{8,10},{10,8},{9,1... | collective-permute-start | bytes 2949128 | tf_op jit(solution)/shard_map/ppermute | solution.py:28
  81.9 28.4 %collective-permute-start.27 = (bf16[1,64,384]{2,1,0:T(8,128)(2,1)S(1)}, bf16[1,64,384]{2,1,0:T(8,128)(2,1)S(1)}, u32[]{:S(2)}, u32[]{:S(2)}) collective-permute-start(bf16[1,64,384]{2,1,0:T(8,128)(2,1)S(1)} %get-tuple-element.59), channel_id=1, source_target_pairs={{0,2},{2,0},{1,3},{3,1},{4,6},{6,4},{5,7},{7,5},{8,10},{10,8},{9,1... | collective-permute-start | bytes 147464 | tf_op jit(solution)/shard_map/ppermute | solution.py:28
  84.8 27.5 %collective-permute-start.14 = (bf16[1,64,384]{2,1,0:T(8,128)(2,1)S(1)}, bf16[1,64,384]{2,1,0:T(8,128)(2,1)S(1)}, u32[]{:S(2)}, u32[]{:S(2)}) collective-permute-start(bf16[1,64,384]{2,1,0:T(8,128)(2,1)S(1)} %get-tuple-element.52), channel_id=1, source_target_pairs={{0,2},{2,0},{1,3},{3,1},{4,6},{6,4},{5,7},{7,5},{8,10},{10,8},{9,1... | collective-permute-start | bytes 147464 | tf_op jit(solution)/shard_map/ppermute | solution.py:28
  110.3 6.6 %collective-permute-start.29 = (bf16[2,1,64,384]{3,2,1,0:T(8,128)(2,1)S(1)}, bf16[2,1,64,384]{3,2,1,0:T(8,128)(2,1)S(1)}, u32[]{:S(2)}, u32[]{:S(2)}) collective-permute-start(bf16[2,1,64,384]{3,2,1,0:T(8,128)(2,1)S(1)} %pad_maximum_fusion.2.refs_8_), channel_id=1, source_target_pairs={{0,4},{4,8},{8,12},{12,0},{1,5},{5,9},{9,13},{13,1},{2,6},{6,10},{... | collective-permute-start | bytes 294920 | tf_op jit(solution)/shard_map/ppermute | solution.py:28
  112.0 9.7 %collective-permute-start.31 = (bf16[2,1,64,384]{3,2,1,0:T(8,128)(2,1)S(1)}, bf16[2,1,64,384]{3,2,1,0:T(8,128)(2,1)S(1)}, u32[]{:S(2)}, u32[]{:S(2)}) collective-permute-start(bf16[2,1,64,384]{3,2,1,0:T(8,128)(2,1)S(1)} %pad_maximum_fusion.2.refs_8_), channel_id=1, source_target_pairs={{0,8},{4,12},{8,0},{12,4},{1,9},{5,13},{9,1},{13,5},{2,10},{6,14},... | collective-permute-start | bytes 294920 | tf_op jit(solution)/shard_map/ppermute | solution.py:28
  112.4 9.4 %collective-permute-start.33 = (bf16[2,1,64,384]{3,2,1,0:T(8,128)(2,1)S(1)}, bf16[2,1,64,384]{3,2,1,0:T(8,128)(2,1)S(1)}, u32[]{:S(2)}, u32[]{:S(2)}) collective-permute-start(bf16[2,1,64,384]{3,2,1,0:T(8,128)(2,1)S(1)} %pad_maximum_fusion.2.refs_8_), channel_id=1, source_target_pairs={{0,12},{4,0},{8,4},{12,8},{1,13},{5,1},{9,5},{13,9},{2,14},{6,2},{... | collective-permute-start | bytes 294920 | tf_op jit(solution)/shard_map/ppermute | solution.py:28
  114.5 8.8 %collective-permute-start.28 = (bf16[2,1,64,384]{3,2,1,0:T(8,128)(2,1)S(1)}, bf16[2,1,64,384]{3,2,1,0:T(8,128)(2,1)S(1)}, u32[]{:S(2)}, u32[]{:S(2)}) collective-permute-start(bf16[2,1,64,384]{3,2,1,0:T(8,128)(2,1)S(1)} %pad_maximum_fusion.2.refs_8_), channel_id=1, source_target_pairs={{0,1},{1,0},{2,3},{3,2},{4,5},{5,4},{6,7},{7,6},{8,9},{9,8},{10,11... | collective-permute-start | bytes 294920 | tf_op jit(solution)/shard_map/ppermute | solution.py:28
  116.9 6.9 %collective-permute-start.16 = (bf16[2,1,64,384]{3,2,1,0:T(8,128)(2,1)S(1)}, bf16[2,1,64,384]{3,2,1,0:T(8,128)(2,1)S(1)}, u32[]{:S(2)}, u32[]{:S(2)}) collective-permute-start(bf16[2,1,64,384]{3,2,1,0:T(8,128)(2,1)S(1)} %pad_maximum_fusion.1.refs_0_), channel_id=1, source_target_pairs={{0,4},{4,8},{8,12},{12,0},{1,5},{5,9},{9,13},{13,1},{2,6},{6,10},{... | collective-permute-start | bytes 294920 | tf_op jit(solution)/shard_map/ppermute | solution.py:28
  121.7 5.9 %collective-permute-start.18 = (bf16[2,1,64,384]{3,2,1,0:T(8,128)(2,1)S(1)}, bf16[2,1,64,384]{3,2,1,0:T(8,128)(2,1)S(1)}, u32[]{:S(2)}, u32[]{:S(2)}) collective-permute-start(bf16[2,1,64,384]{3,2,1,0:T(8,128)(2,1)S(1)} %pad_maximum_fusion.1.refs_0_), channel_id=1, source_target_pairs={{0,8},{4,12},{8,0},{12,4},{1,9},{5,13},{9,1},{13,5},{2,10},{6,14},... | collective-permute-start | bytes 294920 | tf_op jit(solution)/shard_map/ppermute | solution.py:28
  121.7 6.9 %collective-permute-start.20 = (bf16[2,1,64,384]{3,2,1,0:T(8,128)(2,1)S(1)}, bf16[2,1,64,384]{3,2,1,0:T(8,128)(2,1)S(1)}, u32[]{:S(2)}, u32[]{:S(2)}) collective-permute-start(bf16[2,1,64,384]{3,2,1,0:T(8,128)(2,1)S(1)} %pad_maximum_fusion.1.refs_0_), channel_id=1, source_target_pairs={{0,12},{4,0},{8,4},{12,8},{1,13},{5,1},{9,5},{13,9},{2,14},{6,2},{... | collective-permute-start | bytes 294920 | tf_op jit(solution)/shard_map/ppermute | solution.py:28
  123.3 5.3 %collective-permute-start.15 = (bf16[2,1,64,384]{3,2,1,0:T(8,128)(2,1)S(1)}, bf16[2,1,64,384]{3,2,1,0:T(8,128)(2,1)S(1)}, u32[]{:S(2)}, u32[]{:S(2)}) collective-permute-start(bf16[2,1,64,384]{3,2,1,0:T(8,128)(2,1)S(1)} %pad_maximum_fusion.1.refs_0_), channel_id=1, source_target_pairs={{0,1},{1,0},{2,3},{3,2},{4,5},{5,4},{6,7},{7,6},{8,9},{9,8},{10,11... | collective-permute-start | bytes 294920 | tf_op jit(solution)/shard_map/ppermute | solution.py:28
  123.9 5.3 %collective-permute-start.30 = (bf16[2,1,64,384]{3,2,1,0:T(8,128)(2,1)S(1)}, bf16[2,1,64,384]{3,2,1,0:T(8,128)(2,1)S(1)}, u32[]{:S(2)}, u32[]{:S(2)}) collective-permute-start(bf16[2,1,64,384]{3,2,1,0:T(8,128)(2,1)S(1)} %collective-permute-done.29.refs_10_), channel_id=1, source_target_pairs={{0,1},{1,0},{2,3},{3,2},{4,5},{5,4},{6,7},{7,6},{8,9},{9,8},{10,11... | collective-permute-start | bytes 294920 | tf_op jit(solution)/shard_map/ppermute | solution.py:28
  127.6 1.6 %collective-permute-start.32 = (bf16[2,1,64,384]{3,2,1,0:T(8,128)(2,1)S(1)}, bf16[2,1,64,384]{3,2,1,0:T(8,128)(2,1)S(1)}, u32[]{:S(2)}, u32[]{:S(2)}) collective-permute-start(bf16[2,1,64,384]{3,2,1,0:T(8,128)(2,1)S(1)} %collective-permute-done.31.refs_12_), channel_id=1, source_target_pairs={{0,1},{1,0},{2,3},{3,2},{4,5},{5,4},{6,7},{7,6},{8,9},{9,8},{10,11... | collective-permute-start | bytes 294920 | tf_op jit(solution)/shard_map/ppermute | solution.py:28
  128.6 1.3 collective-permute-start.34
  128.6 1.5 collective-permute-start.17
  129.1 1.3 collective-permute-start.19
  129.2 1.4 collective-permute-start.21
  132.2 5.2 %collective-permute-start.39 = (bf16[1,64,640]{2,1,0:T(8,128)(2,1)S(1)}, bf16[1,64,640]{2,1,0:T(8,128)(2,1)S(1)}, u32[]{:S(2)}, u32[]{:S(2)}) collective-permute-start(bf16[1,64,640]{2,1,0:T(8,128)(2,1)S(1)} %get-tuple-element.64), channel_id=1, source_target_pairs={{0,12},{4,0},{8,4},{12,8},{1,13},{5,1},{9,5},{13,9},{2,14},{6,2},{... | collective-permute-start | bytes 245768 | tf_op jit(solution)/shard_map/ppermute | solution.py:28
  134.5 8.6 %collective-permute-start.41 = (bf16[1,64,640]{2,1,0:T(8,128)(2,1)S(1)}, bf16[1,64,640]{2,1,0:T(8,128)(2,1)S(1)}, u32[]{:S(2)}, u32[]{:S(2)}) collective-permute-start(bf16[1,64,640]{2,1,0:T(8,128)(2,1)S(1)} %get-tuple-element.65), channel_id=1, source_target_pairs={{0,8},{4,12},{8,0},{12,4},{1,9},{5,13},{9,1},{13,5},{2,10},{6,14},... | collective-permute-start | bytes 245768 | tf_op jit(solution)/shard_map/ppermute | solution.py:28
  135.1 8.0 %collective-permute-start.43 = (bf16[1,64,640]{2,1,0:T(8,128)(2,1)S(1)}, bf16[1,64,640]{2,1,0:T(8,128)(2,1)S(1)}, u32[]{:S(2)}, u32[]{:S(2)}) collective-permute-start(bf16[1,64,640]{2,1,0:T(8,128)(2,1)S(1)} %get-tuple-element.66), channel_id=1, source_target_pairs={{0,4},{4,8},{8,12},{12,0},{1,5},{5,9},{9,13},{13,1},{2,6},{6,10},{... | collective-permute-start | bytes 245768 | tf_op jit(solution)/shard_map/ppermute | solution.py:28
  135.1 8.5 %collective-permute-start.38 = (bf16[1,64,640]{2,1,0:T(8,128)(2,1)S(1)}, bf16[1,64,640]{2,1,0:T(8,128)(2,1)S(1)}, u32[]{:S(2)}, u32[]{:S(2)}) collective-permute-start(bf16[1,64,640]{2,1,0:T(8,128)(2,1)S(1)} %get-tuple-element.63), channel_id=1, source_target_pairs={{0,1},{1,0},{2,3},{3,2},{4,5},{5,4},{6,7},{7,6},{8,9},{9,8},{10,11... | collective-permute-start | bytes 245768 | tf_op jit(solution)/shard_map/ppermute | solution.py:28
  137.3 6.2 %collective-permute-start.40 = (bf16[1,64,640]{2,1,0:T(8,128)(2,1)S(1)}, bf16[1,64,640]{2,1,0:T(8,128)(2,1)S(1)}, u32[]{:S(2)}, u32[]{:S(2)}) collective-permute-start(bf16[1,64,640]{2,1,0:T(8,128)(2,1)S(1)} %collective-permute-done.39.refs_2_), channel_id=1, source_target_pairs={{0,1},{1,0},{2,3},{3,2},{4,5},{5,4},{6,7},{7,6},{8,9},{9,8},{10,11... | collective-permute-start | bytes 245768 | tf_op jit(solution)/shard_map/ppermute | solution.py:28
  143.1 1.3 collective-permute-start.42
  143.1 1.4 collective-permute-start.44
  (5 other events, 10.2 us)

commit v7 on v6

--- a/solution.py
+++ b/solution.py
@@ -188,7 +188,7 @@
     share = jax.ShapeDtypeStruct((weights.shape[0] // n_mp, weights.shape[1]), weights.dtype)
     return pl.pallas_call(
         functools.partial(load_kernel, n_mp),
-        in_specs=[pl.BlockSpec(memory_space=pl.ANY)],
+        in_specs=[pl.BlockSpec(memory_space=pltpu.HBM)],
         out_specs=[pl.BlockSpec(memory_space=pltpu.VMEM)] * n_mp,
         out_shape=[share] * n_mp,
         scratch_shapes=[pltpu.SemaphoreType.DMA((n_mp,))],
@@ -249,7 +249,7 @@
     return pl.pallas_call(
         functools.partial(modulate_kernel, n_tm, n_seq, n_mp, cuts),
         grid=(n_tm,),
-        in_specs=[pl.BlockSpec(memory_space=pltpu.SMEM), pl.BlockSpec(memory_space=pl.ANY)]
+        in_specs=[pl.BlockSpec(memory_space=pltpu.SMEM), pl.BlockSpec(memory_space=pltpu.HBM)]
         + [pl.BlockSpec((3, window, depth), lambda k: (0, 0, 0))] * n_tm
         + [pl.BlockSpec((1, frames, part, wide), lambda k: (k, 0, 0, 0))] * (n_seq * n_mp),
         out_specs=[
@@ -271,7 +271,7 @@
             bytes_accessed=4 * n_tm * n_seq * frames * n_mp * part * depth,
             transcendentals=0,
         ),
-        compiler_params=pltpu.CompilerParams(vmem_limit_bytes=8 << 20),
+        compiler_params=pltpu.CompilerParams(vmem_limit_bytes=48 << 20),
         name="modulate",
     )(start_step, w_qkv, *shares, *[r for side in rows for r in side])
 
@@ -424,10 +424,11 @@
         weights.append([turn(s, "seq", -j) for s in weights[0]])
 
     groups = head_groups(cols)
-    hidden, coef, *parts_qkv = modulate(start_step, w_qkv, groups, shares, rows)
+    hidden, coef, first_qkv = modulate(start_step, w_qkv, groups[:1], shares, rows)
     hidden = hidden.reshape(n_tm, n_seq * frames * tok, depth)
     proj = []
-    for part_qkv in parts_qkv:
+    for h, (lane, size) in enumerate(groups):
+        part_qkv = w_qkv[:, :, lane : lane + size] if h else first_qkv
         proj.append(
             jnp.einsum(
                 "krd,cdh->kcrh",

time: 146 us -> 146 us (level)
  local copies, waits for them, and re-layouts: 5.32 us -> 2.67 us
  starting transfers between devices: 39.1 us -> 41.2 us
    ppermute x35, starting transfers between devices: 29.2 us -> 32.7 us  [turn(): lax.ppermute(block, axis, [(i, (i + distance) % size) for i in range(size)])]
    unnamed x16 -> x18, local copies, waits for them, and re-layouts: 5.32 us -> 2.66 us
    ppermute x6, starting transfers between devices: 9.96 us -> 8.46 us  [sweep(): first = lax.ppermute(first, 'tm', evens)]
  transfers between devices with their start and end apart: 45 -> 45, of which waited for: 26 -> 23; matrix products, arithmetic and copies ran while one was open for 6% -> 6% of each run, Pallas kernels for 2% -> 2%
where the time goes in v7:
time: 146 us; the launch traced here: 145 us
  waiting for transfers between devices  80.7 us (55%)
  starting transfers between devices  41.2 us (28%)
  Pallas kernels  8.33 us (6%)
  other arithmetic  7.72 us (5%)
  matrix products  3.83 us (3%)
  local copies, waits for them, and re-layouts  2.67 us (2%)
    ppermute x35, waiting for transfers between devices, turn(): lax.ppermute(block, axis, [(i, (i + distance) % size) for i in range(size)])  62.8 us
    ppermute x35, starting transfers between devices, turn(): lax.ppermute(block, axis, [(i, (i + distance) % size) for i in range(size)])  32.7 us
    ppermute x6, waiting for transfers between devices, sweep(): first = lax.ppermute(first, 'tm', evens)  17.8 us
    ppermute x6, starting transfers between devices, sweep(): first = lax.ppermute(first, 'tm', evens)  8.46 us
    convert_element_type x4, other arithmetic, sweep(): second = jnp.where(even, left, right).astype(jnp.float16)  4.51 us
    dot_general x2, matrix products, sweep(): jnp.einsum('krd,cdh->kcrh', hidden, part_qkv, preferred_element_type=jnp....  3.83 us
  transfers between devices with their start and end apart: 45, of which 23 were waited for; matrix products, arithmetic and copies ran while one was open for 6% of the time, Pallas kernels for 2%

profile of v7, /device:TPU:0, one launch (start us, length us, event | category | flops | bytes accessed | tf_op | source)
XLA Modules:
  0.0 145.3 jit_solution(4831318652964248810)
XLA Ops:
  0.0 1.1 copy-done.2
  1.5 5.1 %collective-permute-start.5 = (bf16[1,32,1408]{2,1,0:T(8,128)(2,1)S(1)}, bf16[1,32,1408]{2,1,0:T(8,128)(2,1)S(1)}, u32[]{:S(2)}, u32[]{:S(2)}) collective-permute-start(bf16[1,32,1408]{2,1,0:T(8,128)(2,1)S(1)} %get-tuple-element.42), channel_id=1, source_target_pairs={{0,12},{4,0},{8,4},{12,8},{1,13},{5,1},{9,5},{13,9},{2,14},{6,2},{... | collective-permute-start | bytes 270344 | tf_op jit(solution)/shard_map/ppermute | solution.py:28
  6.6 1.0 collective-permute-start.3
  7.6 2.0 %collective-permute-done.5 = bf16[1,32,1408]{2,1,0:T(8,128)(2,1)S(1)} collective-permute-done((bf16[1,32,1408]{2,1,0:T(8,128)(2,1)S(1)}, bf16[1,32,1408]{2,1,0:T(8,128)(2,1)S(1)}, u32[]{:S(2)}, u32[]{:S(2)}) %collective-permute-start.5) | collective-permute-done | bytes 90144 | tf_op jit(solution)/shard_map/ppermute | solution.py:28
  9.6 5.1 %collective-permute-done.4 = bf16[1,32,1408]{2,1,0:T(8,128)(2,1)S(1)} collective-permute-done((bf16[1,32,1408]{2,1,0:T(8,128)(2,1)S(1)}, bf16[1,32,1408]{2,1,0:T(8,128)(2,1)S(1)}, u32[]{:S(2)}, u32[]{:S(2)}) %collective-permute-start.4) | collective-permute-done | bytes 90144 | tf_op jit(solution)/shard_map/ppermute | solution.py:28
  14.8 1.6 %collective-permute-start.7 = (bf16[4,1,32,1408]{3,2,1,0:T(8,128)(2,1)S(1)}, bf16[4,1,32,1408]{3,2,1,0:T(8,128)(2,1)S(1)}, u32[]{:S(2)}, u32[]{:S(2)}) collective-permute-start(bf16[4,1,32,1408]{3,2,1,0:T(8,128)(2,1)S(1)} %pad_maximum_fusion.refs_4_), channel_id=1, source_target_pairs={{0,2},{2,0},{1,3},{3,1},{4,6},{6,4},{5,7},{7,5},{8,10},{10,8},{9,1... | collective-permute-start | bytes 1081352 | tf_op jit(solution)/shard_map/ppermute | solution.py:28
  16.4 8.5 %collective-permute-done.7.refs_6_ = bf16[4,1,32,1408]{3,2,1,0:T(8,128)(2,1)S(1)} collective-permute-done((bf16[4,1,32,1408]{3,2,1,0:T(8,128)(2,1)S(1)}, bf16[4,1,32,1408]{3,2,1,0:T(8,128)(2,1)S(1)}, u32[]{:S(2)}, u32[]{:S(2)}) %collective-permute-start.7) | collective-permute-done | bytes 360480 | tf_op jit(solution)/shard_map/ppermute | solution.py:28
  25.5 1.5 %copy-done = bf16[64,15360]{1,0:T(8,128)(2,1)S(1)} copy-done((bf16[64,15360]{1,0:T(8,128)(2,1)S(1)}, bf16[64,15360]{1,0:T(8,128)(2,1)}, u32[]{:S(2)}) %copy-start) | copy-done | bytes 1966104
  28.0 1.9 %collective-permute-start.1 = (f32[3,4,1280]{2,1,0:T(4,128)S(1)}, f32[3,4,1280]{2,1,0:T(4,128)S(1)}, u32[]{:S(2)}, u32[]{:S(2)}) collective-permute-start(f32[3,4,1280]{2,1,0:T(4,128)S(1)} %get-tuple-element.37), channel_id=1, source_target_pairs={{0,8},{4,12},{8,0},{12,4},{1,9},{5,13},{9,1},{13,5},{2,10},{6,14},... | collective-permute-start | bytes 184328 | tf_op jit(solution)/shard_map/ppermute | solution.py:28
  29.9 2.8 %collective-permute-start.2 = (f32[3,4,1280]{2,1,0:T(4,128)S(1)}, f32[3,4,1280]{2,1,0:T(4,128)S(1)}, u32[]{:S(2)}, u32[]{:S(2)}) collective-permute-start(f32[3,4,1280]{2,1,0:T(4,128)S(1)} %get-tuple-element.38), channel_id=1, source_target_pairs={{0,12},{4,0},{8,4},{12,8},{1,13},{5,1},{9,5},{13,9},{2,14},{6,2},{... | collective-permute-start | bytes 184328 | tf_op jit(solution)/shard_map/ppermute | solution.py:28
  32.7 2.1 %collective-permute-done.refs_1_ = f32[3,4,1280]{2,1,0:T(4,128)S(1)} collective-permute-done((f32[3,4,1280]{2,1,0:T(4,128)S(1)}, f32[3,4,1280]{2,1,0:T(4,128)S(1)}, u32[]{:S(2)}, u32[]{:S(2)}) %collective-permute-start) | collective-permute-done | bytes 61472 | tf_op jit(solution)/shard_map/ppermute | solution.py:28
  34.7 1.6 %collective-permute-done.1.refs_2_ = f32[3,4,1280]{2,1,0:T(4,128)S(1)} collective-permute-done((f32[3,4,1280]{2,1,0:T(4,128)S(1)}, f32[3,4,1280]{2,1,0:T(4,128)S(1)}, u32[]{:S(2)}, u32[]{:S(2)}) %collective-permute-start.1) | collective-permute-done | bytes 61472 | tf_op jit(solution)/shard_map/ppermute | solution.py:28
  36.4 2.0 %modulate.1 = (bf16[4,2,1,64,1280]{4,3,2,1,0:T(8,128)(2,1)S(1)}, f32[4,1,1280]{2,1,0:T(1,128)S(1)}, bf16[3,1280,384]{2,1,0:T(8,128)(2,1)S(1)}) custom-call(s32[1]{0:T(128)S(6)} %copy.15.step_ref, bf16[3,1280,768]{2,1,0:T(8,128)(2,1)} %w_ref.2, f32[3,4,1280]{2,1,0:T(4,128)S(1)} %get-tuple-element.35.refs_0_, f32[3,4,1280]{2,1,0:T(4,128)S(1)} %collective-permute-done.refs_1_, ...), custom_call_target="tpu_custom_call" | custom-call | flops 2621440 | bytes 2621440 | tf_op jit(solution)/shard_map/modulate/pallas_call | solution.py:249
  38.5 2.0 %fusion.8 = f32[4,3,128,384]{3,2,0,1:T(8,128)S(1)} fusion(bf16[4,128,1280,1]{2,1,0,3:T(8,128)(2,1)S(1)} %bitcast.120, bf16[3,1280,384]{2,1,0:T(8,128)(2,1)S(1)} %get-tuple-element.44), kind=kOutput, calls=%fused_computation.6 | convolution fusion | flops 1509949440 | bytes 6619136 | tf_op jit(solution)/shard_map/krd,cdh->kcrh/dot_general | solution.py:433
  41.3 1.5 %collective-permute-start.9 = (f16[3,128,384]{2,1,0:T(8,128)(2,1)}, f16[3,128,384]{2,1,0:T(8,128)(2,1)}, u32[]{:S(2)}, u32[]{:S(2)}) collective-permute-start(f16[3,128,384]{2,1,0:T(8,128)(2,1)} %select_convert_fusion.9), channel_id=1, source_target_pairs={{0,4},{4,0},{8,12},{12,8},{1,5},{5,1},{9,13},{13,9},{2,6},{6,2},{1... | collective-permute-start | bytes 884744 | tf_op jit(solution)/shard_map/ppermute | solution.py:464
  42.8 1.9 %fusion.5 = f32[4,3,128,384]{3,2,1,0:T(8,128)S(1)} fusion(bf16[4,128,1280,1]{2,1,3,0:T(8,128)(2,1)S(1)} %bitcast.121, bf16[3,1280,768]{2,1,0:T(8,128)(2,1)S(1)} %bitcast.123), kind=kOutput, calls=%fused_computation.5 | convolution fusion | flops 1509949440 | bytes 6619136 | tf_op jit(solution)/shard_map/krd,cdh->kcrh/dot_general | solution.py:433
  46.9 4.7 %collective-permute-done.9 = f16[3,128,384]{2,1,0:T(8,128)(2,1)} collective-permute-done((f16[3,128,384]{2,1,0:T(8,128)(2,1)}, f16[3,128,384]{2,1,0:T(8,128)(2,1)}, u32[]{:S(2)}, u32[]{:S(2)}) %collective-permute-start.9) | collective-permute-done | bytes 294944 | tf_op jit(solution)/shard_map/ppermute | solution.py:464
  51.5 1.4 select_convert_fusion.7
  52.9 1.5 %collective-permute-start.10 = (f16[3,128,384]{2,1,0:T(8,128)(2,1)S(1)}, f16[3,128,384]{2,1,0:T(8,128)(2,1)S(1)}, u32[]{:S(2)}, u32[]{:S(2)}) collective-permute-start(f16[3,128,384]{2,1,0:T(8,128)(2,1)S(1)} %get-tuple-element.72), channel_id=1, source_target_pairs={{0,4},{4,0},{8,12},{12,8},{1,5},{5,1},{9,13},{13,9},{2,6},{6,2},{1... | collective-permute-start | bytes 884744 | tf_op jit(solution)/shard_map/ppermute | solution.py:464
  54.5 3.3 %collective-permute-done.22 = f16[3,128,384]{2,1,0:T(8,128)(2,1)S(1)} collective-permute-done((f16[3,128,384]{2,1,0:T(8,128)(2,1)}, f16[3,128,384]{2,1,0:T(8,128)(2,1)S(1)}, u32[]{:S(2)}, u32[]{:S(2)}) %collective-permute-start.22) | collective-permute-done | bytes 294944 | tf_op jit(solution)/shard_map/ppermute | solution.py:464
  57.8 1.3 select_convert_fusion.2
  59.1 1.5 %collective-permute-start.23 = (f16[3,128,384]{2,1,0:T(8,128)(2,1)S(1)}, f16[3,128,384]{2,1,0:T(8,128)(2,1)S(1)}, u32[]{:S(2)}, u32[]{:S(2)}) collective-permute-start(f16[3,128,384]{2,1,0:T(8,128)(2,1)S(1)} %get-tuple-element.70), channel_id=1, source_target_pairs={{0,4},{4,0},{8,12},{12,8},{1,5},{5,1},{9,13},{13,9},{2,6},{6,2},{1... | collective-permute-start | bytes 884744 | tf_op jit(solution)/shard_map/ppermute | solution.py:464
  60.6 3.5 %collective-permute-done.10 = f16[3,128,384]{2,1,0:T(8,128)(2,1)S(1)} collective-permute-done((f16[3,128,384]{2,1,0:T(8,128)(2,1)S(1)}, f16[3,128,384]{2,1,0:T(8,128)(2,1)S(1)}, u32[]{:S(2)}, u32[]{:S(2)}) %collective-permute-start.10) | collective-permute-done | bytes 294944 | tf_op jit(solution)/shard_map/ppermute | solution.py:464
  64.1 1.5 %collective-permute-start.36 = (bf16[640,768]{1,0:T(8,128)(2,1)S(1)}, bf16[640,768]{1,0:T(8,128)(2,1)S(1)}, u32[]{:S(2)}, u32[]{:S(2)}) collective-permute-start(bf16[640,768]{1,0:T(8,128)(2,1)S(1)} %get-tuple-element.58.refs_16_), channel_id=1, source_target_pairs={{0,2},{2,0},{1,3},{3,1},{4,6},{6,4},{5,7},{7,5},{8,10},{10,8},{9,1... | collective-permute-start | bytes 2949128 | tf_op jit(solution)/shard_map/ppermute | solution.py:28
  65.6 1.5 %select_convert_fusion.5 = (f16[3,128,384]{2,1,0:T(8,128)(2,1)S(1)}, f16[3,128,384]{2,1,0:T(8,128)(2,1)S(1)}) fusion(pred[]{:T(512)S(6)} %eq.5, f16[3,128,384]{2,1,0:T(8,128)(2,1)S(1)} %collective-permute-done.11, f16[3,128,384]{2,1,0:T(8,128)(2,1)S(1)} %collective-permute-done.10, pred[]{:T(512)S(6)} %lt.9, f32[4,3,128,384]{3,2,0,1:T(8,128)} %copy-done.5, ...), kind=kLoop, calls=%fused_computation.56 | loop fusion | flops 1769472 | bytes 2359299 | tf_op jit(solution)/shard_map/convert_element_type | solution.py:463
  67.1 1.5 %collective-permute-start.12 = (f16[3,128,384]{2,1,0:T(8,128)(2,1)S(1)}, f16[3,128,384]{2,1,0:T(8,128)(2,1)S(1)}, u32[]{:S(2)}, u32[]{:S(2)}) collective-permute-start(f16[3,128,384]{2,1,0:T(8,128)(2,1)S(1)} %get-tuple-element.68), channel_id=1, source_target_pairs={{0,4},{4,0},{8,12},{12,8},{1,5},{5,1},{9,13},{13,9},{2,6},{6,2},{1... | collective-permute-start | bytes 884744 | tf_op jit(solution)/shard_map/ppermute | solution.py:464
  68.6 1.7 %collective-permute-done.23 = f16[3,128,384]{2,1,0:T(8,128)(2,1)S(1)} collective-permute-done((f16[3,128,384]{2,1,0:T(8,128)(2,1)S(1)}, f16[3,128,384]{2,1,0:T(8,128)(2,1)S(1)}, u32[]{:S(2)}, u32[]{:S(2)}) %collective-permute-start.23) | collective-permute-done | bytes 294944 | tf_op jit(solution)/shard_map/ppermute | solution.py:464
  70.7 1.8 %collective-permute-start.25 = (f16[3,128,384]{2,1,0:T(8,128)(2,1)S(1)}, f16[3,128,384]{2,1,0:T(8,128)(2,1)S(1)}, u32[]{:S(2)}, u32[]{:S(2)}) collective-permute-start(f16[3,128,384]{2,1,0:T(8,128)(2,1)S(1)} %get-tuple-element.66), channel_id=1, source_target_pairs={{0,4},{4,0},{8,12},{12,8},{1,5},{5,1},{9,13},{13,9},{2,6},{6,2},{1... | collective-permute-start | bytes 884744 | tf_op jit(solution)/shard_map/ppermute | solution.py:464
  72.5 4.0 %collective-permute-done.12 = f16[3,128,384]{2,1,0:T(8,128)(2,1)S(1)} collective-permute-done((f16[3,128,384]{2,1,0:T(8,128)(2,1)S(1)}, f16[3,128,384]{2,1,0:T(8,128)(2,1)S(1)}, u32[]{:S(2)}, u32[]{:S(2)}) %collective-permute-start.12) | collective-permute-done | bytes 294944 | tf_op jit(solution)/shard_map/ppermute | solution.py:464
  76.5 1.5 %collective-permute-start.37 = (bf16[640,768]{1,0:T(8,128)(2,1)S(1)}, bf16[640,768]{1,0:T(8,128)(2,1)S(1)}, u32[]{:S(2)}, u32[]{:S(2)}) collective-permute-start(bf16[640,768]{1,0:T(8,128)(2,1)S(1)} %collective-permute-done.35.refs_17_), channel_id=1, source_target_pairs={{0,2},{2,0},{1,3},{3,1},{4,6},{6,4},{5,7},{7,5},{8,10},{10,8},{9,1... | collective-permute-start | bytes 2949128 | tf_op jit(solution)/shard_map/ppermute | solution.py:28
  78.0 1.2 fusion.21
  79.3 0.9 attend.2
  81.7 0.9 attend.3
  82.6 1.6 %collective-permute-start.27 = (bf16[1,64,384]{2,1,0:T(8,128)(2,1)S(1)}, bf16[1,64,384]{2,1,0:T(8,128)(2,1)S(1)}, u32[]{:S(2)}, u32[]{:S(2)}) collective-permute-start(bf16[1,64,384]{2,1,0:T(8,128)(2,1)S(1)} %get-tuple-element.57), channel_id=1, source_target_pairs={{0,2},{2,0},{1,3},{3,1},{4,6},{6,4},{5,7},{7,5},{8,10},{10,8},{9,1... | collective-permute-start | bytes 147464 | tf_op jit(solution)/shard_map/ppermute | solution.py:28
  84.2 23.2 %collective-permute-done.14 = bf16[1,64,384]{2,1,0:T(8,128)(2,1)S(1)} collective-permute-done((bf16[1,64,384]{2,1,0:T(8,128)(2,1)S(1)}, bf16[1,64,384]{2,1,0:T(8,128)(2,1)S(1)}, u32[]{:S(2)}, u32[]{:S(2)}) %collective-permute-start.14) | collective-permute-done | bytes 49184 | tf_op jit(solution)/shard_map/ppermute | solution.py:28
  107.5 2.1 %collective-permute-start.16 = (bf16[2,1,64,384]{3,2,1,0:T(8,128)(2,1)S(1)}, bf16[2,1,64,384]{3,2,1,0:T(8,128)(2,1)S(1)}, u32[]{:S(2)}, u32[]{:S(2)}) collective-permute-start(bf16[2,1,64,384]{3,2,1,0:T(8,128)(2,1)S(1)} %pad_maximum_fusion.1.refs_0_), channel_id=1, source_target_pairs={{0,4},{4,8},{8,12},{12,0},{1,5},{5,9},{9,13},{13,1},{2,6},{6,10},{... | collective-permute-start | bytes 294920 | tf_op jit(solution)/shard_map/ppermute | solution.py:28
  109.6 2.1 %collective-permute-start.18 = (bf16[2,1,64,384]{3,2,1,0:T(8,128)(2,1)S(1)}, bf16[2,1,64,384]{3,2,1,0:T(8,128)(2,1)S(1)}, u32[]{:S(2)}, u32[]{:S(2)}) collective-permute-start(bf16[2,1,64,384]{3,2,1,0:T(8,128)(2,1)S(1)} %pad_maximum_fusion.1.refs_0_), channel_id=1, source_target_pairs={{0,8},{4,12},{8,0},{12,4},{1,9},{5,13},{9,1},{13,5},{2,10},{6,14},... | collective-permute-start | bytes 294920 | tf_op jit(solution)/shard_map/ppermute | solution.py:28
  111.7 1.5 %collective-permute-start.20 = (bf16[2,1,64,384]{3,2,1,0:T(8,128)(2,1)S(1)}, bf16[2,1,64,384]{3,2,1,0:T(8,128)(2,1)S(1)}, u32[]{:S(2)}, u32[]{:S(2)}) collective-permute-start(bf16[2,1,64,384]{3,2,1,0:T(8,128)(2,1)S(1)} %pad_maximum_fusion.1.refs_0_), channel_id=1, source_target_pairs={{0,12},{4,0},{8,4},{12,8},{1,13},{5,1},{9,5},{13,9},{2,14},{6,2},{... | collective-permute-start | bytes 294920 | tf_op jit(solution)/shard_map/ppermute | solution.py:28
  113.2 1.9 %collective-permute-done.16.refs_2_ = bf16[2,1,64,384]{3,2,1,0:T(8,128)(2,1)S(1)} collective-permute-done((bf16[2,1,64,384]{3,2,1,0:T(8,128)(2,1)S(1)}, bf16[2,1,64,384]{3,2,1,0:T(8,128)(2,1)S(1)}, u32[]{:S(2)}, u32[]{:S(2)}) %collective-permute-start.16) | collective-permute-done | bytes 98336 | tf_op jit(solution)/shard_map/ppermute | solution.py:28
  115.2 4.0 %collective-permute-done.18.refs_4_ = bf16[2,1,64,384]{3,2,1,0:T(8,128)(2,1)S(1)} collective-permute-done((bf16[2,1,64,384]{3,2,1,0:T(8,128)(2,1)S(1)}, bf16[2,1,64,384]{3,2,1,0:T(8,128)(2,1)S(1)}, u32[]{:S(2)}, u32[]{:S(2)}) %collective-permute-start.18) | collective-permute-done | bytes 98336 | tf_op jit(solution)/shard_map/ppermute | solution.py:28
  119.9 3.3 %collective-permute-start.33 = (bf16[2,1,64,384]{3,2,1,0:T(8,128)(2,1)S(1)}, bf16[2,1,64,384]{3,2,1,0:T(8,128)(2,1)S(1)}, u32[]{:S(2)}, u32[]{:S(2)}) collective-permute-start(bf16[2,1,64,384]{3,2,1,0:T(8,128)(2,1)S(1)} %pad_maximum_fusion.2.refs_8_), channel_id=1, source_target_pairs={{0,12},{4,0},{8,4},{12,8},{1,13},{5,1},{9,5},{13,9},{2,14},{6,2},{... | collective-permute-start | bytes 294920 | tf_op jit(solution)/shard_map/ppermute | solution.py:28
  123.7 3.7 %collective-permute-done.31.refs_12_ = bf16[2,1,64,384]{3,2,1,0:T(8,128)(2,1)S(1)} collective-permute-done((bf16[2,1,64,384]{3,2,1,0:T(8,128)(2,1)S(1)}, bf16[2,1,64,384]{3,2,1,0:T(8,128)(2,1)S(1)}, u32[]{:S(2)}, u32[]{:S(2)}) %collective-permute-start.31) | collective-permute-done | bytes 98336 | tf_op jit(solution)/shard_map/ppermute | solution.py:28
  127.4 0.9 collective-permute-done.33.refs_14_
  130.1 1.5 %project.1 = (f32[1,64,640]{2,1,0:T(8,128)S(1)}, bf16[1,64,640]{2,1,0:T(8,128)(2,1)S(1)}, bf16[1,64,640]{2,1,0:T(8,128)(2,1)S(1)}, bf16[1,64,640]{2,1,0:T(8,128)(2,1)S(1)}, bf16[1,64,640]{2,1,0:T(8,128)(2,1)S(1)}) custom-call(f32[4,1,1280]{2,1,0:T(1,128)S(1)} %get-tuple-element.43.coef_ref, bf16[2,1,64,384]{3,2,1,0:T(8,128)(2,1)S(1)} %pad_maximum_fusion.1.refs_0_, ...), custom_call_target="tpu_custom_call" | custom-call | flops 1006632960 | bytes 5505024 | tf_op jit(solution)/shard_map/project/pallas_call | solution.py:343
  131.6 3.0 %collective-permute-start.39 = (bf16[1,64,640]{2,1,0:T(8,128)(2,1)S(1)}, bf16[1,64,640]{2,1,0:T(8,128)(2,1)S(1)}, u32[]{:S(2)}, u32[]{:S(2)}) collective-permute-start(bf16[1,64,640]{2,1,0:T(8,128)(2,1)S(1)} %get-tuple-element.62), channel_id=1, source_target_pairs={{0,12},{4,0},{8,4},{12,8},{1,13},{5,1},{9,5},{13,9},{2,14},{6,2},{... | collective-permute-start | bytes 245768 | tf_op jit(solution)/shard_map/ppermute | solution.py:28
  135.3 2.2 %collective-permute-done.39.refs_2_ = bf16[1,64,640]{2,1,0:T(8,128)(2,1)S(1)} collective-permute-done((bf16[1,64,640]{2,1,0:T(8,128)(2,1)S(1)}, bf16[1,64,640]{2,1,0:T(8,128)(2,1)S(1)}, u32[]{:S(2)}, u32[]{:S(2)}) %collective-permute-start.39) | collective-permute-done | bytes 81952 | tf_op jit(solution)/shard_map/ppermute | solution.py:28
  137.5 5.3 %collective-permute-done.41.refs_4_ = bf16[1,64,640]{2,1,0:T(8,128)(2,1)S(1)} collective-permute-done((bf16[1,64,640]{2,1,0:T(8,128)(2,1)S(1)}, bf16[1,64,640]{2,1,0:T(8,128)(2,1)S(1)}, u32[]{:S(2)}, u32[]{:S(2)}) %collective-permute-start.41) | collective-permute-done | bytes 81952 | tf_op jit(solution)/shard_map/ppermute | solution.py:28
  144.3 1.0 finish.1
  (83 shorter events, 11.4 us)
Async XLA Ops:
  1.5 8.1 %collective-permute-start.5 = (bf16[1,32,1408]{2,1,0:T(8,128)(2,1)S(1)}, bf16[1,32,1408]{2,1,0:T(8,128)(2,1)S(1)}, u32[]{:S(2)}, u32[]{:S(2)}) collective-permute-start(bf16[1,32,1408]{2,1,0:T(8,128)(2,1)S(1)} %get-tuple-element.42), channel_id=1, source_target_pairs={{0,12},{4,0},{8,4},{12,8},{1,13},{5,1},{9,5},{13,9},{2,14},{6,2},{... | collective-permute-start | bytes 270344 | tf_op jit(solution)/shard_map/ppermute | solution.py:28
  6.6 8.1 %collective-permute-start.4 = (bf16[1,32,1408]{2,1,0:T(8,128)(2,1)S(1)}, bf16[1,32,1408]{2,1,0:T(8,128)(2,1)S(1)}, u32[]{:S(2)}, u32[]{:S(2)}) collective-permute-start(bf16[1,32,1408]{2,1,0:T(8,128)(2,1)S(1)} %get-tuple-element.41), channel_id=1, source_target_pairs={{0,8},{4,12},{8,0},{12,4},{1,9},{5,13},{9,1},{13,5},{2,10},{6,14},... | collective-permute-start | bytes 270344 | tf_op jit(solution)/shard_map/ppermute | solution.py:28
  6.6 8.1 %collective-permute-start.3 = (bf16[1,32,1408]{2,1,0:T(8,128)(2,1)S(1)}, bf16[1,32,1408]{2,1,0:T(8,128)(2,1)S(1)}, u32[]{:S(2)}, u32[]{:S(2)}) collective-permute-start(bf16[1,32,1408]{2,1,0:T(8,128)(2,1)S(1)} %get-tuple-element.40), channel_id=1, source_target_pairs={{0,4},{4,8},{8,12},{12,0},{1,5},{5,9},{9,13},{13,1},{2,6},{6,10},{... | collective-permute-start | bytes 270344 | tf_op jit(solution)/shard_map/ppermute | solution.py:28
  14.8 10.1 %collective-permute-start.7 = (bf16[4,1,32,1408]{3,2,1,0:T(8,128)(2,1)S(1)}, bf16[4,1,32,1408]{3,2,1,0:T(8,128)(2,1)S(1)}, u32[]{:S(2)}, u32[]{:S(2)}) collective-permute-start(bf16[4,1,32,1408]{3,2,1,0:T(8,128)(2,1)S(1)} %pad_maximum_fusion.refs_4_), channel_id=1, source_target_pairs={{0,2},{2,0},{1,3},{3,1},{4,6},{6,4},{5,7},{7,5},{8,10},{10,8},{9,1... | collective-permute-start | bytes 1081352 | tf_op jit(solution)/shard_map/ppermute | solution.py:28
  16.4 20.0 %collective-permute-start.6 = (bf16[4,1,32,1408]{3,2,1,0:T(8,128)(2,1)S(1)}, bf16[4,1,32,1408]{3,2,1,0:T(8,128)(2,1)S(1)}, u32[]{:S(2)}, u32[]{:S(2)}) collective-permute-start(bf16[4,1,32,1408]{3,2,1,0:T(8,128)(2,1)S(1)} %pad_maximum_fusion.refs_4_), channel_id=1, source_target_pairs={{0,1},{1,0},{2,3},{3,2},{4,5},{5,4},{6,7},{7,6},{8,9},{9,8},{10,11... | collective-permute-start | bytes 1081352 | tf_op jit(solution)/shard_map/ppermute | solution.py:28
  24.9 11.5 %collective-permute-start.8 = (bf16[4,1,32,1408]{3,2,1,0:T(8,128)(2,1)S(1)}, bf16[4,1,32,1408]{3,2,1,0:T(8,128)(2,1)S(1)}, u32[]{:S(2)}, u32[]{:S(2)}) collective-permute-start(bf16[4,1,32,1408]{3,2,1,0:T(8,128)(2,1)S(1)} %collective-permute-done.7.refs_6_), channel_id=1, source_target_pairs={{0,1},{1,0},{2,3},{3,2},{4,5},{5,4},{6,7},{7,6},{8,9},{9,8},{10,11... | collective-permute-start | bytes 1081352 | tf_op jit(solution)/shard_map/ppermute | solution.py:28
  27.9 6.8 %collective-permute-start = (f32[3,4,1280]{2,1,0:T(4,128)S(1)}, f32[3,4,1280]{2,1,0:T(4,128)S(1)}, u32[]{:S(2)}, u32[]{:S(2)}) collective-permute-start(f32[3,4,1280]{2,1,0:T(4,128)S(1)} %get-tuple-element.36), channel_id=1, source_target_pairs={{0,4},{4,8},{8,12},{12,0},{1,5},{5,9},{9,13},{13,1},{2,6},{6,10},{... | collective-permute-start | bytes 184328 | tf_op jit(solution)/shard_map/ppermute | solution.py:28
  28.0 8.4 %collective-permute-start.1 = (f32[3,4,1280]{2,1,0:T(4,128)S(1)}, f32[3,4,1280]{2,1,0:T(4,128)S(1)}, u32[]{:S(2)}, u32[]{:S(2)}) collective-permute-start(f32[3,4,1280]{2,1,0:T(4,128)S(1)} %get-tuple-element.37), channel_id=1, source_target_pairs={{0,8},{4,12},{8,0},{12,4},{1,9},{5,13},{9,1},{13,5},{2,10},{6,14},... | collective-permute-start | bytes 184328 | tf_op jit(solution)/shard_map/ppermute | solution.py:28
  29.9 6.5 %collective-permute-start.2 = (f32[3,4,1280]{2,1,0:T(4,128)S(1)}, f32[3,4,1280]{2,1,0:T(4,128)S(1)}, u32[]{:S(2)}, u32[]{:S(2)}) collective-permute-start(f32[3,4,1280]{2,1,0:T(4,128)S(1)} %get-tuple-element.38), channel_id=1, source_target_pairs={{0,12},{4,0},{8,4},{12,8},{1,13},{5,1},{9,5},{13,9},{2,14},{6,2},{... | collective-permute-start | bytes 184328 | tf_op jit(solution)/shard_map/ppermute | solution.py:28
  36.4 6.4 %slice-start = ((s8[5898240]{0:T(1024)(128)(4,1)}), s8[4194304]{0:T(1024)(128)(4,1)S(1)}, s32[]{:S(2)}) async-start(s8[5898240]{0:T(1024)(128)(4,1)} %bitcast.122), calls=%async_computation | async-start | bytes 8388608
  41.3 10.2 %collective-permute-start.9 = (f16[3,128,384]{2,1,0:T(8,128)(2,1)}, f16[3,128,384]{2,1,0:T(8,128)(2,1)}, u32[]{:S(2)}, u32[]{:S(2)}) collective-permute-start(f16[3,128,384]{2,1,0:T(8,128)(2,1)} %select_convert_fusion.9), channel_id=1, source_target_pairs={{0,4},{4,0},{8,12},{12,8},{1,5},{5,1},{9,13},{13,9},{2,6},{6,2},{1... | collective-permute-start | bytes 884744 | tf_op jit(solution)/shard_map/ppermute | solution.py:464
  45.6 12.2 %collective-permute-start.22 = (f16[3,128,384]{2,1,0:T(8,128)(2,1)}, f16[3,128,384]{2,1,0:T(8,128)(2,1)S(1)}, u32[]{:S(2)}, u32[]{:S(2)}) collective-permute-start(f16[3,128,384]{2,1,0:T(8,128)(2,1)} %select_convert_fusion.4), channel_id=1, source_target_pairs={{0,4},{4,0},{8,12},{12,8},{1,5},{5,1},{9,13},{13,9},{2,6},{6,2},{1... | collective-permute-start | bytes 884744 | tf_op jit(solution)/shard_map/ppermute | solution.py:464
  46.8 25.7 %collective-permute-start.35 = (bf16[640,768]{1,0:T(8,128)(2,1)S(1)}, bf16[640,768]{1,0:T(8,128)(2,1)S(1)}, u32[]{:S(2)}, u32[]{:S(2)}) collective-permute-start(bf16[640,768]{1,0:T(8,128)(2,1)S(1)} %get-tuple-element.59), channel_id=1, source_target_pairs={{0,1},{1,0},{2,3},{3,2},{4,5},{5,4},{6,7},{7,6},{8,9},{9,8},{10,11... | collective-permute-start | bytes 2949128 | tf_op jit(solution)/shard_map/ppermute | solution.py:28
  46.9 23.5 %copy-start.4 = (f32[4,3,128,384]{3,2,1,0:T(8,128)S(1)}, f32[4,3,128,384]{3,2,1,0:T(8,128)}, u32[]{:S(2)}) copy-start(f32[4,3,128,384]{3,2,1,0:T(8,128)} %copy-done.3) | copy-start | bytes 7077892
  52.9 11.1 %collective-permute-start.10 = (f16[3,128,384]{2,1,0:T(8,128)(2,1)S(1)}, f16[3,128,384]{2,1,0:T(8,128)(2,1)S(1)}, u32[]{:S(2)}, u32[]{:S(2)}) collective-permute-start(f16[3,128,384]{2,1,0:T(8,128)(2,1)S(1)} %get-tuple-element.72), channel_id=1, source_target_pairs={{0,4},{4,0},{8,12},{12,8},{1,5},{5,1},{9,13},{13,9},{2,6},{6,2},{1... | collective-permute-start | bytes 884744 | tf_op jit(solution)/shard_map/ppermute | solution.py:464
  54.5 11.1 %collective-permute-start.11 = (f16[3,128,384]{2,1,0:T(8,128)(2,1)S(1)}, f16[3,128,384]{2,1,0:T(8,128)(2,1)S(1)}, u32[]{:S(2)}, u32[]{:S(2)}) collective-permute-start(f16[3,128,384]{2,1,0:T(8,128)(2,1)S(1)} %get-tuple-element.71), channel_id=1, source_target_pairs={{0,1},{1,0},{4,8},{5,9},{8,4},{9,5},{12,13},{13,12},{2,3},{3,2},{6... | collective-permute-start | bytes 884744 | tf_op jit(solution)/shard_map/ppermute | solution.py:466
  59.1 11.3 %collective-permute-start.23 = (f16[3,128,384]{2,1,0:T(8,128)(2,1)S(1)}, f16[3,128,384]{2,1,0:T(8,128)(2,1)S(1)}, u32[]{:S(2)}, u32[]{:S(2)}) collective-permute-start(f16[3,128,384]{2,1,0:T(8,128)(2,1)S(1)} %get-tuple-element.70), channel_id=1, source_target_pairs={{0,4},{4,0},{8,12},{12,8},{1,5},{5,1},{9,13},{13,9},{2,6},{6,2},{1... | collective-permute-start | bytes 884744 | tf_op jit(solution)/shard_map/ppermute | solution.py:464
  60.6 9.8 %collective-permute-start.24 = (f16[3,128,384]{2,1,0:T(8,128)(2,1)S(1)}, f16[3,128,384]{2,1,0:T(8,128)(2,1)S(1)}, u32[]{:S(2)}, u32[]{:S(2)}) collective-permute-start(f16[3,128,384]{2,1,0:T(8,128)(2,1)S(1)} %get-tuple-element.69), channel_id=1, source_target_pairs={{0,1},{1,0},{4,8},{5,9},{8,4},{9,5},{12,13},{13,12},{2,3},{3,2},{6... | collective-permute-start | bytes 884744 | tf_op jit(solution)/shard_map/ppermute | solution.py:466
  64.1 8.4 %copy-start.6 = (f32[2,768]{1,0:T(2,128)S(1)}, f32[2,768]{1,0:T(2,128)}, u32[]{:S(2)}) copy-start(f32[2,768]{1,0:T(2,128)} %param.9) | copy-start | bytes 18436
  64.1 47.6 %collective-permute-start.36 = (bf16[640,768]{1,0:T(8,128)(2,1)S(1)}, bf16[640,768]{1,0:T(8,128)(2,1)S(1)}, u32[]{:S(2)}, u32[]{:S(2)}) collective-permute-start(bf16[640,768]{1,0:T(8,128)(2,1)S(1)} %get-tuple-element.58.refs_16_), channel_id=1, source_target_pairs={{0,2},{2,0},{1,3},{3,1},{4,6},{6,4},{5,7},{7,5},{8,10},{10,8},{9,1... | collective-permute-start | bytes 2949128 | tf_op jit(solution)/shard_map/ppermute | solution.py:28
  67.1 9.4 %collective-permute-start.12 = (f16[3,128,384]{2,1,0:T(8,128)(2,1)S(1)}, f16[3,128,384]{2,1,0:T(8,128)(2,1)S(1)}, u32[]{:S(2)}, u32[]{:S(2)}) collective-permute-start(f16[3,128,384]{2,1,0:T(8,128)(2,1)S(1)} %get-tuple-element.68), channel_id=1, source_target_pairs={{0,4},{4,0},{8,12},{12,8},{1,5},{5,1},{9,13},{13,9},{2,6},{6,2},{1... | collective-permute-start | bytes 884744 | tf_op jit(solution)/shard_map/ppermute | solution.py:464
  70.4 7.6 %collective-permute-start.13 = (f16[3,128,384]{2,1,0:T(8,128)(2,1)S(1)}, f16[3,128,384]{2,1,0:T(8,128)(2,1)S(1)}, u32[]{:S(2)}, u32[]{:S(2)}) collective-permute-start(f16[3,128,384]{2,1,0:T(8,128)(2,1)S(1)} %get-tuple-element.67), channel_id=1, source_target_pairs={{0,1},{1,0},{4,8},{5,9},{8,4},{9,5},{12,13},{13,12},{2,3},{3,2},{6... | collective-permute-start | bytes 884744 | tf_op jit(solution)/shard_map/ppermute | solution.py:466
  70.7 10.8 %collective-permute-start.25 = (f16[3,128,384]{2,1,0:T(8,128)(2,1)S(1)}, f16[3,128,384]{2,1,0:T(8,128)(2,1)S(1)}, u32[]{:S(2)}, u32[]{:S(2)}) collective-permute-start(f16[3,128,384]{2,1,0:T(8,128)(2,1)S(1)} %get-tuple-element.66), channel_id=1, source_target_pairs={{0,4},{4,0},{8,12},{12,8},{1,5},{5,1},{9,13},{13,9},{2,6},{6,2},{1... | collective-permute-start | bytes 884744 | tf_op jit(solution)/shard_map/ppermute | solution.py:464
  72.5 9.0 %collective-permute-start.26 = (f16[3,128,384]{2,1,0:T(8,128)(2,1)S(1)}, f16[3,128,384]{2,1,0:T(8,128)(2,1)S(1)}, u32[]{:S(2)}, u32[]{:S(2)}) collective-permute-start(f16[3,128,384]{2,1,0:T(8,128)(2,1)S(1)} %get-tuple-element.65), channel_id=1, source_target_pairs={{0,1},{1,0},{4,8},{5,9},{8,4},{9,5},{12,13},{13,12},{2,3},{3,2},{6... | collective-permute-start | bytes 884744 | tf_op jit(solution)/shard_map/ppermute | solution.py:466
  76.5 53.5 %collective-permute-start.37 = (bf16[640,768]{1,0:T(8,128)(2,1)S(1)}, bf16[640,768]{1,0:T(8,128)(2,1)S(1)}, u32[]{:S(2)}, u32[]{:S(2)}) collective-permute-start(bf16[640,768]{1,0:T(8,128)(2,1)S(1)} %collective-permute-done.35.refs_17_), channel_id=1, source_target_pairs={{0,2},{2,0},{1,3},{3,1},{4,6},{6,4},{5,7},{7,5},{8,10},{10,8},{9,1... | collective-permute-start | bytes 2949128 | tf_op jit(solution)/shard_map/ppermute | solution.py:28
  80.2 27.2 %collective-permute-start.14 = (bf16[1,64,384]{2,1,0:T(8,128)(2,1)S(1)}, bf16[1,64,384]{2,1,0:T(8,128)(2,1)S(1)}, u32[]{:S(2)}, u32[]{:S(2)}) collective-permute-start(bf16[1,64,384]{2,1,0:T(8,128)(2,1)S(1)} %get-tuple-element.51), channel_id=1, source_target_pairs={{0,2},{2,0},{1,3},{3,1},{4,6},{6,4},{5,7},{7,5},{8,10},{10,8},{9,1... | collective-permute-start | bytes 147464 | tf_op jit(solution)/shard_map/ppermute | solution.py:28
  82.6 27.0 %collective-permute-start.27 = (bf16[1,64,384]{2,1,0:T(8,128)(2,1)S(1)}, bf16[1,64,384]{2,1,0:T(8,128)(2,1)S(1)}, u32[]{:S(2)}, u32[]{:S(2)}) collective-permute-start(bf16[1,64,384]{2,1,0:T(8,128)(2,1)S(1)} %get-tuple-element.57), channel_id=1, source_target_pairs={{0,2},{2,0},{1,3},{3,1},{4,6},{6,4},{5,7},{7,5},{8,10},{10,8},{9,1... | collective-permute-start | bytes 147464 | tf_op jit(solution)/shard_map/ppermute | solution.py:28
  107.5 5.8 %collective-permute-start.15 = (bf16[2,1,64,384]{3,2,1,0:T(8,128)(2,1)S(1)}, bf16[2,1,64,384]{3,2,1,0:T(8,128)(2,1)S(1)}, u32[]{:S(2)}, u32[]{:S(2)}) collective-permute-start(bf16[2,1,64,384]{3,2,1,0:T(8,128)(2,1)S(1)} %pad_maximum_fusion.1.refs_0_), channel_id=1, source_target_pairs={{0,1},{1,0},{2,3},{3,2},{4,5},{5,4},{6,7},{7,6},{8,9},{9,8},{10,11... | collective-permute-start | bytes 294920 | tf_op jit(solution)/shard_map/ppermute | solution.py:28
  107.5 7.6 %collective-permute-start.16 = (bf16[2,1,64,384]{3,2,1,0:T(8,128)(2,1)S(1)}, bf16[2,1,64,384]{3,2,1,0:T(8,128)(2,1)S(1)}, u32[]{:S(2)}, u32[]{:S(2)}) collective-permute-start(bf16[2,1,64,384]{3,2,1,0:T(8,128)(2,1)S(1)} %pad_maximum_fusion.1.refs_0_), channel_id=1, source_target_pairs={{0,4},{4,8},{8,12},{12,0},{1,5},{5,9},{9,13},{13,1},{2,6},{6,10},{... | collective-permute-start | bytes 294920 | tf_op jit(solution)/shard_map/ppermute | solution.py:28
  109.6 9.5 %collective-permute-start.18 = (bf16[2,1,64,384]{3,2,1,0:T(8,128)(2,1)S(1)}, bf16[2,1,64,384]{3,2,1,0:T(8,128)(2,1)S(1)}, u32[]{:S(2)}, u32[]{:S(2)}) collective-permute-start(bf16[2,1,64,384]{3,2,1,0:T(8,128)(2,1)S(1)} %pad_maximum_fusion.1.refs_0_), channel_id=1, source_target_pairs={{0,8},{4,12},{8,0},{12,4},{1,9},{5,13},{9,1},{13,5},{2,10},{6,14},... | collective-permute-start | bytes 294920 | tf_op jit(solution)/shard_map/ppermute | solution.py:28
  111.7 8.2 %collective-permute-start.20 = (bf16[2,1,64,384]{3,2,1,0:T(8,128)(2,1)S(1)}, bf16[2,1,64,384]{3,2,1,0:T(8,128)(2,1)S(1)}, u32[]{:S(2)}, u32[]{:S(2)}) collective-permute-start(bf16[2,1,64,384]{3,2,1,0:T(8,128)(2,1)S(1)} %pad_maximum_fusion.1.refs_0_), channel_id=1, source_target_pairs={{0,12},{4,0},{8,4},{12,8},{1,13},{5,1},{9,5},{13,9},{2,14},{6,2},{... | collective-permute-start | bytes 294920 | tf_op jit(solution)/shard_map/ppermute | solution.py:28
  113.2 9.9 %collective-permute-start.28 = (bf16[2,1,64,384]{3,2,1,0:T(8,128)(2,1)S(1)}, bf16[2,1,64,384]{3,2,1,0:T(8,128)(2,1)S(1)}, u32[]{:S(2)}, u32[]{:S(2)}) collective-permute-start(bf16[2,1,64,384]{3,2,1,0:T(8,128)(2,1)S(1)} %pad_maximum_fusion.2.refs_8_), channel_id=1, source_target_pairs={{0,1},{1,0},{2,3},{3,2},{4,5},{5,4},{6,7},{7,6},{8,9},{9,8},{10,11... | collective-permute-start | bytes 294920 | tf_op jit(solution)/shard_map/ppermute | solution.py:28
  115.2 8.0 %collective-permute-start.29 = (bf16[2,1,64,384]{3,2,1,0:T(8,128)(2,1)S(1)}, bf16[2,1,64,384]{3,2,1,0:T(8,128)(2,1)S(1)}, u32[]{:S(2)}, u32[]{:S(2)}) collective-permute-start(bf16[2,1,64,384]{3,2,1,0:T(8,128)(2,1)S(1)} %pad_maximum_fusion.2.refs_8_), channel_id=1, source_target_pairs={{0,4},{4,8},{8,12},{12,0},{1,5},{5,9},{9,13},{13,1},{2,6},{6,10},{... | collective-permute-start | bytes 294920 | tf_op jit(solution)/shard_map/ppermute | solution.py:28
  119.1 8.2 %collective-permute-start.31 = (bf16[2,1,64,384]{3,2,1,0:T(8,128)(2,1)S(1)}, bf16[2,1,64,384]{3,2,1,0:T(8,128)(2,1)S(1)}, u32[]{:S(2)}, u32[]{:S(2)}) collective-permute-start(bf16[2,1,64,384]{3,2,1,0:T(8,128)(2,1)S(1)} %pad_maximum_fusion.2.refs_8_), channel_id=1, source_target_pairs={{0,8},{4,12},{8,0},{12,4},{1,9},{5,13},{9,1},{13,5},{2,10},{6,14},... | collective-permute-start | bytes 294920 | tf_op jit(solution)/shard_map/ppermute | solution.py:28
  119.9 8.4 %collective-permute-start.33 = (bf16[2,1,64,384]{3,2,1,0:T(8,128)(2,1)S(1)}, bf16[2,1,64,384]{3,2,1,0:T(8,128)(2,1)S(1)}, u32[]{:S(2)}, u32[]{:S(2)}) collective-permute-start(bf16[2,1,64,384]{3,2,1,0:T(8,128)(2,1)S(1)} %pad_maximum_fusion.2.refs_8_), channel_id=1, source_target_pairs={{0,12},{4,0},{8,4},{12,8},{1,13},{5,1},{9,5},{13,9},{2,14},{6,2},{... | collective-permute-start | bytes 294920 | tf_op jit(solution)/shard_map/ppermute | solution.py:28
  123.1 5.1 %collective-permute-start.17 = (bf16[2,1,64,384]{3,2,1,0:T(8,128)(2,1)S(1)}, bf16[2,1,64,384]{3,2,1,0:T(8,128)(2,1)S(1)}, u32[]{:S(2)}, u32[]{:S(2)}) collective-permute-start(bf16[2,1,64,384]{3,2,1,0:T(8,128)(2,1)S(1)} %collective-permute-done.16.refs_2_), channel_id=1, source_target_pairs={{0,1},{1,0},{2,3},{3,2},{4,5},{5,4},{6,7},{7,6},{8,9},{9,8},{10,11... | collective-permute-start | bytes 294920 | tf_op jit(solution)/shard_map/ppermute | solution.py:28
  123.2 5.6 %collective-permute-start.19 = (bf16[2,1,64,384]{3,2,1,0:T(8,128)(2,1)S(1)}, bf16[2,1,64,384]{3,2,1,0:T(8,128)(2,1)S(1)}, u32[]{:S(2)}, u32[]{:S(2)}) collective-permute-start(bf16[2,1,64,384]{3,2,1,0:T(8,128)(2,1)S(1)} %collective-permute-done.18.refs_4_), channel_id=1, source_target_pairs={{0,1},{1,0},{2,3},{3,2},{4,5},{5,4},{6,7},{7,6},{8,9},{9,8},{10,11... | collective-permute-start | bytes 294920 | tf_op jit(solution)/shard_map/ppermute | solution.py:28
  127.4 1.5 %collective-permute-start.21 = (bf16[2,1,64,384]{3,2,1,0:T(8,128)(2,1)S(1)}, bf16[2,1,64,384]{3,2,1,0:T(8,128)(2,1)S(1)}, u32[]{:S(2)}, u32[]{:S(2)}) collective-permute-start(bf16[2,1,64,384]{3,2,1,0:T(8,128)(2,1)S(1)} %collective-permute-done.20.refs_6_), channel_id=1, source_target_pairs={{0,1},{1,0},{2,3},{3,2},{4,5},{5,4},{6,7},{7,6},{8,9},{9,8},{10,11... | collective-permute-start | bytes 294920 | tf_op jit(solution)/shard_map/ppermute | solution.py:28
  128.2 1.3 collective-permute-start.30
  128.2 1.5 collective-permute-start.32
  128.8 1.3 collective-permute-start.34
  131.6 5.9 %collective-permute-start.39 = (bf16[1,64,640]{2,1,0:T(8,128)(2,1)S(1)}, bf16[1,64,640]{2,1,0:T(8,128)(2,1)S(1)}, u32[]{:S(2)}, u32[]{:S(2)}) collective-permute-start(bf16[1,64,640]{2,1,0:T(8,128)(2,1)S(1)} %get-tuple-element.62), channel_id=1, source_target_pairs={{0,12},{4,0},{8,4},{12,8},{1,13},{5,1},{9,5},{13,9},{2,14},{6,2},{... | collective-permute-start | bytes 245768 | tf_op jit(solution)/shard_map/ppermute | solution.py:28
  134.6 8.2 %collective-permute-start.41 = (bf16[1,64,640]{2,1,0:T(8,128)(2,1)S(1)}, bf16[1,64,640]{2,1,0:T(8,128)(2,1)S(1)}, u32[]{:S(2)}, u32[]{:S(2)}) collective-permute-start(bf16[1,64,640]{2,1,0:T(8,128)(2,1)S(1)} %get-tuple-element.63), channel_id=1, source_target_pairs={{0,8},{4,12},{8,0},{12,4},{1,9},{5,13},{9,1},{13,5},{2,10},{6,14},... | collective-permute-start | bytes 245768 | tf_op jit(solution)/shard_map/ppermute | solution.py:28
  134.7 8.2 %collective-permute-start.43 = (bf16[1,64,640]{2,1,0:T(8,128)(2,1)S(1)}, bf16[1,64,640]{2,1,0:T(8,128)(2,1)S(1)}, u32[]{:S(2)}, u32[]{:S(2)}) collective-permute-start(bf16[1,64,640]{2,1,0:T(8,128)(2,1)S(1)} %get-tuple-element.64), channel_id=1, source_target_pairs={{0,4},{4,8},{8,12},{12,0},{1,5},{5,9},{9,13},{13,1},{2,6},{6,10},{... | collective-permute-start | bytes 245768 | tf_op jit(solution)/shard_map/ppermute | solution.py:28
  135.3 8.1 %collective-permute-start.38 = (bf16[1,64,640]{2,1,0:T(8,128)(2,1)S(1)}, bf16[1,64,640]{2,1,0:T(8,128)(2,1)S(1)}, u32[]{:S(2)}, u32[]{:S(2)}) collective-permute-start(bf16[1,64,640]{2,1,0:T(8,128)(2,1)S(1)} %get-tuple-element.61), channel_id=1, source_target_pairs={{0,1},{1,0},{2,3},{3,2},{4,5},{5,4},{6,7},{7,6},{8,9},{9,8},{10,11... | collective-permute-start | bytes 245768 | tf_op jit(solution)/shard_map/ppermute | solution.py:28
  137.5 5.9 %collective-permute-start.40 = (bf16[1,64,640]{2,1,0:T(8,128)(2,1)S(1)}, bf16[1,64,640]{2,1,0:T(8,128)(2,1)S(1)}, u32[]{:S(2)}, u32[]{:S(2)}) collective-permute-start(bf16[1,64,640]{2,1,0:T(8,128)(2,1)S(1)} %collective-permute-done.39.refs_2_), channel_id=1, source_target_pairs={{0,1},{1,0},{2,3},{3,2},{4,5},{5,4},{6,7},{7,6},{8,9},{9,8},{10,11... | collective-permute-start | bytes 245768 | tf_op jit(solution)/shard_map/ppermute | solution.py:28
  142.9 1.3 collective-permute-start.42
  142.9 1.4 collective-permute-start.44
  (6 other events, 18.7 us)

commit v8 on v7

--- a/solution.py
+++ b/solution.py
@@ -12,6 +12,7 @@
 FREQ = 256
 STEPS = 100
 LANES = 128
+DMA_PIECES = 4
 
 
 sample_shift = 5.0
@@ -201,10 +202,19 @@
 def modulate_kernel(n_tm, n_seq, n_mp, cuts, step_ref, w_ref, *refs):
     shares, rows = refs[:n_tm], refs[n_tm : n_tm + n_seq * n_mp]
     hidden_ref, coef_ref, *w_outs, mod_scr, sems = refs[n_tm + n_seq * n_mp :]
-    copies = [
-        pltpu.make_async_copy(w_ref.at[:, :, pl.ds(lane, size)], out, sems.at[h])
-        for h, ((lane, size), out) in enumerate(zip(cuts, w_outs))
-    ]
+    stride = w_ref.shape[1] // DMA_PIECES
+    copies = []
+    for (lane, size), out in zip(cuts, w_outs):
+        for c in range(w_ref.shape[0]):
+            for piece in range(DMA_PIECES):
+                rows_here = pl.ds(piece * stride, stride)
+                copies.append(
+                    pltpu.make_async_copy(
+                        w_ref.at[c, rows_here, pl.ds(lane, size)],
+                        out.at[c, rows_here],
+                        sems.at[len(copies)],
+                    )
+                )
     z, k = lax.axis_index("tm"), pl.program_id(0)
     _, frames, part, wide = rows[0].shape
     depth = wide - LANES
@@ -243,6 +253,7 @@
 def modulate(start_step, w_qkv, cuts, shares, rows):
     n_tm, n_seq, n_mp = len(shares), len(rows), len(rows[0])
     _, frames, part, wide = rows[0][0].shape
+    three = w_qkv.shape[0]
     depth = wide - LANES
     window = shares[0].shape[1]
     shape = (n_tm, n_seq, frames, n_mp * part, depth)
@@ -259,7 +270,7 @@
         + [pl.BlockSpec(memory_space=pl.ANY)] * len(cuts),
         scratch_shapes=[
             pltpu.VMEM((3, window, depth), jnp.float32),
-            pltpu.SemaphoreType.DMA((len(cuts),)),
+            pltpu.SemaphoreType.DMA((len(cuts) * three * DMA_PIECES,)),
         ],
         out_shape=[
             jax.ShapeDtypeStruct(shape, jnp.bfloat16),

time: 146 us -> 146 us (level)
  no operation moved by 1% of the time
where the time goes in v8:
time: 146 us; the launch traced here: 145 us
  waiting for transfers between devices  80.7 us (55%)
  starting transfers between devices  41.1 us (28%)
  Pallas kernels  8.48 us (6%)
  other arithmetic  7.72 us (5%)
  matrix products  3.83 us (3%)
  local copies, waits for them, and re-layouts  2.67 us (2%)
    ppermute x35, waiting for transfers between devices, turn(): lax.ppermute(block, axis, [(i, (i + distance) % size) for i in range(size)])  62.8 us
    ppermute x35, starting transfers between devices, turn(): lax.ppermute(block, axis, [(i, (i + distance) % size) for i in range(size)])  32.7 us
    ppermute x6, waiting for transfers between devices, sweep(): first = lax.ppermute(first, 'tm', evens)  17.8 us
    ppermute x6, starting transfers between devices, sweep(): first = lax.ppermute(first, 'tm', evens)  8.48 us
    convert_element_type x4, other arithmetic, sweep(): second = jnp.where(even, left, right).astype(jnp.float16)  4.51 us
    dot_general x2, matrix products, sweep(): jnp.einsum('krd,cdh->kcrh', hidden, part_qkv, preferred_element_type=jnp....  3.83 us
  transfers between devices with their start and end apart: 45, of which 23 were waited for; matrix products, arithmetic and copies ran while one was open for 6% of the time, Pallas kernels for 2%

profile of v8, /device:TPU:0, one launch (start us, length us, event | category | flops | bytes accessed | tf_op | source)
XLA Modules:
  0.0 145.4 jit_solution(10010951356615501422)
XLA Ops:
  0.0 1.1 copy-done.2
  1.5 5.1 %collective-permute-start.5 = (bf16[1,32,1408]{2,1,0:T(8,128)(2,1)S(1)}, bf16[1,32,1408]{2,1,0:T(8,128)(2,1)S(1)}, u32[]{:S(2)}, u32[]{:S(2)}) collective-permute-start(bf16[1,32,1408]{2,1,0:T(8,128)(2,1)S(1)} %get-tuple-element.42), channel_id=1, source_target_pairs={{0,12},{4,0},{8,4},{12,8},{1,13},{5,1},{9,5},{13,9},{2,14},{6,2},{... | collective-permute-start | bytes 270344 | tf_op jit(solution)/shard_map/ppermute | solution.py:29
  6.6 1.0 collective-permute-start.3
  7.6 2.0 %collective-permute-done.5 = bf16[1,32,1408]{2,1,0:T(8,128)(2,1)S(1)} collective-permute-done((bf16[1,32,1408]{2,1,0:T(8,128)(2,1)S(1)}, bf16[1,32,1408]{2,1,0:T(8,128)(2,1)S(1)}, u32[]{:S(2)}, u32[]{:S(2)}) %collective-permute-start.5) | collective-permute-done | bytes 90144 | tf_op jit(solution)/shard_map/ppermute | solution.py:29
  9.6 5.1 %collective-permute-done.4 = bf16[1,32,1408]{2,1,0:T(8,128)(2,1)S(1)} collective-permute-done((bf16[1,32,1408]{2,1,0:T(8,128)(2,1)S(1)}, bf16[1,32,1408]{2,1,0:T(8,128)(2,1)S(1)}, u32[]{:S(2)}, u32[]{:S(2)}) %collective-permute-start.4) | collective-permute-done | bytes 90144 | tf_op jit(solution)/shard_map/ppermute | solution.py:29
  14.8 1.6 %collective-permute-start.7 = (bf16[4,1,32,1408]{3,2,1,0:T(8,128)(2,1)S(1)}, bf16[4,1,32,1408]{3,2,1,0:T(8,128)(2,1)S(1)}, u32[]{:S(2)}, u32[]{:S(2)}) collective-permute-start(bf16[4,1,32,1408]{3,2,1,0:T(8,128)(2,1)S(1)} %pad_maximum_fusion.refs_4_), channel_id=1, source_target_pairs={{0,2},{2,0},{1,3},{3,1},{4,6},{6,4},{5,7},{7,5},{8,10},{10,8},{9,1... | collective-permute-start | bytes 1081352 | tf_op jit(solution)/shard_map/ppermute | solution.py:29
  16.4 8.5 %collective-permute-done.7.refs_6_ = bf16[4,1,32,1408]{3,2,1,0:T(8,128)(2,1)S(1)} collective-permute-done((bf16[4,1,32,1408]{3,2,1,0:T(8,128)(2,1)S(1)}, bf16[4,1,32,1408]{3,2,1,0:T(8,128)(2,1)S(1)}, u32[]{:S(2)}, u32[]{:S(2)}) %collective-permute-start.7) | collective-permute-done | bytes 360480 | tf_op jit(solution)/shard_map/ppermute | solution.py:29
  25.5 1.5 %copy-done = bf16[64,15360]{1,0:T(8,128)(2,1)S(1)} copy-done((bf16[64,15360]{1,0:T(8,128)(2,1)S(1)}, bf16[64,15360]{1,0:T(8,128)(2,1)}, u32[]{:S(2)}) %copy-start) | copy-done | bytes 1966104
  28.0 1.9 %collective-permute-start.1 = (f32[3,4,1280]{2,1,0:T(4,128)S(1)}, f32[3,4,1280]{2,1,0:T(4,128)S(1)}, u32[]{:S(2)}, u32[]{:S(2)}) collective-permute-start(f32[3,4,1280]{2,1,0:T(4,128)S(1)} %get-tuple-element.37), channel_id=1, source_target_pairs={{0,8},{4,12},{8,0},{12,4},{1,9},{5,13},{9,1},{13,5},{2,10},{6,14},... | collective-permute-start | bytes 184328 | tf_op jit(solution)/shard_map/ppermute | solution.py:29
  29.9 2.8 %collective-permute-start.2 = (f32[3,4,1280]{2,1,0:T(4,128)S(1)}, f32[3,4,1280]{2,1,0:T(4,128)S(1)}, u32[]{:S(2)}, u32[]{:S(2)}) collective-permute-start(f32[3,4,1280]{2,1,0:T(4,128)S(1)} %get-tuple-element.38), channel_id=1, source_target_pairs={{0,12},{4,0},{8,4},{12,8},{1,13},{5,1},{9,5},{13,9},{2,14},{6,2},{... | collective-permute-start | bytes 184328 | tf_op jit(solution)/shard_map/ppermute | solution.py:29
  32.7 2.1 %collective-permute-done.refs_1_ = f32[3,4,1280]{2,1,0:T(4,128)S(1)} collective-permute-done((f32[3,4,1280]{2,1,0:T(4,128)S(1)}, f32[3,4,1280]{2,1,0:T(4,128)S(1)}, u32[]{:S(2)}, u32[]{:S(2)}) %collective-permute-start) | collective-permute-done | bytes 61472 | tf_op jit(solution)/shard_map/ppermute | solution.py:29
  34.7 1.6 %collective-permute-done.1.refs_2_ = f32[3,4,1280]{2,1,0:T(4,128)S(1)} collective-permute-done((f32[3,4,1280]{2,1,0:T(4,128)S(1)}, f32[3,4,1280]{2,1,0:T(4,128)S(1)}, u32[]{:S(2)}, u32[]{:S(2)}) %collective-permute-start.1) | collective-permute-done | bytes 61472 | tf_op jit(solution)/shard_map/ppermute | solution.py:29
  36.4 2.2 %modulate.1 = (bf16[4,2,1,64,1280]{4,3,2,1,0:T(8,128)(2,1)S(1)}, f32[4,1,1280]{2,1,0:T(1,128)S(1)}, bf16[3,1280,384]{2,1,0:T(8,128)(2,1)S(1)}) custom-call(s32[1]{0:T(128)S(6)} %copy.15.step_ref, bf16[3,1280,768]{2,1,0:T(8,128)(2,1)} %w_ref.2, f32[3,4,1280]{2,1,0:T(4,128)S(1)} %get-tuple-element.35.refs_0_, f32[3,4,1280]{2,1,0:T(4,128)S(1)} %collective-permute-done.refs_1_, ...), custom_call_target="tpu_custom_call" | custom-call | flops 2621440 | bytes 2621440 | tf_op jit(solution)/shard_map/modulate/pallas_call | solution.py:260
  38.6 2.0 %fusion.8 = f32[4,3,128,384]{3,2,0,1:T(8,128)S(1)} fusion(bf16[4,128,1280,1]{2,1,0,3:T(8,128)(2,1)S(1)} %bitcast.120, bf16[3,1280,384]{2,1,0:T(8,128)(2,1)S(1)} %get-tuple-element.44), kind=kOutput, calls=%fused_computation.6 | convolution fusion | flops 1509949440 | bytes 6619136 | tf_op jit(solution)/shard_map/krd,cdh->kcrh/dot_general | solution.py:444
  41.5 1.5 %collective-permute-start.9 = (f16[3,128,384]{2,1,0:T(8,128)(2,1)}, f16[3,128,384]{2,1,0:T(8,128)(2,1)}, u32[]{:S(2)}, u32[]{:S(2)}) collective-permute-start(f16[3,128,384]{2,1,0:T(8,128)(2,1)} %select_convert_fusion.9), channel_id=1, source_target_pairs={{0,4},{4,0},{8,12},{12,8},{1,5},{5,1},{9,13},{13,9},{2,6},{6,2},{1... | collective-permute-start | bytes 884744 | tf_op jit(solution)/shard_map/ppermute | solution.py:475
  43.0 1.9 %fusion.5 = f32[4,3,128,384]{3,2,1,0:T(8,128)S(1)} fusion(bf16[4,128,1280,1]{2,1,3,0:T(8,128)(2,1)S(1)} %bitcast.121, bf16[3,1280,768]{2,1,0:T(8,128)(2,1)S(1)} %bitcast.123), kind=kOutput, calls=%fused_computation.5 | convolution fusion | flops 1509949440 | bytes 6619136 | tf_op jit(solution)/shard_map/krd,cdh->kcrh/dot_general | solution.py:444
  47.0 4.7 %collective-permute-done.9 = f16[3,128,384]{2,1,0:T(8,128)(2,1)} collective-permute-done((f16[3,128,384]{2,1,0:T(8,128)(2,1)}, f16[3,128,384]{2,1,0:T(8,128)(2,1)}, u32[]{:S(2)}, u32[]{:S(2)}) %collective-permute-start.9) | collective-permute-done | bytes 294944 | tf_op jit(solution)/shard_map/ppermute | solution.py:475
  51.7 1.4 select_convert_fusion.7
  53.1 1.5 %collective-permute-start.10 = (f16[3,128,384]{2,1,0:T(8,128)(2,1)S(1)}, f16[3,128,384]{2,1,0:T(8,128)(2,1)S(1)}, u32[]{:S(2)}, u32[]{:S(2)}) collective-permute-start(f16[3,128,384]{2,1,0:T(8,128)(2,1)S(1)} %get-tuple-element.72), channel_id=1, source_target_pairs={{0,4},{4,0},{8,12},{12,8},{1,5},{5,1},{9,13},{13,9},{2,6},{6,2},{1... | collective-permute-start | bytes 884744 | tf_op jit(solution)/shard_map/ppermute | solution.py:475
  54.6 3.3 %collective-permute-done.22 = f16[3,128,384]{2,1,0:T(8,128)(2,1)S(1)} collective-permute-done((f16[3,128,384]{2,1,0:T(8,128)(2,1)}, f16[3,128,384]{2,1,0:T(8,128)(2,1)S(1)}, u32[]{:S(2)}, u32[]{:S(2)}) %collective-permute-start.22) | collective-permute-done | bytes 294944 | tf_op jit(solution)/shard_map/ppermute | solution.py:475
  57.9 1.3 select_convert_fusion.2
  59.2 1.5 %collective-permute-start.23 = (f16[3,128,384]{2,1,0:T(8,128)(2,1)S(1)}, f16[3,128,384]{2,1,0:T(8,128)(2,1)S(1)}, u32[]{:S(2)}, u32[]{:S(2)}) collective-permute-start(f16[3,128,384]{2,1,0:T(8,128)(2,1)S(1)} %get-tuple-element.70), channel_id=1, source_target_pairs={{0,4},{4,0},{8,12},{12,8},{1,5},{5,1},{9,13},{13,9},{2,6},{6,2},{1... | collective-permute-start | bytes 884744 | tf_op jit(solution)/shard_map/ppermute | solution.py:475
  60.8 3.5 %collective-permute-done.10 = f16[3,128,384]{2,1,0:T(8,128)(2,1)S(1)} collective-permute-done((f16[3,128,384]{2,1,0:T(8,128)(2,1)S(1)}, f16[3,128,384]{2,1,0:T(8,128)(2,1)S(1)}, u32[]{:S(2)}, u32[]{:S(2)}) %collective-permute-start.10) | collective-permute-done | bytes 294944 | tf_op jit(solution)/shard_map/ppermute | solution.py:475
  64.2 1.5 %collective-permute-start.36 = (bf16[640,768]{1,0:T(8,128)(2,1)S(1)}, bf16[640,768]{1,0:T(8,128)(2,1)S(1)}, u32[]{:S(2)}, u32[]{:S(2)}) collective-permute-start(bf16[640,768]{1,0:T(8,128)(2,1)S(1)} %get-tuple-element.58.refs_16_), channel_id=1, source_target_pairs={{0,2},{2,0},{1,3},{3,1},{4,6},{6,4},{5,7},{7,5},{8,10},{10,8},{9,1... | collective-permute-start | bytes 2949128 | tf_op jit(solution)/shard_map/ppermute | solution.py:29
  65.7 1.5 %select_convert_fusion.5 = (f16[3,128,384]{2,1,0:T(8,128)(2,1)S(1)}, f16[3,128,384]{2,1,0:T(8,128)(2,1)S(1)}) fusion(pred[]{:T(512)S(6)} %eq.5, f16[3,128,384]{2,1,0:T(8,128)(2,1)S(1)} %collective-permute-done.11, f16[3,128,384]{2,1,0:T(8,128)(2,1)S(1)} %collective-permute-done.10, pred[]{:T(512)S(6)} %lt.9, f32[4,3,128,384]{3,2,0,1:T(8,128)} %copy-done.5, ...), kind=kLoop, calls=%fused_computation.56 | loop fusion | flops 1769472 | bytes 2359299 | tf_op jit(solution)/shard_map/convert_element_type | solution.py:474
  67.2 1.6 %collective-permute-start.12 = (f16[3,128,384]{2,1,0:T(8,128)(2,1)S(1)}, f16[3,128,384]{2,1,0:T(8,128)(2,1)S(1)}, u32[]{:S(2)}, u32[]{:S(2)}) collective-permute-start(f16[3,128,384]{2,1,0:T(8,128)(2,1)S(1)} %get-tuple-element.68), channel_id=1, source_target_pairs={{0,4},{4,0},{8,12},{12,8},{1,5},{5,1},{9,13},{13,9},{2,6},{6,2},{1... | collective-permute-start | bytes 884744 | tf_op jit(solution)/shard_map/ppermute | solution.py:475
  68.8 1.7 %collective-permute-done.23 = f16[3,128,384]{2,1,0:T(8,128)(2,1)S(1)} collective-permute-done((f16[3,128,384]{2,1,0:T(8,128)(2,1)S(1)}, f16[3,128,384]{2,1,0:T(8,128)(2,1)S(1)}, u32[]{:S(2)}, u32[]{:S(2)}) %collective-permute-start.23) | collective-permute-done | bytes 294944 | tf_op jit(solution)/shard_map/ppermute | solution.py:475
  70.8 1.8 %collective-permute-start.25 = (f16[3,128,384]{2,1,0:T(8,128)(2,1)S(1)}, f16[3,128,384]{2,1,0:T(8,128)(2,1)S(1)}, u32[]{:S(2)}, u32[]{:S(2)}) collective-permute-start(f16[3,128,384]{2,1,0:T(8,128)(2,1)S(1)} %get-tuple-element.66), channel_id=1, source_target_pairs={{0,4},{4,0},{8,12},{12,8},{1,5},{5,1},{9,13},{13,9},{2,6},{6,2},{1... | collective-permute-start | bytes 884744 | tf_op jit(solution)/shard_map/ppermute | solution.py:475
  72.7 4.0 %collective-permute-done.12 = f16[3,128,384]{2,1,0:T(8,128)(2,1)S(1)} collective-permute-done((f16[3,128,384]{2,1,0:T(8,128)(2,1)S(1)}, f16[3,128,384]{2,1,0:T(8,128)(2,1)S(1)}, u32[]{:S(2)}, u32[]{:S(2)}) %collective-permute-start.12) | collective-permute-done | bytes 294944 | tf_op jit(solution)/shard_map/ppermute | solution.py:475
  76.7 1.5 %collective-permute-start.37 = (bf16[640,768]{1,0:T(8,128)(2,1)S(1)}, bf16[640,768]{1,0:T(8,128)(2,1)S(1)}, u32[]{:S(2)}, u32[]{:S(2)}) collective-permute-start(bf16[640,768]{1,0:T(8,128)(2,1)S(1)} %collective-permute-done.35.refs_17_), channel_id=1, source_target_pairs={{0,2},{2,0},{1,3},{3,1},{4,6},{6,4},{5,7},{7,5},{8,10},{10,8},{9,1... | collective-permute-start | bytes 2949128 | tf_op jit(solution)/shard_map/ppermute | solution.py:29
  78.2 1.2 fusion.21
  79.4 0.9 attend.2
  81.8 0.9 attend.3
  82.8 1.6 %collective-permute-start.27 = (bf16[1,64,384]{2,1,0:T(8,128)(2,1)S(1)}, bf16[1,64,384]{2,1,0:T(8,128)(2,1)S(1)}, u32[]{:S(2)}, u32[]{:S(2)}) collective-permute-start(bf16[1,64,384]{2,1,0:T(8,128)(2,1)S(1)} %get-tuple-element.57), channel_id=1, source_target_pairs={{0,2},{2,0},{1,3},{3,1},{4,6},{6,4},{5,7},{7,5},{8,10},{10,8},{9,1... | collective-permute-start | bytes 147464 | tf_op jit(solution)/shard_map/ppermute | solution.py:29
  84.3 23.3 %collective-permute-done.14 = bf16[1,64,384]{2,1,0:T(8,128)(2,1)S(1)} collective-permute-done((bf16[1,64,384]{2,1,0:T(8,128)(2,1)S(1)}, bf16[1,64,384]{2,1,0:T(8,128)(2,1)S(1)}, u32[]{:S(2)}, u32[]{:S(2)}) %collective-permute-start.14) | collective-permute-done | bytes 49184 | tf_op jit(solution)/shard_map/ppermute | solution.py:29
  107.7 2.1 %collective-permute-start.16 = (bf16[2,1,64,384]{3,2,1,0:T(8,128)(2,1)S(1)}, bf16[2,1,64,384]{3,2,1,0:T(8,128)(2,1)S(1)}, u32[]{:S(2)}, u32[]{:S(2)}) collective-permute-start(bf16[2,1,64,384]{3,2,1,0:T(8,128)(2,1)S(1)} %pad_maximum_fusion.1.refs_0_), channel_id=1, source_target_pairs={{0,4},{4,8},{8,12},{12,0},{1,5},{5,9},{9,13},{13,1},{2,6},{6,10},{... | collective-permute-start | bytes 294920 | tf_op jit(solution)/shard_map/ppermute | solution.py:29
  109.7 2.1 %collective-permute-start.18 = (bf16[2,1,64,384]{3,2,1,0:T(8,128)(2,1)S(1)}, bf16[2,1,64,384]{3,2,1,0:T(8,128)(2,1)S(1)}, u32[]{:S(2)}, u32[]{:S(2)}) collective-permute-start(bf16[2,1,64,384]{3,2,1,0:T(8,128)(2,1)S(1)} %pad_maximum_fusion.1.refs_0_), channel_id=1, source_target_pairs={{0,8},{4,12},{8,0},{12,4},{1,9},{5,13},{9,1},{13,5},{2,10},{6,14},... | collective-permute-start | bytes 294920 | tf_op jit(solution)/shard_map/ppermute | solution.py:29
  111.8 1.5 %collective-permute-start.20 = (bf16[2,1,64,384]{3,2,1,0:T(8,128)(2,1)S(1)}, bf16[2,1,64,384]{3,2,1,0:T(8,128)(2,1)S(1)}, u32[]{:S(2)}, u32[]{:S(2)}) collective-permute-start(bf16[2,1,64,384]{3,2,1,0:T(8,128)(2,1)S(1)} %pad_maximum_fusion.1.refs_0_), channel_id=1, source_target_pairs={{0,12},{4,0},{8,4},{12,8},{1,13},{5,1},{9,5},{13,9},{2,14},{6,2},{... | collective-permute-start | bytes 294920 | tf_op jit(solution)/shard_map/ppermute | solution.py:29
  113.4 1.9 %collective-permute-done.16.refs_2_ = bf16[2,1,64,384]{3,2,1,0:T(8,128)(2,1)S(1)} collective-permute-done((bf16[2,1,64,384]{3,2,1,0:T(8,128)(2,1)S(1)}, bf16[2,1,64,384]{3,2,1,0:T(8,128)(2,1)S(1)}, u32[]{:S(2)}, u32[]{:S(2)}) %collective-permute-start.16) | collective-permute-done | bytes 98336 | tf_op jit(solution)/shard_map/ppermute | solution.py:29
  115.3 3.9 %collective-permute-done.18.refs_4_ = bf16[2,1,64,384]{3,2,1,0:T(8,128)(2,1)S(1)} collective-permute-done((bf16[2,1,64,384]{3,2,1,0:T(8,128)(2,1)S(1)}, bf16[2,1,64,384]{3,2,1,0:T(8,128)(2,1)S(1)}, u32[]{:S(2)}, u32[]{:S(2)}) %collective-permute-start.18) | collective-permute-done | bytes 98336 | tf_op jit(solution)/shard_map/ppermute | solution.py:29
  120.0 3.3 %collective-permute-start.33 = (bf16[2,1,64,384]{3,2,1,0:T(8,128)(2,1)S(1)}, bf16[2,1,64,384]{3,2,1,0:T(8,128)(2,1)S(1)}, u32[]{:S(2)}, u32[]{:S(2)}) collective-permute-start(bf16[2,1,64,384]{3,2,1,0:T(8,128)(2,1)S(1)} %pad_maximum_fusion.2.refs_8_), channel_id=1, source_target_pairs={{0,12},{4,0},{8,4},{12,8},{1,13},{5,1},{9,5},{13,9},{2,14},{6,2},{... | collective-permute-start | bytes 294920 | tf_op jit(solution)/shard_map/ppermute | solution.py:29
  123.8 3.7 %collective-permute-done.31.refs_12_ = bf16[2,1,64,384]{3,2,1,0:T(8,128)(2,1)S(1)} collective-permute-done((bf16[2,1,64,384]{3,2,1,0:T(8,128)(2,1)S(1)}, bf16[2,1,64,384]{3,2,1,0:T(8,128)(2,1)S(1)}, u32[]{:S(2)}, u32[]{:S(2)}) %collective-permute-start.31) | collective-permute-done | bytes 98336 | tf_op jit(solution)/shard_map/ppermute | solution.py:29
  127.5 0.9 collective-permute-done.33.refs_14_
  130.2 1.5 %project.1 = (f32[1,64,640]{2,1,0:T(8,128)S(1)}, bf16[1,64,640]{2,1,0:T(8,128)(2,1)S(1)}, bf16[1,64,640]{2,1,0:T(8,128)(2,1)S(1)}, bf16[1,64,640]{2,1,0:T(8,128)(2,1)S(1)}, bf16[1,64,640]{2,1,0:T(8,128)(2,1)S(1)}) custom-call(f32[4,1,1280]{2,1,0:T(1,128)S(1)} %get-tuple-element.43.coef_ref, bf16[2,1,64,384]{3,2,1,0:T(8,128)(2,1)S(1)} %pad_maximum_fusion.1.refs_0_, ...), custom_call_target="tpu_custom_call" | custom-call | flops 1006632960 | bytes 5505024 | tf_op jit(solution)/shard_map/project/pallas_call | solution.py:354
  131.7 3.0 %collective-permute-start.39 = (bf16[1,64,640]{2,1,0:T(8,128)(2,1)S(1)}, bf16[1,64,640]{2,1,0:T(8,128)(2,1)S(1)}, u32[]{:S(2)}, u32[]{:S(2)}) collective-permute-start(bf16[1,64,640]{2,1,0:T(8,128)(2,1)S(1)} %get-tuple-element.62), channel_id=1, source_target_pairs={{0,12},{4,0},{8,4},{12,8},{1,13},{5,1},{9,5},{13,9},{2,14},{6,2},{... | collective-permute-start | bytes 245768 | tf_op jit(solution)/shard_map/ppermute | solution.py:29
  135.4 2.2 %collective-permute-done.39.refs_2_ = bf16[1,64,640]{2,1,0:T(8,128)(2,1)S(1)} collective-permute-done((bf16[1,64,640]{2,1,0:T(8,128)(2,1)S(1)}, bf16[1,64,640]{2,1,0:T(8,128)(2,1)S(1)}, u32[]{:S(2)}, u32[]{:S(2)}) %collective-permute-start.39) | collective-permute-done | bytes 81952 | tf_op jit(solution)/shard_map/ppermute | solution.py:29
  137.6 5.3 %collective-permute-done.41.refs_4_ = bf16[1,64,640]{2,1,0:T(8,128)(2,1)S(1)} collective-permute-done((bf16[1,64,640]{2,1,0:T(8,128)(2,1)S(1)}, bf16[1,64,640]{2,1,0:T(8,128)(2,1)S(1)}, u32[]{:S(2)}, u32[]{:S(2)}) %collective-permute-start.41) | collective-permute-done | bytes 81952 | tf_op jit(solution)/shard_map/ppermute | solution.py:29
  144.4 1.0 finish.1
  (83 shorter events, 11.4 us)
Async XLA Ops:
  1.5 8.1 %collective-permute-start.5 = (bf16[1,32,1408]{2,1,0:T(8,128)(2,1)S(1)}, bf16[1,32,1408]{2,1,0:T(8,128)(2,1)S(1)}, u32[]{:S(2)}, u32[]{:S(2)}) collective-permute-start(bf16[1,32,1408]{2,1,0:T(8,128)(2,1)S(1)} %get-tuple-element.42), channel_id=1, source_target_pairs={{0,12},{4,0},{8,4},{12,8},{1,13},{5,1},{9,5},{13,9},{2,14},{6,2},{... | collective-permute-start | bytes 270344 | tf_op jit(solution)/shard_map/ppermute | solution.py:29
  6.6 8.1 %collective-permute-start.4 = (bf16[1,32,1408]{2,1,0:T(8,128)(2,1)S(1)}, bf16[1,32,1408]{2,1,0:T(8,128)(2,1)S(1)}, u32[]{:S(2)}, u32[]{:S(2)}) collective-permute-start(bf16[1,32,1408]{2,1,0:T(8,128)(2,1)S(1)} %get-tuple-element.41), channel_id=1, source_target_pairs={{0,8},{4,12},{8,0},{12,4},{1,9},{5,13},{9,1},{13,5},{2,10},{6,14},... | collective-permute-start | bytes 270344 | tf_op jit(solution)/shard_map/ppermute | solution.py:29
  6.6 8.1 %collective-permute-start.3 = (bf16[1,32,1408]{2,1,0:T(8,128)(2,1)S(1)}, bf16[1,32,1408]{2,1,0:T(8,128)(2,1)S(1)}, u32[]{:S(2)}, u32[]{:S(2)}) collective-permute-start(bf16[1,32,1408]{2,1,0:T(8,128)(2,1)S(1)} %get-tuple-element.40), channel_id=1, source_target_pairs={{0,4},{4,8},{8,12},{12,0},{1,5},{5,9},{9,13},{13,1},{2,6},{6,10},{... | collective-permute-start | bytes 270344 | tf_op jit(solution)/shard_map/ppermute | solution.py:29
  14.8 10.1 %collective-permute-start.7 = (bf16[4,1,32,1408]{3,2,1,0:T(8,128)(2,1)S(1)}, bf16[4,1,32,1408]{3,2,1,0:T(8,128)(2,1)S(1)}, u32[]{:S(2)}, u32[]{:S(2)}) collective-permute-start(bf16[4,1,32,1408]{3,2,1,0:T(8,128)(2,1)S(1)} %pad_maximum_fusion.refs_4_), channel_id=1, source_target_pairs={{0,2},{2,0},{1,3},{3,1},{4,6},{6,4},{5,7},{7,5},{8,10},{10,8},{9,1... | collective-permute-start | bytes 1081352 | tf_op jit(solution)/shard_map/ppermute | solution.py:29
  16.4 20.0 %collective-permute-start.6 = (bf16[4,1,32,1408]{3,2,1,0:T(8,128)(2,1)S(1)}, bf16[4,1,32,1408]{3,2,1,0:T(8,128)(2,1)S(1)}, u32[]{:S(2)}, u32[]{:S(2)}) collective-permute-start(bf16[4,1,32,1408]{3,2,1,0:T(8,128)(2,1)S(1)} %pad_maximum_fusion.refs_4_), channel_id=1, source_target_pairs={{0,1},{1,0},{2,3},{3,2},{4,5},{5,4},{6,7},{7,6},{8,9},{9,8},{10,11... | collective-permute-start | bytes 1081352 | tf_op jit(solution)/shard_map/ppermute | solution.py:29
  24.9 11.5 %collective-permute-start.8 = (bf16[4,1,32,1408]{3,2,1,0:T(8,128)(2,1)S(1)}, bf16[4,1,32,1408]{3,2,1,0:T(8,128)(2,1)S(1)}, u32[]{:S(2)}, u32[]{:S(2)}) collective-permute-start(bf16[4,1,32,1408]{3,2,1,0:T(8,128)(2,1)S(1)} %collective-permute-done.7.refs_6_), channel_id=1, source_target_pairs={{0,1},{1,0},{2,3},{3,2},{4,5},{5,4},{6,7},{7,6},{8,9},{9,8},{10,11... | collective-permute-start | bytes 1081352 | tf_op jit(solution)/shard_map/ppermute | solution.py:29
  27.9 6.8 %collective-permute-start = (f32[3,4,1280]{2,1,0:T(4,128)S(1)}, f32[3,4,1280]{2,1,0:T(4,128)S(1)}, u32[]{:S(2)}, u32[]{:S(2)}) collective-permute-start(f32[3,4,1280]{2,1,0:T(4,128)S(1)} %get-tuple-element.36), channel_id=1, source_target_pairs={{0,4},{4,8},{8,12},{12,0},{1,5},{5,9},{9,13},{13,1},{2,6},{6,10},{... | collective-permute-start | bytes 184328 | tf_op jit(solution)/shard_map/ppermute | solution.py:29
  28.0 8.4 %collective-permute-start.1 = (f32[3,4,1280]{2,1,0:T(4,128)S(1)}, f32[3,4,1280]{2,1,0:T(4,128)S(1)}, u32[]{:S(2)}, u32[]{:S(2)}) collective-permute-start(f32[3,4,1280]{2,1,0:T(4,128)S(1)} %get-tuple-element.37), channel_id=1, source_target_pairs={{0,8},{4,12},{8,0},{12,4},{1,9},{5,13},{9,1},{13,5},{2,10},{6,14},... | collective-permute-start | bytes 184328 | tf_op jit(solution)/shard_map/ppermute | solution.py:29
  29.9 6.5 %collective-permute-start.2 = (f32[3,4,1280]{2,1,0:T(4,128)S(1)}, f32[3,4,1280]{2,1,0:T(4,128)S(1)}, u32[]{:S(2)}, u32[]{:S(2)}) collective-permute-start(f32[3,4,1280]{2,1,0:T(4,128)S(1)} %get-tuple-element.38), channel_id=1, source_target_pairs={{0,12},{4,0},{8,4},{12,8},{1,13},{5,1},{9,5},{13,9},{2,14},{6,2},{... | collective-permute-start | bytes 184328 | tf_op jit(solution)/shard_map/ppermute | solution.py:29
  36.4 6.6 %slice-start = ((s8[5898240]{0:T(1024)(128)(4,1)}), s8[4194304]{0:T(1024)(128)(4,1)S(1)}, s32[]{:S(2)}) async-start(s8[5898240]{0:T(1024)(128)(4,1)} %bitcast.122), calls=%async_computation | async-start | bytes 8388608
  41.5 10.2 %collective-permute-start.9 = (f16[3,128,384]{2,1,0:T(8,128)(2,1)}, f16[3,128,384]{2,1,0:T(8,128)(2,1)}, u32[]{:S(2)}, u32[]{:S(2)}) collective-permute-start(f16[3,128,384]{2,1,0:T(8,128)(2,1)} %select_convert_fusion.9), channel_id=1, source_target_pairs={{0,4},{4,0},{8,12},{12,8},{1,5},{5,1},{9,13},{13,9},{2,6},{6,2},{1... | collective-permute-start | bytes 884744 | tf_op jit(solution)/shard_map/ppermute | solution.py:475
  45.7 12.2 %collective-permute-start.22 = (f16[3,128,384]{2,1,0:T(8,128)(2,1)}, f16[3,128,384]{2,1,0:T(8,128)(2,1)S(1)}, u32[]{:S(2)}, u32[]{:S(2)}) collective-permute-start(f16[3,128,384]{2,1,0:T(8,128)(2,1)} %select_convert_fusion.4), channel_id=1, source_target_pairs={{0,4},{4,0},{8,12},{12,8},{1,5},{5,1},{9,13},{13,9},{2,6},{6,2},{1... | collective-permute-start | bytes 884744 | tf_op jit(solution)/shard_map/ppermute | solution.py:475
  46.9 25.7 %collective-permute-start.35 = (bf16[640,768]{1,0:T(8,128)(2,1)S(1)}, bf16[640,768]{1,0:T(8,128)(2,1)S(1)}, u32[]{:S(2)}, u32[]{:S(2)}) collective-permute-start(bf16[640,768]{1,0:T(8,128)(2,1)S(1)} %get-tuple-element.59), channel_id=1, source_target_pairs={{0,1},{1,0},{2,3},{3,2},{4,5},{5,4},{6,7},{7,6},{8,9},{9,8},{10,11... | collective-permute-start | bytes 2949128 | tf_op jit(solution)/shard_map/ppermute | solution.py:29
  47.0 23.5 %copy-start.4 = (f32[4,3,128,384]{3,2,1,0:T(8,128)S(1)}, f32[4,3,128,384]{3,2,1,0:T(8,128)}, u32[]{:S(2)}) copy-start(f32[4,3,128,384]{3,2,1,0:T(8,128)} %copy-done.3) | copy-start | bytes 7077892
  53.1 11.1 %collective-permute-start.10 = (f16[3,128,384]{2,1,0:T(8,128)(2,1)S(1)}, f16[3,128,384]{2,1,0:T(8,128)(2,1)S(1)}, u32[]{:S(2)}, u32[]{:S(2)}) collective-permute-start(f16[3,128,384]{2,1,0:T(8,128)(2,1)S(1)} %get-tuple-element.72), channel_id=1, source_target_pairs={{0,4},{4,0},{8,12},{12,8},{1,5},{5,1},{9,13},{13,9},{2,6},{6,2},{1... | collective-permute-start | bytes 884744 | tf_op jit(solution)/shard_map/ppermute | solution.py:475
  54.6 11.1 %collective-permute-start.11 = (f16[3,128,384]{2,1,0:T(8,128)(2,1)S(1)}, f16[3,128,384]{2,1,0:T(8,128)(2,1)S(1)}, u32[]{:S(2)}, u32[]{:S(2)}) collective-permute-start(f16[3,128,384]{2,1,0:T(8,128)(2,1)S(1)} %get-tuple-element.71), channel_id=1, source_target_pairs={{0,1},{1,0},{4,8},{5,9},{8,4},{9,5},{12,13},{13,12},{2,3},{3,2},{6... | collective-permute-start | bytes 884744 | tf_op jit(solution)/shard_map/ppermute | solution.py:477
  59.2 11.3 %collective-permute-start.23 = (f16[3,128,384]{2,1,0:T(8,128)(2,1)S(1)}, f16[3,128,384]{2,1,0:T(8,128)(2,1)S(1)}, u32[]{:S(2)}, u32[]{:S(2)}) collective-permute-start(f16[3,128,384]{2,1,0:T(8,128)(2,1)S(1)} %get-tuple-element.70), channel_id=1, source_target_pairs={{0,4},{4,0},{8,12},{12,8},{1,5},{5,1},{9,13},{13,9},{2,6},{6,2},{1... | collective-permute-start | bytes 884744 | tf_op jit(solution)/shard_map/ppermute | solution.py:475
  60.8 9.8 %collective-permute-start.24 = (f16[3,128,384]{2,1,0:T(8,128)(2,1)S(1)}, f16[3,128,384]{2,1,0:T(8,128)(2,1)S(1)}, u32[]{:S(2)}, u32[]{:S(2)}) collective-permute-start(f16[3,128,384]{2,1,0:T(8,128)(2,1)S(1)} %get-tuple-element.69), channel_id=1, source_target_pairs={{0,1},{1,0},{4,8},{5,9},{8,4},{9,5},{12,13},{13,12},{2,3},{3,2},{6... | collective-permute-start | bytes 884744 | tf_op jit(solution)/shard_map/ppermute | solution.py:477
  64.2 8.4 %copy-start.6 = (f32[2,768]{1,0:T(2,128)S(1)}, f32[2,768]{1,0:T(2,128)}, u32[]{:S(2)}) copy-start(f32[2,768]{1,0:T(2,128)} %param.9) | copy-start | bytes 18436
  64.2 47.6 %collective-permute-start.36 = (bf16[640,768]{1,0:T(8,128)(2,1)S(1)}, bf16[640,768]{1,0:T(8,128)(2,1)S(1)}, u32[]{:S(2)}, u32[]{:S(2)}) collective-permute-start(bf16[640,768]{1,0:T(8,128)(2,1)S(1)} %get-tuple-element.58.refs_16_), channel_id=1, source_target_pairs={{0,2},{2,0},{1,3},{3,1},{4,6},{6,4},{5,7},{7,5},{8,10},{10,8},{9,1... | collective-permute-start | bytes 2949128 | tf_op jit(solution)/shard_map/ppermute | solution.py:29
  67.2 9.4 %collective-permute-start.12 = (f16[3,128,384]{2,1,0:T(8,128)(2,1)S(1)}, f16[3,128,384]{2,1,0:T(8,128)(2,1)S(1)}, u32[]{:S(2)}, u32[]{:S(2)}) collective-permute-start(f16[3,128,384]{2,1,0:T(8,128)(2,1)S(1)} %get-tuple-element.68), channel_id=1, source_target_pairs={{0,4},{4,0},{8,12},{12,8},{1,5},{5,1},{9,13},{13,9},{2,6},{6,2},{1... | collective-permute-start | bytes 884744 | tf_op jit(solution)/shard_map/ppermute | solution.py:475
  70.5 7.6 %collective-permute-start.13 = (f16[3,128,384]{2,1,0:T(8,128)(2,1)S(1)}, f16[3,128,384]{2,1,0:T(8,128)(2,1)S(1)}, u32[]{:S(2)}, u32[]{:S(2)}) collective-permute-start(f16[3,128,384]{2,1,0:T(8,128)(2,1)S(1)} %get-tuple-element.67), channel_id=1, source_target_pairs={{0,1},{1,0},{4,8},{5,9},{8,4},{9,5},{12,13},{13,12},{2,3},{3,2},{6... | collective-permute-start | bytes 884744 | tf_op jit(solution)/shard_map/ppermute | solution.py:477
  70.8 10.8 %collective-permute-start.25 = (f16[3,128,384]{2,1,0:T(8,128)(2,1)S(1)}, f16[3,128,384]{2,1,0:T(8,128)(2,1)S(1)}, u32[]{:S(2)}, u32[]{:S(2)}) collective-permute-start(f16[3,128,384]{2,1,0:T(8,128)(2,1)S(1)} %get-tuple-element.66), channel_id=1, source_target_pairs={{0,4},{4,0},{8,12},{12,8},{1,5},{5,1},{9,13},{13,9},{2,6},{6,2},{1... | collective-permute-start | bytes 884744 | tf_op jit(solution)/shard_map/ppermute | solution.py:475
  72.6 9.0 %collective-permute-start.26 = (f16[3,128,384]{2,1,0:T(8,128)(2,1)S(1)}, f16[3,128,384]{2,1,0:T(8,128)(2,1)S(1)}, u32[]{:S(2)}, u32[]{:S(2)}) collective-permute-start(f16[3,128,384]{2,1,0:T(8,128)(2,1)S(1)} %get-tuple-element.65), channel_id=1, source_target_pairs={{0,1},{1,0},{4,8},{5,9},{8,4},{9,5},{12,13},{13,12},{2,3},{3,2},{6... | collective-permute-start | bytes 884744 | tf_op jit(solution)/shard_map/ppermute | solution.py:477
  76.7 53.5 %collective-permute-start.37 = (bf16[640,768]{1,0:T(8,128)(2,1)S(1)}, bf16[640,768]{1,0:T(8,128)(2,1)S(1)}, u32[]{:S(2)}, u32[]{:S(2)}) collective-permute-start(bf16[640,768]{1,0:T(8,128)(2,1)S(1)} %collective-permute-done.35.refs_17_), channel_id=1, source_target_pairs={{0,2},{2,0},{1,3},{3,1},{4,6},{6,4},{5,7},{7,5},{8,10},{10,8},{9,1... | collective-permute-start | bytes 2949128 | tf_op jit(solution)/shard_map/ppermute | solution.py:29
  80.4 27.2 %collective-permute-start.14 = (bf16[1,64,384]{2,1,0:T(8,128)(2,1)S(1)}, bf16[1,64,384]{2,1,0:T(8,128)(2,1)S(1)}, u32[]{:S(2)}, u32[]{:S(2)}) collective-permute-start(bf16[1,64,384]{2,1,0:T(8,128)(2,1)S(1)} %get-tuple-element.51), channel_id=1, source_target_pairs={{0,2},{2,0},{1,3},{3,1},{4,6},{6,4},{5,7},{7,5},{8,10},{10,8},{9,1... | collective-permute-start | bytes 147464 | tf_op jit(solution)/shard_map/ppermute | solution.py:29
  82.8 27.0 %collective-permute-start.27 = (bf16[1,64,384]{2,1,0:T(8,128)(2,1)S(1)}, bf16[1,64,384]{2,1,0:T(8,128)(2,1)S(1)}, u32[]{:S(2)}, u32[]{:S(2)}) collective-permute-start(bf16[1,64,384]{2,1,0:T(8,128)(2,1)S(1)} %get-tuple-element.57), channel_id=1, source_target_pairs={{0,2},{2,0},{1,3},{3,1},{4,6},{6,4},{5,7},{7,5},{8,10},{10,8},{9,1... | collective-permute-start | bytes 147464 | tf_op jit(solution)/shard_map/ppermute | solution.py:29
  107.6 5.7 %collective-permute-start.15 = (bf16[2,1,64,384]{3,2,1,0:T(8,128)(2,1)S(1)}, bf16[2,1,64,384]{3,2,1,0:T(8,128)(2,1)S(1)}, u32[]{:S(2)}, u32[]{:S(2)}) collective-permute-start(bf16[2,1,64,384]{3,2,1,0:T(8,128)(2,1)S(1)} %pad_maximum_fusion.1.refs_0_), channel_id=1, source_target_pairs={{0,1},{1,0},{2,3},{3,2},{4,5},{5,4},{6,7},{7,6},{8,9},{9,8},{10,11... | collective-permute-start | bytes 294920 | tf_op jit(solution)/shard_map/ppermute | solution.py:29
  107.7 7.6 %collective-permute-start.16 = (bf16[2,1,64,384]{3,2,1,0:T(8,128)(2,1)S(1)}, bf16[2,1,64,384]{3,2,1,0:T(8,128)(2,1)S(1)}, u32[]{:S(2)}, u32[]{:S(2)}) collective-permute-start(bf16[2,1,64,384]{3,2,1,0:T(8,128)(2,1)S(1)} %pad_maximum_fusion.1.refs_0_), channel_id=1, source_target_pairs={{0,4},{4,8},{8,12},{12,0},{1,5},{5,9},{9,13},{13,1},{2,6},{6,10},{... | collective-permute-start | bytes 294920 | tf_op jit(solution)/shard_map/ppermute | solution.py:29
  109.7 9.5 %collective-permute-start.18 = (bf16[2,1,64,384]{3,2,1,0:T(8,128)(2,1)S(1)}, bf16[2,1,64,384]{3,2,1,0:T(8,128)(2,1)S(1)}, u32[]{:S(2)}, u32[]{:S(2)}) collective-permute-start(bf16[2,1,64,384]{3,2,1,0:T(8,128)(2,1)S(1)} %pad_maximum_fusion.1.refs_0_), channel_id=1, source_target_pairs={{0,8},{4,12},{8,0},{12,4},{1,9},{5,13},{9,1},{13,5},{2,10},{6,14},... | collective-permute-start | bytes 294920 | tf_op jit(solution)/shard_map/ppermute | solution.py:29
  111.8 8.2 %collective-permute-start.20 = (bf16[2,1,64,384]{3,2,1,0:T(8,128)(2,1)S(1)}, bf16[2,1,64,384]{3,2,1,0:T(8,128)(2,1)S(1)}, u32[]{:S(2)}, u32[]{:S(2)}) collective-permute-start(bf16[2,1,64,384]{3,2,1,0:T(8,128)(2,1)S(1)} %pad_maximum_fusion.1.refs_0_), channel_id=1, source_target_pairs={{0,12},{4,0},{8,4},{12,8},{1,13},{5,1},{9,5},{13,9},{2,14},{6,2},{... | collective-permute-start | bytes 294920 | tf_op jit(solution)/shard_map/ppermute | solution.py:29
  113.3 9.9 %collective-permute-start.28 = (bf16[2,1,64,384]{3,2,1,0:T(8,128)(2,1)S(1)}, bf16[2,1,64,384]{3,2,1,0:T(8,128)(2,1)S(1)}, u32[]{:S(2)}, u32[]{:S(2)}) collective-permute-start(bf16[2,1,64,384]{3,2,1,0:T(8,128)(2,1)S(1)} %pad_maximum_fusion.2.refs_8_), channel_id=1, source_target_pairs={{0,1},{1,0},{2,3},{3,2},{4,5},{5,4},{6,7},{7,6},{8,9},{9,8},{10,11... | collective-permute-start | bytes 294920 | tf_op jit(solution)/shard_map/ppermute | solution.py:29
  115.3 8.0 %collective-permute-start.29 = (bf16[2,1,64,384]{3,2,1,0:T(8,128)(2,1)S(1)}, bf16[2,1,64,384]{3,2,1,0:T(8,128)(2,1)S(1)}, u32[]{:S(2)}, u32[]{:S(2)}) collective-permute-start(bf16[2,1,64,384]{3,2,1,0:T(8,128)(2,1)S(1)} %pad_maximum_fusion.2.refs_8_), channel_id=1, source_target_pairs={{0,4},{4,8},{8,12},{12,0},{1,5},{5,9},{9,13},{13,1},{2,6},{6,10},{... | collective-permute-start | bytes 294920 | tf_op jit(solution)/shard_map/ppermute | solution.py:29
  119.3 8.2 %collective-permute-start.31 = (bf16[2,1,64,384]{3,2,1,0:T(8,128)(2,1)S(1)}, bf16[2,1,64,384]{3,2,1,0:T(8,128)(2,1)S(1)}, u32[]{:S(2)}, u32[]{:S(2)}) collective-permute-start(bf16[2,1,64,384]{3,2,1,0:T(8,128)(2,1)S(1)} %pad_maximum_fusion.2.refs_8_), channel_id=1, source_target_pairs={{0,8},{4,12},{8,0},{12,4},{1,9},{5,13},{9,1},{13,5},{2,10},{6,14},... | collective-permute-start | bytes 294920 | tf_op jit(solution)/shard_map/ppermute | solution.py:29
  120.0 8.4 %collective-permute-start.33 = (bf16[2,1,64,384]{3,2,1,0:T(8,128)(2,1)S(1)}, bf16[2,1,64,384]{3,2,1,0:T(8,128)(2,1)S(1)}, u32[]{:S(2)}, u32[]{:S(2)}) collective-permute-start(bf16[2,1,64,384]{3,2,1,0:T(8,128)(2,1)S(1)} %pad_maximum_fusion.2.refs_8_), channel_id=1, source_target_pairs={{0,12},{4,0},{8,4},{12,8},{1,13},{5,1},{9,5},{13,9},{2,14},{6,2},{... | collective-permute-start | bytes 294920 | tf_op jit(solution)/shard_map/ppermute | solution.py:29
  123.3 5.1 %collective-permute-start.17 = (bf16[2,1,64,384]{3,2,1,0:T(8,128)(2,1)S(1)}, bf16[2,1,64,384]{3,2,1,0:T(8,128)(2,1)S(1)}, u32[]{:S(2)}, u32[]{:S(2)}) collective-permute-start(bf16[2,1,64,384]{3,2,1,0:T(8,128)(2,1)S(1)} %collective-permute-done.16.refs_2_), channel_id=1, source_target_pairs={{0,1},{1,0},{2,3},{3,2},{4,5},{5,4},{6,7},{7,6},{8,9},{9,8},{10,11... | collective-permute-start | bytes 294920 | tf_op jit(solution)/shard_map/ppermute | solution.py:29
  123.3 5.6 %collective-permute-start.19 = (bf16[2,1,64,384]{3,2,1,0:T(8,128)(2,1)S(1)}, bf16[2,1,64,384]{3,2,1,0:T(8,128)(2,1)S(1)}, u32[]{:S(2)}, u32[]{:S(2)}) collective-permute-start(bf16[2,1,64,384]{3,2,1,0:T(8,128)(2,1)S(1)} %collective-permute-done.18.refs_4_), channel_id=1, source_target_pairs={{0,1},{1,0},{2,3},{3,2},{4,5},{5,4},{6,7},{7,6},{8,9},{9,8},{10,11... | collective-permute-start | bytes 294920 | tf_op jit(solution)/shard_map/ppermute | solution.py:29
  127.5 1.5 %collective-permute-start.21 = (bf16[2,1,64,384]{3,2,1,0:T(8,128)(2,1)S(1)}, bf16[2,1,64,384]{3,2,1,0:T(8,128)(2,1)S(1)}, u32[]{:S(2)}, u32[]{:S(2)}) collective-permute-start(bf16[2,1,64,384]{3,2,1,0:T(8,128)(2,1)S(1)} %collective-permute-done.20.refs_6_), channel_id=1, source_target_pairs={{0,1},{1,0},{2,3},{3,2},{4,5},{5,4},{6,7},{7,6},{8,9},{9,8},{10,11... | collective-permute-start | bytes 294920 | tf_op jit(solution)/shard_map/ppermute | solution.py:29
  128.4 1.3 collective-permute-start.30
  128.4 1.5 collective-permute-start.32
  128.9 1.3 collective-permute-start.34
  131.7 5.9 %collective-permute-start.39 = (bf16[1,64,640]{2,1,0:T(8,128)(2,1)S(1)}, bf16[1,64,640]{2,1,0:T(8,128)(2,1)S(1)}, u32[]{:S(2)}, u32[]{:S(2)}) collective-permute-start(bf16[1,64,640]{2,1,0:T(8,128)(2,1)S(1)} %get-tuple-element.62), channel_id=1, source_target_pairs={{0,12},{4,0},{8,4},{12,8},{1,13},{5,1},{9,5},{13,9},{2,14},{6,2},{... | collective-permute-start | bytes 245768 | tf_op jit(solution)/shard_map/ppermute | solution.py:29
  134.7 8.2 %collective-permute-start.41 = (bf16[1,64,640]{2,1,0:T(8,128)(2,1)S(1)}, bf16[1,64,640]{2,1,0:T(8,128)(2,1)S(1)}, u32[]{:S(2)}, u32[]{:S(2)}) collective-permute-start(bf16[1,64,640]{2,1,0:T(8,128)(2,1)S(1)} %get-tuple-element.63), channel_id=1, source_target_pairs={{0,8},{4,12},{8,0},{12,4},{1,9},{5,13},{9,1},{13,5},{2,10},{6,14},... | collective-permute-start | bytes 245768 | tf_op jit(solution)/shard_map/ppermute | solution.py:29
  134.9 8.1 %collective-permute-start.43 = (bf16[1,64,640]{2,1,0:T(8,128)(2,1)S(1)}, bf16[1,64,640]{2,1,0:T(8,128)(2,1)S(1)}, u32[]{:S(2)}, u32[]{:S(2)}) collective-permute-start(bf16[1,64,640]{2,1,0:T(8,128)(2,1)S(1)} %get-tuple-element.64), channel_id=1, source_target_pairs={{0,4},{4,8},{8,12},{12,0},{1,5},{5,9},{9,13},{13,1},{2,6},{6,10},{... | collective-permute-start | bytes 245768 | tf_op jit(solution)/shard_map/ppermute | solution.py:29
  135.4 8.1 %collective-permute-start.38 = (bf16[1,64,640]{2,1,0:T(8,128)(2,1)S(1)}, bf16[1,64,640]{2,1,0:T(8,128)(2,1)S(1)}, u32[]{:S(2)}, u32[]{:S(2)}) collective-permute-start(bf16[1,64,640]{2,1,0:T(8,128)(2,1)S(1)} %get-tuple-element.61), channel_id=1, source_target_pairs={{0,1},{1,0},{2,3},{3,2},{4,5},{5,4},{6,7},{7,6},{8,9},{9,8},{10,11... | collective-permute-start | bytes 245768 | tf_op jit(solution)/shard_map/ppermute | solution.py:29
  137.6 5.9 %collective-permute-start.40 = (bf16[1,64,640]{2,1,0:T(8,128)(2,1)S(1)}, bf16[1,64,640]{2,1,0:T(8,128)(2,1)S(1)}, u32[]{:S(2)}, u32[]{:S(2)}) collective-permute-start(bf16[1,64,640]{2,1,0:T(8,128)(2,1)S(1)} %collective-permute-done.39.refs_2_), channel_id=1, source_target_pairs={{0,1},{1,0},{2,3},{3,2},{4,5},{5,4},{6,7},{7,6},{8,9},{9,8},{10,11... | collective-permute-start | bytes 245768 | tf_op jit(solution)/shard_map/ppermute | solution.py:29
  143.0 1.3 collective-permute-start.42
  143.0 1.4 collective-permute-start.44
  (6 other events, 18.7 us)

commit v9 on v8

--- a/solution.py
+++ b/solution.py
@@ -200,8 +200,9 @@
 
 
 def modulate_kernel(n_tm, n_seq, n_mp, cuts, step_ref, w_ref, *refs):
-    shares, rows = refs[:n_tm], refs[n_tm : n_tm + n_seq * n_mp]
-    hidden_ref, coef_ref, *w_outs, mod_scr, sems = refs[n_tm + n_seq * n_mp :]
+    sides = n_seq * n_mp
+    shares, near, far = refs[:n_tm], refs[n_tm : n_tm + sides], refs[n_tm + sides :][:sides]
+    hidden_ref, coef_ref, *w_outs, mod_scr, sems = refs[n_tm + 2 * sides :]
     stride = w_ref.shape[1] // DMA_PIECES
     copies = []
     for (lane, size), out in zip(cuts, w_outs):
@@ -216,7 +217,7 @@
                     )
                 )
     z, k = lax.axis_index("tm"), pl.program_id(0)
-    _, frames, part, wide = rows[0].shape
+    frames, part, wide = near[0].shape
     depth = wide - LANES
 
     @pl.when(k == 0)
@@ -233,16 +234,25 @@
         shift, scale, gate = (mod_scr[c, pl.ds(step, 1), :] for c in range(3))
         index = jnp.full((1, depth), step_ref[0] + step, jnp.int32)
         coef_ref[0, f : f + 1, :] = (sigma_of(index + 1) - sigma_of(index)) * gate
+
+        def modulated(block):
+            tail = block[:, depth:].astype(jnp.float32)
+            mean = tail[:, 0:1] + tail[:, 1:2] + tail[:, 2:3]
+            rstd = tail[:, 3:4] + tail[:, 4:5] + tail[:, 5:6]
+            normed = (block[:, :depth].astype(jnp.float32) - mean) * rstd
+            return (normed * (1.0 + scale) + shift).astype(jnp.bfloat16)
+
         for j in range(n_seq):
             for i in range(n_mp):
-                row = rows[j * n_mp + i]
-                tail = row[0, f, :, depth:].astype(jnp.float32)
-                mean = tail[:, 0:1] + tail[:, 1:2] + tail[:, 2:3]
-                rstd = tail[:, 3:4] + tail[:, 4:5] + tail[:, 5:6]
-                normed = (row[0, f, :, :depth].astype(jnp.float32) - mean) * rstd
-                hidden_ref[0, j, f, i * part : (i + 1) * part, :] = (
-                    normed * (1.0 + scale) + shift
-                ).astype(jnp.bfloat16)
+                to = slice(i * part, (i + 1) * part)
+
+                @pl.when(k == 0)
+                def _():
+                    hidden_ref[0, j, f, to, :] = modulated(near[j * n_mp + i][f])
+
+                @pl.when(k > 0)
+                def _():
+                    hidden_ref[0, j, f, to, :] = modulated(far[j * n_mp + i][0, f])
 
     @pl.when(k == n_tm - 1)
     def _():
@@ -250,9 +260,9 @@
             copy.wait()
 
 
-def modulate(start_step, w_qkv, cuts, shares, rows):
-    n_tm, n_seq, n_mp = len(shares), len(rows), len(rows[0])
-    _, frames, part, wide = rows[0][0].shape
+def modulate(start_step, w_qkv, cuts, shares, near, far):
+    n_tm, n_seq, n_mp = len(shares), len(near), len(near[0])
+    frames, part, wide = near[0][0].shape
     three = w_qkv.shape[0]
     depth = wide - LANES
     window = shares[0].shape[1]
@@ -262,7 +272,9 @@
         grid=(n_tm,),
         in_specs=[pl.BlockSpec(memory_space=pltpu.SMEM), pl.BlockSpec(memory_space=pltpu.HBM)]
         + [pl.BlockSpec((3, window, depth), lambda k: (0, 0, 0))] * n_tm
-        + [pl.BlockSpec((1, frames, part, wide), lambda k: (k, 0, 0, 0))] * (n_seq * n_mp),
+        + [pl.BlockSpec((frames, part, wide), lambda k: (0, 0, 0))] * (n_seq * n_mp)
+        + [pl.BlockSpec((1, frames, part, wide), lambda k: (jnp.maximum(k - 1, 0), 0, 0, 0))]
+        * (n_seq * n_mp),
         out_specs=[
             pl.BlockSpec((1,) + shape[1:], lambda k: (k, 0, 0, 0, 0)),
             pl.BlockSpec((1, frames, depth), lambda k: (k, 0, 0)),
@@ -282,9 +294,9 @@
             bytes_accessed=4 * n_tm * n_seq * frames * n_mp * part * depth,
             transcendentals=0,
         ),
-        compiler_params=pltpu.CompilerParams(vmem_limit_bytes=48 << 20),
+        compiler_params=pltpu.CompilerParams(vmem_limit_bytes=42 << 20),
         name="modulate",
-    )(start_step, w_qkv, *shares, *[r for side in rows for r in side])
+    )(start_step, w_qkv, *shares, *[r for rows in (near, far) for side in rows for r in side])
 
 
 def project_kernel(dims, widths, coef_ref, *refs):
@@ -416,13 +428,11 @@
     raw = list(spread(states, n_tm, part))
     for k in range(1, n_tm):
         raw[k] = turn(raw[k], "tm", k)
-    raw = jnp.stack(raw)
-    sides = [raw]
-    for j in range(1, n_seq):
-        sides.append(turn(raw, "seq", j))
-    rows = []
-    for side in sides:
-        rows.append([side] + [turn(side, "mp", i) for i in range(1, n_mp)])
+    near, far = [], []
+    for blocks, kept in ((raw[0], near), (jnp.stack(raw[1:]), far)):
+        for j in range(n_seq):
+            side = turn(blocks, "seq", j) if j else blocks
+            kept.append([side] + [turn(side, "mp", i) for i in range(1, n_mp)])
 
     shares = list(time_shares(start_step, time_proj, n_tm, window))
     for k in range(1, n_tm):
@@ -432,14 +442,15 @@
     weights = [turn(share, "mp", i) if i else share for i, share in enumerate(shares_out)]
     weights = [weights]
     for j in range(1, n_seq):
-        weights.append([turn(s, "seq", -j) for s in weights[0]])
+        weights.append([])
+        for share in weights[0]:
+            weights[j].append(turn(share, "seq", -j))
 
     groups = head_groups(cols)
-    hidden, coef, first_qkv = modulate(start_step, w_qkv, groups[:1], shares, rows)
+    hidden, coef, *parts_qkv = modulate(start_step, w_qkv, groups, shares, near, far)
     hidden = hidden.reshape(n_tm, n_seq * frames * tok, depth)
     proj = []
-    for h, (lane, size) in enumerate(groups):
-        part_qkv = w_qkv[:, :, lane : lane + size] if h else first_qkv
+    for part_qkv in parts_qkv:
         proj.append(
             jnp.einsum(
                 "krd,cdh->kcrh",

time: 146 us -> 145 us (level)
  starting transfers between devices: 41.1 us -> 36.4 us
  waiting for transfers between devices: 80.7 us -> 83.6 us
    ppermute x6, waiting for transfers between devices: 17.8 us -> 22.5 us  [sweep(): first = lax.ppermute(first, 'tm', evens)]
    ppermute x6, starting transfers between devices: 8.48 us -> 3.84 us  [sweep(): first = lax.ppermute(first, 'tm', evens)]
    ppermute x35 -> x38, waiting for transfers between devices: 62.8 us -> 61 us  [turn(): lax.ppermute(block, axis, [(i, (i + distance) % size) for i in range(size)])]
    ppermute x35 -> x38, starting transfers between devices: 32.7 us -> 32.5 us  [turn(): lax.ppermute(block, axis, [(i, (i + distance) % size) for i in range(size)])]
  transfers between devices with their start and end apart: 45 -> 48, of which waited for: 23 -> 26; matrix products, arithmetic and copies ran while one was open for 6% -> 6% of each run, Pallas kernels for 2% -> 2%
where the time goes in v9:
time: 145 us
  waiting for transfers between devices  83.6 us (58%)
  starting transfers between devices  36.4 us (25%)
  Pallas kernels  9.59 us (7%)
  other arithmetic  7.7 us (5%)
  matrix products  3.95 us (3%)
  local copies, waits for them, and re-layouts  2.65 us (2%)
    ppermute x38, waiting for transfers between devices, turn(): lax.ppermute(block, axis, [(i, (i + distance) % size) for i in range(size)])  61 us
    ppermute x38, starting transfers between devices, turn(): lax.ppermute(block, axis, [(i, (i + distance) % size) for i in range(size)])  32.5 us
    ppermute x6, waiting for transfers between devices, sweep(): first = lax.ppermute(first, 'tm', evens)  22.5 us
    convert_element_type x4, other arithmetic, sweep(): second = jnp.where(even, left, right).astype(jnp.float16)  4.5 us
    dot_general x2, matrix products, sweep(): jnp.einsum('krd,cdh->kcrh', hidden, part_qkv, preferred_element_type=jnp....  3.95 us
    ppermute x6, starting transfers between devices, sweep(): first = lax.ppermute(first, 'tm', evens)  3.84 us
    pallas_call x1, Pallas kernels, modulate(): pl.pallas_call(functools.partial(modulate_kernel, n_tm, n_seq, n_mp, cuts...  3.29 us
  transfers between devices with their start and end apart: 48, of which 26 were waited for; matrix products, arithmetic and copies ran while one was open for 6% of the time, Pallas kernels for 2%

profile of v9, /device:TPU:0, one launch (start us, length us, event | category | flops | bytes accessed | tf_op | source)
XLA Modules:
  0.0 144.9 jit_solution(4708756543889790925)
XLA Ops:
  0.0 1.1 copy-done.2
  1.5 3.1 %collective-permute-start.6 = (bf16[1,32,1408]{2,1,0:T(8,128)(2,1)S(1)}, bf16[1,32,1408]{2,1,0:T(8,128)(2,1)S(1)}, u32[]{:S(2)}, u32[]{:S(2)}) collective-permute-start(bf16[1,32,1408]{2,1,0:T(8,128)(2,1)S(1)} %get-tuple-element.41), channel_id=1, source_target_pairs={{0,4},{4,8},{8,12},{12,0},{1,5},{5,9},{9,13},{13,1},{2,6},{6,10},{... | collective-permute-start | bytes 270344 | tf_op jit(solution)/shard_map/ppermute | solution.py:29
  4.6 2.6 %collective-permute-start.7 = (bf16[1,32,1408]{2,1,0:T(8,128)(2,1)S(1)}, bf16[1,32,1408]{2,1,0:T(8,128)(2,1)S(1)}, u32[]{:S(2)}, u32[]{:S(2)}) collective-permute-start(bf16[1,32,1408]{2,1,0:T(8,128)(2,1)S(1)} %get-tuple-element.42), channel_id=1, source_target_pairs={{0,8},{4,12},{8,0},{12,4},{1,9},{5,13},{9,1},{13,5},{2,10},{6,14},... | collective-permute-start | bytes 270344 | tf_op jit(solution)/shard_map/ppermute | solution.py:29
  7.2 1.4 collective-permute-start.8
  8.5 1.4 collective-permute-done.6
  9.9 3.3 %collective-permute-done.7 = bf16[1,32,1408]{2,1,0:T(8,128)(2,1)S(1)} collective-permute-done((bf16[1,32,1408]{2,1,0:T(8,128)(2,1)S(1)}, bf16[1,32,1408]{2,1,0:T(8,128)(2,1)S(1)}, u32[]{:S(2)}, u32[]{:S(2)}) %collective-permute-start.7) | collective-permute-done | bytes 90144 | tf_op jit(solution)/shard_map/ppermute | solution.py:29
  13.5 1.6 %collective-permute-start.10 = (bf16[3,1,32,1408]{3,2,1,0:T(8,128)(2,1)S(1)}, bf16[3,1,32,1408]{3,2,1,0:T(8,128)(2,1)S(1)}, u32[]{:S(2)}, u32[]{:S(2)}) collective-permute-start(bf16[3,1,32,1408]{3,2,1,0:T(8,128)(2,1)S(1)} %pad_maximum_fusion.refs_8_), channel_id=1, source_target_pairs={{0,2},{2,0},{1,3},{3,1},{4,6},{6,4},{5,7},{7,5},{8,10},{10,8},{9,1... | collective-permute-start | bytes 811016 | tf_op jit(solution)/shard_map/ppermute | solution.py:29
  15.0 6.6 %collective-permute-done.10.refs_10_ = bf16[3,1,32,1408]{3,2,1,0:T(8,128)(2,1)S(1)} collective-permute-done((bf16[3,1,32,1408]{3,2,1,0:T(8,128)(2,1)S(1)}, bf16[3,1,32,1408]{3,2,1,0:T(8,128)(2,1)S(1)}, u32[]{:S(2)}, u32[]{:S(2)}) %collective-permute-start.10) | collective-permute-done | bytes 270368 | tf_op jit(solution)/shard_map/ppermute | solution.py:29
  21.7 1.5 %collective-permute-start.4 = (bf16[1,32,1408]{2,1,0:T(8,128)(2,1)S(1)}, bf16[1,32,1408]{2,1,0:T(8,128)(2,1)S(1)}, u32[]{:S(2)}, u32[]{:S(2)}) collective-permute-start(bf16[1,32,1408]{2,1,0:T(8,128)(2,1)S(1)} %get-tuple-element.40.refs_4_), channel_id=1, source_target_pairs={{0,2},{2,0},{1,3},{3,1},{4,6},{6,4},{5,7},{7,5},{8,10},{10,8},{9,1... | collective-permute-start | bytes 270344 | tf_op jit(solution)/shard_map/ppermute | solution.py:29
  23.8 1.5 %copy-done = bf16[64,15360]{1,0:T(8,128)(2,1)S(1)} copy-done((bf16[64,15360]{1,0:T(8,128)(2,1)S(1)}, bf16[64,15360]{1,0:T(8,128)(2,1)}, u32[]{:S(2)}) %copy-start) | copy-done | bytes 1966104
  25.3 0.8 time_shares.1
  26.2 2.6 %collective-permute-start = (f32[3,4,1280]{2,1,0:T(4,128)S(1)}, f32[3,4,1280]{2,1,0:T(4,128)S(1)}, u32[]{:S(2)}, u32[]{:S(2)}) collective-permute-start(f32[3,4,1280]{2,1,0:T(4,128)S(1)} %get-tuple-element.37), channel_id=1, source_target_pairs={{0,4},{4,8},{8,12},{12,0},{1,5},{5,9},{9,13},{13,1},{2,6},{6,10},{... | collective-permute-start | bytes 184328 | tf_op jit(solution)/shard_map/ppermute | solution.py:29
  29.2 3.3 %collective-permute-done.refs_1_ = f32[3,4,1280]{2,1,0:T(4,128)S(1)} collective-permute-done((f32[3,4,1280]{2,1,0:T(4,128)S(1)}, f32[3,4,1280]{2,1,0:T(4,128)S(1)}, u32[]{:S(2)}, u32[]{:S(2)}) %collective-permute-start) | collective-permute-done | bytes 61472 | tf_op jit(solution)/shard_map/ppermute | solution.py:29
  33.1 1.8 %collective-permute-done.1.refs_2_ = f32[3,4,1280]{2,1,0:T(4,128)S(1)} collective-permute-done((f32[3,4,1280]{2,1,0:T(4,128)S(1)}, f32[3,4,1280]{2,1,0:T(4,128)S(1)}, u32[]{:S(2)}, u32[]{:S(2)}) %collective-permute-start.1) | collective-permute-done | bytes 61472 | tf_op jit(solution)/shard_map/ppermute | solution.py:29
  34.9 1.3 collective-permute-start.2
  36.2 2.9 %collective-permute-done.2.refs_3_ = f32[3,4,1280]{2,1,0:T(4,128)S(1)} collective-permute-done((f32[3,4,1280]{2,1,0:T(4,128)S(1)}, f32[3,4,1280]{2,1,0:T(4,128)S(1)}, u32[]{:S(2)}, u32[]{:S(2)}) %collective-permute-start.2) | collective-permute-done | bytes 61472 | tf_op jit(solution)/shard_map/ppermute | solution.py:29
  39.1 3.3 %modulate.1 = (bf16[4,2,1,64,1280]{4,3,2,1,0:T(8,128)(2,1)S(1)}, f32[4,1,1280]{2,1,0:T(1,128)S(1)}, bf16[3,1280,384]{2,1,0:T(8,128)(2,1)S(1)}, bf16[3,1280,384]{2,1,0:T(8,128)(2,1)S(1)}) custom-call(s32[1]{0:T(128)S(6)} %copy.17.step_ref, bf16[3,1280,768]{2,1,0:T(8,128)(2,1)} %w_ref.2, f32[3,4,1280]{2,1,0:T(4,128)S(1)} %get-tuple-element.36.refs_0_, ...), custom_call_target="tpu_custom_call" | custom-call | flops 2621440 | bytes 2621440 | tf_op jit(solution)/shard_map/modulate/pallas_call | solution.py:270
  42.4 2.0 %fusion.4 = f32[4,3,128,384]{3,2,1,0:T(8,128)S(1)} fusion(bf16[4,128,1280,1]{2,1,3,0:T(8,128)(2,1)S(1)} %bitcast.118, bf16[3,1280,384]{2,1,0:T(8,128)(2,1)S(1)} %get-tuple-element.53), kind=kOutput, calls=%fused_computation.4 | convolution fusion | flops 1509949440 | bytes 6619136 | tf_op jit(solution)/shard_map/krd,cdh->kcrh/dot_general | solution.py:455
  44.4 0.9 select_convert_fusion.4
  45.3 2.0 %fusion.7 = f32[4,3,128,384]{3,2,0,1:T(8,128)S(1)} fusion(bf16[4,128,1280,1]{2,1,0,3:T(8,128)(2,1)S(1)} %bitcast.119, bf16[3,1280,384]{2,1,0:T(8,128)(2,1)S(1)} %get-tuple-element.45), kind=kOutput, calls=%fused_computation.5 | convolution fusion | flops 1509949440 | bytes 6619136 | tf_op jit(solution)/shard_map/krd,cdh->kcrh/dot_general | solution.py:455
  47.3 0.9 select_convert_fusion.9
  48.1 2.0 %collective-permute-start.12 = (f16[3,128,384]{2,1,0:T(8,128)(2,1)}, f16[3,128,384]{2,1,0:T(8,128)(2,1)S(1)}, u32[]{:S(2)}, u32[]{:S(2)}) collective-permute-start(f16[3,128,384]{2,1,0:T(8,128)(2,1)} %select_convert_fusion.9), channel_id=1, source_target_pairs={{0,4},{4,0},{8,12},{12,8},{1,5},{5,1},{9,13},{13,9},{2,6},{6,2},{1... | collective-permute-start | bytes 884744 | tf_op jit(solution)/shard_map/ppermute | solution.py:486
  50.9 4.5 %collective-permute-done.25 = f16[3,128,384]{2,1,0:T(8,128)(2,1)} collective-permute-done((f16[3,128,384]{2,1,0:T(8,128)(2,1)}, f16[3,128,384]{2,1,0:T(8,128)(2,1)}, u32[]{:S(2)}, u32[]{:S(2)}) %collective-permute-start.25) | collective-permute-done | bytes 294944 | tf_op jit(solution)/shard_map/ppermute | solution.py:486
  55.5 1.4 select_convert_fusion.2
  57.0 4.7 %collective-permute-done.12 = f16[3,128,384]{2,1,0:T(8,128)(2,1)S(1)} collective-permute-done((f16[3,128,384]{2,1,0:T(8,128)(2,1)}, f16[3,128,384]{2,1,0:T(8,128)(2,1)S(1)}, u32[]{:S(2)}, u32[]{:S(2)}) %collective-permute-start.12) | collective-permute-done | bytes 294944 | tf_op jit(solution)/shard_map/ppermute | solution.py:486
  61.7 1.3 select_convert_fusion.7
  63.2 4.8 %collective-permute-done.26 = f16[3,128,384]{2,1,0:T(8,128)(2,1)S(1)} collective-permute-done((f16[3,128,384]{2,1,0:T(8,128)(2,1)S(1)}, f16[3,128,384]{2,1,0:T(8,128)(2,1)S(1)}, u32[]{:S(2)}, u32[]{:S(2)}) %collective-permute-start.26) | collective-permute-done | bytes 294944 | tf_op jit(solution)/shard_map/ppermute | solution.py:486
  68.6 1.5 %select_convert_fusion = (f16[3,128,384]{2,1,0:T(8,128)(2,1)S(1)}, f16[3,128,384]{2,1,0:T(8,128)(2,1)S(1)}) fusion(pred[]{:T(512)S(6)} %eq.5, f16[3,128,384]{2,1,0:T(8,128)(2,1)S(1)} %collective-permute-done.27, f16[3,128,384]{2,1,0:T(8,128)(2,1)S(1)} %collective-permute-done.26, pred[]{:T(512)S(6)} %lt.9, f32[4,3,128,384]{3,2,1,0:T(8,128)} %copy-done.5, ...), kind=kLoop, calls=%fused_computation.50 | loop fusion | flops 1769472 | bytes 2359299 | tf_op jit(solution)/shard_map/convert_element_type | solution.py:485
  70.2 4.2 %collective-permute-done.13 = f16[3,128,384]{2,1,0:T(8,128)(2,1)S(1)} collective-permute-done((f16[3,128,384]{2,1,0:T(8,128)(2,1)S(1)}, f16[3,128,384]{2,1,0:T(8,128)(2,1)S(1)}, u32[]{:S(2)}, u32[]{:S(2)}) %collective-permute-start.13) | collective-permute-done | bytes 294944 | tf_op jit(solution)/shard_map/ppermute | solution.py:486
  74.6 1.6 %collective-permute-start.15 = (f16[3,128,384]{2,1,0:T(8,128)(2,1)S(1)}, f16[3,128,384]{2,1,0:T(8,128)(2,1)S(1)}, u32[]{:S(2)}, u32[]{:S(2)}) collective-permute-start(f16[3,128,384]{2,1,0:T(8,128)(2,1)S(1)} %get-tuple-element.70), channel_id=1, source_target_pairs={{0,4},{4,0},{8,12},{12,8},{1,5},{5,1},{9,13},{13,9},{2,6},{6,2},{1... | collective-permute-start | bytes 884744 | tf_op jit(solution)/shard_map/ppermute | solution.py:486
  76.2 3.1 %collective-permute-done.28 = f16[3,128,384]{2,1,0:T(8,128)(2,1)S(1)} collective-permute-done((f16[3,128,384]{2,1,0:T(8,128)(2,1)S(1)}, f16[3,128,384]{2,1,0:T(8,128)(2,1)S(1)}, u32[]{:S(2)}, u32[]{:S(2)}) %collective-permute-start.28) | collective-permute-done | bytes 294944 | tf_op jit(solution)/shard_map/ppermute | solution.py:486
  79.9 1.2 fusion.32
  81.1 0.9 attend.3
  82.1 1.5 %collective-permute-start.30 = (bf16[1,64,384]{2,1,0:T(8,128)(2,1)S(1)}, bf16[1,64,384]{2,1,0:T(8,128)(2,1)S(1)}, u32[]{:S(2)}, u32[]{:S(2)}) collective-permute-start(bf16[1,64,384]{2,1,0:T(8,128)(2,1)S(1)} %get-tuple-element.59), channel_id=1, source_target_pairs={{0,2},{2,0},{1,3},{3,1},{4,6},{6,4},{5,7},{7,5},{8,10},{10,8},{9,1... | collective-permute-start | bytes 147464 | tf_op jit(solution)/shard_map/ppermute | solution.py:29
  83.6 1.3 collective-permute-done.15
  85.0 0.9 attend.2
  86.6 23.6 %collective-permute-done.30 = bf16[1,64,384]{2,1,0:T(8,128)(2,1)S(1)} collective-permute-done((bf16[1,64,384]{2,1,0:T(8,128)(2,1)S(1)}, bf16[1,64,384]{2,1,0:T(8,128)(2,1)S(1)}, u32[]{:S(2)}, u32[]{:S(2)}) %collective-permute-start.30) | collective-permute-done | bytes 49184 | tf_op jit(solution)/shard_map/ppermute | solution.py:29
  110.9 2.6 %collective-permute-start.34 = (bf16[2,1,64,384]{3,2,1,0:T(8,128)(2,1)S(1)}, bf16[2,1,64,384]{3,2,1,0:T(8,128)(2,1)S(1)}, u32[]{:S(2)}, u32[]{:S(2)}) collective-permute-start(bf16[2,1,64,384]{3,2,1,0:T(8,128)(2,1)S(1)} %pad_maximum_fusion.2.refs_8_), channel_id=1, source_target_pairs={{0,8},{4,12},{8,0},{12,4},{1,9},{5,13},{9,1},{13,5},{2,10},{6,14},... | collective-permute-start | bytes 294920 | tf_op jit(solution)/shard_map/ppermute | solution.py:29
  114.4 2.4 %collective-permute-done.32.refs_10_ = bf16[2,1,64,384]{3,2,1,0:T(8,128)(2,1)S(1)} collective-permute-done((bf16[2,1,64,384]{3,2,1,0:T(8,128)(2,1)S(1)}, bf16[2,1,64,384]{3,2,1,0:T(8,128)(2,1)S(1)}, u32[]{:S(2)}, u32[]{:S(2)}) %collective-permute-start.32) | collective-permute-done | bytes 98336 | tf_op jit(solution)/shard_map/ppermute | solution.py:29
  116.8 1.8 %collective-permute-done.34.refs_12_ = bf16[2,1,64,384]{3,2,1,0:T(8,128)(2,1)S(1)} collective-permute-done((bf16[2,1,64,384]{3,2,1,0:T(8,128)(2,1)S(1)}, bf16[2,1,64,384]{3,2,1,0:T(8,128)(2,1)S(1)}, u32[]{:S(2)}, u32[]{:S(2)}) %collective-permute-start.34) | collective-permute-done | bytes 98336 | tf_op jit(solution)/shard_map/ppermute | solution.py:29
  119.1 3.7 %collective-permute-start.23 = (bf16[2,1,64,384]{3,2,1,0:T(8,128)(2,1)S(1)}, bf16[2,1,64,384]{3,2,1,0:T(8,128)(2,1)S(1)}, u32[]{:S(2)}, u32[]{:S(2)}) collective-permute-start(bf16[2,1,64,384]{3,2,1,0:T(8,128)(2,1)S(1)} %pad_maximum_fusion.1.refs_0_), channel_id=1, source_target_pairs={{0,12},{4,0},{8,4},{12,8},{1,13},{5,1},{9,5},{13,9},{2,14},{6,2},{... | collective-permute-start | bytes 294920 | tf_op jit(solution)/shard_map/ppermute | solution.py:29
  123.6 3.2 %collective-permute-done.21.refs_4_ = bf16[2,1,64,384]{3,2,1,0:T(8,128)(2,1)S(1)} collective-permute-done((bf16[2,1,64,384]{3,2,1,0:T(8,128)(2,1)S(1)}, bf16[2,1,64,384]{3,2,1,0:T(8,128)(2,1)S(1)}, u32[]{:S(2)}, u32[]{:S(2)}) %collective-permute-start.21) | collective-permute-done | bytes 98336 | tf_op jit(solution)/shard_map/ppermute | solution.py:29
  129.4 1.5 %project.1 = (f32[1,64,640]{2,1,0:T(8,128)S(1)}, bf16[1,64,640]{2,1,0:T(8,128)(2,1)S(1)}, bf16[1,64,640]{2,1,0:T(8,128)(2,1)S(1)}, bf16[1,64,640]{2,1,0:T(8,128)(2,1)S(1)}, bf16[1,64,640]{2,1,0:T(8,128)(2,1)S(1)}) custom-call(f32[4,1,1280]{2,1,0:T(1,128)S(1)} %get-tuple-element.44.coef_ref, bf16[2,1,64,384]{3,2,1,0:T(8,128)(2,1)S(1)} %pad_maximum_fusion.1.refs_0_, ...), custom_call_target="tpu_custom_call" | custom-call | flops 1006632960 | bytes 5505024 | tf_op jit(solution)/shard_map/project/pallas_call | solution.py:366
  130.9 3.5 %collective-permute-start.42 = (bf16[1,64,640]{2,1,0:T(8,128)(2,1)S(1)}, bf16[1,64,640]{2,1,0:T(8,128)(2,1)S(1)}, u32[]{:S(2)}, u32[]{:S(2)}) collective-permute-start(bf16[1,64,640]{2,1,0:T(8,128)(2,1)S(1)} %get-tuple-element.64), channel_id=1, source_target_pairs={{0,12},{4,0},{8,4},{12,8},{1,13},{5,1},{9,5},{13,9},{2,14},{6,2},{... | collective-permute-start | bytes 245768 | tf_op jit(solution)/shard_map/ppermute | solution.py:29
  135.0 2.2 %collective-permute-done.42.refs_2_ = bf16[1,64,640]{2,1,0:T(8,128)(2,1)S(1)} collective-permute-done((bf16[1,64,640]{2,1,0:T(8,128)(2,1)S(1)}, bf16[1,64,640]{2,1,0:T(8,128)(2,1)S(1)}, u32[]{:S(2)}, u32[]{:S(2)}) %collective-permute-start.42) | collective-permute-done | bytes 81952 | tf_op jit(solution)/shard_map/ppermute | solution.py:29
  137.3 5.1 %collective-permute-done.44.refs_4_ = bf16[1,64,640]{2,1,0:T(8,128)(2,1)S(1)} collective-permute-done((bf16[1,64,640]{2,1,0:T(8,128)(2,1)S(1)}, bf16[1,64,640]{2,1,0:T(8,128)(2,1)S(1)}, u32[]{:S(2)}, u32[]{:S(2)}) %collective-permute-start.44) | collective-permute-done | bytes 81952 | tf_op jit(solution)/shard_map/ppermute | solution.py:29
  142.9 0.8 collective-permute-done.45.refs_5_
  143.8 1.0 finish.1
  (84 shorter events, 11.6 us)
Async XLA Ops:
  1.5 8.4 %collective-permute-start.6 = (bf16[1,32,1408]{2,1,0:T(8,128)(2,1)S(1)}, bf16[1,32,1408]{2,1,0:T(8,128)(2,1)S(1)}, u32[]{:S(2)}, u32[]{:S(2)}) collective-permute-start(bf16[1,32,1408]{2,1,0:T(8,128)(2,1)S(1)} %get-tuple-element.41), channel_id=1, source_target_pairs={{0,4},{4,8},{8,12},{12,0},{1,5},{5,9},{9,13},{13,1},{2,6},{6,10},{... | collective-permute-start | bytes 270344 | tf_op jit(solution)/shard_map/ppermute | solution.py:29
  4.6 8.6 %collective-permute-start.7 = (bf16[1,32,1408]{2,1,0:T(8,128)(2,1)S(1)}, bf16[1,32,1408]{2,1,0:T(8,128)(2,1)S(1)}, u32[]{:S(2)}, u32[]{:S(2)}) collective-permute-start(bf16[1,32,1408]{2,1,0:T(8,128)(2,1)S(1)} %get-tuple-element.42), channel_id=1, source_target_pairs={{0,8},{4,12},{8,0},{12,4},{1,9},{5,13},{9,1},{13,5},{2,10},{6,14},... | collective-permute-start | bytes 270344 | tf_op jit(solution)/shard_map/ppermute | solution.py:29
  7.2 6.3 %collective-permute-start.8 = (bf16[1,32,1408]{2,1,0:T(8,128)(2,1)S(1)}, bf16[1,32,1408]{2,1,0:T(8,128)(2,1)S(1)}, u32[]{:S(2)}, u32[]{:S(2)}) collective-permute-start(bf16[1,32,1408]{2,1,0:T(8,128)(2,1)S(1)} %get-tuple-element.43), channel_id=1, source_target_pairs={{0,12},{4,0},{8,4},{12,8},{1,13},{5,1},{9,5},{13,9},{2,14},{6,2},{... | collective-permute-start | bytes 270344 | tf_op jit(solution)/shard_map/ppermute | solution.py:29
  13.5 8.2 %collective-permute-start.10 = (bf16[3,1,32,1408]{3,2,1,0:T(8,128)(2,1)S(1)}, bf16[3,1,32,1408]{3,2,1,0:T(8,128)(2,1)S(1)}, u32[]{:S(2)}, u32[]{:S(2)}) collective-permute-start(bf16[3,1,32,1408]{3,2,1,0:T(8,128)(2,1)S(1)} %pad_maximum_fusion.refs_8_), channel_id=1, source_target_pairs={{0,2},{2,0},{1,3},{3,1},{4,6},{6,4},{5,7},{7,5},{8,10},{10,8},{9,1... | collective-permute-start | bytes 811016 | tf_op jit(solution)/shard_map/ppermute | solution.py:29
  15.0 24.1 %collective-permute-start.9 = (bf16[3,1,32,1408]{3,2,1,0:T(8,128)(2,1)S(1)}, bf16[3,1,32,1408]{3,2,1,0:T(8,128)(2,1)S(1)}, u32[]{:S(2)}, u32[]{:S(2)}) collective-permute-start(bf16[3,1,32,1408]{3,2,1,0:T(8,128)(2,1)S(1)} %pad_maximum_fusion.refs_8_), channel_id=1, source_target_pairs={{0,1},{1,0},{2,3},{3,2},{4,5},{5,4},{6,7},{7,6},{8,9},{9,8},{10,11... | collective-permute-start | bytes 811016 | tf_op jit(solution)/shard_map/ppermute | solution.py:29
  21.6 17.5 %collective-permute-start.11 = (bf16[3,1,32,1408]{3,2,1,0:T(8,128)(2,1)S(1)}, bf16[3,1,32,1408]{3,2,1,0:T(8,128)(2,1)S(1)}, u32[]{:S(2)}, u32[]{:S(2)}) collective-permute-start(bf16[3,1,32,1408]{3,2,1,0:T(8,128)(2,1)S(1)} %collective-permute-done.10.refs_10_), channel_id=1, source_target_pairs={{0,1},{1,0},{2,3},{3,2},{4,5},{5,4},{6,7},{7,6},{8,9},{9,8},{10,11... | collective-permute-start | bytes 811016 | tf_op jit(solution)/shard_map/ppermute | solution.py:29
  21.7 10.9 %collective-permute-start.4 = (bf16[1,32,1408]{2,1,0:T(8,128)(2,1)S(1)}, bf16[1,32,1408]{2,1,0:T(8,128)(2,1)S(1)}, u32[]{:S(2)}, u32[]{:S(2)}) collective-permute-start(bf16[1,32,1408]{2,1,0:T(8,128)(2,1)S(1)} %get-tuple-element.40.refs_4_), channel_id=1, source_target_pairs={{0,2},{2,0},{1,3},{3,1},{4,6},{6,4},{5,7},{7,5},{8,10},{10,8},{9,1... | collective-permute-start | bytes 270344 | tf_op jit(solution)/shard_map/ppermute | solution.py:29
  26.2 6.4 %collective-permute-start = (f32[3,4,1280]{2,1,0:T(4,128)S(1)}, f32[3,4,1280]{2,1,0:T(4,128)S(1)}, u32[]{:S(2)}, u32[]{:S(2)}) collective-permute-start(f32[3,4,1280]{2,1,0:T(4,128)S(1)} %get-tuple-element.37), channel_id=1, source_target_pairs={{0,4},{4,8},{8,12},{12,0},{1,5},{5,9},{9,13},{13,1},{2,6},{6,10},{... | collective-permute-start | bytes 184328 | tf_op jit(solution)/shard_map/ppermute | solution.py:29
  28.7 6.1 %collective-permute-start.1 = (f32[3,4,1280]{2,1,0:T(4,128)S(1)}, f32[3,4,1280]{2,1,0:T(4,128)S(1)}, u32[]{:S(2)}, u32[]{:S(2)}) collective-permute-start(f32[3,4,1280]{2,1,0:T(4,128)S(1)} %get-tuple-element.38), channel_id=1, source_target_pairs={{0,8},{4,12},{8,0},{12,4},{1,9},{5,13},{9,1},{13,5},{2,10},{6,14},... | collective-permute-start | bytes 184328 | tf_op jit(solution)/shard_map/ppermute | solution.py:29
  32.5 6.6 %collective-permute-start.3 = (bf16[1,32,1408]{2,1,0:T(8,128)(2,1)S(1)}, bf16[1,32,1408]{2,1,0:T(8,128)(2,1)S(1)}, u32[]{:S(2)}, u32[]{:S(2)}) collective-permute-start(bf16[1,32,1408]{2,1,0:T(8,128)(2,1)S(1)} %get-tuple-element.40.refs_4_), channel_id=1, source_target_pairs={{0,1},{1,0},{2,3},{3,2},{4,5},{5,4},{6,7},{7,6},{8,9},{9,8},{10,11... | collective-permute-start | bytes 270344 | tf_op jit(solution)/shard_map/ppermute | solution.py:29
  32.6 6.5 %collective-permute-start.5 = (bf16[1,32,1408]{2,1,0:T(8,128)(2,1)S(1)}, bf16[1,32,1408]{2,1,0:T(8,128)(2,1)S(1)}, u32[]{:S(2)}, u32[]{:S(2)}) collective-permute-start(bf16[1,32,1408]{2,1,0:T(8,128)(2,1)S(1)} %collective-permute-done.4.refs_6_), channel_id=1, source_target_pairs={{0,1},{1,0},{2,3},{3,2},{4,5},{5,4},{6,7},{7,6},{8,9},{9,8},{10,11... | collective-permute-start | bytes 270344 | tf_op jit(solution)/shard_map/ppermute | solution.py:29
  34.9 4.2 %collective-permute-start.2 = (f32[3,4,1280]{2,1,0:T(4,128)S(1)}, f32[3,4,1280]{2,1,0:T(4,128)S(1)}, u32[]{:S(2)}, u32[]{:S(2)}) collective-permute-start(f32[3,4,1280]{2,1,0:T(4,128)S(1)} %get-tuple-element.39), channel_id=1, source_target_pairs={{0,12},{4,0},{8,4},{12,8},{1,13},{5,1},{9,5},{13,9},{2,14},{6,2},{... | collective-permute-start | bytes 184328 | tf_op jit(solution)/shard_map/ppermute | solution.py:29
  45.3 10.2 %collective-permute-start.25 = (f16[3,128,384]{2,1,0:T(8,128)(2,1)}, f16[3,128,384]{2,1,0:T(8,128)(2,1)}, u32[]{:S(2)}, u32[]{:S(2)}) collective-permute-start(f16[3,128,384]{2,1,0:T(8,128)(2,1)} %select_convert_fusion.4), channel_id=1, source_target_pairs={{0,4},{4,0},{8,12},{12,8},{1,5},{5,1},{9,13},{13,9},{2,6},{6,2},{1... | collective-permute-start | bytes 884744 | tf_op jit(solution)/shard_map/ppermute | solution.py:486
  48.1 13.5 %collective-permute-start.12 = (f16[3,128,384]{2,1,0:T(8,128)(2,1)}, f16[3,128,384]{2,1,0:T(8,128)(2,1)S(1)}, u32[]{:S(2)}, u32[]{:S(2)}) collective-permute-start(f16[3,128,384]{2,1,0:T(8,128)(2,1)} %select_convert_fusion.9), channel_id=1, source_target_pairs={{0,4},{4,0},{8,12},{12,8},{1,5},{5,1},{9,13},{13,9},{2,6},{6,2},{1... | collective-permute-start | bytes 884744 | tf_op jit(solution)/shard_map/ppermute | solution.py:486
  50.8 25.4 %collective-permute-start.38 = (bf16[640,768]{1,0:T(8,128)(2,1)S(1)}, bf16[640,768]{1,0:T(8,128)(2,1)S(1)}, u32[]{:S(2)}, u32[]{:S(2)}) collective-permute-start(bf16[640,768]{1,0:T(8,128)(2,1)S(1)} %get-tuple-element.61), channel_id=1, source_target_pairs={{0,1},{1,0},{2,3},{3,2},{4,5},{5,4},{6,7},{7,6},{8,9},{9,8},{10,11... | collective-permute-start | bytes 2949128 | tf_op jit(solution)/shard_map/ppermute | solution.py:29
  56.9 11.1 %collective-permute-start.26 = (f16[3,128,384]{2,1,0:T(8,128)(2,1)S(1)}, f16[3,128,384]{2,1,0:T(8,128)(2,1)S(1)}, u32[]{:S(2)}, u32[]{:S(2)}) collective-permute-start(f16[3,128,384]{2,1,0:T(8,128)(2,1)S(1)} %get-tuple-element.72), channel_id=1, source_target_pairs={{0,4},{4,0},{8,12},{12,8},{1,5},{5,1},{9,13},{13,9},{2,6},{6,2},{1... | collective-permute-start | bytes 884744 | tf_op jit(solution)/shard_map/ppermute | solution.py:486
  56.9 11.6 %collective-permute-start.27 = (f16[3,128,384]{2,1,0:T(8,128)(2,1)S(1)}, f16[3,128,384]{2,1,0:T(8,128)(2,1)S(1)}, u32[]{:S(2)}, u32[]{:S(2)}) collective-permute-start(f16[3,128,384]{2,1,0:T(8,128)(2,1)S(1)} %get-tuple-element.71), channel_id=1, source_target_pairs={{0,1},{1,0},{4,8},{5,9},{8,4},{9,5},{12,13},{13,12},{2,3},{3,2},{6... | collective-permute-start | bytes 884744 | tf_op jit(solution)/shard_map/ppermute | solution.py:488
  63.0 11.3 %collective-permute-start.13 = (f16[3,128,384]{2,1,0:T(8,128)(2,1)S(1)}, f16[3,128,384]{2,1,0:T(8,128)(2,1)S(1)}, u32[]{:S(2)}, u32[]{:S(2)}) collective-permute-start(f16[3,128,384]{2,1,0:T(8,128)(2,1)S(1)} %get-tuple-element.74), channel_id=1, source_target_pairs={{0,4},{4,0},{8,12},{12,8},{1,5},{5,1},{9,13},{13,9},{2,6},{6,2},{1... | collective-permute-start | bytes 884744 | tf_op jit(solution)/shard_map/ppermute | solution.py:486
  63.1 11.3 %collective-permute-start.14 = (f16[3,128,384]{2,1,0:T(8,128)(2,1)S(1)}, f16[3,128,384]{2,1,0:T(8,128)(2,1)S(1)}, u32[]{:S(2)}, u32[]{:S(2)}) collective-permute-start(f16[3,128,384]{2,1,0:T(8,128)(2,1)S(1)} %get-tuple-element.73), channel_id=1, source_target_pairs={{0,1},{1,0},{4,8},{5,9},{8,4},{9,5},{12,13},{13,12},{2,3},{3,2},{6... | collective-permute-start | bytes 884744 | tf_op jit(solution)/shard_map/ppermute | solution.py:488
  68.0 46.3 %collective-permute-start.39 = (bf16[640,768]{1,0:T(8,128)(2,1)S(1)}, bf16[640,768]{1,0:T(8,128)(2,1)S(1)}, u32[]{:S(2)}, u32[]{:S(2)}) collective-permute-start(bf16[640,768]{1,0:T(8,128)(2,1)S(1)} %get-tuple-element.60.refs_16_), channel_id=1, source_target_pairs={{0,2},{2,0},{1,3},{3,1},{4,6},{6,4},{5,7},{7,5},{8,10},{10,8},{9,1... | collective-permute-start | bytes 2949128 | tf_op jit(solution)/shard_map/ppermute | solution.py:29
  70.1 9.2 %collective-permute-start.28 = (f16[3,128,384]{2,1,0:T(8,128)(2,1)S(1)}, f16[3,128,384]{2,1,0:T(8,128)(2,1)S(1)}, u32[]{:S(2)}, u32[]{:S(2)}) collective-permute-start(f16[3,128,384]{2,1,0:T(8,128)(2,1)S(1)} %get-tuple-element.68), channel_id=1, source_target_pairs={{0,4},{4,0},{8,12},{12,8},{1,5},{5,1},{9,13},{13,9},{2,6},{6,2},{1... | collective-permute-start | bytes 884744 | tf_op jit(solution)/shard_map/ppermute | solution.py:486
  74.3 5.5 %collective-permute-start.29 = (f16[3,128,384]{2,1,0:T(8,128)(2,1)S(1)}, f16[3,128,384]{2,1,0:T(8,128)(2,1)S(1)}, u32[]{:S(2)}, u32[]{:S(2)}) collective-permute-start(f16[3,128,384]{2,1,0:T(8,128)(2,1)S(1)} %get-tuple-element.67), channel_id=1, source_target_pairs={{0,1},{1,0},{4,8},{5,9},{8,4},{9,5},{12,13},{13,12},{2,3},{3,2},{6... | collective-permute-start | bytes 884744 | tf_op jit(solution)/shard_map/ppermute | solution.py:488
  74.6 10.3 %collective-permute-start.15 = (f16[3,128,384]{2,1,0:T(8,128)(2,1)S(1)}, f16[3,128,384]{2,1,0:T(8,128)(2,1)S(1)}, u32[]{:S(2)}, u32[]{:S(2)}) collective-permute-start(f16[3,128,384]{2,1,0:T(8,128)(2,1)S(1)} %get-tuple-element.70), channel_id=1, source_target_pairs={{0,4},{4,0},{8,12},{12,8},{1,5},{5,1},{9,13},{13,9},{2,6},{6,2},{1... | collective-permute-start | bytes 884744 | tf_op jit(solution)/shard_map/ppermute | solution.py:486
  76.2 8.7 %collective-permute-start.16 = (f16[3,128,384]{2,1,0:T(8,128)(2,1)S(1)}, f16[3,128,384]{2,1,0:T(8,128)(2,1)S(1)}, u32[]{:S(2)}, u32[]{:S(2)}) collective-permute-start(f16[3,128,384]{2,1,0:T(8,128)(2,1)S(1)} %get-tuple-element.69), channel_id=1, source_target_pairs={{0,1},{1,0},{4,8},{5,9},{8,4},{9,5},{12,13},{13,12},{2,3},{3,2},{6... | collective-permute-start | bytes 884744 | tf_op jit(solution)/shard_map/ppermute | solution.py:488
  79.3 50.1 %collective-permute-start.40 = (bf16[640,768]{1,0:T(8,128)(2,1)S(1)}, bf16[640,768]{1,0:T(8,128)(2,1)S(1)}, u32[]{:S(2)}, u32[]{:S(2)}) collective-permute-start(bf16[640,768]{1,0:T(8,128)(2,1)S(1)} %collective-permute-done.38.refs_17_), channel_id=1, source_target_pairs={{0,2},{2,0},{1,3},{3,1},{4,6},{6,4},{5,7},{7,5},{8,10},{10,8},{9,1... | collective-permute-start | bytes 2949128 | tf_op jit(solution)/shard_map/ppermute | solution.py:29
  82.1 28.2 %collective-permute-start.30 = (bf16[1,64,384]{2,1,0:T(8,128)(2,1)S(1)}, bf16[1,64,384]{2,1,0:T(8,128)(2,1)S(1)}, u32[]{:S(2)}, u32[]{:S(2)}) collective-permute-start(bf16[1,64,384]{2,1,0:T(8,128)(2,1)S(1)} %get-tuple-element.59), channel_id=1, source_target_pairs={{0,2},{2,0},{1,3},{3,1},{4,6},{6,4},{5,7},{7,5},{8,10},{10,8},{9,1... | collective-permute-start | bytes 147464 | tf_op jit(solution)/shard_map/ppermute | solution.py:29
  86.0 27.5 %collective-permute-start.17 = (bf16[1,64,384]{2,1,0:T(8,128)(2,1)S(1)}, bf16[1,64,384]{2,1,0:T(8,128)(2,1)S(1)}, u32[]{:S(2)}, u32[]{:S(2)}) collective-permute-start(bf16[1,64,384]{2,1,0:T(8,128)(2,1)S(1)} %get-tuple-element.52), channel_id=1, source_target_pairs={{0,2},{2,0},{1,3},{3,1},{4,6},{6,4},{5,7},{7,5},{8,10},{10,8},{9,1... | collective-permute-start | bytes 147464 | tf_op jit(solution)/shard_map/ppermute | solution.py:29
  110.2 6.6 %collective-permute-start.32 = (bf16[2,1,64,384]{3,2,1,0:T(8,128)(2,1)S(1)}, bf16[2,1,64,384]{3,2,1,0:T(8,128)(2,1)S(1)}, u32[]{:S(2)}, u32[]{:S(2)}) collective-permute-start(bf16[2,1,64,384]{3,2,1,0:T(8,128)(2,1)S(1)} %pad_maximum_fusion.2.refs_8_), channel_id=1, source_target_pairs={{0,4},{4,8},{8,12},{12,0},{1,5},{5,9},{9,13},{13,1},{2,6},{6,10},{... | collective-permute-start | bytes 294920 | tf_op jit(solution)/shard_map/ppermute | solution.py:29
  110.9 7.7 %collective-permute-start.34 = (bf16[2,1,64,384]{3,2,1,0:T(8,128)(2,1)S(1)}, bf16[2,1,64,384]{3,2,1,0:T(8,128)(2,1)S(1)}, u32[]{:S(2)}, u32[]{:S(2)}) collective-permute-start(bf16[2,1,64,384]{3,2,1,0:T(8,128)(2,1)S(1)} %pad_maximum_fusion.2.refs_8_), channel_id=1, source_target_pairs={{0,8},{4,12},{8,0},{12,4},{1,9},{5,13},{9,1},{13,5},{2,10},{6,14},... | collective-permute-start | bytes 294920 | tf_op jit(solution)/shard_map/ppermute | solution.py:29
  113.5 5.6 %collective-permute-start.36 = (bf16[2,1,64,384]{3,2,1,0:T(8,128)(2,1)S(1)}, bf16[2,1,64,384]{3,2,1,0:T(8,128)(2,1)S(1)}, u32[]{:S(2)}, u32[]{:S(2)}) collective-permute-start(bf16[2,1,64,384]{3,2,1,0:T(8,128)(2,1)S(1)} %pad_maximum_fusion.2.refs_8_), channel_id=1, source_target_pairs={{0,12},{4,0},{8,4},{12,8},{1,13},{5,1},{9,5},{13,9},{2,14},{6,2},{... | collective-permute-start | bytes 294920 | tf_op jit(solution)/shard_map/ppermute | solution.py:29
  114.3 8.6 %collective-permute-start.31 = (bf16[2,1,64,384]{3,2,1,0:T(8,128)(2,1)S(1)}, bf16[2,1,64,384]{3,2,1,0:T(8,128)(2,1)S(1)}, u32[]{:S(2)}, u32[]{:S(2)}) collective-permute-start(bf16[2,1,64,384]{3,2,1,0:T(8,128)(2,1)S(1)} %pad_maximum_fusion.2.refs_8_), channel_id=1, source_target_pairs={{0,1},{1,0},{2,3},{3,2},{4,5},{5,4},{6,7},{7,6},{8,9},{9,8},{10,11... | collective-permute-start | bytes 294920 | tf_op jit(solution)/shard_map/ppermute | solution.py:29
  116.8 6.8 %collective-permute-start.19 = (bf16[2,1,64,384]{3,2,1,0:T(8,128)(2,1)S(1)}, bf16[2,1,64,384]{3,2,1,0:T(8,128)(2,1)S(1)}, u32[]{:S(2)}, u32[]{:S(2)}) collective-permute-start(bf16[2,1,64,384]{3,2,1,0:T(8,128)(2,1)S(1)} %pad_maximum_fusion.1.refs_0_), channel_id=1, source_target_pairs={{0,4},{4,8},{8,12},{12,0},{1,5},{5,9},{9,13},{13,1},{2,6},{6,10},{... | collective-permute-start | bytes 294920 | tf_op jit(solution)/shard_map/ppermute | solution.py:29
  118.6 8.2 %collective-permute-start.21 = (bf16[2,1,64,384]{3,2,1,0:T(8,128)(2,1)S(1)}, bf16[2,1,64,384]{3,2,1,0:T(8,128)(2,1)S(1)}, u32[]{:S(2)}, u32[]{:S(2)}) collective-permute-start(bf16[2,1,64,384]{3,2,1,0:T(8,128)(2,1)S(1)} %pad_maximum_fusion.1.refs_0_), channel_id=1, source_target_pairs={{0,8},{4,12},{8,0},{12,4},{1,9},{5,13},{9,1},{13,5},{2,10},{6,14},... | collective-permute-start | bytes 294920 | tf_op jit(solution)/shard_map/ppermute | solution.py:29
  119.1 7.7 %collective-permute-start.23 = (bf16[2,1,64,384]{3,2,1,0:T(8,128)(2,1)S(1)}, bf16[2,1,64,384]{3,2,1,0:T(8,128)(2,1)S(1)}, u32[]{:S(2)}, u32[]{:S(2)}) collective-permute-start(bf16[2,1,64,384]{3,2,1,0:T(8,128)(2,1)S(1)} %pad_maximum_fusion.1.refs_0_), channel_id=1, source_target_pairs={{0,12},{4,0},{8,4},{12,8},{1,13},{5,1},{9,5},{13,9},{2,14},{6,2},{... | collective-permute-start | bytes 294920 | tf_op jit(solution)/shard_map/ppermute | solution.py:29
  122.9 4.4 %collective-permute-start.18 = (bf16[2,1,64,384]{3,2,1,0:T(8,128)(2,1)S(1)}, bf16[2,1,64,384]{3,2,1,0:T(8,128)(2,1)S(1)}, u32[]{:S(2)}, u32[]{:S(2)}) collective-permute-start(bf16[2,1,64,384]{3,2,1,0:T(8,128)(2,1)S(1)} %pad_maximum_fusion.1.refs_0_), channel_id=1, source_target_pairs={{0,1},{1,0},{2,3},{3,2},{4,5},{5,4},{6,7},{7,6},{8,9},{9,8},{10,11... | collective-permute-start | bytes 294920 | tf_op jit(solution)/shard_map/ppermute | solution.py:29
  123.6 3.7 %collective-permute-start.33 = (bf16[2,1,64,384]{3,2,1,0:T(8,128)(2,1)S(1)}, bf16[2,1,64,384]{3,2,1,0:T(8,128)(2,1)S(1)}, u32[]{:S(2)}, u32[]{:S(2)}) collective-permute-start(bf16[2,1,64,384]{3,2,1,0:T(8,128)(2,1)S(1)} %collective-permute-done.32.refs_10_), channel_id=1, source_target_pairs={{0,1},{1,0},{2,3},{3,2},{4,5},{5,4},{6,7},{7,6},{8,9},{9,8},{10,11... | collective-permute-start | bytes 294920 | tf_op jit(solution)/shard_map/ppermute | solution.py:29
  126.8 1.3 collective-permute-start.35
  126.8 1.5 %collective-permute-start.37 = (bf16[2,1,64,384]{3,2,1,0:T(8,128)(2,1)S(1)}, bf16[2,1,64,384]{3,2,1,0:T(8,128)(2,1)S(1)}, u32[]{:S(2)}, u32[]{:S(2)}) collective-permute-start(bf16[2,1,64,384]{3,2,1,0:T(8,128)(2,1)S(1)} %collective-permute-done.36.refs_14_), channel_id=1, source_target_pairs={{0,1},{1,0},{2,3},{3,2},{4,5},{5,4},{6,7},{7,6},{8,9},{9,8},{10,11... | collective-permute-start | bytes 294920 | tf_op jit(solution)/shard_map/ppermute | solution.py:29
  127.3 1.3 collective-permute-start.20
  127.4 1.4 collective-permute-start.22
  128.1 1.3 collective-permute-start.24
  130.9 6.3 %collective-permute-start.42 = (bf16[1,64,640]{2,1,0:T(8,128)(2,1)S(1)}, bf16[1,64,640]{2,1,0:T(8,128)(2,1)S(1)}, u32[]{:S(2)}, u32[]{:S(2)}) collective-permute-start(bf16[1,64,640]{2,1,0:T(8,128)(2,1)S(1)} %get-tuple-element.64), channel_id=1, source_target_pairs={{0,12},{4,0},{8,4},{12,8},{1,13},{5,1},{9,5},{13,9},{2,14},{6,2},{... | collective-permute-start | bytes 245768 | tf_op jit(solution)/shard_map/ppermute | solution.py:29
  134.4 8.0 %collective-permute-start.44 = (bf16[1,64,640]{2,1,0:T(8,128)(2,1)S(1)}, bf16[1,64,640]{2,1,0:T(8,128)(2,1)S(1)}, u32[]{:S(2)}, u32[]{:S(2)}) collective-permute-start(bf16[1,64,640]{2,1,0:T(8,128)(2,1)S(1)} %get-tuple-element.65), channel_id=1, source_target_pairs={{0,8},{4,12},{8,0},{12,4},{1,9},{5,13},{9,1},{13,5},{2,10},{6,14},... | collective-permute-start | bytes 245768 | tf_op jit(solution)/shard_map/ppermute | solution.py:29
  134.4 8.0 %collective-permute-start.46 = (bf16[1,64,640]{2,1,0:T(8,128)(2,1)S(1)}, bf16[1,64,640]{2,1,0:T(8,128)(2,1)S(1)}, u32[]{:S(2)}, u32[]{:S(2)}) collective-permute-start(bf16[1,64,640]{2,1,0:T(8,128)(2,1)S(1)} %get-tuple-element.66), channel_id=1, source_target_pairs={{0,4},{4,8},{8,12},{12,0},{1,5},{5,9},{9,13},{13,1},{2,6},{6,10},{... | collective-permute-start | bytes 245768 | tf_op jit(solution)/shard_map/ppermute | solution.py:29
  135.0 7.9 %collective-permute-start.41 = (bf16[1,64,640]{2,1,0:T(8,128)(2,1)S(1)}, bf16[1,64,640]{2,1,0:T(8,128)(2,1)S(1)}, u32[]{:S(2)}, u32[]{:S(2)}) collective-permute-start(bf16[1,64,640]{2,1,0:T(8,128)(2,1)S(1)} %get-tuple-element.63), channel_id=1, source_target_pairs={{0,1},{1,0},{2,3},{3,2},{4,5},{5,4},{6,7},{7,6},{8,9},{9,8},{10,11... | collective-permute-start | bytes 245768 | tf_op jit(solution)/shard_map/ppermute | solution.py:29
  137.3 5.7 %collective-permute-start.43 = (bf16[1,64,640]{2,1,0:T(8,128)(2,1)S(1)}, bf16[1,64,640]{2,1,0:T(8,128)(2,1)S(1)}, u32[]{:S(2)}, u32[]{:S(2)}) collective-permute-start(bf16[1,64,640]{2,1,0:T(8,128)(2,1)S(1)} %collective-permute-done.42.refs_2_), channel_id=1, source_target_pairs={{0,1},{1,0},{2,3},{3,2},{4,5},{5,4},{6,7},{7,6},{8,9},{9,8},{10,11... | collective-permute-start | bytes 245768 | tf_op jit(solution)/shard_map/ppermute | solution.py:29
  142.4 1.3 collective-permute-start.45
  142.4 1.4 collective-permute-start.47
  (7 other events, 49.1 us)

commit v10 on v9

--- a/solution.py
+++ b/solution.py
@@ -199,23 +199,18 @@
     )(weights)
 
 
-def modulate_kernel(n_tm, n_seq, n_mp, cuts, step_ref, w_ref, *refs):
+def modulate_kernel(n_tm, n_seq, n_mp, step_ref, w_ref, *refs):
     sides = n_seq * n_mp
     shares, near, far = refs[:n_tm], refs[n_tm : n_tm + sides], refs[n_tm + sides :][:sides]
-    hidden_ref, coef_ref, *w_outs, mod_scr, sems = refs[n_tm + 2 * sides :]
+    hidden_ref, coef_ref, w_out, mod_scr, sems = refs[n_tm + 2 * sides :]
     stride = w_ref.shape[1] // DMA_PIECES
     copies = []
-    for (lane, size), out in zip(cuts, w_outs):
-        for c in range(w_ref.shape[0]):
-            for piece in range(DMA_PIECES):
-                rows_here = pl.ds(piece * stride, stride)
-                copies.append(
-                    pltpu.make_async_copy(
-                        w_ref.at[c, rows_here, pl.ds(lane, size)],
-                        out.at[c, rows_here],
-                        sems.at[len(copies)],
-                    )
-                )
+    for c in range(w_ref.shape[0]):
+        for piece in range(DMA_PIECES):
+            at = c, pl.ds(piece * stride, stride)
+            copies.append(
+                pltpu.make_async_copy(w_ref.at[at], w_out.at[at], sems.at[len(copies)])
+            )
     z, k = lax.axis_index("tm"), pl.program_id(0)
     frames, part, wide = near[0].shape
     depth = wide - LANES
@@ -260,7 +255,7 @@
             copy.wait()
 
 
-def modulate(start_step, w_qkv, cuts, shares, near, far):
+def modulate(start_step, w_qkv, shares, near, far):
     n_tm, n_seq, n_mp = len(shares), len(near), len(near[0])
     frames, part, wide = near[0][0].shape
     three = w_qkv.shape[0]
@@ -268,7 +263,7 @@
     window = shares[0].shape[1]
     shape = (n_tm, n_seq, frames, n_mp * part, depth)
     return pl.pallas_call(
-        functools.partial(modulate_kernel, n_tm, n_seq, n_mp, cuts),
+        functools.partial(modulate_kernel, n_tm, n_seq, n_mp),
         grid=(n_tm,),
         in_specs=[pl.BlockSpec(memory_space=pltpu.SMEM), pl.BlockSpec(memory_space=pltpu.HBM)]
         + [pl.BlockSpec((3, window, depth), lambda k: (0, 0, 0))] * n_tm
@@ -279,16 +274,16 @@
             pl.BlockSpec((1,) + shape[1:], lambda k: (k, 0, 0, 0, 0)),
             pl.BlockSpec((1, frames, depth), lambda k: (k, 0, 0)),
         ]
-        + [pl.BlockSpec(memory_space=pl.ANY)] * len(cuts),
+        + [pl.BlockSpec(memory_space=pl.ANY)],
         scratch_shapes=[
             pltpu.VMEM((3, window, depth), jnp.float32),
-            pltpu.SemaphoreType.DMA((len(cuts) * three * DMA_PIECES,)),
+            pltpu.SemaphoreType.DMA((three * DMA_PIECES,)),
         ],
         out_shape=[
             jax.ShapeDtypeStruct(shape, jnp.bfloat16),
             jax.ShapeDtypeStruct((n_tm, frames, depth), jnp.float32),
         ]
-        + [jax.ShapeDtypeStruct(w_qkv.shape[:2] + (size,), w_qkv.dtype) for _, size in cuts],
+        + [jax.ShapeDtypeStruct(w_qkv.shape, w_qkv.dtype)],
         cost_estimate=pl.CostEstimate(
             flops=4 * n_tm * n_seq * frames * n_mp * part * depth,
             bytes_accessed=4 * n_tm * n_seq * frames * n_mp * part * depth,
@@ -447,27 +442,27 @@
             weights[j].append(turn(share, "seq", -j))
 
     groups = head_groups(cols)
-    hidden, coef, *parts_qkv = modulate(start_step, w_qkv, groups, shares, near, far)
+    hidden, coef, held_qkv = modulate(start_step, w_qkv, shares, near, far)
     hidden = hidden.reshape(n_tm, n_seq * frames * tok, depth)
     proj = []
-    for part_qkv in parts_qkv:
+    for lane, size in groups:
         proj.append(
             jnp.einsum(
                 "krd,cdh->kcrh",
                 hidden,
-                part_qkv,
+                held_qkv[:, :, lane : lane + size],
                 preferred_element_type=jnp.float32,
             )
         )
     even = z % 2 == 0
-    evens = [(i, i ^ 1) for i in range(n_tm)]
-    odds = []
+    ev = [(i, i ^ 1) for i in range(n_tm)]
+    od = []
     for i in range(n_tm):
         for c in range(n_mp):
             other = i + 1 if i % 2 else i - 1
             inside = 0 <= other < n_tm
             to = other * n_mp + c if inside else i * n_mp + (c + 1) % n_mp
-            odds.append((i * n_mp + c, to))
+            od.append((i * n_mp + c, to))
 
     def incoming(pair):
         first, second = (0.0 if p is None else p.astype(jnp.float32) for p in pair)
@@ -483,9 +478,9 @@
                 right, left = right + more_right, left + more_left
             first = jnp.where(even, right, left).astype(jnp.float16)
             second = jnp.where(even, left, right).astype(jnp.float16)
-            first = lax.ppermute(first, "tm", evens)
+            first = lax.ppermute(first, "tm", ev)
             if t:
-                second = lax.ppermute(second, ("tm", "mp"), odds)
+                second = lax.ppermute(second, ("tm", "mp"), od)
                 first, second = lax.optimization_barrier((first, second))
             flows[h] = (first, second if t else None)
     gathered = []

time: 145 us -> 145 us (level)
  no operation moved by 1% of the time
where the time goes in v10:
time: 145 us
  waiting for transfers between devices  83.8 us (58%)
  starting transfers between devices  35.8 us (25%)
  Pallas kernels  9.4 us (6%)
  other arithmetic  7.66 us (5%)
  matrix products  3.74 us (3%)
  local copies, waits for them, and re-layouts  3.26 us (2%)
    ppermute x38, waiting for transfers between devices, turn(): lax.ppermute(block, axis, [(i, (i + distance) % size) for i in range(size)])  61.1 us
    ppermute x38, starting transfers between devices, turn(): lax.ppermute(block, axis, [(i, (i + distance) % size) for i in range(size)])  32.4 us
    ppermute x6, waiting for transfers between devices, sweep(): first = lax.ppermute(first, 'tm', ev)  22.7 us
    convert_element_type x4, other arithmetic, sweep(): second = jnp.where(even, left, right).astype(jnp.float16)  4.47 us
    dot_general x2, matrix products, sweep(): jnp.einsum('krd,cdh->kcrh', hidden, held_qkv[:, :, lane:lane + size], pre...  3.74 us
    unnamed x14, local copies, waits for them, and re-layouts  3.26 us
    ppermute x6, starting transfers between devices, sweep(): first = lax.ppermute(first, 'tm', ev)  3.23 us
    pallas_call x1, Pallas kernels, modulate(): pl.pallas_call(functools.partial(modulate_kernel, n_tm, n_seq, n_mp), gri...  3.1 us
  transfers between devices with their start and end apart: 48, of which 26 were waited for; matrix products, arithmetic and copies ran while one was open for 6% of the time, Pallas kernels for 2%

profile of v10, /device:TPU:0, one launch (start us, length us, event | category | flops | bytes accessed | tf_op | source)
XLA Modules:
  0.0 144.6 jit_solution(7848567607439525731)
XLA Ops:
  0.0 1.1 copy-done.2
  1.5 3.1 %collective-permute-start.6 = (bf16[1,32,1408]{2,1,0:T(8,128)(2,1)S(1)}, bf16[1,32,1408]{2,1,0:T(8,128)(2,1)S(1)}, u32[]{:S(2)}, u32[]{:S(2)}) collective-permute-start(bf16[1,32,1408]{2,1,0:T(8,128)(2,1)S(1)} %get-tuple-element.40), channel_id=1, source_target_pairs={{0,4},{4,8},{8,12},{12,0},{1,5},{5,9},{9,13},{13,1},{2,6},{6,10},{... | collective-permute-start | bytes 270344 | tf_op jit(solution)/shard_map/ppermute | solution.py:29
  4.6 2.6 %collective-permute-start.7 = (bf16[1,32,1408]{2,1,0:T(8,128)(2,1)S(1)}, bf16[1,32,1408]{2,1,0:T(8,128)(2,1)S(1)}, u32[]{:S(2)}, u32[]{:S(2)}) collective-permute-start(bf16[1,32,1408]{2,1,0:T(8,128)(2,1)S(1)} %get-tuple-element.41), channel_id=1, source_target_pairs={{0,8},{4,12},{8,0},{12,4},{1,9},{5,13},{9,1},{13,5},{2,10},{6,14},... | collective-permute-start | bytes 270344 | tf_op jit(solution)/shard_map/ppermute | solution.py:29
  7.2 1.4 collective-permute-start.8
  8.5 1.4 collective-permute-done.6
  9.9 3.3 %collective-permute-done.7 = bf16[1,32,1408]{2,1,0:T(8,128)(2,1)S(1)} collective-permute-done((bf16[1,32,1408]{2,1,0:T(8,128)(2,1)S(1)}, bf16[1,32,1408]{2,1,0:T(8,128)(2,1)S(1)}, u32[]{:S(2)}, u32[]{:S(2)}) %collective-permute-start.7) | collective-permute-done | bytes 90144 | tf_op jit(solution)/shard_map/ppermute | solution.py:29
  13.5 1.6 %collective-permute-start.10 = (bf16[3,1,32,1408]{3,2,1,0:T(8,128)(2,1)S(1)}, bf16[3,1,32,1408]{3,2,1,0:T(8,128)(2,1)S(1)}, u32[]{:S(2)}, u32[]{:S(2)}) collective-permute-start(bf16[3,1,32,1408]{3,2,1,0:T(8,128)(2,1)S(1)} %pad_maximum_fusion.refs_8_), channel_id=1, source_target_pairs={{0,2},{2,0},{1,3},{3,1},{4,6},{6,4},{5,7},{7,5},{8,10},{10,8},{9,1... | collective-permute-start | bytes 811016 | tf_op jit(solution)/shard_map/ppermute | solution.py:29
  15.0 6.6 %collective-permute-done.10.refs_10_ = bf16[3,1,32,1408]{3,2,1,0:T(8,128)(2,1)S(1)} collective-permute-done((bf16[3,1,32,1408]{3,2,1,0:T(8,128)(2,1)S(1)}, bf16[3,1,32,1408]{3,2,1,0:T(8,128)(2,1)S(1)}, u32[]{:S(2)}, u32[]{:S(2)}) %collective-permute-start.10) | collective-permute-done | bytes 270368 | tf_op jit(solution)/shard_map/ppermute | solution.py:29
  21.7 1.5 %collective-permute-start.4 = (bf16[1,32,1408]{2,1,0:T(8,128)(2,1)S(1)}, bf16[1,32,1408]{2,1,0:T(8,128)(2,1)S(1)}, u32[]{:S(2)}, u32[]{:S(2)}) collective-permute-start(bf16[1,32,1408]{2,1,0:T(8,128)(2,1)S(1)} %get-tuple-element.39.refs_4_), channel_id=1, source_target_pairs={{0,2},{2,0},{1,3},{3,1},{4,6},{6,4},{5,7},{7,5},{8,10},{10,8},{9,1... | collective-permute-start | bytes 270344 | tf_op jit(solution)/shard_map/ppermute | solution.py:29
  23.8 1.5 %copy-done = bf16[64,15360]{1,0:T(8,128)(2,1)S(1)} copy-done((bf16[64,15360]{1,0:T(8,128)(2,1)S(1)}, bf16[64,15360]{1,0:T(8,128)(2,1)}, u32[]{:S(2)}) %copy-start) | copy-done | bytes 1966104
  25.3 0.8 time_shares.1
  26.2 2.6 %collective-permute-start = (f32[3,4,1280]{2,1,0:T(4,128)S(1)}, f32[3,4,1280]{2,1,0:T(4,128)S(1)}, u32[]{:S(2)}, u32[]{:S(2)}) collective-permute-start(f32[3,4,1280]{2,1,0:T(4,128)S(1)} %get-tuple-element.36), channel_id=1, source_target_pairs={{0,4},{4,8},{8,12},{12,0},{1,5},{5,9},{9,13},{13,1},{2,6},{6,10},{... | collective-permute-start | bytes 184328 | tf_op jit(solution)/shard_map/ppermute | solution.py:29
  29.2 3.3 %collective-permute-done.refs_1_ = f32[3,4,1280]{2,1,0:T(4,128)S(1)} collective-permute-done((f32[3,4,1280]{2,1,0:T(4,128)S(1)}, f32[3,4,1280]{2,1,0:T(4,128)S(1)}, u32[]{:S(2)}, u32[]{:S(2)}) %collective-permute-start) | collective-permute-done | bytes 61472 | tf_op jit(solution)/shard_map/ppermute | solution.py:29
  33.1 1.8 %collective-permute-done.1.refs_2_ = f32[3,4,1280]{2,1,0:T(4,128)S(1)} collective-permute-done((f32[3,4,1280]{2,1,0:T(4,128)S(1)}, f32[3,4,1280]{2,1,0:T(4,128)S(1)}, u32[]{:S(2)}, u32[]{:S(2)}) %collective-permute-start.1) | collective-permute-done | bytes 61472 | tf_op jit(solution)/shard_map/ppermute | solution.py:29
  34.9 1.3 collective-permute-start.2
  36.2 2.9 %collective-permute-done.2.refs_3_ = f32[3,4,1280]{2,1,0:T(4,128)S(1)} collective-permute-done((f32[3,4,1280]{2,1,0:T(4,128)S(1)}, f32[3,4,1280]{2,1,0:T(4,128)S(1)}, u32[]{:S(2)}, u32[]{:S(2)}) %collective-permute-start.2) | collective-permute-done | bytes 61472 | tf_op jit(solution)/shard_map/ppermute | solution.py:29
  39.1 3.1 %modulate.1 = (bf16[4,2,1,64,1280]{4,3,2,1,0:T(8,128)(2,1)S(1)}, f32[4,1,1280]{2,1,0:T(1,128)S(1)}, bf16[3,1280,768]{2,1,0:T(8,128)(2,1)S(1)}) custom-call(s32[1]{0:T(128)S(6)} %copy.17.step_ref, bf16[3,1280,768]{2,1,0:T(8,128)(2,1)} %w_ref.2, f32[3,4,1280]{2,1,0:T(4,128)S(1)} %get-tuple-element.35.refs_0_, f32[3,4,1280]{2,1,0:T(4,128)S(1)} %collective-permute-done.refs_1_, ...), custom_call_target="tpu_custom_call" | custom-call | flops 2621440 | bytes 2621440 | tf_op jit(solution)/shard_map/modulate/pallas_call | solution.py:265
  42.2 1.9 %fusion.6 = f32[4,3,128,384]{3,2,1,0:T(8,128)S(1)} fusion(bf16[4,128,1280,1]{2,1,3,0:T(8,128)(2,1)S(1)} %bitcast.118, bf16[3,1280,768]{2,1,0:T(8,128)(2,1)S(1)} %get-tuple-element.44), kind=kOutput, calls=%fused_computation.6 | convolution fusion | flops 1509949440 | bytes 6619136 | tf_op jit(solution)/shard_map/krd,cdh->kcrh/dot_general | solution.py:450
  44.1 0.9 select_convert_fusion.4
  45.6 1.9 %fusion.9 = f32[4,3,128,384]{3,2,0,1:T(8,128)S(1)} fusion(bf16[4,128,1280,1]{2,1,0,3:T(8,128)(2,1)S(1)} %bitcast.119, bf16[3,1280,768]{2,1,0:T(8,128)(2,1)S(1)} %get-tuple-element.44), kind=kOutput, calls=%fused_computation.7 | convolution fusion | flops 1509949440 | bytes 6619136 | tf_op jit(solution)/shard_map/krd,cdh->kcrh/dot_general | solution.py:450
  47.5 0.9 select_convert_fusion.9
  48.4 1.4 collective-permute-start.12
  50.5 4.6 %collective-permute-done.25 = f16[3,128,384]{2,1,0:T(8,128)(2,1)} collective-permute-done((f16[3,128,384]{2,1,0:T(8,128)(2,1)}, f16[3,128,384]{2,1,0:T(8,128)(2,1)}, u32[]{:S(2)}, u32[]{:S(2)}) %collective-permute-start.25) | collective-permute-done | bytes 294944 | tf_op jit(solution)/shard_map/ppermute | solution.py:481
  55.2 1.4 select_convert_fusion.2
  56.7 4.7 %collective-permute-done.12 = f16[3,128,384]{2,1,0:T(8,128)(2,1)S(1)} collective-permute-done((f16[3,128,384]{2,1,0:T(8,128)(2,1)}, f16[3,128,384]{2,1,0:T(8,128)(2,1)S(1)}, u32[]{:S(2)}, u32[]{:S(2)}) %collective-permute-start.12) | collective-permute-done | bytes 294944 | tf_op jit(solution)/shard_map/ppermute | solution.py:481
  61.4 1.3 select_convert_fusion.7
  62.9 4.8 %collective-permute-done.26 = f16[3,128,384]{2,1,0:T(8,128)(2,1)S(1)} collective-permute-done((f16[3,128,384]{2,1,0:T(8,128)(2,1)S(1)}, f16[3,128,384]{2,1,0:T(8,128)(2,1)S(1)}, u32[]{:S(2)}, u32[]{:S(2)}) %collective-permute-start.26) | collective-permute-done | bytes 294944 | tf_op jit(solution)/shard_map/ppermute | solution.py:481
  68.3 1.5 %select_convert_fusion = (f16[3,128,384]{2,1,0:T(8,128)(2,1)S(1)}, f16[3,128,384]{2,1,0:T(8,128)(2,1)S(1)}) fusion(pred[]{:T(512)S(6)} %eq.5, f16[3,128,384]{2,1,0:T(8,128)(2,1)S(1)} %collective-permute-done.27, f16[3,128,384]{2,1,0:T(8,128)(2,1)S(1)} %collective-permute-done.26, pred[]{:T(512)S(6)} %lt.9, f32[4,3,128,384]{3,2,1,0:T(8,128)} %copy-done.5, ...), kind=kLoop, calls=%fused_computation.52 | loop fusion | flops 1769472 | bytes 2359299 | tf_op jit(solution)/shard_map/convert_element_type | solution.py:480
  69.8 4.2 %collective-permute-done.13 = f16[3,128,384]{2,1,0:T(8,128)(2,1)S(1)} collective-permute-done((f16[3,128,384]{2,1,0:T(8,128)(2,1)S(1)}, f16[3,128,384]{2,1,0:T(8,128)(2,1)S(1)}, u32[]{:S(2)}, u32[]{:S(2)}) %collective-permute-start.13) | collective-permute-done | bytes 294944 | tf_op jit(solution)/shard_map/ppermute | solution.py:481
  74.3 1.6 %collective-permute-start.15 = (f16[3,128,384]{2,1,0:T(8,128)(2,1)S(1)}, f16[3,128,384]{2,1,0:T(8,128)(2,1)S(1)}, u32[]{:S(2)}, u32[]{:S(2)}) collective-permute-start(f16[3,128,384]{2,1,0:T(8,128)(2,1)S(1)} %get-tuple-element.68), channel_id=1, source_target_pairs={{0,4},{4,0},{8,12},{12,8},{1,5},{5,1},{9,13},{13,9},{2,6},{6,2},{1... | collective-permute-start | bytes 884744 | tf_op jit(solution)/shard_map/ppermute | solution.py:481
  75.9 3.1 %collective-permute-done.28 = f16[3,128,384]{2,1,0:T(8,128)(2,1)S(1)} collective-permute-done((f16[3,128,384]{2,1,0:T(8,128)(2,1)S(1)}, f16[3,128,384]{2,1,0:T(8,128)(2,1)S(1)}, u32[]{:S(2)}, u32[]{:S(2)}) %collective-permute-start.28) | collective-permute-done | bytes 294944 | tf_op jit(solution)/shard_map/ppermute | solution.py:481
  79.6 1.2 fusion.34
  80.8 0.9 attend.3
  81.8 1.5 %collective-permute-start.30 = (bf16[1,64,384]{2,1,0:T(8,128)(2,1)S(1)}, bf16[1,64,384]{2,1,0:T(8,128)(2,1)S(1)}, u32[]{:S(2)}, u32[]{:S(2)}) collective-permute-start(bf16[1,64,384]{2,1,0:T(8,128)(2,1)S(1)} %get-tuple-element.57), channel_id=1, source_target_pairs={{0,2},{2,0},{1,3},{3,1},{4,6},{6,4},{5,7},{7,5},{8,10},{10,8},{9,1... | collective-permute-start | bytes 147464 | tf_op jit(solution)/shard_map/ppermute | solution.py:29
  83.3 1.3 collective-permute-done.15
  84.7 0.9 attend.2
  86.3 23.6 %collective-permute-done.30 = bf16[1,64,384]{2,1,0:T(8,128)(2,1)S(1)} collective-permute-done((bf16[1,64,384]{2,1,0:T(8,128)(2,1)S(1)}, bf16[1,64,384]{2,1,0:T(8,128)(2,1)S(1)}, u32[]{:S(2)}, u32[]{:S(2)}) %collective-permute-start.30) | collective-permute-done | bytes 49184 | tf_op jit(solution)/shard_map/ppermute | solution.py:29
  110.6 2.6 %collective-permute-start.34 = (bf16[2,1,64,384]{3,2,1,0:T(8,128)(2,1)S(1)}, bf16[2,1,64,384]{3,2,1,0:T(8,128)(2,1)S(1)}, u32[]{:S(2)}, u32[]{:S(2)}) collective-permute-start(bf16[2,1,64,384]{3,2,1,0:T(8,128)(2,1)S(1)} %pad_maximum_fusion.2.refs_8_), channel_id=1, source_target_pairs={{0,8},{4,12},{8,0},{12,4},{1,9},{5,13},{9,1},{13,5},{2,10},{6,14},... | collective-permute-start | bytes 294920 | tf_op jit(solution)/shard_map/ppermute | solution.py:29
  114.0 2.6 %collective-permute-done.32.refs_10_ = bf16[2,1,64,384]{3,2,1,0:T(8,128)(2,1)S(1)} collective-permute-done((bf16[2,1,64,384]{3,2,1,0:T(8,128)(2,1)S(1)}, bf16[2,1,64,384]{3,2,1,0:T(8,128)(2,1)S(1)}, u32[]{:S(2)}, u32[]{:S(2)}) %collective-permute-start.32) | collective-permute-done | bytes 98336 | tf_op jit(solution)/shard_map/ppermute | solution.py:29
  116.5 1.8 %collective-permute-done.34.refs_12_ = bf16[2,1,64,384]{3,2,1,0:T(8,128)(2,1)S(1)} collective-permute-done((bf16[2,1,64,384]{3,2,1,0:T(8,128)(2,1)S(1)}, bf16[2,1,64,384]{3,2,1,0:T(8,128)(2,1)S(1)}, u32[]{:S(2)}, u32[]{:S(2)}) %collective-permute-start.34) | collective-permute-done | bytes 98336 | tf_op jit(solution)/shard_map/ppermute | solution.py:29
  118.8 3.7 %collective-permute-start.23 = (bf16[2,1,64,384]{3,2,1,0:T(8,128)(2,1)S(1)}, bf16[2,1,64,384]{3,2,1,0:T(8,128)(2,1)S(1)}, u32[]{:S(2)}, u32[]{:S(2)}) collective-permute-start(bf16[2,1,64,384]{3,2,1,0:T(8,128)(2,1)S(1)} %pad_maximum_fusion.1.refs_0_), channel_id=1, source_target_pairs={{0,12},{4,0},{8,4},{12,8},{1,13},{5,1},{9,5},{13,9},{2,14},{6,2},{... | collective-permute-start | bytes 294920 | tf_op jit(solution)/shard_map/ppermute | solution.py:29
  123.2 3.2 %collective-permute-done.21.refs_4_ = bf16[2,1,64,384]{3,2,1,0:T(8,128)(2,1)S(1)} collective-permute-done((bf16[2,1,64,384]{3,2,1,0:T(8,128)(2,1)S(1)}, bf16[2,1,64,384]{3,2,1,0:T(8,128)(2,1)S(1)}, u32[]{:S(2)}, u32[]{:S(2)}) %collective-permute-start.21) | collective-permute-done | bytes 98336 | tf_op jit(solution)/shard_map/ppermute | solution.py:29
  129.0 1.5 %project.1 = (f32[1,64,640]{2,1,0:T(8,128)S(1)}, bf16[1,64,640]{2,1,0:T(8,128)(2,1)S(1)}, bf16[1,64,640]{2,1,0:T(8,128)(2,1)S(1)}, bf16[1,64,640]{2,1,0:T(8,128)(2,1)S(1)}, bf16[1,64,640]{2,1,0:T(8,128)(2,1)S(1)}) custom-call(f32[4,1,1280]{2,1,0:T(1,128)S(1)} %get-tuple-element.43.coef_ref, bf16[2,1,64,384]{3,2,1,0:T(8,128)(2,1)S(1)} %pad_maximum_fusion.1.refs_0_, ...), custom_call_target="tpu_custom_call" | custom-call | flops 1006632960 | bytes 5505024 | tf_op jit(solution)/shard_map/project/pallas_call | solution.py:361
  130.5 3.6 %collective-permute-start.42 = (bf16[1,64,640]{2,1,0:T(8,128)(2,1)S(1)}, bf16[1,64,640]{2,1,0:T(8,128)(2,1)S(1)}, u32[]{:S(2)}, u32[]{:S(2)}) collective-permute-start(bf16[1,64,640]{2,1,0:T(8,128)(2,1)S(1)} %get-tuple-element.62), channel_id=1, source_target_pairs={{0,12},{4,0},{8,4},{12,8},{1,13},{5,1},{9,5},{13,9},{2,14},{6,2},{... | collective-permute-start | bytes 245768 | tf_op jit(solution)/shard_map/ppermute | solution.py:29
  134.7 2.2 %collective-permute-done.42.refs_2_ = bf16[1,64,640]{2,1,0:T(8,128)(2,1)S(1)} collective-permute-done((bf16[1,64,640]{2,1,0:T(8,128)(2,1)S(1)}, bf16[1,64,640]{2,1,0:T(8,128)(2,1)S(1)}, u32[]{:S(2)}, u32[]{:S(2)}) %collective-permute-start.42) | collective-permute-done | bytes 81952 | tf_op jit(solution)/shard_map/ppermute | solution.py:29
  137.0 5.1 %collective-permute-done.44.refs_4_ = bf16[1,64,640]{2,1,0:T(8,128)(2,1)S(1)} collective-permute-done((bf16[1,64,640]{2,1,0:T(8,128)(2,1)S(1)}, bf16[1,64,640]{2,1,0:T(8,128)(2,1)S(1)}, u32[]{:S(2)}, u32[]{:S(2)}) %collective-permute-start.44) | collective-permute-done | bytes 81952 | tf_op jit(solution)/shard_map/ppermute | solution.py:29
  142.6 0.8 collective-permute-done.45.refs_5_
  143.5 1.0 finish.1
  (84 shorter events, 12.0 us)
Async XLA Ops:
  1.5 8.4 %collective-permute-start.6 = (bf16[1,32,1408]{2,1,0:T(8,128)(2,1)S(1)}, bf16[1,32,1408]{2,1,0:T(8,128)(2,1)S(1)}, u32[]{:S(2)}, u32[]{:S(2)}) collective-permute-start(bf16[1,32,1408]{2,1,0:T(8,128)(2,1)S(1)} %get-tuple-element.40), channel_id=1, source_target_pairs={{0,4},{4,8},{8,12},{12,0},{1,5},{5,9},{9,13},{13,1},{2,6},{6,10},{... | collective-permute-start | bytes 270344 | tf_op jit(solution)/shard_map/ppermute | solution.py:29
  4.6 8.6 %collective-permute-start.7 = (bf16[1,32,1408]{2,1,0:T(8,128)(2,1)S(1)}, bf16[1,32,1408]{2,1,0:T(8,128)(2,1)S(1)}, u32[]{:S(2)}, u32[]{:S(2)}) collective-permute-start(bf16[1,32,1408]{2,1,0:T(8,128)(2,1)S(1)} %get-tuple-element.41), channel_id=1, source_target_pairs={{0,8},{4,12},{8,0},{12,4},{1,9},{5,13},{9,1},{13,5},{2,10},{6,14},... | collective-permute-start | bytes 270344 | tf_op jit(solution)/shard_map/ppermute | solution.py:29
  7.2 6.3 %collective-permute-start.8 = (bf16[1,32,1408]{2,1,0:T(8,128)(2,1)S(1)}, bf16[1,32,1408]{2,1,0:T(8,128)(2,1)S(1)}, u32[]{:S(2)}, u32[]{:S(2)}) collective-permute-start(bf16[1,32,1408]{2,1,0:T(8,128)(2,1)S(1)} %get-tuple-element.42), channel_id=1, source_target_pairs={{0,12},{4,0},{8,4},{12,8},{1,13},{5,1},{9,5},{13,9},{2,14},{6,2},{... | collective-permute-start | bytes 270344 | tf_op jit(solution)/shard_map/ppermute | solution.py:29
  13.5 8.2 %collective-permute-start.10 = (bf16[3,1,32,1408]{3,2,1,0:T(8,128)(2,1)S(1)}, bf16[3,1,32,1408]{3,2,1,0:T(8,128)(2,1)S(1)}, u32[]{:S(2)}, u32[]{:S(2)}) collective-permute-start(bf16[3,1,32,1408]{3,2,1,0:T(8,128)(2,1)S(1)} %pad_maximum_fusion.refs_8_), channel_id=1, source_target_pairs={{0,2},{2,0},{1,3},{3,1},{4,6},{6,4},{5,7},{7,5},{8,10},{10,8},{9,1... | collective-permute-start | bytes 811016 | tf_op jit(solution)/shard_map/ppermute | solution.py:29
  15.0 24.1 %collective-permute-start.9 = (bf16[3,1,32,1408]{3,2,1,0:T(8,128)(2,1)S(1)}, bf16[3,1,32,1408]{3,2,1,0:T(8,128)(2,1)S(1)}, u32[]{:S(2)}, u32[]{:S(2)}) collective-permute-start(bf16[3,1,32,1408]{3,2,1,0:T(8,128)(2,1)S(1)} %pad_maximum_fusion.refs_8_), channel_id=1, source_target_pairs={{0,1},{1,0},{2,3},{3,2},{4,5},{5,4},{6,7},{7,6},{8,9},{9,8},{10,11... | collective-permute-start | bytes 811016 | tf_op jit(solution)/shard_map/ppermute | solution.py:29
  21.6 17.5 %collective-permute-start.11 = (bf16[3,1,32,1408]{3,2,1,0:T(8,128)(2,1)S(1)}, bf16[3,1,32,1408]{3,2,1,0:T(8,128)(2,1)S(1)}, u32[]{:S(2)}, u32[]{:S(2)}) collective-permute-start(bf16[3,1,32,1408]{3,2,1,0:T(8,128)(2,1)S(1)} %collective-permute-done.10.refs_10_), channel_id=1, source_target_pairs={{0,1},{1,0},{2,3},{3,2},{4,5},{5,4},{6,7},{7,6},{8,9},{9,8},{10,11... | collective-permute-start | bytes 811016 | tf_op jit(solution)/shard_map/ppermute | solution.py:29
  21.7 10.9 %collective-permute-start.4 = (bf16[1,32,1408]{2,1,0:T(8,128)(2,1)S(1)}, bf16[1,32,1408]{2,1,0:T(8,128)(2,1)S(1)}, u32[]{:S(2)}, u32[]{:S(2)}) collective-permute-start(bf16[1,32,1408]{2,1,0:T(8,128)(2,1)S(1)} %get-tuple-element.39.refs_4_), channel_id=1, source_target_pairs={{0,2},{2,0},{1,3},{3,1},{4,6},{6,4},{5,7},{7,5},{8,10},{10,8},{9,1... | collective-permute-start | bytes 270344 | tf_op jit(solution)/shard_map/ppermute | solution.py:29
  26.2 6.4 %collective-permute-start = (f32[3,4,1280]{2,1,0:T(4,128)S(1)}, f32[3,4,1280]{2,1,0:T(4,128)S(1)}, u32[]{:S(2)}, u32[]{:S(2)}) collective-permute-start(f32[3,4,1280]{2,1,0:T(4,128)S(1)} %get-tuple-element.36), channel_id=1, source_target_pairs={{0,4},{4,8},{8,12},{12,0},{1,5},{5,9},{9,13},{13,1},{2,6},{6,10},{... | collective-permute-start | bytes 184328 | tf_op jit(solution)/shard_map/ppermute | solution.py:29
  28.7 6.1 %collective-permute-start.1 = (f32[3,4,1280]{2,1,0:T(4,128)S(1)}, f32[3,4,1280]{2,1,0:T(4,128)S(1)}, u32[]{:S(2)}, u32[]{:S(2)}) collective-permute-start(f32[3,4,1280]{2,1,0:T(4,128)S(1)} %get-tuple-element.37), channel_id=1, source_target_pairs={{0,8},{4,12},{8,0},{12,4},{1,9},{5,13},{9,1},{13,5},{2,10},{6,14},... | collective-permute-start | bytes 184328 | tf_op jit(solution)/shard_map/ppermute | solution.py:29
  32.5 6.6 %collective-permute-start.3 = (bf16[1,32,1408]{2,1,0:T(8,128)(2,1)S(1)}, bf16[1,32,1408]{2,1,0:T(8,128)(2,1)S(1)}, u32[]{:S(2)}, u32[]{:S(2)}) collective-permute-start(bf16[1,32,1408]{2,1,0:T(8,128)(2,1)S(1)} %get-tuple-element.39.refs_4_), channel_id=1, source_target_pairs={{0,1},{1,0},{2,3},{3,2},{4,5},{5,4},{6,7},{7,6},{8,9},{9,8},{10,11... | collective-permute-start | bytes 270344 | tf_op jit(solution)/shard_map/ppermute | solution.py:29
  32.6 6.5 %collective-permute-start.5 = (bf16[1,32,1408]{2,1,0:T(8,128)(2,1)S(1)}, bf16[1,32,1408]{2,1,0:T(8,128)(2,1)S(1)}, u32[]{:S(2)}, u32[]{:S(2)}) collective-permute-start(bf16[1,32,1408]{2,1,0:T(8,128)(2,1)S(1)} %collective-permute-done.4.refs_6_), channel_id=1, source_target_pairs={{0,1},{1,0},{2,3},{3,2},{4,5},{5,4},{6,7},{7,6},{8,9},{9,8},{10,11... | collective-permute-start | bytes 270344 | tf_op jit(solution)/shard_map/ppermute | solution.py:29
  34.9 4.2 %collective-permute-start.2 = (f32[3,4,1280]{2,1,0:T(4,128)S(1)}, f32[3,4,1280]{2,1,0:T(4,128)S(1)}, u32[]{:S(2)}, u32[]{:S(2)}) collective-permute-start(f32[3,4,1280]{2,1,0:T(4,128)S(1)} %get-tuple-element.38), channel_id=1, source_target_pairs={{0,12},{4,0},{8,4},{12,8},{1,13},{5,1},{9,5},{13,9},{2,14},{6,2},{... | collective-permute-start | bytes 184328 | tf_op jit(solution)/shard_map/ppermute | solution.py:29
  45.0 10.2 %collective-permute-start.25 = (f16[3,128,384]{2,1,0:T(8,128)(2,1)}, f16[3,128,384]{2,1,0:T(8,128)(2,1)}, u32[]{:S(2)}, u32[]{:S(2)}) collective-permute-start(f16[3,128,384]{2,1,0:T(8,128)(2,1)} %select_convert_fusion.4), channel_id=1, source_target_pairs={{0,4},{4,0},{8,12},{12,8},{1,5},{5,1},{9,13},{13,9},{2,6},{6,2},{1... | collective-permute-start | bytes 884744 | tf_op jit(solution)/shard_map/ppermute | solution.py:481
  48.4 13.0 %collective-permute-start.12 = (f16[3,128,384]{2,1,0:T(8,128)(2,1)}, f16[3,128,384]{2,1,0:T(8,128)(2,1)S(1)}, u32[]{:S(2)}, u32[]{:S(2)}) collective-permute-start(f16[3,128,384]{2,1,0:T(8,128)(2,1)} %select_convert_fusion.9), channel_id=1, source_target_pairs={{0,4},{4,0},{8,12},{12,8},{1,5},{5,1},{9,13},{13,9},{2,6},{6,2},{1... | collective-permute-start | bytes 884744 | tf_op jit(solution)/shard_map/ppermute | solution.py:481
  50.4 25.5 %collective-permute-start.38 = (bf16[640,768]{1,0:T(8,128)(2,1)S(1)}, bf16[640,768]{1,0:T(8,128)(2,1)S(1)}, u32[]{:S(2)}, u32[]{:S(2)}) collective-permute-start(bf16[640,768]{1,0:T(8,128)(2,1)S(1)} %get-tuple-element.59), channel_id=1, source_target_pairs={{0,1},{1,0},{2,3},{3,2},{4,5},{5,4},{6,7},{7,6},{8,9},{9,8},{10,11... | collective-permute-start | bytes 2949128 | tf_op jit(solution)/shard_map/ppermute | solution.py:29
  56.6 11.1 %collective-permute-start.26 = (f16[3,128,384]{2,1,0:T(8,128)(2,1)S(1)}, f16[3,128,384]{2,1,0:T(8,128)(2,1)S(1)}, u32[]{:S(2)}, u32[]{:S(2)}) collective-permute-start(f16[3,128,384]{2,1,0:T(8,128)(2,1)S(1)} %get-tuple-element.70), channel_id=1, source_target_pairs={{0,4},{4,0},{8,12},{12,8},{1,5},{5,1},{9,13},{13,9},{2,6},{6,2},{1... | collective-permute-start | bytes 884744 | tf_op jit(solution)/shard_map/ppermute | solution.py:481
  56.7 11.6 %collective-permute-start.27 = (f16[3,128,384]{2,1,0:T(8,128)(2,1)S(1)}, f16[3,128,384]{2,1,0:T(8,128)(2,1)S(1)}, u32[]{:S(2)}, u32[]{:S(2)}) collective-permute-start(f16[3,128,384]{2,1,0:T(8,128)(2,1)S(1)} %get-tuple-element.69), channel_id=1, source_target_pairs={{0,1},{1,0},{4,8},{5,9},{8,4},{9,5},{12,13},{13,12},{2,3},{3,2},{6... | collective-permute-start | bytes 884744 | tf_op jit(solution)/shard_map/ppermute | solution.py:483
  62.7 11.3 %collective-permute-start.13 = (f16[3,128,384]{2,1,0:T(8,128)(2,1)S(1)}, f16[3,128,384]{2,1,0:T(8,128)(2,1)S(1)}, u32[]{:S(2)}, u32[]{:S(2)}) collective-permute-start(f16[3,128,384]{2,1,0:T(8,128)(2,1)S(1)} %get-tuple-element.72), channel_id=1, source_target_pairs={{0,4},{4,0},{8,12},{12,8},{1,5},{5,1},{9,13},{13,9},{2,6},{6,2},{1... | collective-permute-start | bytes 884744 | tf_op jit(solution)/shard_map/ppermute | solution.py:481
  62.8 11.3 %collective-permute-start.14 = (f16[3,128,384]{2,1,0:T(8,128)(2,1)S(1)}, f16[3,128,384]{2,1,0:T(8,128)(2,1)S(1)}, u32[]{:S(2)}, u32[]{:S(2)}) collective-permute-start(f16[3,128,384]{2,1,0:T(8,128)(2,1)S(1)} %get-tuple-element.71), channel_id=1, source_target_pairs={{0,1},{1,0},{4,8},{5,9},{8,4},{9,5},{12,13},{13,12},{2,3},{3,2},{6... | collective-permute-start | bytes 884744 | tf_op jit(solution)/shard_map/ppermute | solution.py:483
  67.7 46.2 %collective-permute-start.39 = (bf16[640,768]{1,0:T(8,128)(2,1)S(1)}, bf16[640,768]{1,0:T(8,128)(2,1)S(1)}, u32[]{:S(2)}, u32[]{:S(2)}) collective-permute-start(bf16[640,768]{1,0:T(8,128)(2,1)S(1)} %get-tuple-element.58.refs_16_), channel_id=1, source_target_pairs={{0,2},{2,0},{1,3},{3,1},{4,6},{6,4},{5,7},{7,5},{8,10},{10,8},{9,1... | collective-permute-start | bytes 2949128 | tf_op jit(solution)/shard_map/ppermute | solution.py:29
  69.8 9.3 %collective-permute-start.28 = (f16[3,128,384]{2,1,0:T(8,128)(2,1)S(1)}, f16[3,128,384]{2,1,0:T(8,128)(2,1)S(1)}, u32[]{:S(2)}, u32[]{:S(2)}) collective-permute-start(f16[3,128,384]{2,1,0:T(8,128)(2,1)S(1)} %get-tuple-element.66), channel_id=1, source_target_pairs={{0,4},{4,0},{8,12},{12,8},{1,5},{5,1},{9,13},{13,9},{2,6},{6,2},{1... | collective-permute-start | bytes 884744 | tf_op jit(solution)/shard_map/ppermute | solution.py:481
  74.0 5.5 %collective-permute-start.29 = (f16[3,128,384]{2,1,0:T(8,128)(2,1)S(1)}, f16[3,128,384]{2,1,0:T(8,128)(2,1)S(1)}, u32[]{:S(2)}, u32[]{:S(2)}) collective-permute-start(f16[3,128,384]{2,1,0:T(8,128)(2,1)S(1)} %get-tuple-element.65), channel_id=1, source_target_pairs={{0,1},{1,0},{4,8},{5,9},{8,4},{9,5},{12,13},{13,12},{2,3},{3,2},{6... | collective-permute-start | bytes 884744 | tf_op jit(solution)/shard_map/ppermute | solution.py:483
  74.3 10.3 %collective-permute-start.15 = (f16[3,128,384]{2,1,0:T(8,128)(2,1)S(1)}, f16[3,128,384]{2,1,0:T(8,128)(2,1)S(1)}, u32[]{:S(2)}, u32[]{:S(2)}) collective-permute-start(f16[3,128,384]{2,1,0:T(8,128)(2,1)S(1)} %get-tuple-element.68), channel_id=1, source_target_pairs={{0,4},{4,0},{8,12},{12,8},{1,5},{5,1},{9,13},{13,9},{2,6},{6,2},{1... | collective-permute-start | bytes 884744 | tf_op jit(solution)/shard_map/ppermute | solution.py:481
  75.9 8.7 %collective-permute-start.16 = (f16[3,128,384]{2,1,0:T(8,128)(2,1)S(1)}, f16[3,128,384]{2,1,0:T(8,128)(2,1)S(1)}, u32[]{:S(2)}, u32[]{:S(2)}) collective-permute-start(f16[3,128,384]{2,1,0:T(8,128)(2,1)S(1)} %get-tuple-element.67), channel_id=1, source_target_pairs={{0,1},{1,0},{4,8},{5,9},{8,4},{9,5},{12,13},{13,12},{2,3},{3,2},{6... | collective-permute-start | bytes 884744 | tf_op jit(solution)/shard_map/ppermute | solution.py:483
  79.0 49.9 %collective-permute-start.40 = (bf16[640,768]{1,0:T(8,128)(2,1)S(1)}, bf16[640,768]{1,0:T(8,128)(2,1)S(1)}, u32[]{:S(2)}, u32[]{:S(2)}) collective-permute-start(bf16[640,768]{1,0:T(8,128)(2,1)S(1)} %collective-permute-done.38.refs_17_), channel_id=1, source_target_pairs={{0,2},{2,0},{1,3},{3,1},{4,6},{6,4},{5,7},{7,5},{8,10},{10,8},{9,1... | collective-permute-start | bytes 2949128 | tf_op jit(solution)/shard_map/ppermute | solution.py:29
  81.8 28.2 %collective-permute-start.30 = (bf16[1,64,384]{2,1,0:T(8,128)(2,1)S(1)}, bf16[1,64,384]{2,1,0:T(8,128)(2,1)S(1)}, u32[]{:S(2)}, u32[]{:S(2)}) collective-permute-start(bf16[1,64,384]{2,1,0:T(8,128)(2,1)S(1)} %get-tuple-element.57), channel_id=1, source_target_pairs={{0,2},{2,0},{1,3},{3,1},{4,6},{6,4},{5,7},{7,5},{8,10},{10,8},{9,1... | collective-permute-start | bytes 147464 | tf_op jit(solution)/shard_map/ppermute | solution.py:29
  85.7 27.5 %collective-permute-start.17 = (bf16[1,64,384]{2,1,0:T(8,128)(2,1)S(1)}, bf16[1,64,384]{2,1,0:T(8,128)(2,1)S(1)}, u32[]{:S(2)}, u32[]{:S(2)}) collective-permute-start(bf16[1,64,384]{2,1,0:T(8,128)(2,1)S(1)} %get-tuple-element.51), channel_id=1, source_target_pairs={{0,2},{2,0},{1,3},{3,1},{4,6},{6,4},{5,7},{7,5},{8,10},{10,8},{9,1... | collective-permute-start | bytes 147464 | tf_op jit(solution)/shard_map/ppermute | solution.py:29
  109.9 6.6 %collective-permute-start.32 = (bf16[2,1,64,384]{3,2,1,0:T(8,128)(2,1)S(1)}, bf16[2,1,64,384]{3,2,1,0:T(8,128)(2,1)S(1)}, u32[]{:S(2)}, u32[]{:S(2)}) collective-permute-start(bf16[2,1,64,384]{3,2,1,0:T(8,128)(2,1)S(1)} %pad_maximum_fusion.2.refs_8_), channel_id=1, source_target_pairs={{0,4},{4,8},{8,12},{12,0},{1,5},{5,9},{9,13},{13,1},{2,6},{6,10},{... | collective-permute-start | bytes 294920 | tf_op jit(solution)/shard_map/ppermute | solution.py:29
  110.6 7.7 %collective-permute-start.34 = (bf16[2,1,64,384]{3,2,1,0:T(8,128)(2,1)S(1)}, bf16[2,1,64,384]{3,2,1,0:T(8,128)(2,1)S(1)}, u32[]{:S(2)}, u32[]{:S(2)}) collective-permute-start(bf16[2,1,64,384]{3,2,1,0:T(8,128)(2,1)S(1)} %pad_maximum_fusion.2.refs_8_), channel_id=1, source_target_pairs={{0,8},{4,12},{8,0},{12,4},{1,9},{5,13},{9,1},{13,5},{2,10},{6,14},... | collective-permute-start | bytes 294920 | tf_op jit(solution)/shard_map/ppermute | solution.py:29
  113.2 5.6 %collective-permute-start.36 = (bf16[2,1,64,384]{3,2,1,0:T(8,128)(2,1)S(1)}, bf16[2,1,64,384]{3,2,1,0:T(8,128)(2,1)S(1)}, u32[]{:S(2)}, u32[]{:S(2)}) collective-permute-start(bf16[2,1,64,384]{3,2,1,0:T(8,128)(2,1)S(1)} %pad_maximum_fusion.2.refs_8_), channel_id=1, source_target_pairs={{0,12},{4,0},{8,4},{12,8},{1,13},{5,1},{9,5},{13,9},{2,14},{6,2},{... | collective-permute-start | bytes 294920 | tf_op jit(solution)/shard_map/ppermute | solution.py:29
  113.9 8.7 %collective-permute-start.31 = (bf16[2,1,64,384]{3,2,1,0:T(8,128)(2,1)S(1)}, bf16[2,1,64,384]{3,2,1,0:T(8,128)(2,1)S(1)}, u32[]{:S(2)}, u32[]{:S(2)}) collective-permute-start(bf16[2,1,64,384]{3,2,1,0:T(8,128)(2,1)S(1)} %pad_maximum_fusion.2.refs_8_), channel_id=1, source_target_pairs={{0,1},{1,0},{2,3},{3,2},{4,5},{5,4},{6,7},{7,6},{8,9},{9,8},{10,11... | collective-permute-start | bytes 294920 | tf_op jit(solution)/shard_map/ppermute | solution.py:29
  116.5 6.7 %collective-permute-start.19 = (bf16[2,1,64,384]{3,2,1,0:T(8,128)(2,1)S(1)}, bf16[2,1,64,384]{3,2,1,0:T(8,128)(2,1)S(1)}, u32[]{:S(2)}, u32[]{:S(2)}) collective-permute-start(bf16[2,1,64,384]{3,2,1,0:T(8,128)(2,1)S(1)} %pad_maximum_fusion.1.refs_0_), channel_id=1, source_target_pairs={{0,4},{4,8},{8,12},{12,0},{1,5},{5,9},{9,13},{13,1},{2,6},{6,10},{... | collective-permute-start | bytes 294920 | tf_op jit(solution)/shard_map/ppermute | solution.py:29
  118.3 8.1 %collective-permute-start.21 = (bf16[2,1,64,384]{3,2,1,0:T(8,128)(2,1)S(1)}, bf16[2,1,64,384]{3,2,1,0:T(8,128)(2,1)S(1)}, u32[]{:S(2)}, u32[]{:S(2)}) collective-permute-start(bf16[2,1,64,384]{3,2,1,0:T(8,128)(2,1)S(1)} %pad_maximum_fusion.1.refs_0_), channel_id=1, source_target_pairs={{0,8},{4,12},{8,0},{12,4},{1,9},{5,13},{9,1},{13,5},{2,10},{6,14},... | collective-permute-start | bytes 294920 | tf_op jit(solution)/shard_map/ppermute | solution.py:29
  118.8 7.5 %collective-permute-start.23 = (bf16[2,1,64,384]{3,2,1,0:T(8,128)(2,1)S(1)}, bf16[2,1,64,384]{3,2,1,0:T(8,128)(2,1)S(1)}, u32[]{:S(2)}, u32[]{:S(2)}) collective-permute-start(bf16[2,1,64,384]{3,2,1,0:T(8,128)(2,1)S(1)} %pad_maximum_fusion.1.refs_0_), channel_id=1, source_target_pairs={{0,12},{4,0},{8,4},{12,8},{1,13},{5,1},{9,5},{13,9},{2,14},{6,2},{... | collective-permute-start | bytes 294920 | tf_op jit(solution)/shard_map/ppermute | solution.py:29
  122.5 4.3 %collective-permute-start.18 = (bf16[2,1,64,384]{3,2,1,0:T(8,128)(2,1)S(1)}, bf16[2,1,64,384]{3,2,1,0:T(8,128)(2,1)S(1)}, u32[]{:S(2)}, u32[]{:S(2)}) collective-permute-start(bf16[2,1,64,384]{3,2,1,0:T(8,128)(2,1)S(1)} %pad_maximum_fusion.1.refs_0_), channel_id=1, source_target_pairs={{0,1},{1,0},{2,3},{3,2},{4,5},{5,4},{6,7},{7,6},{8,9},{9,8},{10,11... | collective-permute-start | bytes 294920 | tf_op jit(solution)/shard_map/ppermute | solution.py:29
  123.2 3.7 %collective-permute-start.33 = (bf16[2,1,64,384]{3,2,1,0:T(8,128)(2,1)S(1)}, bf16[2,1,64,384]{3,2,1,0:T(8,128)(2,1)S(1)}, u32[]{:S(2)}, u32[]{:S(2)}) collective-permute-start(bf16[2,1,64,384]{3,2,1,0:T(8,128)(2,1)S(1)} %collective-permute-done.32.refs_10_), channel_id=1, source_target_pairs={{0,1},{1,0},{2,3},{3,2},{4,5},{5,4},{6,7},{7,6},{8,9},{9,8},{10,11... | collective-permute-start | bytes 294920 | tf_op jit(solution)/shard_map/ppermute | solution.py:29
  126.4 1.3 collective-permute-start.35
  126.4 1.5 %collective-permute-start.37 = (bf16[2,1,64,384]{3,2,1,0:T(8,128)(2,1)S(1)}, bf16[2,1,64,384]{3,2,1,0:T(8,128)(2,1)S(1)}, u32[]{:S(2)}, u32[]{:S(2)}) collective-permute-start(bf16[2,1,64,384]{3,2,1,0:T(8,128)(2,1)S(1)} %collective-permute-done.36.refs_14_), channel_id=1, source_target_pairs={{0,1},{1,0},{2,3},{3,2},{4,5},{5,4},{6,7},{7,6},{8,9},{9,8},{10,11... | collective-permute-start | bytes 294920 | tf_op jit(solution)/shard_map/ppermute | solution.py:29
  126.9 1.3 collective-permute-start.20
  127.0 1.4 collective-permute-start.22
  127.7 1.3 collective-permute-start.24
  130.5 6.4 %collective-permute-start.42 = (bf16[1,64,640]{2,1,0:T(8,128)(2,1)S(1)}, bf16[1,64,640]{2,1,0:T(8,128)(2,1)S(1)}, u32[]{:S(2)}, u32[]{:S(2)}) collective-permute-start(bf16[1,64,640]{2,1,0:T(8,128)(2,1)S(1)} %get-tuple-element.62), channel_id=1, source_target_pairs={{0,12},{4,0},{8,4},{12,8},{1,13},{5,1},{9,5},{13,9},{2,14},{6,2},{... | collective-permute-start | bytes 245768 | tf_op jit(solution)/shard_map/ppermute | solution.py:29
  134.1 8.0 %collective-permute-start.44 = (bf16[1,64,640]{2,1,0:T(8,128)(2,1)S(1)}, bf16[1,64,640]{2,1,0:T(8,128)(2,1)S(1)}, u32[]{:S(2)}, u32[]{:S(2)}) collective-permute-start(bf16[1,64,640]{2,1,0:T(8,128)(2,1)S(1)} %get-tuple-element.63), channel_id=1, source_target_pairs={{0,8},{4,12},{8,0},{12,4},{1,9},{5,13},{9,1},{13,5},{2,10},{6,14},... | collective-permute-start | bytes 245768 | tf_op jit(solution)/shard_map/ppermute | solution.py:29
  134.1 8.0 %collective-permute-start.46 = (bf16[1,64,640]{2,1,0:T(8,128)(2,1)S(1)}, bf16[1,64,640]{2,1,0:T(8,128)(2,1)S(1)}, u32[]{:S(2)}, u32[]{:S(2)}) collective-permute-start(bf16[1,64,640]{2,1,0:T(8,128)(2,1)S(1)} %get-tuple-element.64), channel_id=1, source_target_pairs={{0,4},{4,8},{8,12},{12,0},{1,5},{5,9},{9,13},{13,1},{2,6},{6,10},{... | collective-permute-start | bytes 245768 | tf_op jit(solution)/shard_map/ppermute | solution.py:29
  134.7 7.9 %collective-permute-start.41 = (bf16[1,64,640]{2,1,0:T(8,128)(2,1)S(1)}, bf16[1,64,640]{2,1,0:T(8,128)(2,1)S(1)}, u32[]{:S(2)}, u32[]{:S(2)}) collective-permute-start(bf16[1,64,640]{2,1,0:T(8,128)(2,1)S(1)} %get-tuple-element.61), channel_id=1, source_target_pairs={{0,1},{1,0},{2,3},{3,2},{4,5},{5,4},{6,7},{7,6},{8,9},{9,8},{10,11... | collective-permute-start | bytes 245768 | tf_op jit(solution)/shard_map/ppermute | solution.py:29
  137.0 5.7 %collective-permute-start.43 = (bf16[1,64,640]{2,1,0:T(8,128)(2,1)S(1)}, bf16[1,64,640]{2,1,0:T(8,128)(2,1)S(1)}, u32[]{:S(2)}, u32[]{:S(2)}) collective-permute-start(bf16[1,64,640]{2,1,0:T(8,128)(2,1)S(1)} %collective-permute-done.42.refs_2_), channel_id=1, source_target_pairs={{0,1},{1,0},{2,3},{3,2},{4,5},{5,4},{6,7},{7,6},{8,9},{9,8},{10,11... | collective-permute-start | bytes 245768 | tf_op jit(solution)/shard_map/ppermute | solution.py:29
  142.1 1.3 collective-permute-start.45
  142.1 1.4 collective-permute-start.47
  (7 other events, 43.0 us)

commit v11 on v10

--- a/solution.py
+++ b/solution.py
@@ -12,7 +12,6 @@
 FREQ = 256
 STEPS = 100
 LANES = 128
-DMA_PIECES = 4
 
 
 sample_shift = 5.0
@@ -199,26 +198,16 @@
     )(weights)
 
 
-def modulate_kernel(n_tm, n_seq, n_mp, step_ref, w_ref, *refs):
+def modulate_kernel(n_tm, n_seq, n_mp, step_ref, *refs):
     sides = n_seq * n_mp
     shares, near, far = refs[:n_tm], refs[n_tm : n_tm + sides], refs[n_tm + sides :][:sides]
-    hidden_ref, coef_ref, w_out, mod_scr, sems = refs[n_tm + 2 * sides :]
-    stride = w_ref.shape[1] // DMA_PIECES
-    copies = []
-    for c in range(w_ref.shape[0]):
-        for piece in range(DMA_PIECES):
-            at = c, pl.ds(piece * stride, stride)
-            copies.append(
-                pltpu.make_async_copy(w_ref.at[at], w_out.at[at], sems.at[len(copies)])
-            )
+    hidden_ref, coef_ref, mod_scr = refs[n_tm + 2 * sides :]
     z, k = lax.axis_index("tm"), pl.program_id(0)
     frames, part, wide = near[0].shape
     depth = wide - LANES
 
     @pl.when(k == 0)
     def _():
-        for copy in copies:
-            copy.start()
         total = shares[0][...]
         for share in shares[1:]:
             total = total + share[...]
@@ -249,23 +238,17 @@
                 def _():
                     hidden_ref[0, j, f, to, :] = modulated(far[j * n_mp + i][0, f])
 
-    @pl.when(k == n_tm - 1)
-    def _():
-        for copy in copies:
-            copy.wait()
-
-
-def modulate(start_step, w_qkv, shares, near, far):
+
+def modulate(start_step, shares, near, far):
     n_tm, n_seq, n_mp = len(shares), len(near), len(near[0])
     frames, part, wide = near[0][0].shape
-    three = w_qkv.shape[0]
     depth = wide - LANES
     window = shares[0].shape[1]
     shape = (n_tm, n_seq, frames, n_mp * part, depth)
     return pl.pallas_call(
         functools.partial(modulate_kernel, n_tm, n_seq, n_mp),
         grid=(n_tm,),
-        in_specs=[pl.BlockSpec(memory_space=pltpu.SMEM), pl.BlockSpec(memory_space=pltpu.HBM)]
+        in_specs=[pl.BlockSpec(memory_space=pltpu.SMEM)]
         + [pl.BlockSpec((3, window, depth), lambda k: (0, 0, 0))] * n_tm
         + [pl.BlockSpec((frames, part, wide), lambda k: (0, 0, 0))] * (n_seq * n_mp)
         + [pl.BlockSpec((1, frames, part, wide), lambda k: (jnp.maximum(k - 1, 0), 0, 0, 0))]
@@ -273,25 +256,22 @@
         out_specs=[
             pl.BlockSpec((1,) + shape[1:], lambda k: (k, 0, 0, 0, 0)),
             pl.BlockSpec((1, frames, depth), lambda k: (k, 0, 0)),
-        ]
-        + [pl.BlockSpec(memory_space=pl.ANY)],
+        ],
         scratch_shapes=[
             pltpu.VMEM((3, window, depth), jnp.float32),
-            pltpu.SemaphoreType.DMA((three * DMA_PIECES,)),
         ],
         out_shape=[
             jax.ShapeDtypeStruct(shape, jnp.bfloat16),
             jax.ShapeDtypeStruct((n_tm, frames, depth), jnp.float32),
-        ]
-        + [jax.ShapeDtypeStruct(w_qkv.shape, w_qkv.dtype)],
+        ],
         cost_estimate=pl.CostEstimate(
             flops=4 * n_tm * n_seq * frames * n_mp * part * depth,
             bytes_accessed=4 * n_tm * n_seq * frames * n_mp * part * depth,
             transcendentals=0,
         ),
-        compiler_params=pltpu.CompilerParams(vmem_limit_bytes=42 << 20),
+        compiler_params=pltpu.CompilerParams(vmem_limit_bytes=24 << 20),
         name="modulate",
-    )(start_step, w_qkv, *shares, *[r for rows in (near, far) for side in rows for r in side])
+    )(start_step, *shares, *[r for rows in (near, far) for side in rows for r in side])
 
 
 def project_kernel(dims, widths, coef_ref, *refs):
@@ -442,7 +422,7 @@
             weights[j].append(turn(share, "seq", -j))
 
     groups = head_groups(cols)
-    hidden, coef, held_qkv = modulate(start_step, w_qkv, shares, near, far)
+    hidden, coef = modulate(start_step, shares, near, far)
     hidden = hidden.reshape(n_tm, n_seq * frames * tok, depth)
     proj = []
     for lane, size in groups:
@@ -450,7 +430,7 @@
             jnp.einsum(
                 "krd,cdh->kcrh",
                 hidden,
-                held_qkv[:, :, lane : lane + size],
+                w_qkv[:, :, lane : lane + size],
                 preferred_element_type=jnp.float32,
             )
         )

time: 145 us -> 147 us (1.014)
  matrix products: 3.74 us -> 5.71 us
    dot_general x2, matrix products: 3.74 us -> 5.71 us  [sweep(): jnp.einsum('krd,cdh->kcrh', hidden, w_qkv[:, :, lane:lane + size], prefer...]
    unnamed x14 -> x18, local copies, waits for them, and re-layouts: 3.26 us -> 3.27 us
where the time goes in v11:
time: 147 us
  waiting for transfers between devices  84.1 us (57%)
  starting transfers between devices  36 us (24%)
  Pallas kernels  9.23 us (6%)
  other arithmetic  7.7 us (5%)
  matrix products  5.71 us (4%)
  local copies, waits for them, and re-layouts  3.28 us (2%)
    ppermute x38, waiting for transfers between devices, turn(): lax.ppermute(block, axis, [(i, (i + distance) % size) for i in range(size)])  61.6 us
    ppermute x38, starting transfers between devices, turn(): lax.ppermute(block, axis, [(i, (i + distance) % size) for i in range(size)])  31.9 us
    ppermute x6, waiting for transfers between devices, sweep(): first = lax.ppermute(first, 'tm', ev)  22.5 us
    dot_general x2, matrix products, sweep(): jnp.einsum('krd,cdh->kcrh', hidden, w_qkv[:, :, lane:lane + size], prefer...  5.71 us
    convert_element_type x4, other arithmetic, sweep(): second = jnp.where(even, left, right).astype(jnp.float16)  4.52 us
    ppermute x6, starting transfers between devices, sweep(): first = lax.ppermute(first, 'tm', ev)  3.96 us
    unnamed x18, local copies, waits for them, and re-layouts  3.27 us
  transfers between devices with their start and end apart: 48, of which 26 were waited for; matrix products, arithmetic and copies ran while one was open for 6% of the time, Pallas kernels for 2%

profile of v11, /device:TPU:0, one launch (start us, length us, event | category | flops | bytes accessed | tf_op | source)
XLA Modules:
  0.0 147.0 jit_solution(8336014428409023832)
XLA Ops:
  0.0 1.1 copy-done.2
  1.5 3.1 %collective-permute-start.6 = (bf16[1,32,1408]{2,1,0:T(8,128)(2,1)S(1)}, bf16[1,32,1408]{2,1,0:T(8,128)(2,1)S(1)}, u32[]{:S(2)}, u32[]{:S(2)}) collective-permute-start(bf16[1,32,1408]{2,1,0:T(8,128)(2,1)S(1)} %get-tuple-element.39), channel_id=1, source_target_pairs={{0,4},{4,8},{8,12},{12,0},{1,5},{5,9},{9,13},{13,1},{2,6},{6,10},{... | collective-permute-start | bytes 270344 | tf_op jit(solution)/shard_map/ppermute | solution.py:28
  4.6 2.6 %collective-permute-start.7 = (bf16[1,32,1408]{2,1,0:T(8,128)(2,1)S(1)}, bf16[1,32,1408]{2,1,0:T(8,128)(2,1)S(1)}, u32[]{:S(2)}, u32[]{:S(2)}) collective-permute-start(bf16[1,32,1408]{2,1,0:T(8,128)(2,1)S(1)} %get-tuple-element.40), channel_id=1, source_target_pairs={{0,8},{4,12},{8,0},{12,4},{1,9},{5,13},{9,1},{13,5},{2,10},{6,14},... | collective-permute-start | bytes 270344 | tf_op jit(solution)/shard_map/ppermute | solution.py:28
  7.2 1.4 collective-permute-start.8
  8.5 1.4 collective-permute-done.6
  9.9 3.3 %collective-permute-done.7 = bf16[1,32,1408]{2,1,0:T(8,128)(2,1)S(1)} collective-permute-done((bf16[1,32,1408]{2,1,0:T(8,128)(2,1)S(1)}, bf16[1,32,1408]{2,1,0:T(8,128)(2,1)S(1)}, u32[]{:S(2)}, u32[]{:S(2)}) %collective-permute-start.7) | collective-permute-done | bytes 90144 | tf_op jit(solution)/shard_map/ppermute | solution.py:28
  13.5 1.6 %collective-permute-start.10 = (bf16[3,1,32,1408]{3,2,1,0:T(8,128)(2,1)S(1)}, bf16[3,1,32,1408]{3,2,1,0:T(8,128)(2,1)S(1)}, u32[]{:S(2)}, u32[]{:S(2)}) collective-permute-start(bf16[3,1,32,1408]{3,2,1,0:T(8,128)(2,1)S(1)} %pad_maximum_fusion.refs_8_), channel_id=1, source_target_pairs={{0,2},{2,0},{1,3},{3,1},{4,6},{6,4},{5,7},{7,5},{8,10},{10,8},{9,1... | collective-permute-start | bytes 811016 | tf_op jit(solution)/shard_map/ppermute | solution.py:28
  15.0 6.6 %collective-permute-done.10.refs_10_ = bf16[3,1,32,1408]{3,2,1,0:T(8,128)(2,1)S(1)} collective-permute-done((bf16[3,1,32,1408]{3,2,1,0:T(8,128)(2,1)S(1)}, bf16[3,1,32,1408]{3,2,1,0:T(8,128)(2,1)S(1)}, u32[]{:S(2)}, u32[]{:S(2)}) %collective-permute-start.10) | collective-permute-done | bytes 270368 | tf_op jit(solution)/shard_map/ppermute | solution.py:28
  21.7 1.5 %collective-permute-start.4 = (bf16[1,32,1408]{2,1,0:T(8,128)(2,1)S(1)}, bf16[1,32,1408]{2,1,0:T(8,128)(2,1)S(1)}, u32[]{:S(2)}, u32[]{:S(2)}) collective-permute-start(bf16[1,32,1408]{2,1,0:T(8,128)(2,1)S(1)} %get-tuple-element.38.refs_4_), channel_id=1, source_target_pairs={{0,2},{2,0},{1,3},{3,1},{4,6},{6,4},{5,7},{7,5},{8,10},{10,8},{9,1... | collective-permute-start | bytes 270344 | tf_op jit(solution)/shard_map/ppermute | solution.py:28
  23.8 1.5 %copy-done = bf16[64,15360]{1,0:T(8,128)(2,1)S(1)} copy-done((bf16[64,15360]{1,0:T(8,128)(2,1)S(1)}, bf16[64,15360]{1,0:T(8,128)(2,1)}, u32[]{:S(2)}) %copy-start) | copy-done | bytes 1966104
  25.3 0.8 time_shares.1
  26.2 2.6 %collective-permute-start = (f32[3,4,1280]{2,1,0:T(4,128)S(1)}, f32[3,4,1280]{2,1,0:T(4,128)S(1)}, u32[]{:S(2)}, u32[]{:S(2)}) collective-permute-start(f32[3,4,1280]{2,1,0:T(4,128)S(1)} %get-tuple-element.35), channel_id=1, source_target_pairs={{0,4},{4,8},{8,12},{12,0},{1,5},{5,9},{9,13},{13,1},{2,6},{6,10},{... | collective-permute-start | bytes 184328 | tf_op jit(solution)/shard_map/ppermute | solution.py:28
  29.2 3.3 %collective-permute-done.refs_1_ = f32[3,4,1280]{2,1,0:T(4,128)S(1)} collective-permute-done((f32[3,4,1280]{2,1,0:T(4,128)S(1)}, f32[3,4,1280]{2,1,0:T(4,128)S(1)}, u32[]{:S(2)}, u32[]{:S(2)}) %collective-permute-start) | collective-permute-done | bytes 61472 | tf_op jit(solution)/shard_map/ppermute | solution.py:28
  33.1 1.8 %collective-permute-done.1.refs_2_ = f32[3,4,1280]{2,1,0:T(4,128)S(1)} collective-permute-done((f32[3,4,1280]{2,1,0:T(4,128)S(1)}, f32[3,4,1280]{2,1,0:T(4,128)S(1)}, u32[]{:S(2)}, u32[]{:S(2)}) %collective-permute-start.1) | collective-permute-done | bytes 61472 | tf_op jit(solution)/shard_map/ppermute | solution.py:28
  34.9 1.3 collective-permute-start.2
  36.2 2.9 %collective-permute-done.2.refs_3_ = f32[3,4,1280]{2,1,0:T(4,128)S(1)} collective-permute-done((f32[3,4,1280]{2,1,0:T(4,128)S(1)}, f32[3,4,1280]{2,1,0:T(4,128)S(1)}, u32[]{:S(2)}, u32[]{:S(2)}) %collective-permute-start.2) | collective-permute-done | bytes 61472 | tf_op jit(solution)/shard_map/ppermute | solution.py:28
  39.1 2.9 %modulate.1 = (bf16[4,2,1,64,1280]{4,3,2,1,0:T(8,128)(2,1)S(1)}, f32[4,1,1280]{2,1,0:T(1,128)S(1)}) custom-call(s32[1]{0:T(128)S(6)} %copy.8.step_ref, f32[3,4,1280]{2,1,0:T(4,128)S(1)} %get-tuple-element.34.refs_0_, f32[3,4,1280]{2,1,0:T(4,128)S(1)} %collective-permute-done.refs_1_, f32[3,4,1280]{2,1,0:T(4,128)S(1)} %collective-permute-done.1.refs_2_, ...), custom_call_target="tpu_custom_call" | custom-call | flops 2621440 | bytes 2621440 | tf_op jit(solution)/shard_map/modulate/pallas_call | solution.py:248
  42.1 3.8 %fusion.9 = f32[4,3,128,384]{3,2,1,0:T(8,128)S(1)} fusion(bf16[4,128,1280,1]{2,1,3,0:T(8,128)(2,1)S(1)} %bitcast.110, bf16[3,1280,768]{2,1,0:T(8,128)(2,1)} %param.8), kind=kOutput, calls=%fused_computation.7 | convolution fusion | flops 1509949440 | bytes 6619136 | tf_op jit(solution)/shard_map/krd,cdh->kcrh/dot_general | solution.py:430
  45.9 0.8 select_convert_fusion.4
  47.4 1.9 %fusion.6 = f32[4,3,128,384]{3,2,1,0:T(8,128)S(1)} fusion(bf16[4,128,1280,1]{2,1,3,0:T(8,128)(2,1)S(1)} %bitcast.111, bf16[3,1280,768]{2,1,0:T(8,128)(2,1)S(1)} %bitcast.118), kind=kOutput, calls=%fused_computation.6 | convolution fusion | flops 1509949440 | bytes 6619136 | tf_op jit(solution)/shard_map/krd,cdh->kcrh/dot_general | solution.py:430
  49.3 0.9 select_convert_fusion.9
  50.2 2.0 %collective-permute-start.12 = (f16[3,128,384]{2,1,0:T(8,128)(2,1)}, f16[3,128,384]{2,1,0:T(8,128)(2,1)S(1)}, u32[]{:S(2)}, u32[]{:S(2)}) collective-permute-start(f16[3,128,384]{2,1,0:T(8,128)(2,1)} %select_convert_fusion.9), channel_id=1, source_target_pairs={{0,4},{4,0},{8,12},{12,8},{1,5},{5,1},{9,13},{13,9},{2,6},{6,2},{1... | collective-permute-start | bytes 884744 | tf_op jit(solution)/shard_map/ppermute | solution.py:461
  52.9 4.7 %collective-permute-done.25 = f16[3,128,384]{2,1,0:T(8,128)(2,1)} collective-permute-done((f16[3,128,384]{2,1,0:T(8,128)(2,1)}, f16[3,128,384]{2,1,0:T(8,128)(2,1)}, u32[]{:S(2)}, u32[]{:S(2)}) %collective-permute-start.25) | collective-permute-done | bytes 294944 | tf_op jit(solution)/shard_map/ppermute | solution.py:461
  57.6 1.4 select_convert_fusion.2
  59.2 4.7 %collective-permute-done.12 = f16[3,128,384]{2,1,0:T(8,128)(2,1)S(1)} collective-permute-done((f16[3,128,384]{2,1,0:T(8,128)(2,1)}, f16[3,128,384]{2,1,0:T(8,128)(2,1)S(1)}, u32[]{:S(2)}, u32[]{:S(2)}) %collective-permute-start.12) | collective-permute-done | bytes 294944 | tf_op jit(solution)/shard_map/ppermute | solution.py:461
  63.8 1.3 select_convert_fusion.7
  65.3 4.8 %collective-permute-done.26 = f16[3,128,384]{2,1,0:T(8,128)(2,1)S(1)} collective-permute-done((f16[3,128,384]{2,1,0:T(8,128)(2,1)S(1)}, f16[3,128,384]{2,1,0:T(8,128)(2,1)S(1)}, u32[]{:S(2)}, u32[]{:S(2)}) %collective-permute-start.26) | collective-permute-done | bytes 294944 | tf_op jit(solution)/shard_map/ppermute | solution.py:461
  70.7 1.5 %select_convert_fusion = (f16[3,128,384]{2,1,0:T(8,128)(2,1)S(1)}, f16[3,128,384]{2,1,0:T(8,128)(2,1)S(1)}) fusion(pred[]{:T(512)S(6)} %eq.5, f16[3,128,384]{2,1,0:T(8,128)(2,1)S(1)} %collective-permute-done.27, f16[3,128,384]{2,1,0:T(8,128)(2,1)S(1)} %collective-permute-done.26, pred[]{:T(512)S(6)} %lt.9, f32[4,3,128,384]{3,2,1,0:T(8,128)} %copy-done.5, ...), kind=kLoop, calls=%fused_computation.52 | loop fusion | flops 1769472 | bytes 2359299 | tf_op jit(solution)/shard_map/convert_element_type | solution.py:460
  72.3 4.2 %collective-permute-done.13 = f16[3,128,384]{2,1,0:T(8,128)(2,1)S(1)} collective-permute-done((f16[3,128,384]{2,1,0:T(8,128)(2,1)S(1)}, f16[3,128,384]{2,1,0:T(8,128)(2,1)S(1)}, u32[]{:S(2)}, u32[]{:S(2)}) %collective-permute-start.13) | collective-permute-done | bytes 294944 | tf_op jit(solution)/shard_map/ppermute | solution.py:461
  76.8 1.7 %collective-permute-start.15 = (f16[3,128,384]{2,1,0:T(8,128)(2,1)S(1)}, f16[3,128,384]{2,1,0:T(8,128)(2,1)S(1)}, u32[]{:S(2)}, u32[]{:S(2)}) collective-permute-start(f16[3,128,384]{2,1,0:T(8,128)(2,1)S(1)} %get-tuple-element.66), channel_id=1, source_target_pairs={{0,4},{4,0},{8,12},{12,8},{1,5},{5,1},{9,13},{13,9},{2,6},{6,2},{1... | collective-permute-start | bytes 884744 | tf_op jit(solution)/shard_map/ppermute | solution.py:461
  78.5 2.9 %collective-permute-done.28 = f16[3,128,384]{2,1,0:T(8,128)(2,1)S(1)} collective-permute-done((f16[3,128,384]{2,1,0:T(8,128)(2,1)S(1)}, f16[3,128,384]{2,1,0:T(8,128)(2,1)S(1)}, u32[]{:S(2)}, u32[]{:S(2)}) %collective-permute-start.28) | collective-permute-done | bytes 294944 | tf_op jit(solution)/shard_map/ppermute | solution.py:461
  82.0 1.2 fusion.34
  83.2 0.9 attend.3
  84.2 1.5 %collective-permute-start.30 = (bf16[1,64,384]{2,1,0:T(8,128)(2,1)S(1)}, bf16[1,64,384]{2,1,0:T(8,128)(2,1)S(1)}, u32[]{:S(2)}, u32[]{:S(2)}) collective-permute-start(bf16[1,64,384]{2,1,0:T(8,128)(2,1)S(1)} %get-tuple-element.55), channel_id=1, source_target_pairs={{0,2},{2,0},{1,3},{3,1},{4,6},{6,4},{5,7},{7,5},{8,10},{10,8},{9,1... | collective-permute-start | bytes 147464 | tf_op jit(solution)/shard_map/ppermute | solution.py:28
  85.7 1.3 collective-permute-done.15
  87.2 0.9 attend.2
  88.7 23.6 %collective-permute-done.30 = bf16[1,64,384]{2,1,0:T(8,128)(2,1)S(1)} collective-permute-done((bf16[1,64,384]{2,1,0:T(8,128)(2,1)S(1)}, bf16[1,64,384]{2,1,0:T(8,128)(2,1)S(1)}, u32[]{:S(2)}, u32[]{:S(2)}) %collective-permute-start.30) | collective-permute-done | bytes 49184 | tf_op jit(solution)/shard_map/ppermute | solution.py:28
  113.0 2.8 %collective-permute-start.34 = (bf16[2,1,64,384]{3,2,1,0:T(8,128)(2,1)S(1)}, bf16[2,1,64,384]{3,2,1,0:T(8,128)(2,1)S(1)}, u32[]{:S(2)}, u32[]{:S(2)}) collective-permute-start(bf16[2,1,64,384]{3,2,1,0:T(8,128)(2,1)S(1)} %pad_maximum_fusion.2.refs_8_), channel_id=1, source_target_pairs={{0,8},{4,12},{8,0},{12,4},{1,9},{5,13},{9,1},{13,5},{2,10},{6,14},... | collective-permute-start | bytes 294920 | tf_op jit(solution)/shard_map/ppermute | solution.py:28
  116.4 2.6 %collective-permute-done.32.refs_10_ = bf16[2,1,64,384]{3,2,1,0:T(8,128)(2,1)S(1)} collective-permute-done((bf16[2,1,64,384]{3,2,1,0:T(8,128)(2,1)S(1)}, bf16[2,1,64,384]{3,2,1,0:T(8,128)(2,1)S(1)}, u32[]{:S(2)}, u32[]{:S(2)}) %collective-permute-start.32) | collective-permute-done | bytes 98336 | tf_op jit(solution)/shard_map/ppermute | solution.py:28
  118.9 1.8 %collective-permute-done.34.refs_12_ = bf16[2,1,64,384]{3,2,1,0:T(8,128)(2,1)S(1)} collective-permute-done((bf16[2,1,64,384]{3,2,1,0:T(8,128)(2,1)S(1)}, bf16[2,1,64,384]{3,2,1,0:T(8,128)(2,1)S(1)}, u32[]{:S(2)}, u32[]{:S(2)}) %collective-permute-start.34) | collective-permute-done | bytes 98336 | tf_op jit(solution)/shard_map/ppermute | solution.py:28
  121.4 3.1 %collective-permute-start.23 = (bf16[2,1,64,384]{3,2,1,0:T(8,128)(2,1)S(1)}, bf16[2,1,64,384]{3,2,1,0:T(8,128)(2,1)S(1)}, u32[]{:S(2)}, u32[]{:S(2)}) collective-permute-start(bf16[2,1,64,384]{3,2,1,0:T(8,128)(2,1)S(1)} %pad_maximum_fusion.1.refs_0_), channel_id=1, source_target_pairs={{0,12},{4,0},{8,4},{12,8},{1,13},{5,1},{9,5},{13,9},{2,14},{6,2},{... | collective-permute-start | bytes 294920 | tf_op jit(solution)/shard_map/ppermute | solution.py:28
  124.5 1.1 collective-permute-done.19.refs_2_
  125.6 3.2 %collective-permute-done.21.refs_4_ = bf16[2,1,64,384]{3,2,1,0:T(8,128)(2,1)S(1)} collective-permute-done((bf16[2,1,64,384]{3,2,1,0:T(8,128)(2,1)S(1)}, bf16[2,1,64,384]{3,2,1,0:T(8,128)(2,1)S(1)}, u32[]{:S(2)}, u32[]{:S(2)}) %collective-permute-start.21) | collective-permute-done | bytes 98336 | tf_op jit(solution)/shard_map/ppermute | solution.py:28
  131.4 1.5 %project.1 = (f32[1,64,640]{2,1,0:T(8,128)S(1)}, bf16[1,64,640]{2,1,0:T(8,128)(2,1)S(1)}, bf16[1,64,640]{2,1,0:T(8,128)(2,1)S(1)}, bf16[1,64,640]{2,1,0:T(8,128)(2,1)S(1)}, bf16[1,64,640]{2,1,0:T(8,128)(2,1)S(1)}) custom-call(f32[4,1,1280]{2,1,0:T(1,128)S(1)} %get-tuple-element.42.coef_ref, bf16[2,1,64,384]{3,2,1,0:T(8,128)(2,1)S(1)} %pad_maximum_fusion.1.refs_0_, ...), custom_call_target="tpu_custom_call" | custom-call | flops 1006632960 | bytes 5505024 | tf_op jit(solution)/shard_map/project/pallas_call | solution.py:341
  132.9 3.6 %collective-permute-start.42 = (bf16[1,64,640]{2,1,0:T(8,128)(2,1)S(1)}, bf16[1,64,640]{2,1,0:T(8,128)(2,1)S(1)}, u32[]{:S(2)}, u32[]{:S(2)}) collective-permute-start(bf16[1,64,640]{2,1,0:T(8,128)(2,1)S(1)} %get-tuple-element.60), channel_id=1, source_target_pairs={{0,12},{4,0},{8,4},{12,8},{1,13},{5,1},{9,5},{13,9},{2,14},{6,2},{... | collective-permute-start | bytes 245768 | tf_op jit(solution)/shard_map/ppermute | solution.py:28
  137.2 2.2 %collective-permute-done.42.refs_2_ = bf16[1,64,640]{2,1,0:T(8,128)(2,1)S(1)} collective-permute-done((bf16[1,64,640]{2,1,0:T(8,128)(2,1)S(1)}, bf16[1,64,640]{2,1,0:T(8,128)(2,1)S(1)}, u32[]{:S(2)}, u32[]{:S(2)}) %collective-permute-start.42) | collective-permute-done | bytes 81952 | tf_op jit(solution)/shard_map/ppermute | solution.py:28
  139.4 5.1 %collective-permute-done.44.refs_4_ = bf16[1,64,640]{2,1,0:T(8,128)(2,1)S(1)} collective-permute-done((bf16[1,64,640]{2,1,0:T(8,128)(2,1)S(1)}, bf16[1,64,640]{2,1,0:T(8,128)(2,1)S(1)}, u32[]{:S(2)}, u32[]{:S(2)}) %collective-permute-start.44) | collective-permute-done | bytes 81952 | tf_op jit(solution)/shard_map/ppermute | solution.py:28
  146.0 1.0 finish.1
  (89 shorter events, 12.1 us)
Async XLA Ops:
  1.5 8.4 %collective-permute-start.6 = (bf16[1,32,1408]{2,1,0:T(8,128)(2,1)S(1)}, bf16[1,32,1408]{2,1,0:T(8,128)(2,1)S(1)}, u32[]{:S(2)}, u32[]{:S(2)}) collective-permute-start(bf16[1,32,1408]{2,1,0:T(8,128)(2,1)S(1)} %get-tuple-element.39), channel_id=1, source_target_pairs={{0,4},{4,8},{8,12},{12,0},{1,5},{5,9},{9,13},{13,1},{2,6},{6,10},{... | collective-permute-start | bytes 270344 | tf_op jit(solution)/shard_map/ppermute | solution.py:28
  4.6 8.6 %collective-permute-start.7 = (bf16[1,32,1408]{2,1,0:T(8,128)(2,1)S(1)}, bf16[1,32,1408]{2,1,0:T(8,128)(2,1)S(1)}, u32[]{:S(2)}, u32[]{:S(2)}) collective-permute-start(bf16[1,32,1408]{2,1,0:T(8,128)(2,1)S(1)} %get-tuple-element.40), channel_id=1, source_target_pairs={{0,8},{4,12},{8,0},{12,4},{1,9},{5,13},{9,1},{13,5},{2,10},{6,14},... | collective-permute-start | bytes 270344 | tf_op jit(solution)/shard_map/ppermute | solution.py:28
  7.2 6.3 %collective-permute-start.8 = (bf16[1,32,1408]{2,1,0:T(8,128)(2,1)S(1)}, bf16[1,32,1408]{2,1,0:T(8,128)(2,1)S(1)}, u32[]{:S(2)}, u32[]{:S(2)}) collective-permute-start(bf16[1,32,1408]{2,1,0:T(8,128)(2,1)S(1)} %get-tuple-element.41), channel_id=1, source_target_pairs={{0,12},{4,0},{8,4},{12,8},{1,13},{5,1},{9,5},{13,9},{2,14},{6,2},{... | collective-permute-start | bytes 270344 | tf_op jit(solution)/shard_map/ppermute | solution.py:28
  13.5 8.2 %collective-permute-start.10 = (bf16[3,1,32,1408]{3,2,1,0:T(8,128)(2,1)S(1)}, bf16[3,1,32,1408]{3,2,1,0:T(8,128)(2,1)S(1)}, u32[]{:S(2)}, u32[]{:S(2)}) collective-permute-start(bf16[3,1,32,1408]{3,2,1,0:T(8,128)(2,1)S(1)} %pad_maximum_fusion.refs_8_), channel_id=1, source_target_pairs={{0,2},{2,0},{1,3},{3,1},{4,6},{6,4},{5,7},{7,5},{8,10},{10,8},{9,1... | collective-permute-start | bytes 811016 | tf_op jit(solution)/shard_map/ppermute | solution.py:28
  15.0 24.1 %collective-permute-start.9 = (bf16[3,1,32,1408]{3,2,1,0:T(8,128)(2,1)S(1)}, bf16[3,1,32,1408]{3,2,1,0:T(8,128)(2,1)S(1)}, u32[]{:S(2)}, u32[]{:S(2)}) collective-permute-start(bf16[3,1,32,1408]{3,2,1,0:T(8,128)(2,1)S(1)} %pad_maximum_fusion.refs_8_), channel_id=1, source_target_pairs={{0,1},{1,0},{2,3},{3,2},{4,5},{5,4},{6,7},{7,6},{8,9},{9,8},{10,11... | collective-permute-start | bytes 811016 | tf_op jit(solution)/shard_map/ppermute | solution.py:28
  21.6 17.5 %collective-permute-start.11 = (bf16[3,1,32,1408]{3,2,1,0:T(8,128)(2,1)S(1)}, bf16[3,1,32,1408]{3,2,1,0:T(8,128)(2,1)S(1)}, u32[]{:S(2)}, u32[]{:S(2)}) collective-permute-start(bf16[3,1,32,1408]{3,2,1,0:T(8,128)(2,1)S(1)} %collective-permute-done.10.refs_10_), channel_id=1, source_target_pairs={{0,1},{1,0},{2,3},{3,2},{4,5},{5,4},{6,7},{7,6},{8,9},{9,8},{10,11... | collective-permute-start | bytes 811016 | tf_op jit(solution)/shard_map/ppermute | solution.py:28
  21.7 10.9 %collective-permute-start.4 = (bf16[1,32,1408]{2,1,0:T(8,128)(2,1)S(1)}, bf16[1,32,1408]{2,1,0:T(8,128)(2,1)S(1)}, u32[]{:S(2)}, u32[]{:S(2)}) collective-permute-start(bf16[1,32,1408]{2,1,0:T(8,128)(2,1)S(1)} %get-tuple-element.38.refs_4_), channel_id=1, source_target_pairs={{0,2},{2,0},{1,3},{3,1},{4,6},{6,4},{5,7},{7,5},{8,10},{10,8},{9,1... | collective-permute-start | bytes 270344 | tf_op jit(solution)/shard_map/ppermute | solution.py:28
  26.2 6.4 %collective-permute-start = (f32[3,4,1280]{2,1,0:T(4,128)S(1)}, f32[3,4,1280]{2,1,0:T(4,128)S(1)}, u32[]{:S(2)}, u32[]{:S(2)}) collective-permute-start(f32[3,4,1280]{2,1,0:T(4,128)S(1)} %get-tuple-element.35), channel_id=1, source_target_pairs={{0,4},{4,8},{8,12},{12,0},{1,5},{5,9},{9,13},{13,1},{2,6},{6,10},{... | collective-permute-start | bytes 184328 | tf_op jit(solution)/shard_map/ppermute | solution.py:28
  28.7 6.1 %collective-permute-start.1 = (f32[3,4,1280]{2,1,0:T(4,128)S(1)}, f32[3,4,1280]{2,1,0:T(4,128)S(1)}, u32[]{:S(2)}, u32[]{:S(2)}) collective-permute-start(f32[3,4,1280]{2,1,0:T(4,128)S(1)} %get-tuple-element.36), channel_id=1, source_target_pairs={{0,8},{4,12},{8,0},{12,4},{1,9},{5,13},{9,1},{13,5},{2,10},{6,14},... | collective-permute-start | bytes 184328 | tf_op jit(solution)/shard_map/ppermute | solution.py:28
  32.5 6.6 %collective-permute-start.3 = (bf16[1,32,1408]{2,1,0:T(8,128)(2,1)S(1)}, bf16[1,32,1408]{2,1,0:T(8,128)(2,1)S(1)}, u32[]{:S(2)}, u32[]{:S(2)}) collective-permute-start(bf16[1,32,1408]{2,1,0:T(8,128)(2,1)S(1)} %get-tuple-element.38.refs_4_), channel_id=1, source_target_pairs={{0,1},{1,0},{2,3},{3,2},{4,5},{5,4},{6,7},{7,6},{8,9},{9,8},{10,11... | collective-permute-start | bytes 270344 | tf_op jit(solution)/shard_map/ppermute | solution.py:28
  32.6 6.5 %collective-permute-start.5 = (bf16[1,32,1408]{2,1,0:T(8,128)(2,1)S(1)}, bf16[1,32,1408]{2,1,0:T(8,128)(2,1)S(1)}, u32[]{:S(2)}, u32[]{:S(2)}) collective-permute-start(bf16[1,32,1408]{2,1,0:T(8,128)(2,1)S(1)} %collective-permute-done.4.refs_6_), channel_id=1, source_target_pairs={{0,1},{1,0},{2,3},{3,2},{4,5},{5,4},{6,7},{7,6},{8,9},{9,8},{10,11... | collective-permute-start | bytes 270344 | tf_op jit(solution)/shard_map/ppermute | solution.py:28
  34.9 4.2 %collective-permute-start.2 = (f32[3,4,1280]{2,1,0:T(4,128)S(1)}, f32[3,4,1280]{2,1,0:T(4,128)S(1)}, u32[]{:S(2)}, u32[]{:S(2)}) collective-permute-start(f32[3,4,1280]{2,1,0:T(4,128)S(1)} %get-tuple-element.37), channel_id=1, source_target_pairs={{0,12},{4,0},{8,4},{12,8},{1,13},{5,1},{9,5},{13,9},{2,14},{6,2},{... | collective-permute-start | bytes 184328 | tf_op jit(solution)/shard_map/ppermute | solution.py:28
  47.4 10.2 %collective-permute-start.25 = (f16[3,128,384]{2,1,0:T(8,128)(2,1)}, f16[3,128,384]{2,1,0:T(8,128)(2,1)}, u32[]{:S(2)}, u32[]{:S(2)}) collective-permute-start(f16[3,128,384]{2,1,0:T(8,128)(2,1)} %select_convert_fusion.4), channel_id=1, source_target_pairs={{0,4},{4,0},{8,12},{12,8},{1,5},{5,1},{9,13},{13,9},{2,6},{6,2},{1... | collective-permute-start | bytes 884744 | tf_op jit(solution)/shard_map/ppermute | solution.py:461
  50.2 13.6 %collective-permute-start.12 = (f16[3,128,384]{2,1,0:T(8,128)(2,1)}, f16[3,128,384]{2,1,0:T(8,128)(2,1)S(1)}, u32[]{:S(2)}, u32[]{:S(2)}) collective-permute-start(f16[3,128,384]{2,1,0:T(8,128)(2,1)} %select_convert_fusion.9), channel_id=1, source_target_pairs={{0,4},{4,0},{8,12},{12,8},{1,5},{5,1},{9,13},{13,9},{2,6},{6,2},{1... | collective-permute-start | bytes 884744 | tf_op jit(solution)/shard_map/ppermute | solution.py:461
  52.8 25.7 %collective-permute-start.38 = (bf16[640,768]{1,0:T(8,128)(2,1)S(1)}, bf16[640,768]{1,0:T(8,128)(2,1)S(1)}, u32[]{:S(2)}, u32[]{:S(2)}) collective-permute-start(bf16[640,768]{1,0:T(8,128)(2,1)S(1)} %get-tuple-element.57), channel_id=1, source_target_pairs={{0,1},{1,0},{2,3},{3,2},{4,5},{5,4},{6,7},{7,6},{8,9},{9,8},{10,11... | collective-permute-start | bytes 2949128 | tf_op jit(solution)/shard_map/ppermute | solution.py:28
  59.0 11.1 %collective-permute-start.26 = (f16[3,128,384]{2,1,0:T(8,128)(2,1)S(1)}, f16[3,128,384]{2,1,0:T(8,128)(2,1)S(1)}, u32[]{:S(2)}, u32[]{:S(2)}) collective-permute-start(f16[3,128,384]{2,1,0:T(8,128)(2,1)S(1)} %get-tuple-element.68), channel_id=1, source_target_pairs={{0,4},{4,0},{8,12},{12,8},{1,5},{5,1},{9,13},{13,9},{2,6},{6,2},{1... | collective-permute-start | bytes 884744 | tf_op jit(solution)/shard_map/ppermute | solution.py:461
  59.1 11.6 %collective-permute-start.27 = (f16[3,128,384]{2,1,0:T(8,128)(2,1)S(1)}, f16[3,128,384]{2,1,0:T(8,128)(2,1)S(1)}, u32[]{:S(2)}, u32[]{:S(2)}) collective-permute-start(f16[3,128,384]{2,1,0:T(8,128)(2,1)S(1)} %get-tuple-element.67), channel_id=1, source_target_pairs={{0,1},{1,0},{4,8},{5,9},{8,4},{9,5},{12,13},{13,12},{2,3},{3,2},{6... | collective-permute-start | bytes 884744 | tf_op jit(solution)/shard_map/ppermute | solution.py:463
  65.1 11.3 %collective-permute-start.13 = (f16[3,128,384]{2,1,0:T(8,128)(2,1)S(1)}, f16[3,128,384]{2,1,0:T(8,128)(2,1)S(1)}, u32[]{:S(2)}, u32[]{:S(2)}) collective-permute-start(f16[3,128,384]{2,1,0:T(8,128)(2,1)S(1)} %get-tuple-element.70), channel_id=1, source_target_pairs={{0,4},{4,0},{8,12},{12,8},{1,5},{5,1},{9,13},{13,9},{2,6},{6,2},{1... | collective-permute-start | bytes 884744 | tf_op jit(solution)/shard_map/ppermute | solution.py:461
  65.2 11.3 %collective-permute-start.14 = (f16[3,128,384]{2,1,0:T(8,128)(2,1)S(1)}, f16[3,128,384]{2,1,0:T(8,128)(2,1)S(1)}, u32[]{:S(2)}, u32[]{:S(2)}) collective-permute-start(f16[3,128,384]{2,1,0:T(8,128)(2,1)S(1)} %get-tuple-element.69), channel_id=1, source_target_pairs={{0,1},{1,0},{4,8},{5,9},{8,4},{9,5},{12,13},{13,12},{2,3},{3,2},{6... | collective-permute-start | bytes 884744 | tf_op jit(solution)/shard_map/ppermute | solution.py:463
  70.1 46.1 %collective-permute-start.39 = (bf16[640,768]{1,0:T(8,128)(2,1)S(1)}, bf16[640,768]{1,0:T(8,128)(2,1)S(1)}, u32[]{:S(2)}, u32[]{:S(2)}) collective-permute-start(bf16[640,768]{1,0:T(8,128)(2,1)S(1)} %get-tuple-element.56.refs_16_), channel_id=1, source_target_pairs={{0,2},{2,0},{1,3},{3,1},{4,6},{6,4},{5,7},{7,5},{8,10},{10,8},{9,1... | collective-permute-start | bytes 2949128 | tf_op jit(solution)/shard_map/ppermute | solution.py:28
  72.2 9.2 %collective-permute-start.28 = (f16[3,128,384]{2,1,0:T(8,128)(2,1)S(1)}, f16[3,128,384]{2,1,0:T(8,128)(2,1)S(1)}, u32[]{:S(2)}, u32[]{:S(2)}) collective-permute-start(f16[3,128,384]{2,1,0:T(8,128)(2,1)S(1)} %get-tuple-element.64), channel_id=1, source_target_pairs={{0,4},{4,0},{8,12},{12,8},{1,5},{5,1},{9,13},{13,9},{2,6},{6,2},{1... | collective-permute-start | bytes 884744 | tf_op jit(solution)/shard_map/ppermute | solution.py:461
  76.5 5.5 %collective-permute-start.29 = (f16[3,128,384]{2,1,0:T(8,128)(2,1)S(1)}, f16[3,128,384]{2,1,0:T(8,128)(2,1)S(1)}, u32[]{:S(2)}, u32[]{:S(2)}) collective-permute-start(f16[3,128,384]{2,1,0:T(8,128)(2,1)S(1)} %get-tuple-element.63), channel_id=1, source_target_pairs={{0,1},{1,0},{4,8},{5,9},{8,4},{9,5},{12,13},{13,12},{2,3},{3,2},{6... | collective-permute-start | bytes 884744 | tf_op jit(solution)/shard_map/ppermute | solution.py:463
  76.8 10.2 %collective-permute-start.15 = (f16[3,128,384]{2,1,0:T(8,128)(2,1)S(1)}, f16[3,128,384]{2,1,0:T(8,128)(2,1)S(1)}, u32[]{:S(2)}, u32[]{:S(2)}) collective-permute-start(f16[3,128,384]{2,1,0:T(8,128)(2,1)S(1)} %get-tuple-element.66), channel_id=1, source_target_pairs={{0,4},{4,0},{8,12},{12,8},{1,5},{5,1},{9,13},{13,9},{2,6},{6,2},{1... | collective-permute-start | bytes 884744 | tf_op jit(solution)/shard_map/ppermute | solution.py:461
  78.5 8.5 %collective-permute-start.16 = (f16[3,128,384]{2,1,0:T(8,128)(2,1)S(1)}, f16[3,128,384]{2,1,0:T(8,128)(2,1)S(1)}, u32[]{:S(2)}, u32[]{:S(2)}) collective-permute-start(f16[3,128,384]{2,1,0:T(8,128)(2,1)S(1)} %get-tuple-element.65), channel_id=1, source_target_pairs={{0,1},{1,0},{4,8},{5,9},{8,4},{9,5},{12,13},{13,12},{2,3},{3,2},{6... | collective-permute-start | bytes 884744 | tf_op jit(solution)/shard_map/ppermute | solution.py:463
  81.4 49.9 %collective-permute-start.40 = (bf16[640,768]{1,0:T(8,128)(2,1)S(1)}, bf16[640,768]{1,0:T(8,128)(2,1)S(1)}, u32[]{:S(2)}, u32[]{:S(2)}) collective-permute-start(bf16[640,768]{1,0:T(8,128)(2,1)S(1)} %collective-permute-done.38.refs_17_), channel_id=1, source_target_pairs={{0,2},{2,0},{1,3},{3,1},{4,6},{6,4},{5,7},{7,5},{8,10},{10,8},{9,1... | collective-permute-start | bytes 2949128 | tf_op jit(solution)/shard_map/ppermute | solution.py:28
  84.2 28.2 %collective-permute-start.30 = (bf16[1,64,384]{2,1,0:T(8,128)(2,1)S(1)}, bf16[1,64,384]{2,1,0:T(8,128)(2,1)S(1)}, u32[]{:S(2)}, u32[]{:S(2)}) collective-permute-start(bf16[1,64,384]{2,1,0:T(8,128)(2,1)S(1)} %get-tuple-element.55), channel_id=1, source_target_pairs={{0,2},{2,0},{1,3},{3,1},{4,6},{6,4},{5,7},{7,5},{8,10},{10,8},{9,1... | collective-permute-start | bytes 147464 | tf_op jit(solution)/shard_map/ppermute | solution.py:28
  88.1 27.6 %collective-permute-start.17 = (bf16[1,64,384]{2,1,0:T(8,128)(2,1)S(1)}, bf16[1,64,384]{2,1,0:T(8,128)(2,1)S(1)}, u32[]{:S(2)}, u32[]{:S(2)}) collective-permute-start(bf16[1,64,384]{2,1,0:T(8,128)(2,1)S(1)} %get-tuple-element.49), channel_id=1, source_target_pairs={{0,2},{2,0},{1,3},{3,1},{4,6},{6,4},{5,7},{7,5},{8,10},{10,8},{9,1... | collective-permute-start | bytes 147464 | tf_op jit(solution)/shard_map/ppermute | solution.py:28
  112.4 6.6 %collective-permute-start.32 = (bf16[2,1,64,384]{3,2,1,0:T(8,128)(2,1)S(1)}, bf16[2,1,64,384]{3,2,1,0:T(8,128)(2,1)S(1)}, u32[]{:S(2)}, u32[]{:S(2)}) collective-permute-start(bf16[2,1,64,384]{3,2,1,0:T(8,128)(2,1)S(1)} %pad_maximum_fusion.2.refs_8_), channel_id=1, source_target_pairs={{0,4},{4,8},{8,12},{12,0},{1,5},{5,9},{9,13},{13,1},{2,6},{6,10},{... | collective-permute-start | bytes 294920 | tf_op jit(solution)/shard_map/ppermute | solution.py:28
  113.0 7.7 %collective-permute-start.34 = (bf16[2,1,64,384]{3,2,1,0:T(8,128)(2,1)S(1)}, bf16[2,1,64,384]{3,2,1,0:T(8,128)(2,1)S(1)}, u32[]{:S(2)}, u32[]{:S(2)}) collective-permute-start(bf16[2,1,64,384]{3,2,1,0:T(8,128)(2,1)S(1)} %pad_maximum_fusion.2.refs_8_), channel_id=1, source_target_pairs={{0,8},{4,12},{8,0},{12,4},{1,9},{5,13},{9,1},{13,5},{2,10},{6,14},... | collective-permute-start | bytes 294920 | tf_op jit(solution)/shard_map/ppermute | solution.py:28
  115.8 5.6 %collective-permute-start.36 = (bf16[2,1,64,384]{3,2,1,0:T(8,128)(2,1)S(1)}, bf16[2,1,64,384]{3,2,1,0:T(8,128)(2,1)S(1)}, u32[]{:S(2)}, u32[]{:S(2)}) collective-permute-start(bf16[2,1,64,384]{3,2,1,0:T(8,128)(2,1)S(1)} %pad_maximum_fusion.2.refs_8_), channel_id=1, source_target_pairs={{0,12},{4,0},{8,4},{12,8},{1,13},{5,1},{9,5},{13,9},{2,14},{6,2},{... | collective-permute-start | bytes 294920 | tf_op jit(solution)/shard_map/ppermute | solution.py:28
  116.3 8.2 %collective-permute-start.31 = (bf16[2,1,64,384]{3,2,1,0:T(8,128)(2,1)S(1)}, bf16[2,1,64,384]{3,2,1,0:T(8,128)(2,1)S(1)}, u32[]{:S(2)}, u32[]{:S(2)}) collective-permute-start(bf16[2,1,64,384]{3,2,1,0:T(8,128)(2,1)S(1)} %pad_maximum_fusion.2.refs_8_), channel_id=1, source_target_pairs={{0,1},{1,0},{2,3},{3,2},{4,5},{5,4},{6,7},{7,6},{8,9},{9,8},{10,11... | collective-permute-start | bytes 294920 | tf_op jit(solution)/shard_map/ppermute | solution.py:28
  118.9 6.7 %collective-permute-start.19 = (bf16[2,1,64,384]{3,2,1,0:T(8,128)(2,1)S(1)}, bf16[2,1,64,384]{3,2,1,0:T(8,128)(2,1)S(1)}, u32[]{:S(2)}, u32[]{:S(2)}) collective-permute-start(bf16[2,1,64,384]{3,2,1,0:T(8,128)(2,1)S(1)} %pad_maximum_fusion.1.refs_0_), channel_id=1, source_target_pairs={{0,4},{4,8},{8,12},{12,0},{1,5},{5,9},{9,13},{13,1},{2,6},{6,10},{... | collective-permute-start | bytes 294920 | tf_op jit(solution)/shard_map/ppermute | solution.py:28
  120.7 8.1 %collective-permute-start.21 = (bf16[2,1,64,384]{3,2,1,0:T(8,128)(2,1)S(1)}, bf16[2,1,64,384]{3,2,1,0:T(8,128)(2,1)S(1)}, u32[]{:S(2)}, u32[]{:S(2)}) collective-permute-start(bf16[2,1,64,384]{3,2,1,0:T(8,128)(2,1)S(1)} %pad_maximum_fusion.1.refs_0_), channel_id=1, source_target_pairs={{0,8},{4,12},{8,0},{12,4},{1,9},{5,13},{9,1},{13,5},{2,10},{6,14},... | collective-permute-start | bytes 294920 | tf_op jit(solution)/shard_map/ppermute | solution.py:28
  121.4 7.4 %collective-permute-start.23 = (bf16[2,1,64,384]{3,2,1,0:T(8,128)(2,1)S(1)}, bf16[2,1,64,384]{3,2,1,0:T(8,128)(2,1)S(1)}, u32[]{:S(2)}, u32[]{:S(2)}) collective-permute-start(bf16[2,1,64,384]{3,2,1,0:T(8,128)(2,1)S(1)} %pad_maximum_fusion.1.refs_0_), channel_id=1, source_target_pairs={{0,12},{4,0},{8,4},{12,8},{1,13},{5,1},{9,5},{13,9},{2,14},{6,2},{... | collective-permute-start | bytes 294920 | tf_op jit(solution)/shard_map/ppermute | solution.py:28
  124.5 4.8 %collective-permute-start.18 = (bf16[2,1,64,384]{3,2,1,0:T(8,128)(2,1)S(1)}, bf16[2,1,64,384]{3,2,1,0:T(8,128)(2,1)S(1)}, u32[]{:S(2)}, u32[]{:S(2)}) collective-permute-start(bf16[2,1,64,384]{3,2,1,0:T(8,128)(2,1)S(1)} %pad_maximum_fusion.1.refs_0_), channel_id=1, source_target_pairs={{0,1},{1,0},{2,3},{3,2},{4,5},{5,4},{6,7},{7,6},{8,9},{9,8},{10,11... | collective-permute-start | bytes 294920 | tf_op jit(solution)/shard_map/ppermute | solution.py:28
  125.6 3.7 %collective-permute-start.33 = (bf16[2,1,64,384]{3,2,1,0:T(8,128)(2,1)S(1)}, bf16[2,1,64,384]{3,2,1,0:T(8,128)(2,1)S(1)}, u32[]{:S(2)}, u32[]{:S(2)}) collective-permute-start(bf16[2,1,64,384]{3,2,1,0:T(8,128)(2,1)S(1)} %collective-permute-done.32.refs_10_), channel_id=1, source_target_pairs={{0,1},{1,0},{2,3},{3,2},{4,5},{5,4},{6,7},{7,6},{8,9},{9,8},{10,11... | collective-permute-start | bytes 294920 | tf_op jit(solution)/shard_map/ppermute | solution.py:28
  128.8 1.3 collective-permute-start.35
  128.8 1.5 collective-permute-start.37
  129.3 1.3 collective-permute-start.20
  129.4 1.4 collective-permute-start.22
  130.1 1.3 collective-permute-start.24
  132.9 6.5 %collective-permute-start.42 = (bf16[1,64,640]{2,1,0:T(8,128)(2,1)S(1)}, bf16[1,64,640]{2,1,0:T(8,128)(2,1)S(1)}, u32[]{:S(2)}, u32[]{:S(2)}) collective-permute-start(bf16[1,64,640]{2,1,0:T(8,128)(2,1)S(1)} %get-tuple-element.60), channel_id=1, source_target_pairs={{0,12},{4,0},{8,4},{12,8},{1,13},{5,1},{9,5},{13,9},{2,14},{6,2},{... | collective-permute-start | bytes 245768 | tf_op jit(solution)/shard_map/ppermute | solution.py:28
  136.5 8.0 %collective-permute-start.44 = (bf16[1,64,640]{2,1,0:T(8,128)(2,1)S(1)}, bf16[1,64,640]{2,1,0:T(8,128)(2,1)S(1)}, u32[]{:S(2)}, u32[]{:S(2)}) collective-permute-start(bf16[1,64,640]{2,1,0:T(8,128)(2,1)S(1)} %get-tuple-element.61), channel_id=1, source_target_pairs={{0,8},{4,12},{8,0},{12,4},{1,9},{5,13},{9,1},{13,5},{2,10},{6,14},... | collective-permute-start | bytes 245768 | tf_op jit(solution)/shard_map/ppermute | solution.py:28
  136.5 8.0 %collective-permute-start.46 = (bf16[1,64,640]{2,1,0:T(8,128)(2,1)S(1)}, bf16[1,64,640]{2,1,0:T(8,128)(2,1)S(1)}, u32[]{:S(2)}, u32[]{:S(2)}) collective-permute-start(bf16[1,64,640]{2,1,0:T(8,128)(2,1)S(1)} %get-tuple-element.62), channel_id=1, source_target_pairs={{0,4},{4,8},{8,12},{12,0},{1,5},{5,9},{9,13},{13,1},{2,6},{6,10},{... | collective-permute-start | bytes 245768 | tf_op jit(solution)/shard_map/ppermute | solution.py:28
  137.1 7.9 %collective-permute-start.41 = (bf16[1,64,640]{2,1,0:T(8,128)(2,1)S(1)}, bf16[1,64,640]{2,1,0:T(8,128)(2,1)S(1)}, u32[]{:S(2)}, u32[]{:S(2)}) collective-permute-start(bf16[1,64,640]{2,1,0:T(8,128)(2,1)S(1)} %get-tuple-element.59), channel_id=1, source_target_pairs={{0,1},{1,0},{2,3},{3,2},{4,5},{5,4},{6,7},{7,6},{8,9},{9,8},{10,11... | collective-permute-start | bytes 245768 | tf_op jit(solution)/shard_map/ppermute | solution.py:28
  139.4 5.7 %collective-permute-start.43 = (bf16[1,64,640]{2,1,0:T(8,128)(2,1)S(1)}, bf16[1,64,640]{2,1,0:T(8,128)(2,1)S(1)}, u32[]{:S(2)}, u32[]{:S(2)}) collective-permute-start(bf16[1,64,640]{2,1,0:T(8,128)(2,1)S(1)} %collective-permute-done.42.refs_2_), channel_id=1, source_target_pairs={{0,1},{1,0},{2,3},{3,2},{4,5},{5,4},{6,7},{7,6},{8,9},{9,8},{10,11... | collective-permute-start | bytes 245768 | tf_op jit(solution)/shard_map/ppermute | solution.py:28
  144.5 1.3 collective-permute-start.45
  144.6 1.4 collective-permute-start.47
  (9 other events, 57.9 us)

commit v12 on v10

--- a/solution.py
+++ b/solution.py
@@ -224,30 +224,30 @@
             total = total + share[...]
         mod_scr[...] = total
 
-    for f in range(frames):
-        step = lax.rem(z - k + n_tm, n_tm) * frames + f
-        shift, scale, gate = (mod_scr[c, pl.ds(step, 1), :] for c in range(3))
-        index = jnp.full((1, depth), step_ref[0] + step, jnp.int32)
-        coef_ref[0, f : f + 1, :] = (sigma_of(index + 1) - sigma_of(index)) * gate
-
-        def modulated(block):
-            tail = block[:, depth:].astype(jnp.float32)
-            mean = tail[:, 0:1] + tail[:, 1:2] + tail[:, 2:3]
-            rstd = tail[:, 3:4] + tail[:, 4:5] + tail[:, 5:6]
-            normed = (block[:, :depth].astype(jnp.float32) - mean) * rstd
-            return (normed * (1.0 + scale) + shift).astype(jnp.bfloat16)
-
-        for j in range(n_seq):
-            for i in range(n_mp):
-                to = slice(i * part, (i + 1) * part)
-
-                @pl.when(k == 0)
-                def _():
-                    hidden_ref[0, j, f, to, :] = modulated(near[j * n_mp + i][f])
-
-                @pl.when(k > 0)
-                def _():
-                    hidden_ref[0, j, f, to, :] = modulated(far[j * n_mp + i][0, f])
+    def write(blocks):
+        for f in range(frames):
+            step = lax.rem(z - k + n_tm, n_tm) * frames + f
+            shift, scale, gate = (mod_scr[c, pl.ds(step, 1), :] for c in range(3))
+            index = jnp.full((1, depth), step_ref[0] + step, jnp.int32)
+            coef_ref[0, f : f + 1, :] = (sigma_of(index + 1) - sigma_of(index)) * gate
+            for j in range(n_seq):
+                for i in range(n_mp):
+                    block = blocks[j * n_mp + i]
+                    tail = block[f, :, depth:].astype(jnp.float32)
+                    mean = tail[:, 0:1] + tail[:, 1:2] + tail[:, 2:3]
+                    rstd = tail[:, 3:4] + tail[:, 4:5] + tail[:, 5:6]
+                    normed = (block[f, :, :depth].astype(jnp.float32) - mean) * rstd
+                    hidden_ref[0, j, f, i * part : (i + 1) * part, :] = (
+                        normed * (1.0 + scale) + shift
+                    ).astype(jnp.bfloat16)
+
+    @pl.when(k == 0)
+    def _():
+        write(near)
+
+    @pl.when(k > 0)
+    def _():
+        write([block.at[0] for block in far])
 
     @pl.when(k == n_tm - 1)
     def _():

time: 145 us -> 145 us (level)
  no operation moved by 1% of the time
where the time goes in v12:
time: 145 us; the launch traced here: 144 us
  waiting for transfers between devices  83.8 us (58%)
  starting transfers between devices  35.8 us (25%)
  Pallas kernels  9.14 us (6%)
  other arithmetic  7.66 us (5%)
  matrix products  3.74 us (3%)
  local copies, waits for them, and re-layouts  3.26 us (2%)
    ppermute x38, waiting for transfers between devices, turn(): lax.ppermute(block, axis, [(i, (i + distance) % size) for i in range(size)])  61.1 us
    ppermute x38, starting transfers between devices, turn(): lax.ppermute(block, axis, [(i, (i + distance) % size) for i in range(size)])  32.4 us
    ppermute x6, waiting for transfers between devices, sweep(): first = lax.ppermute(first, 'tm', ev)  22.7 us
    convert_element_type x4, other arithmetic, sweep(): second = jnp.where(even, left, right).astype(jnp.float16)  4.47 us
    dot_general x2, matrix products, sweep(): jnp.einsum('krd,cdh->kcrh', hidden, held_qkv[:, :, lane:lane + size], pre...  3.74 us
    unnamed x14, local copies, waits for them, and re-layouts  3.26 us
    ppermute x6, starting transfers between devices, sweep(): first = lax.ppermute(first, 'tm', ev)  3.24 us
  transfers between devices with their start and end apart: 48, of which 26 were waited for; matrix products, arithmetic and copies ran while one was open for 6% of the time, Pallas kernels for 2%

profile of v12, /device:TPU:0, one launch (start us, length us, event | category | flops | bytes accessed | tf_op | source)
XLA Modules:
  0.0 144.3 jit_solution(2115808483203218075)
XLA Ops:
  0.0 1.1 copy-done.2
  1.5 3.1 %collective-permute-start.6 = (bf16[1,32,1408]{2,1,0:T(8,128)(2,1)S(1)}, bf16[1,32,1408]{2,1,0:T(8,128)(2,1)S(1)}, u32[]{:S(2)}, u32[]{:S(2)}) collective-permute-start(bf16[1,32,1408]{2,1,0:T(8,128)(2,1)S(1)} %get-tuple-element.40), channel_id=1, source_target_pairs={{0,4},{4,8},{8,12},{12,0},{1,5},{5,9},{9,13},{13,1},{2,6},{6,10},{... | collective-permute-start | bytes 270344 | tf_op jit(solution)/shard_map/ppermute | solution.py:29
  4.6 2.6 %collective-permute-start.7 = (bf16[1,32,1408]{2,1,0:T(8,128)(2,1)S(1)}, bf16[1,32,1408]{2,1,0:T(8,128)(2,1)S(1)}, u32[]{:S(2)}, u32[]{:S(2)}) collective-permute-start(bf16[1,32,1408]{2,1,0:T(8,128)(2,1)S(1)} %get-tuple-element.41), channel_id=1, source_target_pairs={{0,8},{4,12},{8,0},{12,4},{1,9},{5,13},{9,1},{13,5},{2,10},{6,14},... | collective-permute-start | bytes 270344 | tf_op jit(solution)/shard_map/ppermute | solution.py:29
  7.2 1.4 collective-permute-start.8
  8.5 1.4 collective-permute-done.6
  9.9 3.3 %collective-permute-done.7 = bf16[1,32,1408]{2,1,0:T(8,128)(2,1)S(1)} collective-permute-done((bf16[1,32,1408]{2,1,0:T(8,128)(2,1)S(1)}, bf16[1,32,1408]{2,1,0:T(8,128)(2,1)S(1)}, u32[]{:S(2)}, u32[]{:S(2)}) %collective-permute-start.7) | collective-permute-done | bytes 90144 | tf_op jit(solution)/shard_map/ppermute | solution.py:29
  13.5 1.6 %collective-permute-start.10 = (bf16[3,1,32,1408]{3,2,1,0:T(8,128)(2,1)S(1)}, bf16[3,1,32,1408]{3,2,1,0:T(8,128)(2,1)S(1)}, u32[]{:S(2)}, u32[]{:S(2)}) collective-permute-start(bf16[3,1,32,1408]{3,2,1,0:T(8,128)(2,1)S(1)} %pad_maximum_fusion.refs_8_), channel_id=1, source_target_pairs={{0,2},{2,0},{1,3},{3,1},{4,6},{6,4},{5,7},{7,5},{8,10},{10,8},{9,1... | collective-permute-start | bytes 811016 | tf_op jit(solution)/shard_map/ppermute | solution.py:29
  15.0 6.6 %collective-permute-done.10.refs_10_ = bf16[3,1,32,1408]{3,2,1,0:T(8,128)(2,1)S(1)} collective-permute-done((bf16[3,1,32,1408]{3,2,1,0:T(8,128)(2,1)S(1)}, bf16[3,1,32,1408]{3,2,1,0:T(8,128)(2,1)S(1)}, u32[]{:S(2)}, u32[]{:S(2)}) %collective-permute-start.10) | collective-permute-done | bytes 270368 | tf_op jit(solution)/shard_map/ppermute | solution.py:29
  21.7 1.5 %collective-permute-start.4 = (bf16[1,32,1408]{2,1,0:T(8,128)(2,1)S(1)}, bf16[1,32,1408]{2,1,0:T(8,128)(2,1)S(1)}, u32[]{:S(2)}, u32[]{:S(2)}) collective-permute-start(bf16[1,32,1408]{2,1,0:T(8,128)(2,1)S(1)} %get-tuple-element.39.refs_4_), channel_id=1, source_target_pairs={{0,2},{2,0},{1,3},{3,1},{4,6},{6,4},{5,7},{7,5},{8,10},{10,8},{9,1... | collective-permute-start | bytes 270344 | tf_op jit(solution)/shard_map/ppermute | solution.py:29
  23.8 1.5 %copy-done = bf16[64,15360]{1,0:T(8,128)(2,1)S(1)} copy-done((bf16[64,15360]{1,0:T(8,128)(2,1)S(1)}, bf16[64,15360]{1,0:T(8,128)(2,1)}, u32[]{:S(2)}) %copy-start) | copy-done | bytes 1966104
  25.3 0.8 time_shares.1
  26.2 2.6 %collective-permute-start = (f32[3,4,1280]{2,1,0:T(4,128)S(1)}, f32[3,4,1280]{2,1,0:T(4,128)S(1)}, u32[]{:S(2)}, u32[]{:S(2)}) collective-permute-start(f32[3,4,1280]{2,1,0:T(4,128)S(1)} %get-tuple-element.36), channel_id=1, source_target_pairs={{0,4},{4,8},{8,12},{12,0},{1,5},{5,9},{9,13},{13,1},{2,6},{6,10},{... | collective-permute-start | bytes 184328 | tf_op jit(solution)/shard_map/ppermute | solution.py:29
  29.2 3.3 %collective-permute-done.refs_1_ = f32[3,4,1280]{2,1,0:T(4,128)S(1)} collective-permute-done((f32[3,4,1280]{2,1,0:T(4,128)S(1)}, f32[3,4,1280]{2,1,0:T(4,128)S(1)}, u32[]{:S(2)}, u32[]{:S(2)}) %collective-permute-start) | collective-permute-done | bytes 61472 | tf_op jit(solution)/shard_map/ppermute | solution.py:29
  33.1 1.8 %collective-permute-done.1.refs_2_ = f32[3,4,1280]{2,1,0:T(4,128)S(1)} collective-permute-done((f32[3,4,1280]{2,1,0:T(4,128)S(1)}, f32[3,4,1280]{2,1,0:T(4,128)S(1)}, u32[]{:S(2)}, u32[]{:S(2)}) %collective-permute-start.1) | collective-permute-done | bytes 61472 | tf_op jit(solution)/shard_map/ppermute | solution.py:29
  34.9 1.3 collective-permute-start.2
  36.2 2.9 %collective-permute-done.2.refs_3_ = f32[3,4,1280]{2,1,0:T(4,128)S(1)} collective-permute-done((f32[3,4,1280]{2,1,0:T(4,128)S(1)}, f32[3,4,1280]{2,1,0:T(4,128)S(1)}, u32[]{:S(2)}, u32[]{:S(2)}) %collective-permute-start.2) | collective-permute-done | bytes 61472 | tf_op jit(solution)/shard_map/ppermute | solution.py:29
  39.1 2.8 %modulate.1 = (bf16[4,2,1,64,1280]{4,3,2,1,0:T(8,128)(2,1)S(1)}, f32[4,1,1280]{2,1,0:T(1,128)S(1)}, bf16[3,1280,768]{2,1,0:T(8,128)(2,1)S(1)}) custom-call(s32[1]{0:T(128)S(6)} %copy.17.step_ref, bf16[3,1280,768]{2,1,0:T(8,128)(2,1)} %w_ref.2, f32[3,4,1280]{2,1,0:T(4,128)S(1)} %get-tuple-element.35.refs_0_, f32[3,4,1280]{2,1,0:T(4,128)S(1)} %collective-permute-done.refs_1_, ...), custom_call_target="tpu_custom_call" | custom-call | flops 2621440 | bytes 2621440 | tf_op jit(solution)/shard_map/modulate/pallas_call | solution.py:265
  42.0 1.9 %fusion.6 = f32[4,3,128,384]{3,2,1,0:T(8,128)S(1)} fusion(bf16[4,128,1280,1]{2,1,3,0:T(8,128)(2,1)S(1)} %bitcast.118, bf16[3,1280,768]{2,1,0:T(8,128)(2,1)S(1)} %get-tuple-element.44), kind=kOutput, calls=%fused_computation.6 | convolution fusion | flops 1509949440 | bytes 6619136 | tf_op jit(solution)/shard_map/krd,cdh->kcrh/dot_general | solution.py:450
  43.9 0.9 select_convert_fusion.4
  45.3 1.9 %fusion.9 = f32[4,3,128,384]{3,2,0,1:T(8,128)S(1)} fusion(bf16[4,128,1280,1]{2,1,0,3:T(8,128)(2,1)S(1)} %bitcast.119, bf16[3,1280,768]{2,1,0:T(8,128)(2,1)S(1)} %get-tuple-element.44), kind=kOutput, calls=%fused_computation.7 | convolution fusion | flops 1509949440 | bytes 6619136 | tf_op jit(solution)/shard_map/krd,cdh->kcrh/dot_general | solution.py:450
  47.2 0.9 select_convert_fusion.9
  48.1 1.4 collective-permute-start.12
  50.3 4.6 %collective-permute-done.25 = f16[3,128,384]{2,1,0:T(8,128)(2,1)} collective-permute-done((f16[3,128,384]{2,1,0:T(8,128)(2,1)}, f16[3,128,384]{2,1,0:T(8,128)(2,1)}, u32[]{:S(2)}, u32[]{:S(2)}) %collective-permute-start.25) | collective-permute-done | bytes 294944 | tf_op jit(solution)/shard_map/ppermute | solution.py:481
  54.9 1.4 select_convert_fusion.2
  56.5 4.7 %collective-permute-done.12 = f16[3,128,384]{2,1,0:T(8,128)(2,1)S(1)} collective-permute-done((f16[3,128,384]{2,1,0:T(8,128)(2,1)}, f16[3,128,384]{2,1,0:T(8,128)(2,1)S(1)}, u32[]{:S(2)}, u32[]{:S(2)}) %collective-permute-start.12) | collective-permute-done | bytes 294944 | tf_op jit(solution)/shard_map/ppermute | solution.py:481
  61.1 1.3 select_convert_fusion.7
  62.6 4.8 %collective-permute-done.26 = f16[3,128,384]{2,1,0:T(8,128)(2,1)S(1)} collective-permute-done((f16[3,128,384]{2,1,0:T(8,128)(2,1)S(1)}, f16[3,128,384]{2,1,0:T(8,128)(2,1)S(1)}, u32[]{:S(2)}, u32[]{:S(2)}) %collective-permute-start.26) | collective-permute-done | bytes 294944 | tf_op jit(solution)/shard_map/ppermute | solution.py:481
  68.0 1.5 %select_convert_fusion = (f16[3,128,384]{2,1,0:T(8,128)(2,1)S(1)}, f16[3,128,384]{2,1,0:T(8,128)(2,1)S(1)}) fusion(pred[]{:T(512)S(6)} %eq.5, f16[3,128,384]{2,1,0:T(8,128)(2,1)S(1)} %collective-permute-done.27, f16[3,128,384]{2,1,0:T(8,128)(2,1)S(1)} %collective-permute-done.26, pred[]{:T(512)S(6)} %lt.9, f32[4,3,128,384]{3,2,1,0:T(8,128)} %copy-done.5, ...), kind=kLoop, calls=%fused_computation.52 | loop fusion | flops 1769472 | bytes 2359299 | tf_op jit(solution)/shard_map/convert_element_type | solution.py:480
  69.6 4.2 %collective-permute-done.13 = f16[3,128,384]{2,1,0:T(8,128)(2,1)S(1)} collective-permute-done((f16[3,128,384]{2,1,0:T(8,128)(2,1)S(1)}, f16[3,128,384]{2,1,0:T(8,128)(2,1)S(1)}, u32[]{:S(2)}, u32[]{:S(2)}) %collective-permute-start.13) | collective-permute-done | bytes 294944 | tf_op jit(solution)/shard_map/ppermute | solution.py:481
  74.0 1.6 %collective-permute-start.15 = (f16[3,128,384]{2,1,0:T(8,128)(2,1)S(1)}, f16[3,128,384]{2,1,0:T(8,128)(2,1)S(1)}, u32[]{:S(2)}, u32[]{:S(2)}) collective-permute-start(f16[3,128,384]{2,1,0:T(8,128)(2,1)S(1)} %get-tuple-element.68), channel_id=1, source_target_pairs={{0,4},{4,0},{8,12},{12,8},{1,5},{5,1},{9,13},{13,9},{2,6},{6,2},{1... | collective-permute-start | bytes 884744 | tf_op jit(solution)/shard_map/ppermute | solution.py:481
  75.7 3.1 %collective-permute-done.28 = f16[3,128,384]{2,1,0:T(8,128)(2,1)S(1)} collective-permute-done((f16[3,128,384]{2,1,0:T(8,128)(2,1)S(1)}, f16[3,128,384]{2,1,0:T(8,128)(2,1)S(1)}, u32[]{:S(2)}, u32[]{:S(2)}) %collective-permute-start.28) | collective-permute-done | bytes 294944 | tf_op jit(solution)/shard_map/ppermute | solution.py:481
  79.3 1.2 fusion.34
  80.5 0.9 attend.3
  81.5 1.5 %collective-permute-start.30 = (bf16[1,64,384]{2,1,0:T(8,128)(2,1)S(1)}, bf16[1,64,384]{2,1,0:T(8,128)(2,1)S(1)}, u32[]{:S(2)}, u32[]{:S(2)}) collective-permute-start(bf16[1,64,384]{2,1,0:T(8,128)(2,1)S(1)} %get-tuple-element.57), channel_id=1, source_target_pairs={{0,2},{2,0},{1,3},{3,1},{4,6},{6,4},{5,7},{7,5},{8,10},{10,8},{9,1... | collective-permute-start | bytes 147464 | tf_op jit(solution)/shard_map/ppermute | solution.py:29
  83.0 1.3 collective-permute-done.15
  84.5 0.9 attend.2
  86.0 23.6 %collective-permute-done.30 = bf16[1,64,384]{2,1,0:T(8,128)(2,1)S(1)} collective-permute-done((bf16[1,64,384]{2,1,0:T(8,128)(2,1)S(1)}, bf16[1,64,384]{2,1,0:T(8,128)(2,1)S(1)}, u32[]{:S(2)}, u32[]{:S(2)}) %collective-permute-start.30) | collective-permute-done | bytes 49184 | tf_op jit(solution)/shard_map/ppermute | solution.py:29
  110.3 2.7 %collective-permute-start.34 = (bf16[2,1,64,384]{3,2,1,0:T(8,128)(2,1)S(1)}, bf16[2,1,64,384]{3,2,1,0:T(8,128)(2,1)S(1)}, u32[]{:S(2)}, u32[]{:S(2)}) collective-permute-start(bf16[2,1,64,384]{3,2,1,0:T(8,128)(2,1)S(1)} %pad_maximum_fusion.2.refs_8_), channel_id=1, source_target_pairs={{0,8},{4,12},{8,0},{12,4},{1,9},{5,13},{9,1},{13,5},{2,10},{6,14},... | collective-permute-start | bytes 294920 | tf_op jit(solution)/shard_map/ppermute | solution.py:29
  113.7 2.6 %collective-permute-done.32.refs_10_ = bf16[2,1,64,384]{3,2,1,0:T(8,128)(2,1)S(1)} collective-permute-done((bf16[2,1,64,384]{3,2,1,0:T(8,128)(2,1)S(1)}, bf16[2,1,64,384]{3,2,1,0:T(8,128)(2,1)S(1)}, u32[]{:S(2)}, u32[]{:S(2)}) %collective-permute-start.32) | collective-permute-done | bytes 98336 | tf_op jit(solution)/shard_map/ppermute | solution.py:29
  116.3 1.8 %collective-permute-done.34.refs_12_ = bf16[2,1,64,384]{3,2,1,0:T(8,128)(2,1)S(1)} collective-permute-done((bf16[2,1,64,384]{3,2,1,0:T(8,128)(2,1)S(1)}, bf16[2,1,64,384]{3,2,1,0:T(8,128)(2,1)S(1)}, u32[]{:S(2)}, u32[]{:S(2)}) %collective-permute-start.34) | collective-permute-done | bytes 98336 | tf_op jit(solution)/shard_map/ppermute | solution.py:29
  118.6 3.7 %collective-permute-start.23 = (bf16[2,1,64,384]{3,2,1,0:T(8,128)(2,1)S(1)}, bf16[2,1,64,384]{3,2,1,0:T(8,128)(2,1)S(1)}, u32[]{:S(2)}, u32[]{:S(2)}) collective-permute-start(bf16[2,1,64,384]{3,2,1,0:T(8,128)(2,1)S(1)} %pad_maximum_fusion.1.refs_0_), channel_id=1, source_target_pairs={{0,12},{4,0},{8,4},{12,8},{1,13},{5,1},{9,5},{13,9},{2,14},{6,2},{... | collective-permute-start | bytes 294920 | tf_op jit(solution)/shard_map/ppermute | solution.py:29
  122.9 3.2 %collective-permute-done.21.refs_4_ = bf16[2,1,64,384]{3,2,1,0:T(8,128)(2,1)S(1)} collective-permute-done((bf16[2,1,64,384]{3,2,1,0:T(8,128)(2,1)S(1)}, bf16[2,1,64,384]{3,2,1,0:T(8,128)(2,1)S(1)}, u32[]{:S(2)}, u32[]{:S(2)}) %collective-permute-start.21) | collective-permute-done | bytes 98336 | tf_op jit(solution)/shard_map/ppermute | solution.py:29
  128.7 1.5 %project.1 = (f32[1,64,640]{2,1,0:T(8,128)S(1)}, bf16[1,64,640]{2,1,0:T(8,128)(2,1)S(1)}, bf16[1,64,640]{2,1,0:T(8,128)(2,1)S(1)}, bf16[1,64,640]{2,1,0:T(8,128)(2,1)S(1)}, bf16[1,64,640]{2,1,0:T(8,128)(2,1)S(1)}) custom-call(f32[4,1,1280]{2,1,0:T(1,128)S(1)} %get-tuple-element.43.coef_ref, bf16[2,1,64,384]{3,2,1,0:T(8,128)(2,1)S(1)} %pad_maximum_fusion.1.refs_0_, ...), custom_call_target="tpu_custom_call" | custom-call | flops 1006632960 | bytes 5505024 | tf_op jit(solution)/shard_map/project/pallas_call | solution.py:361
  130.2 3.6 %collective-permute-start.42 = (bf16[1,64,640]{2,1,0:T(8,128)(2,1)S(1)}, bf16[1,64,640]{2,1,0:T(8,128)(2,1)S(1)}, u32[]{:S(2)}, u32[]{:S(2)}) collective-permute-start(bf16[1,64,640]{2,1,0:T(8,128)(2,1)S(1)} %get-tuple-element.62), channel_id=1, source_target_pairs={{0,12},{4,0},{8,4},{12,8},{1,13},{5,1},{9,5},{13,9},{2,14},{6,2},{... | collective-permute-start | bytes 245768 | tf_op jit(solution)/shard_map/ppermute | solution.py:29
  134.5 2.2 %collective-permute-done.42.refs_2_ = bf16[1,64,640]{2,1,0:T(8,128)(2,1)S(1)} collective-permute-done((bf16[1,64,640]{2,1,0:T(8,128)(2,1)S(1)}, bf16[1,64,640]{2,1,0:T(8,128)(2,1)S(1)}, u32[]{:S(2)}, u32[]{:S(2)}) %collective-permute-start.42) | collective-permute-done | bytes 81952 | tf_op jit(solution)/shard_map/ppermute | solution.py:29
  136.7 5.1 %collective-permute-done.44.refs_4_ = bf16[1,64,640]{2,1,0:T(8,128)(2,1)S(1)} collective-permute-done((bf16[1,64,640]{2,1,0:T(8,128)(2,1)S(1)}, bf16[1,64,640]{2,1,0:T(8,128)(2,1)S(1)}, u32[]{:S(2)}, u32[]{:S(2)}) %collective-permute-start.44) | collective-permute-done | bytes 81952 | tf_op jit(solution)/shard_map/ppermute | solution.py:29
  142.4 0.8 collective-permute-done.45.refs_5_
  143.3 1.0 finish.1
  (84 shorter events, 12.0 us)
Async XLA Ops:
  1.5 8.4 %collective-permute-start.6 = (bf16[1,32,1408]{2,1,0:T(8,128)(2,1)S(1)}, bf16[1,32,1408]{2,1,0:T(8,128)(2,1)S(1)}, u32[]{:S(2)}, u32[]{:S(2)}) collective-permute-start(bf16[1,32,1408]{2,1,0:T(8,128)(2,1)S(1)} %get-tuple-element.40), channel_id=1, source_target_pairs={{0,4},{4,8},{8,12},{12,0},{1,5},{5,9},{9,13},{13,1},{2,6},{6,10},{... | collective-permute-start | bytes 270344 | tf_op jit(solution)/shard_map/ppermute | solution.py:29
  4.6 8.6 %collective-permute-start.7 = (bf16[1,32,1408]{2,1,0:T(8,128)(2,1)S(1)}, bf16[1,32,1408]{2,1,0:T(8,128)(2,1)S(1)}, u32[]{:S(2)}, u32[]{:S(2)}) collective-permute-start(bf16[1,32,1408]{2,1,0:T(8,128)(2,1)S(1)} %get-tuple-element.41), channel_id=1, source_target_pairs={{0,8},{4,12},{8,0},{12,4},{1,9},{5,13},{9,1},{13,5},{2,10},{6,14},... | collective-permute-start | bytes 270344 | tf_op jit(solution)/shard_map/ppermute | solution.py:29
  7.2 6.3 %collective-permute-start.8 = (bf16[1,32,1408]{2,1,0:T(8,128)(2,1)S(1)}, bf16[1,32,1408]{2,1,0:T(8,128)(2,1)S(1)}, u32[]{:S(2)}, u32[]{:S(2)}) collective-permute-start(bf16[1,32,1408]{2,1,0:T(8,128)(2,1)S(1)} %get-tuple-element.42), channel_id=1, source_target_pairs={{0,12},{4,0},{8,4},{12,8},{1,13},{5,1},{9,5},{13,9},{2,14},{6,2},{... | collective-permute-start | bytes 270344 | tf_op jit(solution)/shard_map/ppermute | solution.py:29
  13.5 8.2 %collective-permute-start.10 = (bf16[3,1,32,1408]{3,2,1,0:T(8,128)(2,1)S(1)}, bf16[3,1,32,1408]{3,2,1,0:T(8,128)(2,1)S(1)}, u32[]{:S(2)}, u32[]{:S(2)}) collective-permute-start(bf16[3,1,32,1408]{3,2,1,0:T(8,128)(2,1)S(1)} %pad_maximum_fusion.refs_8_), channel_id=1, source_target_pairs={{0,2},{2,0},{1,3},{3,1},{4,6},{6,4},{5,7},{7,5},{8,10},{10,8},{9,1... | collective-permute-start | bytes 811016 | tf_op jit(solution)/shard_map/ppermute | solution.py:29
  15.0 24.1 %collective-permute-start.9 = (bf16[3,1,32,1408]{3,2,1,0:T(8,128)(2,1)S(1)}, bf16[3,1,32,1408]{3,2,1,0:T(8,128)(2,1)S(1)}, u32[]{:S(2)}, u32[]{:S(2)}) collective-permute-start(bf16[3,1,32,1408]{3,2,1,0:T(8,128)(2,1)S(1)} %pad_maximum_fusion.refs_8_), channel_id=1, source_target_pairs={{0,1},{1,0},{2,3},{3,2},{4,5},{5,4},{6,7},{7,6},{8,9},{9,8},{10,11... | collective-permute-start | bytes 811016 | tf_op jit(solution)/shard_map/ppermute | solution.py:29
  21.6 17.5 %collective-permute-start.11 = (bf16[3,1,32,1408]{3,2,1,0:T(8,128)(2,1)S(1)}, bf16[3,1,32,1408]{3,2,1,0:T(8,128)(2,1)S(1)}, u32[]{:S(2)}, u32[]{:S(2)}) collective-permute-start(bf16[3,1,32,1408]{3,2,1,0:T(8,128)(2,1)S(1)} %collective-permute-done.10.refs_10_), channel_id=1, source_target_pairs={{0,1},{1,0},{2,3},{3,2},{4,5},{5,4},{6,7},{7,6},{8,9},{9,8},{10,11... | collective-permute-start | bytes 811016 | tf_op jit(solution)/shard_map/ppermute | solution.py:29
  21.7 10.9 %collective-permute-start.4 = (bf16[1,32,1408]{2,1,0:T(8,128)(2,1)S(1)}, bf16[1,32,1408]{2,1,0:T(8,128)(2,1)S(1)}, u32[]{:S(2)}, u32[]{:S(2)}) collective-permute-start(bf16[1,32,1408]{2,1,0:T(8,128)(2,1)S(1)} %get-tuple-element.39.refs_4_), channel_id=1, source_target_pairs={{0,2},{2,0},{1,3},{3,1},{4,6},{6,4},{5,7},{7,5},{8,10},{10,8},{9,1... | collective-permute-start | bytes 270344 | tf_op jit(solution)/shard_map/ppermute | solution.py:29
  26.2 6.4 %collective-permute-start = (f32[3,4,1280]{2,1,0:T(4,128)S(1)}, f32[3,4,1280]{2,1,0:T(4,128)S(1)}, u32[]{:S(2)}, u32[]{:S(2)}) collective-permute-start(f32[3,4,1280]{2,1,0:T(4,128)S(1)} %get-tuple-element.36), channel_id=1, source_target_pairs={{0,4},{4,8},{8,12},{12,0},{1,5},{5,9},{9,13},{13,1},{2,6},{6,10},{... | collective-permute-start | bytes 184328 | tf_op jit(solution)/shard_map/ppermute | solution.py:29
  28.7 6.1 %collective-permute-start.1 = (f32[3,4,1280]{2,1,0:T(4,128)S(1)}, f32[3,4,1280]{2,1,0:T(4,128)S(1)}, u32[]{:S(2)}, u32[]{:S(2)}) collective-permute-start(f32[3,4,1280]{2,1,0:T(4,128)S(1)} %get-tuple-element.37), channel_id=1, source_target_pairs={{0,8},{4,12},{8,0},{12,4},{1,9},{5,13},{9,1},{13,5},{2,10},{6,14},... | collective-permute-start | bytes 184328 | tf_op jit(solution)/shard_map/ppermute | solution.py:29
  32.5 6.6 %collective-permute-start.3 = (bf16[1,32,1408]{2,1,0:T(8,128)(2,1)S(1)}, bf16[1,32,1408]{2,1,0:T(8,128)(2,1)S(1)}, u32[]{:S(2)}, u32[]{:S(2)}) collective-permute-start(bf16[1,32,1408]{2,1,0:T(8,128)(2,1)S(1)} %get-tuple-element.39.refs_4_), channel_id=1, source_target_pairs={{0,1},{1,0},{2,3},{3,2},{4,5},{5,4},{6,7},{7,6},{8,9},{9,8},{10,11... | collective-permute-start | bytes 270344 | tf_op jit(solution)/shard_map/ppermute | solution.py:29
  32.6 6.5 %collective-permute-start.5 = (bf16[1,32,1408]{2,1,0:T(8,128)(2,1)S(1)}, bf16[1,32,1408]{2,1,0:T(8,128)(2,1)S(1)}, u32[]{:S(2)}, u32[]{:S(2)}) collective-permute-start(bf16[1,32,1408]{2,1,0:T(8,128)(2,1)S(1)} %collective-permute-done.4.refs_6_), channel_id=1, source_target_pairs={{0,1},{1,0},{2,3},{3,2},{4,5},{5,4},{6,7},{7,6},{8,9},{9,8},{10,11... | collective-permute-start | bytes 270344 | tf_op jit(solution)/shard_map/ppermute | solution.py:29
  34.9 4.2 %collective-permute-start.2 = (f32[3,4,1280]{2,1,0:T(4,128)S(1)}, f32[3,4,1280]{2,1,0:T(4,128)S(1)}, u32[]{:S(2)}, u32[]{:S(2)}) collective-permute-start(f32[3,4,1280]{2,1,0:T(4,128)S(1)} %get-tuple-element.38), channel_id=1, source_target_pairs={{0,12},{4,0},{8,4},{12,8},{1,13},{5,1},{9,5},{13,9},{2,14},{6,2},{... | collective-permute-start | bytes 184328 | tf_op jit(solution)/shard_map/ppermute | solution.py:29
  44.7 10.2 %collective-permute-start.25 = (f16[3,128,384]{2,1,0:T(8,128)(2,1)}, f16[3,128,384]{2,1,0:T(8,128)(2,1)}, u32[]{:S(2)}, u32[]{:S(2)}) collective-permute-start(f16[3,128,384]{2,1,0:T(8,128)(2,1)} %select_convert_fusion.4), channel_id=1, source_target_pairs={{0,4},{4,0},{8,12},{12,8},{1,5},{5,1},{9,13},{13,9},{2,6},{6,2},{1... | collective-permute-start | bytes 884744 | tf_op jit(solution)/shard_map/ppermute | solution.py:481
  48.1 13.0 %collective-permute-start.12 = (f16[3,128,384]{2,1,0:T(8,128)(2,1)}, f16[3,128,384]{2,1,0:T(8,128)(2,1)S(1)}, u32[]{:S(2)}, u32[]{:S(2)}) collective-permute-start(f16[3,128,384]{2,1,0:T(8,128)(2,1)} %select_convert_fusion.9), channel_id=1, source_target_pairs={{0,4},{4,0},{8,12},{12,8},{1,5},{5,1},{9,13},{13,9},{2,6},{6,2},{1... | collective-permute-start | bytes 884744 | tf_op jit(solution)/shard_map/ppermute | solution.py:481
  50.2 25.5 %collective-permute-start.38 = (bf16[640,768]{1,0:T(8,128)(2,1)S(1)}, bf16[640,768]{1,0:T(8,128)(2,1)S(1)}, u32[]{:S(2)}, u32[]{:S(2)}) collective-permute-start(bf16[640,768]{1,0:T(8,128)(2,1)S(1)} %get-tuple-element.59), channel_id=1, source_target_pairs={{0,1},{1,0},{2,3},{3,2},{4,5},{5,4},{6,7},{7,6},{8,9},{9,8},{10,11... | collective-permute-start | bytes 2949128 | tf_op jit(solution)/shard_map/ppermute | solution.py:29
  56.3 11.1 %collective-permute-start.26 = (f16[3,128,384]{2,1,0:T(8,128)(2,1)S(1)}, f16[3,128,384]{2,1,0:T(8,128)(2,1)S(1)}, u32[]{:S(2)}, u32[]{:S(2)}) collective-permute-start(f16[3,128,384]{2,1,0:T(8,128)(2,1)S(1)} %get-tuple-element.70), channel_id=1, source_target_pairs={{0,4},{4,0},{8,12},{12,8},{1,5},{5,1},{9,13},{13,9},{2,6},{6,2},{1... | collective-permute-start | bytes 884744 | tf_op jit(solution)/shard_map/ppermute | solution.py:481
  56.4 11.6 %collective-permute-start.27 = (f16[3,128,384]{2,1,0:T(8,128)(2,1)S(1)}, f16[3,128,384]{2,1,0:T(8,128)(2,1)S(1)}, u32[]{:S(2)}, u32[]{:S(2)}) collective-permute-start(f16[3,128,384]{2,1,0:T(8,128)(2,1)S(1)} %get-tuple-element.69), channel_id=1, source_target_pairs={{0,1},{1,0},{4,8},{5,9},{8,4},{9,5},{12,13},{13,12},{2,3},{3,2},{6... | collective-permute-start | bytes 884744 | tf_op jit(solution)/shard_map/ppermute | solution.py:483
  62.4 11.3 %collective-permute-start.13 = (f16[3,128,384]{2,1,0:T(8,128)(2,1)S(1)}, f16[3,128,384]{2,1,0:T(8,128)(2,1)S(1)}, u32[]{:S(2)}, u32[]{:S(2)}) collective-permute-start(f16[3,128,384]{2,1,0:T(8,128)(2,1)S(1)} %get-tuple-element.72), channel_id=1, source_target_pairs={{0,4},{4,0},{8,12},{12,8},{1,5},{5,1},{9,13},{13,9},{2,6},{6,2},{1... | collective-permute-start | bytes 884744 | tf_op jit(solution)/shard_map/ppermute | solution.py:481
  62.5 11.3 %collective-permute-start.14 = (f16[3,128,384]{2,1,0:T(8,128)(2,1)S(1)}, f16[3,128,384]{2,1,0:T(8,128)(2,1)S(1)}, u32[]{:S(2)}, u32[]{:S(2)}) collective-permute-start(f16[3,128,384]{2,1,0:T(8,128)(2,1)S(1)} %get-tuple-element.71), channel_id=1, source_target_pairs={{0,1},{1,0},{4,8},{5,9},{8,4},{9,5},{12,13},{13,12},{2,3},{3,2},{6... | collective-permute-start | bytes 884744 | tf_op jit(solution)/shard_map/ppermute | solution.py:483
  67.5 46.2 %collective-permute-start.39 = (bf16[640,768]{1,0:T(8,128)(2,1)S(1)}, bf16[640,768]{1,0:T(8,128)(2,1)S(1)}, u32[]{:S(2)}, u32[]{:S(2)}) collective-permute-start(bf16[640,768]{1,0:T(8,128)(2,1)S(1)} %get-tuple-element.58.refs_16_), channel_id=1, source_target_pairs={{0,2},{2,0},{1,3},{3,1},{4,6},{6,4},{5,7},{7,5},{8,10},{10,8},{9,1... | collective-permute-start | bytes 2949128 | tf_op jit(solution)/shard_map/ppermute | solution.py:29
  69.5 9.3 %collective-permute-start.28 = (f16[3,128,384]{2,1,0:T(8,128)(2,1)S(1)}, f16[3,128,384]{2,1,0:T(8,128)(2,1)S(1)}, u32[]{:S(2)}, u32[]{:S(2)}) collective-permute-start(f16[3,128,384]{2,1,0:T(8,128)(2,1)S(1)} %get-tuple-element.66), channel_id=1, source_target_pairs={{0,4},{4,0},{8,12},{12,8},{1,5},{5,1},{9,13},{13,9},{2,6},{6,2},{1... | collective-permute-start | bytes 884744 | tf_op jit(solution)/shard_map/ppermute | solution.py:481
  73.8 5.5 %collective-permute-start.29 = (f16[3,128,384]{2,1,0:T(8,128)(2,1)S(1)}, f16[3,128,384]{2,1,0:T(8,128)(2,1)S(1)}, u32[]{:S(2)}, u32[]{:S(2)}) collective-permute-start(f16[3,128,384]{2,1,0:T(8,128)(2,1)S(1)} %get-tuple-element.65), channel_id=1, source_target_pairs={{0,1},{1,0},{4,8},{5,9},{8,4},{9,5},{12,13},{13,12},{2,3},{3,2},{6... | collective-permute-start | bytes 884744 | tf_op jit(solution)/shard_map/ppermute | solution.py:483
  74.0 10.3 %collective-permute-start.15 = (f16[3,128,384]{2,1,0:T(8,128)(2,1)S(1)}, f16[3,128,384]{2,1,0:T(8,128)(2,1)S(1)}, u32[]{:S(2)}, u32[]{:S(2)}) collective-permute-start(f16[3,128,384]{2,1,0:T(8,128)(2,1)S(1)} %get-tuple-element.68), channel_id=1, source_target_pairs={{0,4},{4,0},{8,12},{12,8},{1,5},{5,1},{9,13},{13,9},{2,6},{6,2},{1... | collective-permute-start | bytes 884744 | tf_op jit(solution)/shard_map/ppermute | solution.py:481
  75.7 8.6 %collective-permute-start.16 = (f16[3,128,384]{2,1,0:T(8,128)(2,1)S(1)}, f16[3,128,384]{2,1,0:T(8,128)(2,1)S(1)}, u32[]{:S(2)}, u32[]{:S(2)}) collective-permute-start(f16[3,128,384]{2,1,0:T(8,128)(2,1)S(1)} %get-tuple-element.67), channel_id=1, source_target_pairs={{0,1},{1,0},{4,8},{5,9},{8,4},{9,5},{12,13},{13,12},{2,3},{3,2},{6... | collective-permute-start | bytes 884744 | tf_op jit(solution)/shard_map/ppermute | solution.py:483
  78.8 49.9 %collective-permute-start.40 = (bf16[640,768]{1,0:T(8,128)(2,1)S(1)}, bf16[640,768]{1,0:T(8,128)(2,1)S(1)}, u32[]{:S(2)}, u32[]{:S(2)}) collective-permute-start(bf16[640,768]{1,0:T(8,128)(2,1)S(1)} %collective-permute-done.38.refs_17_), channel_id=1, source_target_pairs={{0,2},{2,0},{1,3},{3,1},{4,6},{6,4},{5,7},{7,5},{8,10},{10,8},{9,1... | collective-permute-start | bytes 2949128 | tf_op jit(solution)/shard_map/ppermute | solution.py:29
  81.5 28.2 %collective-permute-start.30 = (bf16[1,64,384]{2,1,0:T(8,128)(2,1)S(1)}, bf16[1,64,384]{2,1,0:T(8,128)(2,1)S(1)}, u32[]{:S(2)}, u32[]{:S(2)}) collective-permute-start(bf16[1,64,384]{2,1,0:T(8,128)(2,1)S(1)} %get-tuple-element.57), channel_id=1, source_target_pairs={{0,2},{2,0},{1,3},{3,1},{4,6},{6,4},{5,7},{7,5},{8,10},{10,8},{9,1... | collective-permute-start | bytes 147464 | tf_op jit(solution)/shard_map/ppermute | solution.py:29
  85.4 27.5 %collective-permute-start.17 = (bf16[1,64,384]{2,1,0:T(8,128)(2,1)S(1)}, bf16[1,64,384]{2,1,0:T(8,128)(2,1)S(1)}, u32[]{:S(2)}, u32[]{:S(2)}) collective-permute-start(bf16[1,64,384]{2,1,0:T(8,128)(2,1)S(1)} %get-tuple-element.51), channel_id=1, source_target_pairs={{0,2},{2,0},{1,3},{3,1},{4,6},{6,4},{5,7},{7,5},{8,10},{10,8},{9,1... | collective-permute-start | bytes 147464 | tf_op jit(solution)/shard_map/ppermute | solution.py:29
  109.7 6.6 %collective-permute-start.32 = (bf16[2,1,64,384]{3,2,1,0:T(8,128)(2,1)S(1)}, bf16[2,1,64,384]{3,2,1,0:T(8,128)(2,1)S(1)}, u32[]{:S(2)}, u32[]{:S(2)}) collective-permute-start(bf16[2,1,64,384]{3,2,1,0:T(8,128)(2,1)S(1)} %pad_maximum_fusion.2.refs_8_), channel_id=1, source_target_pairs={{0,4},{4,8},{8,12},{12,0},{1,5},{5,9},{9,13},{13,1},{2,6},{6,10},{... | collective-permute-start | bytes 294920 | tf_op jit(solution)/shard_map/ppermute | solution.py:29
  110.3 7.7 %collective-permute-start.34 = (bf16[2,1,64,384]{3,2,1,0:T(8,128)(2,1)S(1)}, bf16[2,1,64,384]{3,2,1,0:T(8,128)(2,1)S(1)}, u32[]{:S(2)}, u32[]{:S(2)}) collective-permute-start(bf16[2,1,64,384]{3,2,1,0:T(8,128)(2,1)S(1)} %pad_maximum_fusion.2.refs_8_), channel_id=1, source_target_pairs={{0,8},{4,12},{8,0},{12,4},{1,9},{5,13},{9,1},{13,5},{2,10},{6,14},... | collective-permute-start | bytes 294920 | tf_op jit(solution)/shard_map/ppermute | solution.py:29
  113.0 5.6 %collective-permute-start.36 = (bf16[2,1,64,384]{3,2,1,0:T(8,128)(2,1)S(1)}, bf16[2,1,64,384]{3,2,1,0:T(8,128)(2,1)S(1)}, u32[]{:S(2)}, u32[]{:S(2)}) collective-permute-start(bf16[2,1,64,384]{3,2,1,0:T(8,128)(2,1)S(1)} %pad_maximum_fusion.2.refs_8_), channel_id=1, source_target_pairs={{0,12},{4,0},{8,4},{12,8},{1,13},{5,1},{9,5},{13,9},{2,14},{6,2},{... | collective-permute-start | bytes 294920 | tf_op jit(solution)/shard_map/ppermute | solution.py:29
  113.6 8.6 %collective-permute-start.31 = (bf16[2,1,64,384]{3,2,1,0:T(8,128)(2,1)S(1)}, bf16[2,1,64,384]{3,2,1,0:T(8,128)(2,1)S(1)}, u32[]{:S(2)}, u32[]{:S(2)}) collective-permute-start(bf16[2,1,64,384]{3,2,1,0:T(8,128)(2,1)S(1)} %pad_maximum_fusion.2.refs_8_), channel_id=1, source_target_pairs={{0,1},{1,0},{2,3},{3,2},{4,5},{5,4},{6,7},{7,6},{8,9},{9,8},{10,11... | collective-permute-start | bytes 294920 | tf_op jit(solution)/shard_map/ppermute | solution.py:29
  116.3 6.7 %collective-permute-start.19 = (bf16[2,1,64,384]{3,2,1,0:T(8,128)(2,1)S(1)}, bf16[2,1,64,384]{3,2,1,0:T(8,128)(2,1)S(1)}, u32[]{:S(2)}, u32[]{:S(2)}) collective-permute-start(bf16[2,1,64,384]{3,2,1,0:T(8,128)(2,1)S(1)} %pad_maximum_fusion.1.refs_0_), channel_id=1, source_target_pairs={{0,4},{4,8},{8,12},{12,0},{1,5},{5,9},{9,13},{13,1},{2,6},{6,10},{... | collective-permute-start | bytes 294920 | tf_op jit(solution)/shard_map/ppermute | solution.py:29
  118.0 8.1 %collective-permute-start.21 = (bf16[2,1,64,384]{3,2,1,0:T(8,128)(2,1)S(1)}, bf16[2,1,64,384]{3,2,1,0:T(8,128)(2,1)S(1)}, u32[]{:S(2)}, u32[]{:S(2)}) collective-permute-start(bf16[2,1,64,384]{3,2,1,0:T(8,128)(2,1)S(1)} %pad_maximum_fusion.1.refs_0_), channel_id=1, source_target_pairs={{0,8},{4,12},{8,0},{12,4},{1,9},{5,13},{9,1},{13,5},{2,10},{6,14},... | collective-permute-start | bytes 294920 | tf_op jit(solution)/shard_map/ppermute | solution.py:29
  118.6 7.5 %collective-permute-start.23 = (bf16[2,1,64,384]{3,2,1,0:T(8,128)(2,1)S(1)}, bf16[2,1,64,384]{3,2,1,0:T(8,128)(2,1)S(1)}, u32[]{:S(2)}, u32[]{:S(2)}) collective-permute-start(bf16[2,1,64,384]{3,2,1,0:T(8,128)(2,1)S(1)} %pad_maximum_fusion.1.refs_0_), channel_id=1, source_target_pairs={{0,12},{4,0},{8,4},{12,8},{1,13},{5,1},{9,5},{13,9},{2,14},{6,2},{... | collective-permute-start | bytes 294920 | tf_op jit(solution)/shard_map/ppermute | solution.py:29
  122.2 4.4 %collective-permute-start.18 = (bf16[2,1,64,384]{3,2,1,0:T(8,128)(2,1)S(1)}, bf16[2,1,64,384]{3,2,1,0:T(8,128)(2,1)S(1)}, u32[]{:S(2)}, u32[]{:S(2)}) collective-permute-start(bf16[2,1,64,384]{3,2,1,0:T(8,128)(2,1)S(1)} %pad_maximum_fusion.1.refs_0_), channel_id=1, source_target_pairs={{0,1},{1,0},{2,3},{3,2},{4,5},{5,4},{6,7},{7,6},{8,9},{9,8},{10,11... | collective-permute-start | bytes 294920 | tf_op jit(solution)/shard_map/ppermute | solution.py:29
  122.9 3.7 %collective-permute-start.33 = (bf16[2,1,64,384]{3,2,1,0:T(8,128)(2,1)S(1)}, bf16[2,1,64,384]{3,2,1,0:T(8,128)(2,1)S(1)}, u32[]{:S(2)}, u32[]{:S(2)}) collective-permute-start(bf16[2,1,64,384]{3,2,1,0:T(8,128)(2,1)S(1)} %collective-permute-done.32.refs_10_), channel_id=1, source_target_pairs={{0,1},{1,0},{2,3},{3,2},{4,5},{5,4},{6,7},{7,6},{8,9},{9,8},{10,11... | collective-permute-start | bytes 294920 | tf_op jit(solution)/shard_map/ppermute | solution.py:29
  126.1 1.3 collective-permute-start.35
  126.1 1.5 %collective-permute-start.37 = (bf16[2,1,64,384]{3,2,1,0:T(8,128)(2,1)S(1)}, bf16[2,1,64,384]{3,2,1,0:T(8,128)(2,1)S(1)}, u32[]{:S(2)}, u32[]{:S(2)}) collective-permute-start(bf16[2,1,64,384]{3,2,1,0:T(8,128)(2,1)S(1)} %collective-permute-done.36.refs_14_), channel_id=1, source_target_pairs={{0,1},{1,0},{2,3},{3,2},{4,5},{5,4},{6,7},{7,6},{8,9},{9,8},{10,11... | collective-permute-start | bytes 294920 | tf_op jit(solution)/shard_map/ppermute | solution.py:29
  126.6 1.3 collective-permute-start.20
  126.7 1.4 collective-permute-start.22
  127.4 1.3 collective-permute-start.24
  130.2 6.4 %collective-permute-start.42 = (bf16[1,64,640]{2,1,0:T(8,128)(2,1)S(1)}, bf16[1,64,640]{2,1,0:T(8,128)(2,1)S(1)}, u32[]{:S(2)}, u32[]{:S(2)}) collective-permute-start(bf16[1,64,640]{2,1,0:T(8,128)(2,1)S(1)} %get-tuple-element.62), channel_id=1, source_target_pairs={{0,12},{4,0},{8,4},{12,8},{1,13},{5,1},{9,5},{13,9},{2,14},{6,2},{... | collective-permute-start | bytes 245768 | tf_op jit(solution)/shard_map/ppermute | solution.py:29
  133.8 8.0 %collective-permute-start.44 = (bf16[1,64,640]{2,1,0:T(8,128)(2,1)S(1)}, bf16[1,64,640]{2,1,0:T(8,128)(2,1)S(1)}, u32[]{:S(2)}, u32[]{:S(2)}) collective-permute-start(bf16[1,64,640]{2,1,0:T(8,128)(2,1)S(1)} %get-tuple-element.63), channel_id=1, source_target_pairs={{0,8},{4,12},{8,0},{12,4},{1,9},{5,13},{9,1},{13,5},{2,10},{6,14},... | collective-permute-start | bytes 245768 | tf_op jit(solution)/shard_map/ppermute | solution.py:29
  133.8 8.0 %collective-permute-start.46 = (bf16[1,64,640]{2,1,0:T(8,128)(2,1)S(1)}, bf16[1,64,640]{2,1,0:T(8,128)(2,1)S(1)}, u32[]{:S(2)}, u32[]{:S(2)}) collective-permute-start(bf16[1,64,640]{2,1,0:T(8,128)(2,1)S(1)} %get-tuple-element.64), channel_id=1, source_target_pairs={{0,4},{4,8},{8,12},{12,0},{1,5},{5,9},{9,13},{13,1},{2,6},{6,10},{... | collective-permute-start | bytes 245768 | tf_op jit(solution)/shard_map/ppermute | solution.py:29
  134.5 7.9 %collective-permute-start.41 = (bf16[1,64,640]{2,1,0:T(8,128)(2,1)S(1)}, bf16[1,64,640]{2,1,0:T(8,128)(2,1)S(1)}, u32[]{:S(2)}, u32[]{:S(2)}) collective-permute-start(bf16[1,64,640]{2,1,0:T(8,128)(2,1)S(1)} %get-tuple-element.61), channel_id=1, source_target_pairs={{0,1},{1,0},{2,3},{3,2},{4,5},{5,4},{6,7},{7,6},{8,9},{9,8},{10,11... | collective-permute-start | bytes 245768 | tf_op jit(solution)/shard_map/ppermute | solution.py:29
  136.7 5.7 %collective-permute-start.43 = (bf16[1,64,640]{2,1,0:T(8,128)(2,1)S(1)}, bf16[1,64,640]{2,1,0:T(8,128)(2,1)S(1)}, u32[]{:S(2)}, u32[]{:S(2)}) collective-permute-start(bf16[1,64,640]{2,1,0:T(8,128)(2,1)S(1)} %collective-permute-done.42.refs_2_), channel_id=1, source_target_pairs={{0,1},{1,0},{2,3},{3,2},{4,5},{5,4},{6,7},{7,6},{8,9},{9,8},{10,11... | collective-permute-start | bytes 245768 | tf_op jit(solution)/shard_map/ppermute | solution.py:29
  141.8 1.3 collective-permute-start.45
  141.9 1.4 collective-permute-start.47
  (7 other events, 43.0 us)

commit v13 on v12

--- a/solution.py
+++ b/solution.py
@@ -12,7 +12,6 @@
 FREQ = 256
 STEPS = 100
 LANES = 128
-DMA_PIECES = 4
 
 
 sample_shift = 5.0
@@ -199,26 +198,16 @@
     )(weights)
 
 
-def modulate_kernel(n_tm, n_seq, n_mp, step_ref, w_ref, *refs):
+def modulate_kernel(n_tm, n_seq, n_mp, step_ref, *refs):
     sides = n_seq * n_mp
     shares, near, far = refs[:n_tm], refs[n_tm : n_tm + sides], refs[n_tm + sides :][:sides]
-    hidden_ref, coef_ref, w_out, mod_scr, sems = refs[n_tm + 2 * sides :]
-    stride = w_ref.shape[1] // DMA_PIECES
-    copies = []
-    for c in range(w_ref.shape[0]):
-        for piece in range(DMA_PIECES):
-            at = c, pl.ds(piece * stride, stride)
-            copies.append(
-                pltpu.make_async_copy(w_ref.at[at], w_out.at[at], sems.at[len(copies)])
-            )
+    hidden_ref, coef_ref, mod_scr = refs[n_tm + 2 * sides :]
     z, k = lax.axis_index("tm"), pl.program_id(0)
     frames, part, wide = near[0].shape
     depth = wide - LANES
 
     @pl.when(k == 0)
     def _():
-        for copy in copies:
-            copy.start()
         total = shares[0][...]
         for share in shares[1:]:
             total = total + share[...]
@@ -249,23 +238,17 @@
     def _():
         write([block.at[0] for block in far])
 
-    @pl.when(k == n_tm - 1)
-    def _():
-        for copy in copies:
-            copy.wait()
-
-
-def modulate(start_step, w_qkv, shares, near, far):
+
+def modulate(start_step, shares, near, far):
     n_tm, n_seq, n_mp = len(shares), len(near), len(near[0])
     frames, part, wide = near[0][0].shape
-    three = w_qkv.shape[0]
     depth = wide - LANES
     window = shares[0].shape[1]
     shape = (n_tm, n_seq, frames, n_mp * part, depth)
     return pl.pallas_call(
         functools.partial(modulate_kernel, n_tm, n_seq, n_mp),
         grid=(n_tm,),
-        in_specs=[pl.BlockSpec(memory_space=pltpu.SMEM), pl.BlockSpec(memory_space=pltpu.HBM)]
+        in_specs=[pl.BlockSpec(memory_space=pltpu.SMEM)]
         + [pl.BlockSpec((3, window, depth), lambda k: (0, 0, 0))] * n_tm
         + [pl.BlockSpec((frames, part, wide), lambda k: (0, 0, 0))] * (n_seq * n_mp)
         + [pl.BlockSpec((1, frames, part, wide), lambda k: (jnp.maximum(k - 1, 0), 0, 0, 0))]
@@ -273,25 +256,22 @@
         out_specs=[
             pl.BlockSpec((1,) + shape[1:], lambda k: (k, 0, 0, 0, 0)),
             pl.BlockSpec((1, frames, depth), lambda k: (k, 0, 0)),
-        ]
-        + [pl.BlockSpec(memory_space=pl.ANY)],
+        ],
         scratch_shapes=[
             pltpu.VMEM((3, window, depth), jnp.float32),
-            pltpu.SemaphoreType.DMA((three * DMA_PIECES,)),
         ],
         out_shape=[
             jax.ShapeDtypeStruct(shape, jnp.bfloat16),
             jax.ShapeDtypeStruct((n_tm, frames, depth), jnp.float32),
-        ]
-        + [jax.ShapeDtypeStruct(w_qkv.shape, w_qkv.dtype)],
+        ],
         cost_estimate=pl.CostEstimate(
             flops=4 * n_tm * n_seq * frames * n_mp * part * depth,
             bytes_accessed=4 * n_tm * n_seq * frames * n_mp * part * depth,
             transcendentals=0,
         ),
-        compiler_params=pltpu.CompilerParams(vmem_limit_bytes=42 << 20),
+        compiler_params=pltpu.CompilerParams(vmem_limit_bytes=24 << 20),
         name="modulate",
-    )(start_step, w_qkv, *shares, *[r for rows in (near, far) for side in rows for r in side])
+    )(start_step, *shares, *[r for rows in (near, far) for side in rows for r in side])
 
 
 def project_kernel(dims, widths, coef_ref, *refs):
@@ -442,7 +422,7 @@
             weights[j].append(turn(share, "seq", -j))
 
     groups = head_groups(cols)
-    hidden, coef, held_qkv = modulate(start_step, w_qkv, shares, near, far)
+    hidden, coef = modulate(start_step, shares, near, far)
     hidden = hidden.reshape(n_tm, n_seq * frames * tok, depth)
     proj = []
     for lane, size in groups:
@@ -450,7 +430,7 @@
             jnp.einsum(
                 "krd,cdh->kcrh",
                 hidden,
-                held_qkv[:, :, lane : lane + size],
+                w_qkv[:, :, lane : lane + size],
                 preferred_element_type=jnp.float32,
             )
         )

time: 145 us -> 146 us (level)
  matrix products: 3.74 us -> 5.72 us
  Pallas kernels: 9.14 us -> 7.47 us
    dot_general x2, matrix products: 3.74 us -> 5.72 us  [sweep(): jnp.einsum('krd,cdh->kcrh', hidden, w_qkv[:, :, lane:lane + size], prefer...]
    pallas_call x1, Pallas kernels: 2.84 us -> 1.18 us  [modulate(): pl.pallas_call(functools.partial(modulate_kernel, n_tm, n_seq, n_mp), gri...]
    unnamed x14 -> x18, local copies, waits for them, and re-layouts: 3.26 us -> 3.27 us
where the time goes in v13:
time: 146 us; the launch traced here: 145 us
  waiting for transfers between devices  84.1 us (58%)
  starting transfers between devices  36.1 us (25%)
  other arithmetic  7.7 us (5%)
  Pallas kernels  7.47 us (5%)
  matrix products  5.72 us (4%)
  local copies, waits for them, and re-layouts  3.28 us (2%)
    ppermute x38, waiting for transfers between devices, turn(): lax.ppermute(block, axis, [(i, (i + distance) % size) for i in range(size)])  61.5 us
    ppermute x38, starting transfers between devices, turn(): lax.ppermute(block, axis, [(i, (i + distance) % size) for i in range(size)])  32 us
    ppermute x6, waiting for transfers between devices, sweep(): first = lax.ppermute(first, 'tm', ev)  22.5 us
    dot_general x2, matrix products, sweep(): jnp.einsum('krd,cdh->kcrh', hidden, w_qkv[:, :, lane:lane + size], prefer...  5.72 us
    convert_element_type x4, other arithmetic, sweep(): second = jnp.where(even, left, right).astype(jnp.float16)  4.52 us
    ppermute x6, starting transfers between devices, sweep(): first = lax.ppermute(first, 'tm', ev)  3.96 us
    unnamed x18, local copies, waits for them, and re-layouts  3.27 us
  transfers between devices with their start and end apart: 48, of which 26 were waited for; matrix products, arithmetic and copies ran while one was open for 6% of the time, Pallas kernels for 2%

profile of v13, /device:TPU:0, one launch (start us, length us, event | category | flops | bytes accessed | tf_op | source)
XLA Modules:
  0.0 145.3 jit_solution(14523563098880028615)
XLA Ops:
  0.0 1.1 copy-done.2
  1.5 3.1 %collective-permute-start.6 = (bf16[1,32,1408]{2,1,0:T(8,128)(2,1)S(1)}, bf16[1,32,1408]{2,1,0:T(8,128)(2,1)S(1)}, u32[]{:S(2)}, u32[]{:S(2)}) collective-permute-start(bf16[1,32,1408]{2,1,0:T(8,128)(2,1)S(1)} %get-tuple-element.39), channel_id=1, source_target_pairs={{0,4},{4,8},{8,12},{12,0},{1,5},{5,9},{9,13},{13,1},{2,6},{6,10},{... | collective-permute-start | bytes 270344 | tf_op jit(solution)/shard_map/ppermute | solution.py:28
  4.6 2.6 %collective-permute-start.7 = (bf16[1,32,1408]{2,1,0:T(8,128)(2,1)S(1)}, bf16[1,32,1408]{2,1,0:T(8,128)(2,1)S(1)}, u32[]{:S(2)}, u32[]{:S(2)}) collective-permute-start(bf16[1,32,1408]{2,1,0:T(8,128)(2,1)S(1)} %get-tuple-element.40), channel_id=1, source_target_pairs={{0,8},{4,12},{8,0},{12,4},{1,9},{5,13},{9,1},{13,5},{2,10},{6,14},... | collective-permute-start | bytes 270344 | tf_op jit(solution)/shard_map/ppermute | solution.py:28
  7.2 1.4 collective-permute-start.8
  8.5 1.4 collective-permute-done.6
  9.9 3.3 %collective-permute-done.7 = bf16[1,32,1408]{2,1,0:T(8,128)(2,1)S(1)} collective-permute-done((bf16[1,32,1408]{2,1,0:T(8,128)(2,1)S(1)}, bf16[1,32,1408]{2,1,0:T(8,128)(2,1)S(1)}, u32[]{:S(2)}, u32[]{:S(2)}) %collective-permute-start.7) | collective-permute-done | bytes 90144 | tf_op jit(solution)/shard_map/ppermute | solution.py:28
  13.5 1.6 %collective-permute-start.10 = (bf16[3,1,32,1408]{3,2,1,0:T(8,128)(2,1)S(1)}, bf16[3,1,32,1408]{3,2,1,0:T(8,128)(2,1)S(1)}, u32[]{:S(2)}, u32[]{:S(2)}) collective-permute-start(bf16[3,1,32,1408]{3,2,1,0:T(8,128)(2,1)S(1)} %pad_maximum_fusion.refs_8_), channel_id=1, source_target_pairs={{0,2},{2,0},{1,3},{3,1},{4,6},{6,4},{5,7},{7,5},{8,10},{10,8},{9,1... | collective-permute-start | bytes 811016 | tf_op jit(solution)/shard_map/ppermute | solution.py:28
  15.0 6.6 %collective-permute-done.10.refs_10_ = bf16[3,1,32,1408]{3,2,1,0:T(8,128)(2,1)S(1)} collective-permute-done((bf16[3,1,32,1408]{3,2,1,0:T(8,128)(2,1)S(1)}, bf16[3,1,32,1408]{3,2,1,0:T(8,128)(2,1)S(1)}, u32[]{:S(2)}, u32[]{:S(2)}) %collective-permute-start.10) | collective-permute-done | bytes 270368 | tf_op jit(solution)/shard_map/ppermute | solution.py:28
  21.7 1.5 %collective-permute-start.4 = (bf16[1,32,1408]{2,1,0:T(8,128)(2,1)S(1)}, bf16[1,32,1408]{2,1,0:T(8,128)(2,1)S(1)}, u32[]{:S(2)}, u32[]{:S(2)}) collective-permute-start(bf16[1,32,1408]{2,1,0:T(8,128)(2,1)S(1)} %get-tuple-element.38.refs_4_), channel_id=1, source_target_pairs={{0,2},{2,0},{1,3},{3,1},{4,6},{6,4},{5,7},{7,5},{8,10},{10,8},{9,1... | collective-permute-start | bytes 270344 | tf_op jit(solution)/shard_map/ppermute | solution.py:28
  23.8 1.5 %copy-done = bf16[64,15360]{1,0:T(8,128)(2,1)S(1)} copy-done((bf16[64,15360]{1,0:T(8,128)(2,1)S(1)}, bf16[64,15360]{1,0:T(8,128)(2,1)}, u32[]{:S(2)}) %copy-start) | copy-done | bytes 1966104
  25.3 0.8 time_shares.1
  26.2 2.6 %collective-permute-start = (f32[3,4,1280]{2,1,0:T(4,128)S(1)}, f32[3,4,1280]{2,1,0:T(4,128)S(1)}, u32[]{:S(2)}, u32[]{:S(2)}) collective-permute-start(f32[3,4,1280]{2,1,0:T(4,128)S(1)} %get-tuple-element.35), channel_id=1, source_target_pairs={{0,4},{4,8},{8,12},{12,0},{1,5},{5,9},{9,13},{13,1},{2,6},{6,10},{... | collective-permute-start | bytes 184328 | tf_op jit(solution)/shard_map/ppermute | solution.py:28
  29.2 3.3 %collective-permute-done.refs_1_ = f32[3,4,1280]{2,1,0:T(4,128)S(1)} collective-permute-done((f32[3,4,1280]{2,1,0:T(4,128)S(1)}, f32[3,4,1280]{2,1,0:T(4,128)S(1)}, u32[]{:S(2)}, u32[]{:S(2)}) %collective-permute-start) | collective-permute-done | bytes 61472 | tf_op jit(solution)/shard_map/ppermute | solution.py:28
  33.1 1.8 %collective-permute-done.1.refs_2_ = f32[3,4,1280]{2,1,0:T(4,128)S(1)} collective-permute-done((f32[3,4,1280]{2,1,0:T(4,128)S(1)}, f32[3,4,1280]{2,1,0:T(4,128)S(1)}, u32[]{:S(2)}, u32[]{:S(2)}) %collective-permute-start.1) | collective-permute-done | bytes 61472 | tf_op jit(solution)/shard_map/ppermute | solution.py:28
  34.9 1.3 collective-permute-start.2
  36.2 2.9 %collective-permute-done.2.refs_3_ = f32[3,4,1280]{2,1,0:T(4,128)S(1)} collective-permute-done((f32[3,4,1280]{2,1,0:T(4,128)S(1)}, f32[3,4,1280]{2,1,0:T(4,128)S(1)}, u32[]{:S(2)}, u32[]{:S(2)}) %collective-permute-start.2) | collective-permute-done | bytes 61472 | tf_op jit(solution)/shard_map/ppermute | solution.py:28
  39.1 1.2 modulate.1
  40.3 3.9 %fusion.9 = f32[4,3,128,384]{3,2,1,0:T(8,128)S(1)} fusion(bf16[4,128,1280,1]{2,1,3,0:T(8,128)(2,1)S(1)} %bitcast.110, bf16[3,1280,768]{2,1,0:T(8,128)(2,1)} %param.8), kind=kOutput, calls=%fused_computation.7 | convolution fusion | flops 1509949440 | bytes 6619136 | tf_op jit(solution)/shard_map/krd,cdh->kcrh/dot_general | solution.py:430
  44.2 0.8 select_convert_fusion.4
  45.7 1.9 %fusion.6 = f32[4,3,128,384]{3,2,1,0:T(8,128)S(1)} fusion(bf16[4,128,1280,1]{2,1,3,0:T(8,128)(2,1)S(1)} %bitcast.111, bf16[3,1280,768]{2,1,0:T(8,128)(2,1)S(1)} %bitcast.118), kind=kOutput, calls=%fused_computation.6 | convolution fusion | flops 1509949440 | bytes 6619136 | tf_op jit(solution)/shard_map/krd,cdh->kcrh/dot_general | solution.py:430
  47.6 0.9 select_convert_fusion.9
  48.4 2.0 %collective-permute-start.12 = (f16[3,128,384]{2,1,0:T(8,128)(2,1)}, f16[3,128,384]{2,1,0:T(8,128)(2,1)S(1)}, u32[]{:S(2)}, u32[]{:S(2)}) collective-permute-start(f16[3,128,384]{2,1,0:T(8,128)(2,1)} %select_convert_fusion.9), channel_id=1, source_target_pairs={{0,4},{4,0},{8,12},{12,8},{1,5},{5,1},{9,13},{13,9},{2,6},{6,2},{1... | collective-permute-start | bytes 884744 | tf_op jit(solution)/shard_map/ppermute | solution.py:461
  51.2 4.7 %collective-permute-done.25 = f16[3,128,384]{2,1,0:T(8,128)(2,1)} collective-permute-done((f16[3,128,384]{2,1,0:T(8,128)(2,1)}, f16[3,128,384]{2,1,0:T(8,128)(2,1)}, u32[]{:S(2)}, u32[]{:S(2)}) %collective-permute-start.25) | collective-permute-done | bytes 294944 | tf_op jit(solution)/shard_map/ppermute | solution.py:461
  55.9 1.4 select_convert_fusion.2
  57.4 4.7 %collective-permute-done.12 = f16[3,128,384]{2,1,0:T(8,128)(2,1)S(1)} collective-permute-done((f16[3,128,384]{2,1,0:T(8,128)(2,1)}, f16[3,128,384]{2,1,0:T(8,128)(2,1)S(1)}, u32[]{:S(2)}, u32[]{:S(2)}) %collective-permute-start.12) | collective-permute-done | bytes 294944 | tf_op jit(solution)/shard_map/ppermute | solution.py:461
  62.1 1.3 select_convert_fusion.7
  63.5 4.8 %collective-permute-done.26 = f16[3,128,384]{2,1,0:T(8,128)(2,1)S(1)} collective-permute-done((f16[3,128,384]{2,1,0:T(8,128)(2,1)S(1)}, f16[3,128,384]{2,1,0:T(8,128)(2,1)S(1)}, u32[]{:S(2)}, u32[]{:S(2)}) %collective-permute-start.26) | collective-permute-done | bytes 294944 | tf_op jit(solution)/shard_map/ppermute | solution.py:461
  68.9 1.5 %select_convert_fusion = (f16[3,128,384]{2,1,0:T(8,128)(2,1)S(1)}, f16[3,128,384]{2,1,0:T(8,128)(2,1)S(1)}) fusion(pred[]{:T(512)S(6)} %eq.5, f16[3,128,384]{2,1,0:T(8,128)(2,1)S(1)} %collective-permute-done.27, f16[3,128,384]{2,1,0:T(8,128)(2,1)S(1)} %collective-permute-done.26, pred[]{:T(512)S(6)} %lt.9, f32[4,3,128,384]{3,2,1,0:T(8,128)} %copy-done.5, ...), kind=kLoop, calls=%fused_computation.52 | loop fusion | flops 1769472 | bytes 2359299 | tf_op jit(solution)/shard_map/convert_element_type | solution.py:460
  70.5 4.2 %collective-permute-done.13 = f16[3,128,384]{2,1,0:T(8,128)(2,1)S(1)} collective-permute-done((f16[3,128,384]{2,1,0:T(8,128)(2,1)S(1)}, f16[3,128,384]{2,1,0:T(8,128)(2,1)S(1)}, u32[]{:S(2)}, u32[]{:S(2)}) %collective-permute-start.13) | collective-permute-done | bytes 294944 | tf_op jit(solution)/shard_map/ppermute | solution.py:461
  75.0 1.7 %collective-permute-start.15 = (f16[3,128,384]{2,1,0:T(8,128)(2,1)S(1)}, f16[3,128,384]{2,1,0:T(8,128)(2,1)S(1)}, u32[]{:S(2)}, u32[]{:S(2)}) collective-permute-start(f16[3,128,384]{2,1,0:T(8,128)(2,1)S(1)} %get-tuple-element.66), channel_id=1, source_target_pairs={{0,4},{4,0},{8,12},{12,8},{1,5},{5,1},{9,13},{13,9},{2,6},{6,2},{1... | collective-permute-start | bytes 884744 | tf_op jit(solution)/shard_map/ppermute | solution.py:461
  76.8 2.9 %collective-permute-done.28 = f16[3,128,384]{2,1,0:T(8,128)(2,1)S(1)} collective-permute-done((f16[3,128,384]{2,1,0:T(8,128)(2,1)S(1)}, f16[3,128,384]{2,1,0:T(8,128)(2,1)S(1)}, u32[]{:S(2)}, u32[]{:S(2)}) %collective-permute-start.28) | collective-permute-done | bytes 294944 | tf_op jit(solution)/shard_map/ppermute | solution.py:461
  80.2 1.2 fusion.34
  81.5 0.9 attend.3
  82.4 1.5 %collective-permute-start.30 = (bf16[1,64,384]{2,1,0:T(8,128)(2,1)S(1)}, bf16[1,64,384]{2,1,0:T(8,128)(2,1)S(1)}, u32[]{:S(2)}, u32[]{:S(2)}) collective-permute-start(bf16[1,64,384]{2,1,0:T(8,128)(2,1)S(1)} %get-tuple-element.55), channel_id=1, source_target_pairs={{0,2},{2,0},{1,3},{3,1},{4,6},{6,4},{5,7},{7,5},{8,10},{10,8},{9,1... | collective-permute-start | bytes 147464 | tf_op jit(solution)/shard_map/ppermute | solution.py:28
  84.0 1.3 collective-permute-done.15
  85.4 0.9 attend.2
  87.0 23.6 %collective-permute-done.30 = bf16[1,64,384]{2,1,0:T(8,128)(2,1)S(1)} collective-permute-done((bf16[1,64,384]{2,1,0:T(8,128)(2,1)S(1)}, bf16[1,64,384]{2,1,0:T(8,128)(2,1)S(1)}, u32[]{:S(2)}, u32[]{:S(2)}) %collective-permute-start.30) | collective-permute-done | bytes 49184 | tf_op jit(solution)/shard_map/ppermute | solution.py:28
  111.3 2.8 %collective-permute-start.34 = (bf16[2,1,64,384]{3,2,1,0:T(8,128)(2,1)S(1)}, bf16[2,1,64,384]{3,2,1,0:T(8,128)(2,1)S(1)}, u32[]{:S(2)}, u32[]{:S(2)}) collective-permute-start(bf16[2,1,64,384]{3,2,1,0:T(8,128)(2,1)S(1)} %pad_maximum_fusion.2.refs_8_), channel_id=1, source_target_pairs={{0,8},{4,12},{8,0},{12,4},{1,9},{5,13},{9,1},{13,5},{2,10},{6,14},... | collective-permute-start | bytes 294920 | tf_op jit(solution)/shard_map/ppermute | solution.py:28
  114.6 2.6 %collective-permute-done.32.refs_10_ = bf16[2,1,64,384]{3,2,1,0:T(8,128)(2,1)S(1)} collective-permute-done((bf16[2,1,64,384]{3,2,1,0:T(8,128)(2,1)S(1)}, bf16[2,1,64,384]{3,2,1,0:T(8,128)(2,1)S(1)}, u32[]{:S(2)}, u32[]{:S(2)}) %collective-permute-start.32) | collective-permute-done | bytes 98336 | tf_op jit(solution)/shard_map/ppermute | solution.py:28
  117.2 1.8 %collective-permute-done.34.refs_12_ = bf16[2,1,64,384]{3,2,1,0:T(8,128)(2,1)S(1)} collective-permute-done((bf16[2,1,64,384]{3,2,1,0:T(8,128)(2,1)S(1)}, bf16[2,1,64,384]{3,2,1,0:T(8,128)(2,1)S(1)}, u32[]{:S(2)}, u32[]{:S(2)}) %collective-permute-start.34) | collective-permute-done | bytes 98336 | tf_op jit(solution)/shard_map/ppermute | solution.py:28
  119.6 3.1 %collective-permute-start.23 = (bf16[2,1,64,384]{3,2,1,0:T(8,128)(2,1)S(1)}, bf16[2,1,64,384]{3,2,1,0:T(8,128)(2,1)S(1)}, u32[]{:S(2)}, u32[]{:S(2)}) collective-permute-start(bf16[2,1,64,384]{3,2,1,0:T(8,128)(2,1)S(1)} %pad_maximum_fusion.1.refs_0_), channel_id=1, source_target_pairs={{0,12},{4,0},{8,4},{12,8},{1,13},{5,1},{9,5},{13,9},{2,14},{6,2},{... | collective-permute-start | bytes 294920 | tf_op jit(solution)/shard_map/ppermute | solution.py:28
  122.8 1.1 collective-permute-done.19.refs_2_
  123.9 3.2 %collective-permute-done.21.refs_4_ = bf16[2,1,64,384]{3,2,1,0:T(8,128)(2,1)S(1)} collective-permute-done((bf16[2,1,64,384]{3,2,1,0:T(8,128)(2,1)S(1)}, bf16[2,1,64,384]{3,2,1,0:T(8,128)(2,1)S(1)}, u32[]{:S(2)}, u32[]{:S(2)}) %collective-permute-start.21) | collective-permute-done | bytes 98336 | tf_op jit(solution)/shard_map/ppermute | solution.py:28
  129.6 1.5 %project.1 = (f32[1,64,640]{2,1,0:T(8,128)S(1)}, bf16[1,64,640]{2,1,0:T(8,128)(2,1)S(1)}, bf16[1,64,640]{2,1,0:T(8,128)(2,1)S(1)}, bf16[1,64,640]{2,1,0:T(8,128)(2,1)S(1)}, bf16[1,64,640]{2,1,0:T(8,128)(2,1)S(1)}) custom-call(f32[4,1,1280]{2,1,0:T(1,128)S(1)} %get-tuple-element.42.coef_ref, bf16[2,1,64,384]{3,2,1,0:T(8,128)(2,1)S(1)} %pad_maximum_fusion.1.refs_0_, ...), custom_call_target="tpu_custom_call" | custom-call | flops 1006632960 | bytes 5505024 | tf_op jit(solution)/shard_map/project/pallas_call | solution.py:341
  131.2 3.6 %collective-permute-start.42 = (bf16[1,64,640]{2,1,0:T(8,128)(2,1)S(1)}, bf16[1,64,640]{2,1,0:T(8,128)(2,1)S(1)}, u32[]{:S(2)}, u32[]{:S(2)}) collective-permute-start(bf16[1,64,640]{2,1,0:T(8,128)(2,1)S(1)} %get-tuple-element.60), channel_id=1, source_target_pairs={{0,12},{4,0},{8,4},{12,8},{1,13},{5,1},{9,5},{13,9},{2,14},{6,2},{... | collective-permute-start | bytes 245768 | tf_op jit(solution)/shard_map/ppermute | solution.py:28
  135.4 2.2 %collective-permute-done.42.refs_2_ = bf16[1,64,640]{2,1,0:T(8,128)(2,1)S(1)} collective-permute-done((bf16[1,64,640]{2,1,0:T(8,128)(2,1)S(1)}, bf16[1,64,640]{2,1,0:T(8,128)(2,1)S(1)}, u32[]{:S(2)}, u32[]{:S(2)}) %collective-permute-start.42) | collective-permute-done | bytes 81952 | tf_op jit(solution)/shard_map/ppermute | solution.py:28
  137.7 5.1 %collective-permute-done.44.refs_4_ = bf16[1,64,640]{2,1,0:T(8,128)(2,1)S(1)} collective-permute-done((bf16[1,64,640]{2,1,0:T(8,128)(2,1)S(1)}, bf16[1,64,640]{2,1,0:T(8,128)(2,1)S(1)}, u32[]{:S(2)}, u32[]{:S(2)}) %collective-permute-start.44) | collective-permute-done | bytes 81952 | tf_op jit(solution)/shard_map/ppermute | solution.py:28
  144.2 1.0 finish.1
  (89 shorter events, 12.1 us)
Async XLA Ops:
  1.5 8.4 %collective-permute-start.6 = (bf16[1,32,1408]{2,1,0:T(8,128)(2,1)S(1)}, bf16[1,32,1408]{2,1,0:T(8,128)(2,1)S(1)}, u32[]{:S(2)}, u32[]{:S(2)}) collective-permute-start(bf16[1,32,1408]{2,1,0:T(8,128)(2,1)S(1)} %get-tuple-element.39), channel_id=1, source_target_pairs={{0,4},{4,8},{8,12},{12,0},{1,5},{5,9},{9,13},{13,1},{2,6},{6,10},{... | collective-permute-start | bytes 270344 | tf_op jit(solution)/shard_map/ppermute | solution.py:28
  4.6 8.6 %collective-permute-start.7 = (bf16[1,32,1408]{2,1,0:T(8,128)(2,1)S(1)}, bf16[1,32,1408]{2,1,0:T(8,128)(2,1)S(1)}, u32[]{:S(2)}, u32[]{:S(2)}) collective-permute-start(bf16[1,32,1408]{2,1,0:T(8,128)(2,1)S(1)} %get-tuple-element.40), channel_id=1, source_target_pairs={{0,8},{4,12},{8,0},{12,4},{1,9},{5,13},{9,1},{13,5},{2,10},{6,14},... | collective-permute-start | bytes 270344 | tf_op jit(solution)/shard_map/ppermute | solution.py:28
  7.2 6.3 %collective-permute-start.8 = (bf16[1,32,1408]{2,1,0:T(8,128)(2,1)S(1)}, bf16[1,32,1408]{2,1,0:T(8,128)(2,1)S(1)}, u32[]{:S(2)}, u32[]{:S(2)}) collective-permute-start(bf16[1,32,1408]{2,1,0:T(8,128)(2,1)S(1)} %get-tuple-element.41), channel_id=1, source_target_pairs={{0,12},{4,0},{8,4},{12,8},{1,13},{5,1},{9,5},{13,9},{2,14},{6,2},{... | collective-permute-start | bytes 270344 | tf_op jit(solution)/shard_map/ppermute | solution.py:28
  13.5 8.2 %collective-permute-start.10 = (bf16[3,1,32,1408]{3,2,1,0:T(8,128)(2,1)S(1)}, bf16[3,1,32,1408]{3,2,1,0:T(8,128)(2,1)S(1)}, u32[]{:S(2)}, u32[]{:S(2)}) collective-permute-start(bf16[3,1,32,1408]{3,2,1,0:T(8,128)(2,1)S(1)} %pad_maximum_fusion.refs_8_), channel_id=1, source_target_pairs={{0,2},{2,0},{1,3},{3,1},{4,6},{6,4},{5,7},{7,5},{8,10},{10,8},{9,1... | collective-permute-start | bytes 811016 | tf_op jit(solution)/shard_map/ppermute | solution.py:28
  15.0 24.1 %collective-permute-start.9 = (bf16[3,1,32,1408]{3,2,1,0:T(8,128)(2,1)S(1)}, bf16[3,1,32,1408]{3,2,1,0:T(8,128)(2,1)S(1)}, u32[]{:S(2)}, u32[]{:S(2)}) collective-permute-start(bf16[3,1,32,1408]{3,2,1,0:T(8,128)(2,1)S(1)} %pad_maximum_fusion.refs_8_), channel_id=1, source_target_pairs={{0,1},{1,0},{2,3},{3,2},{4,5},{5,4},{6,7},{7,6},{8,9},{9,8},{10,11... | collective-permute-start | bytes 811016 | tf_op jit(solution)/shard_map/ppermute | solution.py:28
  21.6 17.5 %collective-permute-start.11 = (bf16[3,1,32,1408]{3,2,1,0:T(8,128)(2,1)S(1)}, bf16[3,1,32,1408]{3,2,1,0:T(8,128)(2,1)S(1)}, u32[]{:S(2)}, u32[]{:S(2)}) collective-permute-start(bf16[3,1,32,1408]{3,2,1,0:T(8,128)(2,1)S(1)} %collective-permute-done.10.refs_10_), channel_id=1, source_target_pairs={{0,1},{1,0},{2,3},{3,2},{4,5},{5,4},{6,7},{7,6},{8,9},{9,8},{10,11... | collective-permute-start | bytes 811016 | tf_op jit(solution)/shard_map/ppermute | solution.py:28
  21.7 10.9 %collective-permute-start.4 = (bf16[1,32,1408]{2,1,0:T(8,128)(2,1)S(1)}, bf16[1,32,1408]{2,1,0:T(8,128)(2,1)S(1)}, u32[]{:S(2)}, u32[]{:S(2)}) collective-permute-start(bf16[1,32,1408]{2,1,0:T(8,128)(2,1)S(1)} %get-tuple-element.38.refs_4_), channel_id=1, source_target_pairs={{0,2},{2,0},{1,3},{3,1},{4,6},{6,4},{5,7},{7,5},{8,10},{10,8},{9,1... | collective-permute-start | bytes 270344 | tf_op jit(solution)/shard_map/ppermute | solution.py:28
  26.2 6.4 %collective-permute-start = (f32[3,4,1280]{2,1,0:T(4,128)S(1)}, f32[3,4,1280]{2,1,0:T(4,128)S(1)}, u32[]{:S(2)}, u32[]{:S(2)}) collective-permute-start(f32[3,4,1280]{2,1,0:T(4,128)S(1)} %get-tuple-element.35), channel_id=1, source_target_pairs={{0,4},{4,8},{8,12},{12,0},{1,5},{5,9},{9,13},{13,1},{2,6},{6,10},{... | collective-permute-start | bytes 184328 | tf_op jit(solution)/shard_map/ppermute | solution.py:28
  28.7 6.1 %collective-permute-start.1 = (f32[3,4,1280]{2,1,0:T(4,128)S(1)}, f32[3,4,1280]{2,1,0:T(4,128)S(1)}, u32[]{:S(2)}, u32[]{:S(2)}) collective-permute-start(f32[3,4,1280]{2,1,0:T(4,128)S(1)} %get-tuple-element.36), channel_id=1, source_target_pairs={{0,8},{4,12},{8,0},{12,4},{1,9},{5,13},{9,1},{13,5},{2,10},{6,14},... | collective-permute-start | bytes 184328 | tf_op jit(solution)/shard_map/ppermute | solution.py:28
  32.5 6.6 %collective-permute-start.3 = (bf16[1,32,1408]{2,1,0:T(8,128)(2,1)S(1)}, bf16[1,32,1408]{2,1,0:T(8,128)(2,1)S(1)}, u32[]{:S(2)}, u32[]{:S(2)}) collective-permute-start(bf16[1,32,1408]{2,1,0:T(8,128)(2,1)S(1)} %get-tuple-element.38.refs_4_), channel_id=1, source_target_pairs={{0,1},{1,0},{2,3},{3,2},{4,5},{5,4},{6,7},{7,6},{8,9},{9,8},{10,11... | collective-permute-start | bytes 270344 | tf_op jit(solution)/shard_map/ppermute | solution.py:28
  32.6 6.5 %collective-permute-start.5 = (bf16[1,32,1408]{2,1,0:T(8,128)(2,1)S(1)}, bf16[1,32,1408]{2,1,0:T(8,128)(2,1)S(1)}, u32[]{:S(2)}, u32[]{:S(2)}) collective-permute-start(bf16[1,32,1408]{2,1,0:T(8,128)(2,1)S(1)} %collective-permute-done.4.refs_6_), channel_id=1, source_target_pairs={{0,1},{1,0},{2,3},{3,2},{4,5},{5,4},{6,7},{7,6},{8,9},{9,8},{10,11... | collective-permute-start | bytes 270344 | tf_op jit(solution)/shard_map/ppermute | solution.py:28
  34.9 4.2 %collective-permute-start.2 = (f32[3,4,1280]{2,1,0:T(4,128)S(1)}, f32[3,4,1280]{2,1,0:T(4,128)S(1)}, u32[]{:S(2)}, u32[]{:S(2)}) collective-permute-start(f32[3,4,1280]{2,1,0:T(4,128)S(1)} %get-tuple-element.37), channel_id=1, source_target_pairs={{0,12},{4,0},{8,4},{12,8},{1,13},{5,1},{9,5},{13,9},{2,14},{6,2},{... | collective-permute-start | bytes 184328 | tf_op jit(solution)/shard_map/ppermute | solution.py:28
  45.7 10.2 %collective-permute-start.25 = (f16[3,128,384]{2,1,0:T(8,128)(2,1)}, f16[3,128,384]{2,1,0:T(8,128)(2,1)}, u32[]{:S(2)}, u32[]{:S(2)}) collective-permute-start(f16[3,128,384]{2,1,0:T(8,128)(2,1)} %select_convert_fusion.4), channel_id=1, source_target_pairs={{0,4},{4,0},{8,12},{12,8},{1,5},{5,1},{9,13},{13,9},{2,6},{6,2},{1... | collective-permute-start | bytes 884744 | tf_op jit(solution)/shard_map/ppermute | solution.py:461
  48.4 13.6 %collective-permute-start.12 = (f16[3,128,384]{2,1,0:T(8,128)(2,1)}, f16[3,128,384]{2,1,0:T(8,128)(2,1)S(1)}, u32[]{:S(2)}, u32[]{:S(2)}) collective-permute-start(f16[3,128,384]{2,1,0:T(8,128)(2,1)} %select_convert_fusion.9), channel_id=1, source_target_pairs={{0,4},{4,0},{8,12},{12,8},{1,5},{5,1},{9,13},{13,9},{2,6},{6,2},{1... | collective-permute-start | bytes 884744 | tf_op jit(solution)/shard_map/ppermute | solution.py:461
  51.1 25.7 %collective-permute-start.38 = (bf16[640,768]{1,0:T(8,128)(2,1)S(1)}, bf16[640,768]{1,0:T(8,128)(2,1)S(1)}, u32[]{:S(2)}, u32[]{:S(2)}) collective-permute-start(bf16[640,768]{1,0:T(8,128)(2,1)S(1)} %get-tuple-element.57), channel_id=1, source_target_pairs={{0,1},{1,0},{2,3},{3,2},{4,5},{5,4},{6,7},{7,6},{8,9},{9,8},{10,11... | collective-permute-start | bytes 2949128 | tf_op jit(solution)/shard_map/ppermute | solution.py:28
  57.3 11.1 %collective-permute-start.26 = (f16[3,128,384]{2,1,0:T(8,128)(2,1)S(1)}, f16[3,128,384]{2,1,0:T(8,128)(2,1)S(1)}, u32[]{:S(2)}, u32[]{:S(2)}) collective-permute-start(f16[3,128,384]{2,1,0:T(8,128)(2,1)S(1)} %get-tuple-element.68), channel_id=1, source_target_pairs={{0,4},{4,0},{8,12},{12,8},{1,5},{5,1},{9,13},{13,9},{2,6},{6,2},{1... | collective-permute-start | bytes 884744 | tf_op jit(solution)/shard_map/ppermute | solution.py:461
  57.3 11.6 %collective-permute-start.27 = (f16[3,128,384]{2,1,0:T(8,128)(2,1)S(1)}, f16[3,128,384]{2,1,0:T(8,128)(2,1)S(1)}, u32[]{:S(2)}, u32[]{:S(2)}) collective-permute-start(f16[3,128,384]{2,1,0:T(8,128)(2,1)S(1)} %get-tuple-element.67), channel_id=1, source_target_pairs={{0,1},{1,0},{4,8},{5,9},{8,4},{9,5},{12,13},{13,12},{2,3},{3,2},{6... | collective-permute-start | bytes 884744 | tf_op jit(solution)/shard_map/ppermute | solution.py:463
  63.4 11.3 %collective-permute-start.13 = (f16[3,128,384]{2,1,0:T(8,128)(2,1)S(1)}, f16[3,128,384]{2,1,0:T(8,128)(2,1)S(1)}, u32[]{:S(2)}, u32[]{:S(2)}) collective-permute-start(f16[3,128,384]{2,1,0:T(8,128)(2,1)S(1)} %get-tuple-element.70), channel_id=1, source_target_pairs={{0,4},{4,0},{8,12},{12,8},{1,5},{5,1},{9,13},{13,9},{2,6},{6,2},{1... | collective-permute-start | bytes 884744 | tf_op jit(solution)/shard_map/ppermute | solution.py:461
  63.5 11.3 %collective-permute-start.14 = (f16[3,128,384]{2,1,0:T(8,128)(2,1)S(1)}, f16[3,128,384]{2,1,0:T(8,128)(2,1)S(1)}, u32[]{:S(2)}, u32[]{:S(2)}) collective-permute-start(f16[3,128,384]{2,1,0:T(8,128)(2,1)S(1)} %get-tuple-element.69), channel_id=1, source_target_pairs={{0,1},{1,0},{4,8},{5,9},{8,4},{9,5},{12,13},{13,12},{2,3},{3,2},{6... | collective-permute-start | bytes 884744 | tf_op jit(solution)/shard_map/ppermute | solution.py:463
  68.4 46.1 %collective-permute-start.39 = (bf16[640,768]{1,0:T(8,128)(2,1)S(1)}, bf16[640,768]{1,0:T(8,128)(2,1)S(1)}, u32[]{:S(2)}, u32[]{:S(2)}) collective-permute-start(bf16[640,768]{1,0:T(8,128)(2,1)S(1)} %get-tuple-element.56.refs_16_), channel_id=1, source_target_pairs={{0,2},{2,0},{1,3},{3,1},{4,6},{6,4},{5,7},{7,5},{8,10},{10,8},{9,1... | collective-permute-start | bytes 2949128 | tf_op jit(solution)/shard_map/ppermute | solution.py:28
  70.5 9.2 %collective-permute-start.28 = (f16[3,128,384]{2,1,0:T(8,128)(2,1)S(1)}, f16[3,128,384]{2,1,0:T(8,128)(2,1)S(1)}, u32[]{:S(2)}, u32[]{:S(2)}) collective-permute-start(f16[3,128,384]{2,1,0:T(8,128)(2,1)S(1)} %get-tuple-element.64), channel_id=1, source_target_pairs={{0,4},{4,0},{8,12},{12,8},{1,5},{5,1},{9,13},{13,9},{2,6},{6,2},{1... | collective-permute-start | bytes 884744 | tf_op jit(solution)/shard_map/ppermute | solution.py:461
  74.7 5.5 %collective-permute-start.29 = (f16[3,128,384]{2,1,0:T(8,128)(2,1)S(1)}, f16[3,128,384]{2,1,0:T(8,128)(2,1)S(1)}, u32[]{:S(2)}, u32[]{:S(2)}) collective-permute-start(f16[3,128,384]{2,1,0:T(8,128)(2,1)S(1)} %get-tuple-element.63), channel_id=1, source_target_pairs={{0,1},{1,0},{4,8},{5,9},{8,4},{9,5},{12,13},{13,12},{2,3},{3,2},{6... | collective-permute-start | bytes 884744 | tf_op jit(solution)/shard_map/ppermute | solution.py:463
  75.0 10.2 %collective-permute-start.15 = (f16[3,128,384]{2,1,0:T(8,128)(2,1)S(1)}, f16[3,128,384]{2,1,0:T(8,128)(2,1)S(1)}, u32[]{:S(2)}, u32[]{:S(2)}) collective-permute-start(f16[3,128,384]{2,1,0:T(8,128)(2,1)S(1)} %get-tuple-element.66), channel_id=1, source_target_pairs={{0,4},{4,0},{8,12},{12,8},{1,5},{5,1},{9,13},{13,9},{2,6},{6,2},{1... | collective-permute-start | bytes 884744 | tf_op jit(solution)/shard_map/ppermute | solution.py:461
  76.8 8.5 %collective-permute-start.16 = (f16[3,128,384]{2,1,0:T(8,128)(2,1)S(1)}, f16[3,128,384]{2,1,0:T(8,128)(2,1)S(1)}, u32[]{:S(2)}, u32[]{:S(2)}) collective-permute-start(f16[3,128,384]{2,1,0:T(8,128)(2,1)S(1)} %get-tuple-element.65), channel_id=1, source_target_pairs={{0,1},{1,0},{4,8},{5,9},{8,4},{9,5},{12,13},{13,12},{2,3},{3,2},{6... | collective-permute-start | bytes 884744 | tf_op jit(solution)/shard_map/ppermute | solution.py:463
  79.7 49.9 %collective-permute-start.40 = (bf16[640,768]{1,0:T(8,128)(2,1)S(1)}, bf16[640,768]{1,0:T(8,128)(2,1)S(1)}, u32[]{:S(2)}, u32[]{:S(2)}) collective-permute-start(bf16[640,768]{1,0:T(8,128)(2,1)S(1)} %collective-permute-done.38.refs_17_), channel_id=1, source_target_pairs={{0,2},{2,0},{1,3},{3,1},{4,6},{6,4},{5,7},{7,5},{8,10},{10,8},{9,1... | collective-permute-start | bytes 2949128 | tf_op jit(solution)/shard_map/ppermute | solution.py:28
  82.4 28.2 %collective-permute-start.30 = (bf16[1,64,384]{2,1,0:T(8,128)(2,1)S(1)}, bf16[1,64,384]{2,1,0:T(8,128)(2,1)S(1)}, u32[]{:S(2)}, u32[]{:S(2)}) collective-permute-start(bf16[1,64,384]{2,1,0:T(8,128)(2,1)S(1)} %get-tuple-element.55), channel_id=1, source_target_pairs={{0,2},{2,0},{1,3},{3,1},{4,6},{6,4},{5,7},{7,5},{8,10},{10,8},{9,1... | collective-permute-start | bytes 147464 | tf_op jit(solution)/shard_map/ppermute | solution.py:28
  86.4 27.6 %collective-permute-start.17 = (bf16[1,64,384]{2,1,0:T(8,128)(2,1)S(1)}, bf16[1,64,384]{2,1,0:T(8,128)(2,1)S(1)}, u32[]{:S(2)}, u32[]{:S(2)}) collective-permute-start(bf16[1,64,384]{2,1,0:T(8,128)(2,1)S(1)} %get-tuple-element.49), channel_id=1, source_target_pairs={{0,2},{2,0},{1,3},{3,1},{4,6},{6,4},{5,7},{7,5},{8,10},{10,8},{9,1... | collective-permute-start | bytes 147464 | tf_op jit(solution)/shard_map/ppermute | solution.py:28
  110.6 6.6 %collective-permute-start.32 = (bf16[2,1,64,384]{3,2,1,0:T(8,128)(2,1)S(1)}, bf16[2,1,64,384]{3,2,1,0:T(8,128)(2,1)S(1)}, u32[]{:S(2)}, u32[]{:S(2)}) collective-permute-start(bf16[2,1,64,384]{3,2,1,0:T(8,128)(2,1)S(1)} %pad_maximum_fusion.2.refs_8_), channel_id=1, source_target_pairs={{0,4},{4,8},{8,12},{12,0},{1,5},{5,9},{9,13},{13,1},{2,6},{6,10},{... | collective-permute-start | bytes 294920 | tf_op jit(solution)/shard_map/ppermute | solution.py:28
  111.3 7.7 %collective-permute-start.34 = (bf16[2,1,64,384]{3,2,1,0:T(8,128)(2,1)S(1)}, bf16[2,1,64,384]{3,2,1,0:T(8,128)(2,1)S(1)}, u32[]{:S(2)}, u32[]{:S(2)}) collective-permute-start(bf16[2,1,64,384]{3,2,1,0:T(8,128)(2,1)S(1)} %pad_maximum_fusion.2.refs_8_), channel_id=1, source_target_pairs={{0,8},{4,12},{8,0},{12,4},{1,9},{5,13},{9,1},{13,5},{2,10},{6,14},... | collective-permute-start | bytes 294920 | tf_op jit(solution)/shard_map/ppermute | solution.py:28
  114.0 5.6 %collective-permute-start.36 = (bf16[2,1,64,384]{3,2,1,0:T(8,128)(2,1)S(1)}, bf16[2,1,64,384]{3,2,1,0:T(8,128)(2,1)S(1)}, u32[]{:S(2)}, u32[]{:S(2)}) collective-permute-start(bf16[2,1,64,384]{3,2,1,0:T(8,128)(2,1)S(1)} %pad_maximum_fusion.2.refs_8_), channel_id=1, source_target_pairs={{0,12},{4,0},{8,4},{12,8},{1,13},{5,1},{9,5},{13,9},{2,14},{6,2},{... | collective-permute-start | bytes 294920 | tf_op jit(solution)/shard_map/ppermute | solution.py:28
  114.5 8.2 %collective-permute-start.31 = (bf16[2,1,64,384]{3,2,1,0:T(8,128)(2,1)S(1)}, bf16[2,1,64,384]{3,2,1,0:T(8,128)(2,1)S(1)}, u32[]{:S(2)}, u32[]{:S(2)}) collective-permute-start(bf16[2,1,64,384]{3,2,1,0:T(8,128)(2,1)S(1)} %pad_maximum_fusion.2.refs_8_), channel_id=1, source_target_pairs={{0,1},{1,0},{2,3},{3,2},{4,5},{5,4},{6,7},{7,6},{8,9},{9,8},{10,11... | collective-permute-start | bytes 294920 | tf_op jit(solution)/shard_map/ppermute | solution.py:28
  117.2 6.7 %collective-permute-start.19 = (bf16[2,1,64,384]{3,2,1,0:T(8,128)(2,1)S(1)}, bf16[2,1,64,384]{3,2,1,0:T(8,128)(2,1)S(1)}, u32[]{:S(2)}, u32[]{:S(2)}) collective-permute-start(bf16[2,1,64,384]{3,2,1,0:T(8,128)(2,1)S(1)} %pad_maximum_fusion.1.refs_0_), channel_id=1, source_target_pairs={{0,4},{4,8},{8,12},{12,0},{1,5},{5,9},{9,13},{13,1},{2,6},{6,10},{... | collective-permute-start | bytes 294920 | tf_op jit(solution)/shard_map/ppermute | solution.py:28
  119.0 8.1 %collective-permute-start.21 = (bf16[2,1,64,384]{3,2,1,0:T(8,128)(2,1)S(1)}, bf16[2,1,64,384]{3,2,1,0:T(8,128)(2,1)S(1)}, u32[]{:S(2)}, u32[]{:S(2)}) collective-permute-start(bf16[2,1,64,384]{3,2,1,0:T(8,128)(2,1)S(1)} %pad_maximum_fusion.1.refs_0_), channel_id=1, source_target_pairs={{0,8},{4,12},{8,0},{12,4},{1,9},{5,13},{9,1},{13,5},{2,10},{6,14},... | collective-permute-start | bytes 294920 | tf_op jit(solution)/shard_map/ppermute | solution.py:28
  119.6 7.4 %collective-permute-start.23 = (bf16[2,1,64,384]{3,2,1,0:T(8,128)(2,1)S(1)}, bf16[2,1,64,384]{3,2,1,0:T(8,128)(2,1)S(1)}, u32[]{:S(2)}, u32[]{:S(2)}) collective-permute-start(bf16[2,1,64,384]{3,2,1,0:T(8,128)(2,1)S(1)} %pad_maximum_fusion.1.refs_0_), channel_id=1, source_target_pairs={{0,12},{4,0},{8,4},{12,8},{1,13},{5,1},{9,5},{13,9},{2,14},{6,2},{... | collective-permute-start | bytes 294920 | tf_op jit(solution)/shard_map/ppermute | solution.py:28
  122.8 4.8 %collective-permute-start.18 = (bf16[2,1,64,384]{3,2,1,0:T(8,128)(2,1)S(1)}, bf16[2,1,64,384]{3,2,1,0:T(8,128)(2,1)S(1)}, u32[]{:S(2)}, u32[]{:S(2)}) collective-permute-start(bf16[2,1,64,384]{3,2,1,0:T(8,128)(2,1)S(1)} %pad_maximum_fusion.1.refs_0_), channel_id=1, source_target_pairs={{0,1},{1,0},{2,3},{3,2},{4,5},{5,4},{6,7},{7,6},{8,9},{9,8},{10,11... | collective-permute-start | bytes 294920 | tf_op jit(solution)/shard_map/ppermute | solution.py:28
  123.9 3.7 %collective-permute-start.33 = (bf16[2,1,64,384]{3,2,1,0:T(8,128)(2,1)S(1)}, bf16[2,1,64,384]{3,2,1,0:T(8,128)(2,1)S(1)}, u32[]{:S(2)}, u32[]{:S(2)}) collective-permute-start(bf16[2,1,64,384]{3,2,1,0:T(8,128)(2,1)S(1)} %collective-permute-done.32.refs_10_), channel_id=1, source_target_pairs={{0,1},{1,0},{2,3},{3,2},{4,5},{5,4},{6,7},{7,6},{8,9},{9,8},{10,11... | collective-permute-start | bytes 294920 | tf_op jit(solution)/shard_map/ppermute | solution.py:28
  127.0 1.3 collective-permute-start.35
  127.0 1.5 %collective-permute-start.37 = (bf16[2,1,64,384]{3,2,1,0:T(8,128)(2,1)S(1)}, bf16[2,1,64,384]{3,2,1,0:T(8,128)(2,1)S(1)}, u32[]{:S(2)}, u32[]{:S(2)}) collective-permute-start(bf16[2,1,64,384]{3,2,1,0:T(8,128)(2,1)S(1)} %collective-permute-done.36.refs_14_), channel_id=1, source_target_pairs={{0,1},{1,0},{2,3},{3,2},{4,5},{5,4},{6,7},{7,6},{8,9},{9,8},{10,11... | collective-permute-start | bytes 294920 | tf_op jit(solution)/shard_map/ppermute | solution.py:28
  127.5 1.3 collective-permute-start.20
  127.6 1.4 collective-permute-start.22
  128.3 1.3 collective-permute-start.24
  131.2 6.5 %collective-permute-start.42 = (bf16[1,64,640]{2,1,0:T(8,128)(2,1)S(1)}, bf16[1,64,640]{2,1,0:T(8,128)(2,1)S(1)}, u32[]{:S(2)}, u32[]{:S(2)}) collective-permute-start(bf16[1,64,640]{2,1,0:T(8,128)(2,1)S(1)} %get-tuple-element.60), channel_id=1, source_target_pairs={{0,12},{4,0},{8,4},{12,8},{1,13},{5,1},{9,5},{13,9},{2,14},{6,2},{... | collective-permute-start | bytes 245768 | tf_op jit(solution)/shard_map/ppermute | solution.py:28
  134.8 8.0 %collective-permute-start.44 = (bf16[1,64,640]{2,1,0:T(8,128)(2,1)S(1)}, bf16[1,64,640]{2,1,0:T(8,128)(2,1)S(1)}, u32[]{:S(2)}, u32[]{:S(2)}) collective-permute-start(bf16[1,64,640]{2,1,0:T(8,128)(2,1)S(1)} %get-tuple-element.61), channel_id=1, source_target_pairs={{0,8},{4,12},{8,0},{12,4},{1,9},{5,13},{9,1},{13,5},{2,10},{6,14},... | collective-permute-start | bytes 245768 | tf_op jit(solution)/shard_map/ppermute | solution.py:28
  134.8 8.0 %collective-permute-start.46 = (bf16[1,64,640]{2,1,0:T(8,128)(2,1)S(1)}, bf16[1,64,640]{2,1,0:T(8,128)(2,1)S(1)}, u32[]{:S(2)}, u32[]{:S(2)}) collective-permute-start(bf16[1,64,640]{2,1,0:T(8,128)(2,1)S(1)} %get-tuple-element.62), channel_id=1, source_target_pairs={{0,4},{4,8},{8,12},{12,0},{1,5},{5,9},{9,13},{13,1},{2,6},{6,10},{... | collective-permute-start | bytes 245768 | tf_op jit(solution)/shard_map/ppermute | solution.py:28
  135.4 7.9 %collective-permute-start.41 = (bf16[1,64,640]{2,1,0:T(8,128)(2,1)S(1)}, bf16[1,64,640]{2,1,0:T(8,128)(2,1)S(1)}, u32[]{:S(2)}, u32[]{:S(2)}) collective-permute-start(bf16[1,64,640]{2,1,0:T(8,128)(2,1)S(1)} %get-tuple-element.59), channel_id=1, source_target_pairs={{0,1},{1,0},{2,3},{3,2},{4,5},{5,4},{6,7},{7,6},{8,9},{9,8},{10,11... | collective-permute-start | bytes 245768 | tf_op jit(solution)/shard_map/ppermute | solution.py:28
  137.7 5.7 %collective-permute-start.43 = (bf16[1,64,640]{2,1,0:T(8,128)(2,1)S(1)}, bf16[1,64,640]{2,1,0:T(8,128)(2,1)S(1)}, u32[]{:S(2)}, u32[]{:S(2)}) collective-permute-start(bf16[1,64,640]{2,1,0:T(8,128)(2,1)S(1)} %collective-permute-done.42.refs_2_), channel_id=1, source_target_pairs={{0,1},{1,0},{2,3},{3,2},{4,5},{5,4},{6,7},{7,6},{8,9},{9,8},{10,11... | collective-permute-start | bytes 245768 | tf_op jit(solution)/shard_map/ppermute | solution.py:28
  142.8 1.3 collective-permute-start.45
  142.8 1.4 collective-permute-start.47
  (9 other events, 56.2 us)

commit v14 on v12

--- a/solution.py
+++ b/solution.py
@@ -207,9 +207,13 @@
     copies = []
     for c in range(w_ref.shape[0]):
         for piece in range(DMA_PIECES):
-            at = c, pl.ds(piece * stride, stride)
+            rows_here = pl.ds(piece * stride, stride)
             copies.append(
-                pltpu.make_async_copy(w_ref.at[at], w_out.at[at], sems.at[len(copies)])
+                pltpu.make_async_copy(
+                    w_ref.at[c, rows_here, pl.ds(0, w_out.shape[2])],
+                    w_out.at[c, rows_here],
+                    sems.at[len(copies)],
+                )
             )
     z, k = lax.axis_index("tm"), pl.program_id(0)
     frames, part, wide = near[0].shape
@@ -255,7 +259,7 @@
             copy.wait()
 
 
-def modulate(start_step, w_qkv, shares, near, far):
+def modulate(start_step, w_qkv, held, shares, near, far):
     n_tm, n_seq, n_mp = len(shares), len(near), len(near[0])
     frames, part, wide = near[0][0].shape
     three = w_qkv.shape[0]
@@ -283,13 +287,13 @@
             jax.ShapeDtypeStruct(shape, jnp.bfloat16),
             jax.ShapeDtypeStruct((n_tm, frames, depth), jnp.float32),
         ]
-        + [jax.ShapeDtypeStruct(w_qkv.shape, w_qkv.dtype)],
+        + [jax.ShapeDtypeStruct(w_qkv.shape[:2] + (held,), w_qkv.dtype)],
         cost_estimate=pl.CostEstimate(
             flops=4 * n_tm * n_seq * frames * n_mp * part * depth,
             bytes_accessed=4 * n_tm * n_seq * frames * n_mp * part * depth,
             transcendentals=0,
         ),
-        compiler_params=pltpu.CompilerParams(vmem_limit_bytes=42 << 20),
+        compiler_params=pltpu.CompilerParams(vmem_limit_bytes=46 << 20),
         name="modulate",
     )(start_step, w_qkv, *shares, *[r for rows in (near, far) for side in rows for r in side])
 
@@ -442,15 +446,15 @@
             weights[j].append(turn(share, "seq", -j))
 
     groups = head_groups(cols)
-    hidden, coef, held_qkv = modulate(start_step, w_qkv, shares, near, far)
+    hidden, coef, held_qkv = modulate(start_step, w_qkv, groups[0][1], shares, near, far)
     hidden = hidden.reshape(n_tm, n_seq * frames * tok, depth)
     proj = []
-    for lane, size in groups:
+    for h, (lane, size) in enumerate(groups):
         proj.append(
             jnp.einsum(
                 "krd,cdh->kcrh",
                 hidden,
-                held_qkv[:, :, lane : lane + size],
+                w_qkv[:, :, lane : lane + size] if h else held_qkv,
                 preferred_element_type=jnp.float32,
             )
         )

time: 145 us -> 148 us (1.021)
  waiting for transfers between devices: 83.8 us -> 87.7 us
    ppermute x38, waiting for transfers between devices: 61.1 us -> 66.6 us  [turn(): lax.ppermute(block, axis, [(i, (i + distance) % size) for i in range(size)])]
    ppermute x6, waiting for transfers between devices: 22.7 us -> 21.1 us  [sweep(): first = lax.ppermute(first, 'tm', ev)]
    unnamed x14 -> x18, local copies, waits for them, and re-layouts: 3.26 us -> 3.19 us
  transfers between devices with their start and end apart: 48 -> 48, of which waited for: 26 -> 25; matrix products, arithmetic and copies ran while one was open for 6% -> 6% of each run, Pallas kernels for 2% -> 2%
where the time goes in v14:
time: 148 us; the launch traced here: 147 us
  waiting for transfers between devices  87.7 us (59%)
  starting transfers between devices  35.5 us (24%)
  Pallas kernels  8.51 us (6%)
  other arithmetic  7.65 us (5%)
  matrix products  3.73 us (3%)
  local copies, waits for them, and re-layouts  3.2 us (2%)
    ppermute x38, waiting for transfers between devices, turn(): lax.ppermute(block, axis, [(i, (i + distance) % size) for i in range(size)])  66.6 us
    ppermute x38, starting transfers between devices, turn(): lax.ppermute(block, axis, [(i, (i + distance) % size) for i in range(size)])  30.9 us
    ppermute x6, waiting for transfers between devices, sweep(): first = lax.ppermute(first, 'tm', ev)  21.1 us
    convert_element_type x4, other arithmetic, sweep(): second = jnp.where(even, left, right).astype(jnp.float16)  4.47 us
    ppermute x6, starting transfers between devices, sweep(): first = lax.ppermute(first, 'tm', ev)  4.39 us
    dot_general x2, matrix products, sweep(): jnp.einsum('krd,cdh->kcrh', hidden, w_qkv[:, :, lane:lane + size] if h el...  3.73 us
    unnamed x18, local copies, waits for them, and re-layouts  3.19 us
  transfers between devices with their start and end apart: 48, of which 25 were waited for; matrix products, arithmetic and copies ran while one was open for 6% of the time, Pallas kernels for 2%

profile of v14, /device:TPU:0, one launch (start us, length us, event | category | flops | bytes accessed | tf_op | source)
XLA Modules:
  0.0 147.2 jit_solution(8650371076388006754)
XLA Ops:
  0.0 1.1 copy-done.2
  1.5 5.1 %collective-permute-start.8 = (bf16[1,32,1408]{2,1,0:T(8,128)(2,1)S(1)}, bf16[1,32,1408]{2,1,0:T(8,128)(2,1)S(1)}, u32[]{:S(2)}, u32[]{:S(2)}) collective-permute-start(bf16[1,32,1408]{2,1,0:T(8,128)(2,1)S(1)} %get-tuple-element.42), channel_id=1, source_target_pairs={{0,12},{4,0},{8,4},{12,8},{1,13},{5,1},{9,5},{13,9},{2,14},{6,2},{... | collective-permute-start | bytes 270344 | tf_op jit(solution)/shard_map/ppermute | solution.py:29
  6.6 1.0 collective-permute-start.6
  7.6 2.0 %collective-permute-done.8 = bf16[1,32,1408]{2,1,0:T(8,128)(2,1)S(1)} collective-permute-done((bf16[1,32,1408]{2,1,0:T(8,128)(2,1)S(1)}, bf16[1,32,1408]{2,1,0:T(8,128)(2,1)S(1)}, u32[]{:S(2)}, u32[]{:S(2)}) %collective-permute-start.8) | collective-permute-done | bytes 90144 | tf_op jit(solution)/shard_map/ppermute | solution.py:29
  9.6 5.1 %collective-permute-done.7 = bf16[1,32,1408]{2,1,0:T(8,128)(2,1)S(1)} collective-permute-done((bf16[1,32,1408]{2,1,0:T(8,128)(2,1)S(1)}, bf16[1,32,1408]{2,1,0:T(8,128)(2,1)S(1)}, u32[]{:S(2)}, u32[]{:S(2)}) %collective-permute-start.7) | collective-permute-done | bytes 90144 | tf_op jit(solution)/shard_map/ppermute | solution.py:29
  14.8 1.6 %collective-permute-start.10 = (bf16[3,1,32,1408]{3,2,1,0:T(8,128)(2,1)S(1)}, bf16[3,1,32,1408]{3,2,1,0:T(8,128)(2,1)S(1)}, u32[]{:S(2)}, u32[]{:S(2)}) collective-permute-start(bf16[3,1,32,1408]{3,2,1,0:T(8,128)(2,1)S(1)} %pad_maximum_fusion.refs_8_), channel_id=1, source_target_pairs={{0,2},{2,0},{1,3},{3,1},{4,6},{6,4},{5,7},{7,5},{8,10},{10,8},{9,1... | collective-permute-start | bytes 811016 | tf_op jit(solution)/shard_map/ppermute | solution.py:29
  16.4 6.6 %collective-permute-done.10.refs_10_ = bf16[3,1,32,1408]{3,2,1,0:T(8,128)(2,1)S(1)} collective-permute-done((bf16[3,1,32,1408]{3,2,1,0:T(8,128)(2,1)S(1)}, bf16[3,1,32,1408]{3,2,1,0:T(8,128)(2,1)S(1)}, u32[]{:S(2)}, u32[]{:S(2)}) %collective-permute-start.10) | collective-permute-done | bytes 270368 | tf_op jit(solution)/shard_map/ppermute | solution.py:29
  22.9 1.5 %collective-permute-start.4 = (bf16[1,32,1408]{2,1,0:T(8,128)(2,1)S(1)}, bf16[1,32,1408]{2,1,0:T(8,128)(2,1)S(1)}, u32[]{:S(2)}, u32[]{:S(2)}) collective-permute-start(bf16[1,32,1408]{2,1,0:T(8,128)(2,1)S(1)} %get-tuple-element.39.refs_4_), channel_id=1, source_target_pairs={{0,2},{2,0},{1,3},{3,1},{4,6},{6,4},{5,7},{7,5},{8,10},{10,8},{9,1... | collective-permute-start | bytes 270344 | tf_op jit(solution)/shard_map/ppermute | solution.py:29
  25.1 1.5 %copy-done = bf16[64,15360]{1,0:T(8,128)(2,1)S(1)} copy-done((bf16[64,15360]{1,0:T(8,128)(2,1)S(1)}, bf16[64,15360]{1,0:T(8,128)(2,1)}, u32[]{:S(2)}) %copy-start) | copy-done | bytes 1966104
  26.6 0.8 time_shares.1
  27.5 1.9 %collective-permute-start.1 = (f32[3,4,1280]{2,1,0:T(4,128)S(1)}, f32[3,4,1280]{2,1,0:T(4,128)S(1)}, u32[]{:S(2)}, u32[]{:S(2)}) collective-permute-start(f32[3,4,1280]{2,1,0:T(4,128)S(1)} %get-tuple-element.37), channel_id=1, source_target_pairs={{0,8},{4,12},{8,0},{12,4},{1,9},{5,13},{9,1},{13,5},{2,10},{6,14},... | collective-permute-start | bytes 184328 | tf_op jit(solution)/shard_map/ppermute | solution.py:29
  29.4 4.8 %collective-permute-done.refs_1_ = f32[3,4,1280]{2,1,0:T(4,128)S(1)} collective-permute-done((f32[3,4,1280]{2,1,0:T(4,128)S(1)}, f32[3,4,1280]{2,1,0:T(4,128)S(1)}, u32[]{:S(2)}, u32[]{:S(2)}) %collective-permute-start) | collective-permute-done | bytes 61472 | tf_op jit(solution)/shard_map/ppermute | solution.py:29
  35.3 1.7 %collective-permute-start.2 = (f32[3,4,1280]{2,1,0:T(4,128)S(1)}, f32[3,4,1280]{2,1,0:T(4,128)S(1)}, u32[]{:S(2)}, u32[]{:S(2)}) collective-permute-start(f32[3,4,1280]{2,1,0:T(4,128)S(1)} %get-tuple-element.38), channel_id=1, source_target_pairs={{0,12},{4,0},{8,4},{12,8},{1,13},{5,1},{9,5},{13,9},{2,14},{6,2},{... | collective-permute-start | bytes 184328 | tf_op jit(solution)/shard_map/ppermute | solution.py:29
  37.1 2.5 %collective-permute-done.2.refs_3_ = f32[3,4,1280]{2,1,0:T(4,128)S(1)} collective-permute-done((f32[3,4,1280]{2,1,0:T(4,128)S(1)}, f32[3,4,1280]{2,1,0:T(4,128)S(1)}, u32[]{:S(2)}, u32[]{:S(2)}) %collective-permute-start.2) | collective-permute-done | bytes 61472 | tf_op jit(solution)/shard_map/ppermute | solution.py:29
  39.6 2.2 %modulate.1 = (bf16[4,2,1,64,1280]{4,3,2,1,0:T(8,128)(2,1)S(1)}, f32[4,1,1280]{2,1,0:T(1,128)S(1)}, bf16[3,1280,384]{2,1,0:T(8,128)(2,1)S(1)}) custom-call(s32[1]{0:T(128)S(6)} %copy.15.step_ref, bf16[3,1280,768]{2,1,0:T(8,128)(2,1)} %w_ref.2, f32[3,4,1280]{2,1,0:T(4,128)S(1)} %get-tuple-element.35.refs_0_, f32[3,4,1280]{2,1,0:T(4,128)S(1)} %collective-permute-done.refs_1_, ...), custom_call_target="tpu_custom_call" | custom-call | flops 2621440 | bytes 2621440 | tf_op jit(solution)/shard_map/modulate/pallas_call | solution.py:269
  41.8 1.9 %fusion.8 = f32[4,3,128,384]{3,2,0,1:T(8,128)S(1)} fusion(bf16[4,128,1280,1]{2,1,0,3:T(8,128)(2,1)S(1)} %bitcast.118, bf16[3,1280,384]{2,1,0:T(8,128)(2,1)S(1)} %get-tuple-element.44), kind=kOutput, calls=%fused_computation.6 | convolution fusion | flops 1509949440 | bytes 6619136 | tf_op jit(solution)/shard_map/krd,cdh->kcrh/dot_general | solution.py:454
  43.7 0.9 select_convert_fusion.9
  45.2 1.9 %fusion.5 = f32[4,3,128,384]{3,2,1,0:T(8,128)S(1)} fusion(bf16[4,128,1280,1]{2,1,3,0:T(8,128)(2,1)S(1)} %bitcast.119, bf16[3,1280,768]{2,1,0:T(8,128)(2,1)S(1)} %bitcast.121), kind=kOutput, calls=%fused_computation.5 | convolution fusion | flops 1509949440 | bytes 6619136 | tf_op jit(solution)/shard_map/krd,cdh->kcrh/dot_general | solution.py:454
  47.1 0.8 select_convert_fusion.4
  47.9 1.4 collective-permute-start.25
  50.1 4.7 %collective-permute-done.12 = f16[3,128,384]{2,1,0:T(8,128)(2,1)} collective-permute-done((f16[3,128,384]{2,1,0:T(8,128)(2,1)}, f16[3,128,384]{2,1,0:T(8,128)(2,1)}, u32[]{:S(2)}, u32[]{:S(2)}) %collective-permute-start.12) | collective-permute-done | bytes 294944 | tf_op jit(solution)/shard_map/ppermute | solution.py:485
  54.8 1.4 select_convert_fusion.7
  56.4 4.7 %collective-permute-done.25 = f16[3,128,384]{2,1,0:T(8,128)(2,1)S(1)} collective-permute-done((f16[3,128,384]{2,1,0:T(8,128)(2,1)}, f16[3,128,384]{2,1,0:T(8,128)(2,1)S(1)}, u32[]{:S(2)}, u32[]{:S(2)}) %collective-permute-start.25) | collective-permute-done | bytes 294944 | tf_op jit(solution)/shard_map/ppermute | solution.py:485
  61.0 1.3 select_convert_fusion.2
  62.5 4.8 %collective-permute-done.13 = f16[3,128,384]{2,1,0:T(8,128)(2,1)S(1)} collective-permute-done((f16[3,128,384]{2,1,0:T(8,128)(2,1)S(1)}, f16[3,128,384]{2,1,0:T(8,128)(2,1)S(1)}, u32[]{:S(2)}, u32[]{:S(2)}) %collective-permute-start.13) | collective-permute-done | bytes 294944 | tf_op jit(solution)/shard_map/ppermute | solution.py:485
  67.9 1.5 %select_convert_fusion.5 = (f16[3,128,384]{2,1,0:T(8,128)(2,1)S(1)}, f16[3,128,384]{2,1,0:T(8,128)(2,1)S(1)}) fusion(pred[]{:T(512)S(6)} %eq.5, f16[3,128,384]{2,1,0:T(8,128)(2,1)S(1)} %collective-permute-done.14, f16[3,128,384]{2,1,0:T(8,128)(2,1)S(1)} %collective-permute-done.13, pred[]{:T(512)S(6)} %lt.9, f32[4,3,128,384]{3,2,0,1:T(8,128)} %copy-done.5, ...), kind=kLoop, calls=%fused_computation.56 | loop fusion | flops 1769472 | bytes 2359299 | tf_op jit(solution)/shard_map/convert_element_type | solution.py:484
  69.5 4.2 %collective-permute-done.26 = f16[3,128,384]{2,1,0:T(8,128)(2,1)S(1)} collective-permute-done((f16[3,128,384]{2,1,0:T(8,128)(2,1)S(1)}, f16[3,128,384]{2,1,0:T(8,128)(2,1)S(1)}, u32[]{:S(2)}, u32[]{:S(2)}) %collective-permute-start.26) | collective-permute-done | bytes 294944 | tf_op jit(solution)/shard_map/ppermute | solution.py:485
  73.9 2.7 %collective-permute-start.28 = (f16[3,128,384]{2,1,0:T(8,128)(2,1)S(1)}, f16[3,128,384]{2,1,0:T(8,128)(2,1)S(1)}, u32[]{:S(2)}, u32[]{:S(2)}) collective-permute-start(f16[3,128,384]{2,1,0:T(8,128)(2,1)S(1)} %get-tuple-element.66), channel_id=1, source_target_pairs={{0,4},{4,0},{8,12},{12,8},{1,5},{5,1},{9,13},{13,9},{2,6},{6,2},{1... | collective-permute-start | bytes 884744 | tf_op jit(solution)/shard_map/ppermute | solution.py:485
  76.6 0.9 collective-permute-done.15
  78.1 1.2 fusion.21
  79.3 0.9 attend.2
  80.3 1.5 %collective-permute-start.17 = (bf16[1,64,384]{2,1,0:T(8,128)(2,1)S(1)}, bf16[1,64,384]{2,1,0:T(8,128)(2,1)S(1)}, u32[]{:S(2)}, u32[]{:S(2)}) collective-permute-start(bf16[1,64,384]{2,1,0:T(8,128)(2,1)S(1)} %get-tuple-element.51), channel_id=1, source_target_pairs={{0,2},{2,0},{1,3},{3,1},{4,6},{6,4},{5,7},{7,5},{8,10},{10,8},{9,1... | collective-permute-start | bytes 147464 | tf_op jit(solution)/shard_map/ppermute | solution.py:29
  81.8 1.8 %collective-permute-done.28 = f16[3,128,384]{2,1,0:T(8,128)(2,1)S(1)} collective-permute-done((f16[3,128,384]{2,1,0:T(8,128)(2,1)S(1)}, f16[3,128,384]{2,1,0:T(8,128)(2,1)S(1)}, u32[]{:S(2)}, u32[]{:S(2)}) %collective-permute-start.28) | collective-permute-done | bytes 294944 | tf_op jit(solution)/shard_map/ppermute | solution.py:485
  83.8 0.9 attend.3
  85.3 23.9 %collective-permute-done.17 = bf16[1,64,384]{2,1,0:T(8,128)(2,1)S(1)} collective-permute-done((bf16[1,64,384]{2,1,0:T(8,128)(2,1)S(1)}, bf16[1,64,384]{2,1,0:T(8,128)(2,1)S(1)}, u32[]{:S(2)}, u32[]{:S(2)}) %collective-permute-start.17) | collective-permute-done | bytes 49184 | tf_op jit(solution)/shard_map/ppermute | solution.py:29
  109.8 3.7 %collective-permute-start.21 = (bf16[2,1,64,384]{3,2,1,0:T(8,128)(2,1)S(1)}, bf16[2,1,64,384]{3,2,1,0:T(8,128)(2,1)S(1)}, u32[]{:S(2)}, u32[]{:S(2)}) collective-permute-start(bf16[2,1,64,384]{3,2,1,0:T(8,128)(2,1)S(1)} %pad_maximum_fusion.1.refs_0_), channel_id=1, source_target_pairs={{0,8},{4,12},{8,0},{12,4},{1,9},{5,13},{9,1},{13,5},{2,10},{6,14},... | collective-permute-start | bytes 294920 | tf_op jit(solution)/shard_map/ppermute | solution.py:29
  113.5 1.3 collective-permute-start.23
  114.9 2.1 %collective-permute-done.19.refs_2_ = bf16[2,1,64,384]{3,2,1,0:T(8,128)(2,1)S(1)} collective-permute-done((bf16[2,1,64,384]{3,2,1,0:T(8,128)(2,1)S(1)}, bf16[2,1,64,384]{3,2,1,0:T(8,128)(2,1)S(1)}, u32[]{:S(2)}, u32[]{:S(2)}) %collective-permute-start.19) | collective-permute-done | bytes 98336 | tf_op jit(solution)/shard_map/ppermute | solution.py:29
  117.0 3.9 %collective-permute-done.21.refs_4_ = bf16[2,1,64,384]{3,2,1,0:T(8,128)(2,1)S(1)} collective-permute-done((bf16[2,1,64,384]{3,2,1,0:T(8,128)(2,1)S(1)}, bf16[2,1,64,384]{3,2,1,0:T(8,128)(2,1)S(1)}, u32[]{:S(2)}, u32[]{:S(2)}) %collective-permute-start.21) | collective-permute-done | bytes 98336 | tf_op jit(solution)/shard_map/ppermute | solution.py:29
  121.3 3.5 %collective-permute-start.36 = (bf16[2,1,64,384]{3,2,1,0:T(8,128)(2,1)S(1)}, bf16[2,1,64,384]{3,2,1,0:T(8,128)(2,1)S(1)}, u32[]{:S(2)}, u32[]{:S(2)}) collective-permute-start(bf16[2,1,64,384]{3,2,1,0:T(8,128)(2,1)S(1)} %pad_maximum_fusion.2.refs_8_), channel_id=1, source_target_pairs={{0,12},{4,0},{8,4},{12,8},{1,13},{5,1},{9,5},{13,9},{2,14},{6,2},{... | collective-permute-start | bytes 294920 | tf_op jit(solution)/shard_map/ppermute | solution.py:29
  125.3 3.8 %collective-permute-done.34.refs_12_ = bf16[2,1,64,384]{3,2,1,0:T(8,128)(2,1)S(1)} collective-permute-done((bf16[2,1,64,384]{3,2,1,0:T(8,128)(2,1)S(1)}, bf16[2,1,64,384]{3,2,1,0:T(8,128)(2,1)S(1)}, u32[]{:S(2)}, u32[]{:S(2)}) %collective-permute-start.34) | collective-permute-done | bytes 98336 | tf_op jit(solution)/shard_map/ppermute | solution.py:29
  129.1 1.0 collective-permute-done.36.refs_14_
  131.9 1.5 %project.1 = (f32[1,64,640]{2,1,0:T(8,128)S(1)}, bf16[1,64,640]{2,1,0:T(8,128)(2,1)S(1)}, bf16[1,64,640]{2,1,0:T(8,128)(2,1)S(1)}, bf16[1,64,640]{2,1,0:T(8,128)(2,1)S(1)}, bf16[1,64,640]{2,1,0:T(8,128)(2,1)S(1)}) custom-call(f32[4,1,1280]{2,1,0:T(1,128)S(1)} %get-tuple-element.43.coef_ref, bf16[2,1,64,384]{3,2,1,0:T(8,128)(2,1)S(1)} %pad_maximum_fusion.1.refs_0_, ...), custom_call_target="tpu_custom_call" | custom-call | flops 1006632960 | bytes 5505024 | tf_op jit(solution)/shard_map/project/pallas_call | solution.py:365
  133.5 3.0 %collective-permute-start.42 = (bf16[1,64,640]{2,1,0:T(8,128)(2,1)S(1)}, bf16[1,64,640]{2,1,0:T(8,128)(2,1)S(1)}, u32[]{:S(2)}, u32[]{:S(2)}) collective-permute-start(bf16[1,64,640]{2,1,0:T(8,128)(2,1)S(1)} %get-tuple-element.62), channel_id=1, source_target_pairs={{0,12},{4,0},{8,4},{12,8},{1,13},{5,1},{9,5},{13,9},{2,14},{6,2},{... | collective-permute-start | bytes 245768 | tf_op jit(solution)/shard_map/ppermute | solution.py:29
  137.1 2.2 %collective-permute-done.42.refs_2_ = bf16[1,64,640]{2,1,0:T(8,128)(2,1)S(1)} collective-permute-done((bf16[1,64,640]{2,1,0:T(8,128)(2,1)S(1)}, bf16[1,64,640]{2,1,0:T(8,128)(2,1)S(1)}, u32[]{:S(2)}, u32[]{:S(2)}) %collective-permute-start.42) | collective-permute-done | bytes 81952 | tf_op jit(solution)/shard_map/ppermute | solution.py:29
  139.4 5.3 %collective-permute-done.44.refs_4_ = bf16[1,64,640]{2,1,0:T(8,128)(2,1)S(1)} collective-permute-done((bf16[1,64,640]{2,1,0:T(8,128)(2,1)S(1)}, bf16[1,64,640]{2,1,0:T(8,128)(2,1)S(1)}, u32[]{:S(2)}, u32[]{:S(2)}) %collective-permute-start.44) | collective-permute-done | bytes 81952 | tf_op jit(solution)/shard_map/ppermute | solution.py:29
  145.2 0.8 collective-permute-done.45.refs_5_
  146.2 1.0 finish.1
  (89 shorter events, 10.0 us)
Async XLA Ops:
  1.5 8.1 %collective-permute-start.8 = (bf16[1,32,1408]{2,1,0:T(8,128)(2,1)S(1)}, bf16[1,32,1408]{2,1,0:T(8,128)(2,1)S(1)}, u32[]{:S(2)}, u32[]{:S(2)}) collective-permute-start(bf16[1,32,1408]{2,1,0:T(8,128)(2,1)S(1)} %get-tuple-element.42), channel_id=1, source_target_pairs={{0,12},{4,0},{8,4},{12,8},{1,13},{5,1},{9,5},{13,9},{2,14},{6,2},{... | collective-permute-start | bytes 270344 | tf_op jit(solution)/shard_map/ppermute | solution.py:29
  6.6 8.1 %collective-permute-start.7 = (bf16[1,32,1408]{2,1,0:T(8,128)(2,1)S(1)}, bf16[1,32,1408]{2,1,0:T(8,128)(2,1)S(1)}, u32[]{:S(2)}, u32[]{:S(2)}) collective-permute-start(bf16[1,32,1408]{2,1,0:T(8,128)(2,1)S(1)} %get-tuple-element.41), channel_id=1, source_target_pairs={{0,8},{4,12},{8,0},{12,4},{1,9},{5,13},{9,1},{13,5},{2,10},{6,14},... | collective-permute-start | bytes 270344 | tf_op jit(solution)/shard_map/ppermute | solution.py:29
  6.6 8.1 %collective-permute-start.6 = (bf16[1,32,1408]{2,1,0:T(8,128)(2,1)S(1)}, bf16[1,32,1408]{2,1,0:T(8,128)(2,1)S(1)}, u32[]{:S(2)}, u32[]{:S(2)}) collective-permute-start(bf16[1,32,1408]{2,1,0:T(8,128)(2,1)S(1)} %get-tuple-element.40), channel_id=1, source_target_pairs={{0,4},{4,8},{8,12},{12,0},{1,5},{5,9},{9,13},{13,1},{2,6},{6,10},{... | collective-permute-start | bytes 270344 | tf_op jit(solution)/shard_map/ppermute | solution.py:29
  14.8 8.1 %collective-permute-start.10 = (bf16[3,1,32,1408]{3,2,1,0:T(8,128)(2,1)S(1)}, bf16[3,1,32,1408]{3,2,1,0:T(8,128)(2,1)S(1)}, u32[]{:S(2)}, u32[]{:S(2)}) collective-permute-start(bf16[3,1,32,1408]{3,2,1,0:T(8,128)(2,1)S(1)} %pad_maximum_fusion.refs_8_), channel_id=1, source_target_pairs={{0,2},{2,0},{1,3},{3,1},{4,6},{6,4},{5,7},{7,5},{8,10},{10,8},{9,1... | collective-permute-start | bytes 811016 | tf_op jit(solution)/shard_map/ppermute | solution.py:29
  16.4 23.2 %collective-permute-start.9 = (bf16[3,1,32,1408]{3,2,1,0:T(8,128)(2,1)S(1)}, bf16[3,1,32,1408]{3,2,1,0:T(8,128)(2,1)S(1)}, u32[]{:S(2)}, u32[]{:S(2)}) collective-permute-start(bf16[3,1,32,1408]{3,2,1,0:T(8,128)(2,1)S(1)} %pad_maximum_fusion.refs_8_), channel_id=1, source_target_pairs={{0,1},{1,0},{2,3},{3,2},{4,5},{5,4},{6,7},{7,6},{8,9},{9,8},{10,11... | collective-permute-start | bytes 811016 | tf_op jit(solution)/shard_map/ppermute | solution.py:29
  22.9 16.7 %collective-permute-start.11 = (bf16[3,1,32,1408]{3,2,1,0:T(8,128)(2,1)S(1)}, bf16[3,1,32,1408]{3,2,1,0:T(8,128)(2,1)S(1)}, u32[]{:S(2)}, u32[]{:S(2)}) collective-permute-start(bf16[3,1,32,1408]{3,2,1,0:T(8,128)(2,1)S(1)} %collective-permute-done.10.refs_10_), channel_id=1, source_target_pairs={{0,1},{1,0},{2,3},{3,2},{4,5},{5,4},{6,7},{7,6},{8,9},{9,8},{10,11... | collective-permute-start | bytes 811016 | tf_op jit(solution)/shard_map/ppermute | solution.py:29
  22.9 11.3 %collective-permute-start.4 = (bf16[1,32,1408]{2,1,0:T(8,128)(2,1)S(1)}, bf16[1,32,1408]{2,1,0:T(8,128)(2,1)S(1)}, u32[]{:S(2)}, u32[]{:S(2)}) collective-permute-start(bf16[1,32,1408]{2,1,0:T(8,128)(2,1)S(1)} %get-tuple-element.39.refs_4_), channel_id=1, source_target_pairs={{0,2},{2,0},{1,3},{3,1},{4,6},{6,4},{5,7},{7,5},{8,10},{10,8},{9,1... | collective-permute-start | bytes 270344 | tf_op jit(solution)/shard_map/ppermute | solution.py:29
  27.5 6.7 %collective-permute-start = (f32[3,4,1280]{2,1,0:T(4,128)S(1)}, f32[3,4,1280]{2,1,0:T(4,128)S(1)}, u32[]{:S(2)}, u32[]{:S(2)}) collective-permute-start(f32[3,4,1280]{2,1,0:T(4,128)S(1)} %get-tuple-element.36), channel_id=1, source_target_pairs={{0,4},{4,8},{8,12},{12,0},{1,5},{5,9},{9,13},{13,1},{2,6},{6,10},{... | collective-permute-start | bytes 184328 | tf_op jit(solution)/shard_map/ppermute | solution.py:29
  27.5 7.8 %collective-permute-start.1 = (f32[3,4,1280]{2,1,0:T(4,128)S(1)}, f32[3,4,1280]{2,1,0:T(4,128)S(1)}, u32[]{:S(2)}, u32[]{:S(2)}) collective-permute-start(f32[3,4,1280]{2,1,0:T(4,128)S(1)} %get-tuple-element.37), channel_id=1, source_target_pairs={{0,8},{4,12},{8,0},{12,4},{1,9},{5,13},{9,1},{13,5},{2,10},{6,14},... | collective-permute-start | bytes 184328 | tf_op jit(solution)/shard_map/ppermute | solution.py:29
  34.2 5.4 %collective-permute-start.3 = (bf16[1,32,1408]{2,1,0:T(8,128)(2,1)S(1)}, bf16[1,32,1408]{2,1,0:T(8,128)(2,1)S(1)}, u32[]{:S(2)}, u32[]{:S(2)}) collective-permute-start(bf16[1,32,1408]{2,1,0:T(8,128)(2,1)S(1)} %get-tuple-element.39.refs_4_), channel_id=1, source_target_pairs={{0,1},{1,0},{2,3},{3,2},{4,5},{5,4},{6,7},{7,6},{8,9},{9,8},{10,11... | collective-permute-start | bytes 270344 | tf_op jit(solution)/shard_map/ppermute | solution.py:29
  34.2 5.4 %collective-permute-start.5 = (bf16[1,32,1408]{2,1,0:T(8,128)(2,1)S(1)}, bf16[1,32,1408]{2,1,0:T(8,128)(2,1)S(1)}, u32[]{:S(2)}, u32[]{:S(2)}) collective-permute-start(bf16[1,32,1408]{2,1,0:T(8,128)(2,1)S(1)} %collective-permute-done.4.refs_6_), channel_id=1, source_target_pairs={{0,1},{1,0},{2,3},{3,2},{4,5},{5,4},{6,7},{7,6},{8,9},{9,8},{10,11... | collective-permute-start | bytes 270344 | tf_op jit(solution)/shard_map/ppermute | solution.py:29
  35.3 4.2 %collective-permute-start.2 = (f32[3,4,1280]{2,1,0:T(4,128)S(1)}, f32[3,4,1280]{2,1,0:T(4,128)S(1)}, u32[]{:S(2)}, u32[]{:S(2)}) collective-permute-start(f32[3,4,1280]{2,1,0:T(4,128)S(1)} %get-tuple-element.38), channel_id=1, source_target_pairs={{0,12},{4,0},{8,4},{12,8},{1,13},{5,1},{9,5},{13,9},{2,14},{6,2},{... | collective-permute-start | bytes 184328 | tf_op jit(solution)/shard_map/ppermute | solution.py:29
  44.6 10.2 %collective-permute-start.12 = (f16[3,128,384]{2,1,0:T(8,128)(2,1)}, f16[3,128,384]{2,1,0:T(8,128)(2,1)}, u32[]{:S(2)}, u32[]{:S(2)}) collective-permute-start(f16[3,128,384]{2,1,0:T(8,128)(2,1)} %select_convert_fusion.9), channel_id=1, source_target_pairs={{0,4},{4,0},{8,12},{12,8},{1,5},{5,1},{9,13},{13,9},{2,6},{6,2},{1... | collective-permute-start | bytes 884744 | tf_op jit(solution)/shard_map/ppermute | solution.py:485
  47.9 13.1 %collective-permute-start.25 = (f16[3,128,384]{2,1,0:T(8,128)(2,1)}, f16[3,128,384]{2,1,0:T(8,128)(2,1)S(1)}, u32[]{:S(2)}, u32[]{:S(2)}) collective-permute-start(f16[3,128,384]{2,1,0:T(8,128)(2,1)} %select_convert_fusion.4), channel_id=1, source_target_pairs={{0,4},{4,0},{8,12},{12,8},{1,5},{5,1},{9,13},{13,9},{2,6},{6,2},{1... | collective-permute-start | bytes 884744 | tf_op jit(solution)/shard_map/ppermute | solution.py:485
  50.0 26.6 %collective-permute-start.38 = (bf16[640,768]{1,0:T(8,128)(2,1)S(1)}, bf16[640,768]{1,0:T(8,128)(2,1)S(1)}, u32[]{:S(2)}, u32[]{:S(2)}) collective-permute-start(bf16[640,768]{1,0:T(8,128)(2,1)S(1)} %get-tuple-element.59), channel_id=1, source_target_pairs={{0,1},{1,0},{2,3},{3,2},{4,5},{5,4},{6,7},{7,6},{8,9},{9,8},{10,11... | collective-permute-start | bytes 2949128 | tf_op jit(solution)/shard_map/ppermute | solution.py:29
  56.2 11.1 %collective-permute-start.13 = (f16[3,128,384]{2,1,0:T(8,128)(2,1)S(1)}, f16[3,128,384]{2,1,0:T(8,128)(2,1)S(1)}, u32[]{:S(2)}, u32[]{:S(2)}) collective-permute-start(f16[3,128,384]{2,1,0:T(8,128)(2,1)S(1)} %get-tuple-element.72), channel_id=1, source_target_pairs={{0,4},{4,0},{8,12},{12,8},{1,5},{5,1},{9,13},{13,9},{2,6},{6,2},{1... | collective-permute-start | bytes 884744 | tf_op jit(solution)/shard_map/ppermute | solution.py:485
  56.3 11.6 %collective-permute-start.14 = (f16[3,128,384]{2,1,0:T(8,128)(2,1)S(1)}, f16[3,128,384]{2,1,0:T(8,128)(2,1)S(1)}, u32[]{:S(2)}, u32[]{:S(2)}) collective-permute-start(f16[3,128,384]{2,1,0:T(8,128)(2,1)S(1)} %get-tuple-element.71), channel_id=1, source_target_pairs={{0,1},{1,0},{4,8},{5,9},{8,4},{9,5},{12,13},{13,12},{2,3},{3,2},{6... | collective-permute-start | bytes 884744 | tf_op jit(solution)/shard_map/ppermute | solution.py:487
  62.3 11.3 %collective-permute-start.26 = (f16[3,128,384]{2,1,0:T(8,128)(2,1)S(1)}, f16[3,128,384]{2,1,0:T(8,128)(2,1)S(1)}, u32[]{:S(2)}, u32[]{:S(2)}) collective-permute-start(f16[3,128,384]{2,1,0:T(8,128)(2,1)S(1)} %get-tuple-element.70), channel_id=1, source_target_pairs={{0,4},{4,0},{8,12},{12,8},{1,5},{5,1},{9,13},{13,9},{2,6},{6,2},{1... | collective-permute-start | bytes 884744 | tf_op jit(solution)/shard_map/ppermute | solution.py:485
  62.4 11.3 %collective-permute-start.27 = (f16[3,128,384]{2,1,0:T(8,128)(2,1)S(1)}, f16[3,128,384]{2,1,0:T(8,128)(2,1)S(1)}, u32[]{:S(2)}, u32[]{:S(2)}) collective-permute-start(f16[3,128,384]{2,1,0:T(8,128)(2,1)S(1)} %get-tuple-element.69), channel_id=1, source_target_pairs={{0,1},{1,0},{4,8},{5,9},{8,4},{9,5},{12,13},{13,12},{2,3},{3,2},{6... | collective-permute-start | bytes 884744 | tf_op jit(solution)/shard_map/ppermute | solution.py:487
  67.3 46.2 %collective-permute-start.39 = (bf16[640,768]{1,0:T(8,128)(2,1)S(1)}, bf16[640,768]{1,0:T(8,128)(2,1)S(1)}, u32[]{:S(2)}, u32[]{:S(2)}) collective-permute-start(bf16[640,768]{1,0:T(8,128)(2,1)S(1)} %get-tuple-element.58.refs_16_), channel_id=1, source_target_pairs={{0,2},{2,0},{1,3},{3,1},{4,6},{6,4},{5,7},{7,5},{8,10},{10,8},{9,1... | collective-permute-start | bytes 2949128 | tf_op jit(solution)/shard_map/ppermute | solution.py:29
  69.4 8.1 %collective-permute-start.15 = (f16[3,128,384]{2,1,0:T(8,128)(2,1)S(1)}, f16[3,128,384]{2,1,0:T(8,128)(2,1)S(1)}, u32[]{:S(2)}, u32[]{:S(2)}) collective-permute-start(f16[3,128,384]{2,1,0:T(8,128)(2,1)S(1)} %get-tuple-element.68), channel_id=1, source_target_pairs={{0,4},{4,0},{8,12},{12,8},{1,5},{5,1},{9,13},{13,9},{2,6},{6,2},{1... | collective-permute-start | bytes 884744 | tf_op jit(solution)/shard_map/ppermute | solution.py:485
  73.7 4.5 %collective-permute-start.16 = (f16[3,128,384]{2,1,0:T(8,128)(2,1)S(1)}, f16[3,128,384]{2,1,0:T(8,128)(2,1)S(1)}, u32[]{:S(2)}, u32[]{:S(2)}) collective-permute-start(f16[3,128,384]{2,1,0:T(8,128)(2,1)S(1)} %get-tuple-element.67), channel_id=1, source_target_pairs={{0,1},{1,0},{4,8},{5,9},{8,4},{9,5},{12,13},{13,12},{2,3},{3,2},{6... | collective-permute-start | bytes 884744 | tf_op jit(solution)/shard_map/ppermute | solution.py:487
  73.9 9.7 %collective-permute-start.28 = (f16[3,128,384]{2,1,0:T(8,128)(2,1)S(1)}, f16[3,128,384]{2,1,0:T(8,128)(2,1)S(1)}, u32[]{:S(2)}, u32[]{:S(2)}) collective-permute-start(f16[3,128,384]{2,1,0:T(8,128)(2,1)S(1)} %get-tuple-element.66), channel_id=1, source_target_pairs={{0,4},{4,0},{8,12},{12,8},{1,5},{5,1},{9,13},{13,9},{2,6},{6,2},{1... | collective-permute-start | bytes 884744 | tf_op jit(solution)/shard_map/ppermute | solution.py:485
  76.6 7.0 %collective-permute-start.29 = (f16[3,128,384]{2,1,0:T(8,128)(2,1)S(1)}, f16[3,128,384]{2,1,0:T(8,128)(2,1)S(1)}, u32[]{:S(2)}, u32[]{:S(2)}) collective-permute-start(f16[3,128,384]{2,1,0:T(8,128)(2,1)S(1)} %get-tuple-element.65), channel_id=1, source_target_pairs={{0,1},{1,0},{4,8},{5,9},{8,4},{9,5},{12,13},{13,12},{2,3},{3,2},{6... | collective-permute-start | bytes 884744 | tf_op jit(solution)/shard_map/ppermute | solution.py:487
  77.5 54.4 %collective-permute-start.40 = (bf16[640,768]{1,0:T(8,128)(2,1)S(1)}, bf16[640,768]{1,0:T(8,128)(2,1)S(1)}, u32[]{:S(2)}, u32[]{:S(2)}) collective-permute-start(bf16[640,768]{1,0:T(8,128)(2,1)S(1)} %collective-permute-done.38.refs_17_), channel_id=1, source_target_pairs={{0,2},{2,0},{1,3},{3,1},{4,6},{6,4},{5,7},{7,5},{8,10},{10,8},{9,1... | collective-permute-start | bytes 2949128 | tf_op jit(solution)/shard_map/ppermute | solution.py:29
  80.3 29.0 %collective-permute-start.17 = (bf16[1,64,384]{2,1,0:T(8,128)(2,1)S(1)}, bf16[1,64,384]{2,1,0:T(8,128)(2,1)S(1)}, u32[]{:S(2)}, u32[]{:S(2)}) collective-permute-start(bf16[1,64,384]{2,1,0:T(8,128)(2,1)S(1)} %get-tuple-element.51), channel_id=1, source_target_pairs={{0,2},{2,0},{1,3},{3,1},{4,6},{6,4},{5,7},{7,5},{8,10},{10,8},{9,1... | collective-permute-start | bytes 147464 | tf_op jit(solution)/shard_map/ppermute | solution.py:29
  84.7 25.1 %collective-permute-start.30 = (bf16[1,64,384]{2,1,0:T(8,128)(2,1)S(1)}, bf16[1,64,384]{2,1,0:T(8,128)(2,1)S(1)}, u32[]{:S(2)}, u32[]{:S(2)}) collective-permute-start(bf16[1,64,384]{2,1,0:T(8,128)(2,1)S(1)} %get-tuple-element.57), channel_id=1, source_target_pairs={{0,2},{2,0},{1,3},{3,1},{4,6},{6,4},{5,7},{7,5},{8,10},{10,8},{9,1... | collective-permute-start | bytes 147464 | tf_op jit(solution)/shard_map/ppermute | solution.py:29
  109.3 5.6 %collective-permute-start.18 = (bf16[2,1,64,384]{3,2,1,0:T(8,128)(2,1)S(1)}, bf16[2,1,64,384]{3,2,1,0:T(8,128)(2,1)S(1)}, u32[]{:S(2)}, u32[]{:S(2)}) collective-permute-start(bf16[2,1,64,384]{3,2,1,0:T(8,128)(2,1)S(1)} %pad_maximum_fusion.1.refs_0_), channel_id=1, source_target_pairs={{0,1},{1,0},{2,3},{3,2},{4,5},{5,4},{6,7},{7,6},{8,9},{9,8},{10,11... | collective-permute-start | bytes 294920 | tf_op jit(solution)/shard_map/ppermute | solution.py:29
  109.4 7.6 %collective-permute-start.19 = (bf16[2,1,64,384]{3,2,1,0:T(8,128)(2,1)S(1)}, bf16[2,1,64,384]{3,2,1,0:T(8,128)(2,1)S(1)}, u32[]{:S(2)}, u32[]{:S(2)}) collective-permute-start(bf16[2,1,64,384]{3,2,1,0:T(8,128)(2,1)S(1)} %pad_maximum_fusion.1.refs_0_), channel_id=1, source_target_pairs={{0,4},{4,8},{8,12},{12,0},{1,5},{5,9},{9,13},{13,1},{2,6},{6,10},{... | collective-permute-start | bytes 294920 | tf_op jit(solution)/shard_map/ppermute | solution.py:29
  109.8 11.1 %collective-permute-start.21 = (bf16[2,1,64,384]{3,2,1,0:T(8,128)(2,1)S(1)}, bf16[2,1,64,384]{3,2,1,0:T(8,128)(2,1)S(1)}, u32[]{:S(2)}, u32[]{:S(2)}) collective-permute-start(bf16[2,1,64,384]{3,2,1,0:T(8,128)(2,1)S(1)} %pad_maximum_fusion.1.refs_0_), channel_id=1, source_target_pairs={{0,8},{4,12},{8,0},{12,4},{1,9},{5,13},{9,1},{13,5},{2,10},{6,14},... | collective-permute-start | bytes 294920 | tf_op jit(solution)/shard_map/ppermute | solution.py:29
  113.5 7.7 %collective-permute-start.23 = (bf16[2,1,64,384]{3,2,1,0:T(8,128)(2,1)S(1)}, bf16[2,1,64,384]{3,2,1,0:T(8,128)(2,1)S(1)}, u32[]{:S(2)}, u32[]{:S(2)}) collective-permute-start(bf16[2,1,64,384]{3,2,1,0:T(8,128)(2,1)S(1)} %pad_maximum_fusion.1.refs_0_), channel_id=1, source_target_pairs={{0,12},{4,0},{8,4},{12,8},{1,13},{5,1},{9,5},{13,9},{2,14},{6,2},{... | collective-permute-start | bytes 294920 | tf_op jit(solution)/shard_map/ppermute | solution.py:29
  114.9 9.9 %collective-permute-start.31 = (bf16[2,1,64,384]{3,2,1,0:T(8,128)(2,1)S(1)}, bf16[2,1,64,384]{3,2,1,0:T(8,128)(2,1)S(1)}, u32[]{:S(2)}, u32[]{:S(2)}) collective-permute-start(bf16[2,1,64,384]{3,2,1,0:T(8,128)(2,1)S(1)} %pad_maximum_fusion.2.refs_8_), channel_id=1, source_target_pairs={{0,1},{1,0},{2,3},{3,2},{4,5},{5,4},{6,7},{7,6},{8,9},{9,8},{10,11... | collective-permute-start | bytes 294920 | tf_op jit(solution)/shard_map/ppermute | solution.py:29
  117.0 7.8 %collective-permute-start.32 = (bf16[2,1,64,384]{3,2,1,0:T(8,128)(2,1)S(1)}, bf16[2,1,64,384]{3,2,1,0:T(8,128)(2,1)S(1)}, u32[]{:S(2)}, u32[]{:S(2)}) collective-permute-start(bf16[2,1,64,384]{3,2,1,0:T(8,128)(2,1)S(1)} %pad_maximum_fusion.2.refs_8_), channel_id=1, source_target_pairs={{0,4},{4,8},{8,12},{12,0},{1,5},{5,9},{9,13},{13,1},{2,6},{6,10},{... | collective-permute-start | bytes 294920 | tf_op jit(solution)/shard_map/ppermute | solution.py:29
  120.9 8.1 %collective-permute-start.34 = (bf16[2,1,64,384]{3,2,1,0:T(8,128)(2,1)S(1)}, bf16[2,1,64,384]{3,2,1,0:T(8,128)(2,1)S(1)}, u32[]{:S(2)}, u32[]{:S(2)}) collective-permute-start(bf16[2,1,64,384]{3,2,1,0:T(8,128)(2,1)S(1)} %pad_maximum_fusion.2.refs_8_), channel_id=1, source_target_pairs={{0,8},{4,12},{8,0},{12,4},{1,9},{5,13},{9,1},{13,5},{2,10},{6,14},... | collective-permute-start | bytes 294920 | tf_op jit(solution)/shard_map/ppermute | solution.py:29
  121.3 8.8 %collective-permute-start.36 = (bf16[2,1,64,384]{3,2,1,0:T(8,128)(2,1)S(1)}, bf16[2,1,64,384]{3,2,1,0:T(8,128)(2,1)S(1)}, u32[]{:S(2)}, u32[]{:S(2)}) collective-permute-start(bf16[2,1,64,384]{3,2,1,0:T(8,128)(2,1)S(1)} %pad_maximum_fusion.2.refs_8_), channel_id=1, source_target_pairs={{0,12},{4,0},{8,4},{12,8},{1,13},{5,1},{9,5},{13,9},{2,14},{6,2},{... | collective-permute-start | bytes 294920 | tf_op jit(solution)/shard_map/ppermute | solution.py:29
  124.8 5.3 %collective-permute-start.20 = (bf16[2,1,64,384]{3,2,1,0:T(8,128)(2,1)S(1)}, bf16[2,1,64,384]{3,2,1,0:T(8,128)(2,1)S(1)}, u32[]{:S(2)}, u32[]{:S(2)}) collective-permute-start(bf16[2,1,64,384]{3,2,1,0:T(8,128)(2,1)S(1)} %collective-permute-done.19.refs_2_), channel_id=1, source_target_pairs={{0,1},{1,0},{2,3},{3,2},{4,5},{5,4},{6,7},{7,6},{8,9},{9,8},{10,11... | collective-permute-start | bytes 294920 | tf_op jit(solution)/shard_map/ppermute | solution.py:29
  124.8 5.8 %collective-permute-start.22 = (bf16[2,1,64,384]{3,2,1,0:T(8,128)(2,1)S(1)}, bf16[2,1,64,384]{3,2,1,0:T(8,128)(2,1)S(1)}, u32[]{:S(2)}, u32[]{:S(2)}) collective-permute-start(bf16[2,1,64,384]{3,2,1,0:T(8,128)(2,1)S(1)} %collective-permute-done.21.refs_4_), channel_id=1, source_target_pairs={{0,1},{1,0},{2,3},{3,2},{4,5},{5,4},{6,7},{7,6},{8,9},{9,8},{10,11... | collective-permute-start | bytes 294920 | tf_op jit(solution)/shard_map/ppermute | solution.py:29
  129.1 1.6 %collective-permute-start.24 = (bf16[2,1,64,384]{3,2,1,0:T(8,128)(2,1)S(1)}, bf16[2,1,64,384]{3,2,1,0:T(8,128)(2,1)S(1)}, u32[]{:S(2)}, u32[]{:S(2)}) collective-permute-start(bf16[2,1,64,384]{3,2,1,0:T(8,128)(2,1)S(1)} %collective-permute-done.23.refs_6_), channel_id=1, source_target_pairs={{0,1},{1,0},{2,3},{3,2},{4,5},{5,4},{6,7},{7,6},{8,9},{9,8},{10,11... | collective-permute-start | bytes 294920 | tf_op jit(solution)/shard_map/ppermute | solution.py:29
  130.1 1.3 collective-permute-start.33
  130.1 1.5 collective-permute-start.35
  130.6 1.3 collective-permute-start.37
  133.5 5.9 %collective-permute-start.42 = (bf16[1,64,640]{2,1,0:T(8,128)(2,1)S(1)}, bf16[1,64,640]{2,1,0:T(8,128)(2,1)S(1)}, u32[]{:S(2)}, u32[]{:S(2)}) collective-permute-start(bf16[1,64,640]{2,1,0:T(8,128)(2,1)S(1)} %get-tuple-element.62), channel_id=1, source_target_pairs={{0,12},{4,0},{8,4},{12,8},{1,13},{5,1},{9,5},{13,9},{2,14},{6,2},{... | collective-permute-start | bytes 245768 | tf_op jit(solution)/shard_map/ppermute | solution.py:29
  136.5 8.2 %collective-permute-start.44 = (bf16[1,64,640]{2,1,0:T(8,128)(2,1)S(1)}, bf16[1,64,640]{2,1,0:T(8,128)(2,1)S(1)}, u32[]{:S(2)}, u32[]{:S(2)}) collective-permute-start(bf16[1,64,640]{2,1,0:T(8,128)(2,1)S(1)} %get-tuple-element.63), channel_id=1, source_target_pairs={{0,8},{4,12},{8,0},{12,4},{1,9},{5,13},{9,1},{13,5},{2,10},{6,14},... | collective-permute-start | bytes 245768 | tf_op jit(solution)/shard_map/ppermute | solution.py:29
  136.6 8.2 %collective-permute-start.46 = (bf16[1,64,640]{2,1,0:T(8,128)(2,1)S(1)}, bf16[1,64,640]{2,1,0:T(8,128)(2,1)S(1)}, u32[]{:S(2)}, u32[]{:S(2)}) collective-permute-start(bf16[1,64,640]{2,1,0:T(8,128)(2,1)S(1)} %get-tuple-element.64), channel_id=1, source_target_pairs={{0,4},{4,8},{8,12},{12,0},{1,5},{5,9},{9,13},{13,1},{2,6},{6,10},{... | collective-permute-start | bytes 245768 | tf_op jit(solution)/shard_map/ppermute | solution.py:29
  137.1 8.1 %collective-permute-start.41 = (bf16[1,64,640]{2,1,0:T(8,128)(2,1)S(1)}, bf16[1,64,640]{2,1,0:T(8,128)(2,1)S(1)}, u32[]{:S(2)}, u32[]{:S(2)}) collective-permute-start(bf16[1,64,640]{2,1,0:T(8,128)(2,1)S(1)} %get-tuple-element.61), channel_id=1, source_target_pairs={{0,1},{1,0},{2,3},{3,2},{4,5},{5,4},{6,7},{7,6},{8,9},{9,8},{10,11... | collective-permute-start | bytes 245768 | tf_op jit(solution)/shard_map/ppermute | solution.py:29
  139.4 5.9 %collective-permute-start.43 = (bf16[1,64,640]{2,1,0:T(8,128)(2,1)S(1)}, bf16[1,64,640]{2,1,0:T(8,128)(2,1)S(1)}, u32[]{:S(2)}, u32[]{:S(2)}) collective-permute-start(bf16[1,64,640]{2,1,0:T(8,128)(2,1)S(1)} %collective-permute-done.42.refs_2_), channel_id=1, source_target_pairs={{0,1},{1,0},{2,3},{3,2},{4,5},{5,4},{6,7},{7,6},{8,9},{9,8},{10,11... | collective-permute-start | bytes 245768 | tf_op jit(solution)/shard_map/ppermute | solution.py:29
  144.7 1.3 collective-permute-start.45
  144.7 1.4 collective-permute-start.47
  (9 other events, 53.1 us)
